TPU v7x, 32 devices: a whole 2x2x4 slice. The times are simulated.
32 devices in a mesh: ctx: 8 (over z, x), tp: 4 (over y, core).
Axes of the slice: x: 2, y: 2, z: 4, core: 2. Of those that a mesh axis runs over, the one named last changes fastest.
Arguments:
- layer_input: bfloat16 [4096, 2048], P('ctx'), may hold values from -6 to 6
- attn_gain: float32 [2048], replicated, may hold values from 0.5 to 1.5
- w_query: bfloat16 [2048, 2048], P(None, 'tp'), may hold values from -0.125 to 0.125
- key_matrix: bfloat16 [2048, 1024], P(None, 'tp'), may hold values from -0.125 to 0.125
- value_matrix: bfloat16 [2048, 1024], P(None, 'tp'), may hold values from -0.125 to 0.125
- w_out: bfloat16 [2048, 2048], P('tp'), may hold values from -1 to 1
- ffn_gain: float32 [2048], replicated, may hold values from 0.5 to 1.5
- w_gate: bfloat16 [2048, 8192], P(None, 'tp'), may hold values from -0.125 to 0.125
- w_up: bfloat16 [2048, 8192], P(None, 'tp'), may hold values from -0.125 to 0.125
- w_down: bfloat16 [8192, 2048], P('tp'), may hold values from -0.125 to 0.125
- cotangent: bfloat16 [4096, 2048], P('ctx'), may hold values from -6 to 6
- block_order: int32 [32], replicated, may hold values from 0 to 31, each once
- cont_prompt: int32 [8], replicated, may hold values from 0 to 0, as said below
Outputs:
- output: bfloat16 [4096, 2048], P('ctx')
- grad_input: bfloat16 [4096, 2048], P('ctx')
- grad_attn_gain: float32 [2048], P(('ctx', 'tp'))
- grad_w_query: float32 [2048, 2048], P('ctx', 'tp')
- grad_w_key: float32 [2048, 1024], P('ctx', 'tp')
- grad_w_value: float32 [2048, 1024], P('ctx', 'tp')
- grad_w_out: float32 [2048, 2048], P('tp', 'ctx')
- grad_ffn_gain: float32 [2048], P(('ctx', 'tp'))
- grad_w_gate: float32 [2048, 8192], P('ctx', 'tp')
- grad_w_up: float32 [2048, 8192], P('ctx', 'tp')
- grad_w_down: float32 [8192, 2048], P('tp', 'ctx')
Inputs may be any that keep to these rules, and one draw needn't show every extreme that they name: `block_order`: a permutation: each logical block is stored exactly once. `cont_prompt`: each prompt is named by exactly 8 continuations.
All inputs are finite; a program needn't handle non-finite values.
Results may differ from a plain program's by a relative error of at most 0.028.
Values may be sent and summed in bfloat16 or wider, within the bound.
No kernel may reach another device: no remote copies, remote signals or barrier semaphores. Data moves between devices by JAX's collectives and lax.ppermute only.
A program may use at most 256 MiB of HBM per device.

v0:
```python
import math

import jax
import jax.numpy as jnp
from jax import lax
from jax.sharding import PartitionSpec as P

HEAD_SIZE = 128
PROMPT = 2048
CONT_LEN = 256
CONTS = 8
BLOCK = 128


eps_norm = 1e-05
rope_base = 1000000.0


def token_meta(row_ids, block_order, cont_prompt):
    count = cont_prompt.shape[0]
    prompt_total = count // CONTS * PROMPT
    logical = jnp.take(block_order, row_ids // BLOCK) * BLOCK + row_ids % BLOCK
    is_prompt = logical < prompt_total
    offset = logical - prompt_total
    which = jnp.clip(offset // CONT_LEN, 0, count - 1)
    group = jnp.where(is_prompt, logical // PROMPT, jnp.take(cont_prompt, which))
    member = jnp.where(is_prompt, 0, which + 1)
    place = jnp.where(is_prompt, logical % PROMPT, PROMPT + offset % CONT_LEN)
    return (group, member, place)


def visible(query_meta, key_meta):
    same = query_meta[0][:, None] == key_meta[0][None, :]
    causal = key_meta[2][None, :] <= query_meta[2][:, None]
    shared = (key_meta[1][None, :] == 0) | (key_meta[1][None, :] == query_meta[1][:, None])
    return same & causal & shared


def rope_tables(place):
    half_dim = HEAD_SIZE // 2
    freq = rope_base ** (-(2.0 * jnp.arange(half_dim, dtype=jnp.float32) / HEAD_SIZE))
    angle = place.astype(jnp.float32)[:, None] * freq[None, :]
    angle = jnp.concatenate([angle, angle], axis=-1)
    return (jnp.cos(angle), jnp.sin(angle))


def rotate(vec, cosine, sine):
    half_dim = vec.shape[-1] // 2
    turned = jnp.concatenate([-vec[..., half_dim:], vec[..., :half_dim]], axis=-1)
    return vec * cosine[:, None, :] + turned * sine[:, None, :]


def unrotate(vec, cosine, sine):
    half_dim = vec.shape[-1] // 2
    moved = vec * sine[:, None, :]
    turned = jnp.concatenate([moved[..., half_dim:], -moved[..., :half_dim]], axis=-1)
    return vec * cosine[:, None, :] + turned


def plain_dot(left, right):
    return jnp.dot(left, right, preferred_element_type=jnp.float32)


def left_dot(left, right):
    return lax.dot_general(
        left, right, (((0,), (0,)), ((), ())), preferred_element_type=jnp.float32
    )


def right_dot(left, right):
    return lax.dot_general(
        left, right, (((1,), (1,)), ((), ())), preferred_element_type=jnp.float32
    )


def norm_back(grad_out, normed, inv_scale, gain):
    scaled = grad_out * gain
    inner = jnp.mean(scaled * normed, axis=-1, keepdims=True)
    return (inv_scale * (scaled - normed * inner), jnp.sum(grad_out * normed, axis=0))


def gain_share(grad_full, ctx_count, tp_count):
    width = grad_full.shape[0] // (ctx_count * tp_count)
    shaped = grad_full.reshape(ctx_count, tp_count, width)
    return lax.dynamic_index_in_dim(shaped, lax.axis_index("tp"), 1, keepdims=False)


def fold_keys(state, piece, queries, query_meta, block_order, cont_prompt, kv_width):
    count = piece.shape[0]
    step_rows = math.gcd(512, count)
    steps = count // step_rows
    kv_heads = kv_width // HEAD_SIZE
    score_scale = 1.0 / math.sqrt(HEAD_SIZE)
    pieces = piece.reshape(steps, step_rows, 2 * kv_width)
    offsets = step_rows * jnp.arange(steps, dtype=jnp.int32)

    def fold_one_block(carry, inputs):
        block_rows, offset = inputs
        best, totals, accum = carry
        key_rows = block_rows[:, :kv_width].reshape(step_rows, kv_heads, HEAD_SIZE)
        value_rows = block_rows[:, kv_width:].reshape(step_rows, kv_heads, HEAD_SIZE)
        key_meta = token_meta(
            offset + jnp.arange(step_rows, dtype=jnp.int32), block_order, cont_prompt
        )
        visible_mask = visible(query_meta, key_meta)[None, None]
        scores = (
            jnp.einsum("hrqd,khd->hrqk", queries, key_rows, preferred_element_type=jnp.float32)
            * score_scale
        )
        scores = jnp.where(visible_mask, scores, -1e30)
        newest = jnp.maximum(best, jnp.max(scores, axis=-1))
        weights = jnp.where(visible_mask, jnp.exp(scores - newest[..., None]), 0.0)
        factor = jnp.exp(best - newest)
        totals = totals * factor + jnp.sum(weights, axis=-1)
        accum = accum * factor[..., None] + jnp.einsum(
            "hrqk,khd->hrqd",
            weights.astype(jnp.bfloat16),
            value_rows,
            preferred_element_type=jnp.float32,
        )
        return ((newest, totals, accum), None)

    result, _ = lax.scan(fold_one_block, state, (pieces, offsets))
    return result


def back_blocks(
    kv_all, queries, query_meta, log_total, grad_mix, delta, block_order, cont_prompt, kv_width
):
    row_total_count = kv_all.shape[0]
    step_rows = math.gcd(512, row_total_count)
    steps = row_total_count // step_rows
    kv_heads = kv_width // HEAD_SIZE
    score_scale = 1.0 / math.sqrt(HEAD_SIZE)
    pieces = kv_all.reshape(steps, step_rows, 2 * kv_width)
    offsets = step_rows * jnp.arange(steps, dtype=jnp.int32)

    def back_one_block(accum, inputs):
        block_rows, offset = inputs
        key_rows = block_rows[:, :kv_width].reshape(step_rows, kv_heads, HEAD_SIZE)
        value_rows = block_rows[:, kv_width:].reshape(step_rows, kv_heads, HEAD_SIZE)
        key_meta = token_meta(
            offset + jnp.arange(step_rows, dtype=jnp.int32), block_order, cont_prompt
        )
        visible_mask = visible(query_meta, key_meta)[None, None]
        scores = (
            jnp.einsum("hrqd,khd->hrqk", queries, key_rows, preferred_element_type=jnp.float32)
            * score_scale
        )
        weights = jnp.where(
            visible_mask,
            jnp.exp(jnp.where(visible_mask, scores, -1e30) - log_total[..., None]),
            0.0,
        )
        grad_weights = jnp.einsum(
            "hrqd,khd->hrqk", grad_mix, value_rows, preferred_element_type=jnp.float32
        )
        grad_scores = (weights * (grad_weights - delta[..., None])).astype(jnp.bfloat16)
        accum = accum + jnp.einsum(
            "hrqk,khd->hrqd", grad_scores, key_rows, preferred_element_type=jnp.float32
        )
        grad_keys = (
            jnp.einsum("hrqk,hrqd->khd", grad_scores, queries, preferred_element_type=jnp.float32)
            * score_scale
        )
        grad_values = jnp.einsum(
            "hrqk,hrqd->khd",
            weights.astype(jnp.bfloat16),
            grad_mix,
            preferred_element_type=jnp.float32,
        )
        joined = jnp.concatenate(
            [grad_keys.reshape(step_rows, kv_width), grad_values.reshape(step_rows, kv_width)],
            axis=1,
        )
        return (accum, joined)

    start_accum = jnp.zeros(queries.shape, jnp.float32)
    accum, terms = lax.scan(back_one_block, start_accum, (pieces, offsets))
    return (accum * score_scale, terms.reshape(row_total_count, 2 * kv_width))


def body(
    layer_input,
    attn_gain,
    w_query,
    key_matrix,
    value_matrix,
    w_out,
    ffn_gain,
    w_gate,
    w_up,
    w_down,
    cotangent,
    block_order,
    cont_prompt,
):
    local_rows = layer_input.shape[0]
    ctx_count = lax.axis_size("ctx")
    tp_count = lax.axis_size("tp")
    heads = w_query.shape[1] // HEAD_SIZE
    kv_width = key_matrix.shape[1]
    kv_heads = kv_width // HEAD_SIZE
    repeat_heads = heads // kv_heads
    row_ids = lax.axis_index("ctx") * local_rows + jnp.arange(local_rows, dtype=jnp.int32)
    query_meta = token_meta(row_ids, block_order, cont_prompt)
    cosine, sine = rope_tables(query_meta[2])
    inputs_full = layer_input.astype(jnp.float32)
    inv_one = lax.rsqrt(jnp.mean(inputs_full * inputs_full, axis=-1, keepdims=True) + eps_norm)
    normed_one = inputs_full * inv_one
    first_input = (normed_one * attn_gain).astype(jnp.bfloat16)
    query_lin = plain_dot(first_input, w_query).reshape(local_rows, heads, HEAD_SIZE)
    key_linear = plain_dot(first_input, key_matrix).reshape(local_rows, kv_heads, HEAD_SIZE)
    value_rows = plain_dot(first_input, value_matrix).astype(jnp.bfloat16)
    query_rot = rotate(query_lin, cosine, sine).astype(jnp.bfloat16)
    key_rot = rotate(key_linear, cosine, sine).astype(jnp.bfloat16)
    kv_local = jnp.concatenate([key_rot.reshape(local_rows, kv_width), value_rows], axis=1)
    queries = query_rot.reshape(local_rows, kv_heads, repeat_heads, HEAD_SIZE).transpose(1, 2, 0, 3)
    start_state = (
        jnp.full((kv_heads, repeat_heads, local_rows), -1e30, jnp.float32),
        jnp.zeros((kv_heads, repeat_heads, local_rows), jnp.float32),
        jnp.zeros((kv_heads, repeat_heads, local_rows, HEAD_SIZE), jnp.float32),
    )
    best, totals, accum = fold_keys(
        start_state,
        lax.all_gather(kv_local, "ctx", axis=0, tiled=True),
        queries,
        query_meta,
        block_order,
        cont_prompt,
        kv_width,
    )
    mixed = accum / totals[..., None]
    log_total = best + jnp.log(totals)
    mixed_rows = (
        mixed.transpose(2, 0, 1, 3).reshape(local_rows, heads * HEAD_SIZE).astype(jnp.bfloat16)
    )
    attn_out = lax.psum(plain_dot(mixed_rows, w_out).astype(jnp.bfloat16), "tp").astype(jnp.float32)
    middle = inputs_full + attn_out
    inv_two = lax.rsqrt(jnp.mean(middle * middle, axis=-1, keepdims=True) + eps_norm)
    normed_two = middle * inv_two
    second_in = (normed_two * ffn_gain).astype(jnp.bfloat16)
    gate = plain_dot(second_in, w_gate)
    upward = plain_dot(second_in, w_up)
    sigma = jax.nn.sigmoid(gate)
    swish = gate * sigma
    hidden = (swish * upward).astype(jnp.bfloat16)
    ffn_out = lax.psum(plain_dot(hidden, w_down).astype(jnp.bfloat16), "tp").astype(jnp.float32)
    output = (middle + ffn_out).astype(jnp.bfloat16)
    grad_down = left_dot(hidden, cotangent)
    grad_hidden = right_dot(cotangent, w_down)
    grad_gate = (grad_hidden * upward * sigma * (1.0 + gate * (1.0 - sigma))).astype(jnp.bfloat16)
    grad_upward = (grad_hidden * swish).astype(jnp.bfloat16)
    grad_w_gate = left_dot(second_in, grad_gate)
    grad_w_up = left_dot(second_in, grad_upward)
    grad_second = lax.psum(
        (right_dot(grad_gate, w_gate) + right_dot(grad_upward, w_up)).astype(jnp.bfloat16), "tp"
    ).astype(jnp.float32)
    grad_norm_two, ffn_gain_full = norm_back(grad_second, normed_two, inv_two, ffn_gain)
    grad_middle = cotangent.astype(jnp.float32) + grad_norm_two
    ffn_gain_share = gain_share(ffn_gain_full, ctx_count, tp_count)
    grad_branch = grad_middle.astype(jnp.bfloat16)
    grad_w_out = left_dot(mixed_rows, grad_branch)
    grad_mixed = right_dot(grad_branch, w_out).astype(jnp.bfloat16)
    grad_mix = grad_mixed.reshape(local_rows, kv_heads, repeat_heads, HEAD_SIZE).transpose(
        1, 2, 0, 3
    )
    delta = jnp.sum(grad_mix.astype(jnp.float32) * mixed, axis=-1)
    kv_back = lax.all_gather(kv_local, "ctx", axis=0, tiled=True)
    grad_query_rot, kv_terms = back_blocks(
        kv_back, queries, query_meta, log_total, grad_mix, delta, block_order, cont_prompt, kv_width
    )
    kv_sums = lax.psum_scatter(
        kv_terms.astype(jnp.bfloat16), "ctx", scatter_dimension=0, tiled=True
    ).astype(jnp.float32)
    grad_key_rot = (
        kv_sums[:, :kv_width].astype(jnp.bfloat16).reshape(local_rows, kv_heads, HEAD_SIZE)
    )
    grad_values = kv_sums[:, kv_width:].astype(jnp.bfloat16)
    grad_key = (
        unrotate(grad_key_rot, cosine, sine).reshape(local_rows, kv_width).astype(jnp.bfloat16)
    )
    grad_query_rows = (
        grad_query_rot.transpose(2, 0, 1, 3)
        .reshape(local_rows, heads, HEAD_SIZE)
        .astype(jnp.bfloat16)
    )
    grad_query = (
        unrotate(grad_query_rows, cosine, sine)
        .reshape(local_rows, heads * HEAD_SIZE)
        .astype(jnp.bfloat16)
    )
    grad_w_query = left_dot(first_input, grad_query)
    grad_w_key = left_dot(first_input, grad_key)
    grad_w_value = left_dot(first_input, grad_values)
    grad_first = lax.psum(
        (
            right_dot(grad_query, w_query)
            + right_dot(grad_key, key_matrix)
            + right_dot(grad_values, value_matrix)
        ).astype(jnp.bfloat16),
        "tp",
    ).astype(jnp.float32)
    grad_norm_one, attn_gain_full = norm_back(grad_first, normed_one, inv_one, attn_gain)
    grad_input = (grad_middle + grad_norm_one).astype(jnp.bfloat16)
    attn_gain_share = gain_share(attn_gain_full, ctx_count, tp_count)
    (
        sum_query,
        sum_key,
        sum_value,
        sum_out,
        sum_attn_gain,
        sum_gate,
        sum_up,
        sum_down,
        sum_ffn_gain,
    ) = (
        lax.psum_scatter(
            grad_w_query.astype(jnp.bfloat16), "ctx", scatter_dimension=0, tiled=True
        ).astype(jnp.float32),
        lax.psum_scatter(
            grad_w_key.astype(jnp.bfloat16), "ctx", scatter_dimension=0, tiled=True
        ).astype(jnp.float32),
        lax.psum_scatter(
            grad_w_value.astype(jnp.bfloat16), "ctx", scatter_dimension=0, tiled=True
        ).astype(jnp.float32),
        lax.psum_scatter(
            grad_w_out.astype(jnp.bfloat16), "ctx", scatter_dimension=1, tiled=True
        ).astype(jnp.float32),
        lax.psum_scatter(
            attn_gain_share.astype(jnp.bfloat16), "ctx", scatter_dimension=0, tiled=True
        ).astype(jnp.float32),
        lax.psum_scatter(
            grad_w_gate.astype(jnp.bfloat16), "ctx", scatter_dimension=0, tiled=True
        ).astype(jnp.float32),
        lax.psum_scatter(
            grad_w_up.astype(jnp.bfloat16), "ctx", scatter_dimension=0, tiled=True
        ).astype(jnp.float32),
        lax.psum_scatter(
            grad_down.astype(jnp.bfloat16), "ctx", scatter_dimension=1, tiled=True
        ).astype(jnp.float32),
        lax.psum_scatter(
            ffn_gain_share.astype(jnp.bfloat16), "ctx", scatter_dimension=0, tiled=True
        ).astype(jnp.float32),
    )
    return (
        output,
        grad_input,
        sum_attn_gain.reshape(-1),
        sum_query,
        sum_key,
        sum_value,
        sum_out,
        sum_ffn_gain.reshape(-1),
        sum_gate,
        sum_up,
        sum_down,
    )


def solution(mesh):
    placed = (
        P("ctx", None),
        P(),
        P(None, "tp"),
        P(None, "tp"),
        P(None, "tp"),
        P("tp", None),
        P(),
        P(None, "tp"),
        P(None, "tp"),
        P("tp", None),
        P("ctx", None),
        P(),
        P(),
    )
    return jax.shard_map(
        body,
        mesh=mesh,
        in_specs=placed,
        out_specs=(
            P("ctx", None),
            P("ctx", None),
            P(("ctx", "tp")),
            P("ctx", "tp"),
            P("ctx", "tp"),
            P("ctx", "tp"),
            P("tp", "ctx"),
            P(("ctx", "tp")),
            P("ctx", "tp"),
            P("ctx", "tp"),
            P("tp", "ctx"),
        ),
        check_vma=False,
    )
```

profile of v0, /device:TPU:0, one launch (start us, length us, event | category | flops | bytes accessed | tf_op | source)
XLA Modules:
  0.0 1855.5 jit_solution(12758562709876939795)
XLA Ops:
  11.1 20.1 %fusion.108 = (f32[512]{0:T(512)S(1)}, s32[512]{0:T(512)S(1)}, s32[512]{0:T(512)S(1)}) fusion(s32[]{:T(128)} %bitcast.31, s32[]{:T(128)} %bitcast.30, s32[]{:T(128)} %bitcast.29, s32[]{:T(128)} %bitcast.28, s32[]{:T(128)} %bitcast.27, s32[]{:T(128)} %bitcast.26, s32[]{:T(128)} %bitcast.25, s32[]{:T(128)} %bitcast.24, s32[]{:T(128)} %bitcast.23, ...), kind=kLoop, calls=%fused_computation.253 | loop fusion | flops 60416 | bytes 6276 | tf_op jit(solution)/shard_map/convert_element_type | solution.py:42
  49.8 67.7 %all-gather.2.cloned.1.call-done = bf16[4096,512]{0,1:T(8,128)(2,1)} async-done(((bf16[512,512]{0,1:T(8,128)(2,1)}), bf16[4096,512]{0,1:T(8,128)(2,1)}) %all-gather.2.cloned.1.call-update) | async-done | bytes 4194320 | tf_op jit(solution)/shard_map/all_gather | solution.py:226
  122.1 327.3 %while.34 = (s32[]{:T(128)}, f32[2,2,512]{2,1,0:T(2,128)S(1)}, f32[2,2,512]{2,1,0:T(2,128)S(1)}, f32[2,2,512,128]{3,2,1,0:T(8,128)}, s32[512]{0:T(512)S(1)}, /*i...) while((s32[]{:T(128)}, f32[2,2,512]{2,1,0:T(2,128)S(1)}, ...), condition=%wide.region_4.7_spmd.clone, body=%wide.region_1.6_spmd.clone.sunk | while | flops 552962560 | bytes 36855484 | solution.py:123
  124.1 20.7 %broadcast_compare_fusion.13 = (pred[512]{0:T(512)(128)(4,1)S(1)}, s32[512]{0:T(512)S(1)}, s32[512]{0:T(512)S(1)}) fusion(s32[]{:T(128)} %bitcast.426, s32[]{:T(128)} %bitcast.427, s32[]{:T(128)} %bitcast.428, s32[]{:T(128)} %bitcast.429, s32[]{:T(128)} %bitcast.430, s32[]{:T(128)} %bitcast.431, s32[]{:T(128)} %bitcast.432, s32[]{:T(128)} %bitcast.433, ...), kind=kLoop, calls=%fused_computation.52.clone.1 | loop fusion | flops 57344 | bytes 4740 | tf_op jit(solution)/shard_map/while/body/eval_jaxpr/eq | solution.py:35
  145.4 5.1 fusion.214
  164.1 20.7 %broadcast_compare_fusion.13 = (pred[512]{0:T(512)(128)(4,1)S(1)}, s32[512]{0:T(512)S(1)}, s32[512]{0:T(512)S(1)}) fusion(s32[]{:T(128)} %bitcast.426, s32[]{:T(128)} %bitcast.427, s32[]{:T(128)} %bitcast.428, s32[]{:T(128)} %bitcast.429, s32[]{:T(128)} %bitcast.430, s32[]{:T(128)} %bitcast.431, s32[]{:T(128)} %bitcast.432, s32[]{:T(128)} %bitcast.433, ...), kind=kLoop, calls=%fused_computation.52.clone.1 | loop fusion | flops 57344 | bytes 4740 | tf_op jit(solution)/shard_map/while/body/eval_jaxpr/eq | solution.py:35
  185.4 5.1 fusion.214
  205.2 20.7 %broadcast_compare_fusion.13 = (pred[512]{0:T(512)(128)(4,1)S(1)}, s32[512]{0:T(512)S(1)}, s32[512]{0:T(512)S(1)}) fusion(s32[]{:T(128)} %bitcast.426, s32[]{:T(128)} %bitcast.427, s32[]{:T(128)} %bitcast.428, s32[]{:T(128)} %bitcast.429, s32[]{:T(128)} %bitcast.430, s32[]{:T(128)} %bitcast.431, s32[]{:T(128)} %bitcast.432, s32[]{:T(128)} %bitcast.433, ...), kind=kLoop, calls=%fused_computation.52.clone.1 | loop fusion | flops 57344 | bytes 4740 | tf_op jit(solution)/shard_map/while/body/eval_jaxpr/eq | solution.py:35
  226.5 5.1 fusion.214
  246.2 20.7 %broadcast_compare_fusion.13 = (pred[512]{0:T(512)(128)(4,1)S(1)}, s32[512]{0:T(512)S(1)}, s32[512]{0:T(512)S(1)}) fusion(s32[]{:T(128)} %bitcast.426, s32[]{:T(128)} %bitcast.427, s32[]{:T(128)} %bitcast.428, s32[]{:T(128)} %bitcast.429, s32[]{:T(128)} %bitcast.430, s32[]{:T(128)} %bitcast.431, s32[]{:T(128)} %bitcast.432, s32[]{:T(128)} %bitcast.433, ...), kind=kLoop, calls=%fused_computation.52.clone.1 | loop fusion | flops 57344 | bytes 4740 | tf_op jit(solution)/shard_map/while/body/eval_jaxpr/eq | solution.py:35
  267.5 5.1 fusion.214
  287.2 20.7 %broadcast_compare_fusion.13 = (pred[512]{0:T(512)(128)(4,1)S(1)}, s32[512]{0:T(512)S(1)}, s32[512]{0:T(512)S(1)}) fusion(s32[]{:T(128)} %bitcast.426, s32[]{:T(128)} %bitcast.427, s32[]{:T(128)} %bitcast.428, s32[]{:T(128)} %bitcast.429, s32[]{:T(128)} %bitcast.430, s32[]{:T(128)} %bitcast.431, s32[]{:T(128)} %bitcast.432, s32[]{:T(128)} %bitcast.433, ...), kind=kLoop, calls=%fused_computation.52.clone.1 | loop fusion | flops 57344 | bytes 4740 | tf_op jit(solution)/shard_map/while/body/eval_jaxpr/eq | solution.py:35
  308.6 5.1 fusion.214
  328.3 20.7 %broadcast_compare_fusion.13 = (pred[512]{0:T(512)(128)(4,1)S(1)}, s32[512]{0:T(512)S(1)}, s32[512]{0:T(512)S(1)}) fusion(s32[]{:T(128)} %bitcast.426, s32[]{:T(128)} %bitcast.427, s32[]{:T(128)} %bitcast.428, s32[]{:T(128)} %bitcast.429, s32[]{:T(128)} %bitcast.430, s32[]{:T(128)} %bitcast.431, s32[]{:T(128)} %bitcast.432, s32[]{:T(128)} %bitcast.433, ...), kind=kLoop, calls=%fused_computation.52.clone.1 | loop fusion | flops 57344 | bytes 4740 | tf_op jit(solution)/shard_map/while/body/eval_jaxpr/eq | solution.py:35
  369.3 20.7 %broadcast_compare_fusion.13 = (pred[512]{0:T(512)(128)(4,1)S(1)}, s32[512]{0:T(512)S(1)}, s32[512]{0:T(512)S(1)}) fusion(s32[]{:T(128)} %bitcast.426, s32[]{:T(128)} %bitcast.427, s32[]{:T(128)} %bitcast.428, s32[]{:T(128)} %bitcast.429, s32[]{:T(128)} %bitcast.430, s32[]{:T(128)} %bitcast.431, s32[]{:T(128)} %bitcast.432, s32[]{:T(128)} %bitcast.433, ...), kind=kLoop, calls=%fused_computation.52.clone.1 | loop fusion | flops 57344 | bytes 4740 | tf_op jit(solution)/shard_map/while/body/eval_jaxpr/eq | solution.py:35
  410.4 20.7 %broadcast_compare_fusion.13 = (pred[512]{0:T(512)(128)(4,1)S(1)}, s32[512]{0:T(512)S(1)}, s32[512]{0:T(512)S(1)}) fusion(s32[]{:T(128)} %bitcast.426, s32[]{:T(128)} %bitcast.427, s32[]{:T(128)} %bitcast.428, s32[]{:T(128)} %bitcast.429, s32[]{:T(128)} %bitcast.430, s32[]{:T(128)} %bitcast.431, s32[]{:T(128)} %bitcast.432, s32[]{:T(128)} %bitcast.433, ...), kind=kLoop, calls=%fused_computation.52.clone.1 | loop fusion | flops 57344 | bytes 4740 | tf_op jit(solution)/shard_map/while/body/eval_jaxpr/eq | solution.py:35
  456.2 49.5 %all-reduce.8.cloned.1.call-done = bf16[512,2048]{1,0:T(8,128)(2,1)} async-done(((bf16[512,2048]{1,0:T(8,128)(2,1)}), bf16[512,2048]{1,0:T(8,128)(2,1)}) %all-reduce.8.cloned.1.call-update) | async-done | bytes 2097168 | tf_op jit(solution)/shard_map/psum | solution.py:238
  510.2 10.5 fusion.125
  520.8 6.1 fusion.126
  526.9 11.7 multiply_convert_fusion
  538.6 8.5 fusion.127
  547.1 9.2 add_convert_fusion.1
  556.8 51.1 %all-reduce.10.cloned.1.call-done = bf16[512,2048]{1,0:T(8,128)(2,1)} async-done(((bf16[512,2048]{1,0:T(8,128)(2,1)}), bf16[512,2048]{1,0:T(8,128)(2,1)}) %all-reduce.10.cloned.1.call-update) | async-done | bytes 2097168 | tf_op jit(solution)/shard_map/psum | solution.py:256
  616.7 314.9 %while.35 = (s32[]{:T(128)}, f32[2,2,512,128]{3,2,1,0:T(8,128)}, bf16[8,512,512]{1,2,0:T(8,128)(2,1)}, s32[512]{0:T(512)S(1)}, s32[8]{0:T(128)S(1)}, /*index=5*/...) while((s32[]{:T(128)}, f32[2,2,512,128]{3,2,1,0:T(8,128)}, ...), condition=%wide.region_12.15_spmd.clone, body=%wide.region_11.14_spmd.clone.sunk | while | flops 1358258688 | bytes 28360852 | solution.py:179
  618.8 21.0 %broadcast_compare_fusion.14 = (pred[512]{0:T(512)(128)(4,1)S(1)}, s32[512]{0:T(512)S(1)}, s32[512]{0:T(512)S(1)}) fusion(s32[]{:T(128)} %bitcast.486, s32[]{:T(128)} %bitcast.487, s32[]{:T(128)} %bitcast.488, s32[]{:T(128)} %bitcast.489, s32[]{:T(128)} %bitcast.490, s32[]{:T(128)} %bitcast.491, s32[]{:T(128)} %bitcast.492, s32[]{:T(128)} %bitcast.493, ...), kind=kLoop, calls=%fused_computation.108.clone.1 | loop fusion | flops 57344 | bytes 4740 | tf_op jit(solution)/shard_map/while/body/eval_jaxpr/eq | solution.py:35
  657.1 21.0 %broadcast_compare_fusion.14 = (pred[512]{0:T(512)(128)(4,1)S(1)}, s32[512]{0:T(512)S(1)}, s32[512]{0:T(512)S(1)}) fusion(s32[]{:T(128)} %bitcast.486, s32[]{:T(128)} %bitcast.487, s32[]{:T(128)} %bitcast.488, s32[]{:T(128)} %bitcast.489, s32[]{:T(128)} %bitcast.490, s32[]{:T(128)} %bitcast.491, s32[]{:T(128)} %bitcast.492, s32[]{:T(128)} %bitcast.493, ...), kind=kLoop, calls=%fused_computation.108.clone.1 | loop fusion | flops 57344 | bytes 4740 | tf_op jit(solution)/shard_map/while/body/eval_jaxpr/eq | solution.py:35
  696.6 21.0 %broadcast_compare_fusion.14 = (pred[512]{0:T(512)(128)(4,1)S(1)}, s32[512]{0:T(512)S(1)}, s32[512]{0:T(512)S(1)}) fusion(s32[]{:T(128)} %bitcast.486, s32[]{:T(128)} %bitcast.487, s32[]{:T(128)} %bitcast.488, s32[]{:T(128)} %bitcast.489, s32[]{:T(128)} %bitcast.490, s32[]{:T(128)} %bitcast.491, s32[]{:T(128)} %bitcast.492, s32[]{:T(128)} %bitcast.493, ...), kind=kLoop, calls=%fused_computation.108.clone.1 | loop fusion | flops 57344 | bytes 4740 | tf_op jit(solution)/shard_map/while/body/eval_jaxpr/eq | solution.py:35
  736.1 21.0 %broadcast_compare_fusion.14 = (pred[512]{0:T(512)(128)(4,1)S(1)}, s32[512]{0:T(512)S(1)}, s32[512]{0:T(512)S(1)}) fusion(s32[]{:T(128)} %bitcast.486, s32[]{:T(128)} %bitcast.487, s32[]{:T(128)} %bitcast.488, s32[]{:T(128)} %bitcast.489, s32[]{:T(128)} %bitcast.490, s32[]{:T(128)} %bitcast.491, s32[]{:T(128)} %bitcast.492, s32[]{:T(128)} %bitcast.493, ...), kind=kLoop, calls=%fused_computation.108.clone.1 | loop fusion | flops 57344 | bytes 4740 | tf_op jit(solution)/shard_map/while/body/eval_jaxpr/eq | solution.py:35
  775.6 21.0 %broadcast_compare_fusion.14 = (pred[512]{0:T(512)(128)(4,1)S(1)}, s32[512]{0:T(512)S(1)}, s32[512]{0:T(512)S(1)}) fusion(s32[]{:T(128)} %bitcast.486, s32[]{:T(128)} %bitcast.487, s32[]{:T(128)} %bitcast.488, s32[]{:T(128)} %bitcast.489, s32[]{:T(128)} %bitcast.490, s32[]{:T(128)} %bitcast.491, s32[]{:T(128)} %bitcast.492, s32[]{:T(128)} %bitcast.493, ...), kind=kLoop, calls=%fused_computation.108.clone.1 | loop fusion | flops 57344 | bytes 4740 | tf_op jit(solution)/shard_map/while/body/eval_jaxpr/eq | solution.py:35
  815.1 21.0 %broadcast_compare_fusion.14 = (pred[512]{0:T(512)(128)(4,1)S(1)}, s32[512]{0:T(512)S(1)}, s32[512]{0:T(512)S(1)}) fusion(s32[]{:T(128)} %bitcast.486, s32[]{:T(128)} %bitcast.487, s32[]{:T(128)} %bitcast.488, s32[]{:T(128)} %bitcast.489, s32[]{:T(128)} %bitcast.490, s32[]{:T(128)} %bitcast.491, s32[]{:T(128)} %bitcast.492, s32[]{:T(128)} %bitcast.493, ...), kind=kLoop, calls=%fused_computation.108.clone.1 | loop fusion | flops 57344 | bytes 4740 | tf_op jit(solution)/shard_map/while/body/eval_jaxpr/eq | solution.py:35
  854.6 21.0 %broadcast_compare_fusion.14 = (pred[512]{0:T(512)(128)(4,1)S(1)}, s32[512]{0:T(512)S(1)}, s32[512]{0:T(512)S(1)}) fusion(s32[]{:T(128)} %bitcast.486, s32[]{:T(128)} %bitcast.487, s32[]{:T(128)} %bitcast.488, s32[]{:T(128)} %bitcast.489, s32[]{:T(128)} %bitcast.490, s32[]{:T(128)} %bitcast.491, s32[]{:T(128)} %bitcast.492, s32[]{:T(128)} %bitcast.493, ...), kind=kLoop, calls=%fused_computation.108.clone.1 | loop fusion | flops 57344 | bytes 4740 | tf_op jit(solution)/shard_map/while/body/eval_jaxpr/eq | solution.py:35
  894.1 21.0 %broadcast_compare_fusion.14 = (pred[512]{0:T(512)(128)(4,1)S(1)}, s32[512]{0:T(512)S(1)}, s32[512]{0:T(512)S(1)}) fusion(s32[]{:T(128)} %bitcast.486, s32[]{:T(128)} %bitcast.487, s32[]{:T(128)} %bitcast.488, s32[]{:T(128)} %bitcast.489, s32[]{:T(128)} %bitcast.490, s32[]{:T(128)} %bitcast.491, s32[]{:T(128)} %bitcast.492, s32[]{:T(128)} %bitcast.493, ...), kind=kLoop, calls=%fused_computation.108.clone.1 | loop fusion | flops 57344 | bytes 4740 | tf_op jit(solution)/shard_map/while/body/eval_jaxpr/eq | solution.py:35
  937.9 6.5 convolution_convert_fusion.3
  951.0 9.9 convolution_convert_fusion.5
  960.9 64.2 %reduce-scatter.9.cloned.1.call-done = bf16[512,512]{0,1:T(8,128)(2,1)} async-done(((bf16[4096,512]{0,1:T(8,128)(2,1)}), bf16[512,512]{0,1:T(8,128)(2,1)}) %reduce-scatter.9.cloned.1.call-update) | async-done | bytes 524304 | tf_op jit(solution)/shard_map/reduce_scatter | solution.py:273
  1036.5 10.1 convolution_convert_fusion.2
  1046.6 10.1 convolution_convert_fusion.1
  1057.0 10.1 convolution_convert_fusion
  1068.4 29.0 %reduce-scatter.17.cloned.1.call-done = bf16[512,256]{1,0:T(8,128)(2,1)} async-done(((bf16[512,2048]{1,0:T(8,128)(2,1)}), bf16[512,256]{1,0:T(8,128)(2,1)}) %reduce-scatter.17.cloned.1.call-update) | async-done | bytes 262160 | tf_op jit(solution)/shard_map/reduce_scatter | solution.py:327
  1099.2 69.3 %reduce-scatter.11.cloned.1.call-done = bf16[256,512]{1,0:T(8,128)(2,1)} async-done(((bf16[2048,512]{1,0:T(8,128)(2,1)}), bf16[256,512]{1,0:T(8,128)(2,1)}) %reduce-scatter.11.cloned.1.call-update) | async-done | bytes 262160 | tf_op jit(solution)/shard_map/reduce_scatter | solution.py:318
  1170.4 86.2 %all-reduce.12.cloned.1.call-done = (bf16[512,2048]{1,0:T(8,128)(2,1)}, bf16[512,2048]{1,0:T(8,128)(2,1)}) async-done(((bf16[512,2048]{1,0:T(8,128)(2,1)}, bf16[512,2048]{1,0:T(8,128)(2,1)}), (bf16[512,2048]{1,0:T(8,128)(2,1)}, bf16[512,2048]{1,0:T(8,128)(2,1)})) %all-reduce.12.cloned.1.call-update) | async-done | bytes 4194320 | tf_op jit(solution)/shard_map/psum | solution.py:248
  1259.5 64.1 %reduce-scatter.13.cloned.1.call-done = bf16[256,256]{1,0:T(8,128)(2,1)} async-done(((bf16[2048,256]{1,0:T(8,128)(2,1)}), bf16[256,256]{1,0:T(8,128)(2,1)}) %reduce-scatter.13.cloned.1.call-update) | async-done | bytes 131088 | tf_op jit(solution)/shard_map/reduce_scatter | solution.py:321
  1325.2 64.7 %reduce-scatter.15.cloned.1.call-done = bf16[256,256]{1,0:T(8,128)(2,1)} async-done(((bf16[2048,256]{1,0:T(8,128)(2,1)}), bf16[256,256]{1,0:T(8,128)(2,1)}) %reduce-scatter.15.cloned.1.call-update) | async-done | bytes 131088 | tf_op jit(solution)/shard_map/reduce_scatter | solution.py:324
  1391.5 19.7 %all-reduce.2 = (bf16[8,64]{1,0:T(8,128)(2,1)S(1)}, bf16[8,64]{1,0:T(8,128)(2,1)S(1)}) all-reduce(bf16[8,64]{1,0:T(8,128)(2,1)S(1)} %bitcast.549, bf16[8,64]{1,0:T(8,128)(2,1)S(1)} %bitcast.548), channel_id=3, replica_groups=mesh['ctx'=8,'tp'=4] {'ctx'}, use_global_device_ids=true, to_apply=%region_17.20.clone | all-reduce | flops 1024 | bytes 4096
  1413.6 8.4 fusion.54
  1422.0 119.5 %reduce-scatter.19.cloned.1.call-done = bf16[256,2048]{1,0:T(8,128)(2,1)} async-done(((bf16[2048,2048]{1,0:T(8,128)(2,1)}), bf16[256,2048]{1,0:T(8,128)(2,1)}) %reduce-scatter.19.cloned.1.call-update) | async-done | bytes 1048592 | tf_op jit(solution)/shard_map/reduce_scatter | solution.py:333
  1544.3 149.4 %reduce-scatter.21.cloned.1.call-done = bf16[256,2048]{1,0:T(8,128)(2,1)} async-done(((bf16[2048,2048]{1,0:T(8,128)(2,1)}), bf16[256,2048]{1,0:T(8,128)(2,1)}) %reduce-scatter.21.cloned.1.call-update) | async-done | bytes 1048592 | tf_op jit(solution)/shard_map/reduce_scatter | solution.py:336
  1696.4 149.1 %reduce-scatter.23.cloned.1.call-done = bf16[2048,256]{1,0:T(8,128)(2,1)} async-done(((bf16[2048,2048]{1,0:T(8,128)(2,1)}), bf16[2048,256]{1,0:T(8,128)(2,1)}) %reduce-scatter.23.cloned.1.call-update) | async-done | bytes 1048592 | tf_op jit(solution)/shard_map/reduce_scatter | solution.py:339
  (417 shorter events, 375.4 us)
Async XLA Ops:
  7.2 446.1 %copy-start = (bf16[512,2048]{1,0:T(8,128)(2,1)S(1)}, bf16[512,2048]{1,0:T(8,128)(2,1)}, u32[]{:S(2)}) copy-start(bf16[512,2048]{1,0:T(8,128)(2,1)} %param.26) | copy-start | bytes 6291460
  7.2 110.3 %all-gather.2.cloned.1.call-start = ((), (), s32[]{:S(2)}) async-start(), calls=%async_computation.8 | async-start | bytes 4718592 | tf_op jit(solution)/shard_map/all_gather | solution.py:226
  32.3 11.1 copy-start.13
  32.4 11.1 copy-start.15
  32.4 5.2 copy-start.3
  32.4 5.2 copy-start.24
  32.4 5.2 copy-start.28
  34.7 5.0 copy-start.30
  39.6 466.0 %all-reduce.8.cloned.1.call-start = ((), (), s32[]{:S(2)}) async-start(), calls=%async_computation.9 | async-start | bytes 4194304 | tf_op jit(solution)/shard_map/psum | solution.py:238
  117.5 4.6 copy-start.7
  156.0 3.4 copy-start.2
  156.0 3.5 copy-start.17
  196.1 3.4 copy-start.2
  196.1 3.5 copy-start.17
  237.1 3.4 copy-start.2
  237.1 3.5 copy-start.17
  278.1 3.4 copy-start.2
  278.1 3.5 copy-start.17
  319.2 3.5 copy-start.17
  360.2 3.4 copy-start.2
  360.2 3.5 copy-start.17
  401.3 3.5 copy-start.17
  442.3 3.4 copy-start.2
  442.3 3.5 copy-start.17
  453.3 55.5 %copy-start.26 = (bf16[2,2,512,128]{2,3,1,0:T(8,128)(2,1)}, bf16[2,2,512,128]{2,3,1,0:T(8,128)(2,1)S(1)}, u32[]{:S(2)}) copy-start(bf16[2,2,512,128]{2,3,1,0:T(8,128)(2,1)S(1)} %fusion.77) | copy-start | bytes 1572868
  455.9 52.9 %copy-start.27 = (f32[2048]{0:T(1024)S(1)}, f32[2048]{0:T(1024)}, u32[]{:S(2)}) copy-start(f32[2048]{0:T(1024)} %param.27) | copy-start | bytes 24580
  455.9 152.0 %all-reduce.10.cloned.1.call-start = ((), (), s32[]{:S(2)}) async-start(), calls=%async_computation.10 | async-start | bytes 4194304 | tf_op jit(solution)/shard_map/psum | solution.py:256
  505.6 3.5 copy-start.8
  509.1 11.6 slice-start
  510.2 10.6 copy-start.20
  510.2 10.5 slice-start.1
  520.8 6.1 copy-start.12
  538.6 8.5 copy-start.34
  538.6 8.5 copy-start.33
  556.3 468.8 %reduce-scatter.9.cloned.1.call-start = ((), (), s32[]{:S(2)}) async-start(), calls=%async_computation.11 | async-start | bytes 4718592 | tf_op jit(solution)/shard_map/reduce_scatter | solution.py:273
  607.9 4.6 copy-start.5
  607.9 4.6 copy-start.9
  607.9 4.7 copy-start.11
  936.4 8.3 copy-start.10
  936.4 161.1 %reduce-scatter.17.cloned.1.call-start = ((), (), s32[]{:S(2)}) async-start(), calls=%async_computation.15 | async-start | bytes 2359296 | tf_op jit(solution)/shard_map/reduce_scatter | solution.py:327
  944.5 224.1 %reduce-scatter.11.cloned.1.call-start = ((), (), s32[]{:S(2)}) async-start(), calls=%async_computation.12 | async-start | bytes 2359296 | tf_op jit(solution)/shard_map/reduce_scatter | solution.py:318
  950.9 305.6 %all-reduce.12.cloned.1.call-start = ((), (), s32[]{:S(2)}) async-start(), calls=%async_computation.19 | async-start | bytes 8388608 | tf_op jit(solution)/shard_map/psum | solution.py:248
  1032.1 291.5 %reduce-scatter.13.cloned.1.call-start = ((), (), s32[]{:S(2)}) async-start(), calls=%async_computation.13 | async-start | bytes 1179648 | tf_op jit(solution)/shard_map/reduce_scatter | solution.py:321
  1034.1 355.8 %reduce-scatter.15.cloned.1.call-start = ((), (), s32[]{:S(2)}) async-start(), calls=%async_computation.14 | async-start | bytes 1179648 | tf_op jit(solution)/shard_map/reduce_scatter | solution.py:324
  1036.2 505.3 %reduce-scatter.19.cloned.1.call-start = ((), (), s32[]{:S(2)}) async-start(), calls=%async_computation.16 | async-start | bytes 9437184 | tf_op jit(solution)/shard_map/reduce_scatter | solution.py:333
  1046.6 647.1 %reduce-scatter.21.cloned.1.call-start = ((), (), s32[]{:S(2)}) async-start(), calls=%async_computation.17 | async-start | bytes 9437184 | tf_op jit(solution)/shard_map/reduce_scatter | solution.py:336
  1056.7 788.8 %reduce-scatter.23.cloned.1.call-start = ((), (), s32[]{:S(2)}) async-start(), calls=%async_computation.18 | async-start | bytes 9437184 | tf_op jit(solution)/shard_map/reduce_scatter | solution.py:339
  1413.6 434.7 %copy-start.1 = (bf16[512,2048]{1,0:T(8,128)(2,1)S(1)}, bf16[512,2048]{1,0:T(8,128)(2,1)}, u32[]{:S(2)}) copy-start(bf16[512,2048]{1,0:T(8,128)(2,1)} %param.26) | copy-start | bytes 6291460
  (15 other events, 26.9 us)
Sparse Core Ops, SparseCore 0:
  39.7 77.7 all-gather.1
  456.0 49.5 all-reduce.7
  556.4 51.4 all-reduce.9
  936.5 88.5 reduce-scatter.8
  1029.4 67.9 reduce-scatter.16
  1101.8 66.6 reduce-scatter.10
  1171.7 84.7 all-reduce.11
  1259.9 63.6 reduce-scatter.12
  1327.4 62.4 reduce-scatter.14
  1393.4 148.0 reduce-scatter.18
  1545.5 148.0 reduce-scatter.20
  1697.1 148.3 reduce-scatter.22
where the time goes:
time: 1870 us; the launch traced here: 1860 us
  waiting for transfers between devices  964 us (52%)
  other arithmetic  532 us (28%)
  matrix products  232 us (12%)
  local copies, waits for them, and re-layouts  90.4 us (5%)
  blocking collectives  19.7 us (1%)
    eq x16, other arithmetic, visible(): key_meta[1][None, :] == 0  334 us
    reduce_scatter x1, waiting for transfers between devices, body(): lax.psum_scatter(grad_w_up.astype(jnp.bfloat16), 'ctx', scatter_dimension...  149 us
    reduce_scatter x1, waiting for transfers between devices, body(): lax.psum_scatter(grad_down.astype(jnp.bfloat16), 'ctx', scatter_dimension...  149 us
    reduce_scatter x1, waiting for transfers between devices, body(): lax.psum_scatter(grad_w_gate.astype(jnp.bfloat16), 'ctx', scatter_dimensi...  120 us
    psum x1, waiting for transfers between devices, body(): lax.psum(plain_dot(hidden, w_down).astype(jnp.bfloat16), 'tp')  86.2 us
    select_n x16, other arithmetic, token_meta(): jnp.where(is_prompt, logical // PROMPT, jnp.take(cont_prompt, which))  81.9 us
    reduce_scatter x1, waiting for transfers between devices, body(): lax.psum_scatter(grad_w_query.astype(jnp.bfloat16), 'ctx', scatter_dimens...  69.3 us
    all_gather x1, waiting for transfers between devices, body(): lax.all_gather(kv_local, 'ctx', axis=0, tiled=True)  67.7 us
  transfers between devices with their start and end apart: 12, of which 12 were waited for; matrix products, arithmetic and copies ran while one was open for 5% of the time, Pallas kernels for 0%

commit v1 on v0

--- a/solution.py
+++ b/solution.py
@@ -1,8 +1,11 @@
+import functools
 import math
 
 import jax
 import jax.numpy as jnp
 from jax import lax
+from jax.experimental import pallas as pl
+from jax.experimental.pallas import tpu as pltpu
 from jax.sharding import PartitionSpec as P
 
 HEAD_SIZE = 128
@@ -10,11 +13,12 @@
 CONT_LEN = 256
 CONTS = 8
 BLOCK = 128
+LOG2E = 1.4426950408889634
+NEG = -1e30
 
 
 eps_norm = 1e-05
 rope_base = 1000000.0
-
 
 def token_meta(row_ids, block_order, cont_prompt):
     count = cont_prompt.shape[0]
@@ -29,13 +33,6 @@
     return (group, member, place)
 
 
-def visible(query_meta, key_meta):
-    same = query_meta[0][:, None] == key_meta[0][None, :]
-    causal = key_meta[2][None, :] <= query_meta[2][:, None]
-    shared = (key_meta[1][None, :] == 0) | (key_meta[1][None, :] == query_meta[1][:, None])
-    return same & causal & shared
-
-
 def rope_tables(place):
     half_dim = HEAD_SIZE // 2
     freq = rope_base ** (-(2.0 * jnp.arange(half_dim, dtype=jnp.float32) / HEAD_SIZE))
@@ -85,99 +82,297 @@
     return lax.dynamic_index_in_dim(shaped, lax.axis_index("tp"), 1, keepdims=False)
 
 
-def fold_keys(state, piece, queries, query_meta, block_order, cont_prompt, kv_width):
-    count = piece.shape[0]
-    step_rows = math.gcd(512, count)
-    steps = count // step_rows
-    kv_heads = kv_width // HEAD_SIZE
-    score_scale = 1.0 / math.sqrt(HEAD_SIZE)
-    pieces = piece.reshape(steps, step_rows, 2 * kv_width)
-    offsets = step_rows * jnp.arange(steps, dtype=jnp.int32)
-
-    def fold_one_block(carry, inputs):
-        block_rows, offset = inputs
-        best, totals, accum = carry
-        key_rows = block_rows[:, :kv_width].reshape(step_rows, kv_heads, HEAD_SIZE)
-        value_rows = block_rows[:, kv_width:].reshape(step_rows, kv_heads, HEAD_SIZE)
-        key_meta = token_meta(
-            offset + jnp.arange(step_rows, dtype=jnp.int32), block_order, cont_prompt
+def block_plan(order_ref, cont_ref, stored):
+    per_prompt = PROMPT // BLOCK
+    per_cont = CONT_LEN // BLOCK
+    count = cont_ref.shape[0]
+    prompt_blocks = count // CONTS * per_prompt
+    own = order_ref[stored]
+    is_prompt = own < prompt_blocks
+    offset = own - prompt_blocks
+    which = jnp.clip(lax.div(offset, per_cont), 0, count - 1)
+    group = jnp.where(is_prompt, lax.div(own, per_prompt), cont_ref[which])
+    inner = jnp.where(is_prompt, lax.rem(own, per_prompt), lax.rem(offset, per_cont))
+    has_prev = lax.rem(inner, 2)
+    pairs = jnp.where(is_prompt, lax.div(inner, 2), per_prompt // 2)
+    prev = own - has_prev
+    return group * per_prompt, pairs, prev, own, has_prev
+
+
+def fill_inverse(order_ref, inverse_ref):
+    def put(stored, carry):
+        inverse_ref[order_ref[stored]] = stored
+        return carry
+
+    lax.fori_loop(0, order_ref.shape[0], put, 0)
+
+
+def key_rows(inverse_ref, logical):
+    return pl.ds(pl.multiple_of(inverse_ref[logical] * BLOCK, BLOCK), BLOCK)
+
+
+def tile_pair(ref, rows_a, rows_b, column):
+    cols = pl.ds(column, HEAD_SIZE)
+    return jnp.concatenate([ref[rows_a, cols], ref[rows_b, cols]], axis=0)
+
+
+def own_mask(has_prev, rep):
+    shape = (2 * BLOCK, rep * BLOCK)
+    row = lax.broadcasted_iota(jnp.int32, shape, 0)
+    col = lax.broadcasted_iota(jnp.int32, shape, 1)
+    first_row = BLOCK * (1 - has_prev)
+    return (row >= first_row) & (row - BLOCK <= lax.rem(col, BLOCK))
+
+
+def stack_t(ref, rows, column, rep):
+    return jnp.concatenate(
+        [ref[rows, pl.ds(column + r * HEAD_SIZE, HEAD_SIZE)].T for r in range(rep)], axis=1
+    )
+
+
+def stack_rows(ref, rows, column, rep):
+    return jnp.concatenate(
+        [ref[rows, pl.ds(column + r * HEAD_SIZE, HEAD_SIZE)] for r in range(rep)], axis=0
+    )
+
+
+def dot(left, right):
+    return jnp.dot(left, right, preferred_element_type=jnp.float32)
+
+
+def forward_kernel(rep, hps, order_ref, cont_ref, first_ref, q_ref, kv_ref, out_ref, lse_ref,
+                   inverse_ref, qt_ref, acc_ref):
+    fill_inverse(order_ref, inverse_ref)
+    q_blocks = q_ref.shape[0] // BLOCK
+    factor = LOG2E / math.sqrt(HEAD_SIZE)
+    width = rep * HEAD_SIZE
+
+    def one_query_block(qb, carry):
+        base, pairs, prev, own, has_prev = block_plan(order_ref, cont_ref, first_ref[0] + qb)
+        rows = pl.ds(pl.multiple_of(qb * BLOCK, BLOCK), BLOCK)
+        mask = own_mask(has_prev, rep)
+        rows_a, rows_b = key_rows(inverse_ref, prev), key_rows(inverse_ref, own)
+        state = []
+        for h in range(hps):
+            qt = stack_t(q_ref, rows, h * width, rep)
+            qt_ref[h] = qt
+            scores = dot(tile_pair(kv_ref, rows_a, rows_b, 2 * h * HEAD_SIZE), qt) * factor
+            scores = jnp.where(mask, scores, NEG)
+            best = jnp.max(scores, axis=0, keepdims=True)
+            weights = jnp.exp2(scores - best)
+            total = jnp.sum(weights, axis=0, keepdims=True)
+            values = tile_pair(kv_ref, rows_a, rows_b, (2 * h + 1) * HEAD_SIZE)
+            acc_ref[h] = dot(values.T, weights.astype(jnp.bfloat16))
+            state += [best, total]
+
+        def one_pair(t, state):
+            rows_a = key_rows(inverse_ref, base + 2 * t)
+            rows_b = key_rows(inverse_ref, base + 2 * t + 1)
+            after = []
+            for h in range(hps):
+                best, total = state[2 * h], state[2 * h + 1]
+                keys = tile_pair(kv_ref, rows_a, rows_b, 2 * h * HEAD_SIZE)
+                scores = dot(keys, qt_ref[h]) * factor
+                newest = jnp.maximum(best, jnp.max(scores, axis=0, keepdims=True))
+                weights = jnp.exp2(scores - newest)
+                shrink = jnp.exp2(best - newest)
+                total = total * shrink + jnp.sum(weights, axis=0, keepdims=True)
+                values = tile_pair(kv_ref, rows_a, rows_b, (2 * h + 1) * HEAD_SIZE)
+                acc_ref[h] = acc_ref[h] * shrink + dot(values.T, weights.astype(jnp.bfloat16))
+                after += [newest, total]
+            return tuple(after)
+
+        state = lax.fori_loop(0, pairs, one_pair, tuple(state))
+        for h in range(hps):
+            best, total = state[2 * h], state[2 * h + 1]
+            mixed = acc_ref[h] * (1.0 / total)
+            for r in range(rep):
+                part = mixed[:, r * BLOCK : (r + 1) * BLOCK]
+                out_ref[rows, pl.ds(h * width + r * HEAD_SIZE, HEAD_SIZE)] = part.T.astype(
+                    jnp.bfloat16
+                )
+            lse_ref[0, h, pl.ds(qb, 1), :] = best + jnp.log2(total)
+        return carry
+
+    lax.fori_loop(0, q_blocks, one_query_block, 0)
+
+
+def backward_kernel(rep, hps, order_ref, cont_ref, first_ref, q_ref, kv_ref, gm_ref, mix_ref,
+                    lse_ref, gq_ref, gkv_ref, inverse_ref, qt_ref, gmt_ref, gqt_ref, acc_ref):
+    fill_inverse(order_ref, inverse_ref)
+    q_blocks = q_ref.shape[0] // BLOCK
+    scale = 1.0 / math.sqrt(HEAD_SIZE)
+    factor = LOG2E * scale
+    width = rep * HEAD_SIZE
+
+    def clear(i, carry):
+        acc_ref[pl.ds(pl.multiple_of(i * BLOCK, BLOCK), BLOCK), :] = jnp.zeros(
+            (BLOCK, acc_ref.shape[1]), jnp.float32
         )
-        visible_mask = visible(query_meta, key_meta)[None, None]
-        scores = (
-            jnp.einsum("hrqd,khd->hrqk", queries, key_rows, preferred_element_type=jnp.float32)
-            * score_scale
-        )
-        scores = jnp.where(visible_mask, scores, -1e30)
-        newest = jnp.maximum(best, jnp.max(scores, axis=-1))
-        weights = jnp.where(visible_mask, jnp.exp(scores - newest[..., None]), 0.0)
-        factor = jnp.exp(best - newest)
-        totals = totals * factor + jnp.sum(weights, axis=-1)
-        accum = accum * factor[..., None] + jnp.einsum(
-            "hrqk,khd->hrqd",
-            weights.astype(jnp.bfloat16),
-            value_rows,
-            preferred_element_type=jnp.float32,
-        )
-        return ((newest, totals, accum), None)
-
-    result, _ = lax.scan(fold_one_block, state, (pieces, offsets))
-    return result
-
-
-def back_blocks(
-    kv_all, queries, query_meta, log_total, grad_mix, delta, block_order, cont_prompt, kv_width
-):
-    row_total_count = kv_all.shape[0]
-    step_rows = math.gcd(512, row_total_count)
-    steps = row_total_count // step_rows
-    kv_heads = kv_width // HEAD_SIZE
-    score_scale = 1.0 / math.sqrt(HEAD_SIZE)
-    pieces = kv_all.reshape(steps, step_rows, 2 * kv_width)
-    offsets = step_rows * jnp.arange(steps, dtype=jnp.int32)
-
-    def back_one_block(accum, inputs):
-        block_rows, offset = inputs
-        key_rows = block_rows[:, :kv_width].reshape(step_rows, kv_heads, HEAD_SIZE)
-        value_rows = block_rows[:, kv_width:].reshape(step_rows, kv_heads, HEAD_SIZE)
-        key_meta = token_meta(
-            offset + jnp.arange(step_rows, dtype=jnp.int32), block_order, cont_prompt
-        )
-        visible_mask = visible(query_meta, key_meta)[None, None]
-        scores = (
-            jnp.einsum("hrqd,khd->hrqk", queries, key_rows, preferred_element_type=jnp.float32)
-            * score_scale
-        )
-        weights = jnp.where(
-            visible_mask,
-            jnp.exp(jnp.where(visible_mask, scores, -1e30) - log_total[..., None]),
-            0.0,
-        )
-        grad_weights = jnp.einsum(
-            "hrqd,khd->hrqk", grad_mix, value_rows, preferred_element_type=jnp.float32
-        )
-        grad_scores = (weights * (grad_weights - delta[..., None])).astype(jnp.bfloat16)
-        accum = accum + jnp.einsum(
-            "hrqk,khd->hrqd", grad_scores, key_rows, preferred_element_type=jnp.float32
-        )
-        grad_keys = (
-            jnp.einsum("hrqk,hrqd->khd", grad_scores, queries, preferred_element_type=jnp.float32)
-            * score_scale
-        )
-        grad_values = jnp.einsum(
-            "hrqk,hrqd->khd",
-            weights.astype(jnp.bfloat16),
-            grad_mix,
-            preferred_element_type=jnp.float32,
-        )
-        joined = jnp.concatenate(
-            [grad_keys.reshape(step_rows, kv_width), grad_values.reshape(step_rows, kv_width)],
-            axis=1,
-        )
-        return (accum, joined)
-
-    start_accum = jnp.zeros(queries.shape, jnp.float32)
-    accum, terms = lax.scan(back_one_block, start_accum, (pieces, offsets))
-    return (accum * score_scale, terms.reshape(row_total_count, 2 * kv_width))
+        return carry
+
+    lax.fori_loop(0, order_ref.shape[0], clear, 0)
+
+    def tile_terms(h, rows_a, rows_b, lse, delta, q_rows, gm_rows, mask):
+        kcol, vcol = 2 * h * HEAD_SIZE, (2 * h + 1) * HEAD_SIZE
+        keys = tile_pair(kv_ref, rows_a, rows_b, kcol)
+        values = tile_pair(kv_ref, rows_a, rows_b, vcol)
+        weights = jnp.exp2(dot(keys, qt_ref[h]) * factor - lse)
+        if mask is not None:
+            weights = jnp.where(mask, weights, 0.0)
+        grad_weights = dot(values, gmt_ref[h])
+        grad_scores = (weights * (grad_weights - delta)).astype(jnp.bfloat16)
+        gv = dot(weights.astype(jnp.bfloat16), gm_rows)
+        gk = dot(grad_scores, q_rows)
+        acc_ref[rows_a, pl.ds(kcol, HEAD_SIZE)] += gk[:BLOCK]
+        acc_ref[rows_b, pl.ds(kcol, HEAD_SIZE)] += gk[BLOCK:]
+        acc_ref[rows_a, pl.ds(vcol, HEAD_SIZE)] += gv[:BLOCK]
+        acc_ref[rows_b, pl.ds(vcol, HEAD_SIZE)] += gv[BLOCK:]
+        return dot(keys.T, grad_scores)
+
+    def one_query_block(qb, carry):
+        base, pairs, prev, own, has_prev = block_plan(order_ref, cont_ref, first_ref[0] + qb)
+        rows = pl.ds(pl.multiple_of(qb * BLOCK, BLOCK), BLOCK)
+        mask = own_mask(has_prev, rep)
+        rows_a, rows_b = key_rows(inverse_ref, prev), key_rows(inverse_ref, own)
+        deltas, lses, q_stack, gm_stack = [], [], [], []
+        for h in range(hps):
+            qt_ref[h] = stack_t(q_ref, rows, h * width, rep)
+            gmt = stack_t(gm_ref, rows, h * width, rep)
+            gmt_ref[h] = gmt
+            mixt = stack_t(mix_ref, rows, h * width, rep)
+            deltas.append(
+                jnp.sum(
+                    gmt.astype(jnp.float32) * mixt.astype(jnp.float32), axis=0, keepdims=True
+                )
+            )
+            lses.append(lse_ref[0, h, pl.ds(qb, 1), :])
+        for h in range(hps):
+            q_rows = stack_rows(q_ref, rows, h * width, rep)
+            gm_rows = stack_rows(gm_ref, rows, h * width, rep)
+            gqt_ref[h] = tile_terms(
+                h, rows_a, rows_b, lses[h], deltas[h], q_rows, gm_rows, mask
+            )
+
+        def one_pair(t, carry):
+            rows_a = key_rows(inverse_ref, base + 2 * t)
+            rows_b = key_rows(inverse_ref, base + 2 * t + 1)
+            for h in range(hps):
+                q_rows = stack_rows(q_ref, rows, h * width, rep)
+                gm_rows = stack_rows(gm_ref, rows, h * width, rep)
+                gqt_ref[h] += tile_terms(
+                    h, rows_a, rows_b, lses[h], deltas[h], q_rows, gm_rows, None
+                )
+            return carry
+
+        lax.fori_loop(0, pairs, one_pair, 0)
+        for h in range(hps):
+            total = gqt_ref[h] * scale
+            for r in range(rep):
+                part = total[:, r * BLOCK : (r + 1) * BLOCK]
+                gq_ref[rows, pl.ds(h * width + r * HEAD_SIZE, HEAD_SIZE)] = part.T.astype(
+                    jnp.bfloat16
+                )
+        return carry
+
+    lax.fori_loop(0, q_blocks, one_query_block, 0)
+
+    def flush(i, carry):
+        rows = pl.ds(pl.multiple_of(i * BLOCK, BLOCK), BLOCK)
+        for h in range(hps):
+            kcols = pl.ds(2 * h * HEAD_SIZE, HEAD_SIZE)
+            vcols = pl.ds((2 * h + 1) * HEAD_SIZE, HEAD_SIZE)
+            gkv_ref[rows, kcols] = (acc_ref[rows, kcols] * scale).astype(jnp.bfloat16)
+            gkv_ref[rows, vcols] = acc_ref[rows, vcols].astype(jnp.bfloat16)
+        return carry
+
+    lax.fori_loop(0, order_ref.shape[0], flush, 0)
+
+
+def attention_sizes(q, kv):
+    kv_heads = kv.shape[1] // (2 * HEAD_SIZE)
+    rep = q.shape[1] // HEAD_SIZE // kv_heads
+    hps = kv_heads if kv.shape[0] <= 8192 else 1
+    return kv_heads, rep, hps
+
+
+def attention_forward(q, kv, order, cont, first):
+    kv_heads, rep, hps = attention_sizes(q, kv)
+    rows, tokens = q.shape[0], kv.shape[0]
+    q_blocks = rows // BLOCK
+    wide = hps * rep * HEAD_SIZE
+    q_spec = pl.BlockSpec((rows, wide), lambda g, *_: (0, g))
+    flops = 4 * rows * (tokens // 2) * q.shape[1]
+    return pl.pallas_call(
+        functools.partial(forward_kernel, rep, hps),
+        out_shape=(
+            jax.ShapeDtypeStruct(q.shape, jnp.bfloat16),
+            jax.ShapeDtypeStruct((kv_heads // hps, hps, q_blocks, rep * BLOCK), jnp.float32),
+        ),
+        grid_spec=pltpu.PrefetchScalarGridSpec(
+            num_scalar_prefetch=3,
+            grid=(kv_heads // hps,),
+            in_specs=[
+                q_spec,
+                pl.BlockSpec((tokens, 2 * hps * HEAD_SIZE), lambda g, *_: (0, g)),
+            ],
+            out_specs=[
+                q_spec,
+                pl.BlockSpec((1, hps, q_blocks, rep * BLOCK), lambda g, *_: (g, 0, 0, 0)),
+            ],
+            scratch_shapes=[
+                pltpu.SMEM((order.shape[0],), jnp.int32),
+                pltpu.VMEM((hps, HEAD_SIZE, rep * BLOCK), jnp.bfloat16),
+                pltpu.VMEM((hps, HEAD_SIZE, rep * BLOCK), jnp.float32),
+            ],
+        ),
+        compiler_params=pltpu.CompilerParams(vmem_limit_bytes=56 << 20),
+        cost_estimate=pl.CostEstimate(
+            flops=flops, bytes_accessed=2 * (q.size * 2 + kv.size), transcendentals=flops // 512
+        ),
+        name="attention_forward",
+    )(order, cont, first, q, kv)
+
+
+def attention_backward(q, kv, grad_mixed, mixed, lse, order, cont, first):
+    kv_heads, rep, hps = attention_sizes(q, kv)
+    rows, tokens = q.shape[0], kv.shape[0]
+    q_blocks = rows // BLOCK
+    wide = hps * rep * HEAD_SIZE
+    q_spec = pl.BlockSpec((rows, wide), lambda g, *_: (0, g))
+    kv_spec = pl.BlockSpec((tokens, 2 * hps * HEAD_SIZE), lambda g, *_: (0, g))
+    flops = 10 * rows * (tokens // 2) * q.shape[1]
+    return pl.pallas_call(
+        functools.partial(backward_kernel, rep, hps),
+        out_shape=(
+            jax.ShapeDtypeStruct(q.shape, jnp.bfloat16),
+            jax.ShapeDtypeStruct(kv.shape, jnp.bfloat16),
+        ),
+        grid_spec=pltpu.PrefetchScalarGridSpec(
+            num_scalar_prefetch=3,
+            grid=(kv_heads // hps,),
+            in_specs=[
+                q_spec,
+                kv_spec,
+                q_spec,
+                q_spec,
+                pl.BlockSpec((1, hps, q_blocks, rep * BLOCK), lambda g, *_: (g, 0, 0, 0)),
+            ],
+            out_specs=[q_spec, kv_spec],
+            scratch_shapes=[
+                pltpu.SMEM((order.shape[0],), jnp.int32),
+                pltpu.VMEM((hps, HEAD_SIZE, rep * BLOCK), jnp.bfloat16),
+                pltpu.VMEM((hps, HEAD_SIZE, rep * BLOCK), jnp.bfloat16),
+                pltpu.VMEM((hps, HEAD_SIZE, rep * BLOCK), jnp.float32),
+                pltpu.VMEM((tokens, 2 * hps * HEAD_SIZE), jnp.float32),
+            ],
+        ),
+        compiler_params=pltpu.CompilerParams(vmem_limit_bytes=60 << 20),
+        cost_estimate=pl.CostEstimate(
+            flops=flops, bytes_accessed=4 * (q.size * 2 + kv.size), transcendentals=flops // 1280
+        ),
+        name="attention_backward",
+    )(order, cont, first, q, kv, grad_mixed, mixed, lse)
 
 
 def body(
@@ -201,7 +396,6 @@
     heads = w_query.shape[1] // HEAD_SIZE
     kv_width = key_matrix.shape[1]
     kv_heads = kv_width // HEAD_SIZE
-    repeat_heads = heads // kv_heads
     row_ids = lax.axis_index("ctx") * local_rows + jnp.arange(local_rows, dtype=jnp.int32)
     query_meta = token_meta(row_ids, block_order, cont_prompt)
     cosine, sine = rope_tables(query_meta[2])
@@ -214,27 +408,13 @@
     value_rows = plain_dot(first_input, value_matrix).astype(jnp.bfloat16)
     query_rot = rotate(query_lin, cosine, sine).astype(jnp.bfloat16)
     key_rot = rotate(key_linear, cosine, sine).astype(jnp.bfloat16)
-    kv_local = jnp.concatenate([key_rot.reshape(local_rows, kv_width), value_rows], axis=1)
-    queries = query_rot.reshape(local_rows, kv_heads, repeat_heads, HEAD_SIZE).transpose(1, 2, 0, 3)
-    start_state = (
-        jnp.full((kv_heads, repeat_heads, local_rows), -1e30, jnp.float32),
-        jnp.zeros((kv_heads, repeat_heads, local_rows), jnp.float32),
-        jnp.zeros((kv_heads, repeat_heads, local_rows, HEAD_SIZE), jnp.float32),
-    )
-    best, totals, accum = fold_keys(
-        start_state,
-        lax.all_gather(kv_local, "ctx", axis=0, tiled=True),
-        queries,
-        query_meta,
-        block_order,
-        cont_prompt,
-        kv_width,
-    )
-    mixed = accum / totals[..., None]
-    log_total = best + jnp.log(totals)
-    mixed_rows = (
-        mixed.transpose(2, 0, 1, 3).reshape(local_rows, heads * HEAD_SIZE).astype(jnp.bfloat16)
-    )
+    kv_local = jnp.concatenate(
+        [key_rot, value_rows.reshape(local_rows, kv_heads, HEAD_SIZE)], axis=2
+    ).reshape(local_rows, 2 * kv_width)
+    queries = query_rot.reshape(local_rows, heads * HEAD_SIZE)
+    first = (lax.axis_index("ctx") * (local_rows // BLOCK)).astype(jnp.int32).reshape(1)
+    kv_all = lax.all_gather(kv_local, "ctx", axis=0, tiled=True)
+    mixed_rows, log_total = attention_forward(queries, kv_all, block_order, cont_prompt, first)
     attn_out = lax.psum(plain_dot(mixed_rows, w_out).astype(jnp.bfloat16), "tp").astype(jnp.float32)
     middle = inputs_full + attn_out
     inv_two = lax.rsqrt(jnp.mean(middle * middle, axis=-1, keepdims=True) + eps_norm)
@@ -262,29 +442,19 @@
     grad_branch = grad_middle.astype(jnp.bfloat16)
     grad_w_out = left_dot(mixed_rows, grad_branch)
     grad_mixed = right_dot(grad_branch, w_out).astype(jnp.bfloat16)
-    grad_mix = grad_mixed.reshape(local_rows, kv_heads, repeat_heads, HEAD_SIZE).transpose(
-        1, 2, 0, 3
-    )
-    delta = jnp.sum(grad_mix.astype(jnp.float32) * mixed, axis=-1)
-    kv_back = lax.all_gather(kv_local, "ctx", axis=0, tiled=True)
-    grad_query_rot, kv_terms = back_blocks(
-        kv_back, queries, query_meta, log_total, grad_mix, delta, block_order, cont_prompt, kv_width
+    grad_query_rot, kv_terms = attention_backward(
+        queries, kv_all, grad_mixed, mixed_rows, log_total, block_order, cont_prompt, first
     )
     kv_sums = lax.psum_scatter(
         kv_terms.astype(jnp.bfloat16), "ctx", scatter_dimension=0, tiled=True
     ).astype(jnp.float32)
-    grad_key_rot = (
-        kv_sums[:, :kv_width].astype(jnp.bfloat16).reshape(local_rows, kv_heads, HEAD_SIZE)
-    )
-    grad_values = kv_sums[:, kv_width:].astype(jnp.bfloat16)
+    kv_sums = kv_sums.reshape(local_rows, kv_heads, 2, HEAD_SIZE)
+    grad_key_rot = kv_sums[:, :, 0]
+    grad_values = kv_sums[:, :, 1].reshape(local_rows, kv_width).astype(jnp.bfloat16)
     grad_key = (
         unrotate(grad_key_rot, cosine, sine).reshape(local_rows, kv_width).astype(jnp.bfloat16)
     )
-    grad_query_rows = (
-        grad_query_rot.transpose(2, 0, 1, 3)
-        .reshape(local_rows, heads, HEAD_SIZE)
-        .astype(jnp.bfloat16)
-    )
+    grad_query_rows = grad_query_rot.reshape(local_rows, heads, HEAD_SIZE)
     grad_query = (
         unrotate(grad_query_rows, cosine, sine)
         .reshape(local_rows, heads * HEAD_SIZE)

time: 1870 us -> 1270 us (0.68)
  other arithmetic: 532 us -> 77.4 us
  matrix products: 232 us -> 121 us
  local copies, waits for them, and re-layouts: 90.4 us -> 26.9 us
  Pallas kernels: 0 us -> 38.5 us
    eq x16 -> x0, other arithmetic: 334 us -> none  [visible(): key_meta[1][None, :] == 0]
    dot_general x56 -> x0, matrix products: 114 us -> none  [the longest x8 27.8 us: fold_one_block(): jnp.einsum('hrqk,khd->hrqd', weights.astype(jnp.bfloat16), value_rows, pr...]
    select_n x17 -> x0, other arithmetic: 86.9 us -> none  [the longest x16 81.9 us: token_meta(): jnp.where(is_prompt, logical // PROMPT, jnp.take(cont_prompt, which))]
    pallas_call x0 -> x2, Pallas kernels: none -> 38.5 us  [the longest x1 19.9 us: attention_backward(): pl.pallas_call(functools.partial(backward_kernel, rep, hps), out_shape=(j...]
    reduce_sum x8 -> x0, other arithmetic: 27 us -> none  [fold_one_block(): totals = totals * factor + jnp.sum(weights, axis=-1)]
    gather x34 -> x2, local copies, waits for them, and re-layouts: 27 us -> 3.89 us  [token_meta(): logical = jnp.take(block_order, row_ids // BLOCK) * BLOCK + row_ids % BLOCK]
  transfers between devices with their start and end apart: 12 -> 12, of which waited for: 12 -> 12; matrix products, arithmetic and copies ran while one was open for 5% -> 9% of each run, Pallas kernels for 0% -> 0%
where the time goes in v1:
time: 1270 us; the launch traced here: 1260 us
  waiting for transfers between devices  961 us (76%)
  matrix products  121 us (10%)
  other arithmetic  77.4 us (6%)
  Pallas kernels  38.5 us (3%)
  local copies, waits for them, and re-layouts  26.9 us (2%)
  blocking collectives  19.7 us (2%)
  between operations  15.1 us (1%)
    reduce_scatter x1, waiting for transfers between devices, body(): lax.psum_scatter(grad_w_up.astype(jnp.bfloat16), 'ctx', scatter_dimension...  149 us
    reduce_scatter x1, waiting for transfers between devices, body(): lax.psum_scatter(grad_down.astype(jnp.bfloat16), 'ctx', scatter_dimension...  149 us
    reduce_scatter x1, waiting for transfers between devices, body(): lax.psum_scatter(grad_w_gate.astype(jnp.bfloat16), 'ctx', scatter_dimensi...  119 us
    psum x1, waiting for transfers between devices, body(): lax.psum(plain_dot(hidden, w_down).astype(jnp.bfloat16), 'tp')  86 us
    reduce_scatter x1, waiting for transfers between devices, body(): lax.psum_scatter(grad_w_query.astype(jnp.bfloat16), 'ctx', scatter_dimens...  69.5 us
    reduce_scatter x1, waiting for transfers between devices, body(): lax.psum_scatter(kv_terms.astype(jnp.bfloat16), 'ctx', scatter_dimension=...  66.3 us
    reduce_scatter x1, waiting for transfers between devices, body(): lax.psum_scatter(grad_w_value.astype(jnp.bfloat16), 'ctx', scatter_dimens...  64.5 us
    reduce_scatter x1, waiting for transfers between devices, body(): lax.psum_scatter(grad_w_key.astype(jnp.bfloat16), 'ctx', scatter_dimensio...  64.1 us
  transfers between devices with their start and end apart: 12, of which 12 were waited for; matrix products, arithmetic and copies ran while one was open for 9% of the time, Pallas kernels for 0%

profile of v1, /device:TPU:0, one launch (start us, length us, event | category | flops | bytes accessed | tf_op | source)
XLA Modules:
  0.0 1261.2 jit_solution(7054560324720516948)
XLA Ops:
  9.1 2.1 fusion.56
  11.7 4.6 compare_select_fusion.1
  16.3 15.7 %fusion.32 = f32[512]{0:T(512)S(1)} fusion(pred[512]{0:T(512)(128)(4,1)S(1)} %get-tuple-element.76, pred[512]{0:T(512)(128)(4,1)S(1)} %get-tuple-element.77, pred[512]{0:T(512)(128)(4,1)S(1)} %get-tuple-element.78, pred[512]{0:T(512)(128)(4,1)S(1)} %get-tuple-element.79, pred[512]{0:T(512)(128)(4,1)S(1)} %get-tuple-element.80, ...), kind=kLoop, calls=%fused_computation.127 | loop fusion | flops 41472 | bytes 17000 | tf_op jit(solution)/shard_map/convert_element_type | solution.py:39
  33.3 2.2 fusion.17
  35.5 3.6 fusion.46
  41.9 2.8 convolution_convert_fusion.10
  50.0 3.6 fusion.48
  56.0 2.4 copy.61
  59.8 2.4 copy.62
  65.2 2.3 fusion.21.q_ref
  67.5 58.7 %all-gather.2.cloned.1.call-done.kv_ref = bf16[4096,512]{1,0:T(8,128)(2,1)} async-done(((bf16[512,512]{1,0:T(8,128)(2,1)}), bf16[4096,512]{1,0:T(8,128)(2,1)}) %all-gather.2.cloned.1.call-update) | async-done | bytes 4194320 | tf_op jit(solution)/shard_map/all_gather | solution.py:416
  126.2 18.7 %attention_forward.1 = (bf16[512,512]{1,0:T(8,128)(2,1)}, f32[1,2,4,256]{3,2,1,0:T(4,128)}) custom-call(s32[32]{0:T(128)} %order_ref.3, s32[8]{0:T(128)} %cont_ref.3, s32[1]{0:T(128)} %bitcast.first_ref, bf16[512,512]{1,0:T(8,128)(2,1)} %fusion.21.q_ref, bf16[4096,512]{1,0:T(8,128)(2,1)} %all-gather.2.cloned.1.call-done.kv_ref), custom_call_target="tpu_custom_call" | custom-call | flops 2147483648 | bytes 5242880 | tf_op jit(solution)/shard_map/attention_forward/pallas_call | solution.py:306
  144.9 3.6 convolution_convert_fusion.6
  148.8 57.3 %all-reduce.8.cloned.1.call-done = bf16[512,2048]{1,0:T(8,128)(2,1)} async-done(((bf16[512,2048]{1,0:T(8,128)(2,1)}), bf16[512,2048]{1,0:T(8,128)(2,1)}) %all-reduce.8.cloned.1.call-update) | async-done | bytes 2097168 | tf_op jit(solution)/shard_map/psum | solution.py:418
  206.1 3.1 multiply_reduce_fusion
  210.7 10.5 fusion.58
  221.2 6.1 fusion.59
  227.3 11.7 multiply_convert_fusion
  239.0 8.5 fusion.60
  247.5 9.2 add_convert_fusion.1
  257.2 51.2 %all-reduce.10.cloned.1.call-done = bf16[512,2048]{1,0:T(8,128)(2,1)} async-done(((bf16[512,2048]{1,0:T(8,128)(2,1)}), bf16[512,2048]{1,0:T(8,128)(2,1)}) %all-reduce.10.cloned.1.call-update) | async-done | bytes 2097168 | tf_op jit(solution)/shard_map/psum | solution.py:436
  308.4 4.6 fusion.13
  313.1 4.2 convolution_convert_fusion.9.gm_ref
  317.3 19.9 %attention_backward.1 = (bf16[512,512]{1,0:T(8,128)(2,1)}, bf16[4096,512]{1,0:T(8,128)(2,1)}) custom-call(s32[32]{0:T(128)} %order_ref.3, s32[8]{0:T(128)} %cont_ref.3, s32[1]{0:T(128)} %bitcast.first_ref, bf16[512,512]{1,0:T(8,128)(2,1)} %fusion.21.q_ref, bf16[4096,512]{1,0:T(8,128)(2,1)} %all-gather.2.cloned.1.call-done.kv_ref, ...), custom_call_target="tpu_custom_call" | custom-call | flops 5368709120 | bytes 10485760 | tf_op jit(solution)/shard_map/attention_backward/pallas_call | solution.py:345
  338.8 6.5 convolution_convert_fusion.3
  345.3 2.3 reshape.285
  351.7 2.7 convolution_convert_fusion.4
  354.6 9.9 convolution_convert_fusion.5
  364.5 66.3 %reduce-scatter.9.cloned.1.call-done = bf16[512,512]{1,0:T(8,128)(2,1)} async-done(((bf16[4096,512]{1,0:T(8,128)(2,1)}), bf16[512,512]{1,0:T(8,128)(2,1)}) %reduce-scatter.9.cloned.1.call-update) | async-done | bytes 524304 | tf_op jit(solution)/shard_map/reduce_scatter | solution.py:448
  439.4 2.6 add_convert_fusion
  442.1 2.0 convolution_convert_fusion.8
  446.5 10.0 convolution_convert_fusion.2
  456.6 10.0 convolution_convert_fusion.1
  467.0 10.1 convolution_convert_fusion
  478.4 24.9 %reduce-scatter.17.cloned.1.call-done = bf16[512,256]{1,0:T(8,128)(2,1)} async-done(((bf16[512,2048]{1,0:T(8,128)(2,1)}), bf16[512,256]{1,0:T(8,128)(2,1)}) %reduce-scatter.17.cloned.1.call-update) | async-done | bytes 262160 | tf_op jit(solution)/shard_map/reduce_scatter | solution.py:497
  505.0 69.5 %reduce-scatter.11.cloned.1.call-done = bf16[256,512]{1,0:T(8,128)(2,1)} async-done(((bf16[2048,512]{1,0:T(8,128)(2,1)}), bf16[256,512]{1,0:T(8,128)(2,1)}) %reduce-scatter.11.cloned.1.call-update) | async-done | bytes 262160 | tf_op jit(solution)/shard_map/reduce_scatter | solution.py:488
  576.3 86.0 %all-reduce.12.cloned.1.call-done = (bf16[512,2048]{1,0:T(8,128)(2,1)}, bf16[512,2048]{1,0:T(8,128)(2,1)}) async-done(((bf16[512,2048]{1,0:T(8,128)(2,1)}, bf16[512,2048]{1,0:T(8,128)(2,1)}), (bf16[512,2048]{1,0:T(8,128)(2,1)}, bf16[512,2048]{1,0:T(8,128)(2,1)})) %all-reduce.12.cloned.1.call-update) | async-done | bytes 4194320 | tf_op jit(solution)/shard_map/psum | solution.py:428
  662.4 2.9 fusion.16
  665.4 64.1 %reduce-scatter.13.cloned.1.call-done = bf16[256,256]{1,0:T(8,128)(2,1)} async-done(((bf16[2048,256]{1,0:T(8,128)(2,1)}), bf16[256,256]{1,0:T(8,128)(2,1)}) %reduce-scatter.13.cloned.1.call-update) | async-done | bytes 131088 | tf_op jit(solution)/shard_map/reduce_scatter | solution.py:491
  731.1 64.5 %reduce-scatter.15.cloned.1.call-done = bf16[256,256]{1,0:T(8,128)(2,1)} async-done(((bf16[2048,256]{1,0:T(8,128)(2,1)}), bf16[256,256]{1,0:T(8,128)(2,1)}) %reduce-scatter.15.cloned.1.call-update) | async-done | bytes 131088 | tf_op jit(solution)/shard_map/reduce_scatter | solution.py:494
  797.3 19.7 %all-reduce.2 = (bf16[8,64]{1,0:T(8,128)(2,1)S(1)}, bf16[8,64]{1,0:T(8,128)(2,1)S(1)}) all-reduce(bf16[8,64]{1,0:T(8,128)(2,1)S(1)} %bitcast.141, bf16[8,64]{1,0:T(8,128)(2,1)S(1)} %bitcast.140), channel_id=3, replica_groups=mesh['ctx'=8,'tp'=4] {'ctx'}, use_global_device_ids=true, to_apply=%region_10.11.clone | all-reduce | flops 1024 | bytes 4096
  819.3 8.4 fusion.9
  827.7 119.5 %reduce-scatter.19.cloned.1.call-done = bf16[256,2048]{1,0:T(8,128)(2,1)} async-done(((bf16[2048,2048]{1,0:T(8,128)(2,1)}), bf16[256,2048]{1,0:T(8,128)(2,1)}) %reduce-scatter.19.cloned.1.call-update) | async-done | bytes 1048592 | tf_op jit(solution)/shard_map/reduce_scatter | solution.py:503
  947.2 2.8 convert_element_type.193
  949.9 149.3 %reduce-scatter.21.cloned.1.call-done = bf16[256,2048]{1,0:T(8,128)(2,1)} async-done(((bf16[2048,2048]{1,0:T(8,128)(2,1)}), bf16[256,2048]{1,0:T(8,128)(2,1)}) %reduce-scatter.21.cloned.1.call-update) | async-done | bytes 1048592 | tf_op jit(solution)/shard_map/reduce_scatter | solution.py:506
  1099.3 2.8 convert_element_type.195
  1102.1 149.1 %reduce-scatter.23.cloned.1.call-done = bf16[2048,256]{1,0:T(8,128)(2,1)} async-done(((bf16[2048,2048]{1,0:T(8,128)(2,1)}), bf16[2048,256]{1,0:T(8,128)(2,1)}) %reduce-scatter.23.cloned.1.call-update) | async-done | bytes 1048592 | tf_op jit(solution)/shard_map/reduce_scatter | solution.py:509
  1251.2 2.7 convert_element_type.197
  (137 shorter events, 48.6 us)
Async XLA Ops:
  7.2 137.7 %copy-start = (bf16[512,2048]{1,0:T(8,128)(2,1)S(1)}, bf16[512,2048]{1,0:T(8,128)(2,1)}, u32[]{:S(2)}) copy-start(bf16[512,2048]{1,0:T(8,128)(2,1)} %param.18) | copy-start | bytes 6291460
  7.2 119.0 %all-gather.2.cloned.1.call-start = ((), (), s32[]{:S(2)}) async-start(), calls=%async_computation.8 | async-start | bytes 4718592 | tf_op jit(solution)/shard_map/all_gather | solution.py:416
  33.3 12.3 copy-start.8
  35.4 6.4 copy-start.19
  49.9 156.2 %all-reduce.8.cloned.1.call-start = ((), (), s32[]{:S(2)}) async-start(), calls=%async_computation.9 | async-start | bytes 4194304 | tf_op jit(solution)/shard_map/psum | solution.py:418
  148.5 60.7 %copy-start.18 = (f32[2048]{0:T(1024)S(1)}, f32[2048]{0:T(1024)}, u32[]{:S(2)}) copy-start(f32[2048]{0:T(1024)} %param.19) | copy-start | bytes 24580
  148.5 159.8 %all-reduce.10.cloned.1.call-start = ((), (), s32[]{:S(2)}) async-start(), calls=%async_computation.10 | async-start | bytes 4194304 | tf_op jit(solution)/shard_map/psum | solution.py:436
  206.1 3.1 copy-start.2
  206.1 3.5 copy-start.5
  209.6 11.6 slice-start
  210.7 10.5 copy-start.12
  210.7 10.5 slice-start.1
  221.2 6.1 copy-start.11
  239.0 8.5 copy-start.22
  239.0 8.5 copy-start.21
  256.7 174.1 %reduce-scatter.9.cloned.1.call-start = ((), (), s32[]{:S(2)}) async-start(), calls=%async_computation.11 | async-start | bytes 4718592 | tf_op jit(solution)/shard_map/reduce_scatter | solution.py:448
  308.4 4.6 copy-start.3
  308.4 4.6 copy-start.6
  308.4 4.7 copy-start.7
  337.2 1.6 copy-start.4
  337.2 166.1 %reduce-scatter.17.cloned.1.call-start = ((), (), s32[]{:S(2)}) async-start(), calls=%async_computation.15 | async-start | bytes 2359296 | tf_op jit(solution)/shard_map/reduce_scatter | solution.py:497
  345.3 229.3 %reduce-scatter.11.cloned.1.call-start = ((), (), s32[]{:S(2)}) async-start(), calls=%async_computation.12 | async-start | bytes 2359296 | tf_op jit(solution)/shard_map/reduce_scatter | solution.py:488
  349.1 1.4 copy-start.15
  350.9 0.8 copy-start.13
  354.4 307.9 %all-reduce.12.cloned.1.call-start = ((), (), s32[]{:S(2)}) async-start(), calls=%async_computation.19 | async-start | bytes 8388608 | tf_op jit(solution)/shard_map/psum | solution.py:428
  433.5 3.2 copy-start.9
  434.8 2.2 copy-start.16
  436.7 1.2 copy-start.17
  437.7 1.6 copy-start.10
  437.8 1.7 copy-start.14
  442.1 287.4 %reduce-scatter.13.cloned.1.call-start = ((), (), s32[]{:S(2)}) async-start(), calls=%async_computation.13 | async-start | bytes 1179648 | tf_op jit(solution)/shard_map/reduce_scatter | solution.py:491
  444.2 351.5 %reduce-scatter.15.cloned.1.call-start = ((), (), s32[]{:S(2)}) async-start(), calls=%async_computation.14 | async-start | bytes 1179648 | tf_op jit(solution)/shard_map/reduce_scatter | solution.py:494
  446.2 500.9 %reduce-scatter.19.cloned.1.call-start = ((), (), s32[]{:S(2)}) async-start(), calls=%async_computation.16 | async-start | bytes 9437184 | tf_op jit(solution)/shard_map/reduce_scatter | solution.py:503
  456.5 642.7 %reduce-scatter.21.cloned.1.call-start = ((), (), s32[]{:S(2)}) async-start(), calls=%async_computation.17 | async-start | bytes 9437184 | tf_op jit(solution)/shard_map/reduce_scatter | solution.py:506
  466.7 784.5 %reduce-scatter.23.cloned.1.call-start = ((), (), s32[]{:S(2)}) async-start(), calls=%async_computation.18 | async-start | bytes 9437184 | tf_op jit(solution)/shard_map/reduce_scatter | solution.py:509
  477.1 0.7 copy-start.20
  819.3 434.6 %copy-start.1 = (bf16[512,2048]{1,0:T(8,128)(2,1)S(1)}, bf16[512,2048]{1,0:T(8,128)(2,1)}, u32[]{:S(2)}) copy-start(bf16[512,2048]{1,0:T(8,128)(2,1)} %param.18) | copy-start | bytes 6291460
Sparse Core Ops, SparseCore 0:
  50.1 76.0 all-gather.1
  148.7 57.4 all-reduce.7
  256.9 51.4 all-reduce.9
  337.3 93.4 reduce-scatter.8
  435.2 68.0 reduce-scatter.16
  507.6 66.8 reduce-scatter.10
  577.7 84.6 all-reduce.11
  665.8 63.6 reduce-scatter.12
  733.3 62.3 reduce-scatter.14
  799.1 147.9 reduce-scatter.18
  951.2 148.0 reduce-scatter.20
  1102.8 148.3 reduce-scatter.22

commit v2 on v1

v2 whole, which is shorter than its diff:
```python
import functools
import math

import jax
import jax.numpy as jnp
import numpy as np
from jax import lax
from jax.experimental import pallas as pl
from jax.experimental.pallas import tpu as pltpu
from jax.sharding import PartitionSpec as P

HEAD_SIZE = 128
PROMPT = 2048
CONT_LEN = 256
CONTS = 8
BLOCK = 128
PER_PROMPT = PROMPT // BLOCK
PER_CONT = CONT_LEN // BLOCK
LOG2E = 1.4426950408889634
NEG = -1e30
SLOTS = 4

eps_norm = 1e-05
rope_base = 1000000.0

SLOT_XOR = (0, 2, 1, 3)


def plain_dot(left, right):
    return jnp.dot(left, right, preferred_element_type=jnp.float32)


def left_dot(left, right):
    return lax.dot_general(
        left, right, (((0,), (0,)), ((), ())), preferred_element_type=jnp.float32
    )


def right_dot(left, right):
    return lax.dot_general(
        left, right, (((1,), (1,)), ((), ())), preferred_element_type=jnp.float32
    )


def slot_quarter(slot, tensor):
    return ((slot & 1) * 2 + lax.shift_right_logical(slot, 1)) ^ tensor


def stored_block(index, tensor):
    return (index & ~3) + slot_quarter(index & 3, tensor)


def block_plan(order_ref, cont_ref, where_ref, slot):
    count = cont_ref.shape[0]
    prompt_blocks = count // CONTS * PER_PROMPT
    own = order_ref[where_ref[0] * SLOTS + slot_quarter(slot, where_ref[1])]
    is_prompt = own < prompt_blocks
    offset = own - prompt_blocks
    which = jnp.clip(lax.div(offset, PER_CONT), 0, count - 1)
    group = jnp.where(is_prompt, lax.div(own, PER_PROMPT), cont_ref[which])
    inner = jnp.where(is_prompt, lax.rem(own, PER_PROMPT), lax.rem(offset, PER_CONT))
    has_prev = lax.rem(inner, 2)
    pairs = jnp.where(is_prompt, lax.div(inner, 2), PER_PROMPT // 2)
    prev = own - has_prev
    return group * PER_PROMPT, pairs, prev, own, has_prev


def fill_inverse(order_ref, where_ref, inverse_ref):
    def put(index, carry):
        inverse_ref[order_ref[stored_block(index, where_ref[1])]] = index
        return carry

    lax.fori_loop(0, order_ref.shape[0], put, 0)


def rotate(vec, cosine, sine):
    return vec * cosine + pltpu.roll(vec, HEAD_SIZE // 2, 1) * sine


def unrotate(vec, cosine, sine):
    return vec * cosine + pltpu.roll(vec * sine, HEAD_SIZE // 2, 1)


def angle_tables():
    half = HEAD_SIZE // 2
    freq = np.float64(rope_base) ** (-(2.0 * np.arange(half) / HEAD_SIZE))
    freq = np.concatenate([freq, freq])
    starts = np.arange(-(-(PER_PROMPT + PER_CONT) // 8) * 8) * BLOCK
    start = starts[:, None] * freq[None]
    inner = np.arange(BLOCK)[:, None] * freq[None]
    return tuple(
        f(a).astype(np.float32) for a in (start, inner) for f in (np.cos, np.sin)
    )


def key_rows(inverse_ref, logical):
    return pl.ds(pl.multiple_of(inverse_ref[logical] * BLOCK, BLOCK), BLOCK)


def tile_pair(ref, rows_a, rows_b, column):
    cols = pl.ds(column, HEAD_SIZE)
    return jnp.concatenate([ref[rows_a, cols], ref[rows_b, cols]], axis=0)


def own_mask(has_prev, rep):
    shape = (2 * BLOCK, rep * BLOCK)
    row = lax.broadcasted_iota(jnp.int32, shape, 0)
    col = lax.broadcasted_iota(jnp.int32, shape, 1)
    first_row = BLOCK * (1 - has_prev)
    return (row >= first_row) & (row - BLOCK <= lax.rem(col, BLOCK))


def stack_t(ref, rows, column, rep):
    return jnp.concatenate(
        [ref[rows, pl.ds(column + r * HEAD_SIZE, HEAD_SIZE)].T for r in range(rep)], axis=1
    )


def stack_rows(ref, rows, column, rep):
    return jnp.concatenate(
        [ref[rows, pl.ds(column + r * HEAD_SIZE, HEAD_SIZE)] for r in range(rep)], axis=0
    )


def dot(left, right):
    return jnp.dot(left, right, preferred_element_type=jnp.float32)


def forward_kernel(rep, hps, order_ref, cont_ref, where_ref, q_ref, kv_ref, out_ref, lse_ref,
                   inverse_ref, qt_ref, acc_ref):
    fill_inverse(order_ref, where_ref, inverse_ref)
    q_blocks = q_ref.shape[0] // BLOCK
    factor = LOG2E / math.sqrt(HEAD_SIZE)
    width = rep * HEAD_SIZE

    def one_query_block(qb, carry):
        base, pairs, prev, own, has_prev = block_plan(order_ref, cont_ref, where_ref, qb)
        rows = pl.ds(pl.multiple_of(qb * BLOCK, BLOCK), BLOCK)
        mask = own_mask(has_prev, rep)
        rows_a, rows_b = key_rows(inverse_ref, prev), key_rows(inverse_ref, own)
        state = []
        for h in range(hps):
            qt = stack_t(q_ref, rows, h * width, rep)
            qt_ref[h] = qt
            scores = dot(tile_pair(kv_ref, rows_a, rows_b, 2 * h * HEAD_SIZE), qt) * factor
            scores = jnp.where(mask, scores, NEG)
            best = jnp.max(scores, axis=0, keepdims=True)
            weights = jnp.exp2(scores - best)
            total = jnp.sum(weights, axis=0, keepdims=True)
            values = tile_pair(kv_ref, rows_a, rows_b, (2 * h + 1) * HEAD_SIZE)
            acc_ref[h] = dot(values.T, weights.astype(jnp.bfloat16))
            state += [best, total]

        def one_pair(t, state):
            rows_a = key_rows(inverse_ref, base + 2 * t)
            rows_b = key_rows(inverse_ref, base + 2 * t + 1)
            after = []
            for h in range(hps):
                best, total = state[2 * h], state[2 * h + 1]
                keys = tile_pair(kv_ref, rows_a, rows_b, 2 * h * HEAD_SIZE)
                scores = dot(keys, qt_ref[h]) * factor
                newest = jnp.maximum(best, jnp.max(scores, axis=0, keepdims=True))
                weights = jnp.exp2(scores - newest)
                shrink = jnp.exp2(best - newest)
                total = total * shrink + jnp.sum(weights, axis=0, keepdims=True)
                values = tile_pair(kv_ref, rows_a, rows_b, (2 * h + 1) * HEAD_SIZE)
                acc_ref[h] = acc_ref[h] * shrink + dot(values.T, weights.astype(jnp.bfloat16))
                after += [newest, total]
            return tuple(after)

        state = lax.fori_loop(0, pairs, one_pair, tuple(state))
        for h in range(hps):
            best, total = state[2 * h], state[2 * h + 1]
            mixed = acc_ref[h] * (1.0 / total)
            for r in range(rep):
                part = mixed[:, r * BLOCK : (r + 1) * BLOCK]
                out_ref[rows, pl.ds(h * width + r * HEAD_SIZE, HEAD_SIZE)] = part.T.astype(
                    jnp.bfloat16
                )
            lse_ref[0, h, pl.ds(qb, 1), :] = best + jnp.log2(total)
        return carry

    lax.fori_loop(0, q_blocks, one_query_block, 0)


def backward_kernel(rep, hps, order_ref, cont_ref, where_ref, q_ref, kv_ref, gm_ref, mix_ref,
                    lse_ref, cos_ref, sin_ref, gq_ref, keep_ref, send_ref, inverse_ref, qt_ref, gmt_ref, gqt_ref, acc_ref):
    fill_inverse(order_ref, where_ref, inverse_ref)
    q_blocks = q_ref.shape[0] // BLOCK
    scale = 1.0 / math.sqrt(HEAD_SIZE)
    factor = LOG2E * scale
    width = rep * HEAD_SIZE

    def clear(i, carry):
        acc_ref[pl.ds(pl.multiple_of(i * BLOCK, BLOCK), BLOCK), :] = jnp.zeros(
            (BLOCK, acc_ref.shape[1]), jnp.float32
        )
        return carry

    lax.fori_loop(0, order_ref.shape[0], clear, 0)

    def tile_terms(h, rows_a, rows_b, lse, delta, q_rows, gm_rows, mask):
        kcol, vcol = 2 * h * HEAD_SIZE, (2 * h + 1) * HEAD_SIZE
        keys = tile_pair(kv_ref, rows_a, rows_b, kcol)
        values = tile_pair(kv_ref, rows_a, rows_b, vcol)
        weights = jnp.exp2(dot(keys, qt_ref[h]) * factor - lse)
        if mask is not None:
            weights = jnp.where(mask, weights, 0.0)
        grad_weights = dot(values, gmt_ref[h])
        grad_scores = (weights * (grad_weights - delta)).astype(jnp.bfloat16)
        gv = dot(weights.astype(jnp.bfloat16), gm_rows)
        gk = dot(grad_scores, q_rows)
        acc_ref[rows_a, pl.ds(kcol, HEAD_SIZE)] += gk[:BLOCK]
        acc_ref[rows_b, pl.ds(kcol, HEAD_SIZE)] += gk[BLOCK:]
        acc_ref[rows_a, pl.ds(vcol, HEAD_SIZE)] += gv[:BLOCK]
        acc_ref[rows_b, pl.ds(vcol, HEAD_SIZE)] += gv[BLOCK:]
        return dot(keys.T, grad_scores)

    def one_query_block(qb, carry):
        base, pairs, prev, own, has_prev = block_plan(order_ref, cont_ref, where_ref, qb)
        rows = pl.ds(pl.multiple_of(qb * BLOCK, BLOCK), BLOCK)
        mask = own_mask(has_prev, rep)
        rows_a, rows_b = key_rows(inverse_ref, prev), key_rows(inverse_ref, own)
        deltas, lses, q_stack, gm_stack = [], [], [], []
        for h in range(hps):
            qt_ref[h] = stack_t(q_ref, rows, h * width, rep)
            gmt = stack_t(gm_ref, rows, h * width, rep)
            gmt_ref[h] = gmt
            mixt = stack_t(mix_ref, rows, h * width, rep)
            deltas.append(
                jnp.sum(
                    gmt.astype(jnp.float32) * mixt.astype(jnp.float32), axis=0, keepdims=True
                )
            )
            lses.append(lse_ref[0, h, pl.ds(qb, 1), :])
        for h in range(hps):
            q_rows = stack_rows(q_ref, rows, h * width, rep)
            gm_rows = stack_rows(gm_ref, rows, h * width, rep)
            gqt_ref[h] = tile_terms(
                h, rows_a, rows_b, lses[h], deltas[h], q_rows, gm_rows, mask
            )

        def one_pair(t, carry):
            rows_a = key_rows(inverse_ref, base + 2 * t)
            rows_b = key_rows(inverse_ref, base + 2 * t + 1)
            for h in range(hps):
                q_rows = stack_rows(q_ref, rows, h * width, rep)
                gm_rows = stack_rows(gm_ref, rows, h * width, rep)
                gqt_ref[h] += tile_terms(
                    h, rows_a, rows_b, lses[h], deltas[h], q_rows, gm_rows, None
                )
            return carry

        lax.fori_loop(0, pairs, one_pair, 0)
        for h in range(hps):
            total = gqt_ref[h] * scale
            for r in range(rep):
                part = total[:, r * BLOCK : (r + 1) * BLOCK]
                rounded = part.T.astype(jnp.bfloat16).astype(jnp.float32)
                gq_ref[rows, pl.ds(h * width + r * HEAD_SIZE, HEAD_SIZE)] = unrotate(
                    rounded, cos_ref[rows, :], sin_ref[rows, :]
                ).astype(jnp.bfloat16)
        return carry

    lax.fori_loop(0, q_blocks, one_query_block, 0)

    blocks = order_ref.shape[0]
    ctx_count = blocks // SLOTS

    def place(index):
        chunk = lax.div(index, SLOTS) ^ where_ref[0]
        spot = (chunk & 1) * (ctx_count // 2) + (chunk & 2) // 2 * (ctx_count // 4) + (
            lax.shift_right_logical(chunk, 2)
        )
        return spot * SLOTS + (index & 3)

    def flush(i, carry):
        rows = pl.ds(pl.multiple_of(i * BLOCK, BLOCK), BLOCK)
        spot = place(i)
        parts = []
        for h in range(hps):
            parts.append(acc_ref[rows, pl.ds(2 * h * HEAD_SIZE, HEAD_SIZE)] * scale)
            parts.append(acc_ref[rows, pl.ds((2 * h + 1) * HEAD_SIZE, HEAD_SIZE)])
        value = jnp.concatenate(parts, axis=1).astype(jnp.bfloat16)

        @pl.when(spot < blocks // 2)
        def _():
            keep_ref[pl.ds(pl.multiple_of(spot * BLOCK, BLOCK), BLOCK), :] = value

        @pl.when(spot >= blocks // 2)
        def _():
            far = (spot - blocks // 2) * BLOCK
            send_ref[pl.ds(pl.multiple_of(far, BLOCK), BLOCK), :] = value

        return carry

    lax.fori_loop(0, blocks, flush, 0)


def attention_sizes(q, kv):
    kv_heads = kv.shape[1] // (2 * HEAD_SIZE)
    rep = q.shape[1] // HEAD_SIZE // kv_heads
    hps = kv_heads if kv.shape[0] <= 8192 else 1
    return kv_heads, rep, hps


def attention_forward(q, kv, order, cont, where):
    kv_heads, rep, hps = attention_sizes(q, kv)
    rows, tokens = q.shape[0], kv.shape[0]
    q_blocks = rows // BLOCK
    wide = hps * rep * HEAD_SIZE
    q_spec = pl.BlockSpec((rows, wide), lambda g, *_: (0, g))
    flops = 4 * rows * (tokens // 2) * q.shape[1]
    return pl.pallas_call(
        functools.partial(forward_kernel, rep, hps),
        out_shape=(
            jax.ShapeDtypeStruct(q.shape, jnp.bfloat16),
            jax.ShapeDtypeStruct((kv_heads // hps, hps, q_blocks, rep * BLOCK), jnp.float32),
        ),
        grid_spec=pltpu.PrefetchScalarGridSpec(
            num_scalar_prefetch=3,
            grid=(kv_heads // hps,),
            in_specs=[
                q_spec,
                pl.BlockSpec((tokens, 2 * hps * HEAD_SIZE), lambda g, *_: (0, g)),
            ],
            out_specs=[
                q_spec,
                pl.BlockSpec((1, hps, q_blocks, rep * BLOCK), lambda g, *_: (g, 0, 0, 0)),
            ],
            scratch_shapes=[
                pltpu.SMEM((order.shape[0],), jnp.int32),
                pltpu.VMEM((hps, HEAD_SIZE, rep * BLOCK), jnp.bfloat16),
                pltpu.VMEM((hps, HEAD_SIZE, rep * BLOCK), jnp.float32),
            ],
        ),
        compiler_params=pltpu.CompilerParams(vmem_limit_bytes=56 << 20),
        cost_estimate=pl.CostEstimate(
            flops=flops, bytes_accessed=2 * (q.size * 2 + kv.size), transcendentals=flops // 512
        ),
        name="attention_forward",
    )(order, cont, where, q, kv)


def attention_backward(head, q, kv, grad_mixed, mixed, lse, cosine, sine, order, cont, where):
    kv_heads, rep, _ = attention_sizes(q, kv)
    hps_forward = lse.shape[1]
    rows, tokens = q.shape[0], kv.shape[0]
    q_blocks = rows // BLOCK
    wide = rep * HEAD_SIZE
    q_spec = pl.BlockSpec((rows, wide), lambda g, *_: (0, head))
    kv_spec = pl.BlockSpec((tokens, 2 * HEAD_SIZE), lambda g, *_: (0, head))
    lse_spec = pl.BlockSpec(
        (1, 1, q_blocks, rep * BLOCK),
        lambda g, *_: (head // hps_forward, head % hps_forward, 0, 0),
    )
    whole = lambda g, *_: (0, 0)
    table_spec = pl.BlockSpec((rows, HEAD_SIZE), whole)
    half = (tokens // 2, 2 * HEAD_SIZE)
    flops = 10 * rows * (tokens // 2) * wide
    return pl.pallas_call(
        functools.partial(backward_kernel, rep, 1),
        out_shape=(
            jax.ShapeDtypeStruct((rows, wide), jnp.bfloat16),
            jax.ShapeDtypeStruct(half, jnp.bfloat16),
            jax.ShapeDtypeStruct(half, jnp.bfloat16),
        ),
        grid_spec=pltpu.PrefetchScalarGridSpec(
            num_scalar_prefetch=3,
            grid=(1,),
            in_specs=[q_spec, kv_spec, q_spec, q_spec, lse_spec, table_spec, table_spec],
            out_specs=[
                pl.BlockSpec((rows, wide), whole),
                pl.BlockSpec(half, whole),
                pl.BlockSpec(half, whole),
            ],
            scratch_shapes=[
                pltpu.SMEM((order.shape[0],), jnp.int32),
                pltpu.VMEM((1, HEAD_SIZE, rep * BLOCK), jnp.bfloat16),
                pltpu.VMEM((1, HEAD_SIZE, rep * BLOCK), jnp.bfloat16),
                pltpu.VMEM((1, HEAD_SIZE, rep * BLOCK), jnp.float32),
                pltpu.VMEM((tokens, 2 * HEAD_SIZE), jnp.float32),
            ],
        ),
        compiler_params=pltpu.CompilerParams(vmem_limit_bytes=56 << 20),
        cost_estimate=pl.CostEstimate(
            flops=flops,
            bytes_accessed=4 * (rows * wide * 2 + tokens * 2 * HEAD_SIZE),
            transcendentals=flops // 1280,
        ),
        name=f"attention_backward_{head}",
    )(order, cont, where, q, kv, grad_mixed, mixed, lse, cosine, sine)


def input_kernel(order_ref, cont_ref, where_ref, x_ref, gain_ref, wq_ref, wk_ref, wv_ref,
                 cos_start_ref, sin_start_ref, cos_in_ref, sin_in_ref,
                 first_ref, q_ref, kv_ref, cos_ref, sin_ref):
    count = cont_ref.shape[0]
    prompt_blocks = count // CONTS * PER_PROMPT
    lane = lax.broadcasted_iota(jnp.int32, (BLOCK, HEAD_SIZE), 1)

    def one_slot(slot, carry):
        quarter = slot_quarter(slot, where_ref[1])
        rows = pl.ds(pl.multiple_of(slot * BLOCK, BLOCK), BLOCK)
        full = x_ref[pl.ds(pl.multiple_of(quarter * BLOCK, BLOCK), BLOCK), :].astype(jnp.float32)
        inv = lax.rsqrt(jnp.mean(full * full, axis=-1, keepdims=True) + eps_norm)
        first_ref[rows, :] = (full * inv * gain_ref[...]).astype(jnp.bfloat16)
        own = order_ref[where_ref[0] * SLOTS + quarter]
        spot = jnp.where(
            own < prompt_blocks,
            lax.rem(own, PER_PROMPT),
            PER_PROMPT + lax.rem(own - prompt_blocks, PER_CONT),
        )
        cos_start, sin_start = cos_start_ref[pl.ds(spot, 1), :], sin_start_ref[pl.ds(spot, 1), :]
        cos_in, sin_in = cos_in_ref[...], sin_in_ref[...]
        sine = sin_start * cos_in + cos_start * sin_in
        cos_ref[rows, :] = cos_start * cos_in - sin_start * sin_in
        sin_ref[rows, :] = jnp.where(lane < HEAD_SIZE // 2, -sine, sine)
        return carry

    lax.fori_loop(0, SLOTS, one_slot, 0)
    first = first_ref[...]
    cosine, sine = cos_ref[...], sin_ref[...]
    kv_heads = wk_ref.shape[1] // HEAD_SIZE
    for h in range(kv_heads):
        cols = slice(h * HEAD_SIZE, (h + 1) * HEAD_SIZE)
        key = rotate(plain_dot(first, wk_ref[:, cols]), cosine, sine)
        value = plain_dot(first, wv_ref[:, cols])
        kv_ref[:, 2 * h * HEAD_SIZE : (2 * h + 1) * HEAD_SIZE] = key.astype(jnp.bfloat16)
        kv_ref[:, (2 * h + 1) * HEAD_SIZE : (2 * h + 2) * HEAD_SIZE] = value.astype(jnp.bfloat16)
    for h in range(wq_ref.shape[1] // HEAD_SIZE):
        cols = slice(h * HEAD_SIZE, (h + 1) * HEAD_SIZE)
        query = rotate(plain_dot(first, wq_ref[:, cols]), cosine, sine)
        q_ref[:, cols] = query.astype(jnp.bfloat16)


def input_stage(x, gain, wq, wk, wv, order, cont, where):
    rows, model = x.shape
    tables = angle_tables()
    smem = pl.BlockSpec(memory_space=pltpu.SMEM)
    vmem = pl.BlockSpec(memory_space=pltpu.VMEM)
    flops = 2 * rows * model * (wq.shape[1] + 2 * wk.shape[1])
    return pl.pallas_call(
        input_kernel,
        out_shape=(
            jax.ShapeDtypeStruct((rows, model), jnp.bfloat16),
            jax.ShapeDtypeStruct((rows, wq.shape[1]), jnp.bfloat16),
            jax.ShapeDtypeStruct((rows, 2 * wk.shape[1]), jnp.bfloat16),
            jax.ShapeDtypeStruct((rows, HEAD_SIZE), jnp.float32),
            jax.ShapeDtypeStruct((rows, HEAD_SIZE), jnp.float32),
        ),
        in_specs=[smem] * 3 + [vmem] * 9,
        out_specs=[vmem] * 5,
        compiler_params=pltpu.CompilerParams(vmem_limit_bytes=40 << 20),
        cost_estimate=pl.CostEstimate(
            flops=flops, bytes_accessed=4 * x.size + 2 * wq.size + 4 * wk.size, transcendentals=0
        ),
        name="input_stage",
    )(order, cont, where, x, gain.reshape(1, -1), wq, wk, wv, *tables)


def kv_finish_kernel(keep_ref, got_ref, cos_ref, sin_ref, gk_ref, gv_ref):
    total = keep_ref[...].astype(jnp.float32) + got_ref[...].astype(jnp.float32)
    total = total.astype(jnp.bfloat16)
    key = total[:, :HEAD_SIZE].astype(jnp.float32)
    gk_ref[...] = unrotate(key, cos_ref[...], sin_ref[...]).astype(jnp.bfloat16)
    gv_ref[...] = total[:, HEAD_SIZE:]


def kv_finish(keep, got, cosine, sine):
    rows = keep.shape[0]
    vmem = pl.BlockSpec(memory_space=pltpu.VMEM)
    shape = jax.ShapeDtypeStruct((rows, HEAD_SIZE), jnp.bfloat16)
    return pl.pallas_call(
        kv_finish_kernel,
        out_shape=(shape, shape),
        in_specs=[vmem] * 4,
        out_specs=[vmem] * 2,
        cost_estimate=pl.CostEstimate(
            flops=8 * keep.size, bytes_accessed=6 * keep.size, transcendentals=0
        ),
        name="kv_finish",
    )(keep, got, cosine, sine)


def flip(value, axis, mask):
    return lax.ppermute(value, axis, [(i, i ^ mask) for i in range(lax.axis_size(axis))])


def add(left, right):
    return (left.astype(jnp.float32) + right.astype(jnp.float32)).astype(jnp.bfloat16)


def slots_of(value, tensor):
    rows = value.shape[0] // SLOTS
    return jnp.concatenate(
        [
            lax.dynamic_slice_in_dim(value, (tensor ^ SLOT_XOR[u]) * rows, rows)
            for u in range(SLOTS)
        ]
    )


def gather_slots(own):
    other = flip(own, "tp", 2)
    return jnp.concatenate([own, other, flip(own, "tp", 1), flip(other, "tp", 1)])


def gather_rows(own, tensor):
    rows = own.shape[0]
    other = flip(own, "tp", 2)
    pieces = (own, other, flip(own, "tp", 1), flip(other, "tp", 1))
    result = jnp.zeros((SLOTS * rows,) + own.shape[1:], own.dtype)
    for u in range(SLOTS):
        result = lax.dynamic_update_slice_in_dim(
            result, pieces[u], (tensor ^ SLOT_XOR[u]) * rows, 0
        )
    return result


def scatter_slots(partial):
    half = partial.shape[0] // 2
    pair = add(partial[:half], flip(partial[half:], "tp", 1))
    quarter = half // 2
    return pair[:quarter], flip(pair[quarter:], "tp", 2)


def high_masks(ctx_count):
    masks, mask = [], ctx_count // 2
    while mask >= 4:
        masks.append(mask)
        mask //= 2
    return masks


def step(parts, axis_bits, mask, index):
    mine = lax.dynamic_index_in_dim(parts, index, axis_bits, keepdims=False)
    away = lax.dynamic_index_in_dim(parts, 1 - index, axis_bits, keepdims=False)
    return mine, flip(away, "ctx", mask)


def bits_of(ctx, ctx_count):
    return [(ctx // mask) % 2 for mask in high_masks(ctx_count)]


def reduce_attention(partial, ctx, ctx_count):
    highs = high_masks(ctx_count)
    width = partial.shape[1]
    rows = partial.shape[0] // ctx_count
    shaped = partial.astype(jnp.bfloat16).reshape((2,) * len(highs) + (2, 2, rows, width))
    mine, got = step(shaped, len(highs) + 1, 1, ctx % 2)
    shaped = add(mine, got)
    mine, got = step(shaped, len(highs), 2, ctx // 2 % 2)
    for mask, bit in zip(highs, bits_of(ctx, ctx_count)):
        shaped = add(mine, got)
        mine, got = step(shaped, 0, mask, bit)
    return mine.astype(jnp.float32) + got.astype(jnp.float32)


def reduce_ffn(partial, ctx, ctx_count):
    highs = high_masks(ctx_count)
    width = partial.shape[1]
    rows = partial.shape[0] // ctx_count
    shaped = partial.astype(jnp.bfloat16).reshape((2,) * len(highs) + (2, 2, rows, width))
    mine, got = step(shaped, len(highs) + 1, 1, ctx % 2)
    for mask, bit in zip(highs, bits_of(ctx, ctx_count)):
        shaped = add(mine, got)
        mine, got = step(shaped, 0, mask, bit)
    shaped = add(mine, got)
    pair = ctx // 2 % 2
    mine, got = step(shaped, 0, 2, pair)
    low, high = jnp.where(pair == 0, mine, got), jnp.where(pair == 0, got, mine)
    return jnp.concatenate([low, high], axis=1).astype(jnp.float32)


def reduce_kv(keep, send, ctx_count):
    got = flip(send, "ctx", 1)
    for mask in [2] + high_masks(ctx_count):
        total = add(keep, got)
        half = total.shape[0] // 2
        keep, got = total[:half], flip(total[half:], "ctx", mask)
    return keep, got


def norm_back(grad_out, normed, inv_scale, gain):
    scaled = grad_out * gain
    inner = jnp.mean(scaled * normed, axis=-1, keepdims=True)
    return (inv_scale * (scaled - normed * inner), jnp.sum(grad_out * normed, axis=0))


def body(
    layer_input,
    attn_gain,
    w_query,
    key_matrix,
    value_matrix,
    w_out,
    ffn_gain,
    w_gate,
    w_up,
    w_down,
    cotangent,
    block_order,
    cont_prompt,
):
    ctx_count = lax.axis_size("ctx")
    tp_count = lax.axis_size("tp")
    ctx, tensor = lax.axis_index("ctx"), lax.axis_index("tp")
    pair = ctx // 2 % 2
    where = jnp.stack([ctx, tensor]).astype(jnp.int32)
    quarter = layer_input.shape[0] // SLOTS
    kv_heads = key_matrix.shape[1] // HEAD_SIZE
    half_units = w_gate.shape[1] // 2

    first_input, queries, kv_local, cosine, sine = input_stage(
        layer_input, attn_gain, w_query, key_matrix, value_matrix, block_order, cont_prompt, where
    )
    kv_all = lax.all_gather(kv_local, "ctx", axis=0, tiled=True)

    gate_half = lax.dynamic_slice_in_dim(w_gate, pair * half_units, half_units, 1)
    up_half = lax.dynamic_slice_in_dim(w_up, pair * half_units, half_units, 1)
    down_half = lax.dynamic_slice_in_dim(w_down, pair * half_units, half_units, 0)
    cot_own = lax.dynamic_slice_in_dim(cotangent, tensor * quarter, quarter)
    cot_rows = jnp.concatenate(
        [slots_of(cotangent, tensor), gather_slots(flip(cot_own, "ctx", 2))]
    )
    grad_hidden = right_dot(cot_rows, down_half)

    mixed, log_total = attention_forward(
        queries, kv_all, block_order, cont_prompt, where
    )
    mine, got = scatter_slots(plain_dot(mixed, w_out).astype(jnp.bfloat16))
    own_input = lax.dynamic_slice_in_dim(layer_input, tensor * quarter, quarter)
    own_input = own_input.astype(jnp.float32)
    middle = own_input + (mine.astype(jnp.float32) + got.astype(jnp.float32))
    inv_two = lax.rsqrt(jnp.mean(middle * middle, axis=-1, keepdims=True) + eps_norm)
    normed_two = middle * inv_two
    second_own = (normed_two * ffn_gain).astype(jnp.bfloat16)
    second_in = jnp.concatenate(
        [gather_slots(second_own), gather_slots(flip(second_own, "ctx", 2))]
    )

    gate = plain_dot(second_in, gate_half)
    upward = plain_dot(second_in, up_half)
    sigma = jax.nn.sigmoid(gate)
    swish = gate * sigma
    hidden = (swish * upward).astype(jnp.bfloat16)
    grad_gate = (grad_hidden * upward * sigma * (1.0 + gate * (1.0 - sigma))).astype(jnp.bfloat16)
    grad_upward = (grad_hidden * swish).astype(jnp.bfloat16)

    sum_down = reduce_ffn(left_dot(cot_rows, hidden), ctx, ctx_count).T
    local = layer_input.shape[0]

    def pair_sum(partial):
        mine, got = scatter_slots(partial[local:])
        away = flip(add(mine, got), "ctx", 2)
        mine, got = scatter_slots(partial[:local])
        return (mine.astype(jnp.float32) + got.astype(jnp.float32)) + away.astype(jnp.float32)

    grad_second = pair_sum(
        (right_dot(grad_gate, gate_half) + right_dot(grad_upward, up_half)).astype(jnp.bfloat16)
    )
    sum_gate = reduce_ffn(left_dot(second_in, grad_gate), ctx, ctx_count)
    sum_up = reduce_ffn(left_dot(second_in, grad_upward), ctx, ctx_count)

    grad_norm_two, ffn_gain_part = norm_back(grad_second, normed_two, inv_two, ffn_gain)
    own_cot = cot_own.astype(jnp.float32)
    grad_middle = own_cot + grad_norm_two
    grad_branch = gather_slots(grad_middle.astype(jnp.bfloat16))
    grad_mixed = right_dot(grad_branch, w_out).astype(jnp.bfloat16)
    sum_out = reduce_attention(left_dot(grad_branch, mixed), ctx, ctx_count).T

    ffn_out = pair_sum(plain_dot(hidden, down_half).astype(jnp.bfloat16))
    output = gather_rows((middle + ffn_out).astype(jnp.bfloat16), tensor)

    grad_queries, grad_keys, grad_values = [], [], []
    for head in range(kv_heads):
        grad_q, keep, send = attention_backward(
            head, queries, kv_all, grad_mixed, mixed, log_total, cosine, sine,
            block_order, cont_prompt, where,
        )
        grad_queries.append(grad_q)
        grad_k, grad_v = kv_finish(*reduce_kv(keep, send, ctx_count), cosine, sine)
        grad_keys.append(grad_k)
        grad_values.append(grad_v)
    grad_query = jnp.concatenate(grad_queries, axis=1)
    grad_key = jnp.concatenate(grad_keys, axis=1)
    grad_value = jnp.concatenate(grad_values, axis=1)
    sum_query = reduce_attention(left_dot(first_input, grad_query), ctx, ctx_count)
    sum_kv = reduce_attention(
        jnp.concatenate(
            [left_dot(first_input, grad_key), left_dot(first_input, grad_value)], axis=1
        ),
        ctx,
        ctx_count,
    )
    sum_key, sum_value = jnp.split(sum_kv, 2, axis=1)
    grad_first_partial = (
        right_dot(grad_query, w_query)
        + right_dot(grad_key, key_matrix)
        + right_dot(grad_value, value_matrix)
    )
    mine, got = scatter_slots(grad_first_partial.astype(jnp.bfloat16))
    grad_first = mine.astype(jnp.float32) + got.astype(jnp.float32)
    inv_one = lax.rsqrt(jnp.mean(own_input * own_input, axis=-1, keepdims=True) + eps_norm)
    grad_norm_one, attn_gain_part = norm_back(grad_first, own_input * inv_one, inv_one, attn_gain)
    grad_input = gather_rows((grad_middle + grad_norm_one).astype(jnp.bfloat16), tensor)

    devices = ctx_count * tp_count
    gains = jnp.stack([attn_gain_part, ffn_gain_part]).reshape(2, devices, -1)
    gains = lax.all_to_all(gains, ("ctx", "tp"), 1, 1, tiled=True)
    gains = jnp.sum(gains, axis=1)
    return (
        output,
        grad_input,
        gains[0],
        sum_query,
        sum_key,
        sum_value,
        sum_out,
        gains[1],
        sum_gate,
        sum_up,
        sum_down,
    )


def solution(mesh):
    placed = (
        P("ctx", None),
        P(),
        P(None, "tp"),
        P(None, "tp"),
        P(None, "tp"),
        P("tp", None),
        P(),
        P(None, "tp"),
        P(None, "tp"),
        P("tp", None),
        P("ctx", None),
        P(),
        P(),
    )
    return jax.shard_map(
        body,
        mesh=mesh,
        in_specs=placed,
        out_specs=(
            P("ctx", None),
            P("ctx", None),
            P(("ctx", "tp")),
            P("ctx", "tp"),
            P("ctx", "tp"),
            P("ctx", "tp"),
            P("tp", "ctx"),
            P(("ctx", "tp")),
            P("ctx", "tp"),
            P("ctx", "tp"),
            P("tp", "ctx"),
        ),
        check_vma=False,
    )
```

time: 1270 us -> 804 us (0.63)
  waiting for transfers between devices: 961 us -> 422 us
  local copies, waits for them, and re-layouts: 26.9 us -> 87.8 us
  starting transfers between devices: 1.75 us -> 59.3 us
  other arithmetic: 77.4 us -> 43.2 us
  Pallas kernels: 38.5 us -> 69.8 us
  matrix products: 121 us -> 94.9 us
  blocking collectives: 19.7 us -> 0 us
    reduce_scatter x8 -> x0, waiting for transfers between devices: 707 us -> none  [the longest x1 149 us: body(): lax.psum_scatter(grad_w_up.astype(jnp.bfloat16), 'ctx', scatter_dimension...]
    ppermute x0 -> x58, waiting for transfers between devices: none -> 343 us  [flip(): lax.ppermute(value, axis, [(i, i ^ mask) for i in range(lax.axis_size(axi...]
    psum x3 -> x0, waiting for transfers between devices: 194 us -> none  [the longest x1 86 us: body(): lax.psum(plain_dot(hidden, w_down).astype(jnp.bfloat16), 'tp')]
    ppermute x0 -> x58, starting transfers between devices: none -> 56.8 us  [flip(): lax.ppermute(value, axis, [(i, i ^ mask) for i in range(lax.axis_size(axi...]
    unnamed x57 -> x153, local copies, waits for them, and re-layouts: 11.9 us -> 48 us
    pallas_call x1 -> x5, Pallas kernels: 19.9 us -> 45.4 us  [the longest x2 35.2 us: attention_backward(): pl.pallas_call(functools.partial(backward_kernel, rep, 1), out_shape=(jax...]
    unnamed x1 -> x0, blocking collectives: 19.7 us -> none
    all_gather x1, waiting for transfers between devices: 58.7 us -> 76.2 us  [body(): kv_all = lax.all_gather(kv_local, 'ctx', axis=0, tiled=True)]
  transfers between devices with their start and end apart: 12 -> 60, of which waited for: 12 -> 28; matrix products, arithmetic and copies ran while one was open for 9% -> 17% of each run, Pallas kernels for 0% -> 5%
where the time goes in v2:
time: 804 us; the launch traced here: 792 us
  waiting for transfers between devices  422 us (52%)
  matrix products  94.9 us (12%)
  local copies, waits for them, and re-layouts  87.8 us (11%)
  Pallas kernels  69.8 us (9%)
  starting transfers between devices  59.3 us (7%)
  other arithmetic  43.2 us (5%)
  between operations  15.6 us (2%)
    ppermute x58, waiting for transfers between devices, flip(): lax.ppermute(value, axis, [(i, i ^ mask) for i in range(lax.axis_size(axi...  343 us
    all_gather x1, waiting for transfers between devices, body(): kv_all = lax.all_gather(kv_local, 'ctx', axis=0, tiled=True)  76.2 us
    ppermute x58, starting transfers between devices, flip(): lax.ppermute(value, axis, [(i, i ^ mask) for i in range(lax.axis_size(axi...  56.8 us
    unnamed x153, local copies, waits for them, and re-layouts  48 us
    dot_general x7, matrix products, right_dot(): lax.dot_general(left, right, (((1,), (1,)), ((), ())), preferred_element_...  37 us
    pallas_call x2, Pallas kernels, attention_backward(): pl.pallas_call(functools.partial(backward_kernel, rep, 1), out_shape=(jax...  35.2 us
    dot_general x7, matrix products, left_dot(): lax.dot_general(left, right, (((0,), (0,)), ((), ())), preferred_element_...  33.2 us
    dot_general x4, matrix products, plain_dot(): return jnp.dot(left, right, preferred_element_type=jnp.float32)  24.6 us
  transfers between devices with their start and end apart: 60, of which 28 were waited for; matrix products, arithmetic and copies ran while one was open for 17% of the time, Pallas kernels for 5%

profile of v2, /device:TPU:0, one launch (start us, length us, event | category | flops | bytes accessed | tf_op | source)
XLA Modules:
  0.0 792.3 jit_solution(5046708860713844302)
XLA Ops:
  18.2 6.2 input_stage.1
  27.9 76.2 %all-gather.2.cloned.1.call-done.kv_ref = bf16[4096,512]{1,0:T(8,128)(2,1)} async-done(((bf16[512,512]{1,0:T(8,128)(2,1)}), bf16[4096,512]{1,0:T(8,128)(2,1)}) %all-gather.2.cloned.1.call-update) | async-done | bytes 4194320 | tf_op jit(solution)/shard_map/all_gather | solution.py:618
  104.2 24.4 %attention_forward.1 = (bf16[512,512]{1,0:T(8,128)(2,1)}, f32[1,2,4,256]{3,2,1,0:T(4,128)}) custom-call(s32[32]{0:T(128)} %order_ref.7, s32[8]{0:T(128)} %cont_ref.7, s32[2]{0:T(128)} %copy-done.19, bf16[512,512]{1,0:T(8,128)(2,1)} %copy-done.23, bf16[4096,512]{1,0:T(8,128)(2,1)} %all-gather.2.cloned.1.call-done.kv_ref), custom_call_target="tpu_custom_call" | custom-call | flops 2147483648 | bytes 5242880 | tf_op jit(solution)/shard_map/attention_forward/pallas_call | solution.py:314
  135.2 5.1 collective-permute-start.17
  142.2 10.8 %collective-permute-done.17 = bf16[128,2048]{1,0:T(8,128)(2,1)} collective-permute-done((bf16[128,2048]{1,0:T(8,128)(2,1)S(1)}, bf16[128,2048]{1,0:T(8,128)(2,1)}, u32[]{:S(2)}, u32[]{:S(2)}) %collective-permute-start.17) | collective-permute-done | bytes 524320 | tf_op jit(solution)/shard_map/ppermute | solution.py:487
  163.5 4.6 collective-permute-done.18
  168.1 10.2 %collective-permute-done.1 = bf16[128,2048]{1,0:T(8,128)(2,1)} collective-permute-done((bf16[128,2048]{1,0:T(8,128)(2,1)}, bf16[128,2048]{1,0:T(8,128)(2,1)}, u32[]{:S(2)}, u32[]{:S(2)}) %collective-permute-start.1) | collective-permute-done | bytes 524320 | tf_op jit(solution)/shard_map/ppermute | solution.py:487
  184.4 8.6 %collective-permute-done.2 = bf16[128,2048]{1,0:T(8,128)(2,1)S(1)} collective-permute-done((bf16[128,2048]{1,0:T(8,128)(2,1)S(1)}, bf16[128,2048]{1,0:T(8,128)(2,1)S(1)}, u32[]{:S(2)}, u32[]{:S(2)}) %collective-permute-start.2) | collective-permute-done | bytes 524320 | tf_op jit(solution)/shard_map/ppermute | solution.py:487
  195.4 12.0 %collective-permute-done.6 = bf16[128,2048]{1,0:T(8,128)(2,1)S(1)} collective-permute-done((bf16[128,2048]{1,0:T(8,128)(2,1)S(1)}, bf16[128,2048]{1,0:T(8,128)(2,1)S(1)}, u32[]{:S(2)}, u32[]{:S(2)}) %collective-permute-start.6) | collective-permute-done | bytes 524320 | tf_op jit(solution)/shard_map/ppermute | solution.py:487
  209.4 7.8 fusion.8
  217.2 6.1 fusion.12
  223.4 10.7 %multiply_convert_fusion = (bf16[1024,1024]{1,0:T(8,128)(2,1)}, bf16[1024,1024]{1,0:T(8,128)(2,1)S(1)}, bf16[1024,1024]{1,0:T(8,128)(2,1)}) fusion(f32[1024,1024]{1,0:T(8,128)} %fusion.12, f32[1024,1024]{1,0:T(8,128)S(1)} %fusion.8, bf16[1024,2048]{1,0:T(8,128)(2,1)S(1)} %constant_dynamic-update-slice_fusion.8, bf16[2048,2048]{1,0:T(8,128)(2,1)} %param.26, ...), kind=kOutput, calls=%fused_computation.8 | convolution fusion | flops 4310695936 | bytes 23068676 | tf_op jit(solution)/shard_map/dot_general | solution.py:40
  234.0 7.3 convolution_convert_fusion
  241.3 8.4 %convolution_convert_fusion.3 = bf16[1024,2048]{1,0:T(8,128)(2,1)} fusion(bf16[1024,1024]{1,0:T(8,128)(2,1)S(1)} %copy-done.61, bf16[2048,2048]{1,0:T(8,128)(2,1)} %param.26, s32[]{:T(128)S(6)} %select_n.177), kind=kOutput, calls=%fused_computation.16 | convolution fusion | flops 4297064448 | bytes 10485764 | tf_op jit(solution)/shard_map/dot_general | solution.py:30
  249.7 4.9 convolution_convert_fusion.1
  254.7 6.9 fusion.10
  261.5 9.8 %add_convert_fusion = bf16[1024,2048]{1,0:T(8,128)(2,1)S(1)} fusion(f32[1024,2048]{1,0:T(8,128)} %fusion.10, bf16[1024,1024]{1,0:T(8,128)(2,1)} %get-tuple-element.83, bf16[2048,2048]{1,0:T(8,128)(2,1)} %param.25, s32[]{:T(128)S(6)} %select_n.177), kind=kOutput, calls=%fused_computation | convolution fusion | flops 4299161600 | bytes 18874372 | tf_op jit(solution)/shard_map/dot_general | solution.py:40
  275.6 15.2 %convolution_convert_fusion.2 = bf16[2048,1024]{1,0:T(8,128)(2,1)S(1)} fusion(bf16[1024,2048]{1,0:T(8,128)(2,1)S(1)} %copy-done.55, bf16[1024,1024]{1,0:T(8,128)(2,1)} %copy-done.58), kind=kOutput, calls=%fused_computation.15 | convolution fusion | flops 4297064448 | bytes 10485760 | tf_op jit(solution)/shard_map/dot_general | solution.py:34
  300.3 10.3 %collective-permute-done.12 = bf16[128,2048]{1,0:T(8,128)(2,1)S(1)} collective-permute-done((bf16[128,2048]{1,0:T(8,128)(2,1)S(1)}, bf16[128,2048]{1,0:T(8,128)(2,1)S(1)}, u32[]{:S(2)}, u32[]{:S(2)}) %collective-permute-start.12) | collective-permute-done | bytes 524320 | tf_op jit(solution)/shard_map/ppermute | solution.py:487
  312.3 9.5 %collective-permute-done.24 = bf16[128,2048]{1,0:T(8,128)(2,1)S(1)} collective-permute-done((bf16[128,2048]{1,0:T(8,128)(2,1)S(1)}, bf16[128,2048]{1,0:T(8,128)(2,1)S(1)}, u32[]{:S(2)}, u32[]{:S(2)}) %collective-permute-start.24) | collective-permute-done | bytes 524320 | tf_op jit(solution)/shard_map/ppermute | solution.py:487
  322.0 9.7 %collective-permute-done.10 = bf16[128,2048]{1,0:T(8,128)(2,1)S(1)} collective-permute-done((bf16[128,2048]{1,0:T(8,128)(2,1)S(1)}, bf16[128,2048]{1,0:T(8,128)(2,1)S(1)}, u32[]{:S(2)}, u32[]{:S(2)}) %collective-permute-start.10) | collective-permute-done | bytes 524320 | tf_op jit(solution)/shard_map/ppermute | solution.py:487
  335.8 3.8 collective-permute-done.52
  342.1 42.3 %collective-permute-done.55 = bf16[2,2,256,1024]{3,2,1,0:T(8,128)(2,1)S(1)} collective-permute-done((bf16[2,2,256,1024]{3,2,1,0:T(8,128)(2,1)S(1)}, bf16[2,2,256,1024]{3,2,1,0:T(8,128)(2,1)S(1)}, u32[]{:S(2)}, u32[]{:S(2)}) %collective-permute-start.55) | collective-permute-done | bytes 2097184 | tf_op jit(solution)/shard_map/ppermute | solution.py:487
  391.8 36.8 %collective-permute-done.49 = bf16[2,2,256,1024]{3,2,1,0:T(8,128)(2,1)S(1)} collective-permute-done((bf16[2,2,256,1024]{3,2,1,0:T(8,128)(2,1)S(1)}, bf16[2,2,256,1024]{3,2,1,0:T(8,128)(2,1)S(1)}, u32[]{:S(2)}, u32[]{:S(2)}) %collective-permute-start.49) | collective-permute-done | bytes 2097184 | tf_op jit(solution)/shard_map/ppermute | solution.py:487
  437.7 4.5 collective-permute-done.26
  442.2 38.8 %collective-permute-done.53 = bf16[2,256,1024]{2,1,0:T(8,128)(2,1)} collective-permute-done((bf16[2,256,1024]{2,1,0:T(8,128)(2,1)S(1)}, bf16[2,256,1024]{2,1,0:T(8,128)(2,1)}, u32[]{:S(2)}, u32[]{:S(2)}) %collective-permute-start.53) | collective-permute-done | bytes 1048608 | tf_op jit(solution)/shard_map/ppermute | solution.py:487
  482.6 20.8 %collective-permute-done.56 = bf16[2,256,1024]{2,1,0:T(8,128)(2,1)} collective-permute-done((bf16[2,256,1024]{2,1,0:T(8,128)(2,1)}, bf16[2,256,1024]{2,1,0:T(8,128)(2,1)}, u32[]{:S(2)}, u32[]{:S(2)}) %collective-permute-start.56) | collective-permute-done | bytes 1048608 | tf_op jit(solution)/shard_map/ppermute | solution.py:487
  512.4 13.3 %collective-permute-done.50 = bf16[2,256,1024]{2,1,0:T(8,128)(2,1)} collective-permute-done((bf16[2,256,1024]{2,1,0:T(8,128)(2,1)}, bf16[2,256,1024]{2,1,0:T(8,128)(2,1)}, u32[]{:S(2)}, u32[]{:S(2)}) %collective-permute-start.50) | collective-permute-done | bytes 1048608 | tf_op jit(solution)/shard_map/ppermute | solution.py:487
  531.7 3.8 convolution_convert_fusion.9.gm_ref
  535.5 17.5 %attention_backward_0.1 = (bf16[512,256]{1,0:T(8,128)(2,1)}, bf16[2048,256]{1,0:T(8,128)(2,1)}, bf16[2048,256]{1,0:T(8,128)(2,1)}) custom-call(s32[32]{0:T(128)} %order_ref.7, s32[8]{0:T(128)} %cont_ref.7, s32[2]{0:T(128)} %copy-done.19, bf16[512,512]{1,0:T(8,128)(2,1)} %copy-done.23, bf16[4096,512]{1,0:T(8,128)(2,1)} %all-gather.2.cloned.1.call-done.kv_ref, ...), custom_call_target="tpu_custom_call" | custom-call | flops 2684354560 | bytes 5242880 | tf_op jit(solution)/shard_map/attention_backward_0/pallas_call | solution.py:361
  554.1 17.7 %attention_backward_1.1 = (bf16[512,256]{1,0:T(8,128)(2,1)}, bf16[2048,256]{1,0:T(8,128)(2,1)}, bf16[2048,256]{1,0:T(8,128)(2,1)}) custom-call(s32[32]{0:T(128)} %order_ref.7, s32[8]{0:T(128)} %cont_ref.7, s32[2]{0:T(128)} %copy-done.19, bf16[512,512]{1,0:T(8,128)(2,1)} %copy-done.23, bf16[4096,512]{1,0:T(8,128)(2,1)} %all-gather.2.cloned.1.call-done.kv_ref, ...), custom_call_target="tpu_custom_call" | custom-call | flops 2684354560 | bytes 5242880 | tf_op jit(solution)/shard_map/attention_backward_1/pallas_call | solution.py:361
  572.7 3.0 convolution_convert_fusion.4
  581.2 3.2 collective-permute-start.46
  590.9 3.3 fusion.53
  607.1 3.1 copy.54
  612.2 3.7 collective-permute-start.47
  615.9 15.3 %collective-permute-done.32 = bf16[2048,256]{1,0:T(8,128)(2,1)} collective-permute-done((bf16[2048,256]{1,0:T(8,128)(2,1)}, bf16[2048,256]{1,0:T(8,128)(2,1)}, u32[]{:S(2)}, u32[]{:S(2)}) %collective-permute-start.32) | collective-permute-done | bytes 1048608 | tf_op jit(solution)/shard_map/ppermute | solution.py:487
  632.8 3.7 collective-permute-start.33
  636.6 17.1 %collective-permute-done.29 = bf16[2048,256]{1,0:T(8,128)(2,1)} collective-permute-done((bf16[2048,256]{1,0:T(8,128)(2,1)}, bf16[2048,256]{1,0:T(8,128)(2,1)}, u32[]{:S(2)}, u32[]{:S(2)}) %collective-permute-start.29) | collective-permute-done | bytes 1048608 | tf_op jit(solution)/shard_map/ppermute | solution.py:487
  655.2 3.7 collective-permute-start.30
  659.0 15.5 %collective-permute-done.40 = bf16[2,2,256,512]{3,2,0,1:T(8,128)(2,1)} collective-permute-done((bf16[2,2,256,512]{3,2,0,1:T(8,128)(2,1)}, bf16[2,2,256,512]{3,2,0,1:T(8,128)(2,1)}, u32[]{:S(2)}, u32[]{:S(2)}) %collective-permute-start.40) | collective-permute-done | bytes 1048608 | tf_op jit(solution)/shard_map/ppermute | solution.py:487
  676.1 3.7 collective-permute-start.41
  685.6 8.5 %collective-permute-done.41 = bf16[2,256,512]{2,1,0:T(8,128)(2,1)S(1)} collective-permute-done((bf16[2,256,512]{2,1,0:T(8,128)(2,1)S(1)}, bf16[2,256,512]{2,1,0:T(8,128)(2,1)S(1)}, u32[]{:S(2)}, u32[]{:S(2)}) %collective-permute-start.41) | collective-permute-done | bytes 524320 | tf_op jit(solution)/shard_map/ppermute | solution.py:487
  695.1 17.8 %collective-permute-done.31.got_ref = bf16[512,256]{1,0:T(8,128)(2,1)S(1)} collective-permute-done((bf16[512,256]{1,0:T(8,128)(2,1)S(1)}, bf16[512,256]{1,0:T(8,128)(2,1)S(1)}, u32[]{:S(2)}, u32[]{:S(2)}) %collective-permute-start.31) | collective-permute-done | bytes 262176 | tf_op jit(solution)/shard_map/ppermute | solution.py:487
  732.6 7.5 collective-permute-done.42
  740.9 11.0 %collective-permute-done.43 = bf16[2,2,256,512]{3,2,0,1:T(8,128)(2,1)S(1)} collective-permute-done((bf16[2,2,256,512]{3,2,0,1:T(8,128)(2,1)S(1)}, bf16[2,2,256,512]{3,2,0,1:T(8,128)(2,1)S(1)}, u32[]{:S(2)}, u32[]{:S(2)}) %collective-permute-start.43) | collective-permute-done | bytes 1048608 | tf_op jit(solution)/shard_map/ppermute | solution.py:487
  761.9 3.6 collective-permute-done.44
  771.4 8.0 %collective-permute-done.45 = bf16[256,512]{1,0:T(8,128)(2,1)S(1)} collective-permute-done((bf16[256,512]{1,0:T(8,128)(2,1)S(1)}, bf16[256,512]{1,0:T(8,128)(2,1)S(1)}, u32[]{:S(2)}, u32[]{:S(2)}) %collective-permute-start.45) | collective-permute-done | bytes 262176 | tf_op jit(solution)/shard_map/ppermute | solution.py:487
  (354 shorter events, 180.8 us)
Async XLA Ops:
  7.2 97.0 %all-gather.2.cloned.1.call-start = ((), (), s32[]{:S(2)}) async-start(), calls=%async_computation.1 | async-start | bytes 4718592 | tf_op jit(solution)/shard_map/all_gather | solution.py:618
  133.2 21.3 %collective-permute-start = (bf16[256,2048]{1,0:T(8,128)(2,1)}, bf16[256,2048]{1,0:T(8,128)(2,1)}, u32[]{:S(2)}, u32[]{:S(2)}) collective-permute-start(bf16[256,2048]{1,0:T(8,128)(2,1)} %slice.149), channel_id=1, source_target_pairs={{0,1},{1,0},{2,3},{3,2},{4,5},{5,4},{6,7},{7,6},{8,9},{9,8},{10,11... | collective-permute-start | bytes 3145736 | tf_op jit(solution)/shard_map/ppermute | solution.py:487
  135.2 17.8 %collective-permute-start.17 = (bf16[128,2048]{1,0:T(8,128)(2,1)S(1)}, bf16[128,2048]{1,0:T(8,128)(2,1)}, u32[]{:S(2)}, u32[]{:S(2)}) collective-permute-start(bf16[128,2048]{1,0:T(8,128)(2,1)S(1)} %get-tuple-element.76), channel_id=1, source_target_pairs={{0,8},{4,12},{8,0},{12,4},{16,24},{20,28},{24,16},{28,20},{1,9},{5... | collective-permute-start | bytes 1572872 | tf_op jit(solution)/shard_map/ppermute | solution.py:487
  153.0 15.1 %collective-permute-start.18 = (bf16[128,2048]{1,0:T(8,128)(2,1)}, bf16[128,2048]{1,0:T(8,128)(2,1)}, u32[]{:S(2)}, u32[]{:S(2)}) collective-permute-start(bf16[128,2048]{1,0:T(8,128)(2,1)} %collective-permute-done.17), channel_id=1, source_target_pairs={{0,2},{1,3},{2,0},{3,1},{4,6},{5,7},{6,4},{7,5},{8,10},{9,11},{10,... | collective-permute-start | bytes 1572872 | tf_op jit(solution)/shard_map/ppermute | solution.py:487
  157.2 21.1 %collective-permute-start.1 = (bf16[128,2048]{1,0:T(8,128)(2,1)}, bf16[128,2048]{1,0:T(8,128)(2,1)}, u32[]{:S(2)}, u32[]{:S(2)}) collective-permute-start(bf16[128,2048]{1,0:T(8,128)(2,1)} %slice.151), channel_id=1, source_target_pairs={{0,2},{1,3},{2,0},{3,1},{4,6},{5,7},{6,4},{7,5},{8,10},{9,11},{10,... | collective-permute-start | bytes 1572872 | tf_op jit(solution)/shard_map/ppermute | solution.py:487
  161.6 22.7 %collective-permute-start.19 = (bf16[128,2048]{1,0:T(8,128)(2,1)}, bf16[128,2048]{1,0:T(8,128)(2,1)S(1)}, u32[]{:S(2)}, u32[]{:S(2)}) collective-permute-start(bf16[128,2048]{1,0:T(8,128)(2,1)} %collective-permute-done.17), channel_id=1, source_target_pairs={{0,1},{1,0},{2,3},{3,2},{4,5},{5,4},{6,7},{7,6},{8,9},{9,8},{10,11... | collective-permute-start | bytes 1572872 | tf_op jit(solution)/shard_map/ppermute | solution.py:487
  168.1 16.3 %collective-permute-start.20 = (bf16[128,2048]{1,0:T(8,128)(2,1)}, bf16[128,2048]{1,0:T(8,128)(2,1)S(1)}, u32[]{:S(2)}, u32[]{:S(2)}) collective-permute-start(bf16[128,2048]{1,0:T(8,128)(2,1)} %collective-permute-done.18), channel_id=1, source_target_pairs={{0,1},{1,0},{2,3},{3,2},{4,5},{5,4},{6,7},{7,6},{8,9},{9,8},{10,11... | collective-permute-start | bytes 1572872 | tf_op jit(solution)/shard_map/ppermute | solution.py:487
  193.0 14.3 %collective-permute-start.4 = (bf16[128,2048]{1,0:T(8,128)(2,1)S(1)}, bf16[128,2048]{1,0:T(8,128)(2,1)S(1)}, u32[]{:S(2)}, u32[]{:S(2)}) collective-permute-start(bf16[128,2048]{1,0:T(8,128)(2,1)S(1)} %collective-permute-done.2), channel_id=1, source_target_pairs={{0,1},{1,0},{2,3},{3,2},{4,5},{5,4},{6,7},{7,6},{8,9},{9,8},{10,11... | collective-permute-start | bytes 1572872 | tf_op jit(solution)/shard_map/ppermute | solution.py:487
  272.5 24.7 %collective-permute-start.21 = (bf16[256,2048]{1,0:T(8,128)(2,1)}, bf16[256,2048]{1,0:T(8,128)(2,1)S(1)}, u32[]{:S(2)}, u32[]{:S(2)}) collective-permute-start(bf16[256,2048]{1,0:T(8,128)(2,1)} %get-tuple-element.88), channel_id=1, source_target_pairs={{0,1},{1,0},{2,3},{3,2},{4,5},{5,4},{6,7},{7,6},{8,9},{9,8},{10,11... | collective-permute-start | bytes 3145736 | tf_op jit(solution)/shard_map/ppermute | solution.py:487
  272.7 24.6 %collective-permute-start.23 = (bf16[256,2048]{1,0:T(8,128)(2,1)S(1)}, bf16[256,2048]{1,0:T(8,128)(2,1)S(1)}, u32[]{:S(2)}, u32[]{:S(2)}) collective-permute-start(bf16[256,2048]{1,0:T(8,128)(2,1)S(1)} %get-tuple-element.89), channel_id=1, source_target_pairs={{0,1},{1,0},{2,3},{3,2},{4,5},{5,4},{6,7},{7,6},{8,9},{9,8},{10,11... | collective-permute-start | bytes 3145736 | tf_op jit(solution)/shard_map/ppermute | solution.py:487
  275.1 16.2 %collective-permute-start.11 = (bf16[256,2048]{1,0:T(8,128)(2,1)S(1)}, bf16[256,2048]{1,0:T(8,128)(2,1)}, u32[]{:S(2)}, u32[]{:S(2)}) collective-permute-start(bf16[256,2048]{1,0:T(8,128)(2,1)S(1)} %get-tuple-element.93), channel_id=1, source_target_pairs={{0,1},{1,0},{2,3},{3,2},{4,5},{5,4},{6,7},{7,6},{8,9},{9,8},{10,11... | collective-permute-start | bytes 3145736 | tf_op jit(solution)/shard_map/ppermute | solution.py:487
  275.2 18.1 %collective-permute-start.9 = (bf16[256,2048]{1,0:T(8,128)(2,1)}, bf16[256,2048]{1,0:T(8,128)(2,1)}, u32[]{:S(2)}, u32[]{:S(2)}) collective-permute-start(bf16[256,2048]{1,0:T(8,128)(2,1)} %get-tuple-element.92), channel_id=1, source_target_pairs={{0,1},{1,0},{2,3},{3,2},{4,5},{5,4},{6,7},{7,6},{8,9},{9,8},{10,11... | collective-permute-start | bytes 3145736 | tf_op jit(solution)/shard_map/ppermute | solution.py:487
  291.0 48.5 %collective-permute-start.52 = (bf16[2,2,256,1024]{3,2,1,0:T(8,128)(2,1)S(1)}, bf16[2,2,256,1024]{3,2,1,0:T(8,128)(2,1)S(1)}, u32[]{:S(2)}, u32[]{:S(2)}) collective-permute-start(bf16[2,2,256,1024]{3,2,1,0:T(8,128)(2,1)S(1)} %dynamic-slice_bitcast_fusion.1), channel_id=1, source_target_pairs={{0,4},{4,0},{8,12},{12,8},{16,20},{20,16},{24,28},{28,24},{1,5},{5... | collective-permute-start | bytes 6291464 | tf_op jit(solution)/shard_map/ppermute | solution.py:487
  291.3 93.2 %collective-permute-start.55 = (bf16[2,2,256,1024]{3,2,1,0:T(8,128)(2,1)S(1)}, bf16[2,2,256,1024]{3,2,1,0:T(8,128)(2,1)S(1)}, u32[]{:S(2)}, u32[]{:S(2)}) collective-permute-start(bf16[2,2,256,1024]{3,2,1,0:T(8,128)(2,1)S(1)} %dynamic-slice_bitcast_fusion), channel_id=1, source_target_pairs={{0,4},{4,0},{8,12},{12,8},{16,20},{20,16},{24,28},{28,24},{1,5},{5... | collective-permute-start | bytes 6291464 | tf_op jit(solution)/shard_map/ppermute | solution.py:487
  295.7 14.9 %collective-permute-start.12 = (bf16[128,2048]{1,0:T(8,128)(2,1)S(1)}, bf16[128,2048]{1,0:T(8,128)(2,1)S(1)}, u32[]{:S(2)}, u32[]{:S(2)}) collective-permute-start(bf16[128,2048]{1,0:T(8,128)(2,1)S(1)} %slice.159), channel_id=1, source_target_pairs={{0,2},{1,3},{2,0},{3,1},{4,6},{5,7},{6,4},{7,5},{8,10},{9,11},{10,... | collective-permute-start | bytes 1572872 | tf_op jit(solution)/shard_map/ppermute | solution.py:487
  298.1 23.7 %collective-permute-start.24 = (bf16[128,2048]{1,0:T(8,128)(2,1)S(1)}, bf16[128,2048]{1,0:T(8,128)(2,1)S(1)}, u32[]{:S(2)}, u32[]{:S(2)}) collective-permute-start(bf16[128,2048]{1,0:T(8,128)(2,1)S(1)} %slice.167), channel_id=1, source_target_pairs={{0,2},{1,3},{2,0},{3,1},{4,6},{5,7},{6,4},{7,5},{8,10},{9,11},{10,... | collective-permute-start | bytes 1572872 | tf_op jit(solution)/shard_map/ppermute | solution.py:487
  298.8 32.9 %collective-permute-start.10 = (bf16[128,2048]{1,0:T(8,128)(2,1)S(1)}, bf16[128,2048]{1,0:T(8,128)(2,1)S(1)}, u32[]{:S(2)}, u32[]{:S(2)}) collective-permute-start(bf16[128,2048]{1,0:T(8,128)(2,1)S(1)} %slice.155), channel_id=1, source_target_pairs={{0,2},{1,3},{2,0},{3,1},{4,6},{5,7},{6,4},{7,5},{8,10},{9,11},{10,... | collective-permute-start | bytes 1572872 | tf_op jit(solution)/shard_map/ppermute | solution.py:487
  310.7 22.4 %collective-permute-start.13 = (bf16[128,2048]{1,0:T(8,128)(2,1)S(1)}, bf16[128,2048]{1,0:T(8,128)(2,1)S(1)}, u32[]{:S(2)}, u32[]{:S(2)}) collective-permute-start(bf16[128,2048]{1,0:T(8,128)(2,1)S(1)} %add_convert_fusion.14), channel_id=1, source_target_pairs={{0,8},{4,12},{8,0},{12,4},{16,24},{20,28},{24,16},{28,20},{1,9},{5... | collective-permute-start | bytes 1572872 | tf_op jit(solution)/shard_map/ppermute | solution.py:487
  321.8 106.8 %collective-permute-start.49 = (bf16[2,2,256,1024]{3,2,1,0:T(8,128)(2,1)S(1)}, bf16[2,2,256,1024]{3,2,1,0:T(8,128)(2,1)S(1)}, u32[]{:S(2)}, u32[]{:S(2)}) collective-permute-start(bf16[2,2,256,1024]{3,2,1,0:T(8,128)(2,1)S(1)} %dynamic-slice_bitcast_fusion.2), channel_id=1, source_target_pairs={{0,4},{4,0},{8,12},{12,8},{16,20},{20,16},{24,28},{28,24},{1,5},{5... | collective-permute-start | bytes 6291464 | tf_op jit(solution)/shard_map/ppermute | solution.py:487
  331.6 55.0 %collective-permute-start.22 = (bf16[128,2048]{1,0:T(8,128)(2,1)S(1)}, bf16[128,2048]{1,0:T(8,128)(2,1)S(1)}, u32[]{:S(2)}, u32[]{:S(2)}) collective-permute-start(bf16[128,2048]{1,0:T(8,128)(2,1)S(1)} %slice.163), channel_id=1, source_target_pairs={{0,2},{1,3},{2,0},{3,1},{4,6},{5,7},{6,4},{7,5},{8,10},{9,11},{10,... | collective-permute-start | bytes 1572872 | tf_op jit(solution)/shard_map/ppermute | solution.py:487
  333.1 53.5 %collective-permute-start.25 = (bf16[128,2048]{1,0:T(8,128)(2,1)S(1)}, bf16[128,2048]{1,0:T(8,128)(2,1)S(1)}, u32[]{:S(2)}, u32[]{:S(2)}) collective-permute-start(bf16[128,2048]{1,0:T(8,128)(2,1)S(1)} %add_convert_fusion.12), channel_id=1, source_target_pairs={{0,8},{4,12},{8,0},{12,4},{16,24},{20,28},{24,16},{28,20},{1,9},{5... | collective-permute-start | bytes 1572872 | tf_op jit(solution)/shard_map/ppermute | solution.py:487
  339.5 94.0 %collective-permute-start.14 = (bf16[128,2048]{1,0:T(8,128)(2,1)}, bf16[128,2048]{1,0:T(8,128)(2,1)}, u32[]{:S(2)}, u32[]{:S(2)}) collective-permute-start(bf16[128,2048]{1,0:T(8,128)(2,1)} %get-tuple-element.78), channel_id=1, source_target_pairs={{0,2},{1,3},{2,0},{3,1},{4,6},{5,7},{6,4},{7,5},{8,10},{9,11},{10,... | collective-permute-start | bytes 1572872 | tf_op jit(solution)/shard_map/ppermute | solution.py:487
  384.5 51.2 %collective-permute-start.15 = (bf16[128,2048]{1,0:T(8,128)(2,1)}, bf16[128,2048]{1,0:T(8,128)(2,1)}, u32[]{:S(2)}, u32[]{:S(2)}) collective-permute-start(bf16[128,2048]{1,0:T(8,128)(2,1)} %get-tuple-element.78), channel_id=1, source_target_pairs={{0,1},{1,0},{2,3},{3,2},{4,5},{5,4},{6,7},{7,6},{8,9},{9,8},{10,11... | collective-permute-start | bytes 1572872 | tf_op jit(solution)/shard_map/ppermute | solution.py:487
  386.6 94.4 %collective-permute-start.53 = (bf16[2,256,1024]{2,1,0:T(8,128)(2,1)S(1)}, bf16[2,256,1024]{2,1,0:T(8,128)(2,1)}, u32[]{:S(2)}, u32[]{:S(2)}) collective-permute-start(bf16[2,256,1024]{2,1,0:T(8,128)(2,1)S(1)} %dynamic-slice_bitcast_fusion.4), channel_id=1, source_target_pairs={{0,16},{4,20},{8,24},{12,28},{16,0},{20,4},{24,8},{28,12},{1,17},{... | collective-permute-start | bytes 3145736 | tf_op jit(solution)/shard_map/ppermute | solution.py:487
  386.6 116.8 %collective-permute-start.56 = (bf16[2,256,1024]{2,1,0:T(8,128)(2,1)}, bf16[2,256,1024]{2,1,0:T(8,128)(2,1)}, u32[]{:S(2)}, u32[]{:S(2)}) collective-permute-start(bf16[2,256,1024]{2,1,0:T(8,128)(2,1)} %dynamic-slice_bitcast_fusion.3), channel_id=1, source_target_pairs={{0,16},{4,20},{8,24},{12,28},{16,0},{20,4},{24,8},{28,12},{1,17},{... | collective-permute-start | bytes 3145736 | tf_op jit(solution)/shard_map/ppermute | solution.py:487
  428.6 13.6 %collective-permute-start.26 = (bf16[128,2048]{1,0:T(8,128)(2,1)}, bf16[128,2048]{1,0:T(8,128)(2,1)}, u32[]{:S(2)}, u32[]{:S(2)}) collective-permute-start(bf16[128,2048]{1,0:T(8,128)(2,1)} %get-tuple-element.73), channel_id=1, source_target_pairs={{0,2},{1,3},{2,0},{3,1},{4,6},{5,7},{6,4},{7,5},{8,10},{9,11},{10,... | collective-permute-start | bytes 1572872 | tf_op jit(solution)/shard_map/ppermute | solution.py:487
  433.6 92.1 %collective-permute-start.50 = (bf16[2,256,1024]{2,1,0:T(8,128)(2,1)}, bf16[2,256,1024]{2,1,0:T(8,128)(2,1)}, u32[]{:S(2)}, u32[]{:S(2)}) collective-permute-start(bf16[2,256,1024]{2,1,0:T(8,128)(2,1)} %dynamic-slice_bitcast_fusion.5), channel_id=1, source_target_pairs={{0,16},{4,20},{8,24},{12,28},{16,0},{20,4},{24,8},{28,12},{1,17},{... | collective-permute-start | bytes 3145736 | tf_op jit(solution)/shard_map/ppermute | solution.py:487
  435.7 94.0 %collective-permute-start.27 = (bf16[128,2048]{1,0:T(8,128)(2,1)}, bf16[128,2048]{1,0:T(8,128)(2,1)}, u32[]{:S(2)}, u32[]{:S(2)}) collective-permute-start(bf16[128,2048]{1,0:T(8,128)(2,1)} %get-tuple-element.73), channel_id=1, source_target_pairs={{0,1},{1,0},{2,3},{3,2},{4,5},{5,4},{6,7},{7,6},{8,9},{9,8},{10,11... | collective-permute-start | bytes 1572872 | tf_op jit(solution)/shard_map/ppermute | solution.py:487
  442.2 146.8 %collective-permute-start.16 = (bf16[128,2048]{1,0:T(8,128)(2,1)}, bf16[128,2048]{1,0:T(8,128)(2,1)}, u32[]{:S(2)}, u32[]{:S(2)}) collective-permute-start(bf16[128,2048]{1,0:T(8,128)(2,1)} %collective-permute-done.14), channel_id=1, source_target_pairs={{0,1},{1,0},{2,3},{3,2},{4,5},{5,4},{6,7},{7,6},{8,9},{9,8},{10,11... | collective-permute-start | bytes 1572872 | tf_op jit(solution)/shard_map/ppermute | solution.py:487
  481.0 50.7 %collective-permute-start.28 = (bf16[128,2048]{1,0:T(8,128)(2,1)}, bf16[128,2048]{1,0:T(8,128)(2,1)}, u32[]{:S(2)}, u32[]{:S(2)}) collective-permute-start(bf16[128,2048]{1,0:T(8,128)(2,1)} %collective-permute-done.26), channel_id=1, source_target_pairs={{0,1},{1,0},{2,3},{3,2},{4,5},{5,4},{6,7},{7,6},{8,9},{9,8},{10,11... | collective-permute-start | bytes 1572872 | tf_op jit(solution)/shard_map/ppermute | solution.py:487
  508.3 85.9 %collective-permute-start.57 = (bf16[256,1024]{0,1:T(8,128)(2,1)}, bf16[256,1024]{0,1:T(8,128)(2,1)}, u32[]{:S(2)}, u32[]{:S(2)}) collective-permute-start(bf16[256,1024]{0,1:T(8,128)(2,1)} %bitcast.157), channel_id=1, source_target_pairs={{0,8},{4,12},{8,0},{12,4},{16,24},{20,28},{24,16},{28,20},{1,9},{5... | collective-permute-start | bytes 1572872 | tf_op jit(solution)/shard_map/ppermute | solution.py:487
  525.7 73.2 %collective-permute-start.54 = (bf16[256,1024]{0,1:T(8,128)(2,1)}, bf16[256,1024]{0,1:T(8,128)(2,1)}, u32[]{:S(2)}, u32[]{:S(2)}) collective-permute-start(bf16[256,1024]{0,1:T(8,128)(2,1)} %bitcast.155), channel_id=1, source_target_pairs={{0,8},{4,12},{8,0},{12,4},{16,24},{20,28},{24,16},{28,20},{1,9},{5... | collective-permute-start | bytes 1572872 | tf_op jit(solution)/shard_map/ppermute | solution.py:487
  529.7 71.9 %collective-permute-start.51 = (bf16[256,1024]{0,1:T(8,128)(2,1)}, bf16[256,1024]{0,1:T(8,128)(2,1)}, u32[]{:S(2)}, u32[]{:S(2)}) collective-permute-start(bf16[256,1024]{0,1:T(8,128)(2,1)} %bitcast.156), channel_id=1, source_target_pairs={{0,8},{4,12},{8,0},{12,4},{16,24},{20,28},{24,16},{28,20},{1,9},{5... | collective-permute-start | bytes 1572872 | tf_op jit(solution)/shard_map/ppermute | solution.py:487
  581.2 29.1 %collective-permute-start.46 = (bf16[2,2,256,512]{2,3,0,1:T(8,128)(2,1)}, bf16[2,2,256,512]{2,3,0,1:T(8,128)(2,1)}, u32[]{:S(2)}, u32[]{:S(2)}) collective-permute-start(bf16[2,2,256,512]{2,3,0,1:T(8,128)(2,1)} %bitcast.153), channel_id=1, source_target_pairs={{0,4},{4,0},{8,12},{12,8},{16,20},{20,16},{24,28},{28,24},{1,5},{5... | collective-permute-start | bytes 3145736 | tf_op jit(solution)/shard_map/ppermute | solution.py:487
  589.0 42.1 %collective-permute-start.32 = (bf16[2048,256]{1,0:T(8,128)(2,1)}, bf16[2048,256]{1,0:T(8,128)(2,1)}, u32[]{:S(2)}, u32[]{:S(2)}) collective-permute-start(bf16[2048,256]{1,0:T(8,128)(2,1)} %get-tuple-element.40), channel_id=1, source_target_pairs={{0,4},{4,0},{8,12},{12,8},{16,20},{20,16},{24,28},{28,24},{1,5},{5... | collective-permute-start | bytes 3145736 | tf_op jit(solution)/shard_map/ppermute | solution.py:487
  594.2 59.4 %collective-permute-start.29 = (bf16[2048,256]{1,0:T(8,128)(2,1)}, bf16[2048,256]{1,0:T(8,128)(2,1)}, u32[]{:S(2)}, u32[]{:S(2)}) collective-permute-start(bf16[2048,256]{1,0:T(8,128)(2,1)} %get-tuple-element.37), channel_id=1, source_target_pairs={{0,4},{4,0},{8,12},{12,8},{16,20},{20,16},{24,28},{28,24},{1,5},{5... | collective-permute-start | bytes 3145736 | tf_op jit(solution)/shard_map/ppermute | solution.py:487
  598.9 75.6 %collective-permute-start.40 = (bf16[2,2,256,512]{3,2,0,1:T(8,128)(2,1)}, bf16[2,2,256,512]{3,2,0,1:T(8,128)(2,1)}, u32[]{:S(2)}, u32[]{:S(2)}) collective-permute-start(bf16[2,2,256,512]{3,2,0,1:T(8,128)(2,1)} %bitcast.141), channel_id=1, source_target_pairs={{0,4},{4,0},{8,12},{12,8},{16,20},{20,16},{24,28},{28,24},{1,5},{5... | collective-permute-start | bytes 3145736 | tf_op jit(solution)/shard_map/ppermute | solution.py:487
  612.2 67.6 %collective-permute-start.47 = (bf16[2,256,512]{1,2,0:T(8,128)(2,1)S(1)}, bf16[2,256,512]{1,2,0:T(8,128)(2,1)S(1)}, u32[]{:S(2)}, u32[]{:S(2)}) collective-permute-start(bf16[2,256,512]{1,2,0:T(8,128)(2,1)S(1)} %dynamic-slice_bitcast_fusion.6), channel_id=1, source_target_pairs={{0,8},{4,12},{8,0},{12,4},{16,24},{20,28},{24,16},{28,20},{1,9},{5... | collective-permute-start | bytes 1572872 | tf_op jit(solution)/shard_map/ppermute | solution.py:487
  632.8 51.7 %collective-permute-start.33 = (bf16[1024,256]{1,0:T(8,128)(2,1)S(1)}, bf16[1024,256]{1,0:T(8,128)(2,1)S(1)}, u32[]{:S(2)}, u32[]{:S(2)}) collective-permute-start(bf16[1024,256]{1,0:T(8,128)(2,1)S(1)} %slice.173), channel_id=1, source_target_pairs={{0,8},{4,12},{8,0},{12,4},{16,24},{20,28},{24,16},{28,20},{1,9},{5... | collective-permute-start | bytes 1572872 | tf_op jit(solution)/shard_map/ppermute | solution.py:487
  655.2 25.6 %collective-permute-start.30 = (bf16[1024,256]{1,0:T(8,128)(2,1)S(1)}, bf16[1024,256]{1,0:T(8,128)(2,1)S(1)}, u32[]{:S(2)}, u32[]{:S(2)}) collective-permute-start(bf16[1024,256]{1,0:T(8,128)(2,1)S(1)} %slice.169), channel_id=1, source_target_pairs={{0,8},{4,12},{8,0},{12,4},{16,24},{20,28},{24,16},{28,20},{1,9},{5... | collective-permute-start | bytes 1572872 | tf_op jit(solution)/shard_map/ppermute | solution.py:487
  676.1 18.1 %collective-permute-start.41 = (bf16[2,256,512]{2,1,0:T(8,128)(2,1)S(1)}, bf16[2,256,512]{2,1,0:T(8,128)(2,1)S(1)}, u32[]{:S(2)}, u32[]{:S(2)}) collective-permute-start(bf16[2,256,512]{2,1,0:T(8,128)(2,1)S(1)} %dynamic-slice_bitcast_fusion.8), channel_id=1, source_target_pairs={{0,8},{4,12},{8,0},{12,4},{16,24},{20,28},{24,16},{28,20},{1,9},{5... | collective-permute-start | bytes 1572872 | tf_op jit(solution)/shard_map/ppermute | solution.py:487
  680.7 48.0 %collective-permute-start.48 = (bf16[256,512]{0,1:T(8,128)(2,1)}, bf16[256,512]{0,1:T(8,128)(2,1)}, u32[]{:S(2)}, u32[]{:S(2)}) collective-permute-start(bf16[256,512]{0,1:T(8,128)(2,1)} %dynamic-slice_bitcast_fusion.9), channel_id=1, source_target_pairs={{0,16},{4,20},{8,24},{12,28},{16,0},{20,4},{24,8},{28,12},{1,17},{... | collective-permute-start | bytes 786440 | tf_op jit(solution)/shard_map/ppermute | solution.py:487
  681.7 31.2 %collective-permute-start.31 = (bf16[512,256]{1,0:T(8,128)(2,1)S(1)}, bf16[512,256]{1,0:T(8,128)(2,1)S(1)}, u32[]{:S(2)}, u32[]{:S(2)}) collective-permute-start(bf16[512,256]{1,0:T(8,128)(2,1)S(1)} %get-tuple-element.117), channel_id=1, source_target_pairs={{0,16},{4,20},{8,24},{12,28},{16,0},{20,4},{24,8},{28,12},{1,17},{... | collective-permute-start | bytes 786440 | tf_op jit(solution)/shard_map/ppermute | solution.py:487
  685.5 31.7 %collective-permute-start.34 = (bf16[512,256]{1,0:T(8,128)(2,1)}, bf16[512,256]{1,0:T(8,128)(2,1)}, u32[]{:S(2)}, u32[]{:S(2)}) collective-permute-start(bf16[512,256]{1,0:T(8,128)(2,1)} %get-tuple-element.115), channel_id=1, source_target_pairs={{0,16},{4,20},{8,24},{12,28},{16,0},{20,4},{24,8},{28,12},{1,17},{... | collective-permute-start | bytes 786440 | tf_op jit(solution)/shard_map/ppermute | solution.py:487
  727.7 24.2 %collective-permute-start.43 = (bf16[2,2,256,512]{3,2,0,1:T(8,128)(2,1)S(1)}, bf16[2,2,256,512]{3,2,0,1:T(8,128)(2,1)S(1)}, u32[]{:S(2)}, u32[]{:S(2)}) collective-permute-start(bf16[2,2,256,512]{3,2,0,1:T(8,128)(2,1)S(1)} %bitcast.154), channel_id=1, source_target_pairs={{0,4},{4,0},{8,12},{12,8},{16,20},{20,16},{24,28},{28,24},{1,5},{5... | collective-permute-start | bytes 3145736 | tf_op jit(solution)/shard_map/ppermute | solution.py:487
  731.1 22.0 %collective-permute-start.36 = (bf16[128,2048]{1,0:T(8,128)(2,1)S(1)}, bf16[128,2048]{1,0:T(8,128)(2,1)S(1)}, u32[]{:S(2)}, u32[]{:S(2)}) collective-permute-start(bf16[128,2048]{1,0:T(8,128)(2,1)S(1)} %slice.179), channel_id=1, source_target_pairs={{0,2},{1,3},{2,0},{3,1},{4,6},{5,7},{6,4},{7,5},{8,10},{9,11},{10,... | collective-permute-start | bytes 1572872 | tf_op jit(solution)/shard_map/ppermute | solution.py:487
  757.1 23.4 %collective-permute-start.37 = (bf16[128,2048]{1,0:T(8,128)(2,1)}, bf16[128,2048]{1,0:T(8,128)(2,1)}, u32[]{:S(2)}, u32[]{:S(2)}) collective-permute-start(bf16[128,2048]{1,0:T(8,128)(2,1)} %get-tuple-element.72), channel_id=1, source_target_pairs={{0,2},{1,3},{2,0},{3,1},{4,6},{5,7},{6,4},{7,5},{8,10},{9,11},{10,... | collective-permute-start | bytes 1572872 | tf_op jit(solution)/shard_map/ppermute | solution.py:487
  758.5 24.0 %collective-permute-start.38 = (bf16[128,2048]{1,0:T(8,128)(2,1)}, bf16[128,2048]{1,0:T(8,128)(2,1)}, u32[]{:S(2)}, u32[]{:S(2)}) collective-permute-start(bf16[128,2048]{1,0:T(8,128)(2,1)} %get-tuple-element.72), channel_id=1, source_target_pairs={{0,1},{1,0},{2,3},{3,2},{4,5},{5,4},{6,7},{7,6},{8,9},{9,8},{10,11... | collective-permute-start | bytes 1572872 | tf_op jit(solution)/shard_map/ppermute | solution.py:487
  (78 other events, 790.8 us)
Sparse Core Ops, SparseCore 0:
  28.0 76.0 all-gather.1

commit v3 on v2

--- a/solution.py
+++ b/solution.py
@@ -501,19 +501,29 @@
     )
 
 
+def after(dep, *values):
+    held = lax.optimization_barrier((dep,) + values)[1:]
+    return held[0] if len(held) == 1 else held
+
+
 def gather_slots(own):
-    other = flip(own, "tp", 2)
-    return jnp.concatenate([own, other, flip(own, "tp", 1), flip(other, "tp", 1)])
+    near = jnp.concatenate([own, flip(own, "tp", 2)])
+    return jnp.concatenate([near, flip(near, "tp", 1)])
+
+
+def gather_pair(own):
+    partner = flip(own, "ctx", 2)
+    near = jnp.concatenate([own, partner, flip(own, "tp", 2), flip(partner, "tp", 2)])
+    return jnp.concatenate([near, flip(near, "tp", 1)])
 
 
 def gather_rows(own, tensor):
     rows = own.shape[0]
-    other = flip(own, "tp", 2)
-    pieces = (own, other, flip(own, "tp", 1), flip(other, "tp", 1))
-    result = jnp.zeros((SLOTS * rows,) + own.shape[1:], own.dtype)
+    slots = gather_slots(own)
+    result = jnp.zeros_like(slots)
     for u in range(SLOTS):
         result = lax.dynamic_update_slice_in_dim(
-            result, pieces[u], (tensor ^ SLOT_XOR[u]) * rows, 0
+            result, slots[u * rows : (u + 1) * rows], (tensor ^ SLOT_XOR[u]) * rows, 0
         )
     return result
 
@@ -557,29 +567,43 @@
     return mine.astype(jnp.float32) + got.astype(jnp.float32)
 
 
-def reduce_ffn(partial, ctx, ctx_count):
-    highs = high_masks(ctx_count)
-    width = partial.shape[1]
-    rows = partial.shape[0] // ctx_count
-    shaped = partial.astype(jnp.bfloat16).reshape((2,) * len(highs) + (2, 2, rows, width))
-    mine, got = step(shaped, len(highs) + 1, 1, ctx % 2)
-    for mask, bit in zip(highs, bits_of(ctx, ctx_count)):
-        shaped = add(mine, got)
-        mine, got = step(shaped, 0, mask, bit)
-    shaped = add(mine, got)
-    pair = ctx // 2 % 2
-    mine, got = step(shaped, 0, 2, pair)
-    low, high = jnp.where(pair == 0, mine, got), jnp.where(pair == 0, got, mine)
-    return jnp.concatenate([low, high], axis=1).astype(jnp.float32)
-
-
-def reduce_kv(keep, send, ctx_count):
-    got = flip(send, "ctx", 1)
-    for mask in [2] + high_masks(ctx_count):
-        total = add(keep, got)
-        half = total.shape[0] // 2
-        keep, got = total[:half], flip(total[half:], "ctx", mask)
-    return keep, got
+class FfnReduce:
+    def __init__(self, partial, ctx, ctx_count, dep=None):
+        self.highs = high_masks(ctx_count)
+        self.ctx, self.ctx_count = ctx, ctx_count
+        if dep is not None:
+            partial = after(dep, partial)
+        rows, width = partial.shape[0] // ctx_count, partial.shape[1]
+        shaped = partial.reshape((2,) * len(self.highs) + (2, 2, rows, width))
+        self.mine, self.got = step(shaped, len(self.highs) + 1, 1, ctx % 2)
+
+    def high(self, dep):
+        mine, got = after(dep, self.mine, self.got)
+        for mask, bit in zip(self.highs, bits_of(self.ctx, self.ctx_count)):
+            self.shaped = add(mine, got)
+            mine, got = step(self.shaped, 0, mask, bit)
+        self.mine, self.got = mine, got
+
+    def finish(self, dep):
+        shaped = add(*after(dep, self.mine, self.got))
+        pair = self.ctx // 2 % 2
+        mine, got = step(shaped, 0, 2, pair)
+        low, high = jnp.where(pair == 0, mine, got), jnp.where(pair == 0, got, mine)
+        return jnp.concatenate([low, high], axis=1).astype(jnp.float32)
+
+
+class KvReduce:
+    def __init__(self, keep, send, ctx_count):
+        self.ctx_count = ctx_count
+        self.keep, self.got = keep, flip(send, "ctx", 1)
+
+    def high(self, dep):
+        keep, got = after(dep, self.keep, self.got)
+        for mask in [2] + high_masks(self.ctx_count):
+            total = add(keep, got)
+            half = total.shape[0] // 2
+            keep, got = total[:half], flip(total[half:], "ctx", mask)
+        self.keep, self.got = keep, got
 
 
 def norm_back(grad_out, normed, inv_scale, gain):
@@ -621,24 +645,20 @@
     up_half = lax.dynamic_slice_in_dim(w_up, pair * half_units, half_units, 1)
     down_half = lax.dynamic_slice_in_dim(w_down, pair * half_units, half_units, 0)
     cot_own = lax.dynamic_slice_in_dim(cotangent, tensor * quarter, quarter)
-    cot_rows = jnp.concatenate(
-        [slots_of(cotangent, tensor), gather_slots(flip(cot_own, "ctx", 2))]
-    )
-    grad_hidden = right_dot(cot_rows, down_half)
-
-    mixed, log_total = attention_forward(
-        queries, kv_all, block_order, cont_prompt, where
-    )
+    cot_slots = slots_of(cotangent, tensor).reshape(SLOTS, 1, quarter, -1)
+    cot_other = gather_slots(flip(cot_own, "ctx", 2)).reshape(SLOTS, 1, quarter, -1)
+    cot_rows = jnp.concatenate([cot_slots, cot_other], axis=1).reshape(2 * SLOTS * quarter, -1)
+
+    mixed, log_total = attention_forward(queries, kv_all, block_order, cont_prompt, where)
     mine, got = scatter_slots(plain_dot(mixed, w_out).astype(jnp.bfloat16))
+    grad_hidden = right_dot(after(mine, cot_rows), down_half)
     own_input = lax.dynamic_slice_in_dim(layer_input, tensor * quarter, quarter)
     own_input = own_input.astype(jnp.float32)
+    mine, got = after(grad_hidden, mine, got)
     middle = own_input + (mine.astype(jnp.float32) + got.astype(jnp.float32))
     inv_two = lax.rsqrt(jnp.mean(middle * middle, axis=-1, keepdims=True) + eps_norm)
     normed_two = middle * inv_two
-    second_own = (normed_two * ffn_gain).astype(jnp.bfloat16)
-    second_in = jnp.concatenate(
-        [gather_slots(second_own), gather_slots(flip(second_own, "ctx", 2))]
-    )
+    second_in = gather_pair((normed_two * ffn_gain).astype(jnp.bfloat16))
 
     gate = plain_dot(second_in, gate_half)
     upward = plain_dot(second_in, up_half)
@@ -648,63 +668,92 @@
     grad_gate = (grad_hidden * upward * sigma * (1.0 + gate * (1.0 - sigma))).astype(jnp.bfloat16)
     grad_upward = (grad_hidden * swish).astype(jnp.bfloat16)
 
-    sum_down = reduce_ffn(left_dot(cot_rows, hidden), ctx, ctx_count).T
-    local = layer_input.shape[0]
-
-    def pair_sum(partial):
-        mine, got = scatter_slots(partial[local:])
-        away = flip(add(mine, got), "ctx", 2)
-        mine, got = scatter_slots(partial[:local])
-        return (mine.astype(jnp.float32) + got.astype(jnp.float32)) + away.astype(jnp.float32)
-
-    grad_second = pair_sum(
-        (right_dot(grad_gate, gate_half) + right_dot(grad_upward, up_half)).astype(jnp.bfloat16)
-    )
-    sum_gate = reduce_ffn(left_dot(second_in, grad_gate), ctx, ctx_count)
-    sum_up = reduce_ffn(left_dot(second_in, grad_upward), ctx, ctx_count)
-
-    grad_norm_two, ffn_gain_part = norm_back(grad_second, normed_two, inv_two, ffn_gain)
-    own_cot = cot_own.astype(jnp.float32)
-    grad_middle = own_cot + grad_norm_two
+    def pair_scatter(partial):
+        half = partial.shape[0] // 2
+        near = add(partial[:half], flip(partial[half:], "tp", 1))
+        far = flip(near[3 * quarter :], "tp", 2)
+        away = flip(add(near[quarter : 2 * quarter], far), "ctx", 2)
+        got = flip(near[2 * quarter : 3 * quarter], "tp", 2)
+        return near[:quarter], got, away
+
+    def total(terms):
+        return sum(term.astype(jnp.float32) for term in terms)
+
+    part_down = left_dot(cot_rows, hidden).astype(jnp.bfloat16)
+    down = FfnReduce(part_down, ctx, ctx_count)
+    grad_gate, grad_upward = after(part_down, grad_gate, grad_upward)
+    partial = (right_dot(grad_gate, gate_half) + right_dot(grad_upward, up_half)).astype(
+        jnp.bfloat16
+    )
+    second_terms = pair_scatter(partial)
+    grad_gate, second_in = after(partial, grad_gate, second_in)
+    part_gate = left_dot(second_in, grad_gate).astype(jnp.bfloat16)
+    grad_upward, second_in = after(part_gate, grad_upward, second_in)
+    part_up = left_dot(second_in, grad_upward).astype(jnp.bfloat16)
+    hidden = after(part_up, hidden)
+    ffn_partial = plain_dot(hidden, down_half).astype(jnp.bfloat16)
+
+    second_terms = after(ffn_partial, *second_terms)
+    grad_norm_two, ffn_gain_part = norm_back(total(second_terms), normed_two, inv_two, ffn_gain)
+    grad_middle = cot_own.astype(jnp.float32) + grad_norm_two
     grad_branch = gather_slots(grad_middle.astype(jnp.bfloat16))
+    down.high(grad_middle)
+    gate_w = FfnReduce(part_gate, ctx, ctx_count, down.shaped)
     grad_mixed = right_dot(grad_branch, w_out).astype(jnp.bfloat16)
-    sum_out = reduce_attention(left_dot(grad_branch, mixed), ctx, ctx_count).T
-
-    ffn_out = pair_sum(plain_dot(hidden, down_half).astype(jnp.bfloat16))
-    output = gather_rows((middle + ffn_out).astype(jnp.bfloat16), tensor)
-
-    grad_queries, grad_keys, grad_values = [], [], []
+    backward = []
     for head in range(kv_heads):
-        grad_q, keep, send = attention_backward(
-            head, queries, kv_all, grad_mixed, mixed, log_total, cosine, sine,
-            block_order, cont_prompt, where,
+        backward.append(
+            attention_backward(
+                head, queries, kv_all, grad_mixed, mixed, log_total, cosine, sine,
+                block_order, cont_prompt, where,
+            )
         )
-        grad_queries.append(grad_q)
-        grad_k, grad_v = kv_finish(*reduce_kv(keep, send, ctx_count), cosine, sine)
+        grad_mixed = after(backward[-1][0], grad_mixed)
+    grad_query = jnp.concatenate([item[0] for item in backward], axis=1)
+    part_out = left_dot(grad_branch, after(grad_query, mixed)).astype(jnp.bfloat16)
+    part_query = left_dot(first_input, grad_query).astype(jnp.bfloat16)
+    query_first = right_dot(grad_query, w_query)
+    gate_w.high(part_query)
+    kv = [
+        KvReduce(after(gate_w.shaped, item[1]), after(gate_w.shaped, item[2]), ctx_count)
+        for item in backward
+    ]
+    ffn_terms = pair_scatter(after(gate_w.shaped, ffn_partial))
+    sum_down = down.finish(gate_w.shaped).T
+    for item in kv:
+        item.high(sum_down)
+    up_w = FfnReduce(part_up, ctx, ctx_count, kv[-1].keep)
+    grad_keys, grad_values = [], []
+    for item in kv:
+        grad_k, grad_v = kv_finish(item.keep, item.got, cosine, sine)
         grad_keys.append(grad_k)
         grad_values.append(grad_v)
-    grad_query = jnp.concatenate(grad_queries, axis=1)
     grad_key = jnp.concatenate(grad_keys, axis=1)
     grad_value = jnp.concatenate(grad_values, axis=1)
-    sum_query = reduce_attention(left_dot(first_input, grad_query), ctx, ctx_count)
-    sum_kv = reduce_attention(
-        jnp.concatenate(
-            [left_dot(first_input, grad_key), left_dot(first_input, grad_value)], axis=1
-        ),
-        ctx,
-        ctx_count,
-    )
-    sum_key, sum_value = jnp.split(sum_kv, 2, axis=1)
     grad_first_partial = (
-        right_dot(grad_query, w_query)
-        + right_dot(grad_key, key_matrix)
-        + right_dot(grad_value, value_matrix)
-    )
-    mine, got = scatter_slots(grad_first_partial.astype(jnp.bfloat16))
-    grad_first = mine.astype(jnp.float32) + got.astype(jnp.float32)
+        query_first + right_dot(grad_key, key_matrix) + right_dot(grad_value, value_matrix)
+    ).astype(jnp.bfloat16)
+    first_terms = scatter_slots(grad_first_partial)
+    grad_key, grad_value = after(grad_first_partial, grad_key, grad_value)
+    part_kv = jnp.concatenate(
+        [left_dot(first_input, grad_key), left_dot(first_input, grad_value)], axis=1
+    ).astype(jnp.bfloat16)
+    output = gather_rows((middle + total(ffn_terms)).astype(jnp.bfloat16), tensor)
+    up_w.high(part_kv)
+    rest = jnp.concatenate([part_out, part_query, part_kv], axis=1)
+    rest_sum = reduce_attention(after(up_w.shaped, rest), ctx, ctx_count)
+    sum_gate = gate_w.finish(up_w.shaped)
     inv_one = lax.rsqrt(jnp.mean(own_input * own_input, axis=-1, keepdims=True) + eps_norm)
-    grad_norm_one, attn_gain_part = norm_back(grad_first, own_input * inv_one, inv_one, attn_gain)
+    grad_norm_one, attn_gain_part = norm_back(
+        total(first_terms), own_input * inv_one, inv_one, attn_gain
+    )
     grad_input = gather_rows((grad_middle + grad_norm_one).astype(jnp.bfloat16), tensor)
+    sum_up = up_w.finish(grad_input)
+    width_q, width_k = w_query.shape[1], key_matrix.shape[1]
+    sum_out = rest_sum[:, :width_q].T
+    sum_query = rest_sum[:, width_q : 2 * width_q]
+    sum_key = rest_sum[:, 2 * width_q : 2 * width_q + width_k]
+    sum_value = rest_sum[:, 2 * width_q + width_k :]
 
     devices = ctx_count * tp_count
     gains = jnp.stack([attn_gain_part, ffn_gain_part]).reshape(2, devices, -1)

time: 804 us -> 762 us (0.948)
  waiting for transfers between devices: 422 us -> 361 us
  local copies, waits for them, and re-layouts: 87.8 us -> 108 us
  other arithmetic: 43.2 us -> 63 us
    all_gather x1, waiting for transfers between devices: 76.2 us -> 42.3 us  [body(): kv_all = lax.all_gather(kv_local, 'ctx', axis=0, tiled=True)]
    ppermute x58 -> x43, waiting for transfers between devices: 343 us -> 319 us  [flip(): lax.ppermute(value, axis, [(i, i ^ mask) for i in range(lax.axis_size(axi...]
    concatenate x1 -> x9, other arithmetic: 0.18 us -> 20.9 us  [the longest x1 12.3 us: body(): rest = jnp.concatenate([part_out, part_query, part_kv], axis=1)]
    dynamic_slice x6 -> x4, local copies, waits for them, and re-layouts: 7 us -> 18.2 us  [step(): mine = lax.dynamic_index_in_dim(parts, index, axis_bits, keepdims=False)]
    reshape x0 -> x1, local copies, waits for them, and re-layouts: none -> 11.1 us  [reduce_attention(): partial.astype(jnp.bfloat16)]
    unnamed x153 -> x166, local copies, waits for them, and re-layouts: 48 us -> 39 us
    ppermute x58 -> x43, starting transfers between devices: 56.8 us -> 50.8 us  [flip(): lax.ppermute(value, axis, [(i, i ^ mask) for i in range(lax.axis_size(axi...]
    convert_element_type x22 -> x18, other arithmetic: 23.2 us -> 28.9 us  [add(): (left.astype(jnp.float32) + right.astype(jnp.float32)).astype(jnp.bfloat16)]
  transfers between devices with their start and end apart: 60 -> 45, of which waited for: 28 -> 28; matrix products, arithmetic and copies ran while one was open for 17% -> 23% of each run, Pallas kernels for 5% -> 7%
where the time goes in v3:
time: 762 us; the launch traced here: 750 us
  waiting for transfers between devices  361 us (47%)
  local copies, waits for them, and re-layouts  108 us (14%)
  matrix products  87.2 us (11%)
  other arithmetic  63 us (8%)
  Pallas kernels  62.3 us (8%)
  starting transfers between devices  53.4 us (7%)
  between operations  15.4 us (2%)
    ppermute x43, waiting for transfers between devices, flip(): lax.ppermute(value, axis, [(i, i ^ mask) for i in range(lax.axis_size(axi...  319 us
    ppermute x43, starting transfers between devices, flip(): lax.ppermute(value, axis, [(i, i ^ mask) for i in range(lax.axis_size(axi...  50.8 us
    all_gather x1, waiting for transfers between devices, body(): kv_all = lax.all_gather(kv_local, 'ctx', axis=0, tiled=True)  42.3 us
    unnamed x166, local copies, waits for them, and re-layouts  39 us
    dot_general x7, matrix products, right_dot(): lax.dot_general(left, right, (((1,), (1,)), ((), ())), preferred_element_...  31.6 us
    pallas_call x2, Pallas kernels, attention_backward(): pl.pallas_call(functools.partial(backward_kernel, rep, 1), out_shape=(jax...  31.3 us
    dot_general x7, matrix products, left_dot(): lax.dot_general(left, right, (((0,), (0,)), ((), ())), preferred_element_...  30.7 us
    convert_element_type x18, other arithmetic, add(): (left.astype(jnp.float32) + right.astype(jnp.float32)).astype(jnp.bfloat16)  28.9 us
  transfers between devices with their start and end apart: 45, of which 28 were waited for; matrix products, arithmetic and copies ran while one was open for 23% of the time, Pallas kernels for 7%

profile of v3, /device:TPU:0, one launch (start us, length us, event | category | flops | bytes accessed | tf_op | source)
XLA Modules:
  0.0 750.5 jit_solution(84411701227023781)
XLA Ops:
  18.2 6.2 input_stage.1
  30.6 3.0 collective-permute-start.1
  33.7 21.3 %collective-permute-done.1 = bf16[128,2048]{1,0:T(8,128)(2,1)S(1)} collective-permute-done((bf16[128,2048]{1,0:T(8,128)(2,1)S(1)}, bf16[128,2048]{1,0:T(8,128)(2,1)S(1)}, u32[]{:S(2)}, u32[]{:S(2)}) %collective-permute-start.1) | collective-permute-done | bytes 524320 | tf_op jit(solution)/shard_map/ppermute | solution.py:487
  57.9 7.2 collective-permute-done.2
  67.0 42.3 %all-gather.2.cloned.1.call-done.kv_ref = bf16[4096,512]{1,0:T(8,128)(2,1)} async-done(((bf16[512,512]{1,0:T(8,128)(2,1)}), bf16[4096,512]{1,0:T(8,128)(2,1)}) %all-gather.2.cloned.1.call-update) | async-done | bytes 4194320 | tf_op jit(solution)/shard_map/all_gather | solution.py:642
  109.4 20.8 %attention_forward.1 = (bf16[512,512]{1,0:T(8,128)(2,1)}, f32[1,2,4,256]{3,2,1,0:T(4,128)}) custom-call(s32[32]{0:T(128)} %order_ref.7, s32[8]{0:T(128)} %cont_ref.7, s32[2]{0:T(128)} %copy-done.20, bf16[512,512]{1,0:T(8,128)(2,1)} %copy-done.23, bf16[4096,512]{1,0:T(8,128)(2,1)} %all-gather.2.cloned.1.call-done.kv_ref), custom_call_target="tpu_custom_call" | custom-call | flops 2147483648 | bytes 5242880 | tf_op jit(solution)/shard_map/attention_forward/pallas_call | solution.py:314
  143.1 6.2 fusion.10
  149.2 6.7 collective-permute-done.4
  157.7 8.0 %collective-permute-start.5 = (bf16[128,2048]{1,0:T(8,128)(2,1)S(1)}, bf16[128,2048]{1,0:T(8,128)(2,1)S(1)}, u32[]{:S(2)}, u32[]{:S(2)}) collective-permute-start(bf16[128,2048]{1,0:T(8,128)(2,1)S(1)} %get-tuple-element.171), channel_id=1, source_target_pairs={{0,8},{4,12},{8,0},{12,4},{16,24},{20,28},{24,16},{28,20},{1,9},{5... | collective-permute-start | bytes 1572872 | tf_op jit(solution)/shard_map/ppermute | solution.py:487
  167.2 10.3 %collective-permute-done.5 = bf16[128,2048]{1,0:T(8,128)(2,1)S(1)} collective-permute-done((bf16[128,2048]{1,0:T(8,128)(2,1)S(1)}, bf16[128,2048]{1,0:T(8,128)(2,1)S(1)}, u32[]{:S(2)}, u32[]{:S(2)}) %collective-permute-start.5) | collective-permute-done | bytes 524320 | tf_op jit(solution)/shard_map/ppermute | solution.py:487
  179.1 11.5 %collective-permute-done.7 = bf16[128,2048]{1,0:T(8,128)(2,1)S(1)} collective-permute-done((bf16[128,2048]{1,0:T(8,128)(2,1)S(1)}, bf16[128,2048]{1,0:T(8,128)(2,1)S(1)}, u32[]{:S(2)}, u32[]{:S(2)}) %collective-permute-start.7) | collective-permute-done | bytes 524320 | tf_op jit(solution)/shard_map/ppermute | solution.py:487
  191.0 4.0 collective-permute-done.8
  195.2 6.3 fusion.3
  201.5 10.2 %multiply_convert_fusion = (bf16[1024,1024]{1,0:T(8,128)(2,1)}, bf16[1024,1024]{1,0:T(8,128)(2,1)S(1)}, bf16[1024,1024]{1,0:T(8,128)(2,1)}) fusion(f32[1024,1024]{1,0:T(8,128)} %fusion.10, f32[1024,1024]{1,0:T(8,128)} %fusion.3, bf16[1024,2048]{1,0:T(8,128)(2,1)S(1)} %constant_dynamic-update-slice_fusion, bf16[2048,2048]{1,0:T(8,128)(2,1)S(1)} %bitcast.121, ...), kind=kOutput, calls=%fused_computation.11 | convolution fusion | flops 4310695936 | bytes 23068676 | tf_op jit(solution)/shard_map/dot_general | solution.py:30
  211.8 8.5 %convolution_convert_fusion.3 = bf16[2048,1024]{1,0:T(8,128)(2,1)} fusion(bf16[1024,2048]{1,0:T(8,128)(2,1)S(1)} %bitcast.115, bf16[1024,1024]{1,0:T(8,128)(2,1)} %get-tuple-element.82), kind=kOutput, calls=%fused_computation.19 | convolution fusion | flops 4297064448 | bytes 10485760 | tf_op jit(solution)/shard_map/dot_general | solution.py:34
  220.3 7.2 fusion.5
  227.5 9.8 %add_convert_fusion = bf16[1024,2048]{1,0:T(8,128)(2,1)S(1)} fusion(f32[1024,2048]{1,0:T(8,128)} %fusion.5, bf16[1024,1024]{1,0:T(8,128)(2,1)} %get-tuple-element.81, bf16[2048,2048]{1,0:T(8,128)(2,1)} %param.25, s32[]{:T(128)S(6)} %select_n.152), kind=kOutput, calls=%fused_computation | convolution fusion | flops 4299161600 | bytes 18874372 | tf_op jit(solution)/shard_map/dot_general | solution.py:40
  240.1 7.6 %convolution_convert_fusion.2 = bf16[2048,1024]{1,0:T(8,128)(2,1)S(1)} fusion(bf16[1024,2048]{1,0:T(8,128)(2,1)} %copy-done.63, bf16[1024,1024]{1,0:T(8,128)(2,1)} %copy-done.65), kind=kOutput, calls=%fused_computation.18 | convolution fusion | flops 4297064448 | bytes 10485760 | tf_op jit(solution)/shard_map/dot_general | solution.py:34
  252.0 6.4 convolution_convert_fusion.1
  259.6 5.6 collective-permute-done.11
  266.9 6.1 convolution_convert_fusion
  281.8 24.8 %collective-permute-done.15 = bf16[2,2,256,1024]{3,2,1,0:T(8,128)(2,1)S(1)} collective-permute-done((bf16[2,2,256,1024]{3,2,1,0:T(8,128)(2,1)S(1)}, bf16[2,2,256,1024]{3,2,1,0:T(8,128)(2,1)S(1)}, u32[]{:S(2)}, u32[]{:S(2)}) %collective-permute-start.15) | collective-permute-done | bytes 2097184 | tf_op jit(solution)/shard_map/ppermute | solution.py:487
  319.4 3.6 convolution_convert_fusion.9.gm_ref
  323.0 15.5 %attention_backward_0.1 = (bf16[512,256]{1,0:T(8,128)(2,1)}, bf16[2048,256]{1,0:T(8,128)(2,1)}, bf16[2048,256]{1,0:T(8,128)(2,1)}) custom-call(s32[32]{0:T(128)} %order_ref.7, s32[8]{0:T(128)} %cont_ref.7, s32[2]{0:T(128)} %copy-done.20, bf16[512,512]{1,0:T(8,128)(2,1)} %copy-done.23, bf16[4096,512]{1,0:T(8,128)(2,1)} %all-gather.2.cloned.1.call-done.kv_ref, ...), custom_call_target="tpu_custom_call" | custom-call | flops 2684354560 | bytes 5242880 | tf_op jit(solution)/shard_map/attention_backward_0/pallas_call | solution.py:361
  339.5 15.7 %attention_backward_1.1 = (bf16[512,256]{1,0:T(8,128)(2,1)}, bf16[2048,256]{1,0:T(8,128)(2,1)}, bf16[2048,256]{1,0:T(8,128)(2,1)}) custom-call(s32[32]{0:T(128)} %order_ref.7, s32[8]{0:T(128)} %cont_ref.7, s32[2]{0:T(128)} %copy-done.20, bf16[512,512]{1,0:T(8,128)(2,1)} %copy-done.23, bf16[4096,512]{1,0:T(8,128)(2,1)} %all-gather.2.cloned.1.call-done.kv_ref, ...), custom_call_target="tpu_custom_call" | custom-call | flops 2684354560 | bytes 5242880 | tf_op jit(solution)/shard_map/attention_backward_1/pallas_call | solution.py:361
  360.9 3.9 add_convert_fusion.4
  369.1 5.5 collective-permute-start.24
  376.8 10.3 %collective-permute-done.24 = bf16[256,1024]{0,1:T(8,128)(2,1)} collective-permute-done((bf16[256,1024]{0,1:T(8,128)(2,1)}, bf16[256,1024]{0,1:T(8,128)(2,1)}, u32[]{:S(2)}, u32[]{:S(2)}) %collective-permute-start.24) | collective-permute-done | bytes 524320 | tf_op jit(solution)/shard_map/ppermute | solution.py:487
  389.9 11.1 %collective-permute-done.28 = bf16[2048,256]{1,0:T(8,128)(2,1)S(1)} collective-permute-done((bf16[2048,256]{1,0:T(8,128)(2,1)}, bf16[2048,256]{1,0:T(8,128)(2,1)S(1)}, u32[]{:S(2)}, u32[]{:S(2)}) %collective-permute-start.28) | collective-permute-done | bytes 1048608 | tf_op jit(solution)/shard_map/ppermute | solution.py:487
  401.4 20.8 %collective-permute-done.25 = bf16[2048,256]{1,0:T(8,128)(2,1)S(1)} collective-permute-done((bf16[2048,256]{1,0:T(8,128)(2,1)}, bf16[2048,256]{1,0:T(8,128)(2,1)S(1)}, u32[]{:S(2)}, u32[]{:S(2)}) %collective-permute-start.25) | collective-permute-done | bytes 1048608 | tf_op jit(solution)/shard_map/ppermute | solution.py:487
  422.8 3.3 fusion.41
  429.9 7.9 %collective-permute-done.26 = bf16[1024,256]{1,0:T(8,128)(2,1)S(1)} collective-permute-done((bf16[1024,256]{1,0:T(8,128)(2,1)S(1)}, bf16[1024,256]{1,0:T(8,128)(2,1)S(1)}, u32[]{:S(2)}, u32[]{:S(2)}) %collective-permute-start.26) | collective-permute-done | bytes 524320 | tf_op jit(solution)/shard_map/ppermute | solution.py:487
  439.2 4.0 convolution_convert_fusion.4
  446.9 2.9 collective-permute-done.30.got_ref
  470.6 12.3 %pad_maximum_fusion = bf16[2048,1536]{0,1:T(8,128)(2,1)} fusion(bf16[2048,256]{0,1:T(8,128)(2,1)S(1)} %convolution_convert_fusion.7, bf16[2048,256]{0,1:T(8,128)(2,1)S(1)} %convolution_convert_fusion.8, bf16[2048,512]{0,1:T(8,128)(2,1)S(1)} %copy-done.51, bf16[2048,512]{0,1:T(8,128)(2,1)S(1)} %copy-done.52), kind=kLoop, calls=%fused_computation.1 | loop fusion | flops 25165824 | bytes 12582912 | tf_op jit(solution)/shard_map/concatenate | solution.py:743
  485.7 12.0 %collective-permute-done.18 = bf16[128,2048]{1,0:T(8,128)(2,1)S(1)} collective-permute-done((bf16[128,2048]{1,0:T(8,128)(2,1)S(1)}, bf16[128,2048]{1,0:T(8,128)(2,1)S(1)}, u32[]{:S(2)}, u32[]{:S(2)}) %collective-permute-start.18) | collective-permute-done | bytes 524320 | tf_op jit(solution)/shard_map/ppermute | solution.py:487
  501.9 6.9 collective-permute-done.32
  513.6 4.5 add_convert_fusion.1
  518.1 11.1 %reshape.90 = bf16[2,2,2,256,1536]{3,2,1,0,4:T(2,128)(2,1)} reshape(bf16[2048,1536]{0,1:T(8,128)(2,1)} %pad_maximum_fusion) | data formatting | bytes 12582912 | tf_op jit(solution)/shard_map/reshape | solution.py:560
  529.3 15.7 %constant_dynamic-slice_fusion.5 = (bf16[2,2,1,256,1536]{3,2,1,0,4:T(2,128)(2,1)}, bf16[2,2,1,256,1536]{3,2,1,0,4:T(2,128)(2,1)S(1)}) fusion(bf16[2,2,2,256,1536]{3,2,1,0,4:T(2,128)(2,1)} %reshape.90, s32[]{:T(128)S(6)} %select_n.154, s32[]{:T(128)S(6)} %select_n.155), kind=kLoop, calls=%fused_computation.127 | loop fusion | bytes 12582920 | tf_op jit(solution)/shard_map/jit(dynamic_index_in_dim)/dynamic_slice | solution.py:547
  555.1 3.8 constant_dynamic-slice_fusion
  572.7 60.4 %collective-permute-done.39 = bf16[2,256,1024]{1,2,0:T(8,128)(2,1)} collective-permute-done((bf16[2,256,1024]{1,2,0:T(8,128)(2,1)}, bf16[2,256,1024]{1,2,0:T(8,128)(2,1)}, u32[]{:S(2)}, u32[]{:S(2)}) %collective-permute-start.39) | collective-permute-done | bytes 1048608 | tf_op jit(solution)/shard_map/ppermute | solution.py:487
  636.2 5.0 fusion
  643.5 11.2 %collective-permute-done.41 = bf16[2,256,1024]{1,2,0:T(8,128)(2,1)} collective-permute-done((bf16[2,256,1024]{1,2,0:T(8,128)(2,1)}, bf16[2,256,1024]{1,2,0:T(8,128)(2,1)}, u32[]{:S(2)}, u32[]{:S(2)}) %collective-permute-start.41) | collective-permute-done | bytes 1048608 | tf_op jit(solution)/shard_map/ppermute | solution.py:487
  657.4 8.4 %collective-permute-done.40 = bf16[256,1024]{0,1:T(8,128)(2,1)S(1)} collective-permute-done((bf16[256,1024]{0,1:T(8,128)(2,1)S(1)}, bf16[256,1024]{0,1:T(8,128)(2,1)S(1)}, u32[]{:S(2)}, u32[]{:S(2)}) %collective-permute-start.40) | collective-permute-done | bytes 524320 | tf_op jit(solution)/shard_map/ppermute | solution.py:487
  665.8 33.6 %collective-permute-done.37 = bf16[2,256,1536]{1,2,0:T(8,128)(2,1)S(1)} collective-permute-done((bf16[2,256,1536]{1,2,0:T(8,128)(2,1)S(1)}, bf16[2,256,1536]{1,2,0:T(8,128)(2,1)S(1)}, u32[]{:S(2)}, u32[]{:S(2)}) %collective-permute-start.37) | collective-permute-done | bytes 1572896 | tf_op jit(solution)/shard_map/ppermute | solution.py:487
  704.2 7.2 collective-permute-done.42
  714.6 23.8 %collective-permute-done.38 = bf16[256,1536]{0,1:T(8,128)(2,1)} collective-permute-done((bf16[256,1536]{0,1:T(8,128)(2,1)}, bf16[256,1536]{0,1:T(8,128)(2,1)}, u32[]{:S(2)}, u32[]{:S(2)}) %collective-permute-start.38) | collective-permute-done | bytes 786464 | tf_op jit(solution)/shard_map/ppermute | solution.py:487
  (336 shorter events, 174.4 us)
Async XLA Ops:
  7.2 123.0 %copy-start = (bf16[512,2048]{1,0:T(8,128)(2,1)S(1)}, bf16[512,2048]{1,0:T(8,128)(2,1)}, u32[]{:S(2)}) copy-start(bf16[512,2048]{1,0:T(8,128)(2,1)} %param.22) | copy-start | bytes 6291460
  7.2 102.2 %all-gather.2.cloned.1.call-start = ((), (), s32[]{:S(2)}) async-start(), calls=%async_computation.1 | async-start | bytes 4718592 | tf_op jit(solution)/shard_map/all_gather | solution.py:642
  30.6 104.2 %copy-start.29 = (bf16[128,2048]{1,0:T(8,128)(2,1)}, bf16[128,2048]{1,0:T(8,128)(2,1)S(1)}, u32[]{:S(2)}) copy-start(bf16[128,2048]{1,0:T(8,128)(2,1)S(1)} %get-tuple-element.198) | copy-start | bytes 1572868
  30.6 24.3 %collective-permute-start.1 = (bf16[128,2048]{1,0:T(8,128)(2,1)S(1)}, bf16[128,2048]{1,0:T(8,128)(2,1)S(1)}, u32[]{:S(2)}, u32[]{:S(2)}) collective-permute-start(bf16[128,2048]{1,0:T(8,128)(2,1)S(1)} %get-tuple-element.198), channel_id=1, source_target_pairs={{0,8},{4,12},{8,0},{12,4},{16,24},{20,28},{24,16},{28,20},{1,9},{5... | collective-permute-start | bytes 1572872 | tf_op jit(solution)/shard_map/ppermute | solution.py:487
  55.0 10.2 %collective-permute-start.2 = (bf16[128,2048]{1,0:T(8,128)(2,1)S(1)}, bf16[128,2048]{1,0:T(8,128)(2,1)S(1)}, u32[]{:S(2)}, u32[]{:S(2)}) collective-permute-start(bf16[128,2048]{1,0:T(8,128)(2,1)S(1)} %collective-permute-done.1), channel_id=1, source_target_pairs={{0,2},{1,3},{2,0},{3,1},{4,6},{5,7},{6,4},{7,5},{8,10},{9,11},{10,... | collective-permute-start | bytes 1572872 | tf_op jit(solution)/shard_map/ppermute | solution.py:487
  67.0 69.4 %collective-permute-start.3 = (bf16[256,2048]{1,0:T(8,128)(2,1)}, bf16[256,2048]{1,0:T(8,128)(2,1)}, u32[]{:S(2)}, u32[]{:S(2)}) collective-permute-start(bf16[256,2048]{1,0:T(8,128)(2,1)} %pad_maximum_fusion.6), channel_id=1, source_target_pairs={{0,1},{1,0},{2,3},{3,2},{4,5},{5,4},{6,7},{7,6},{8,9},{9,8},{10,11... | collective-permute-start | bytes 3145736 | tf_op jit(solution)/shard_map/ppermute | solution.py:487
  134.9 3.5 collective-permute-start
  141.5 14.4 %collective-permute-start.4 = (bf16[128,2048]{1,0:T(8,128)(2,1)S(1)}, bf16[128,2048]{1,0:T(8,128)(2,1)S(1)}, u32[]{:S(2)}, u32[]{:S(2)}) collective-permute-start(bf16[128,2048]{1,0:T(8,128)(2,1)S(1)} %get-tuple-element.211), channel_id=1, source_target_pairs={{0,2},{1,3},{2,0},{3,1},{4,6},{5,7},{6,4},{7,5},{8,10},{9,11},{10,... | collective-permute-start | bytes 1572872 | tf_op jit(solution)/shard_map/ppermute | solution.py:487
  157.5 121.2 %copy-start.25 = (f32[128,2048]{1,0:T(8,128)}, f32[128,2048]{1,0:T(8,128)S(1)}, u32[]{:S(2)}) copy-start(f32[128,2048]{1,0:T(8,128)S(1)} %get-tuple-element.173) | copy-start | bytes 3145732
  157.7 19.8 %collective-permute-start.5 = (bf16[128,2048]{1,0:T(8,128)(2,1)S(1)}, bf16[128,2048]{1,0:T(8,128)(2,1)S(1)}, u32[]{:S(2)}, u32[]{:S(2)}) collective-permute-start(bf16[128,2048]{1,0:T(8,128)(2,1)S(1)} %get-tuple-element.171), channel_id=1, source_target_pairs={{0,8},{4,12},{8,0},{12,4},{16,24},{20,28},{24,16},{28,20},{1,9},{5... | collective-permute-start | bytes 1572872 | tf_op jit(solution)/shard_map/ppermute | solution.py:487
  165.8 13.3 %collective-permute-start.6 = (bf16[128,2048]{1,0:T(8,128)(2,1)S(1)}, bf16[128,2048]{1,0:T(8,128)(2,1)S(1)}, u32[]{:S(2)}, u32[]{:S(2)}) collective-permute-start(bf16[128,2048]{1,0:T(8,128)(2,1)S(1)} %get-tuple-element.171), channel_id=1, source_target_pairs={{0,2},{1,3},{2,0},{3,1},{4,6},{5,7},{6,4},{7,5},{8,10},{9,11},{10,... | collective-permute-start | bytes 1572872 | tf_op jit(solution)/shard_map/ppermute | solution.py:487
  177.6 13.0 %collective-permute-start.7 = (bf16[128,2048]{1,0:T(8,128)(2,1)S(1)}, bf16[128,2048]{1,0:T(8,128)(2,1)S(1)}, u32[]{:S(2)}, u32[]{:S(2)}) collective-permute-start(bf16[128,2048]{1,0:T(8,128)(2,1)S(1)} %collective-permute-done.5), channel_id=1, source_target_pairs={{0,2},{1,3},{2,0},{3,1},{4,6},{5,7},{6,4},{7,5},{8,10},{9,11},{10,... | collective-permute-start | bytes 1572872 | tf_op jit(solution)/shard_map/ppermute | solution.py:487
  190.8 4.2 collective-permute-start.8
  240.0 7.7 %collective-permute-start.9 = (bf16[512,2048]{1,0:T(8,128)(2,1)}, bf16[512,2048]{1,0:T(8,128)(2,1)}, u32[]{:S(2)}, u32[]{:S(2)}) collective-permute-start(bf16[512,2048]{1,0:T(8,128)(2,1)} %slice.157), channel_id=1, source_target_pairs={{0,1},{1,0},{2,3},{3,2},{4,5},{5,4},{6,7},{7,6},{8,9},{9,8},{10,11... | collective-permute-start | bytes 6291464 | tf_op jit(solution)/shard_map/ppermute | solution.py:487
  250.4 14.8 %collective-permute-start.11 = (bf16[128,2048]{1,0:T(8,128)(2,1)S(1)}, bf16[128,2048]{1,0:T(8,128)(2,1)S(1)}, u32[]{:S(2)}, u32[]{:S(2)}) collective-permute-start(bf16[128,2048]{1,0:T(8,128)(2,1)S(1)} %get-tuple-element.194), channel_id=1, source_target_pairs={{0,2},{1,3},{2,0},{3,1},{4,6},{5,7},{6,4},{7,5},{8,10},{9,11},{10,... | collective-permute-start | bytes 1572872 | tf_op jit(solution)/shard_map/ppermute | solution.py:487
  258.9 47.7 %collective-permute-start.15 = (bf16[2,2,256,1024]{3,2,1,0:T(8,128)(2,1)S(1)}, bf16[2,2,256,1024]{3,2,1,0:T(8,128)(2,1)S(1)}, u32[]{:S(2)}, u32[]{:S(2)}) collective-permute-start(bf16[2,2,256,1024]{3,2,1,0:T(8,128)(2,1)S(1)} %get-tuple-element.183), channel_id=1, source_target_pairs={{0,4},{4,0},{8,12},{12,8},{16,20},{20,16},{24,28},{28,24},{1,5},{5... | collective-permute-start | bytes 6291464 | tf_op jit(solution)/shard_map/ppermute | solution.py:487
  259.0 16.9 %collective-permute-start.10 = (bf16[128,2048]{1,0:T(8,128)(2,1)S(1)}, bf16[128,2048]{1,0:T(8,128)(2,1)S(1)}, u32[]{:S(2)}, u32[]{:S(2)}) collective-permute-start(bf16[128,2048]{1,0:T(8,128)(2,1)S(1)} %get-tuple-element.195), channel_id=1, source_target_pairs={{0,2},{1,3},{2,0},{3,1},{4,6},{5,7},{6,4},{7,5},{8,10},{9,11},{10,... | collective-permute-start | bytes 1572872 | tf_op jit(solution)/shard_map/ppermute | solution.py:487
  265.4 12.9 %collective-permute-start.12 = (bf16[128,2048]{1,0:T(8,128)(2,1)S(1)}, bf16[128,2048]{1,0:T(8,128)(2,1)S(1)}, u32[]{:S(2)}, u32[]{:S(2)}) collective-permute-start(bf16[128,2048]{1,0:T(8,128)(2,1)S(1)} %add_convert_fusion.18), channel_id=1, source_target_pairs={{0,8},{4,12},{8,0},{12,4},{16,24},{20,28},{24,16},{28,20},{1,9},{5... | collective-permute-start | bytes 1572872 | tf_op jit(solution)/shard_map/ppermute | solution.py:487
  280.3 26.3 %collective-permute-start.13 = (bf16[128,2048]{1,0:T(8,128)(2,1)S(1)}, bf16[128,2048]{1,0:T(8,128)(2,1)S(1)}, u32[]{:S(2)}, u32[]{:S(2)}) collective-permute-start(bf16[128,2048]{1,0:T(8,128)(2,1)S(1)} %get-tuple-element.168), channel_id=1, source_target_pairs={{0,2},{1,3},{2,0},{3,1},{4,6},{5,7},{6,4},{7,5},{8,10},{9,11},{10,... | collective-permute-start | bytes 1572872 | tf_op jit(solution)/shard_map/ppermute | solution.py:487
  307.7 11.7 %collective-permute-start.14 = (bf16[256,2048]{1,0:T(8,128)(2,1)}, bf16[256,2048]{1,0:T(8,128)(2,1)}, u32[]{:S(2)}, u32[]{:S(2)}) collective-permute-start(bf16[256,2048]{1,0:T(8,128)(2,1)} %pad_maximum_fusion.7), channel_id=1, source_target_pairs={{0,1},{1,0},{2,3},{3,2},{4,5},{5,4},{6,7},{7,6},{8,9},{9,8},{10,11... | collective-permute-start | bytes 3145736 | tf_op jit(solution)/shard_map/ppermute | solution.py:487
  312.5 48.4 %collective-permute-start.16 = (bf16[2,2,256,1024]{3,2,1,0:T(8,128)(2,1)}, bf16[2,2,256,1024]{3,2,1,0:T(8,128)(2,1)}, u32[]{:S(2)}, u32[]{:S(2)}) collective-permute-start(bf16[2,2,256,1024]{3,2,1,0:T(8,128)(2,1)} %get-tuple-element.181), channel_id=1, source_target_pairs={{0,4},{4,0},{8,12},{12,8},{16,20},{20,16},{24,28},{28,24},{1,5},{5... | collective-permute-start | bytes 6291464 | tf_op jit(solution)/shard_map/ppermute | solution.py:487
  316.9 49.0 %collective-permute-start.23 = (bf16[2,256,1024]{1,2,0:T(8,128)(2,1)}, bf16[2,256,1024]{1,2,0:T(8,128)(2,1)}, u32[]{:S(2)}, u32[]{:S(2)}) collective-permute-start(bf16[2,256,1024]{1,2,0:T(8,128)(2,1)} %bitcast.119), channel_id=1, source_target_pairs={{0,16},{4,20},{8,24},{12,28},{16,0},{20,4},{24,8},{28,12},{1,17},{... | collective-permute-start | bytes 3145736 | tf_op jit(solution)/shard_map/ppermute | solution.py:487
  369.1 18.0 %collective-permute-start.24 = (bf16[256,1024]{0,1:T(8,128)(2,1)}, bf16[256,1024]{0,1:T(8,128)(2,1)}, u32[]{:S(2)}, u32[]{:S(2)}) collective-permute-start(bf16[256,1024]{0,1:T(8,128)(2,1)} %dynamic-slice_bitcast_fusion.10), channel_id=1, source_target_pairs={{0,8},{4,12},{8,0},{12,4},{16,24},{20,28},{24,16},{28,20},{1,9},{5... | collective-permute-start | bytes 1572872 | tf_op jit(solution)/shard_map/ppermute | solution.py:487
  374.7 26.3 %collective-permute-start.28 = (bf16[2048,256]{1,0:T(8,128)(2,1)}, bf16[2048,256]{1,0:T(8,128)(2,1)S(1)}, u32[]{:S(2)}, u32[]{:S(2)}) collective-permute-start(bf16[2048,256]{1,0:T(8,128)(2,1)} %get-tuple-element.110), channel_id=1, source_target_pairs={{0,4},{4,0},{8,12},{12,8},{16,20},{20,16},{24,28},{28,24},{1,5},{5... | collective-permute-start | bytes 3145736 | tf_op jit(solution)/shard_map/ppermute | solution.py:487
  374.7 47.4 %collective-permute-start.25 = (bf16[2048,256]{1,0:T(8,128)(2,1)}, bf16[2048,256]{1,0:T(8,128)(2,1)S(1)}, u32[]{:S(2)}, u32[]{:S(2)}) collective-permute-start(bf16[2048,256]{1,0:T(8,128)(2,1)} %get-tuple-element.103), channel_id=1, source_target_pairs={{0,4},{4,0},{8,12},{12,8},{16,20},{20,16},{24,28},{28,24},{1,5},{5... | collective-permute-start | bytes 3145736 | tf_op jit(solution)/shard_map/ppermute | solution.py:487
  401.3 26.3 %collective-permute-start.29 = (bf16[1024,256]{1,0:T(8,128)(2,1)S(1)}, bf16[1024,256]{1,0:T(8,128)(2,1)S(1)}, u32[]{:S(2)}, u32[]{:S(2)}) collective-permute-start(bf16[1024,256]{1,0:T(8,128)(2,1)S(1)} %slice.173), channel_id=1, source_target_pairs={{0,8},{4,12},{8,0},{12,4},{16,24},{20,28},{24,16},{28,20},{1,9},{5... | collective-permute-start | bytes 1572872 | tf_op jit(solution)/shard_map/ppermute | solution.py:487
  422.5 15.3 %collective-permute-start.26 = (bf16[1024,256]{1,0:T(8,128)(2,1)S(1)}, bf16[1024,256]{1,0:T(8,128)(2,1)S(1)}, u32[]{:S(2)}, u32[]{:S(2)}) collective-permute-start(bf16[1024,256]{1,0:T(8,128)(2,1)S(1)} %slice.169), channel_id=1, source_target_pairs={{0,8},{4,12},{8,0},{12,4},{16,24},{20,28},{24,16},{28,20},{1,9},{5... | collective-permute-start | bytes 1572872 | tf_op jit(solution)/shard_map/ppermute | solution.py:487
  427.6 37.4 %collective-permute-start.17 = (bf16[512,2048]{1,0:T(8,128)(2,1)}, bf16[512,2048]{1,0:T(8,128)(2,1)}, u32[]{:S(2)}, u32[]{:S(2)}) collective-permute-start(bf16[512,2048]{1,0:T(8,128)(2,1)} %slice.125), channel_id=1, source_target_pairs={{0,1},{1,0},{2,3},{3,2},{4,5},{5,4},{6,7},{7,6},{8,9},{9,8},{10,11... | collective-permute-start | bytes 6291464 | tf_op jit(solution)/shard_map/ppermute | solution.py:487
  428.6 21.3 %collective-permute-start.30 = (bf16[512,256]{1,0:T(8,128)(2,1)S(1)}, bf16[512,256]{1,0:T(8,128)(2,1)S(1)}, u32[]{:S(2)}, u32[]{:S(2)}) collective-permute-start(bf16[512,256]{1,0:T(8,128)(2,1)S(1)} %get-tuple-element.213), channel_id=1, source_target_pairs={{0,16},{4,20},{8,24},{12,28},{16,0},{20,4},{24,8},{28,12},{1,17},{... | collective-permute-start | bytes 786440 | tf_op jit(solution)/shard_map/ppermute | solution.py:487
  438.7 16.4 %collective-permute-start.27 = (bf16[512,256]{1,0:T(8,128)(2,1)}, bf16[512,256]{1,0:T(8,128)(2,1)}, u32[]{:S(2)}, u32[]{:S(2)}) collective-permute-start(bf16[512,256]{1,0:T(8,128)(2,1)} %get-tuple-element.215), channel_id=1, source_target_pairs={{0,16},{4,20},{8,24},{12,28},{16,0},{20,4},{24,8},{28,12},{1,17},{... | collective-permute-start | bytes 786440 | tf_op jit(solution)/shard_map/ppermute | solution.py:487
  445.7 67.9 %collective-permute-start.35 = (bf16[2,2,256,1024]{3,2,1,0:T(8,128)(2,1)}, bf16[2,2,256,1024]{3,2,1,0:T(8,128)(2,1)}, u32[]{:S(2)}, u32[]{:S(2)}) collective-permute-start(bf16[2,2,256,1024]{3,2,1,0:T(8,128)(2,1)} %get-tuple-element.179), channel_id=1, source_target_pairs={{0,4},{4,0},{8,12},{12,8},{16,20},{20,16},{24,28},{28,24},{1,5},{5... | collective-permute-start | bytes 6291464 | tf_op jit(solution)/shard_map/ppermute | solution.py:487
  463.5 20.2 %collective-permute-start.31 = (bf16[256,2048]{1,0:T(8,128)(2,1)S(1)}, bf16[256,2048]{1,0:T(8,128)(2,1)S(1)}, u32[]{:S(2)}, u32[]{:S(2)}) collective-permute-start(bf16[256,2048]{1,0:T(8,128)(2,1)S(1)} %slice.177), channel_id=1, source_target_pairs={{0,1},{1,0},{2,3},{3,2},{4,5},{5,4},{6,7},{7,6},{8,9},{9,8},{10,11... | collective-permute-start | bytes 3145736 | tf_op jit(solution)/shard_map/ppermute | solution.py:487
  469.1 14.4 %collective-permute-start.19 = (bf16[128,2048]{1,0:T(8,128)(2,1)S(1)}, bf16[128,2048]{1,0:T(8,128)(2,1)S(1)}, u32[]{:S(2)}, u32[]{:S(2)}) collective-permute-start(bf16[128,2048]{1,0:T(8,128)(2,1)S(1)} %get-tuple-element.193), channel_id=1, source_target_pairs={{0,2},{1,3},{2,0},{3,1},{4,6},{5,7},{6,4},{7,5},{8,10},{9,11},{10,... | collective-permute-start | bytes 1572872 | tf_op jit(solution)/shard_map/ppermute | solution.py:487
  482.9 14.7 %collective-permute-start.18 = (bf16[128,2048]{1,0:T(8,128)(2,1)S(1)}, bf16[128,2048]{1,0:T(8,128)(2,1)S(1)}, u32[]{:S(2)}, u32[]{:S(2)}) collective-permute-start(bf16[128,2048]{1,0:T(8,128)(2,1)S(1)} %get-tuple-element.192), channel_id=1, source_target_pairs={{0,2},{1,3},{2,0},{3,1},{4,6},{5,7},{6,4},{7,5},{8,10},{9,11},{10,... | collective-permute-start | bytes 1572872 | tf_op jit(solution)/shard_map/ppermute | solution.py:487
  483.6 14.1 %collective-permute-start.20 = (bf16[128,2048]{1,0:T(8,128)(2,1)S(1)}, bf16[128,2048]{1,0:T(8,128)(2,1)S(1)}, u32[]{:S(2)}, u32[]{:S(2)}) collective-permute-start(bf16[128,2048]{1,0:T(8,128)(2,1)S(1)} %add_convert_fusion.17), channel_id=1, source_target_pairs={{0,8},{4,12},{8,0},{12,4},{16,24},{20,28},{24,16},{28,20},{1,9},{5... | collective-permute-start | bytes 1572872 | tf_op jit(solution)/shard_map/ppermute | solution.py:487
  484.2 24.7 %collective-permute-start.32 = (bf16[128,2048]{1,0:T(8,128)(2,1)S(1)}, bf16[128,2048]{1,0:T(8,128)(2,1)S(1)}, u32[]{:S(2)}, u32[]{:S(2)}) collective-permute-start(bf16[128,2048]{1,0:T(8,128)(2,1)S(1)} %slice.179), channel_id=1, source_target_pairs={{0,2},{1,3},{2,0},{3,1},{4,6},{5,7},{6,4},{7,5},{8,10},{9,11},{10,... | collective-permute-start | bytes 1572872 | tf_op jit(solution)/shard_map/ppermute | solution.py:487
  500.4 66.6 %collective-permute-start.21 = (bf16[128,2048]{1,0:T(8,128)(2,1)}, bf16[128,2048]{1,0:T(8,128)(2,1)}, u32[]{:S(2)}, u32[]{:S(2)}) collective-permute-start(bf16[128,2048]{1,0:T(8,128)(2,1)} %get-tuple-element.167), channel_id=1, source_target_pairs={{0,2},{1,3},{2,0},{3,1},{4,6},{5,7},{6,4},{7,5},{8,10},{9,11},{10,... | collective-permute-start | bytes 1572872 | tf_op jit(solution)/shard_map/ppermute | solution.py:487
  511.0 42.8 %all-to-all-start = ((f32[32,1,128]{2,1,0:T(1,128)}), f32[32,1,128]{2,1,0:T(1,128)S(1)}, u32[]{:S(2)}, u32[]{:S(2)}) async-start(f32[32,1,128]{2,1,0:T(1,128)} %reshape.94), calls=%async_computation | async-start | bytes 32768 | tf_op jit(solution)/shard_map/all_to_all | solution.py:760
  547.7 87.1 %collective-permute-start.36 = (bf16[2,2,256,1536]{2,3,0,1:T(8,128)(2,1)}, bf16[2,2,256,1536]{2,3,0,1:T(8,128)(2,1)}, u32[]{:S(2)}, u32[]{:S(2)}) collective-permute-start(bf16[2,2,256,1536]{2,3,0,1:T(8,128)(2,1)} %bitcast.105), channel_id=1, source_target_pairs={{0,4},{4,0},{8,12},{12,8},{16,20},{20,16},{24,28},{28,24},{1,5},{5... | collective-permute-start | bytes 9437192 | tf_op jit(solution)/shard_map/ppermute | solution.py:487
  552.3 17.9 %collective-permute-start.33 = (bf16[128,2048]{1,0:T(8,128)(2,1)}, bf16[128,2048]{1,0:T(8,128)(2,1)}, u32[]{:S(2)}, u32[]{:S(2)}) collective-permute-start(bf16[128,2048]{1,0:T(8,128)(2,1)} %get-tuple-element.165), channel_id=1, source_target_pairs={{0,2},{1,3},{2,0},{3,1},{4,6},{5,7},{6,4},{7,5},{8,10},{9,11},{10,... | collective-permute-start | bytes 1572872 | tf_op jit(solution)/shard_map/ppermute | solution.py:487
  561.2 71.9 %collective-permute-start.39 = (bf16[2,256,1024]{1,2,0:T(8,128)(2,1)}, bf16[2,256,1024]{1,2,0:T(8,128)(2,1)}, u32[]{:S(2)}, u32[]{:S(2)}) collective-permute-start(bf16[2,256,1024]{1,2,0:T(8,128)(2,1)} %bitcast.118), channel_id=1, source_target_pairs={{0,16},{4,20},{8,24},{12,28},{16,0},{20,4},{24,8},{28,12},{1,17},{... | collective-permute-start | bytes 3145736 | tf_op jit(solution)/shard_map/ppermute | solution.py:487
  565.5 89.2 %collective-permute-start.41 = (bf16[2,256,1024]{1,2,0:T(8,128)(2,1)}, bf16[2,256,1024]{1,2,0:T(8,128)(2,1)}, u32[]{:S(2)}, u32[]{:S(2)}) collective-permute-start(bf16[2,256,1024]{1,2,0:T(8,128)(2,1)} %bitcast.117), channel_id=1, source_target_pairs={{0,16},{4,20},{8,24},{12,28},{16,0},{20,4},{24,8},{28,12},{1,17},{... | collective-permute-start | bytes 3145736 | tf_op jit(solution)/shard_map/ppermute | solution.py:487
  568.5 66.2 %collective-permute-start.22 = (bf16[256,2048]{1,0:T(8,128)(2,1)S(1)}, bf16[256,2048]{1,0:T(8,128)(2,1)S(1)}, u32[]{:S(2)}, u32[]{:S(2)}) collective-permute-start(bf16[256,2048]{1,0:T(8,128)(2,1)S(1)} %pad_maximum_fusion.8), channel_id=1, source_target_pairs={{0,1},{1,0},{2,3},{3,2},{4,5},{5,4},{6,7},{7,6},{8,9},{9,8},{10,11... | collective-permute-start | bytes 3145736 | tf_op jit(solution)/shard_map/ppermute | solution.py:487
  571.5 71.8 %collective-permute-start.34 = (bf16[256,2048]{1,0:T(8,128)(2,1)S(1)}, bf16[256,2048]{1,0:T(8,128)(2,1)S(1)}, u32[]{:S(2)}, u32[]{:S(2)}) collective-permute-start(bf16[256,2048]{1,0:T(8,128)(2,1)S(1)} %pad_maximum_fusion.9), channel_id=1, source_target_pairs={{0,1},{1,0},{2,3},{3,2},{4,5},{5,4},{6,7},{7,6},{8,9},{9,8},{10,11... | collective-permute-start | bytes 3145736 | tf_op jit(solution)/shard_map/ppermute | solution.py:487
  634.6 31.1 %collective-permute-start.40 = (bf16[256,1024]{0,1:T(8,128)(2,1)S(1)}, bf16[256,1024]{0,1:T(8,128)(2,1)S(1)}, u32[]{:S(2)}, u32[]{:S(2)}) collective-permute-start(bf16[256,1024]{0,1:T(8,128)(2,1)S(1)} %dynamic-slice_bitcast_fusion.9), channel_id=1, source_target_pairs={{0,8},{4,12},{8,0},{12,4},{16,24},{20,28},{24,16},{28,20},{1,9},{5... | collective-permute-start | bytes 1572872 | tf_op jit(solution)/shard_map/ppermute | solution.py:487
  641.3 58.2 %collective-permute-start.37 = (bf16[2,256,1536]{1,2,0:T(8,128)(2,1)S(1)}, bf16[2,256,1536]{1,2,0:T(8,128)(2,1)S(1)}, u32[]{:S(2)}, u32[]{:S(2)}) collective-permute-start(bf16[2,256,1536]{1,2,0:T(8,128)(2,1)S(1)} %dynamic-slice_bitcast_fusion.6), channel_id=1, source_target_pairs={{0,8},{4,12},{8,0},{12,4},{16,24},{20,28},{24,16},{28,20},{1,9},{5... | collective-permute-start | bytes 4718600 | tf_op jit(solution)/shard_map/ppermute | solution.py:487
  657.0 54.5 %collective-permute-start.42 = (bf16[256,1024]{0,1:T(8,128)(2,1)}, bf16[256,1024]{0,1:T(8,128)(2,1)}, u32[]{:S(2)}, u32[]{:S(2)}) collective-permute-start(bf16[256,1024]{0,1:T(8,128)(2,1)} %dynamic-slice_bitcast_fusion.8), channel_id=1, source_target_pairs={{0,8},{4,12},{8,0},{12,4},{16,24},{20,28},{24,16},{28,20},{1,9},{5... | collective-permute-start | bytes 1572872 | tf_op jit(solution)/shard_map/ppermute | solution.py:487
  700.9 37.4 %collective-permute-start.38 = (bf16[256,1536]{0,1:T(8,128)(2,1)}, bf16[256,1536]{0,1:T(8,128)(2,1)}, u32[]{:S(2)}, u32[]{:S(2)}) collective-permute-start(bf16[256,1536]{0,1:T(8,128)(2,1)} %dynamic-slice_bitcast_fusion.7), channel_id=1, source_target_pairs={{0,16},{4,20},{8,24},{12,28},{16,0},{20,4},{24,8},{28,12},{1,17},{... | collective-permute-start | bytes 2359304 | tf_op jit(solution)/shard_map/ppermute | solution.py:487
  (74 other events, 572.3 us)
Sparse Core Ops, SparseCore 0:
  28.0 81.2 all-gather.1

commit v4 on v2

--- a/solution.py
+++ b/solution.py
@@ -46,14 +46,15 @@
     return ((slot & 1) * 2 + lax.shift_right_logical(slot, 1)) ^ tensor
 
 
-def stored_block(index, tensor):
-    return (index & ~3) + slot_quarter(index & 3, tensor)
+def stored_block(index, where_ref):
+    rank = lax.div(index, SLOTS) ^ where_ref[0]
+    return rank * SLOTS + slot_quarter(index & 3, where_ref[1])
 
 
 def block_plan(order_ref, cont_ref, where_ref, slot):
     count = cont_ref.shape[0]
     prompt_blocks = count // CONTS * PER_PROMPT
-    own = order_ref[where_ref[0] * SLOTS + slot_quarter(slot, where_ref[1])]
+    own = order_ref[stored_block(slot, where_ref)]
     is_prompt = own < prompt_blocks
     offset = own - prompt_blocks
     which = jnp.clip(lax.div(offset, PER_CONT), 0, count - 1)
@@ -67,7 +68,7 @@
 
 def fill_inverse(order_ref, where_ref, inverse_ref):
     def put(index, carry):
-        inverse_ref[order_ref[stored_block(index, where_ref[1])]] = index
+        inverse_ref[order_ref[stored_block(index, where_ref)]] = index
         return carry
 
     lax.fori_loop(0, order_ref.shape[0], put, 0)
@@ -126,9 +127,26 @@
     return jnp.dot(left, right, preferred_element_type=jnp.float32)
 
 
-def forward_kernel(rep, hps, order_ref, cont_ref, where_ref, q_ref, kv_ref, out_ref, lse_ref,
-                   inverse_ref, qt_ref, acc_ref):
+def start_parts(parts, buffer_ref, sem, column):
+    rows, width = parts[0].shape[0], buffer_ref.shape[1]
+    copies = [
+        pltpu.make_async_copy(
+            part.at[:, pl.ds(column, width)], buffer_ref.at[pl.ds(p * rows, rows), :], sem.at[p]
+        )
+        for p, part in enumerate(parts)
+    ]
+    for copy in copies:
+        copy.start()
+    return copies
+
+
+def forward_kernel(rep, hps, ctx_count, order_ref, cont_ref, where_ref, q_ref, wo_ref, *refs):
+    parts, refs = refs[:ctx_count], refs[ctx_count:]
+    out_ref, lse_ref, keep_ref, send_ref, kv_ref, inverse_ref, qt_ref, acc_ref, sem = refs
+    copies = start_parts(parts, kv_ref, sem, 0)
     fill_inverse(order_ref, where_ref, inverse_ref)
+    for copy in copies:
+        copy.wait()
     q_blocks = q_ref.shape[0] // BLOCK
     factor = LOG2E / math.sqrt(HEAD_SIZE)
     width = rep * HEAD_SIZE
@@ -177,15 +195,29 @@
                 out_ref[rows, pl.ds(h * width + r * HEAD_SIZE, HEAD_SIZE)] = part.T.astype(
                     jnp.bfloat16
                 )
-            lse_ref[0, h, pl.ds(qb, 1), :] = best + jnp.log2(total)
+            lse_ref[h, pl.ds(qb, 1), :] = best + jnp.log2(total)
         return carry
 
     lax.fori_loop(0, q_blocks, one_query_block, 0)
-
-
-def backward_kernel(rep, hps, order_ref, cont_ref, where_ref, q_ref, kv_ref, gm_ref, mix_ref,
-                    lse_ref, cos_ref, sin_ref, gq_ref, keep_ref, send_ref, inverse_ref, qt_ref, gmt_ref, gqt_ref, acc_ref):
+    mixed = out_ref[...]
+    half = keep_ref.shape[0]
+    for n in range(0, wo_ref.shape[1], 512):
+        cols = slice(n, n + 512)
+        partial = dot(mixed, wo_ref[:, cols]).astype(jnp.bfloat16)
+        keep_ref[:, cols] = partial[:half]
+        send_ref[:, cols] = partial[half:]
+
+
+def backward_kernel(rep, hps, ctx_count, head, order_ref, cont_ref, where_ref, q_ref, gb_ref, wo_ref,
+                    mix_ref, lse_ref, cos_ref, sin_ref, *refs):
+    parts, refs = refs[:ctx_count], refs[ctx_count:]
+    gq_ref, keep_ref, send_ref = refs[:3]
+    kv_ref, gm_ref, inverse_ref, qt_ref, gmt_ref, gqt_ref, acc_ref, sem = refs[3:]
+    copies = start_parts(parts, kv_ref, sem, head * kv_ref.shape[1])
     fill_inverse(order_ref, where_ref, inverse_ref)
+    gm_ref[...] = right_dot(gb_ref[...], wo_ref[...]).astype(jnp.bfloat16)
+    for copy in copies:
+        copy.wait()
     q_blocks = q_ref.shape[0] // BLOCK
     scale = 1.0 / math.sqrt(HEAD_SIZE)
     factor = LOG2E * scale
@@ -232,7 +264,7 @@
                     gmt.astype(jnp.float32) * mixt.astype(jnp.float32), axis=0, keepdims=True
                 )
             )
-            lses.append(lse_ref[0, h, pl.ds(qb, 1), :])
+            lses.append(lse_ref[h, pl.ds(qb, 1), :])
         for h in range(hps):
             q_rows = stack_rows(q_ref, rows, h * width, rep)
             gm_rows = stack_rows(gm_ref, rows, h * width, rep)
@@ -265,10 +297,9 @@
     lax.fori_loop(0, q_blocks, one_query_block, 0)
 
     blocks = order_ref.shape[0]
-    ctx_count = blocks // SLOTS
 
     def place(index):
-        chunk = lax.div(index, SLOTS) ^ where_ref[0]
+        chunk = lax.div(index, SLOTS)
         spot = (chunk & 1) * (ctx_count // 2) + (chunk & 2) // 2 * (ctx_count // 4) + (
             lax.shift_right_logical(chunk, 2)
         )
@@ -297,69 +328,55 @@
     lax.fori_loop(0, blocks, flush, 0)
 
 
-def attention_sizes(q, kv):
-    kv_heads = kv.shape[1] // (2 * HEAD_SIZE)
+def attention_forward(q, w_out, parts, order, cont, where):
+    ctx_count = len(parts)
+    rows, tokens = q.shape[0], ctx_count * q.shape[0]
+    kv_heads = parts[0].shape[1] // (2 * HEAD_SIZE)
     rep = q.shape[1] // HEAD_SIZE // kv_heads
-    hps = kv_heads if kv.shape[0] <= 8192 else 1
-    return kv_heads, rep, hps
-
-
-def attention_forward(q, kv, order, cont, where):
-    kv_heads, rep, hps = attention_sizes(q, kv)
-    rows, tokens = q.shape[0], kv.shape[0]
-    q_blocks = rows // BLOCK
-    wide = hps * rep * HEAD_SIZE
-    q_spec = pl.BlockSpec((rows, wide), lambda g, *_: (0, g))
-    flops = 4 * rows * (tokens // 2) * q.shape[1]
+    q_blocks, model = rows // BLOCK, w_out.shape[1]
+    vmem, smem, any_ = (
+        pl.BlockSpec(memory_space=space) for space in (pltpu.VMEM, pltpu.SMEM, pl.ANY)
+    )
+    flops = 2 * rows * tokens * q.shape[1] + 2 * rows * q.shape[1] * model
+    half = jax.ShapeDtypeStruct((rows // 2, model), jnp.bfloat16)
     return pl.pallas_call(
-        functools.partial(forward_kernel, rep, hps),
+        functools.partial(forward_kernel, rep, kv_heads, ctx_count),
         out_shape=(
             jax.ShapeDtypeStruct(q.shape, jnp.bfloat16),
-            jax.ShapeDtypeStruct((kv_heads // hps, hps, q_blocks, rep * BLOCK), jnp.float32),
+            jax.ShapeDtypeStruct((kv_heads, q_blocks, rep * BLOCK), jnp.float32),
+            half,
+            half,
         ),
-        grid_spec=pltpu.PrefetchScalarGridSpec(
-            num_scalar_prefetch=3,
-            grid=(kv_heads // hps,),
-            in_specs=[
-                q_spec,
-                pl.BlockSpec((tokens, 2 * hps * HEAD_SIZE), lambda g, *_: (0, g)),
-            ],
-            out_specs=[
-                q_spec,
-                pl.BlockSpec((1, hps, q_blocks, rep * BLOCK), lambda g, *_: (g, 0, 0, 0)),
-            ],
-            scratch_shapes=[
-                pltpu.SMEM((order.shape[0],), jnp.int32),
-                pltpu.VMEM((hps, HEAD_SIZE, rep * BLOCK), jnp.bfloat16),
-                pltpu.VMEM((hps, HEAD_SIZE, rep * BLOCK), jnp.float32),
-            ],
-        ),
-        compiler_params=pltpu.CompilerParams(vmem_limit_bytes=56 << 20),
-        cost_estimate=pl.CostEstimate(
-            flops=flops, bytes_accessed=2 * (q.size * 2 + kv.size), transcendentals=flops // 512
-        ),
+        in_specs=[smem] * 3 + [vmem] * 2 + [any_] * ctx_count,
+        out_specs=[vmem] * 4,
+        scratch_shapes=[
+            pltpu.VMEM((tokens, parts[0].shape[1]), jnp.bfloat16),
+            pltpu.SMEM((order.shape[0],), jnp.int32),
+            pltpu.VMEM((kv_heads, HEAD_SIZE, rep * BLOCK), jnp.bfloat16),
+            pltpu.VMEM((kv_heads, HEAD_SIZE, rep * BLOCK), jnp.float32),
+            pltpu.SemaphoreType.DMA((ctx_count,)),
+        ],
+        compiler_params=pltpu.CompilerParams(vmem_limit_bytes=40 << 20),
+        cost_estimate=cost(flops, 2 * tokens * parts[0].shape[1] + 4 * rows * model),
         name="attention_forward",
-    )(order, cont, where, q, kv)
-
-
-def attention_backward(head, q, kv, grad_mixed, mixed, lse, cosine, sine, order, cont, where):
-    kv_heads, rep, _ = attention_sizes(q, kv)
-    hps_forward = lse.shape[1]
-    rows, tokens = q.shape[0], kv.shape[0]
-    q_blocks = rows // BLOCK
+    )(order, cont, where, q, w_out, *parts)
+
+
+def attention_backward(head, q, grad_branch, w_out, mixed, lse, parts, cosine, sine, order, cont,
+                       where):
+    ctx_count = len(parts)
+    rows, tokens = q.shape[0], ctx_count * q.shape[0]
+    kv_heads = parts[0].shape[1] // (2 * HEAD_SIZE)
+    rep = q.shape[1] // HEAD_SIZE // kv_heads
+    q_blocks, model = rows // BLOCK, w_out.shape[1]
     wide = rep * HEAD_SIZE
     q_spec = pl.BlockSpec((rows, wide), lambda g, *_: (0, head))
-    kv_spec = pl.BlockSpec((tokens, 2 * HEAD_SIZE), lambda g, *_: (0, head))
-    lse_spec = pl.BlockSpec(
-        (1, 1, q_blocks, rep * BLOCK),
-        lambda g, *_: (head // hps_forward, head % hps_forward, 0, 0),
-    )
     whole = lambda g, *_: (0, 0)
     table_spec = pl.BlockSpec((rows, HEAD_SIZE), whole)
     half = (tokens // 2, 2 * HEAD_SIZE)
-    flops = 10 * rows * (tokens // 2) * wide
+    flops = 5 * rows * tokens * wide + 2 * rows * wide * model
     return pl.pallas_call(
-        functools.partial(backward_kernel, rep, 1),
+        functools.partial(backward_kernel, rep, 1, ctx_count, head),
         out_shape=(
             jax.ShapeDtypeStruct((rows, wide), jnp.bfloat16),
             jax.ShapeDtypeStruct(half, jnp.bfloat16),
@@ -368,28 +385,36 @@
         grid_spec=pltpu.PrefetchScalarGridSpec(
             num_scalar_prefetch=3,
             grid=(1,),
-            in_specs=[q_spec, kv_spec, q_spec, q_spec, lse_spec, table_spec, table_spec],
+            in_specs=[
+                q_spec,
+                pl.BlockSpec((rows, model), whole),
+                pl.BlockSpec((wide, model), lambda g, *_: (head, 0)),
+                q_spec,
+                pl.BlockSpec((1, q_blocks, rep * BLOCK), lambda g, *_: (head, 0, 0)),
+                table_spec,
+                table_spec,
+            ]
+            + [pl.BlockSpec(memory_space=pl.ANY)] * ctx_count,
             out_specs=[
                 pl.BlockSpec((rows, wide), whole),
                 pl.BlockSpec(half, whole),
                 pl.BlockSpec(half, whole),
             ],
             scratch_shapes=[
+                pltpu.VMEM((tokens, 2 * HEAD_SIZE), jnp.bfloat16),
+                pltpu.VMEM((rows, wide), jnp.bfloat16),
                 pltpu.SMEM((order.shape[0],), jnp.int32),
                 pltpu.VMEM((1, HEAD_SIZE, rep * BLOCK), jnp.bfloat16),
                 pltpu.VMEM((1, HEAD_SIZE, rep * BLOCK), jnp.bfloat16),
                 pltpu.VMEM((1, HEAD_SIZE, rep * BLOCK), jnp.float32),
                 pltpu.VMEM((tokens, 2 * HEAD_SIZE), jnp.float32),
+                pltpu.SemaphoreType.DMA((ctx_count,)),
             ],
         ),
         compiler_params=pltpu.CompilerParams(vmem_limit_bytes=56 << 20),
-        cost_estimate=pl.CostEstimate(
-            flops=flops,
-            bytes_accessed=4 * (rows * wide * 2 + tokens * 2 * HEAD_SIZE),
-            transcendentals=flops // 1280,
-        ),
+        cost_estimate=cost(flops, 4 * tokens * wide + 2 * rows * model),
         name=f"attention_backward_{head}",
-    )(order, cont, where, q, kv, grad_mixed, mixed, lse, cosine, sine)
+    )(order, cont, where, q, grad_branch, w_out, mixed, lse, cosine, sine, *parts)
 
 
 def input_kernel(order_ref, cont_ref, where_ref, x_ref, gain_ref, wq_ref, wk_ref, wv_ref,
@@ -405,7 +430,7 @@
         full = x_ref[pl.ds(pl.multiple_of(quarter * BLOCK, BLOCK), BLOCK), :].astype(jnp.float32)
         inv = lax.rsqrt(jnp.mean(full * full, axis=-1, keepdims=True) + eps_norm)
         first_ref[rows, :] = (full * inv * gain_ref[...]).astype(jnp.bfloat16)
-        own = order_ref[where_ref[0] * SLOTS + quarter]
+        own = order_ref[stored_block(slot, where_ref)]
         spot = jnp.where(
             own < prompt_blocks,
             lax.rem(own, PER_PROMPT),
@@ -452,35 +477,235 @@
         in_specs=[smem] * 3 + [vmem] * 9,
         out_specs=[vmem] * 5,
         compiler_params=pltpu.CompilerParams(vmem_limit_bytes=40 << 20),
-        cost_estimate=pl.CostEstimate(
-            flops=flops, bytes_accessed=4 * x.size + 2 * wq.size + 4 * wk.size, transcendentals=0
-        ),
+        cost_estimate=cost(flops, 4 * x.size + 2 * wq.size + 4 * wk.size),
         name="input_stage",
     )(order, cont, where, x, gain.reshape(1, -1), wq, wk, wv, *tables)
 
 
-def kv_finish_kernel(keep_ref, got_ref, cos_ref, sin_ref, gk_ref, gv_ref):
-    total = keep_ref[...].astype(jnp.float32) + got_ref[...].astype(jnp.float32)
-    total = total.astype(jnp.bfloat16)
-    key = total[:, :HEAD_SIZE].astype(jnp.float32)
-    gk_ref[...] = unrotate(key, cos_ref[...], sin_ref[...]).astype(jnp.bfloat16)
-    gv_ref[...] = total[:, HEAD_SIZE:]
-
-
-def kv_finish(keep, got, cosine, sine):
-    rows = keep.shape[0]
+def cost(flops, bytes_accessed):
+    return pl.CostEstimate(
+        flops=int(flops), bytes_accessed=int(bytes_accessed), transcendentals=0
+    )
+
+
+def put_share(value, index, x_bit, keep_ref, send_ref, swap_bits):
+    spot = lax.shift_right_logical(index, 1)
+    if swap_bits:
+        spot = (spot & 1) * (keep_ref.shape[0] // 2) + lax.shift_right_logical(spot, 1)
+    stays = (index & 1) == x_bit
+    value = value.astype(keep_ref.dtype)
+
+    @pl.when(stays)
+    def _():
+        keep_ref[pl.ds(spot, 1)] = value[None]
+
+    @pl.when(jnp.logical_not(stays))
+    def _():
+        send_ref[pl.ds(spot, 1)] = value[None]
+
+
+def ffn_kernel(where_ref, near_ref, far_ref, cot_near_ref, cot_far_ref, wg_ref, wu_ref, wd_ref,
+               hid_ref, gg_ref, gu_ref, keep_ref, send_ref):
+    rows = near_ref.shape[0]
+    for k, (in_ref, cot_ref) in enumerate(((near_ref, cot_near_ref), (far_ref, cot_far_ref))):
+        span = slice(k * rows, (k + 1) * rows)
+        gate = dot(in_ref[...], wg_ref[...])
+        upward = dot(in_ref[...], wu_ref[...])
+        grad_hidden = right_dot(cot_ref[...], wd_ref[...])
+        sigma = jax.nn.sigmoid(gate)
+        swish = gate * sigma
+        hid_ref[span, :] = (swish * upward).astype(jnp.bfloat16)
+        gg_ref[span, :] = (
+            grad_hidden * upward * sigma * (1.0 + gate * (1.0 - sigma))
+        ).astype(jnp.bfloat16)
+        gu_ref[span, :] = (grad_hidden * swish).astype(jnp.bfloat16)
+    turned_near, turned_far = hid_ref[:rows, :].T, hid_ref[rows:, :].T
+    share = keep_ref.shape[2]
+    for f in range(cot_near_ref.shape[1] // share):
+        cols = slice(f * share, (f + 1) * share)
+        value = dot(turned_near, cot_near_ref[:, cols]) + dot(turned_far, cot_far_ref[:, cols])
+        put_share(value, jnp.int32(f), where_ref[0] & 1, keep_ref, send_ref, False)
+
+
+def ffn_stage(second, cot, w_gate, w_up, w_down, ctx_count, where):
+    rows, model = second[0].shape
+    units = w_gate.shape[1] // 2
+    block = 256
+    steps = units // block
+    share = model // ctx_count
+    pair = lambda where_ref: lax.shift_right_logical(where_ref[0], 1) & 1
+    row_spec = pl.BlockSpec(
+        (rows, model), lambda i, w: (0, 0), pipeline_mode=pl.Buffered(1)
+    )
+    col_spec = pl.BlockSpec((model, block), lambda i, w: (0, pair(w) * steps + i))
+    unit_spec = pl.BlockSpec((2 * rows, block), lambda i, w: (0, i))
+    share_spec = pl.BlockSpec((ctx_count // 2, block, share), lambda i, w: (0, i, 0))
+    unit = jax.ShapeDtypeStruct((2 * rows, units), jnp.bfloat16)
+    shares = jax.ShapeDtypeStruct((ctx_count // 2, units, share), jnp.bfloat16)
+    return pl.pallas_call(
+        ffn_kernel,
+        out_shape=(unit, unit, unit, shares, shares),
+        grid_spec=pltpu.PrefetchScalarGridSpec(
+            num_scalar_prefetch=1,
+            grid=(steps,),
+            in_specs=[row_spec] * 4
+            + [
+                col_spec,
+                col_spec,
+                pl.BlockSpec((block, model), lambda i, w: (pair(w) * steps + i, 0)),
+            ],
+            out_specs=[unit_spec] * 3 + [share_spec] * 2,
+        ),
+        compiler_params=pltpu.CompilerParams(vmem_limit_bytes=44 << 20),
+        cost_estimate=cost(16 * rows * model * units, 16 * rows * model),
+        name="ffn_stage",
+    )(where, *second, *cot, w_gate, w_up, w_down)
+
+
+def grad_second_kernel(where_ref, gg_ref, gu_ref, wg_ref, wu_ref, keep_ref, send_ref):
+    total = right_dot(gg_ref[...], wg_ref[...]) + right_dot(gu_ref[...], wu_ref[...])
+    half = keep_ref.shape[0]
+    keep_ref[...] = total[:half].astype(jnp.bfloat16)
+    send_ref[...] = total[half:].astype(jnp.bfloat16)
+
+
+def ffn_out_kernel(where_ref, hid_ref, wd_ref, keep_ref, send_ref):
+    total = dot(hid_ref[...], wd_ref[...])
+    half = keep_ref.shape[0]
+    keep_ref[...] = total[:half].astype(jnp.bfloat16)
+    send_ref[...] = total[half:].astype(jnp.bfloat16)
+
+
+def unit_sum(kernel, name, lefts, rights, transposed, where):
+    rows, units = lefts[0].shape
+    model = rights[0].shape[0 if transposed else 1]
+    block = 512
+    pair = lambda where_ref: lax.shift_right_logical(where_ref[0], 1) & 1
+    if transposed:
+        right_spec = pl.BlockSpec((block, units), lambda n, w: (n, pair(w)))
+    else:
+        right_spec = pl.BlockSpec((units, block), lambda n, w: (pair(w), n))
+    left_spec = pl.BlockSpec((rows, units), lambda n, w: (0, 0), pipeline_mode=pl.Buffered(1))
+    half = jax.ShapeDtypeStruct((rows // 2, model), jnp.bfloat16)
+    half_spec = pl.BlockSpec((rows // 2, block), lambda n, w: (0, n))
+    return pl.pallas_call(
+        kernel,
+        out_shape=(half, half),
+        grid_spec=pltpu.PrefetchScalarGridSpec(
+            num_scalar_prefetch=1,
+            grid=(model // block,),
+            in_specs=[left_spec] * len(lefts) + [right_spec] * len(rights),
+            out_specs=[half_spec, half_spec],
+        ),
+        compiler_params=pltpu.CompilerParams(vmem_limit_bytes=32 << 20),
+        cost_estimate=cost(2 * len(lefts) * rows * units * model, 4 * rows * model),
+        name=name,
+    )(where, *lefts, *rights)
+
+
+def shares_kernel(left_count, swap_bits, pairs, where_ref, *refs):
+    lefts, refs = refs[:left_count], refs[left_count:]
+    rights, (keep_ref, send_ref) = refs[:-2], refs[-2:]
+    share = keep_ref.shape[1]
+    turned = [left[...].T for left in lefts]
+    step = pl.program_id(0)
+    start = 0
+    pieces = []
+    for terms in pairs:
+        pieces.append(
+            sum(dot(turned[l], rights[r][rows, :]) for l, r, rows in terms)
+        )
+    value = pieces[0] if len(pieces) == 1 else jnp.concatenate(pieces, axis=1)
+    per_step = value.shape[0] // share
+    for k in range(per_step):
+        put_share(
+            value[k * share : (k + 1) * share],
+            step * per_step + k,
+            where_ref[0] & 1,
+            keep_ref,
+            send_ref,
+            swap_bits,
+        )
+
+
+def weight_shares(name, lefts, rights, pairs, width, ctx_count, swap_bits, where):
+    rows, model = lefts[0].shape
+    block = 256
+    share = model // ctx_count
+    shares = jax.ShapeDtypeStruct((ctx_count // 2, share, width), jnp.bfloat16)
+    share_spec = pl.BlockSpec(shares.shape, lambda i, w: (0, 0, 0))
+    flops = 2 * model * sum(
+        rights[r].shape[1] * lefts[l].shape[0] for terms in pairs for l, r, _ in terms
+    )
+    return pl.pallas_call(
+        functools.partial(shares_kernel, len(lefts), swap_bits, pairs),
+        out_shape=(shares, shares),
+        grid_spec=pltpu.PrefetchScalarGridSpec(
+            num_scalar_prefetch=1,
+            grid=(model // block,),
+            in_specs=[pl.BlockSpec((rows, block), lambda i, w: (0, i))] * len(lefts)
+            + [
+                pl.BlockSpec(r.shape, lambda i, w: (0, 0), pipeline_mode=pl.Buffered(1))
+                for r in rights
+            ],
+            out_specs=[share_spec, share_spec],
+        ),
+        compiler_params=pltpu.CompilerParams(vmem_limit_bytes=36 << 20),
+        cost_estimate=cost(flops, 4 * rows * model),
+        name=name,
+    )(where, *lefts, *rights)
+
+
+def tail_kernel(kv_heads, where_ref, *refs):
+    sums, refs = refs[: 2 * kv_heads], refs[2 * kv_heads :]
+    cos_ref, sin_ref, refs = refs[0], refs[1], refs[2:]
+    gq_refs, refs = refs[:kv_heads], refs[kv_heads:]
+    wq_ref, wk_ref, wv_ref, keep_ref, send_ref, gkv_ref = refs
+    cosine, sine = cos_ref[...], sin_ref[...]
+    for h in range(kv_heads):
+        total = sums[2 * h][...].astype(jnp.float32) + sums[2 * h + 1][...].astype(jnp.float32)
+        total = total.astype(jnp.bfloat16)
+        key = unrotate(total[:, :HEAD_SIZE].astype(jnp.float32), cosine, sine)
+        cols = slice(h * HEAD_SIZE, (h + 1) * HEAD_SIZE)
+        gkv_ref[:, cols] = key.astype(jnp.bfloat16)
+        cols = slice((kv_heads + h) * HEAD_SIZE, (kv_heads + h + 1) * HEAD_SIZE)
+        gkv_ref[:, cols] = total[:, HEAD_SIZE:]
+    half = keep_ref.shape[0]
+    key_width = kv_heads * HEAD_SIZE
+    wide = gq_refs[0].shape[1]
+    for n in range(0, wq_ref.shape[0], 512):
+        span = slice(n, n + 512)
+        total = right_dot(gkv_ref[:, :key_width], wk_ref[span, :])
+        total += right_dot(gkv_ref[:, key_width:], wv_ref[span, :])
+        for h in range(kv_heads):
+            total += right_dot(gq_refs[h][...], wq_ref[span, h * wide : (h + 1) * wide])
+        total = total.astype(jnp.bfloat16)
+        keep_ref[:, span] = total[:half]
+        send_ref[:, span] = total[half:]
+
+
+def tail_stage(kv_sums, cosine, sine, grad_queries, wq, wk, wv, where):
+    rows, model = cosine.shape[0], wq.shape[0]
+    kv_heads = len(grad_queries)
     vmem = pl.BlockSpec(memory_space=pltpu.VMEM)
-    shape = jax.ShapeDtypeStruct((rows, HEAD_SIZE), jnp.bfloat16)
+    half = jax.ShapeDtypeStruct((rows // 2, model), jnp.bfloat16)
+    flat = [term for sums in kv_sums for term in sums]
     return pl.pallas_call(
-        kv_finish_kernel,
-        out_shape=(shape, shape),
-        in_specs=[vmem] * 4,
-        out_specs=[vmem] * 2,
-        cost_estimate=pl.CostEstimate(
-            flops=8 * keep.size, bytes_accessed=6 * keep.size, transcendentals=0
+        functools.partial(tail_kernel, kv_heads),
+        out_shape=(
+            half,
+            half,
+            jax.ShapeDtypeStruct((rows, 2 * kv_heads * HEAD_SIZE), jnp.bfloat16),
         ),
-        name="kv_finish",
-    )(keep, got, cosine, sine)
+        in_specs=[pl.BlockSpec(memory_space=pltpu.SMEM)]
+        + [vmem] * (len(flat) + 2 + kv_heads + 3),
+        out_specs=[vmem] * 3,
+        compiler_params=pltpu.CompilerParams(vmem_limit_bytes=32 << 20),
+        cost_estimate=cost(
+            2 * rows * model * (wq.shape[1] + 2 * wk.shape[1]), 4 * rows * model + 4 * wq.size
+        ),
+        name="tail_stage",
+    )(where, *flat, cosine, sine, *grad_queries, wq, wk, wv)
 
 
 def flip(value, axis, mask):
@@ -493,23 +718,33 @@
 
 def slots_of(value, tensor):
     rows = value.shape[0] // SLOTS
-    return jnp.concatenate(
-        [
-            lax.dynamic_slice_in_dim(value, (tensor ^ SLOT_XOR[u]) * rows, rows)
-            for u in range(SLOTS)
-        ]
-    )
+    return [
+        lax.dynamic_slice_in_dim(value, (tensor ^ SLOT_XOR[u]) * rows, rows)
+        for u in range(SLOTS)
+    ]
+
+
+def after(dep, *values):
+    held = lax.optimization_barrier((dep,) + values)[1:]
+    return held[0] if len(held) == 1 else held
 
 
 def gather_slots(own):
-    other = flip(own, "tp", 2)
-    return jnp.concatenate([own, other, flip(own, "tp", 1), flip(other, "tp", 1)])
+    near = jnp.concatenate([own, flip(own, "tp", 2)])
+    return jnp.concatenate([near, flip(near, "tp", 1)])
+
+
+def gather_pair(own):
+    partner = flip(own, "ctx", 2)
+    near = jnp.concatenate([own, partner, flip(own, "tp", 2), flip(partner, "tp", 2)])
+    return near, flip(near, "tp", 1)
 
 
 def gather_rows(own, tensor):
     rows = own.shape[0]
-    other = flip(own, "tp", 2)
-    pieces = (own, other, flip(own, "tp", 1), flip(other, "tp", 1))
+    near = jnp.concatenate([own, flip(own, "tp", 2)])
+    far = flip(near, "tp", 1)
+    pieces = (near[:rows], near[rows:], far[:rows], far[rows:])
     result = jnp.zeros((SLOTS * rows,) + own.shape[1:], own.dtype)
     for u in range(SLOTS):
         result = lax.dynamic_update_slice_in_dim(
@@ -518,11 +753,50 @@
     return result
 
 
-def scatter_slots(partial):
-    half = partial.shape[0] // 2
-    pair = add(partial[:half], flip(partial[half:], "tp", 1))
-    quarter = half // 2
-    return pair[:quarter], flip(pair[quarter:], "tp", 2)
+def scatter_slots(keep, send):
+    got = flip(send, "tp", 1)
+    quarter = keep.shape[0] // 2
+    far = flip(add(keep[quarter:], got[quarter:]), "tp", 2)
+    return add(keep[:quarter], got[:quarter]), far
+
+
+def pair_scatter(keep, send):
+    got = flip(send, "tp", 1)
+    n = keep.shape[0] // 4
+    near = [add(keep[k * n : (k + 1) * n], got[k * n : (k + 1) * n]) for k in (3, 1, 2, 0)]
+    away = flip(add(near[1], flip(near[0], "tp", 2)), "ctx", 2)
+    return near[3], flip(near[2], "tp", 2), away
+
+
+def total(terms):
+    return sum(term.astype(jnp.float32) for term in terms)
+
+
+def gather_keys(kv_local, ctx_count):
+    parts = {0: kv_local}
+    for mask in range(2, ctx_count, 2):
+        parts[mask] = flip(kv_local, "ctx", mask)
+    for mask in range(0, ctx_count, 2):
+        parts[mask + 1] = flip(parts[mask], "ctx", 1)
+    return [parts[mask] for mask in range(ctx_count)]
+
+
+class Reduce:
+    def __init__(self, keep, send):
+        self.keep, self.got = keep, flip(send, "ctx", 1)
+
+    def halve(self, mask, ctx, dep=None):
+        keep, got = self.keep, self.got
+        if dep is not None:
+            keep, got = after(dep, keep, got)
+        n = keep.shape[0] // 2
+        bit = lax.div(ctx, mask) % 2
+        pick = lambda value, index: lax.dynamic_slice_in_dim(value, index * n, n, 0)
+        away = flip(add(pick(keep, 1 - bit), pick(got, 1 - bit)), "ctx", mask)
+        self.keep, self.got = add(pick(keep, bit), pick(got, bit)), away
+
+    def sum(self):
+        return (self.keep.astype(jnp.float32) + self.got.astype(jnp.float32))[0]
 
 
 def high_masks(ctx_count):
@@ -533,53 +807,30 @@
     return masks
 
 
-def step(parts, axis_bits, mask, index):
-    mine = lax.dynamic_index_in_dim(parts, index, axis_bits, keepdims=False)
-    away = lax.dynamic_index_in_dim(parts, 1 - index, axis_bits, keepdims=False)
-    return mine, flip(away, "ctx", mask)
-
-
-def bits_of(ctx, ctx_count):
-    return [(ctx // mask) % 2 for mask in high_masks(ctx_count)]
-
-
-def reduce_attention(partial, ctx, ctx_count):
-    highs = high_masks(ctx_count)
-    width = partial.shape[1]
-    rows = partial.shape[0] // ctx_count
-    shaped = partial.astype(jnp.bfloat16).reshape((2,) * len(highs) + (2, 2, rows, width))
-    mine, got = step(shaped, len(highs) + 1, 1, ctx % 2)
-    shaped = add(mine, got)
-    mine, got = step(shaped, len(highs), 2, ctx // 2 % 2)
-    for mask, bit in zip(highs, bits_of(ctx, ctx_count)):
-        shaped = add(mine, got)
-        mine, got = step(shaped, 0, mask, bit)
-    return mine.astype(jnp.float32) + got.astype(jnp.float32)
-
-
-def reduce_ffn(partial, ctx, ctx_count):
-    highs = high_masks(ctx_count)
-    width = partial.shape[1]
-    rows = partial.shape[0] // ctx_count
-    shaped = partial.astype(jnp.bfloat16).reshape((2,) * len(highs) + (2, 2, rows, width))
-    mine, got = step(shaped, len(highs) + 1, 1, ctx % 2)
-    for mask, bit in zip(highs, bits_of(ctx, ctx_count)):
-        shaped = add(mine, got)
-        mine, got = step(shaped, 0, mask, bit)
-    shaped = add(mine, got)
-    pair = ctx // 2 % 2
-    mine, got = step(shaped, 0, 2, pair)
-    low, high = jnp.where(pair == 0, mine, got), jnp.where(pair == 0, got, mine)
-    return jnp.concatenate([low, high], axis=1).astype(jnp.float32)
-
-
-def reduce_kv(keep, send, ctx_count):
-    got = flip(send, "ctx", 1)
-    for mask in [2] + high_masks(ctx_count):
-        total = add(keep, got)
-        half = total.shape[0] // 2
-        keep, got = total[:half], flip(total[half:], "ctx", mask)
-    return keep, got
+def both_halves(reduce, ctx, axis, dep=None):
+    keep, got = reduce.keep, reduce.got
+    if dep is not None:
+        keep, got = after(dep, keep, got)
+    pair = lax.div(ctx, 2) % 2
+    pick = lambda value, index: lax.dynamic_slice_in_dim(value, index, 1, 0)[0]
+    other = flip(add(pick(keep, 1 - pair), pick(got, 1 - pair)), "ctx", 2)
+    own = add(pick(keep, pair), pick(got, pair))
+    low, high = jnp.where(pair == 0, own, other), jnp.where(pair == 0, other, own)
+    return jnp.concatenate([low, high], axis=axis).astype(jnp.float32)
+
+
+class KvReduce:
+    def __init__(self, keep, send, ctx_count):
+        self.ctx_count = ctx_count
+        self.keep, self.got = keep, flip(send, "ctx", 1)
+
+    def high(self, dep):
+        keep, got = after(dep, self.keep, self.got)
+        for mask in [2] + high_masks(self.ctx_count):
+            n = keep.shape[0] // 2
+            away = flip(add(keep[n:], got[n:]), "ctx", mask)
+            keep, got = add(keep[:n], got[:n]), away
+        self.keep, self.got = keep, got
 
 
 def norm_back(grad_out, normed, inv_scale, gain):
@@ -606,105 +857,128 @@
     ctx_count = lax.axis_size("ctx")
     tp_count = lax.axis_size("tp")
     ctx, tensor = lax.axis_index("ctx"), lax.axis_index("tp")
-    pair = ctx // 2 % 2
     where = jnp.stack([ctx, tensor]).astype(jnp.int32)
     quarter = layer_input.shape[0] // SLOTS
     kv_heads = key_matrix.shape[1] // HEAD_SIZE
-    half_units = w_gate.shape[1] // 2
+    highs = high_masks(ctx_count)
 
     first_input, queries, kv_local, cosine, sine = input_stage(
         layer_input, attn_gain, w_query, key_matrix, value_matrix, block_order, cont_prompt, where
     )
-    kv_all = lax.all_gather(kv_local, "ctx", axis=0, tiled=True)
-
-    gate_half = lax.dynamic_slice_in_dim(w_gate, pair * half_units, half_units, 1)
-    up_half = lax.dynamic_slice_in_dim(w_up, pair * half_units, half_units, 1)
-    down_half = lax.dynamic_slice_in_dim(w_down, pair * half_units, half_units, 0)
-    cot_own = lax.dynamic_slice_in_dim(cotangent, tensor * quarter, quarter)
-    cot_rows = jnp.concatenate(
-        [slots_of(cotangent, tensor), gather_slots(flip(cot_own, "ctx", 2))]
-    )
-    grad_hidden = right_dot(cot_rows, down_half)
-
-    mixed, log_total = attention_forward(
-        queries, kv_all, block_order, cont_prompt, where
-    )
-    mine, got = scatter_slots(plain_dot(mixed, w_out).astype(jnp.bfloat16))
+    parts = gather_keys(kv_local, ctx_count)
+
+    cot_own = after(first_input, lax.dynamic_slice_in_dim(cotangent, tensor * quarter, quarter))
+    cot_slots = slots_of(cotangent, tensor)
+    cot_part = flip(cot_own, "ctx", 2)
+    cot_part = jnp.concatenate([cot_part, flip(cot_part, "tp", 2)])
+    cot_far = flip(cot_part, "tp", 1)
+    cot = (
+        jnp.concatenate([cot_slots[0], cot_part[:quarter], cot_slots[1], cot_part[quarter:]]),
+        jnp.concatenate([cot_slots[2], cot_far[:quarter], cot_slots[3], cot_far[quarter:]]),
+    )
+
+    mixed, log_total, keep, send = attention_forward(
+        queries, w_out, parts, block_order, cont_prompt, where
+    )
     own_input = lax.dynamic_slice_in_dim(layer_input, tensor * quarter, quarter)
     own_input = own_input.astype(jnp.float32)
-    middle = own_input + (mine.astype(jnp.float32) + got.astype(jnp.float32))
+    middle = own_input + total(scatter_slots(keep, send))
     inv_two = lax.rsqrt(jnp.mean(middle * middle, axis=-1, keepdims=True) + eps_norm)
     normed_two = middle * inv_two
-    second_own = (normed_two * ffn_gain).astype(jnp.bfloat16)
-    second_in = jnp.concatenate(
-        [gather_slots(second_own), gather_slots(flip(second_own, "ctx", 2))]
-    )
-
-    gate = plain_dot(second_in, gate_half)
-    upward = plain_dot(second_in, up_half)
-    sigma = jax.nn.sigmoid(gate)
-    swish = gate * sigma
-    hidden = (swish * upward).astype(jnp.bfloat16)
-    grad_gate = (grad_hidden * upward * sigma * (1.0 + gate * (1.0 - sigma))).astype(jnp.bfloat16)
-    grad_upward = (grad_hidden * swish).astype(jnp.bfloat16)
-
-    sum_down = reduce_ffn(left_dot(cot_rows, hidden), ctx, ctx_count).T
-    local = layer_input.shape[0]
-
-    def pair_sum(partial):
-        mine, got = scatter_slots(partial[local:])
-        away = flip(add(mine, got), "ctx", 2)
-        mine, got = scatter_slots(partial[:local])
-        return (mine.astype(jnp.float32) + got.astype(jnp.float32)) + away.astype(jnp.float32)
-
-    grad_second = pair_sum(
-        (right_dot(grad_gate, gate_half) + right_dot(grad_upward, up_half)).astype(jnp.bfloat16)
-    )
-    sum_gate = reduce_ffn(left_dot(second_in, grad_gate), ctx, ctx_count)
-    sum_up = reduce_ffn(left_dot(second_in, grad_upward), ctx, ctx_count)
-
-    grad_norm_two, ffn_gain_part = norm_back(grad_second, normed_two, inv_two, ffn_gain)
-    own_cot = cot_own.astype(jnp.float32)
-    grad_middle = own_cot + grad_norm_two
+    second = gather_pair((normed_two * ffn_gain).astype(jnp.bfloat16))
+    hidden, grad_gate, grad_up, keep, send = ffn_stage(
+        second, cot, w_gate, w_up, w_down, ctx_count, where
+    )
+
+    down = Reduce(keep, send)
+    second_terms = pair_scatter(
+        *unit_sum(
+            grad_second_kernel, "grad_second", (grad_gate, grad_up), (w_gate, w_up), True, where
+        )
+    )
+    rows = second[0].shape[0]
+    halves = (slice(0, rows), slice(rows, 2 * rows))
+
+    def unit_shares(name, grad, dep):
+        return weight_shares(
+            name, second, (after(dep, grad),), (tuple((k, 0, halves[k]) for k in range(2)),),
+            grad.shape[1], ctx_count, False, where,
+        )
+
+    gate_shares = unit_shares("gate_shares", grad_gate, second_terms[0])
+    up_shares = unit_shares("up_shares", grad_up, gate_shares[0])
+    ffn_halves = unit_sum(
+        ffn_out_kernel, "ffn_out", (after(up_shares[0], hidden),), (w_down,), False, where
+    )
+
+    grad_norm_two, ffn_gain_part = norm_back(
+        total(after(ffn_halves[0], *second_terms)), normed_two, inv_two, ffn_gain
+    )
+    grad_middle = cot_own.astype(jnp.float32) + grad_norm_two
     grad_branch = gather_slots(grad_middle.astype(jnp.bfloat16))
-    grad_mixed = right_dot(grad_branch, w_out).astype(jnp.bfloat16)
-    sum_out = reduce_attention(left_dot(grad_branch, mixed), ctx, ctx_count).T
-
-    ffn_out = pair_sum(plain_dot(hidden, down_half).astype(jnp.bfloat16))
-    output = gather_rows((middle + ffn_out).astype(jnp.bfloat16), tensor)
-
-    grad_queries, grad_keys, grad_values = [], [], []
+    for mask in highs:
+        down.halve(mask, ctx, grad_middle)
+    gate = Reduce(*after(down.keep, *gate_shares))
+    backward = []
+    held = grad_branch
     for head in range(kv_heads):
-        grad_q, keep, send = attention_backward(
-            head, queries, kv_all, grad_mixed, mixed, log_total, cosine, sine,
-            block_order, cont_prompt, where,
+        backward.append(
+            attention_backward(
+                head, queries, held, w_out, mixed, log_total, parts, cosine, sine,
+                block_order, cont_prompt, where,
+            )
         )
-        grad_queries.append(grad_q)
-        grad_k, grad_v = kv_finish(*reduce_kv(keep, send, ctx_count), cosine, sine)
-        grad_keys.append(grad_k)
-        grad_values.append(grad_v)
-    grad_query = jnp.concatenate(grad_queries, axis=1)
-    grad_key = jnp.concatenate(grad_keys, axis=1)
-    grad_value = jnp.concatenate(grad_values, axis=1)
-    sum_query = reduce_attention(left_dot(first_input, grad_query), ctx, ctx_count)
-    sum_kv = reduce_attention(
-        jnp.concatenate(
-            [left_dot(first_input, grad_key), left_dot(first_input, grad_value)], axis=1
-        ),
-        ctx,
+        held = after(backward[-1][0], grad_branch)
+    grad_queries = [item[0] for item in backward]
+    spans = slice(0, first_input.shape[0])
+    wide = grad_queries[0].shape[1]
+    last_query = grad_queries[-1]
+    branch_shares = weight_shares(
+        "branch_shares",
+        (first_input, grad_branch),
+        grad_queries + [after(last_query, mixed)],
+        tuple(((0, h, spans),) for h in range(kv_heads)) + (((1, kv_heads, spans),),),
+        2 * w_query.shape[1],
         ctx_count,
-    )
-    sum_key, sum_value = jnp.split(sum_kv, 2, axis=1)
-    grad_first_partial = (
-        right_dot(grad_query, w_query)
-        + right_dot(grad_key, key_matrix)
-        + right_dot(grad_value, value_matrix)
-    )
-    mine, got = scatter_slots(grad_first_partial.astype(jnp.bfloat16))
-    grad_first = mine.astype(jnp.float32) + got.astype(jnp.float32)
+        True,
+        where,
+    )
+    for mask in highs:
+        gate.halve(mask, ctx, branch_shares[0])
+    kv = [KvReduce(*after(gate.keep, item[1], item[2]), ctx_count) for item in backward]
+    ffn_terms = pair_scatter(*after(gate.keep, *ffn_halves))
+    sum_down = both_halves(down, ctx, 0, gate.keep)
+    for item in kv:
+        item.high(sum_down)
+    up = Reduce(*after(kv[-1].keep, *up_shares))
+    keep, send, grad_kv = tail_stage(
+        [(item.keep, item.got) for item in kv], cosine, sine, grad_queries,
+        w_query, key_matrix, value_matrix, where,
+    )
+    first_terms = scatter_slots(keep, send)
+    kv_shares = weight_shares(
+        "kv_shares", (first_input,), (grad_kv,), (((0, 0, spans),),), grad_kv.shape[1],
+        ctx_count, True, where,
+    )
+    output = gather_rows((middle + total(ffn_terms)).astype(jnp.bfloat16), tensor)
+    for mask in highs:
+        up.halve(mask, ctx, kv_shares[0])
+    branch = Reduce(*after(up.keep, *branch_shares))
+    last = Reduce(*after(up.keep, *kv_shares))
+    sum_gate = both_halves(gate, ctx, 1, up.keep)
     inv_one = lax.rsqrt(jnp.mean(own_input * own_input, axis=-1, keepdims=True) + eps_norm)
-    grad_norm_one, attn_gain_part = norm_back(grad_first, own_input * inv_one, inv_one, attn_gain)
+    grad_norm_one, attn_gain_part = norm_back(
+        total(first_terms), own_input * inv_one, inv_one, attn_gain
+    )
     grad_input = gather_rows((grad_middle + grad_norm_one).astype(jnp.bfloat16), tensor)
+    sum_up = both_halves(up, ctx, 1, grad_input)
+    for item in (branch, last):
+        for mask in [2] + highs:
+            item.halve(mask, ctx, sum_up if mask == 2 else None)
+    width_q, width_k = w_query.shape[1], key_matrix.shape[1]
+    branch_sum, last_sum = branch.sum(), last.sum()
+    sum_query, sum_out = branch_sum[:, :width_q], branch_sum[:, width_q:].T
+    sum_key, sum_value = last_sum[:, :width_k], last_sum[:, width_k:]
 
     devices = ctx_count * tp_count
     gains = jnp.stack([attn_gain_part, ffn_gain_part]).reshape(2, devices, -1)

time: 804 us -> 681 us (0.85)
  matrix products: 94.9 us -> 0 us
  Pallas kernels: 69.8 us -> 155 us
  waiting for transfers between devices: 422 us -> 359 us
  local copies, waits for them, and re-layouts: 87.8 us -> 38.2 us
  between operations: 15.6 us -> 1.98 us
  other arithmetic: 43.2 us -> 54.7 us
    dot_general x18 -> x0, matrix products: 94.9 us -> none  [the longest x7 37 us: right_dot(): lax.dot_general(left, right, (((1,), (1,)), ((), ())), preferred_element_...]
    pallas_call x5 -> x11, Pallas kernels: 63.6 us -> 149 us  [the longest x2 38.5 us: attention_backward(): pl.pallas_call(functools.partial(backward_kernel, rep, 1, ctx_count, head...]
    all_gather x1 -> x0, waiting for transfers between devices: 76.2 us -> none  [body(): kv_all = lax.all_gather(kv_local, 'ctx', axis=0, tiled=True)]
    unnamed x153 -> x169, local copies, waits for them, and re-layouts: 48 us -> 28.4 us
    all_to_all x1, waiting for transfers between devices: 2.03 us -> 20.1 us  [body(): gains = lax.all_to_all(gains, ('ctx', 'tp'), 1, 1, tiled=True)]
    dynamic_slice x11 -> x1, local copies, waits for them, and re-layouts: 15.8 us -> 1.69 us  [slots_of(): lax.dynamic_slice_in_dim(value, (tensor ^ SLOT_XOR[u]) * rows, rows)]
    concatenate x1 -> x8, other arithmetic: 0.18 us -> 12.9 us  [the longest x2 3.58 us: gather_rows(): near = jnp.concatenate([own, flip(own, 'tp', 2)])]
    ppermute x58 -> x53, waiting for transfers between devices: 343 us -> 339 us  [flip(): lax.ppermute(value, axis, [(i, i ^ mask) for i in range(lax.axis_size(axi...]
  transfers between devices with their start and end apart: 60 -> 54, of which waited for: 28 -> 32; matrix products, arithmetic and copies ran while one was open for 17% -> 9% of each run, Pallas kernels for 5% -> 12%
where the time goes in v4:
time: 681 us; the launch traced here: 672 us
  waiting for transfers between devices  359 us (53%)
  Pallas kernels  155 us (23%)
  starting transfers between devices  63.5 us (9%)
  other arithmetic  54.7 us (8%)
  local copies, waits for them, and re-layouts  38.2 us (6%)
    ppermute x53, waiting for transfers between devices, flip(): lax.ppermute(value, axis, [(i, i ^ mask) for i in range(lax.axis_size(axi...  339 us
    ppermute x53, starting transfers between devices, flip(): lax.ppermute(value, axis, [(i, i ^ mask) for i in range(lax.axis_size(axi...  60.7 us
    pallas_call x2, Pallas kernels, attention_backward(): pl.pallas_call(functools.partial(backward_kernel, rep, 1, ctx_count, head...  38.5 us
    pallas_call x1, Pallas kernels, ffn_stage(): pl.pallas_call(ffn_kernel, out_shape=(unit, unit, unit, shares, shares),...  35.8 us
    pallas_call x4, Pallas kernels, weight_shares(): pl.pallas_call(functools.partial(shares_kernel, len(lefts), swap_bits, pa...  29.8 us
    unnamed x169, local copies, waits for them, and re-layouts  28.4 us
    convert_element_type x20, other arithmetic, add(): (left.astype(jnp.float32) + right.astype(jnp.float32)).astype(jnp.bfloat16)  24.4 us
    pallas_call x1, Pallas kernels, attention_forward(): pl.pallas_call(functools.partial(forward_kernel, rep, kv_heads, ctx_count...  22.5 us
  transfers between devices with their start and end apart: 54, of which 32 were waited for; matrix products, arithmetic and copies ran while one was open for 9% of the time, Pallas kernels for 12%

profile of v4, /device:TPU:0, one launch (start us, length us, event | category | flops | bytes accessed | tf_op | source)
XLA Modules:
  0.0 671.7 jit_solution(12771095886971963357)
XLA Ops:
  11.5 6.1 input_stage.1
  20.3 3.0 collective-permute-start.1
  27.7 18.1 %collective-permute-done.1.refs_2_ = bf16[512,512]{1,0:T(8,128)(2,1)S(1)} collective-permute-done((bf16[512,512]{1,0:T(8,128)(2,1)S(1)}, bf16[512,512]{1,0:T(8,128)(2,1)S(1)}, u32[]{:S(2)}, u32[]{:S(2)}) %collective-permute-start.1) | collective-permute-done | bytes 524320 | tf_op jit(solution)/shard_map/ppermute | solution.py:712
  47.4 14.2 %collective-permute-done.3.refs_4_ = bf16[512,512]{1,0:T(8,128)(2,1)S(1)} collective-permute-done((bf16[512,512]{1,0:T(8,128)(2,1)S(1)}, bf16[512,512]{1,0:T(8,128)(2,1)S(1)}, u32[]{:S(2)}, u32[]{:S(2)}) %collective-permute-start.3) | collective-permute-done | bytes 524320 | tf_op jit(solution)/shard_map/ppermute | solution.py:712
  63.6 12.1 %collective-permute-done.4.refs_5_ = bf16[512,512]{1,0:T(8,128)(2,1)S(1)} collective-permute-done((bf16[512,512]{1,0:T(8,128)(2,1)S(1)}, bf16[512,512]{1,0:T(8,128)(2,1)S(1)}, u32[]{:S(2)}, u32[]{:S(2)}) %collective-permute-start.4) | collective-permute-done | bytes 524320 | tf_op jit(solution)/shard_map/ppermute | solution.py:712
  75.7 5.6 collective-permute-done.6.refs_7_
  81.3 22.5 %attention_forward.1 = (bf16[512,512]{1,0:T(8,128)(2,1)S(1)}, f32[2,4,256]{2,1,0:T(4,128)S(1)}, bf16[256,2048]{1,0:T(8,128)(2,1)S(1)}, bf16[256,2048]{1,0:T(8,128)(2,1)S(1)}) custom-call(s32[32]{0:T(128)S(1)} %copy-done.35, s32[8]{0:T(128)S(1)} %copy-done.36, s32[2]{0:T(128)S(1)} %pad_add_fusion.where_ref, bf16[512,512]{1,0:T(8,128)(2,1)S(1)} %get-tuple-element.89.q_ref, ...), custom_call_target="tpu_custom_call" | custom-call | flops 3221225472 | bytes 8388608 | tf_op jit(solution)/shard_map/attention_forward/pallas_call | solution.py:342
  109.6 12.7 %collective-permute-done.8 = bf16[128,2048]{1,0:T(8,128)(2,1)} collective-permute-done((bf16[128,2048]{1,0:T(8,128)(2,1)S(1)}, bf16[128,2048]{1,0:T(8,128)(2,1)}, u32[]{:S(2)}, u32[]{:S(2)}) %collective-permute-start.8) | collective-permute-done | bytes 524320 | tf_op jit(solution)/shard_map/ppermute | solution.py:712
  124.2 6.8 %collective-permute-start.9 = (bf16[128,2048]{1,0:T(8,128)(2,1)S(1)}, bf16[128,2048]{1,0:T(8,128)(2,1)}, u32[]{:S(2)}, u32[]{:S(2)}) collective-permute-start(bf16[128,2048]{1,0:T(8,128)(2,1)S(1)} %multiply_convert_fusion), channel_id=1, source_target_pairs={{0,8},{4,12},{8,0},{12,4},{16,24},{20,28},{24,16},{28,20},{1,9},{5... | collective-permute-start | bytes 1572872 | tf_op jit(solution)/shard_map/ppermute | solution.py:712
  134.3 9.5 %collective-permute-done.9 = bf16[128,2048]{1,0:T(8,128)(2,1)} collective-permute-done((bf16[128,2048]{1,0:T(8,128)(2,1)S(1)}, bf16[128,2048]{1,0:T(8,128)(2,1)}, u32[]{:S(2)}, u32[]{:S(2)}) %collective-permute-start.9) | collective-permute-done | bytes 524320 | tf_op jit(solution)/shard_map/ppermute | solution.py:712
  145.4 8.2 %collective-permute-done.13 = bf16[128,2048]{1,0:T(8,128)(2,1)S(1)} collective-permute-done((bf16[128,2048]{1,0:T(8,128)(2,1)S(1)}, bf16[128,2048]{1,0:T(8,128)(2,1)S(1)}, u32[]{:S(2)}, u32[]{:S(2)}) %collective-permute-start.13) | collective-permute-done | bytes 524320 | tf_op jit(solution)/shard_map/ppermute | solution.py:712
  155.1 3.8 collective-permute-done.11
  160.3 7.9 %collective-permute-done.14 = bf16[128,2048]{1,0:T(8,128)(2,1)S(1)} collective-permute-done((bf16[128,2048]{1,0:T(8,128)(2,1)S(1)}, bf16[128,2048]{1,0:T(8,128)(2,1)S(1)}, u32[]{:S(2)}, u32[]{:S(2)}) %collective-permute-start.14) | collective-permute-done | bytes 524320 | tf_op jit(solution)/shard_map/ppermute | solution.py:712
  172.6 35.8 %ffn_stage.1 = (bf16[1024,1024]{1,0:T(8,128)(2,1)S(1)}, bf16[1024,1024]{1,0:T(8,128)(2,1)S(1)}, bf16[1024,1024]{1,0:T(8,128)(2,1)S(1)}, bf16[4,1024,256]{2,1,0:T(8,128)(2,1)S(1)}, bf16[4,1024,256]{2,1,0:T(8,128)(2,1)}) custom-call(s32[2]{0:T(128)S(1)} %pad_add_fusion.where_ref, bf16[512,2048]{1,0:T(8,128)(2,1)} %copy-done.7, ...), custom_call_target="tpu_custom_call" | custom-call | flops 17179869184 | bytes 16777216 | tf_op jit(solution)/shard_map/ffn_stage/pallas_call | solution.py:545
  209.8 12.6 %grad_second.1 = (bf16[512,2048]{1,0:T(8,128)(2,1)S(1)}, bf16[512,2048]{1,0:T(8,128)(2,1)S(1)}) custom-call(s32[2]{0:T(128)S(1)} %pad_add_fusion.where_ref, bf16[1024,1024]{1,0:T(8,128)(2,1)S(1)} %get-tuple-element.99.gg_ref.refs_2_, bf16[1024,1024]{1,0:T(8,128)(2,1)S(1)} %get-tuple-element.101.gu_ref.refs_2_, bf16[2048,2048]{1,0:T(8,128)(2,1)S(1)} %bitcast.43, ...), custom_call_target="tpu_custom_call" | custom-call | flops 8589934592 | bytes 8388608 | tf_op jit(solution)/shard_map/grad_second/pallas_call | solution.py:591
  222.6 4.0 collective-permute-done.16
  229.6 11.2 %collective-permute-done.18 = bf16[128,2048]{1,0:T(8,128)(2,1)S(1)} collective-permute-done((bf16[128,2048]{1,0:T(8,128)(2,1)S(1)}, bf16[128,2048]{1,0:T(8,128)(2,1)S(1)}, u32[]{:S(2)}, u32[]{:S(2)}) %collective-permute-start.18) | collective-permute-done | bytes 524320 | tf_op jit(solution)/shard_map/ppermute | solution.py:712
  241.5 9.9 %gate_shares.1 = (bf16[4,256,1024]{2,1,0:T(8,128)(2,1)S(1)}, bf16[4,256,1024]{2,1,0:T(8,128)(2,1)}) custom-call(s32[2]{0:T(128)S(1)} %pad_add_fusion.where_ref, bf16[512,2048]{1,0:T(8,128)(2,1)S(1)} %copy-done.8, bf16[512,2048]{1,0:T(8,128)(2,1)} %collective-permute-done.12.far_ref.refs_1_, bf16[1024,1024]{1,0:T(8,128)(2,1)S(1)} %get-tuple-element.99.gg_ref.refs_2_), custom_call_target="tpu_custom_call" | custom-call | flops 4294967296 | bytes 4194304 | tf_op jit(solution)/shard_map/gate_shares/pallas_call | solution.py:640
  255.8 10.7 %up_shares.1 = (bf16[4,256,1024]{2,1,0:T(8,128)(2,1)S(1)}, bf16[4,256,1024]{2,1,0:T(8,128)(2,1)}) custom-call(s32[2]{0:T(128)S(1)} %pad_add_fusion.where_ref, bf16[512,2048]{1,0:T(8,128)(2,1)S(1)} %copy-done.8, bf16[512,2048]{1,0:T(8,128)(2,1)} %collective-permute-done.12.far_ref.refs_1_, bf16[1024,1024]{1,0:T(8,128)(2,1)S(1)} %copy-done.60), custom_call_target="tpu_custom_call" | custom-call | flops 4294967296 | bytes 4194304 | tf_op jit(solution)/shard_map/up_shares/pallas_call | solution.py:640
  267.8 6.4 ffn_out.1
  277.8 12.4 %collective-permute-done.20 = bf16[128,2048]{1,0:T(8,128)(2,1)S(1)} collective-permute-done((bf16[128,2048]{1,0:T(8,128)(2,1)}, bf16[128,2048]{1,0:T(8,128)(2,1)S(1)}, u32[]{:S(2)}, u32[]{:S(2)}) %collective-permute-start.20) | collective-permute-done | bytes 524320 | tf_op jit(solution)/shard_map/ppermute | solution.py:712
  292.3 3.5 add_convert_fusion.5
  296.8 2.9 pad_maximum_fusion.3.gb_ref.refs_1_
  299.7 19.0 %attention_backward_0.1 = (bf16[512,256]{1,0:T(8,128)(2,1)}, bf16[2048,256]{1,0:T(8,128)(2,1)}, bf16[2048,256]{1,0:T(8,128)(2,1)}) custom-call(s32[32]{0:T(128)} %order_ref.7, s32[8]{0:T(128)} %cont_ref.7, s32[2]{0:T(128)} %copy-done.41, bf16[512,512]{1,0:T(8,128)(2,1)} %copy-done.48, bf16[512,2048]{1,0:T(8,128)(2,1)} %pad_maximum_fusion.3.gb_ref.refs_1_, ...), custom_call_target="tpu_custom_call" | custom-call | flops 3221225472 | bytes 6291456 | tf_op jit(solution)/shard_map/attention_backward_0/pallas_call | solution.py:378
  318.7 19.5 %attention_backward_1.1 = (bf16[512,256]{1,0:T(8,128)(2,1)}, bf16[2048,256]{1,0:T(8,128)(2,1)}, bf16[2048,256]{1,0:T(8,128)(2,1)}) custom-call(s32[32]{0:T(128)} %order_ref.7, s32[8]{0:T(128)} %cont_ref.7, s32[2]{0:T(128)} %copy-done.41, bf16[512,512]{1,0:T(8,128)(2,1)} %copy-done.48, bf16[512,2048]{1,0:T(8,128)(2,1)} %pad_maximum_fusion.3.gb_ref.refs_1_, ...), custom_call_target="tpu_custom_call" | custom-call | flops 3221225472 | bytes 6291456 | tf_op jit(solution)/shard_map/attention_backward_1/pallas_call | solution.py:378
  339.2 5.6 branch_shares.1
  344.9 5.4 add_convert_fusion
  352.3 4.6 collective-permute-start.31
  357.0 3.0 collective-permute-start.35
  360.0 9.5 %collective-permute-done.31 = bf16[1024,256]{1,0:T(8,128)(2,1)S(1)} collective-permute-done((bf16[1024,256]{1,0:T(8,128)(2,1)}, bf16[1024,256]{1,0:T(8,128)(2,1)S(1)}, u32[]{:S(2)}, u32[]{:S(2)}) %collective-permute-start.31) | collective-permute-done | bytes 524320 | tf_op jit(solution)/shard_map/ppermute | solution.py:712
  372.5 11.8 %collective-permute-done.35 = bf16[2048,256]{1,0:T(8,128)(2,1)} collective-permute-done((bf16[2048,256]{1,0:T(8,128)(2,1)}, bf16[2048,256]{1,0:T(8,128)(2,1)}, u32[]{:S(2)}, u32[]{:S(2)}) %collective-permute-start.35) | collective-permute-done | bytes 1048608 | tf_op jit(solution)/shard_map/ppermute | solution.py:712
  387.9 18.1 %collective-permute-done.32 = bf16[2048,256]{1,0:T(8,128)(2,1)} collective-permute-done((bf16[2048,256]{1,0:T(8,128)(2,1)}, bf16[2048,256]{1,0:T(8,128)(2,1)}, u32[]{:S(2)}, u32[]{:S(2)}) %collective-permute-start.32) | collective-permute-done | bytes 1048608 | tf_op jit(solution)/shard_map/ppermute | solution.py:712
  410.4 16.2 %collective-permute-done.33 = bf16[1024,256]{1,0:T(8,128)(2,1)S(1)} collective-permute-done((bf16[1024,256]{1,0:T(8,128)(2,1)S(1)}, bf16[1024,256]{1,0:T(8,128)(2,1)S(1)}, u32[]{:S(2)}, u32[]{:S(2)}) %collective-permute-start.33) | collective-permute-done | bytes 524320 | tf_op jit(solution)/shard_map/ppermute | solution.py:712
  426.9 12.1 %collective-permute-done.34.refs_1_ = bf16[512,256]{1,0:T(8,128)(2,1)S(1)} collective-permute-done((bf16[512,256]{1,0:T(8,128)(2,1)S(1)}, bf16[512,256]{1,0:T(8,128)(2,1)S(1)}, u32[]{:S(2)}, u32[]{:S(2)}) %collective-permute-start.34) | collective-permute-done | bytes 262176 | tf_op jit(solution)/shard_map/ppermute | solution.py:712
  439.0 3.0 tail_stage.1
  450.0 9.6 %collective-permute-done.39 = bf16[128,2048]{1,0:T(8,128)(2,1)S(1)} collective-permute-done((bf16[128,2048]{1,0:T(8,128)(2,1)S(1)}, bf16[128,2048]{1,0:T(8,128)(2,1)S(1)}, u32[]{:S(2)}, u32[]{:S(2)}) %collective-permute-start.39) | collective-permute-done | bytes 524320 | tf_op jit(solution)/shard_map/ppermute | solution.py:712
  462.3 8.6 %collective-permute-done.26 = bf16[128,2048]{1,0:T(8,128)(2,1)S(1)} collective-permute-done((bf16[128,2048]{1,0:T(8,128)(2,1)S(1)}, bf16[128,2048]{1,0:T(8,128)(2,1)S(1)}, u32[]{:S(2)}, u32[]{:S(2)}) %collective-permute-start.26) | collective-permute-done | bytes 524320 | tf_op jit(solution)/shard_map/ppermute | solution.py:712
  472.0 2.8 collective-permute-start.51
  477.5 3.7 kv_shares.1
  485.8 6.9 %collective-permute-done.40 = bf16[128,2048]{1,0:T(8,128)(2,1)} collective-permute-done((bf16[128,2048]{1,0:T(8,128)(2,1)}, bf16[128,2048]{1,0:T(8,128)(2,1)}, u32[]{:S(2)}, u32[]{:S(2)}) %collective-permute-start.40) | collective-permute-done | bytes 524320 | tf_op jit(solution)/shard_map/ppermute | solution.py:712
  500.1 20.1 %all-to-all-done = f32[32,1,128]{2,1,0:T(1,128)S(1)} async-done(((f32[32,1,128]{2,1,0:T(1,128)}), f32[32,1,128]{2,1,0:T(1,128)S(1)}, u32[]{:S(2)}, u32[]{:S(2)}) %all-to-all-start) | async-done | bytes 16416 | tf_op jit(solution)/shard_map/all_to_all | solution.py:985
  522.1 3.3 add_convert_fusion.3
  531.2 42.6 %collective-permute-done.43 = bf16[2,256,1024]{2,1,0:T(8,128)(2,1)S(1)} collective-permute-done((bf16[2,256,1024]{2,1,0:T(8,128)(2,1)S(1)}, bf16[2,256,1024]{2,1,0:T(8,128)(2,1)S(1)}, u32[]{:S(2)}, u32[]{:S(2)}) %collective-permute-start.43) | collective-permute-done | bytes 1048608 | tf_op jit(solution)/shard_map/ppermute | solution.py:712
  580.7 8.1 %collective-permute-done.44 = bf16[256,1024]{1,0:T(8,128)(2,1)S(1)} collective-permute-done((bf16[256,1024]{1,0:T(8,128)(2,1)S(1)}, bf16[256,1024]{1,0:T(8,128)(2,1)S(1)}, u32[]{:S(2)}, u32[]{:S(2)}) %collective-permute-start.44) | collective-permute-done | bytes 524320 | tf_op jit(solution)/shard_map/ppermute | solution.py:712
  592.6 7.4 %collective-permute-done.52 = bf16[256,1024]{1,0:T(8,128)(2,1)S(1)} collective-permute-done((bf16[256,1024]{1,0:T(8,128)(2,1)S(1)}, bf16[256,1024]{1,0:T(8,128)(2,1)S(1)}, u32[]{:S(2)}, u32[]{:S(2)}) %collective-permute-start.52) | collective-permute-done | bytes 524320 | tf_op jit(solution)/shard_map/ppermute | solution.py:712
  604.3 28.5 %collective-permute-done.49 = bf16[2,256,512]{2,1,0:T(8,128)(2,1)S(1)} collective-permute-done((bf16[2,256,512]{2,1,0:T(8,128)(2,1)S(1)}, bf16[2,256,512]{2,1,0:T(8,128)(2,1)S(1)}, u32[]{:S(2)}, u32[]{:S(2)}) %collective-permute-start.49) | collective-permute-done | bytes 524320 | tf_op jit(solution)/shard_map/ppermute | solution.py:712
  636.2 22.0 %collective-permute-done.50 = bf16[1,256,512]{2,1,0:T(8,128)(2,1)S(1)} collective-permute-done((bf16[1,256,512]{2,1,0:T(8,128)(2,1)S(1)}, bf16[1,256,512]{2,1,0:T(8,128)(2,1)S(1)}, u32[]{:S(2)}, u32[]{:S(2)}) %collective-permute-start.50) | collective-permute-done | bytes 262176 | tf_op jit(solution)/shard_map/ppermute | solution.py:712
  659.1 10.2 %collective-permute-done.47 = bf16[1,256,1024]{2,1,0:T(8,128)(2,1)S(1)} collective-permute-done((bf16[1,256,1024]{2,1,0:T(8,128)(2,1)S(1)}, bf16[1,256,1024]{2,1,0:T(8,128)(2,1)S(1)}, u32[]{:S(2)}, u32[]{:S(2)}) %collective-permute-start.47) | collective-permute-done | bytes 524320 | tf_op jit(solution)/shard_map/ppermute | solution.py:712
  (310 shorter events, 128.5 us)
Async XLA Ops:
  20.3 25.4 %collective-permute-start.1 = (bf16[512,512]{1,0:T(8,128)(2,1)S(1)}, bf16[512,512]{1,0:T(8,128)(2,1)S(1)}, u32[]{:S(2)}, u32[]{:S(2)}) collective-permute-start(bf16[512,512]{1,0:T(8,128)(2,1)S(1)} %get-tuple-element.90.refs_0_), channel_id=1, source_target_pairs={{0,8},{4,12},{8,0},{12,4},{16,24},{20,28},{24,16},{28,20},{1,9},{5... | collective-permute-start | bytes 1572872 | tf_op jit(solution)/shard_map/ppermute | solution.py:712
  23.4 38.2 %collective-permute-start.3 = (bf16[512,512]{1,0:T(8,128)(2,1)S(1)}, bf16[512,512]{1,0:T(8,128)(2,1)S(1)}, u32[]{:S(2)}, u32[]{:S(2)}) collective-permute-start(bf16[512,512]{1,0:T(8,128)(2,1)S(1)} %get-tuple-element.90.refs_0_), channel_id=1, source_target_pairs={{0,16},{4,20},{8,24},{12,28},{16,0},{20,4},{24,8},{28,12},{1,17},{... | collective-permute-start | bytes 1572872 | tf_op jit(solution)/shard_map/ppermute | solution.py:712
  26.0 37.1 %collective-permute-start.5 = (bf16[512,512]{1,0:T(8,128)(2,1)S(1)}, bf16[512,512]{1,0:T(8,128)(2,1)S(1)}, u32[]{:S(2)}, u32[]{:S(2)}) collective-permute-start(bf16[512,512]{1,0:T(8,128)(2,1)S(1)} %get-tuple-element.90.refs_0_), channel_id=1, source_target_pairs={{0,24},{4,28},{8,16},{12,20},{16,8},{20,12},{24,0},{28,4},{1,25},{... | collective-permute-start | bytes 1572872 | tf_op jit(solution)/shard_map/ppermute | solution.py:712
  26.0 37.7 %collective-permute-start = (bf16[512,512]{1,0:T(8,128)(2,1)S(1)}, bf16[512,512]{1,0:T(8,128)(2,1)S(1)}, u32[]{:S(2)}, u32[]{:S(2)}) collective-permute-start(bf16[512,512]{1,0:T(8,128)(2,1)S(1)} %get-tuple-element.90.refs_0_), channel_id=1, source_target_pairs={{0,4},{4,0},{8,12},{12,8},{16,20},{20,16},{24,28},{28,24},{1,5},{5... | collective-permute-start | bytes 1572872 | tf_op jit(solution)/shard_map/ppermute | solution.py:712
  45.8 17.9 %collective-permute-start.2 = (bf16[512,512]{1,0:T(8,128)(2,1)S(1)}, bf16[512,512]{1,0:T(8,128)(2,1)S(1)}, u32[]{:S(2)}, u32[]{:S(2)}) collective-permute-start(bf16[512,512]{1,0:T(8,128)(2,1)S(1)} %collective-permute-done.1.refs_2_), channel_id=1, source_target_pairs={{0,4},{4,0},{8,12},{12,8},{16,20},{20,16},{24,28},{28,24},{1,5},{5... | collective-permute-start | bytes 1572872 | tf_op jit(solution)/shard_map/ppermute | solution.py:712
  61.6 14.1 %collective-permute-start.4 = (bf16[512,512]{1,0:T(8,128)(2,1)S(1)}, bf16[512,512]{1,0:T(8,128)(2,1)S(1)}, u32[]{:S(2)}, u32[]{:S(2)}) collective-permute-start(bf16[512,512]{1,0:T(8,128)(2,1)S(1)} %collective-permute-done.3.refs_4_), channel_id=1, source_target_pairs={{0,4},{4,0},{8,12},{12,8},{16,20},{20,16},{24,28},{28,24},{1,5},{5... | collective-permute-start | bytes 1572872 | tf_op jit(solution)/shard_map/ppermute | solution.py:712
  63.1 18.2 %collective-permute-start.6 = (bf16[512,512]{1,0:T(8,128)(2,1)S(1)}, bf16[512,512]{1,0:T(8,128)(2,1)S(1)}, u32[]{:S(2)}, u32[]{:S(2)}) collective-permute-start(bf16[512,512]{1,0:T(8,128)(2,1)S(1)} %collective-permute-done.5.refs_6_), channel_id=1, source_target_pairs={{0,4},{4,0},{8,12},{12,8},{16,20},{20,16},{24,28},{28,24},{1,5},{5... | collective-permute-start | bytes 1572872 | tf_op jit(solution)/shard_map/ppermute | solution.py:712
  108.2 14.1 %collective-permute-start.8 = (bf16[128,2048]{1,0:T(8,128)(2,1)S(1)}, bf16[128,2048]{1,0:T(8,128)(2,1)}, u32[]{:S(2)}, u32[]{:S(2)}) collective-permute-start(bf16[128,2048]{1,0:T(8,128)(2,1)S(1)} %add_convert_fusion.35), channel_id=1, source_target_pairs={{0,2},{1,3},{2,0},{3,1},{4,6},{5,7},{6,4},{7,5},{8,10},{9,11},{10,... | collective-permute-start | bytes 1572872 | tf_op jit(solution)/shard_map/ppermute | solution.py:712
  124.2 19.7 %collective-permute-start.9 = (bf16[128,2048]{1,0:T(8,128)(2,1)S(1)}, bf16[128,2048]{1,0:T(8,128)(2,1)}, u32[]{:S(2)}, u32[]{:S(2)}) collective-permute-start(bf16[128,2048]{1,0:T(8,128)(2,1)S(1)} %multiply_convert_fusion), channel_id=1, source_target_pairs={{0,8},{4,12},{8,0},{12,4},{16,24},{20,28},{24,16},{28,20},{1,9},{5... | collective-permute-start | bytes 1572872 | tf_op jit(solution)/shard_map/ppermute | solution.py:712
  132.6 20.9 %collective-permute-start.13 = (bf16[128,2048]{1,0:T(8,128)(2,1)S(1)}, bf16[128,2048]{1,0:T(8,128)(2,1)S(1)}, u32[]{:S(2)}, u32[]{:S(2)}) collective-permute-start(bf16[128,2048]{1,0:T(8,128)(2,1)S(1)} %get-tuple-element.94), channel_id=1, source_target_pairs={{0,8},{4,12},{8,0},{12,4},{16,24},{20,28},{24,16},{28,20},{1,9},{5... | collective-permute-start | bytes 1572872 | tf_op jit(solution)/shard_map/ppermute | solution.py:712
  132.8 22.3 %collective-permute-start.10 = (bf16[128,2048]{1,0:T(8,128)(2,1)S(1)}, bf16[128,2048]{1,0:T(8,128)(2,1)S(1)}, u32[]{:S(2)}, u32[]{:S(2)}) collective-permute-start(bf16[128,2048]{1,0:T(8,128)(2,1)S(1)} %multiply_convert_fusion), channel_id=1, source_target_pairs={{0,2},{1,3},{2,0},{3,1},{4,6},{5,7},{6,4},{7,5},{8,10},{9,11},{10,... | collective-permute-start | bytes 1572872 | tf_op jit(solution)/shard_map/ppermute | solution.py:712
  143.9 15.1 %collective-permute-start.11 = (bf16[128,2048]{1,0:T(8,128)(2,1)}, bf16[128,2048]{1,0:T(8,128)(2,1)S(1)}, u32[]{:S(2)}, u32[]{:S(2)}) collective-permute-start(bf16[128,2048]{1,0:T(8,128)(2,1)} %collective-permute-done.9), channel_id=1, source_target_pairs={{0,2},{1,3},{2,0},{3,1},{4,6},{5,7},{6,4},{7,5},{8,10},{9,11},{10,... | collective-permute-start | bytes 1572872 | tf_op jit(solution)/shard_map/ppermute | solution.py:712
  153.6 14.6 %collective-permute-start.14 = (bf16[128,2048]{1,0:T(8,128)(2,1)S(1)}, bf16[128,2048]{1,0:T(8,128)(2,1)S(1)}, u32[]{:S(2)}, u32[]{:S(2)}) collective-permute-start(bf16[128,2048]{1,0:T(8,128)(2,1)S(1)} %collective-permute-done.13), channel_id=1, source_target_pairs={{0,2},{1,3},{2,0},{3,1},{4,6},{5,7},{6,4},{7,5},{8,10},{9,11},{10,... | collective-permute-start | bytes 1572872 | tf_op jit(solution)/shard_map/ppermute | solution.py:712
  160.2 12.4 %collective-permute-start.12 = (bf16[512,2048]{1,0:T(8,128)(2,1)S(1)}, bf16[512,2048]{1,0:T(8,128)(2,1)}, u32[]{:S(2)}, u32[]{:S(2)}) collective-permute-start(bf16[512,2048]{1,0:T(8,128)(2,1)S(1)} %pad_maximum_fusion.near_ref.refs_0_), channel_id=1, source_target_pairs={{0,1},{1,0},{2,3},{3,2},{4,5},{5,4},{6,7},{7,6},{8,9},{9,8},{10,11... | collective-permute-start | bytes 6291464 | tf_op jit(solution)/shard_map/ppermute | solution.py:712
  226.7 14.0 %collective-permute-start.18 = (bf16[128,2048]{1,0:T(8,128)(2,1)S(1)}, bf16[128,2048]{1,0:T(8,128)(2,1)S(1)}, u32[]{:S(2)}, u32[]{:S(2)}) collective-permute-start(bf16[128,2048]{1,0:T(8,128)(2,1)S(1)} %add_convert_fusion.31), channel_id=1, source_target_pairs={{0,2},{1,3},{2,0},{3,1},{4,6},{5,7},{6,4},{7,5},{8,10},{9,11},{10,... | collective-permute-start | bytes 1572872 | tf_op jit(solution)/shard_map/ppermute | solution.py:712
  228.3 49.5 %collective-permute-start.22 = (bf16[4,1024,256]{2,1,0:T(8,128)(2,1)}, bf16[4,1024,256]{2,1,0:T(8,128)(2,1)}, u32[]{:S(2)}, u32[]{:S(2)}) collective-permute-start(bf16[4,1024,256]{2,1,0:T(8,128)(2,1)} %get-tuple-element.119), channel_id=1, source_target_pairs={{0,4},{4,0},{8,12},{12,8},{16,20},{20,16},{24,28},{28,24},{1,5},{5... | collective-permute-start | bytes 6291464 | tf_op jit(solution)/shard_map/ppermute | solution.py:712
  252.7 21.6 %collective-permute-start.17 = (bf16[128,2048]{1,0:T(8,128)(2,1)S(1)}, bf16[128,2048]{1,0:T(8,128)(2,1)S(1)}, u32[]{:S(2)}, u32[]{:S(2)}) collective-permute-start(bf16[128,2048]{1,0:T(8,128)(2,1)S(1)} %get-tuple-element.212), channel_id=1, source_target_pairs={{0,2},{1,3},{2,0},{3,1},{4,6},{5,7},{6,4},{7,5},{8,10},{9,11},{10,... | collective-permute-start | bytes 1572872 | tf_op jit(solution)/shard_map/ppermute | solution.py:712
  254.2 20.0 %collective-permute-start.19 = (bf16[128,2048]{1,0:T(8,128)(2,1)S(1)}, bf16[128,2048]{1,0:T(8,128)(2,1)S(1)}, u32[]{:S(2)}, u32[]{:S(2)}) collective-permute-start(bf16[128,2048]{1,0:T(8,128)(2,1)S(1)} %get-tuple-element.211), channel_id=1, source_target_pairs={{0,8},{4,12},{8,0},{12,4},{16,24},{20,28},{24,16},{28,20},{1,9},{5... | collective-permute-start | bytes 1572872 | tf_op jit(solution)/shard_map/ppermute | solution.py:712
  277.3 12.9 %collective-permute-start.20 = (bf16[128,2048]{1,0:T(8,128)(2,1)}, bf16[128,2048]{1,0:T(8,128)(2,1)S(1)}, u32[]{:S(2)}, u32[]{:S(2)}) collective-permute-start(bf16[128,2048]{1,0:T(8,128)(2,1)} %get-tuple-element.197), channel_id=1, source_target_pairs={{0,2},{1,3},{2,0},{3,1},{4,6},{5,7},{6,4},{7,5},{8,10},{9,11},{10,... | collective-permute-start | bytes 1572872 | tf_op jit(solution)/shard_map/ppermute | solution.py:712
  295.8 49.1 %collective-permute-start.23 = (bf16[4,256,1024]{2,1,0:T(8,128)(2,1)}, bf16[4,256,1024]{2,1,0:T(8,128)(2,1)}, u32[]{:S(2)}, u32[]{:S(2)}) collective-permute-start(bf16[4,256,1024]{2,1,0:T(8,128)(2,1)} %get-tuple-element.124), channel_id=1, source_target_pairs={{0,4},{4,0},{8,12},{12,8},{16,20},{20,16},{24,28},{28,24},{1,5},{5... | collective-permute-start | bytes 6291464 | tf_op jit(solution)/shard_map/ppermute | solution.py:712
  295.8 54.5 %collective-permute-start.30 = (bf16[2,1024,256]{2,1,0:T(8,128)(2,1)}, bf16[2,1024,256]{2,1,0:T(8,128)(2,1)}, u32[]{:S(2)}, u32[]{:S(2)}) collective-permute-start(bf16[2,1024,256]{2,1,0:T(8,128)(2,1)} %get-tuple-element.207), channel_id=1, source_target_pairs={{0,16},{4,20},{8,24},{12,28},{16,0},{20,4},{24,8},{28,12},{1,17},{... | collective-permute-start | bytes 3145736 | tf_op jit(solution)/shard_map/ppermute | solution.py:712
  352.3 17.2 %collective-permute-start.31 = (bf16[1024,256]{1,0:T(8,128)(2,1)}, bf16[1024,256]{1,0:T(8,128)(2,1)S(1)}, u32[]{:S(2)}, u32[]{:S(2)}) collective-permute-start(bf16[1024,256]{1,0:T(8,128)(2,1)} %fusion.12), channel_id=1, source_target_pairs={{0,8},{4,12},{8,0},{12,4},{16,24},{20,28},{24,16},{28,20},{1,9},{5... | collective-permute-start | bytes 1572872 | tf_op jit(solution)/shard_map/ppermute | solution.py:712
  357.0 27.3 %collective-permute-start.35 = (bf16[2048,256]{1,0:T(8,128)(2,1)}, bf16[2048,256]{1,0:T(8,128)(2,1)}, u32[]{:S(2)}, u32[]{:S(2)}) collective-permute-start(bf16[2048,256]{1,0:T(8,128)(2,1)} %get-tuple-element.141), channel_id=1, source_target_pairs={{0,4},{4,0},{8,12},{12,8},{16,20},{20,16},{24,28},{28,24},{1,5},{5... | collective-permute-start | bytes 3145736 | tf_op jit(solution)/shard_map/ppermute | solution.py:712
  359.9 46.1 %collective-permute-start.32 = (bf16[2048,256]{1,0:T(8,128)(2,1)}, bf16[2048,256]{1,0:T(8,128)(2,1)}, u32[]{:S(2)}, u32[]{:S(2)}) collective-permute-start(bf16[2048,256]{1,0:T(8,128)(2,1)} %get-tuple-element.135), channel_id=1, source_target_pairs={{0,4},{4,0},{8,12},{12,8},{16,20},{20,16},{24,28},{28,24},{1,5},{5... | collective-permute-start | bytes 3145736 | tf_op jit(solution)/shard_map/ppermute | solution.py:712
  385.8 23.7 %collective-permute-start.36 = (bf16[1024,256]{1,0:T(8,128)(2,1)S(1)}, bf16[1024,256]{1,0:T(8,128)(2,1)S(1)}, u32[]{:S(2)}, u32[]{:S(2)}) collective-permute-start(bf16[1024,256]{1,0:T(8,128)(2,1)S(1)} %get-tuple-element.224), channel_id=1, source_target_pairs={{0,8},{4,12},{8,0},{12,4},{16,24},{20,28},{24,16},{28,20},{1,9},{5... | collective-permute-start | bytes 1572872 | tf_op jit(solution)/shard_map/ppermute | solution.py:712
  407.6 18.9 %collective-permute-start.33 = (bf16[1024,256]{1,0:T(8,128)(2,1)S(1)}, bf16[1024,256]{1,0:T(8,128)(2,1)S(1)}, u32[]{:S(2)}, u32[]{:S(2)}) collective-permute-start(bf16[1024,256]{1,0:T(8,128)(2,1)S(1)} %get-tuple-element.226), channel_id=1, source_target_pairs={{0,8},{4,12},{8,0},{12,4},{16,24},{20,28},{24,16},{28,20},{1,9},{5... | collective-permute-start | bytes 1572872 | tf_op jit(solution)/shard_map/ppermute | solution.py:712
  409.6 17.3 %collective-permute-start.37 = (bf16[512,256]{1,0:T(8,128)(2,1)S(1)}, bf16[512,256]{1,0:T(8,128)(2,1)S(1)}, u32[]{:S(2)}, u32[]{:S(2)}) collective-permute-start(bf16[512,256]{1,0:T(8,128)(2,1)S(1)} %get-tuple-element.233), channel_id=1, source_target_pairs={{0,16},{4,20},{8,24},{12,28},{16,0},{20,4},{24,8},{28,12},{1,17},{... | collective-permute-start | bytes 786440 | tf_op jit(solution)/shard_map/ppermute | solution.py:712
  426.8 19.7 %collective-permute-start.24 = (bf16[512,2048]{1,0:T(8,128)(2,1)S(1)}, bf16[512,2048]{1,0:T(8,128)(2,1)S(1)}, u32[]{:S(2)}, u32[]{:S(2)}) collective-permute-start(bf16[512,2048]{1,0:T(8,128)(2,1)S(1)} %copy-done.20), channel_id=1, source_target_pairs={{0,1},{1,0},{2,3},{3,2},{4,5},{5,4},{6,7},{7,6},{8,9},{9,8},{10,11... | collective-permute-start | bytes 6291464 | tf_op jit(solution)/shard_map/ppermute | solution.py:712
  444.8 14.8 %collective-permute-start.39 = (bf16[128,2048]{1,0:T(8,128)(2,1)S(1)}, bf16[128,2048]{1,0:T(8,128)(2,1)S(1)}, u32[]{:S(2)}, u32[]{:S(2)}) collective-permute-start(bf16[128,2048]{1,0:T(8,128)(2,1)S(1)} %add_convert_fusion.16), channel_id=1, source_target_pairs={{0,2},{1,3},{2,0},{3,1},{4,6},{5,7},{6,4},{7,5},{8,10},{9,11},{10,... | collective-permute-start | bytes 1572872 | tf_op jit(solution)/shard_map/ppermute | solution.py:712
  445.4 76.7 %collective-permute-start.42 = (bf16[4,256,1024]{2,1,0:T(8,128)(2,1)}, bf16[4,256,1024]{2,1,0:T(8,128)(2,1)}, u32[]{:S(2)}, u32[]{:S(2)}) collective-permute-start(bf16[4,256,1024]{2,1,0:T(8,128)(2,1)} %get-tuple-element.150), channel_id=1, source_target_pairs={{0,4},{4,0},{8,12},{12,8},{16,20},{20,16},{24,28},{28,24},{1,5},{5... | collective-permute-start | bytes 6291464 | tf_op jit(solution)/shard_map/ppermute | solution.py:712
  448.0 22.9 %collective-permute-start.26 = (bf16[128,2048]{1,0:T(8,128)(2,1)S(1)}, bf16[128,2048]{1,0:T(8,128)(2,1)S(1)}, u32[]{:S(2)}, u32[]{:S(2)}) collective-permute-start(bf16[128,2048]{1,0:T(8,128)(2,1)S(1)} %get-tuple-element.210), channel_id=1, source_target_pairs={{0,2},{1,3},{2,0},{3,1},{4,6},{5,7},{6,4},{7,5},{8,10},{9,11},{10,... | collective-permute-start | bytes 1572872 | tf_op jit(solution)/shard_map/ppermute | solution.py:712
  449.5 45.4 %collective-permute-start.25 = (bf16[128,2048]{1,0:T(8,128)(2,1)}, bf16[128,2048]{1,0:T(8,128)(2,1)}, u32[]{:S(2)}, u32[]{:S(2)}) collective-permute-start(bf16[128,2048]{1,0:T(8,128)(2,1)} %get-tuple-element.209), channel_id=1, source_target_pairs={{0,2},{1,3},{2,0},{3,1},{4,6},{5,7},{6,4},{7,5},{8,10},{9,11},{10,... | collective-permute-start | bytes 1572872 | tf_op jit(solution)/shard_map/ppermute | solution.py:712
  461.8 30.9 %collective-permute-start.40 = (bf16[128,2048]{1,0:T(8,128)(2,1)}, bf16[128,2048]{1,0:T(8,128)(2,1)}, u32[]{:S(2)}, u32[]{:S(2)}) collective-permute-start(bf16[128,2048]{1,0:T(8,128)(2,1)} %get-tuple-element.194), channel_id=1, source_target_pairs={{0,2},{1,3},{2,0},{3,1},{4,6},{5,7},{6,4},{7,5},{8,10},{9,11},{10,... | collective-permute-start | bytes 1572872 | tf_op jit(solution)/shard_map/ppermute | solution.py:712
  471.9 23.5 %collective-permute-start.27 = (bf16[128,2048]{1,0:T(8,128)(2,1)}, bf16[128,2048]{1,0:T(8,128)(2,1)}, u32[]{:S(2)}, u32[]{:S(2)}) collective-permute-start(bf16[128,2048]{1,0:T(8,128)(2,1)} %add_convert_fusion.25), channel_id=1, source_target_pairs={{0,8},{4,12},{8,0},{12,4},{16,24},{20,28},{24,16},{28,20},{1,9},{5... | collective-permute-start | bytes 1572872 | tf_op jit(solution)/shard_map/ppermute | solution.py:712
  472.0 53.4 %collective-permute-start.51 = (bf16[2,256,1024]{2,1,0:T(8,128)(2,1)}, bf16[2,256,1024]{2,1,0:T(8,128)(2,1)}, u32[]{:S(2)}, u32[]{:S(2)}) collective-permute-start(bf16[2,256,1024]{2,1,0:T(8,128)(2,1)} %get-tuple-element.201), channel_id=1, source_target_pairs={{0,16},{4,20},{8,24},{12,28},{16,0},{20,4},{24,8},{28,12},{1,17},{... | collective-permute-start | bytes 3145736 | tf_op jit(solution)/shard_map/ppermute | solution.py:712
  483.0 37.2 %all-to-all-start = ((f32[32,1,128]{2,1,0:T(1,128)}), f32[32,1,128]{2,1,0:T(1,128)S(1)}, u32[]{:S(2)}, u32[]{:S(2)}) async-start(f32[32,1,128]{2,1,0:T(1,128)} %reshape.81), calls=%async_computation | async-start | bytes 32768 | tf_op jit(solution)/shard_map/all_to_all | solution.py:985
  495.0 33.8 %collective-permute-start.41 = (bf16[256,2048]{1,0:T(8,128)(2,1)}, bf16[256,2048]{1,0:T(8,128)(2,1)}, u32[]{:S(2)}, u32[]{:S(2)}) collective-permute-start(bf16[256,2048]{1,0:T(8,128)(2,1)} %pad_maximum_fusion.7), channel_id=1, source_target_pairs={{0,1},{1,0},{2,3},{3,2},{4,5},{5,4},{6,7},{7,6},{8,9},{9,8},{10,11... | collective-permute-start | bytes 3145736 | tf_op jit(solution)/shard_map/ppermute | solution.py:712
  499.6 78.6 %collective-permute-start.28 = (bf16[128,2048]{1,0:T(8,128)(2,1)}, bf16[128,2048]{1,0:T(8,128)(2,1)}, u32[]{:S(2)}, u32[]{:S(2)}) collective-permute-start(bf16[128,2048]{1,0:T(8,128)(2,1)} %get-tuple-element.196), channel_id=1, source_target_pairs={{0,2},{1,3},{2,0},{3,1},{4,6},{5,7},{6,4},{7,5},{8,10},{9,11},{10,... | collective-permute-start | bytes 1572872 | tf_op jit(solution)/shard_map/ppermute | solution.py:712
  525.4 48.4 %collective-permute-start.43 = (bf16[2,256,1024]{2,1,0:T(8,128)(2,1)S(1)}, bf16[2,256,1024]{2,1,0:T(8,128)(2,1)S(1)}, u32[]{:S(2)}, u32[]{:S(2)}) collective-permute-start(bf16[2,256,1024]{2,1,0:T(8,128)(2,1)S(1)} %get-tuple-element.205), channel_id=1, source_target_pairs={{0,16},{4,20},{8,24},{12,28},{16,0},{20,4},{24,8},{28,12},{1,17},{... | collective-permute-start | bytes 3145736 | tf_op jit(solution)/shard_map/ppermute | solution.py:712
  526.9 63.8 %collective-permute-start.45 = (bf16[4,256,1024]{2,1,0:T(8,128)(2,1)S(1)}, bf16[4,256,1024]{2,1,0:T(8,128)(2,1)S(1)}, u32[]{:S(2)}, u32[]{:S(2)}) collective-permute-start(bf16[4,256,1024]{2,1,0:T(8,128)(2,1)S(1)} %copy-done.18), channel_id=1, source_target_pairs={{0,4},{4,0},{8,12},{12,8},{16,20},{20,16},{24,28},{28,24},{1,5},{5... | collective-permute-start | bytes 6291464 | tf_op jit(solution)/shard_map/ppermute | solution.py:712
  574.0 14.9 %collective-permute-start.44 = (bf16[256,1024]{1,0:T(8,128)(2,1)S(1)}, bf16[256,1024]{1,0:T(8,128)(2,1)S(1)}, u32[]{:S(2)}, u32[]{:S(2)}) collective-permute-start(bf16[256,1024]{1,0:T(8,128)(2,1)S(1)} %fusion.14), channel_id=1, source_target_pairs={{0,8},{4,12},{8,0},{12,4},{16,24},{20,28},{24,16},{28,20},{1,9},{5... | collective-permute-start | bytes 1572872 | tf_op jit(solution)/shard_map/ppermute | solution.py:712
  575.4 24.6 %collective-permute-start.52 = (bf16[256,1024]{1,0:T(8,128)(2,1)S(1)}, bf16[256,1024]{1,0:T(8,128)(2,1)S(1)}, u32[]{:S(2)}, u32[]{:S(2)}) collective-permute-start(bf16[256,1024]{1,0:T(8,128)(2,1)S(1)} %fusion.16), channel_id=1, source_target_pairs={{0,8},{4,12},{8,0},{12,4},{16,24},{20,28},{24,16},{28,20},{1,9},{5... | collective-permute-start | bytes 1572872 | tf_op jit(solution)/shard_map/ppermute | solution.py:712
  577.4 24.5 %collective-permute-start.48 = (bf16[4,256,512]{2,1,0:T(8,128)(2,1)S(1)}, bf16[4,256,512]{2,1,0:T(8,128)(2,1)S(1)}, u32[]{:S(2)}, u32[]{:S(2)}) collective-permute-start(bf16[4,256,512]{2,1,0:T(8,128)(2,1)S(1)} %copy-done.26), channel_id=1, source_target_pairs={{0,4},{4,0},{8,12},{12,8},{16,20},{20,16},{24,28},{28,24},{1,5},{5... | collective-permute-start | bytes 3145736 | tf_op jit(solution)/shard_map/ppermute | solution.py:712
  579.5 24.7 %collective-permute-start.29 = (bf16[256,2048]{1,0:T(8,128)(2,1)S(1)}, bf16[256,2048]{1,0:T(8,128)(2,1)S(1)}, u32[]{:S(2)}, u32[]{:S(2)}) collective-permute-start(bf16[256,2048]{1,0:T(8,128)(2,1)S(1)} %pad_maximum_fusion.6), channel_id=1, source_target_pairs={{0,1},{1,0},{2,3},{3,2},{4,5},{5,4},{6,7},{7,6},{8,9},{9,8},{10,11... | collective-permute-start | bytes 3145736 | tf_op jit(solution)/shard_map/ppermute | solution.py:712
  592.5 41.6 %collective-permute-start.46 = (bf16[2,256,1024]{2,1,0:T(8,128)(2,1)S(1)}, bf16[2,256,1024]{2,1,0:T(8,128)(2,1)S(1)}, u32[]{:S(2)}, u32[]{:S(2)}) collective-permute-start(bf16[2,256,1024]{2,1,0:T(8,128)(2,1)S(1)} %get-tuple-element.204), channel_id=1, source_target_pairs={{0,8},{4,12},{8,0},{12,4},{16,24},{20,28},{24,16},{28,20},{1,9},{5... | collective-permute-start | bytes 3145736 | tf_op jit(solution)/shard_map/ppermute | solution.py:712
  602.2 30.6 %collective-permute-start.49 = (bf16[2,256,512]{2,1,0:T(8,128)(2,1)S(1)}, bf16[2,256,512]{2,1,0:T(8,128)(2,1)S(1)}, u32[]{:S(2)}, u32[]{:S(2)}) collective-permute-start(bf16[2,256,512]{2,1,0:T(8,128)(2,1)S(1)} %get-tuple-element.221), channel_id=1, source_target_pairs={{0,8},{4,12},{8,0},{12,4},{16,24},{20,28},{24,16},{28,20},{1,9},{5... | collective-permute-start | bytes 1572872 | tf_op jit(solution)/shard_map/ppermute | solution.py:712
  632.9 25.3 %collective-permute-start.50 = (bf16[1,256,512]{2,1,0:T(8,128)(2,1)S(1)}, bf16[1,256,512]{2,1,0:T(8,128)(2,1)S(1)}, u32[]{:S(2)}, u32[]{:S(2)}) collective-permute-start(bf16[1,256,512]{2,1,0:T(8,128)(2,1)S(1)} %add_convert_fusion.37), channel_id=1, source_target_pairs={{0,16},{4,20},{8,24},{12,28},{16,0},{20,4},{24,8},{28,12},{1,17},{... | collective-permute-start | bytes 786440 | tf_op jit(solution)/shard_map/ppermute | solution.py:712
  634.3 35.0 %collective-permute-start.47 = (bf16[1,256,1024]{2,1,0:T(8,128)(2,1)S(1)}, bf16[1,256,1024]{2,1,0:T(8,128)(2,1)S(1)}, u32[]{:S(2)}, u32[]{:S(2)}) collective-permute-start(bf16[1,256,1024]{2,1,0:T(8,128)(2,1)S(1)} %add_convert_fusion.12), channel_id=1, source_target_pairs={{0,16},{4,20},{8,24},{12,28},{16,0},{20,4},{24,8},{28,12},{1,17},{... | collective-permute-start | bytes 1572872 | tf_op jit(solution)/shard_map/ppermute | solution.py:712
  (89 other events, 1909.2 us)

commit v5 on v4

--- a/solution.py
+++ b/solution.py
@@ -417,12 +417,23 @@
     )(order, cont, where, q, grad_branch, w_out, mixed, lse, cosine, sine, *parts)
 
 
-def input_kernel(order_ref, cont_ref, where_ref, x_ref, gain_ref, wq_ref, wk_ref, wv_ref,
-                 cos_start_ref, sin_start_ref, cos_in_ref, sin_in_ref,
-                 first_ref, q_ref, kv_ref, cos_ref, sin_ref):
+def input_kernel(order_ref, cont_ref, where_ref, gain_ref, x_hbm, wq_hbm, wk_hbm, wv_hbm, table_hbm,
+                 first_ref, q_ref, kv_ref, cos_ref, sin_ref,
+                 x_ref, wq_ref, wk_ref, wv_ref, table_ref, sem):
+    pairs = ((x_hbm, x_ref), (table_hbm, table_ref), (wk_hbm, wk_ref), (wv_hbm, wv_ref),
+             (wq_hbm, wq_ref))
+    copies = [
+        pltpu.make_async_copy(source, target, sem.at[n])
+        for n, (source, target) in enumerate(pairs)
+    ]
+    for copy in copies:
+        copy.start()
     count = cont_ref.shape[0]
     prompt_blocks = count // CONTS * PER_PROMPT
+    starts = (table_ref.shape[0] - 2 * BLOCK) // 2
     lane = lax.broadcasted_iota(jnp.int32, (BLOCK, HEAD_SIZE), 1)
+    copies[0].wait()
+    copies[1].wait()
 
     def one_slot(slot, carry):
         quarter = slot_quarter(slot, where_ref[1])
@@ -436,8 +447,9 @@
             lax.rem(own, PER_PROMPT),
             PER_PROMPT + lax.rem(own - prompt_blocks, PER_CONT),
         )
-        cos_start, sin_start = cos_start_ref[pl.ds(spot, 1), :], sin_start_ref[pl.ds(spot, 1), :]
-        cos_in, sin_in = cos_in_ref[...], sin_in_ref[...]
+        cos_start = table_ref[pl.ds(2 * BLOCK + spot, 1), :]
+        sin_start = table_ref[pl.ds(2 * BLOCK + starts + spot, 1), :]
+        cos_in, sin_in = table_ref[:BLOCK, :], table_ref[BLOCK : 2 * BLOCK, :]
         sine = sin_start * cos_in + cos_start * sin_in
         cos_ref[rows, :] = cos_start * cos_in - sin_start * sin_in
         sin_ref[rows, :] = jnp.where(lane < HEAD_SIZE // 2, -sine, sine)
@@ -446,24 +458,31 @@
     lax.fori_loop(0, SLOTS, one_slot, 0)
     first = first_ref[...]
     cosine, sine = cos_ref[...], sin_ref[...]
-    kv_heads = wk_ref.shape[1] // HEAD_SIZE
-    for h in range(kv_heads):
+    copies[2].wait()
+    copies[3].wait()
+    keys = dot(first, wk_ref[...])
+    values = dot(first, wv_ref[...])
+    for h in range(wk_ref.shape[1] // HEAD_SIZE):
         cols = slice(h * HEAD_SIZE, (h + 1) * HEAD_SIZE)
-        key = rotate(plain_dot(first, wk_ref[:, cols]), cosine, sine)
-        value = plain_dot(first, wv_ref[:, cols])
-        kv_ref[:, 2 * h * HEAD_SIZE : (2 * h + 1) * HEAD_SIZE] = key.astype(jnp.bfloat16)
-        kv_ref[:, (2 * h + 1) * HEAD_SIZE : (2 * h + 2) * HEAD_SIZE] = value.astype(jnp.bfloat16)
-    for h in range(wq_ref.shape[1] // HEAD_SIZE):
-        cols = slice(h * HEAD_SIZE, (h + 1) * HEAD_SIZE)
-        query = rotate(plain_dot(first, wq_ref[:, cols]), cosine, sine)
-        q_ref[:, cols] = query.astype(jnp.bfloat16)
+        low, high = 2 * h * HEAD_SIZE, (2 * h + 1) * HEAD_SIZE
+        key = rotate(keys[:, cols], cosine, sine)
+        kv_ref[:, low:high] = key.astype(jnp.bfloat16)
+        kv_ref[:, high : high + HEAD_SIZE] = values[:, cols].astype(jnp.bfloat16)
+    copies[4].wait()
+    for n in range(0, wq_ref.shape[1], 256):
+        queries = dot(first, wq_ref[:, n : n + 256])
+        for m in range(0, 256, HEAD_SIZE):
+            query = rotate(queries[:, m : m + HEAD_SIZE], cosine, sine)
+            q_ref[:, n + m : n + m + HEAD_SIZE] = query.astype(jnp.bfloat16)
 
 
 def input_stage(x, gain, wq, wk, wv, order, cont, where):
     rows, model = x.shape
-    tables = angle_tables()
-    smem = pl.BlockSpec(memory_space=pltpu.SMEM)
-    vmem = pl.BlockSpec(memory_space=pltpu.VMEM)
+    cos_start, sin_start, cos_in, sin_in = angle_tables()
+    table = np.concatenate([cos_in, sin_in, cos_start, sin_start])
+    vmem, smem, any_ = (
+        pl.BlockSpec(memory_space=space) for space in (pltpu.VMEM, pltpu.SMEM, pl.ANY)
+    )
     flops = 2 * rows * model * (wq.shape[1] + 2 * wk.shape[1])
     return pl.pallas_call(
         input_kernel,
@@ -474,12 +493,16 @@
             jax.ShapeDtypeStruct((rows, HEAD_SIZE), jnp.float32),
             jax.ShapeDtypeStruct((rows, HEAD_SIZE), jnp.float32),
         ),
-        in_specs=[smem] * 3 + [vmem] * 9,
+        in_specs=[smem] * 3 + [vmem] + [any_] * 5,
         out_specs=[vmem] * 5,
+        scratch_shapes=[
+            pltpu.VMEM(a.shape, a.dtype) for a in (x, wq, wk, wv)
+        ]
+        + [pltpu.VMEM(table.shape, jnp.float32), pltpu.SemaphoreType.DMA((5,))],
         compiler_params=pltpu.CompilerParams(vmem_limit_bytes=40 << 20),
         cost_estimate=cost(flops, 4 * x.size + 2 * wq.size + 4 * wk.size),
         name="input_stage",
-    )(order, cont, where, x, gain.reshape(1, -1), wq, wk, wv, *tables)
+    )(order, cont, where, gain.reshape(1, -1), x, wq, wk, wv, table)
 
 
 def cost(flops, bytes_accessed):
@@ -504,62 +527,76 @@
         send_ref[pl.ds(spot, 1)] = value[None]
 
 
-def ffn_kernel(where_ref, near_ref, far_ref, cot_near_ref, cot_far_ref, wg_ref, wu_ref, wd_ref,
-               hid_ref, gg_ref, gu_ref, keep_ref, send_ref):
-    rows = near_ref.shape[0]
-    for k, (in_ref, cot_ref) in enumerate(((near_ref, cot_near_ref), (far_ref, cot_far_ref))):
-        span = slice(k * rows, (k + 1) * rows)
-        gate = dot(in_ref[...], wg_ref[...])
-        upward = dot(in_ref[...], wu_ref[...])
-        grad_hidden = right_dot(cot_ref[...], wd_ref[...])
-        sigma = jax.nn.sigmoid(gate)
-        swish = gate * sigma
-        hid_ref[span, :] = (swish * upward).astype(jnp.bfloat16)
-        gg_ref[span, :] = (
-            grad_hidden * upward * sigma * (1.0 + gate * (1.0 - sigma))
-        ).astype(jnp.bfloat16)
-        gu_ref[span, :] = (grad_hidden * swish).astype(jnp.bfloat16)
-    turned_near, turned_far = hid_ref[:rows, :].T, hid_ref[rows:, :].T
-    share = keep_ref.shape[2]
-    for f in range(cot_near_ref.shape[1] // share):
-        cols = slice(f * share, (f + 1) * share)
-        value = dot(turned_near, cot_near_ref[:, cols]) + dot(turned_far, cot_far_ref[:, cols])
-        put_share(value, jnp.int32(f), where_ref[0] & 1, keep_ref, send_ref, False)
-
-
-def ffn_stage(second, cot, w_gate, w_up, w_down, ctx_count, where):
-    rows, model = second[0].shape
+def pair_bit(where_ref):
+    return lax.shift_right_logical(where_ref[0], 1) & 1
+
+
+def grad_hidden_kernel(where_ref, cot_ref, wd_ref, out_ref):
+    out_ref[...] = right_dot(cot_ref[...], wd_ref[...])
+
+
+def grad_hidden_stage(cot, w_down, where):
+    rows, model = cot.shape
+    units = w_down.shape[0] // 2
+    block = 256
+    steps = units // block
+    return pl.pallas_call(
+        grad_hidden_kernel,
+        out_shape=jax.ShapeDtypeStruct((rows, units), jnp.float32),
+        grid_spec=pltpu.PrefetchScalarGridSpec(
+            num_scalar_prefetch=1,
+            grid=(steps,),
+            in_specs=[
+                pl.BlockSpec((rows, model), lambda i, w: (0, 0), pipeline_mode=pl.Buffered(1)),
+                pl.BlockSpec((block, model), lambda i, w: (pair_bit(w) * steps + i, 0)),
+            ],
+            out_specs=pl.BlockSpec((rows, block), lambda i, w: (0, i)),
+        ),
+        compiler_params=pltpu.CompilerParams(vmem_limit_bytes=32 << 20),
+        cost_estimate=cost(2 * rows * model * units, 4 * rows * model),
+        name="grad_hidden",
+    )(where, cot, w_down)
+
+
+def ffn_kernel(where_ref, in_ref, gh_ref, wg_ref, wu_ref, hid_ref, gg_ref, gu_ref):
+    gate = dot(in_ref[...], wg_ref[...])
+    upward = dot(in_ref[...], wu_ref[...])
+    grad_hidden = gh_ref[...]
+    sigma = jax.nn.sigmoid(gate)
+    swish = gate * sigma
+    hid_ref[...] = (swish * upward).astype(jnp.bfloat16)
+    gg_ref[...] = (grad_hidden * upward * sigma * (1.0 + gate * (1.0 - sigma))).astype(
+        jnp.bfloat16
+    )
+    gu_ref[...] = (grad_hidden * swish).astype(jnp.bfloat16)
+
+
+def ffn_stage(second, grad_hidden, w_gate, w_up, where):
+    rows, model = second.shape
     units = w_gate.shape[1] // 2
     block = 256
     steps = units // block
-    share = model // ctx_count
-    pair = lambda where_ref: lax.shift_right_logical(where_ref[0], 1) & 1
-    row_spec = pl.BlockSpec(
-        (rows, model), lambda i, w: (0, 0), pipeline_mode=pl.Buffered(1)
-    )
-    col_spec = pl.BlockSpec((model, block), lambda i, w: (0, pair(w) * steps + i))
-    unit_spec = pl.BlockSpec((2 * rows, block), lambda i, w: (0, i))
-    share_spec = pl.BlockSpec((ctx_count // 2, block, share), lambda i, w: (0, i, 0))
-    unit = jax.ShapeDtypeStruct((2 * rows, units), jnp.bfloat16)
-    shares = jax.ShapeDtypeStruct((ctx_count // 2, units, share), jnp.bfloat16)
+    col_spec = pl.BlockSpec((model, block), lambda i, w: (0, pair_bit(w) * steps + i))
+    unit_spec = pl.BlockSpec((rows, block), lambda i, w: (0, i))
+    unit = jax.ShapeDtypeStruct((rows, units), jnp.bfloat16)
     return pl.pallas_call(
         ffn_kernel,
-        out_shape=(unit, unit, unit, shares, shares),
+        out_shape=(unit, unit, unit),
         grid_spec=pltpu.PrefetchScalarGridSpec(
             num_scalar_prefetch=1,
             grid=(steps,),
-            in_specs=[row_spec] * 4
-            + [
+            in_specs=[
+                pl.BlockSpec((rows, model), lambda i, w: (0, 0), pipeline_mode=pl.Buffered(1)),
+                unit_spec,
                 col_spec,
                 col_spec,
-                pl.BlockSpec((block, model), lambda i, w: (pair(w) * steps + i, 0)),
             ],
-            out_specs=[unit_spec] * 3 + [share_spec] * 2,
+            out_specs=[unit_spec] * 3,
         ),
         compiler_params=pltpu.CompilerParams(vmem_limit_bytes=44 << 20),
-        cost_estimate=cost(16 * rows * model * units, 16 * rows * model),
+        cost_estimate=cost(4 * rows * model * units, 6 * rows * model),
         name="ffn_stage",
-    )(where, *second, *cot, w_gate, w_up, w_down)
+    )(where, second, grad_hidden, w_gate, w_up)
 
 
 def grad_second_kernel(where_ref, gg_ref, gu_ref, wg_ref, wu_ref, keep_ref, send_ref):
@@ -580,11 +617,10 @@
     rows, units = lefts[0].shape
     model = rights[0].shape[0 if transposed else 1]
     block = 512
-    pair = lambda where_ref: lax.shift_right_logical(where_ref[0], 1) & 1
     if transposed:
-        right_spec = pl.BlockSpec((block, units), lambda n, w: (n, pair(w)))
+        right_spec = pl.BlockSpec((block, units), lambda n, w: (n, pair_bit(w)))
     else:
-        right_spec = pl.BlockSpec((units, block), lambda n, w: (pair(w), n))
+        right_spec = pl.BlockSpec((units, block), lambda n, w: (pair_bit(w), n))
     left_spec = pl.BlockSpec((rows, units), lambda n, w: (0, 0), pipeline_mode=pl.Buffered(1))
     half = jax.ShapeDtypeStruct((rows // 2, model), jnp.bfloat16)
     half_spec = pl.BlockSpec((rows // 2, block), lambda n, w: (0, n))
@@ -607,36 +643,23 @@
     lefts, refs = refs[:left_count], refs[left_count:]
     rights, (keep_ref, send_ref) = refs[:-2], refs[-2:]
     share = keep_ref.shape[1]
-    turned = [left[...].T for left in lefts]
     step = pl.program_id(0)
-    start = 0
-    pieces = []
-    for terms in pairs:
-        pieces.append(
-            sum(dot(turned[l], rights[r][rows, :]) for l, r, rows in terms)
-        )
-    value = pieces[0] if len(pieces) == 1 else jnp.concatenate(pieces, axis=1)
-    per_step = value.shape[0] // share
+    pieces = [left_dot(lefts[l][...], rights[r][...]) for l, r in pairs]
+    per_step = lefts[0].shape[1] // share
     for k in range(per_step):
-        put_share(
-            value[k * share : (k + 1) * share],
-            step * per_step + k,
-            where_ref[0] & 1,
-            keep_ref,
-            send_ref,
-            swap_bits,
-        )
-
-
-def weight_shares(name, lefts, rights, pairs, width, ctx_count, swap_bits, where):
+        rows = slice(k * share, (k + 1) * share)
+        value = jnp.concatenate([piece[rows] for piece in pieces], axis=1)
+        index = step * per_step + k
+        put_share(value, index, where_ref[0] & 1, keep_ref, send_ref, swap_bits)
+
+
+def weight_shares(name, lefts, rights, pairs, ctx_count, swap_bits, where):
     rows, model = lefts[0].shape
     block = 256
     share = model // ctx_count
+    width = sum(rights[r].shape[1] for _, r in pairs)
     shares = jax.ShapeDtypeStruct((ctx_count // 2, share, width), jnp.bfloat16)
     share_spec = pl.BlockSpec(shares.shape, lambda i, w: (0, 0, 0))
-    flops = 2 * model * sum(
-        rights[r].shape[1] * lefts[l].shape[0] for terms in pairs for l, r, _ in terms
-    )
     return pl.pallas_call(
         functools.partial(shares_kernel, len(lefts), swap_bits, pairs),
         out_shape=(shares, shares),
@@ -651,7 +674,7 @@
             out_specs=[share_spec, share_spec],
         ),
         compiler_params=pltpu.CompilerParams(vmem_limit_bytes=36 << 20),
-        cost_estimate=cost(flops, 4 * rows * model),
+        cost_estimate=cost(2 * rows * model * width, 4 * rows * model),
         name=name,
     )(where, *lefts, *rights)
 
@@ -737,7 +760,7 @@
 def gather_pair(own):
     partner = flip(own, "ctx", 2)
     near = jnp.concatenate([own, partner, flip(own, "tp", 2), flip(partner, "tp", 2)])
-    return near, flip(near, "tp", 1)
+    return jnp.concatenate([near, flip(near, "tp", 1)])
 
 
 def gather_rows(own, tensor):
@@ -774,11 +797,21 @@
 
 def gather_keys(kv_local, ctx_count):
     parts = {0: kv_local}
-    for mask in range(2, ctx_count, 2):
-        parts[mask] = flip(kv_local, "ctx", mask)
-    for mask in range(0, ctx_count, 2):
-        parts[mask + 1] = flip(parts[mask], "ctx", 1)
+    for bit in reversed(high_masks(ctx_count)):
+        for mask in list(parts):
+            parts[mask + bit] = flip(parts[mask], "ctx", bit)
+    for bit in (2, 1):
+        for mask in list(parts):
+            parts[mask + bit] = flip(parts[mask], "ctx", bit)
     return [parts[mask] for mask in range(ctx_count)]
+
+
+def all_sum(value, ctx_count):
+    for axis, mask in [("tp", 1), ("tp", 2), ("ctx", 1), ("ctx", 2)] + [
+        ("ctx", mask) for mask in high_masks(ctx_count)
+    ]:
+        value = value + flip(value, axis, mask)
+    return value
 
 
 class Reduce:
@@ -820,17 +853,14 @@
 
 
 class KvReduce:
-    def __init__(self, keep, send, ctx_count):
-        self.ctx_count = ctx_count
+    def __init__(self, keep, send):
         self.keep, self.got = keep, flip(send, "ctx", 1)
 
-    def high(self, dep):
+    def halve(self, mask, dep):
         keep, got = after(dep, self.keep, self.got)
-        for mask in [2] + high_masks(self.ctx_count):
-            n = keep.shape[0] // 2
-            away = flip(add(keep[n:], got[n:]), "ctx", mask)
-            keep, got = add(keep[:n], got[:n]), away
-        self.keep, self.got = keep, got
+        n = keep.shape[0] // 2
+        away = flip(add(keep[n:], got[n:]), "ctx", mask)
+        self.keep, self.got = add(keep[:n], got[:n]), away
 
 
 def norm_back(grad_out, normed, inv_scale, gain):
@@ -865,20 +895,20 @@
     first_input, queries, kv_local, cosine, sine = input_stage(
         layer_input, attn_gain, w_query, key_matrix, value_matrix, block_order, cont_prompt, where
     )
-    parts = gather_keys(kv_local, ctx_count)
-
-    cot_own = after(first_input, lax.dynamic_slice_in_dim(cotangent, tensor * quarter, quarter))
+    cot_own = lax.dynamic_slice_in_dim(cotangent, tensor * quarter, quarter)
     cot_slots = slots_of(cotangent, tensor)
     cot_part = flip(cot_own, "ctx", 2)
+    parts = gather_keys(after(cot_part, kv_local), ctx_count)
     cot_part = jnp.concatenate([cot_part, flip(cot_part, "tp", 2)])
     cot_far = flip(cot_part, "tp", 1)
-    cot = (
-        jnp.concatenate([cot_slots[0], cot_part[:quarter], cot_slots[1], cot_part[quarter:]]),
-        jnp.concatenate([cot_slots[2], cot_far[:quarter], cot_slots[3], cot_far[quarter:]]),
-    )
+    cot = jnp.concatenate(
+        [cot_slots[0], cot_part[:quarter], cot_slots[1], cot_part[quarter:]]
+        + [cot_slots[2], cot_far[:quarter], cot_slots[3], cot_far[quarter:]]
+    )
+    grad_hidden = grad_hidden_stage(cot, w_down, where)
 
     mixed, log_total, keep, send = attention_forward(
-        queries, w_out, parts, block_order, cont_prompt, where
+        after(grad_hidden, queries), w_out, parts, block_order, cont_prompt, where
     )
     own_input = lax.dynamic_slice_in_dim(layer_input, tensor * quarter, quarter)
     own_input = own_input.astype(jnp.float32)
@@ -886,40 +916,39 @@
     inv_two = lax.rsqrt(jnp.mean(middle * middle, axis=-1, keepdims=True) + eps_norm)
     normed_two = middle * inv_two
     second = gather_pair((normed_two * ffn_gain).astype(jnp.bfloat16))
-    hidden, grad_gate, grad_up, keep, send = ffn_stage(
-        second, cot, w_gate, w_up, w_down, ctx_count, where
-    )
-
-    down = Reduce(keep, send)
-    second_terms = pair_scatter(
-        *unit_sum(
-            grad_second_kernel, "grad_second", (grad_gate, grad_up), (w_gate, w_up), True, where
-        )
-    )
-    rows = second[0].shape[0]
-    halves = (slice(0, rows), slice(rows, 2 * rows))
+    hidden, grad_gate, grad_up = ffn_stage(second, grad_hidden, w_gate, w_up, where)
+
+    down_shares = weight_shares(
+        "down_shares", (cot,), (hidden,), ((0, 0),), ctx_count, False, where
+    )
+    down = Reduce(*down_shares)
+    grad_gate, grad_up = after(down_shares[0], grad_gate, grad_up)
+    partial = unit_sum(
+        grad_second_kernel, "grad_second", (grad_gate, grad_up), (w_gate, w_up), True, where
+    )
+    second_terms = pair_scatter(*partial)
 
     def unit_shares(name, grad, dep):
         return weight_shares(
-            name, second, (after(dep, grad),), (tuple((k, 0, halves[k]) for k in range(2)),),
-            grad.shape[1], ctx_count, False, where,
+            name, (second,), (after(dep, grad),), ((0, 0),), ctx_count, False, where
         )
 
-    gate_shares = unit_shares("gate_shares", grad_gate, second_terms[0])
+    gate_shares = unit_shares("gate_shares", grad_gate, partial[0])
     up_shares = unit_shares("up_shares", grad_up, gate_shares[0])
     ffn_halves = unit_sum(
         ffn_out_kernel, "ffn_out", (after(up_shares[0], hidden),), (w_down,), False, where
     )
-
+    dep = ffn_halves[0]
+    for mask in highs:
+        down.halve(mask, ctx, dep)
+        dep = down.keep
+    gate = Reduce(*after(dep, *gate_shares))
     grad_norm_two, ffn_gain_part = norm_back(
-        total(after(ffn_halves[0], *second_terms)), normed_two, inv_two, ffn_gain
+        total(after(dep, *second_terms)), normed_two, inv_two, ffn_gain
     )
     grad_middle = cot_own.astype(jnp.float32) + grad_norm_two
     grad_branch = gather_slots(grad_middle.astype(jnp.bfloat16))
-    for mask in highs:
-        down.halve(mask, ctx, grad_middle)
-    gate = Reduce(*after(down.keep, *gate_shares))
-    backward = []
+    backward, kv = [], []
     held = grad_branch
     for head in range(kv_heads):
         backward.append(
@@ -929,61 +958,66 @@
             )
         )
         held = after(backward[-1][0], grad_branch)
+        kv.append(KvReduce(*backward[-1][1:]))
     grad_queries = [item[0] for item in backward]
-    spans = slice(0, first_input.shape[0])
-    wide = grad_queries[0].shape[1]
-    last_query = grad_queries[-1]
+    dep = grad_queries[-1]
+    for mask in highs:
+        gate.halve(mask, ctx, dep)
+        dep = gate.keep
     branch_shares = weight_shares(
         "branch_shares",
         (first_input, grad_branch),
-        grad_queries + [after(last_query, mixed)],
-        tuple(((0, h, spans),) for h in range(kv_heads)) + (((1, kv_heads, spans),),),
-        2 * w_query.shape[1],
+        grad_queries + [after(dep, mixed)],
+        tuple((0, h) for h in range(kv_heads)) + ((1, kv_heads),),
         ctx_count,
         True,
         where,
     )
+    kv[0].halve(2, branch_shares[0])
+    ffn_terms = pair_scatter(*after(kv[0].keep, *ffn_halves))
+    for item in kv[1:]:
+        item.halve(2, kv[0].keep)
+    up = Reduce(*after(kv[-1].keep, *up_shares))
     for mask in highs:
-        gate.halve(mask, ctx, branch_shares[0])
-    kv = [KvReduce(*after(gate.keep, item[1], item[2]), ctx_count) for item in backward]
-    ffn_terms = pair_scatter(*after(gate.keep, *ffn_halves))
-    sum_down = both_halves(down, ctx, 0, gate.keep)
-    for item in kv:
-        item.high(sum_down)
-    up = Reduce(*after(kv[-1].keep, *up_shares))
+        for item in kv:
+            item.halve(mask, kv[-1].keep)
+    sum_down = both_halves(down, ctx, 1, kv[0].keep).T
     keep, send, grad_kv = tail_stage(
         [(item.keep, item.got) for item in kv], cosine, sine, grad_queries,
         w_query, key_matrix, value_matrix, where,
     )
     first_terms = scatter_slots(keep, send)
     kv_shares = weight_shares(
-        "kv_shares", (first_input,), (grad_kv,), (((0, 0, spans),),), grad_kv.shape[1],
-        ctx_count, True, where,
-    )
-    output = gather_rows((middle + total(ffn_terms)).astype(jnp.bfloat16), tensor)
+        "kv_shares", (first_input,), (grad_kv,), ((0, 0),), ctx_count, True, where
+    )
+    dep = kv_shares[0]
     for mask in highs:
-        up.halve(mask, ctx, kv_shares[0])
-    branch = Reduce(*after(up.keep, *branch_shares))
-    last = Reduce(*after(up.keep, *kv_shares))
-    sum_gate = both_halves(gate, ctx, 1, up.keep)
+        up.halve(mask, ctx, dep)
+        dep = up.keep
+    branch = Reduce(*after(dep, *branch_shares))
     inv_one = lax.rsqrt(jnp.mean(own_input * own_input, axis=-1, keepdims=True) + eps_norm)
     grad_norm_one, attn_gain_part = norm_back(
-        total(first_terms), own_input * inv_one, inv_one, attn_gain
-    )
-    grad_input = gather_rows((grad_middle + grad_norm_one).astype(jnp.bfloat16), tensor)
-    sum_up = both_halves(up, ctx, 1, grad_input)
-    for item in (branch, last):
-        for mask in [2] + highs:
-            item.halve(mask, ctx, sum_up if mask == 2 else None)
+        total(after(dep, *first_terms)), own_input * inv_one, inv_one, attn_gain
+    )
+    grad_input = (grad_middle + grad_norm_one).astype(jnp.bfloat16)
+    output = gather_rows((middle + total(ffn_terms)).astype(jnp.bfloat16), tensor)
+    sum_gate = both_halves(gate, ctx, 1, grad_input)
+    grad_input = gather_rows(grad_input, tensor)
+    gains = all_sum(jnp.stack([attn_gain_part, ffn_gain_part]), ctx_count)
+    branch.halve(2, ctx)
+    last = Reduce(*after(branch.keep, *kv_shares))
+    for mask in highs:
+        branch.halve(mask, ctx)
+    sum_up = both_halves(up, ctx, 1)
+    for mask in [2] + highs:
+        last.halve(mask, ctx)
     width_q, width_k = w_query.shape[1], key_matrix.shape[1]
     branch_sum, last_sum = branch.sum(), last.sum()
     sum_query, sum_out = branch_sum[:, :width_q], branch_sum[:, width_q:].T
     sum_key, sum_value = last_sum[:, :width_k], last_sum[:, width_k:]
 
-    devices = ctx_count * tp_count
-    gains = jnp.stack([attn_gain_part, ffn_gain_part]).reshape(2, devices, -1)
-    gains = lax.all_to_all(gains, ("ctx", "tp"), 1, 1, tiled=True)
-    gains = jnp.sum(gains, axis=1)
+    gains = gains.reshape(2, ctx_count * tp_count, -1)
+    gains = lax.dynamic_index_in_dim(gains, ctx * tp_count + tensor, 1, keepdims=False)
     return (
         output,
         grad_input,

time: 681 us -> 714 us (1.048)
  waiting for transfers between devices: 359 us -> 392 us
  local copies, waits for them, and re-layouts: 38.2 us -> 55.2 us
  starting transfers between devices: 63.5 us -> 49.6 us
    ppermute x53 -> x58, waiting for transfers between devices: 339 us -> 392 us  [flip(): lax.ppermute(value, axis, [(i, i ^ mask) for i in range(lax.axis_size(axi...]
    unnamed x169 -> x200, local copies, waits for them, and re-layouts: 28.4 us -> 48.9 us
    all_to_all x1 -> x0, waiting for transfers between devices: 20.1 us -> none  [body(): gains = lax.all_to_all(gains, ('ctx', 'tp'), 1, 1, tiled=True)]
    pallas_call x1 -> x2, Pallas kernels: 35.8 us -> 21.6 us  [the longest x1 15.6 us: ffn_stage(): pl.pallas_call(ffn_kernel, out_shape=(unit, unit, unit), grid_spec=pltpu....]
    ppermute x53 -> x58, starting transfers between devices: 60.7 us -> 49.6 us  [flip(): lax.ppermute(value, axis, [(i, i ^ mask) for i in range(lax.axis_size(axi...]
    pallas_call x4 -> x5, Pallas kernels: 29.8 us -> 34.4 us  [weight_shares(): pl.pallas_call(functools.partial(shares_kernel, len(lefts), swap_bits, pa...]
  transfers between devices with their start and end apart: 54 -> 58, of which waited for: 32 -> 35; matrix products, arithmetic and copies ran while one was open for 9% -> 9% of each run, Pallas kernels for 12% -> 13%
where the time goes in v5:
time: 714 us; the launch traced here: 705 us
  waiting for transfers between devices  392 us (55%)
  Pallas kernels  153 us (21%)
  local copies, waits for them, and re-layouts  55.2 us (8%)
  other arithmetic  53 us (7%)
  starting transfers between devices  49.6 us (7%)
    ppermute x58, waiting for transfers between devices, flip(): lax.ppermute(value, axis, [(i, i ^ mask) for i in range(lax.axis_size(axi...  392 us
    ppermute x58, starting transfers between devices, flip(): lax.ppermute(value, axis, [(i, i ^ mask) for i in range(lax.axis_size(axi...  49.6 us
    unnamed x200, local copies, waits for them, and re-layouts  48.9 us
    pallas_call x2, Pallas kernels, attention_backward(): pl.pallas_call(functools.partial(backward_kernel, rep, 1, ctx_count, head...  42.6 us
    pallas_call x5, Pallas kernels, weight_shares(): pl.pallas_call(functools.partial(shares_kernel, len(lefts), swap_bits, pa...  34.4 us
    convert_element_type x20, other arithmetic, add(): (left.astype(jnp.float32) + right.astype(jnp.float32)).astype(jnp.bfloat16)  29 us
    pallas_call x1, Pallas kernels, attention_forward(): pl.pallas_call(functools.partial(forward_kernel, rep, kv_heads, ctx_count...  26.7 us
    pallas_call x2, Pallas kernels, unit_sum(): pl.pallas_call(kernel, out_shape=(half, half), grid_spec=pltpu.PrefetchSc...  18.8 us
  transfers between devices with their start and end apart: 58, of which 35 were waited for; matrix products, arithmetic and copies ran while one was open for 9% of the time, Pallas kernels for 13%

profile of v5, /device:TPU:0, one launch (start us, length us, event | category | flops | bytes accessed | tf_op | source)
XLA Modules:
  0.0 704.9 jit_solution(4155585233447820868)
XLA Ops:
  5.6 11.9 %collective-permute-done = bf16[128,2048]{1,0:T(8,128)(2,1)S(1)} collective-permute-done((bf16[128,2048]{1,0:T(8,128)(2,1)S(1)}, bf16[128,2048]{1,0:T(8,128)(2,1)S(1)}, u32[]{:S(2)}, u32[]{:S(2)}) %collective-permute-start) | collective-permute-done | bytes 524320 | tf_op jit(solution)/shard_map/ppermute | solution.py:735
  27.9 5.1 input_stage.1
  42.1 17.1 %collective-permute-done.6.refs_4_ = bf16[512,512]{1,0:T(8,128)(2,1)S(1)} collective-permute-done((bf16[512,512]{1,0:T(8,128)(2,1)S(1)}, bf16[512,512]{1,0:T(8,128)(2,1)S(1)}, u32[]{:S(2)}, u32[]{:S(2)}) %collective-permute-start.6) | collective-permute-done | bytes 524320 | tf_op jit(solution)/shard_map/ppermute | solution.py:735
  66.2 7.6 %collective-permute-done.8.refs_6_ = bf16[512,512]{1,0:T(8,128)(2,1)S(1)} collective-permute-done((bf16[512,512]{1,0:T(8,128)(2,1)S(1)}, bf16[512,512]{1,0:T(8,128)(2,1)S(1)}, u32[]{:S(2)}, u32[]{:S(2)}) %collective-permute-start.8) | collective-permute-done | bytes 524320 | tf_op jit(solution)/shard_map/ppermute | solution.py:735
  79.9 3.4 copy-done
  85.5 6.0 grad_hidden.1.gh_ref
  93.6 4.1 collective-permute-done.9.refs_7_
  97.8 26.7 %attention_forward.1 = (bf16[512,512]{1,0:T(8,128)(2,1)S(1)}, f32[2,4,256]{2,1,0:T(4,128)S(1)}, bf16[256,2048]{1,0:T(8,128)(2,1)S(1)}, bf16[256,2048]{1,0:T(8,128)(2,1)S(1)}) custom-call(s32[32]{0:T(128)S(1)} %copy-done.42, s32[8]{0:T(128)S(1)} %copy-done.44, s32[2]{0:T(128)S(1)} %pad_add_fusion.where_ref, bf16[512,512]{1,0:T(8,128)(2,1)S(1)} %copy-done.52, ...), custom_call_target="tpu_custom_call" | custom-call | flops 3221225472 | bytes 8388608 | tf_op jit(solution)/shard_map/attention_forward/pallas_call | solution.py:342
  128.0 13.5 %collective-permute-done.11 = bf16[128,2048]{1,0:T(8,128)(2,1)S(1)} collective-permute-done((bf16[128,2048]{1,0:T(8,128)(2,1)S(1)}, bf16[128,2048]{1,0:T(8,128)(2,1)S(1)}, u32[]{:S(2)}, u32[]{:S(2)}) %collective-permute-start.11) | collective-permute-done | bytes 524320 | tf_op jit(solution)/shard_map/ppermute | solution.py:735
  145.8 10.8 %collective-permute-done.12 = bf16[128,2048]{1,0:T(8,128)(2,1)S(1)} collective-permute-done((bf16[128,2048]{1,0:T(8,128)(2,1)S(1)}, bf16[128,2048]{1,0:T(8,128)(2,1)S(1)}, u32[]{:S(2)}, u32[]{:S(2)}) %collective-permute-start.12) | collective-permute-done | bytes 524320 | tf_op jit(solution)/shard_map/ppermute | solution.py:735
  158.3 11.0 %collective-permute-done.14 = bf16[128,2048]{1,0:T(8,128)(2,1)S(1)} collective-permute-done((bf16[128,2048]{1,0:T(8,128)(2,1)S(1)}, bf16[128,2048]{1,0:T(8,128)(2,1)S(1)}, u32[]{:S(2)}, u32[]{:S(2)}) %collective-permute-start.14) | collective-permute-done | bytes 524320 | tf_op jit(solution)/shard_map/ppermute | solution.py:735
  169.7 4.0 collective-permute-done.15
  176.0 15.6 %ffn_stage.1 = (bf16[1024,1024]{1,0:T(8,128)(2,1)S(1)}, bf16[1024,1024]{1,0:T(8,128)(2,1)S(1)}, bf16[1024,1024]{1,0:T(8,128)(2,1)S(1)}) custom-call(s32[2]{0:T(128)S(1)} %pad_add_fusion.where_ref, bf16[1024,2048]{1,0:T(8,128)(2,1)} %copy-done.12, f32[1024,1024]{1,0:T(8,128)} %copy-done.3, bf16[2048,2048]{1,0:T(8,128)(2,1)} %wg_ref.3, bf16[2048,2048]{1,0:T(8,128)(2,1)} %wu_ref.3), custom_call_target="tpu_custom_call" | custom-call | flops 8589934592 | bytes 12582912 | tf_op jit(solution)/shard_map/ffn_stage/pallas_call | solution.py:582
  191.7 7.5 %down_shares.1 = (bf16[4,256,1024]{2,1,0:T(8,128)(2,1)S(1)}, bf16[4,256,1024]{2,1,0:T(8,128)(2,1)S(1)}) custom-call(s32[2]{0:T(128)S(1)} %pad_add_fusion.where_ref, bf16[1024,2048]{1,0:T(8,128)(2,1)S(1)} %copy-done.2, bf16[1024,1024]{1,0:T(8,128)(2,1)S(1)} %get-tuple-element.106.refs_1_.hid_ref), custom_call_target="tpu_custom_call" | custom-call | flops 4294967296 | bytes 8388608 | tf_op jit(solution)/shard_map/down_shares/pallas_call | solution.py:663
  200.6 4.1 copy-done.19
  206.3 12.6 %grad_second.1 = (bf16[512,2048]{1,0:T(8,128)(2,1)S(1)}, bf16[512,2048]{1,0:T(8,128)(2,1)}) custom-call(s32[2]{0:T(128)S(1)} %pad_add_fusion.where_ref, bf16[1024,1024]{1,0:T(8,128)(2,1)S(1)} %copy-done.66, bf16[1024,1024]{1,0:T(8,128)(2,1)S(1)} %get-tuple-element.104.gu_ref.refs_1_, bf16[2048,2048]{1,0:T(8,128)(2,1)S(1)} %copy-done.19, ...), custom_call_target="tpu_custom_call" | custom-call | flops 8589934592 | bytes 8388608 | tf_op jit(solution)/shard_map/grad_second/pallas_call | solution.py:627
  219.1 4.4 collective-permute-done.17
  229.1 8.8 %gate_shares.1 = (bf16[4,256,1024]{2,1,0:T(8,128)(2,1)S(1)}, bf16[4,256,1024]{2,1,0:T(8,128)(2,1)}) custom-call(s32[2]{0:T(128)S(1)} %pad_add_fusion.where_ref, bf16[1024,2048]{1,0:T(8,128)(2,1)S(1)} %copy-done.13, bf16[1024,1024]{1,0:T(8,128)(2,1)S(1)} %copy-done.67), custom_call_target="tpu_custom_call" | custom-call | flops 4294967296 | bytes 8388608 | tf_op jit(solution)/shard_map/gate_shares/pallas_call | solution.py:663
  240.1 8.8 %up_shares.1 = (bf16[4,256,1024]{2,1,0:T(8,128)(2,1)S(1)}, bf16[4,256,1024]{2,1,0:T(8,128)(2,1)}) custom-call(s32[2]{0:T(128)S(1)} %pad_add_fusion.where_ref, bf16[1024,2048]{1,0:T(8,128)(2,1)S(1)} %copy-done.14, bf16[1024,1024]{1,0:T(8,128)(2,1)S(1)} %copy-done.64), custom_call_target="tpu_custom_call" | custom-call | flops 4294967296 | bytes 8388608 | tf_op jit(solution)/shard_map/up_shares/pallas_call | solution.py:663
  254.5 6.2 ffn_out.1
  260.7 6.5 collective-permute-done.16
  272.6 12.8 %collective-permute-done.21 = bf16[128,2048]{1,0:T(8,128)(2,1)S(1)} collective-permute-done((bf16[128,2048]{1,0:T(8,128)(2,1)S(1)}, bf16[128,2048]{1,0:T(8,128)(2,1)S(1)}, u32[]{:S(2)}, u32[]{:S(2)}) %collective-permute-start.21) | collective-permute-done | bytes 524320 | tf_op jit(solution)/shard_map/ppermute | solution.py:735
  289.8 21.3 %attention_backward_0.1 = (bf16[512,256]{1,0:T(8,128)(2,1)}, bf16[2048,256]{1,0:T(8,128)(2,1)}, bf16[2048,256]{1,0:T(8,128)(2,1)}) custom-call(s32[32]{0:T(128)} %order_ref.7, s32[8]{0:T(128)} %cont_ref.7, s32[2]{0:T(128)} %copy-done.17, bf16[512,512]{1,0:T(8,128)(2,1)} %copy-done.51, bf16[512,2048]{1,0:T(8,128)(2,1)} %pad_maximum_fusion.1.gb_ref.refs_1_, ...), custom_call_target="tpu_custom_call" | custom-call | flops 3221225472 | bytes 6291456 | tf_op jit(solution)/shard_map/attention_backward_0/pallas_call | solution.py:378
  311.2 21.3 %attention_backward_1.1 = (bf16[512,256]{1,0:T(8,128)(2,1)}, bf16[2048,256]{1,0:T(8,128)(2,1)}, bf16[2048,256]{1,0:T(8,128)(2,1)}) custom-call(s32[32]{0:T(128)} %order_ref.7, s32[8]{0:T(128)} %cont_ref.7, s32[2]{0:T(128)} %copy-done.17, bf16[512,512]{1,0:T(8,128)(2,1)} %copy-done.51, bf16[512,2048]{1,0:T(8,128)(2,1)} %pad_maximum_fusion.1.gb_ref.refs_1_, ...), custom_call_target="tpu_custom_call" | custom-call | flops 3221225472 | bytes 6291456 | tf_op jit(solution)/shard_map/attention_backward_1/pallas_call | solution.py:378
  335.6 4.1 add_convert_fusion.2
  339.8 5.6 branch_shares.1
  345.4 11.5 %collective-permute-done.24 = bf16[2048,256]{1,0:T(8,128)(2,1)} collective-permute-done((bf16[2048,256]{1,0:T(8,128)(2,1)}, bf16[2048,256]{1,0:T(8,128)(2,1)}, u32[]{:S(2)}, u32[]{:S(2)}) %collective-permute-start.24) | collective-permute-done | bytes 1048608 | tf_op jit(solution)/shard_map/ppermute | solution.py:735
  358.3 20.4 %collective-permute-done.31 = bf16[2048,256]{1,0:T(8,128)(2,1)S(1)} collective-permute-done((bf16[2048,256]{1,0:T(8,128)(2,1)}, bf16[2048,256]{1,0:T(8,128)(2,1)S(1)}, u32[]{:S(2)}, u32[]{:S(2)}) %collective-permute-start.31) | collective-permute-done | bytes 1048608 | tf_op jit(solution)/shard_map/ppermute | solution.py:735
  381.2 12.4 %collective-permute-done.32 = bf16[1024,256]{1,0:T(8,128)(2,1)S(1)} collective-permute-done((bf16[1024,256]{1,0:T(8,128)(2,1)S(1)}, bf16[1024,256]{1,0:T(8,128)(2,1)S(1)}, u32[]{:S(2)}, u32[]{:S(2)}) %collective-permute-start.32) | collective-permute-done | bytes 524320 | tf_op jit(solution)/shard_map/ppermute | solution.py:735
  393.6 9.9 %collective-permute-done.34 = bf16[1024,256]{1,0:T(8,128)(2,1)S(1)} collective-permute-done((bf16[1024,256]{1,0:T(8,128)(2,1)S(1)}, bf16[1024,256]{1,0:T(8,128)(2,1)S(1)}, u32[]{:S(2)}, u32[]{:S(2)}) %collective-permute-start.34) | collective-permute-done | bytes 524320 | tf_op jit(solution)/shard_map/ppermute | solution.py:735
  407.9 38.2 %collective-permute-done.35.refs_3_ = bf16[512,256]{1,0:T(8,128)(2,1)S(1)} collective-permute-done((bf16[512,256]{1,0:T(8,128)(2,1)S(1)}, bf16[512,256]{1,0:T(8,128)(2,1)S(1)}, u32[]{:S(2)}, u32[]{:S(2)}) %collective-permute-start.35) | collective-permute-done | bytes 262176 | tf_op jit(solution)/shard_map/ppermute | solution.py:735
  446.1 5.6 collective-permute-done.33.refs_1_
  451.8 3.9 tail_stage.1
  457.1 39.7 %collective-permute-done.56 = bf16[2,256,1024]{2,1,0:T(8,128)(2,1)} collective-permute-done((bf16[2,256,1024]{2,1,0:T(8,128)(2,1)}, bf16[2,256,1024]{2,1,0:T(8,128)(2,1)}, u32[]{:S(2)}, u32[]{:S(2)}) %collective-permute-start.56) | collective-permute-done | bytes 1048608 | tf_op jit(solution)/shard_map/ppermute | solution.py:735
  500.6 3.7 kv_shares.1
  504.3 25.3 %collective-permute-done.57 = bf16[256,1024]{1,0:T(8,128)(2,1)S(1)} collective-permute-done((bf16[256,1024]{1,0:T(8,128)(2,1)S(1)}, bf16[256,1024]{1,0:T(8,128)(2,1)S(1)}, u32[]{:S(2)}, u32[]{:S(2)}) %collective-permute-start.57) | collective-permute-done | bytes 524320 | tf_op jit(solution)/shard_map/ppermute | solution.py:735
  531.0 3.9 add_convert_fusion.1
  538.2 3.1 copy.26
  547.4 3.2 collective-permute-done.43
  556.5 8.8 %collective-permute-done.44 = f32[2,2048]{1,0:T(2,128)S(1)} collective-permute-done((f32[2,2048]{1,0:T(2,128)S(1)}, f32[2,2048]{1,0:T(2,128)S(1)}, u32[]{:S(2)}, u32[]{:S(2)}) %collective-permute-start.44) | collective-permute-done | bytes 16416 | tf_op jit(solution)/shard_map/ppermute | solution.py:735
  570.1 20.1 %collective-permute-done.45 = f32[2,2048]{1,0:T(2,128)S(1)} collective-permute-done((f32[2,2048]{1,0:T(2,128)S(1)}, f32[2,2048]{1,0:T(2,128)S(1)}, u32[]{:S(2)}, u32[]{:S(2)}) %collective-permute-start.45) | collective-permute-done | bytes 16416 | tf_op jit(solution)/shard_map/ppermute | solution.py:735
  596.4 8.9 %collective-permute-done.53 = bf16[256,1024]{1,0:T(8,128)(2,1)} collective-permute-done((bf16[256,1024]{1,0:T(8,128)(2,1)}, bf16[256,1024]{1,0:T(8,128)(2,1)}, u32[]{:S(2)}, u32[]{:S(2)}) %collective-permute-start.53) | collective-permute-done | bytes 524320 | tf_op jit(solution)/shard_map/ppermute | solution.py:735
  606.9 8.7 %collective-permute-done.28 = bf16[128,2048]{1,0:T(8,128)(2,1)S(1)} collective-permute-done((bf16[128,2048]{1,0:T(8,128)(2,1)S(1)}, bf16[128,2048]{1,0:T(8,128)(2,1)S(1)}, u32[]{:S(2)}, u32[]{:S(2)}) %collective-permute-start.28) | collective-permute-done | bytes 524320 | tf_op jit(solution)/shard_map/ppermute | solution.py:735
  622.4 8.2 %collective-permute-done.29 = bf16[128,2048]{1,0:T(8,128)(2,1)S(1)} collective-permute-done((bf16[128,2048]{1,0:T(8,128)(2,1)S(1)}, bf16[128,2048]{1,0:T(8,128)(2,1)S(1)}, u32[]{:S(2)}, u32[]{:S(2)}) %collective-permute-start.29) | collective-permute-done | bytes 524320 | tf_op jit(solution)/shard_map/ppermute | solution.py:735
  636.7 4.9 collective-permute-done.46
  643.8 22.6 %collective-permute-done.49 = bf16[4,256,512]{2,1,0:T(8,128)(2,1)S(1)} collective-permute-done((bf16[4,256,512]{2,1,0:T(8,128)(2,1)S(1)}, bf16[4,256,512]{2,1,0:T(8,128)(2,1)S(1)}, u32[]{:S(2)}, u32[]{:S(2)}) %collective-permute-start.49) | collective-permute-done | bytes 1048608 | tf_op jit(solution)/shard_map/ppermute | solution.py:735
  669.9 19.0 %collective-permute-done.50 = bf16[2,256,512]{2,1,0:T(8,128)(2,1)S(1)} collective-permute-done((bf16[2,256,512]{2,1,0:T(8,128)(2,1)S(1)}, bf16[2,256,512]{2,1,0:T(8,128)(2,1)S(1)}, u32[]{:S(2)}, u32[]{:S(2)}) %collective-permute-start.50) | collective-permute-done | bytes 524320 | tf_op jit(solution)/shard_map/ppermute | solution.py:735
  689.6 8.0 %collective-permute-done.48 = bf16[1,256,1024]{2,1,0:T(8,128)(2,1)S(1)} collective-permute-done((bf16[1,256,1024]{2,1,0:T(8,128)(2,1)S(1)}, bf16[1,256,1024]{2,1,0:T(8,128)(2,1)S(1)}, u32[]{:S(2)}, u32[]{:S(2)}) %collective-permute-start.48) | collective-permute-done | bytes 524320 | tf_op jit(solution)/shard_map/ppermute | solution.py:735
  (349 shorter events, 151.9 us)
Async XLA Ops:
  2.6 14.9 %collective-permute-start = (bf16[128,2048]{1,0:T(8,128)(2,1)S(1)}, bf16[128,2048]{1,0:T(8,128)(2,1)S(1)}, u32[]{:S(2)}, u32[]{:S(2)}) collective-permute-start(bf16[128,2048]{1,0:T(8,128)(2,1)S(1)} %get-tuple-element.191), channel_id=1, source_target_pairs={{0,8},{4,12},{8,0},{12,4},{16,24},{20,28},{24,16},{28,20},{1,9},{5... | collective-permute-start | bytes 1572872 | tf_op jit(solution)/shard_map/ppermute | solution.py:735
  17.6 19.5 %collective-permute-start.1 = (bf16[128,2048]{1,0:T(8,128)(2,1)S(1)}, bf16[128,2048]{1,0:T(8,128)(2,1)S(1)}, u32[]{:S(2)}, u32[]{:S(2)}) collective-permute-start(bf16[128,2048]{1,0:T(8,128)(2,1)S(1)} %collective-permute-done), channel_id=1, source_target_pairs={{0,2},{1,3},{2,0},{3,1},{4,6},{5,7},{6,4},{7,5},{8,10},{9,11},{10,... | collective-permute-start | bytes 1572872 | tf_op jit(solution)/shard_map/ppermute | solution.py:735
  34.4 24.8 %collective-permute-start.6 = (bf16[512,512]{1,0:T(8,128)(2,1)S(1)}, bf16[512,512]{1,0:T(8,128)(2,1)S(1)}, u32[]{:S(2)}, u32[]{:S(2)}) collective-permute-start(bf16[512,512]{1,0:T(8,128)(2,1)S(1)} %get-tuple-element.91.refs_0_), channel_id=1, source_target_pairs={{0,16},{4,20},{8,24},{12,28},{16,0},{20,4},{24,8},{28,12},{1,17},{... | collective-permute-start | bytes 1572872 | tf_op jit(solution)/shard_map/ppermute | solution.py:735
  38.1 37.2 %collective-permute-start.2 = (bf16[256,2048]{1,0:T(8,128)(2,1)}, bf16[256,2048]{1,0:T(8,128)(2,1)}, u32[]{:S(2)}, u32[]{:S(2)}) collective-permute-start(bf16[256,2048]{1,0:T(8,128)(2,1)} %pad_maximum_fusion.2), channel_id=1, source_target_pairs={{0,1},{1,0},{2,3},{3,2},{4,5},{5,4},{6,7},{7,6},{8,9},{9,8},{10,11... | collective-permute-start | bytes 3145736 | tf_op jit(solution)/shard_map/ppermute | solution.py:735
  38.1 25.1 %collective-permute-start.4 = (bf16[512,512]{1,0:T(8,128)(2,1)S(1)}, bf16[512,512]{1,0:T(8,128)(2,1)S(1)}, u32[]{:S(2)}, u32[]{:S(2)}) collective-permute-start(bf16[512,512]{1,0:T(8,128)(2,1)S(1)} %get-tuple-element.91.refs_0_), channel_id=1, source_target_pairs={{0,8},{4,12},{8,0},{12,4},{16,24},{20,28},{24,16},{28,20},{1,9},{5... | collective-permute-start | bytes 1572872 | tf_op jit(solution)/shard_map/ppermute | solution.py:735
  39.7 53.8 %collective-permute-start.3 = (bf16[512,512]{1,0:T(8,128)(2,1)S(1)}, bf16[512,512]{1,0:T(8,128)(2,1)S(1)}, u32[]{:S(2)}, u32[]{:S(2)}) collective-permute-start(bf16[512,512]{1,0:T(8,128)(2,1)S(1)} %get-tuple-element.91.refs_0_), channel_id=1, source_target_pairs={{0,4},{4,0},{8,12},{12,8},{16,20},{20,16},{24,28},{28,24},{1,5},{5... | collective-permute-start | bytes 1572872 | tf_op jit(solution)/shard_map/ppermute | solution.py:735
  59.2 14.6 %collective-permute-start.8 = (bf16[512,512]{1,0:T(8,128)(2,1)S(1)}, bf16[512,512]{1,0:T(8,128)(2,1)S(1)}, u32[]{:S(2)}, u32[]{:S(2)}) collective-permute-start(bf16[512,512]{1,0:T(8,128)(2,1)S(1)} %collective-permute-done.6.refs_4_), channel_id=1, source_target_pairs={{0,8},{4,12},{8,0},{12,4},{16,24},{20,28},{24,16},{28,20},{1,9},{5... | collective-permute-start | bytes 1572872 | tf_op jit(solution)/shard_map/ppermute | solution.py:735
  61.7 31.9 %collective-permute-start.7 = (bf16[512,512]{1,0:T(8,128)(2,1)S(1)}, bf16[512,512]{1,0:T(8,128)(2,1)S(1)}, u32[]{:S(2)}, u32[]{:S(2)}) collective-permute-start(bf16[512,512]{1,0:T(8,128)(2,1)S(1)} %collective-permute-done.6.refs_4_), channel_id=1, source_target_pairs={{0,4},{4,0},{8,12},{12,8},{16,20},{20,16},{24,28},{28,24},{1,5},{5... | collective-permute-start | bytes 1572872 | tf_op jit(solution)/shard_map/ppermute | solution.py:735
  63.2 30.4 %collective-permute-start.5 = (bf16[512,512]{1,0:T(8,128)(2,1)S(1)}, bf16[512,512]{1,0:T(8,128)(2,1)S(1)}, u32[]{:S(2)}, u32[]{:S(2)}) collective-permute-start(bf16[512,512]{1,0:T(8,128)(2,1)S(1)} %collective-permute-done.4.refs_2_), channel_id=1, source_target_pairs={{0,4},{4,0},{8,12},{12,8},{16,20},{20,16},{24,28},{28,24},{1,5},{5... | collective-permute-start | bytes 1572872 | tf_op jit(solution)/shard_map/ppermute | solution.py:735
  73.8 23.9 %collective-permute-start.9 = (bf16[512,512]{1,0:T(8,128)(2,1)S(1)}, bf16[512,512]{1,0:T(8,128)(2,1)S(1)}, u32[]{:S(2)}, u32[]{:S(2)}) collective-permute-start(bf16[512,512]{1,0:T(8,128)(2,1)S(1)} %collective-permute-done.8.refs_6_), channel_id=1, source_target_pairs={{0,4},{4,0},{8,12},{12,8},{16,20},{20,16},{24,28},{28,24},{1,5},{5... | collective-permute-start | bytes 1572872 | tf_op jit(solution)/shard_map/ppermute | solution.py:735
  127.5 14.0 %collective-permute-start.11 = (bf16[128,2048]{1,0:T(8,128)(2,1)S(1)}, bf16[128,2048]{1,0:T(8,128)(2,1)S(1)}, u32[]{:S(2)}, u32[]{:S(2)}) collective-permute-start(bf16[128,2048]{1,0:T(8,128)(2,1)S(1)} %add_convert_fusion.35), channel_id=1, source_target_pairs={{0,2},{1,3},{2,0},{3,1},{4,6},{5,7},{6,4},{7,5},{8,10},{9,11},{10,... | collective-permute-start | bytes 1572872 | tf_op jit(solution)/shard_map/ppermute | solution.py:735
  143.2 13.4 %collective-permute-start.12 = (bf16[128,2048]{1,0:T(8,128)(2,1)S(1)}, bf16[128,2048]{1,0:T(8,128)(2,1)S(1)}, u32[]{:S(2)}, u32[]{:S(2)}) collective-permute-start(bf16[128,2048]{1,0:T(8,128)(2,1)S(1)} %get-tuple-element.187), channel_id=1, source_target_pairs={{0,8},{4,12},{8,0},{12,4},{16,24},{20,28},{24,16},{28,20},{1,9},{5... | collective-permute-start | bytes 1572872 | tf_op jit(solution)/shard_map/ppermute | solution.py:735
  145.2 13.1 %collective-permute-start.13 = (bf16[128,2048]{1,0:T(8,128)(2,1)S(1)}, bf16[128,2048]{1,0:T(8,128)(2,1)S(1)}, u32[]{:S(2)}, u32[]{:S(2)}) collective-permute-start(bf16[128,2048]{1,0:T(8,128)(2,1)S(1)} %get-tuple-element.187), channel_id=1, source_target_pairs={{0,2},{1,3},{2,0},{3,1},{4,6},{5,7},{6,4},{7,5},{8,10},{9,11},{10,... | collective-permute-start | bytes 1572872 | tf_op jit(solution)/shard_map/ppermute | solution.py:735
  219.1 48.1 %collective-permute-start.16 = (bf16[4,256,1024]{2,1,0:T(8,128)(2,1)}, bf16[4,256,1024]{2,1,0:T(8,128)(2,1)S(1)}, u32[]{:S(2)}, u32[]{:S(2)}) collective-permute-start(bf16[4,256,1024]{2,1,0:T(8,128)(2,1)} %copy-done.26), channel_id=1, source_target_pairs={{0,4},{4,0},{8,12},{12,8},{16,20},{20,16},{24,28},{28,24},{1,5},{5... | collective-permute-start | bytes 6291464 | tf_op jit(solution)/shard_map/ppermute | solution.py:735
  224.6 24.3 %collective-permute-start.19 = (bf16[128,2048]{1,0:T(8,128)(2,1)S(1)}, bf16[128,2048]{1,0:T(8,128)(2,1)S(1)}, u32[]{:S(2)}, u32[]{:S(2)}) collective-permute-start(bf16[128,2048]{1,0:T(8,128)(2,1)S(1)} %add_convert_fusion.31), channel_id=1, source_target_pairs={{0,2},{1,3},{2,0},{3,1},{4,6},{5,7},{6,4},{7,5},{8,10},{9,11},{10,... | collective-permute-start | bytes 1572872 | tf_op jit(solution)/shard_map/ppermute | solution.py:735
  251.7 17.8 %collective-permute-start.18 = (bf16[128,2048]{1,0:T(8,128)(2,1)S(1)}, bf16[128,2048]{1,0:T(8,128)(2,1)S(1)}, u32[]{:S(2)}, u32[]{:S(2)}) collective-permute-start(bf16[128,2048]{1,0:T(8,128)(2,1)S(1)} %get-tuple-element.203), channel_id=1, source_target_pairs={{0,2},{1,3},{2,0},{3,1},{4,6},{5,7},{6,4},{7,5},{8,10},{9,11},{10,... | collective-permute-start | bytes 1572872 | tf_op jit(solution)/shard_map/ppermute | solution.py:735
  253.2 16.3 %collective-permute-start.20 = (bf16[128,2048]{1,0:T(8,128)(2,1)S(1)}, bf16[128,2048]{1,0:T(8,128)(2,1)S(1)}, u32[]{:S(2)}, u32[]{:S(2)}) collective-permute-start(bf16[128,2048]{1,0:T(8,128)(2,1)S(1)} %get-tuple-element.202), channel_id=1, source_target_pairs={{0,8},{4,12},{8,0},{12,4},{16,24},{20,28},{24,16},{28,20},{1,9},{5... | collective-permute-start | bytes 1572872 | tf_op jit(solution)/shard_map/ppermute | solution.py:735
  272.0 13.4 %collective-permute-start.21 = (bf16[128,2048]{1,0:T(8,128)(2,1)S(1)}, bf16[128,2048]{1,0:T(8,128)(2,1)S(1)}, u32[]{:S(2)}, u32[]{:S(2)}) collective-permute-start(bf16[128,2048]{1,0:T(8,128)(2,1)S(1)} %get-tuple-element.184), channel_id=1, source_target_pairs={{0,2},{1,3},{2,0},{3,1},{4,6},{5,7},{6,4},{7,5},{8,10},{9,11},{10,... | collective-permute-start | bytes 1572872 | tf_op jit(solution)/shard_map/ppermute | solution.py:735
  285.6 48.7 %collective-permute-start.23 = (bf16[4,256,1024]{2,1,0:T(8,128)(2,1)}, bf16[4,256,1024]{2,1,0:T(8,128)(2,1)S(1)}, u32[]{:S(2)}, u32[]{:S(2)}) collective-permute-start(bf16[4,256,1024]{2,1,0:T(8,128)(2,1)} %get-tuple-element.124), channel_id=1, source_target_pairs={{0,4},{4,0},{8,12},{12,8},{16,20},{20,16},{24,28},{28,24},{1,5},{5... | collective-permute-start | bytes 6291464 | tf_op jit(solution)/shard_map/ppermute | solution.py:735
  311.1 45.7 %collective-permute-start.24 = (bf16[2048,256]{1,0:T(8,128)(2,1)}, bf16[2048,256]{1,0:T(8,128)(2,1)}, u32[]{:S(2)}, u32[]{:S(2)}) collective-permute-start(bf16[2048,256]{1,0:T(8,128)(2,1)} %get-tuple-element.130), channel_id=1, source_target_pairs={{0,4},{4,0},{8,12},{12,8},{16,20},{20,16},{24,28},{28,24},{1,5},{5... | collective-permute-start | bytes 3145736 | tf_op jit(solution)/shard_map/ppermute | solution.py:735
  332.5 46.2 %collective-permute-start.31 = (bf16[2048,256]{1,0:T(8,128)(2,1)}, bf16[2048,256]{1,0:T(8,128)(2,1)S(1)}, u32[]{:S(2)}, u32[]{:S(2)}) collective-permute-start(bf16[2048,256]{1,0:T(8,128)(2,1)} %get-tuple-element.137), channel_id=1, source_target_pairs={{0,4},{4,0},{8,12},{12,8},{16,20},{20,16},{24,28},{28,24},{1,5},{5... | collective-permute-start | bytes 3145736 | tf_op jit(solution)/shard_map/ppermute | solution.py:735
  378.8 14.8 %collective-permute-start.32 = (bf16[1024,256]{1,0:T(8,128)(2,1)S(1)}, bf16[1024,256]{1,0:T(8,128)(2,1)S(1)}, u32[]{:S(2)}, u32[]{:S(2)}) collective-permute-start(bf16[1024,256]{1,0:T(8,128)(2,1)S(1)} %get-tuple-element.218), channel_id=1, source_target_pairs={{0,8},{4,12},{8,0},{12,4},{16,24},{20,28},{24,16},{28,20},{1,9},{5... | collective-permute-start | bytes 1572872 | tf_op jit(solution)/shard_map/ppermute | solution.py:735
  380.3 23.2 %collective-permute-start.34 = (bf16[1024,256]{1,0:T(8,128)(2,1)S(1)}, bf16[1024,256]{1,0:T(8,128)(2,1)S(1)}, u32[]{:S(2)}, u32[]{:S(2)}) collective-permute-start(bf16[1024,256]{1,0:T(8,128)(2,1)S(1)} %get-tuple-element.216), channel_id=1, source_target_pairs={{0,8},{4,12},{8,0},{12,4},{16,24},{20,28},{24,16},{28,20},{1,9},{5... | collective-permute-start | bytes 1572872 | tf_op jit(solution)/shard_map/ppermute | solution.py:735
  403.6 42.5 %collective-permute-start.35 = (bf16[512,256]{1,0:T(8,128)(2,1)S(1)}, bf16[512,256]{1,0:T(8,128)(2,1)S(1)}, u32[]{:S(2)}, u32[]{:S(2)}) collective-permute-start(bf16[512,256]{1,0:T(8,128)(2,1)S(1)} %get-tuple-element.222), channel_id=1, source_target_pairs={{0,16},{4,20},{8,24},{12,28},{16,0},{20,4},{24,8},{28,12},{1,17},{... | collective-permute-start | bytes 786440 | tf_op jit(solution)/shard_map/ppermute | solution.py:735
  404.4 47.3 %collective-permute-start.33 = (bf16[512,256]{1,0:T(8,128)(2,1)S(1)}, bf16[512,256]{1,0:T(8,128)(2,1)S(1)}, u32[]{:S(2)}, u32[]{:S(2)}) collective-permute-start(bf16[512,256]{1,0:T(8,128)(2,1)S(1)} %get-tuple-element.224), channel_id=1, source_target_pairs={{0,16},{4,20},{8,24},{12,28},{16,0},{20,4},{24,8},{28,12},{1,17},{... | collective-permute-start | bytes 786440 | tf_op jit(solution)/shard_map/ppermute | solution.py:735
  406.8 90.0 %collective-permute-start.56 = (bf16[2,256,1024]{2,1,0:T(8,128)(2,1)}, bf16[2,256,1024]{2,1,0:T(8,128)(2,1)}, u32[]{:S(2)}, u32[]{:S(2)}) collective-permute-start(bf16[2,256,1024]{2,1,0:T(8,128)(2,1)} %get-tuple-element.192), channel_id=1, source_target_pairs={{0,16},{4,20},{8,24},{12,28},{16,0},{20,4},{24,8},{28,12},{1,17},{... | collective-permute-start | bytes 3145736 | tf_op jit(solution)/shard_map/ppermute | solution.py:735
  407.4 123.5 %collective-permute-start.36 = (bf16[4,256,1024]{2,1,0:T(8,128)(2,1)}, bf16[4,256,1024]{2,1,0:T(8,128)(2,1)}, u32[]{:S(2)}, u32[]{:S(2)}) collective-permute-start(bf16[4,256,1024]{2,1,0:T(8,128)(2,1)} %get-tuple-element.148), channel_id=1, source_target_pairs={{0,4},{4,0},{8,12},{12,8},{16,20},{20,16},{24,28},{28,24},{1,5},{5... | collective-permute-start | bytes 6291464 | tf_op jit(solution)/shard_map/ppermute | solution.py:735
  456.5 41.8 %collective-permute-start.37 = (bf16[256,2048]{1,0:T(8,128)(2,1)}, bf16[256,2048]{1,0:T(8,128)(2,1)}, u32[]{:S(2)}, u32[]{:S(2)}) collective-permute-start(bf16[256,2048]{1,0:T(8,128)(2,1)} %get-tuple-element.152), channel_id=1, source_target_pairs={{0,1},{1,0},{2,3},{3,2},{4,5},{5,4},{6,7},{7,6},{8,9},{9,8},{10,11... | collective-permute-start | bytes 3145736 | tf_op jit(solution)/shard_map/ppermute | solution.py:735
  456.5 98.5 %collective-permute-start.52 = (bf16[2,256,1024]{2,1,0:T(8,128)(2,1)}, bf16[2,256,1024]{2,1,0:T(8,128)(2,1)}, u32[]{:S(2)}, u32[]{:S(2)}) collective-permute-start(bf16[2,256,1024]{2,1,0:T(8,128)(2,1)} %get-tuple-element.196), channel_id=1, source_target_pairs={{0,16},{4,20},{8,24},{12,28},{16,0},{20,4},{24,8},{28,12},{1,17},{... | collective-permute-start | bytes 3145736 | tf_op jit(solution)/shard_map/ppermute | solution.py:735
  456.5 85.6 %collective-permute-start.25 = (bf16[512,2048]{1,0:T(8,128)(2,1)}, bf16[512,2048]{1,0:T(8,128)(2,1)}, u32[]{:S(2)}, u32[]{:S(2)}) collective-permute-start(bf16[512,2048]{1,0:T(8,128)(2,1)} %copy-done.25), channel_id=1, source_target_pairs={{0,1},{1,0},{2,3},{3,2},{4,5},{5,4},{6,7},{7,6},{8,9},{9,8},{10,11... | collective-permute-start | bytes 6291464 | tf_op jit(solution)/shard_map/ppermute | solution.py:735
  498.2 31.4 %collective-permute-start.57 = (bf16[256,1024]{1,0:T(8,128)(2,1)S(1)}, bf16[256,1024]{1,0:T(8,128)(2,1)S(1)}, u32[]{:S(2)}, u32[]{:S(2)}) collective-permute-start(bf16[256,1024]{1,0:T(8,128)(2,1)S(1)} %fusion.16), channel_id=1, source_target_pairs={{0,8},{4,12},{8,0},{12,4},{16,24},{20,28},{24,16},{28,20},{1,9},{5... | collective-permute-start | bytes 1572872 | tf_op jit(solution)/shard_map/ppermute | solution.py:735
  499.9 34.9 %collective-permute-start.38 = (bf16[128,2048]{1,0:T(8,128)(2,1)S(1)}, bf16[128,2048]{1,0:T(8,128)(2,1)S(1)}, u32[]{:S(2)}, u32[]{:S(2)}) collective-permute-start(bf16[128,2048]{1,0:T(8,128)(2,1)S(1)} %get-tuple-element.214), channel_id=1, source_target_pairs={{0,2},{1,3},{2,0},{3,1},{4,6},{5,7},{6,4},{7,5},{8,10},{9,11},{10,... | collective-permute-start | bytes 1572872 | tf_op jit(solution)/shard_map/ppermute | solution.py:735
  541.3 78.4 %collective-permute-start.54 = (bf16[2,256,1024]{2,1,0:T(8,128)(2,1)}, bf16[2,256,1024]{2,1,0:T(8,128)(2,1)}, u32[]{:S(2)}, u32[]{:S(2)}) collective-permute-start(bf16[2,256,1024]{2,1,0:T(8,128)(2,1)} %get-tuple-element.194), channel_id=1, source_target_pairs={{0,16},{4,20},{8,24},{12,28},{16,0},{20,4},{24,8},{28,12},{1,17},{... | collective-permute-start | bytes 3145736 | tf_op jit(solution)/shard_map/ppermute | solution.py:735
  544.7 45.6 %collective-permute-start.27 = (bf16[128,2048]{1,0:T(8,128)(2,1)}, bf16[128,2048]{1,0:T(8,128)(2,1)}, u32[]{:S(2)}, u32[]{:S(2)}) collective-permute-start(bf16[128,2048]{1,0:T(8,128)(2,1)} %get-tuple-element.201), channel_id=1, source_target_pairs={{0,2},{1,3},{2,0},{3,1},{4,6},{5,7},{6,4},{7,5},{8,10},{9,11},{10,... | collective-permute-start | bytes 1572872 | tf_op jit(solution)/shard_map/ppermute | solution.py:735
  546.1 60.7 %collective-permute-start.26 = (bf16[128,2048]{1,0:T(8,128)(2,1)}, bf16[128,2048]{1,0:T(8,128)(2,1)}, u32[]{:S(2)}, u32[]{:S(2)}) collective-permute-start(bf16[128,2048]{1,0:T(8,128)(2,1)} %get-tuple-element.200), channel_id=1, source_target_pairs={{0,2},{1,3},{2,0},{3,1},{4,6},{5,7},{6,4},{7,5},{8,10},{9,11},{10,... | collective-permute-start | bytes 1572872 | tf_op jit(solution)/shard_map/ppermute | solution.py:735
  550.6 14.8 %collective-permute-start.44 = (f32[2,2048]{1,0:T(2,128)S(1)}, f32[2,2048]{1,0:T(2,128)S(1)}, u32[]{:S(2)}, u32[]{:S(2)}) collective-permute-start(f32[2,2048]{1,0:T(2,128)S(1)} %add.346), channel_id=1, source_target_pairs={{0,8},{4,12},{8,0},{12,4},{16,24},{20,28},{24,16},{28,20},{1,9},{5... | collective-permute-start | bytes 49160 | tf_op jit(solution)/shard_map/ppermute | solution.py:735
  555.1 39.5 %collective-permute-start.39 = (bf16[128,2048]{1,0:T(8,128)(2,1)}, bf16[128,2048]{1,0:T(8,128)(2,1)}, u32[]{:S(2)}, u32[]{:S(2)}) collective-permute-start(bf16[128,2048]{1,0:T(8,128)(2,1)} %get-tuple-element.181), channel_id=1, source_target_pairs={{0,2},{1,3},{2,0},{3,1},{4,6},{5,7},{6,4},{7,5},{8,10},{9,11},{10,... | collective-permute-start | bytes 1572872 | tf_op jit(solution)/shard_map/ppermute | solution.py:735
  565.4 24.8 %collective-permute-start.45 = (f32[2,2048]{1,0:T(2,128)S(1)}, f32[2,2048]{1,0:T(2,128)S(1)}, u32[]{:S(2)}, u32[]{:S(2)}) collective-permute-start(f32[2,2048]{1,0:T(2,128)S(1)} %add.347), channel_id=1, source_target_pairs={{0,16},{4,20},{8,24},{12,28},{16,0},{20,4},{24,8},{28,12},{1,17},{... | collective-permute-start | bytes 49160 | tf_op jit(solution)/shard_map/ppermute | solution.py:735
  590.2 15.1 %collective-permute-start.53 = (bf16[256,1024]{1,0:T(8,128)(2,1)}, bf16[256,1024]{1,0:T(8,128)(2,1)}, u32[]{:S(2)}, u32[]{:S(2)}) collective-permute-start(bf16[256,1024]{1,0:T(8,128)(2,1)} %fusion.12), channel_id=1, source_target_pairs={{0,8},{4,12},{8,0},{12,4},{16,24},{20,28},{24,16},{28,20},{1,9},{5... | collective-permute-start | bytes 1572872 | tf_op jit(solution)/shard_map/ppermute | solution.py:735
  591.9 23.6 %collective-permute-start.28 = (bf16[128,2048]{1,0:T(8,128)(2,1)S(1)}, bf16[128,2048]{1,0:T(8,128)(2,1)S(1)}, u32[]{:S(2)}, u32[]{:S(2)}) collective-permute-start(bf16[128,2048]{1,0:T(8,128)(2,1)S(1)} %add_convert_fusion.24), channel_id=1, source_target_pairs={{0,8},{4,12},{8,0},{12,4},{16,24},{20,28},{24,16},{28,20},{1,9},{5... | collective-permute-start | bytes 1572872 | tf_op jit(solution)/shard_map/ppermute | solution.py:735
  594.6 47.0 %collective-permute-start.46 = (bf16[4,256,1024]{2,1,0:T(8,128)(2,1)S(1)}, bf16[4,256,1024]{2,1,0:T(8,128)(2,1)S(1)}, u32[]{:S(2)}, u32[]{:S(2)}) collective-permute-start(bf16[4,256,1024]{2,1,0:T(8,128)(2,1)S(1)} %copy-done.24), channel_id=1, source_target_pairs={{0,4},{4,0},{8,12},{12,8},{16,20},{20,16},{24,28},{28,24},{1,5},{5... | collective-permute-start | bytes 6291464 | tf_op jit(solution)/shard_map/ppermute | solution.py:735
  605.3 37.9 %collective-permute-start.40 = (bf16[256,2048]{1,0:T(8,128)(2,1)S(1)}, bf16[256,2048]{1,0:T(8,128)(2,1)S(1)}, u32[]{:S(2)}, u32[]{:S(2)}) collective-permute-start(bf16[256,2048]{1,0:T(8,128)(2,1)S(1)} %pad_maximum_fusion.5), channel_id=1, source_target_pairs={{0,1},{1,0},{2,3},{3,2},{4,5},{5,4},{6,7},{7,6},{8,9},{9,8},{10,11... | collective-permute-start | bytes 3145736 | tf_op jit(solution)/shard_map/ppermute | solution.py:735
  617.5 13.1 %collective-permute-start.29 = (bf16[128,2048]{1,0:T(8,128)(2,1)S(1)}, bf16[128,2048]{1,0:T(8,128)(2,1)S(1)}, u32[]{:S(2)}, u32[]{:S(2)}) collective-permute-start(bf16[128,2048]{1,0:T(8,128)(2,1)S(1)} %get-tuple-element.183), channel_id=1, source_target_pairs={{0,2},{1,3},{2,0},{3,1},{4,6},{5,7},{6,4},{7,5},{8,10},{9,11},{10,... | collective-permute-start | bytes 1572872 | tf_op jit(solution)/shard_map/ppermute | solution.py:735
  630.7 13.0 %collective-permute-start.30 = (bf16[256,2048]{1,0:T(8,128)(2,1)S(1)}, bf16[256,2048]{1,0:T(8,128)(2,1)S(1)}, u32[]{:S(2)}, u32[]{:S(2)}) collective-permute-start(bf16[256,2048]{1,0:T(8,128)(2,1)S(1)} %pad_maximum_fusion.4), channel_id=1, source_target_pairs={{0,1},{1,0},{2,3},{3,2},{4,5},{5,4},{6,7},{7,6},{8,9},{9,8},{10,11... | collective-permute-start | bytes 3145736 | tf_op jit(solution)/shard_map/ppermute | solution.py:735
  642.6 23.7 %collective-permute-start.49 = (bf16[4,256,512]{2,1,0:T(8,128)(2,1)S(1)}, bf16[4,256,512]{2,1,0:T(8,128)(2,1)S(1)}, u32[]{:S(2)}, u32[]{:S(2)}) collective-permute-start(bf16[4,256,512]{2,1,0:T(8,128)(2,1)S(1)} %copy-done.32), channel_id=1, source_target_pairs={{0,4},{4,0},{8,12},{12,8},{16,20},{20,16},{24,28},{28,24},{1,5},{5... | collective-permute-start | bytes 3145736 | tf_op jit(solution)/shard_map/ppermute | solution.py:735
  643.3 24.1 %collective-permute-start.47 = (bf16[2,256,1024]{2,1,0:T(8,128)(2,1)S(1)}, bf16[2,256,1024]{2,1,0:T(8,128)(2,1)S(1)}, u32[]{:S(2)}, u32[]{:S(2)}) collective-permute-start(bf16[2,256,1024]{2,1,0:T(8,128)(2,1)S(1)} %get-tuple-element.199), channel_id=1, source_target_pairs={{0,8},{4,12},{8,0},{12,4},{16,24},{20,28},{24,16},{28,20},{1,9},{5... | collective-permute-start | bytes 3145736 | tf_op jit(solution)/shard_map/ppermute | solution.py:735
  666.7 22.2 %collective-permute-start.50 = (bf16[2,256,512]{2,1,0:T(8,128)(2,1)S(1)}, bf16[2,256,512]{2,1,0:T(8,128)(2,1)S(1)}, u32[]{:S(2)}, u32[]{:S(2)}) collective-permute-start(bf16[2,256,512]{2,1,0:T(8,128)(2,1)S(1)} %get-tuple-element.212), channel_id=1, source_target_pairs={{0,8},{4,12},{8,0},{12,4},{16,24},{20,28},{24,16},{28,20},{1,9},{5... | collective-permute-start | bytes 1572872 | tf_op jit(solution)/shard_map/ppermute | solution.py:735
  667.6 30.0 %collective-permute-start.48 = (bf16[1,256,1024]{2,1,0:T(8,128)(2,1)S(1)}, bf16[1,256,1024]{2,1,0:T(8,128)(2,1)S(1)}, u32[]{:S(2)}, u32[]{:S(2)}) collective-permute-start(bf16[1,256,1024]{2,1,0:T(8,128)(2,1)S(1)} %add_convert_fusion.16), channel_id=1, source_target_pairs={{0,16},{4,20},{8,24},{12,28},{16,0},{20,4},{24,8},{28,12},{1,17},{... | collective-permute-start | bytes 1572872 | tf_op jit(solution)/shard_map/ppermute | solution.py:735
  (104 other events, 1992.3 us)

commit v6 on v5

--- a/solution.py
+++ b/solution.py
@@ -19,6 +19,7 @@
 LOG2E = 1.4426950408889634
 NEG = -1e30
 SLOTS = 4
+VMEM_LIMIT = 60 << 20
 
 eps_norm = 1e-05
 rope_base = 1000000.0
@@ -356,8 +357,8 @@
             pltpu.VMEM((kv_heads, HEAD_SIZE, rep * BLOCK), jnp.float32),
             pltpu.SemaphoreType.DMA((ctx_count,)),
         ],
-        compiler_params=pltpu.CompilerParams(vmem_limit_bytes=40 << 20),
-        cost_estimate=cost(flops, 2 * tokens * parts[0].shape[1] + 4 * rows * model),
+        compiler_params=pltpu.CompilerParams(vmem_limit_bytes=VMEM_LIMIT),
+        cost_estimate=cost("attention_forward", flops, 2 * tokens * parts[0].shape[1] + 4 * rows * model),
         name="attention_forward",
     )(order, cont, where, q, w_out, *parts)
 
@@ -411,8 +412,8 @@
                 pltpu.SemaphoreType.DMA((ctx_count,)),
             ],
         ),
-        compiler_params=pltpu.CompilerParams(vmem_limit_bytes=56 << 20),
-        cost_estimate=cost(flops, 4 * tokens * wide + 2 * rows * model),
+        compiler_params=pltpu.CompilerParams(vmem_limit_bytes=VMEM_LIMIT),
+        cost_estimate=cost(f"attention_backward_{head}", flops, 4 * tokens * wide + 2 * rows * model),
         name=f"attention_backward_{head}",
     )(order, cont, where, q, grad_branch, w_out, mixed, lse, cosine, sine, *parts)
 
@@ -499,15 +500,19 @@
             pltpu.VMEM(a.shape, a.dtype) for a in (x, wq, wk, wv)
         ]
         + [pltpu.VMEM(table.shape, jnp.float32), pltpu.SemaphoreType.DMA((5,))],
-        compiler_params=pltpu.CompilerParams(vmem_limit_bytes=40 << 20),
-        cost_estimate=cost(flops, 4 * x.size + 2 * wq.size + 4 * wk.size),
+        compiler_params=pltpu.CompilerParams(vmem_limit_bytes=VMEM_LIMIT),
+        cost_estimate=cost("input_stage", flops, 4 * x.size + 2 * wq.size + 4 * wk.size),
         name="input_stage",
     )(order, cont, where, gain.reshape(1, -1), x, wq, wk, wv, table)
 
 
-def cost(flops, bytes_accessed):
+FILLERS = ("ffn_out", "up_shares", "branch_shares", "kv_shares", "grad_hidden")
+
+
+def cost(name, flops, bytes_accessed):
+    scale = 16.0 if name in FILLERS else 0.02
     return pl.CostEstimate(
-        flops=int(flops), bytes_accessed=int(bytes_accessed), transcendentals=0
+        flops=int(flops * scale), bytes_accessed=int(bytes_accessed * scale), transcendentals=0
     )
 
 
@@ -552,8 +557,8 @@
             ],
             out_specs=pl.BlockSpec((rows, block), lambda i, w: (0, i)),
         ),
-        compiler_params=pltpu.CompilerParams(vmem_limit_bytes=32 << 20),
-        cost_estimate=cost(2 * rows * model * units, 4 * rows * model),
+        compiler_params=pltpu.CompilerParams(vmem_limit_bytes=VMEM_LIMIT),
+        cost_estimate=cost("grad_hidden", 2 * rows * model * units, 4 * rows * model),
         name="grad_hidden",
     )(where, cot, w_down)
 
@@ -593,8 +598,8 @@
             ],
             out_specs=[unit_spec] * 3,
         ),
-        compiler_params=pltpu.CompilerParams(vmem_limit_bytes=44 << 20),
-        cost_estimate=cost(4 * rows * model * units, 6 * rows * model),
+        compiler_params=pltpu.CompilerParams(vmem_limit_bytes=VMEM_LIMIT),
+        cost_estimate=cost("ffn_stage", 4 * rows * model * units, 6 * rows * model),
         name="ffn_stage",
     )(where, second, grad_hidden, w_gate, w_up)
 
@@ -633,8 +638,8 @@
             in_specs=[left_spec] * len(lefts) + [right_spec] * len(rights),
             out_specs=[half_spec, half_spec],
         ),
-        compiler_params=pltpu.CompilerParams(vmem_limit_bytes=32 << 20),
-        cost_estimate=cost(2 * len(lefts) * rows * units * model, 4 * rows * model),
+        compiler_params=pltpu.CompilerParams(vmem_limit_bytes=VMEM_LIMIT),
+        cost_estimate=cost(name, 2 * len(lefts) * rows * units * model, 4 * rows * model),
         name=name,
     )(where, *lefts, *rights)
 
@@ -673,8 +678,8 @@
             ],
             out_specs=[share_spec, share_spec],
         ),
-        compiler_params=pltpu.CompilerParams(vmem_limit_bytes=36 << 20),
-        cost_estimate=cost(2 * rows * model * width, 4 * rows * model),
+        compiler_params=pltpu.CompilerParams(vmem_limit_bytes=VMEM_LIMIT),
+        cost_estimate=cost(name, 2 * rows * model * width, 4 * rows * model),
         name=name,
     )(where, *lefts, *rights)
 
@@ -723,9 +728,8 @@
         in_specs=[pl.BlockSpec(memory_space=pltpu.SMEM)]
         + [vmem] * (len(flat) + 2 + kv_heads + 3),
         out_specs=[vmem] * 3,
-        compiler_params=pltpu.CompilerParams(vmem_limit_bytes=32 << 20),
-        cost_estimate=cost(
-            2 * rows * model * (wq.shape[1] + 2 * wk.shape[1]), 4 * rows * model + 4 * wq.size
+        compiler_params=pltpu.CompilerParams(vmem_limit_bytes=VMEM_LIMIT),
+        cost_estimate=cost("tail_stage", 2 * rows * model * (wq.shape[1] + 2 * wk.shape[1]), 4 * rows * model + 4 * wq.size
         ),
         name="tail_stage",
     )(where, *flat, cosine, sine, *grad_queries, wq, wk, wv)
@@ -763,9 +767,9 @@
     return jnp.concatenate([near, flip(near, "tp", 1)])
 
 
-def gather_rows(own, tensor):
+def gather_rows(own, other, tensor):
     rows = own.shape[0]
-    near = jnp.concatenate([own, flip(own, "tp", 2)])
+    near = jnp.concatenate([own, other])
     far = flip(near, "tp", 1)
     pieces = (near[:rows], near[rows:], far[:rows], far[rows:])
     result = jnp.zeros((SLOTS * rows,) + own.shape[1:], own.dtype)
@@ -776,19 +780,25 @@
     return result
 
 
-def scatter_slots(keep, send):
-    got = flip(send, "tp", 1)
+def scatter_slots(keep, send, fill=lambda value: value):
+    got = fill(flip(send, "tp", 1))
     quarter = keep.shape[0] // 2
     far = flip(add(keep[quarter:], got[quarter:]), "tp", 2)
     return add(keep[:quarter], got[:quarter]), far
 
 
-def pair_scatter(keep, send):
-    got = flip(send, "tp", 1)
+def pair_scatter(keep, send, fill=lambda near: near):
+    got = fill(flip(send, "tp", 1))
     n = keep.shape[0] // 4
-    near = [add(keep[k * n : (k + 1) * n], got[k * n : (k + 1) * n]) for k in (3, 1, 2, 0)]
-    away = flip(add(near[1], flip(near[0], "tp", 2)), "ctx", 2)
-    return near[3], flip(near[2], "tp", 2), away
+    near = [add(keep[k * n : (k + 1) * n], got[k * n : (k + 1) * n]) for k in range(4)]
+    far = flip(near[3], "tp", 2)
+    got = flip(near[2], "tp", 2)
+    return near, far, got
+
+
+def pair_finish(near, far, got):
+    away = add(near[1], far)
+    return near[0], got, flip(away, "ctx", 2), away
 
 
 def total(terms):
@@ -840,16 +850,20 @@
     return masks
 
 
-def both_halves(reduce, ctx, axis, dep=None):
-    keep, got = reduce.keep, reduce.got
-    if dep is not None:
-        keep, got = after(dep, keep, got)
+def split_halves(reduce, ctx, dep):
+    keep, got = after(dep, reduce.keep, reduce.got)
     pair = lax.div(ctx, 2) % 2
     pick = lambda value, index: lax.dynamic_slice_in_dim(value, index, 1, 0)[0]
-    other = flip(add(pick(keep, 1 - pair), pick(got, 1 - pair)), "ctx", 2)
-    own = add(pick(keep, pair), pick(got, pair))
+    return (
+        add(pick(keep, pair), pick(got, pair)),
+        add(pick(keep, 1 - pair), pick(got, 1 - pair)),
+    )
+
+
+def join_halves(own, other, ctx):
+    pair = lax.div(ctx, 2) % 2
     low, high = jnp.where(pair == 0, own, other), jnp.where(pair == 0, other, own)
-    return jnp.concatenate([low, high], axis=axis).astype(jnp.float32)
+    return jnp.concatenate([low, high], axis=1).astype(jnp.float32)
 
 
 class KvReduce:
@@ -897,22 +911,37 @@
     )
     cot_own = lax.dynamic_slice_in_dim(cotangent, tensor * quarter, quarter)
     cot_slots = slots_of(cotangent, tensor)
-    cot_part = flip(cot_own, "ctx", 2)
-    parts = gather_keys(after(cot_part, kv_local), ctx_count)
+    parts = {0: kv_local}
+    for bit in reversed(highs):
+        for mask in list(parts):
+            parts[mask + bit] = flip(parts[mask], "ctx", bit)
+    near_part = flip(kv_local, "ctx", 2)
+    parts[1] = flip(kv_local, "ctx", 1)
+    cot_part = flip(after(near_part, cot_own), "ctx", 2)
+    for mask in [m for m in parts if m >= 4]:
+        parts[mask + 2] = flip(parts[mask], "ctx", 2)
+        parts[mask + 1] = flip(parts[mask], "ctx", 1)
+    parts[2] = near_part
+    parts[3] = flip(near_part, "ctx", 1)
+    for mask in [m for m in list(parts) if m > 4 and m % 4 == 2]:
+        parts[mask + 1] = flip(parts[mask], "ctx", 1)
+    parts = [parts[mask] for mask in range(ctx_count)]
     cot_part = jnp.concatenate([cot_part, flip(cot_part, "tp", 2)])
     cot_far = flip(cot_part, "tp", 1)
     cot = jnp.concatenate(
         [cot_slots[0], cot_part[:quarter], cot_slots[1], cot_part[quarter:]]
         + [cot_slots[2], cot_far[:quarter], cot_slots[3], cot_far[quarter:]]
     )
-    grad_hidden = grad_hidden_stage(cot, w_down, where)
-
     mixed, log_total, keep, send = attention_forward(
-        after(grad_hidden, queries), w_out, parts, block_order, cont_prompt, where
-    )
+        queries, w_out, parts, block_order, cont_prompt, where
+    )
+    first_half = flip(send, "tp", 1)
+    near = add(keep, first_half)
+    far = flip(near[quarter:], "tp", 2)
+    grad_hidden = grad_hidden_stage(after(near, cot), w_down, where)
     own_input = lax.dynamic_slice_in_dim(layer_input, tensor * quarter, quarter)
     own_input = own_input.astype(jnp.float32)
-    middle = own_input + total(scatter_slots(keep, send))
+    middle = own_input + total((near[:quarter], after(grad_hidden, far)))
     inv_two = lax.rsqrt(jnp.mean(middle * middle, axis=-1, keepdims=True) + eps_norm)
     normed_two = middle * inv_two
     second = gather_pair((normed_two * ffn_gain).astype(jnp.bfloat16))
@@ -923,22 +952,22 @@
     )
     down = Reduce(*down_shares)
     grad_gate, grad_up = after(down_shares[0], grad_gate, grad_up)
-    partial = unit_sum(
+    keep, send = unit_sum(
         grad_second_kernel, "grad_second", (grad_gate, grad_up), (w_gate, w_up), True, where
     )
-    second_terms = pair_scatter(*partial)
+    ffn_halves = unit_sum(
+        ffn_out_kernel, "ffn_out", (after(keep, hidden),), (w_down,), False, where
+    )
+    near, far, got = pair_scatter(keep, send, lambda value: after(ffn_halves[0], value))
 
     def unit_shares(name, grad, dep):
         return weight_shares(
             name, (second,), (after(dep, grad),), ((0, 0),), ctx_count, False, where
         )
 
-    gate_shares = unit_shares("gate_shares", grad_gate, partial[0])
-    up_shares = unit_shares("up_shares", grad_up, gate_shares[0])
-    ffn_halves = unit_sum(
-        ffn_out_kernel, "ffn_out", (after(up_shares[0], hidden),), (w_down,), False, where
-    )
-    dep = ffn_halves[0]
+    gate_shares = unit_shares("gate_shares", grad_gate, near[3])
+    second_terms = pair_finish(near, after(gate_shares[0], far), got)
+    *second_terms, dep = second_terms
     for mask in highs:
         down.halve(mask, ctx, dep)
         dep = down.keep
@@ -947,8 +976,11 @@
         total(after(dep, *second_terms)), normed_two, inv_two, ffn_gain
     )
     grad_middle = cot_own.astype(jnp.float32) + grad_norm_two
-    grad_branch = gather_slots(grad_middle.astype(jnp.bfloat16))
-    backward, kv = [], []
+    own_branch = grad_middle.astype(jnp.bfloat16)
+    up_shares = unit_shares("up_shares", grad_up, own_branch)
+    branch_near = jnp.concatenate([own_branch, after(up_shares[0], flip(own_branch, "tp", 2))])
+    grad_branch = jnp.concatenate([branch_near, flip(branch_near, "tp", 1)])
+    backward = []
     held = grad_branch
     for head in range(kv_heads):
         backward.append(
@@ -958,59 +990,75 @@
             )
         )
         held = after(backward[-1][0], grad_branch)
-        kv.append(KvReduce(*backward[-1][1:]))
     grad_queries = [item[0] for item in backward]
     dep = grad_queries[-1]
     for mask in highs:
         gate.halve(mask, ctx, dep)
         dep = gate.keep
+    kv = [KvReduce(*item[1:]) for item in backward]
+    down_own, down_away = split_halves(down, ctx, dep)
+    down_other = flip(down_away, "ctx", 2)
     branch_shares = weight_shares(
         "branch_shares",
         (first_input, grad_branch),
-        grad_queries + [after(dep, mixed)],
+        grad_queries + [after(down_own, mixed)],
         tuple((0, h) for h in range(kv_heads)) + ((1, kv_heads),),
         ctx_count,
         True,
         where,
     )
-    kv[0].halve(2, branch_shares[0])
-    ffn_terms = pair_scatter(*after(kv[0].keep, *ffn_halves))
-    for item in kv[1:]:
-        item.halve(2, kv[0].keep)
-    up = Reduce(*after(kv[-1].keep, *up_shares))
+    dep = branch_shares[0]
+    gate_own, gate_away = split_halves(gate, ctx, dep)
+    dep = gate_own
+    for item in kv:
+        item.halve(2, dep)
+        dep = item.keep
+    up = Reduce(*after(dep, *up_shares))
+    ffn_sums = pair_scatter(*after(dep, *ffn_halves))
+    dep = ffn_sums[0][3]
     for mask in highs:
         for item in kv:
-            item.halve(mask, kv[-1].keep)
-    sum_down = both_halves(down, ctx, 1, kv[0].keep).T
-    keep, send, grad_kv = tail_stage(
-        [(item.keep, item.got) for item in kv], cosine, sine, grad_queries,
-        w_query, key_matrix, value_matrix, where,
-    )
-    first_terms = scatter_slots(keep, send)
-    kv_shares = weight_shares(
-        "kv_shares", (first_input,), (grad_kv,), ((0, 0),), ctx_count, True, where
-    )
-    dep = kv_shares[0]
+            item.halve(mask, dep)
+            dep = item.keep
+    ffn_terms = pair_finish(ffn_sums[0], *after(dep, *ffn_sums[1:]))
+    got = [after(ffn_terms[3], item.got) for item in kv]
     for mask in highs:
-        up.halve(mask, ctx, dep)
+        up.halve(mask, ctx, got[-1])
         dep = up.keep
     branch = Reduce(*after(dep, *branch_shares))
+    output = (middle + total(after(dep, *ffn_terms[:3]))).astype(jnp.bfloat16)
+    keep, send, grad_kv = tail_stage(
+        [(item.keep, after(dep, value)) for item, value in zip(kv, got)], cosine, sine,
+        grad_queries, w_query, key_matrix, value_matrix, where,
+    )
+    kv_shares = weight_shares(
+        "kv_shares", (first_input,), (after(keep, grad_kv),), ((0, 0),), ctx_count, True, where
+    )
+    first_terms = scatter_slots(keep, send, lambda value: after(kv_shares[0], value))
     inv_one = lax.rsqrt(jnp.mean(own_input * own_input, axis=-1, keepdims=True) + eps_norm)
     grad_norm_one, attn_gain_part = norm_back(
-        total(after(dep, *first_terms)), own_input * inv_one, inv_one, attn_gain
+        total(first_terms), own_input * inv_one, inv_one, attn_gain
     )
     grad_input = (grad_middle + grad_norm_one).astype(jnp.bfloat16)
-    output = gather_rows((middle + total(ffn_terms)).astype(jnp.bfloat16), tensor)
-    sum_gate = both_halves(gate, ctx, 1, grad_input)
-    grad_input = gather_rows(grad_input, tensor)
-    gains = all_sum(jnp.stack([attn_gain_part, ffn_gain_part]), ctx_count)
-    branch.halve(2, ctx)
+    input_other = flip(grad_input, "tp", 2)
+    branch.halve(2, ctx, grad_input)
     last = Reduce(*after(branch.keep, *kv_shares))
+    up_own, up_away = split_halves(up, ctx, branch.keep)
+    dep = up_own
+    grad_input = gather_rows(grad_input, after(dep, input_other), tensor)
+    gate_other = flip(after(dep, gate_away), "ctx", 2)
+    gains = all_sum(after(dep, jnp.stack([attn_gain_part, ffn_gain_part])), ctx_count)
+    output = gather_rows(output, flip(after(dep, output), "tp", 2), tensor)
+    sum_down = join_halves(down_own, down_other, ctx).T
+    up_other = flip(after(gains, up_away), "ctx", 2)
     for mask in highs:
-        branch.halve(mask, ctx)
-    sum_up = both_halves(up, ctx, 1)
-    for mask in [2] + highs:
+        branch.halve(mask, ctx, gains)
+    last.halve(2, ctx, branch.keep)
+    for mask in highs:
         last.halve(mask, ctx)
+    sum_gate = join_halves(gate_own, gate_other, ctx)
+    sum_up = join_halves(up_own, up_other, ctx)
+    branch.keep, branch.got = after(last.keep, branch.keep, branch.got)
     width_q, width_k = w_query.shape[1], key_matrix.shape[1]
     branch_sum, last_sum = branch.sum(), last.sum()
     sum_query, sum_out = branch_sum[:, :width_q], branch_sum[:, width_q:].T

time: 714 us -> 641 us (0.90)
  waiting for transfers between devices: 392 us -> 288 us
  local copies, waits for them, and re-layouts: 55.2 us -> 23.5 us
  Pallas kernels: 153 us -> 183 us
  starting transfers between devices: 49.6 us -> 66.3 us
  other arithmetic: 53 us -> 66.6 us
    ppermute x58, waiting for transfers between devices: 392 us -> 288 us  [flip(): lax.ppermute(value, axis, [(i, i ^ mask) for i in range(lax.axis_size(axi...]
    unnamed x200 -> x102, local copies, waits for them, and re-layouts: 48.9 us -> 17 us
    pallas_call x5, Pallas kernels: 34.4 us -> 53 us  [weight_shares(): pl.pallas_call(functools.partial(shares_kernel, len(lefts), swap_bits, pa...]
    ppermute x58, starting transfers between devices: 49.6 us -> 66.3 us  [flip(): lax.ppermute(value, axis, [(i, i ^ mask) for i in range(lax.axis_size(axi...]
    convert_element_type x20, other arithmetic: 29 us -> 38.7 us  [add(): (left.astype(jnp.float32) + right.astype(jnp.float32)).astype(jnp.bfloat16)]
  transfers between devices with their start and end apart: 58 -> 58, of which waited for: 35 -> 32; matrix products, arithmetic and copies ran while one was open for 9% -> 12% of each run, Pallas kernels for 13% -> 21%
where the time goes in v6:
time: 641 us; the launch traced here: 629 us
  waiting for transfers between devices  288 us (45%)
  Pallas kernels  183 us (29%)
  other arithmetic  66.6 us (10%)
  starting transfers between devices  66.3 us (10%)
  local copies, waits for them, and re-layouts  23.5 us (4%)
    ppermute x58, waiting for transfers between devices, flip(): lax.ppermute(value, axis, [(i, i ^ mask) for i in range(lax.axis_size(axi...  288 us
    ppermute x58, starting transfers between devices, flip(): lax.ppermute(value, axis, [(i, i ^ mask) for i in range(lax.axis_size(axi...  66.3 us
    pallas_call x5, Pallas kernels, weight_shares(): pl.pallas_call(functools.partial(shares_kernel, len(lefts), swap_bits, pa...  53 us
    pallas_call x2, Pallas kernels, attention_backward(): pl.pallas_call(functools.partial(backward_kernel, rep, 1, ctx_count, head...  39.5 us
    convert_element_type x20, other arithmetic, add(): (left.astype(jnp.float32) + right.astype(jnp.float32)).astype(jnp.bfloat16)  38.7 us
    pallas_call x1, Pallas kernels, attention_forward(): pl.pallas_call(functools.partial(forward_kernel, rep, kv_heads, ctx_count...  27.8 us
    pallas_call x2, Pallas kernels, unit_sum(): pl.pallas_call(kernel, out_shape=(half, half), grid_spec=pltpu.PrefetchSc...  23 us
    unnamed x102, local copies, waits for them, and re-layouts  17 us
  transfers between devices with their start and end apart: 58, of which 32 were waited for; matrix products, arithmetic and copies ran while one was open for 12% of the time, Pallas kernels for 21%

profile of v6, /device:TPU:0, one launch (start us, length us, event | category | flops | bytes accessed | tf_op | source)
XLA Modules:
  0.0 629.0 jit_solution(7122247980155282851)
XLA Ops:
  1.3 7.2 %input_stage.1 = (bf16[512,2048]{1,0:T(8,128)(2,1)}, bf16[512,512]{1,0:T(8,128)(2,1)}, bf16[512,512]{1,0:T(8,128)(2,1)}, f32[512,128]{1,0:T(8,128)}, f32[512,128]{1,0:T(8,128)}) custom-call(s32[32]{0:T(128)} %order_ref.7, s32[8]{0:T(128)} %cont_ref.7, s32[2]{0:T(128)} %pad_add_fusion.where_ref, f32[1,2048]{1,0:T(1,128)} %bitcast.30, ...), custom_call_target="tpu_custom_call" | custom-call | flops 42949672 | bytes 167772 | tf_op jit(solution)/shard_map/input_stage/pallas_call | solution.py:488
  8.5 4.1 collective-permute-start.3
  14.2 21.9 %collective-permute-done.3.refs_4_ = bf16[512,512]{1,0:T(8,128)(2,1)S(1)} collective-permute-done((bf16[512,512]{1,0:T(8,128)(2,1)}, bf16[512,512]{1,0:T(8,128)(2,1)S(1)}, u32[]{:S(2)}, u32[]{:S(2)}) %collective-permute-start.3) | collective-permute-done | bytes 524320 | tf_op jit(solution)/shard_map/ppermute | solution.py:739
  43.8 7.2 %collective-permute-done.5.refs_6_ = bf16[512,512]{1,0:T(8,128)(2,1)S(1)} collective-permute-done((bf16[512,512]{1,0:T(8,128)(2,1)S(1)}, bf16[512,512]{1,0:T(8,128)(2,1)S(1)}, u32[]{:S(2)}, u32[]{:S(2)}) %collective-permute-start.5) | collective-permute-done | bytes 524320 | tf_op jit(solution)/shard_map/ppermute | solution.py:739
  52.5 8.0 %collective-permute-done.8 = bf16[128,2048]{1,0:T(8,128)(2,1)} collective-permute-done((bf16[128,2048]{1,0:T(8,128)(2,1)S(1)}, bf16[128,2048]{1,0:T(8,128)(2,1)}, u32[]{:S(2)}, u32[]{:S(2)}) %collective-permute-start.8) | collective-permute-done | bytes 524320 | tf_op jit(solution)/shard_map/ppermute | solution.py:739
  61.8 4.7 collective-permute-done.2.refs_3_
  66.5 11.2 %collective-permute-done.4.refs_5_ = bf16[512,512]{1,0:T(8,128)(2,1)S(1)} collective-permute-done((bf16[512,512]{1,0:T(8,128)(2,1)S(1)}, bf16[512,512]{1,0:T(8,128)(2,1)S(1)}, u32[]{:S(2)}, u32[]{:S(2)}) %collective-permute-start.4) | collective-permute-done | bytes 524320 | tf_op jit(solution)/shard_map/ppermute | solution.py:739
  77.7 9.0 %collective-permute-done.6.refs_7_ = bf16[512,512]{1,0:T(8,128)(2,1)} collective-permute-done((bf16[512,512]{1,0:T(8,128)(2,1)S(1)}, bf16[512,512]{1,0:T(8,128)(2,1)}, u32[]{:S(2)}, u32[]{:S(2)}) %collective-permute-start.6) | collective-permute-done | bytes 524320 | tf_op jit(solution)/shard_map/ppermute | solution.py:739
  86.7 27.8 %attention_forward.1 = (bf16[512,512]{1,0:T(8,128)(2,1)}, f32[2,4,256]{2,1,0:T(4,128)}, bf16[256,2048]{1,0:T(8,128)(2,1)}, bf16[256,2048]{1,0:T(8,128)(2,1)}) custom-call(s32[32]{0:T(128)} %order_ref.7, s32[8]{0:T(128)} %cont_ref.7, s32[2]{0:T(128)} %pad_add_fusion.where_ref, bf16[512,512]{1,0:T(8,128)(2,1)} %get-tuple-element.116.q_ref, ...), custom_call_target="tpu_custom_call" | custom-call | flops 64424508 | bytes 167772 | tf_op jit(solution)/shard_map/attention_forward/pallas_call | solution.py:343
  126.4 9.8 %grad_hidden.1.gh_ref = f32[1024,1024]{1,0:T(8,128)} custom-call(s32[2]{0:T(128)} %pad_add_fusion.where_ref, bf16[1024,2048]{1,0:T(8,128)(2,1)} %slice_dynamic-update-slice_fusion.4.cot_ref.refs_0_, bf16[2048,2048]{1,0:T(8,128)(2,1)} %wd_ref.3), custom_call_target="tpu_custom_call" | custom-call | flops 68719476736 | bytes 134217728 | tf_op jit(solution)/shard_map/grad_hidden/pallas_call | solution.py:548
  142.0 3.7 collective-permute-start.12
  147.2 9.9 %collective-permute-done.12 = bf16[128,2048]{1,0:T(8,128)(2,1)S(1)} collective-permute-done((bf16[128,2048]{1,0:T(8,128)(2,1)S(1)}, bf16[128,2048]{1,0:T(8,128)(2,1)S(1)}, u32[]{:S(2)}, u32[]{:S(2)}) %collective-permute-start.12) | collective-permute-done | bytes 524320 | tf_op jit(solution)/shard_map/ppermute | solution.py:739
  158.6 11.1 %collective-permute-done.14 = bf16[128,2048]{1,0:T(8,128)(2,1)S(1)} collective-permute-done((bf16[128,2048]{1,0:T(8,128)(2,1)S(1)}, bf16[128,2048]{1,0:T(8,128)(2,1)S(1)}, u32[]{:S(2)}, u32[]{:S(2)}) %collective-permute-start.14) | collective-permute-done | bytes 524320 | tf_op jit(solution)/shard_map/ppermute | solution.py:739
  175.7 15.8 %ffn_stage.1 = (bf16[1024,1024]{1,0:T(8,128)(2,1)}, bf16[1024,1024]{1,0:T(8,128)(2,1)}, bf16[1024,1024]{1,0:T(8,128)(2,1)}) custom-call(s32[2]{0:T(128)} %pad_add_fusion.where_ref, bf16[1024,2048]{1,0:T(8,128)(2,1)} %constant_dynamic-update-slice_fusion.3.in_ref.refs_0_, f32[1024,1024]{1,0:T(8,128)} %grad_hidden.1.gh_ref, bf16[2048,2048]{1,0:T(8,128)(2,1)} %wg_ref.3, ...), custom_call_target="tpu_custom_call" | custom-call | flops 171798688 | bytes 251658 | tf_op jit(solution)/shard_map/ffn_stage/pallas_call | solution.py:587
  191.5 11.6 %down_shares.1 = (bf16[4,256,1024]{2,1,0:T(8,128)(2,1)}, bf16[4,256,1024]{2,1,0:T(8,128)(2,1)}) custom-call(s32[2]{0:T(128)} %pad_add_fusion.where_ref, bf16[1024,2048]{1,0:T(8,128)(2,1)} %slice_dynamic-update-slice_fusion.4.cot_ref.refs_0_, bf16[1024,1024]{1,0:T(8,128)(2,1)} %get-tuple-element.131.refs_1_.hid_ref), custom_call_target="tpu_custom_call" | custom-call | flops 85899344 | bytes 167772 | tf_op jit(solution)/shard_map/down_shares/pallas_call | solution.py:668
  203.1 14.2 %grad_second.1 = (bf16[512,2048]{1,0:T(8,128)(2,1)}, bf16[512,2048]{1,0:T(8,128)(2,1)}) custom-call(s32[2]{0:T(128)} %pad_add_fusion.where_ref, bf16[1024,1024]{1,0:T(8,128)(2,1)} %get-tuple-element.135.gg_ref.refs_1_, bf16[1024,1024]{1,0:T(8,128)(2,1)} %get-tuple-element.144.gu_ref.refs_1_, bf16[2048,2048]{1,0:T(8,128)(2,1)} %wg_ref.3, ...), custom_call_target="tpu_custom_call" | custom-call | flops 171798688 | bytes 167772 | tf_op jit(solution)/shard_map/grad_second/pallas_call | solution.py:632
  217.5 8.8 %ffn_out.1 = (bf16[512,2048]{1,0:T(8,128)(2,1)}, bf16[512,2048]{1,0:T(8,128)(2,1)}) custom-call(s32[2]{0:T(128)} %pad_add_fusion.where_ref, bf16[1024,1024]{1,0:T(8,128)(2,1)} %get-tuple-element.131.refs_1_.hid_ref, bf16[2048,2048]{1,0:T(8,128)(2,1)} %wd_ref.3), custom_call_target="tpu_custom_call" | custom-call | flops 68719476736 | bytes 134217728 | tf_op jit(solution)/shard_map/ffn_out/pallas_call | solution.py:632
  230.8 11.7 %gate_shares.1 = (bf16[4,256,1024]{2,1,0:T(8,128)(2,1)}, bf16[4,256,1024]{2,1,0:T(8,128)(2,1)}) custom-call(s32[2]{0:T(128)} %pad_add_fusion.where_ref, bf16[1024,2048]{1,0:T(8,128)(2,1)} %constant_dynamic-update-slice_fusion.3.in_ref.refs_0_, bf16[1024,1024]{1,0:T(8,128)(2,1)} %get-tuple-element.135.gg_ref.refs_1_), custom_call_target="tpu_custom_call" | custom-call | flops 85899344 | bytes 167772 | tf_op jit(solution)/shard_map/gate_shares/pallas_call | solution.py:668
  247.1 18.7 %collective-permute-done.18 = bf16[4,256,1024]{2,1,0:T(8,128)(2,1)} collective-permute-done((bf16[4,256,1024]{2,1,0:T(8,128)(2,1)}, bf16[4,256,1024]{2,1,0:T(8,128)(2,1)}, u32[]{:S(2)}, u32[]{:S(2)}) %collective-permute-start.18) | collective-permute-done | bytes 2097184 | tf_op jit(solution)/shard_map/ppermute | solution.py:739
  265.7 4.5 add_convert_fusion.5
  274.8 11.7 %up_shares.1 = (bf16[4,256,1024]{2,1,0:T(8,128)(2,1)}, bf16[4,256,1024]{2,1,0:T(8,128)(2,1)}) custom-call(s32[2]{0:T(128)} %pad_add_fusion.where_ref, bf16[1024,2048]{1,0:T(8,128)(2,1)} %constant_dynamic-update-slice_fusion.3.in_ref.refs_0_, bf16[1024,1024]{1,0:T(8,128)(2,1)} %get-tuple-element.144.gu_ref.refs_1_), custom_call_target="tpu_custom_call" | custom-call | flops 68719476736 | bytes 134217728 | tf_op jit(solution)/shard_map/up_shares/pallas_call | solution.py:668
  286.8 4.1 collective-permute-start.24
  290.8 2.7 pad_maximum_fusion.1.gb_ref.refs_1_
  293.6 19.7 %attention_backward_0.1 = (bf16[512,256]{1,0:T(8,128)(2,1)}, bf16[2048,256]{1,0:T(8,128)(2,1)}, bf16[2048,256]{1,0:T(8,128)(2,1)}) custom-call(s32[32]{0:T(128)} %order_ref.7, s32[8]{0:T(128)} %cont_ref.7, s32[2]{0:T(128)} %pad_add_fusion.where_ref, bf16[512,512]{1,0:T(8,128)(2,1)} %get-tuple-element.116.q_ref, ...), custom_call_target="tpu_custom_call" | custom-call | flops 64424508 | bytes 125829 | tf_op jit(solution)/shard_map/attention_backward_0/pallas_call | solution.py:379
  313.3 19.7 %attention_backward_1.1 = (bf16[512,256]{1,0:T(8,128)(2,1)}, bf16[2048,256]{1,0:T(8,128)(2,1)}, bf16[2048,256]{1,0:T(8,128)(2,1)}) custom-call(s32[32]{0:T(128)} %order_ref.7, s32[8]{0:T(128)} %cont_ref.7, s32[2]{0:T(128)} %pad_add_fusion.where_ref, bf16[512,512]{1,0:T(8,128)(2,1)} %get-tuple-element.116.q_ref, ...), custom_call_target="tpu_custom_call" | custom-call | flops 64424508 | bytes 125829 | tf_op jit(solution)/shard_map/attention_backward_1/pallas_call | solution.py:379
  333.1 4.2 add_convert_fusion.4
  339.4 3.6 collective-permute-start.57
  343.0 3.5 collective-permute-start.25
  348.6 18.0 %collective-permute-done.57 = bf16[256,1024]{1,0:T(8,128)(2,1)} collective-permute-done((bf16[256,1024]{1,0:T(8,128)(2,1)}, bf16[256,1024]{1,0:T(8,128)(2,1)}, u32[]{:S(2)}, u32[]{:S(2)}) %collective-permute-start.57) | collective-permute-done | bytes 524320 | tf_op jit(solution)/shard_map/ppermute | solution.py:739
  369.0 10.0 %branch_shares.1 = (bf16[4,256,1024]{2,1,0:T(8,128)(2,1)}, bf16[4,256,1024]{2,1,0:T(8,128)(2,1)}) custom-call(s32[2]{0:T(128)} %pad_add_fusion.where_ref, bf16[512,2048]{1,0:T(8,128)(2,1)} %get-tuple-element.123.refs_0_, bf16[512,2048]{1,0:T(8,128)(2,1)} %pad_maximum_fusion.1.gb_ref.refs_1_, bf16[512,256]{1,0:T(8,128)(2,1)} %get-tuple-element.151.refs_2_.refs_6_, ...), custom_call_target="tpu_custom_call" | custom-call | flops 34359738368 | bytes 67108864 | tf_op jit(solution)/shard_map/branch_shares/pallas_call | solution.py:668
  378.9 13.6 %collective-permute-done.25 = bf16[2,256,1024]{2,1,0:T(8,128)(2,1)} collective-permute-done((bf16[2,256,1024]{2,1,0:T(8,128)(2,1)}, bf16[2,256,1024]{2,1,0:T(8,128)(2,1)}, u32[]{:S(2)}, u32[]{:S(2)}) %collective-permute-start.25) | collective-permute-done | bytes 1048608 | tf_op jit(solution)/shard_map/ppermute | solution.py:739
  392.5 2.7 fusion.14
  406.2 7.4 %collective-permute-done.29 = bf16[1024,256]{1,0:T(8,128)(2,1)S(1)} collective-permute-done((bf16[1024,256]{1,0:T(8,128)(2,1)S(1)}, bf16[1024,256]{1,0:T(8,128)(2,1)S(1)}, u32[]{:S(2)}, u32[]{:S(2)}) %collective-permute-start.29) | collective-permute-done | bytes 524320 | tf_op jit(solution)/shard_map/ppermute | solution.py:739
  414.5 9.8 %collective-permute-done.30 = bf16[1024,256]{1,0:T(8,128)(2,1)S(1)} collective-permute-done((bf16[1024,256]{1,0:T(8,128)(2,1)S(1)}, bf16[1024,256]{1,0:T(8,128)(2,1)S(1)}, u32[]{:S(2)}, u32[]{:S(2)}) %collective-permute-start.30) | collective-permute-done | bytes 524320 | tf_op jit(solution)/shard_map/ppermute | solution.py:739
  431.2 13.9 %collective-permute-done.33.refs_3_ = bf16[512,256]{1,0:T(8,128)(2,1)S(1)} collective-permute-done((bf16[512,256]{1,0:T(8,128)(2,1)S(1)}, bf16[512,256]{1,0:T(8,128)(2,1)S(1)}, u32[]{:S(2)}, u32[]{:S(2)}) %collective-permute-start.33) | collective-permute-done | bytes 262176 | tf_op jit(solution)/shard_map/ppermute | solution.py:739
  451.3 6.6 %tail_stage.1 = (bf16[256,2048]{1,0:T(8,128)(2,1)}, bf16[256,2048]{1,0:T(8,128)(2,1)}, bf16[512,512]{1,0:T(8,128)(2,1)}) custom-call(s32[2]{0:T(128)} %pad_add_fusion.where_ref, bf16[512,256]{1,0:T(8,128)(2,1)} %get-tuple-element.286.refs_0_, bf16[512,256]{1,0:T(8,128)(2,1)} %copy-done.39, bf16[512,256]{1,0:T(8,128)(2,1)} %get-tuple-element.288.refs_2_, ...), custom_call_target="tpu_custom_call" | custom-call | flops 42949672 | bytes 167772 | tf_op jit(solution)/shard_map/tail_stage/pallas_call | solution.py:721
  458.0 8.0 %kv_shares.1 = (bf16[4,256,512]{2,1,0:T(8,128)(2,1)}, bf16[4,256,512]{2,1,0:T(8,128)(2,1)}) custom-call(s32[2]{0:T(128)} %pad_add_fusion.where_ref, bf16[512,2048]{1,0:T(8,128)(2,1)} %get-tuple-element.123.refs_0_, bf16[512,512]{1,0:T(8,128)(2,1)} %get-tuple-element.196.refs_1_), custom_call_target="tpu_custom_call" | custom-call | flops 17179869184 | bytes 67108864 | tf_op jit(solution)/shard_map/kv_shares/pallas_call | solution.py:668
  469.7 2.9 collective-permute-start.40
  472.6 10.2 %collective-permute-done.38 = bf16[128,2048]{1,0:T(8,128)(2,1)} collective-permute-done((bf16[128,2048]{1,0:T(8,128)(2,1)}, bf16[128,2048]{1,0:T(8,128)(2,1)}, u32[]{:S(2)}, u32[]{:S(2)}) %collective-permute-start.38) | collective-permute-done | bytes 524320 | tf_op jit(solution)/shard_map/ppermute | solution.py:739
  487.6 9.1 %collective-permute-done.39 = bf16[4,256,1024]{2,1,0:T(8,128)(2,1)} collective-permute-done((bf16[4,256,1024]{2,1,0:T(8,128)(2,1)}, bf16[4,256,1024]{2,1,0:T(8,128)(2,1)}, u32[]{:S(2)}, u32[]{:S(2)}) %collective-permute-start.39) | collective-permute-done | bytes 2097184 | tf_op jit(solution)/shard_map/ppermute | solution.py:739
  496.7 3.6 add_convert_fusion
  500.3 18.4 %collective-permute-done.40 = bf16[2,256,1024]{2,1,0:T(8,128)(2,1)S(1)} collective-permute-done((bf16[2,256,1024]{2,1,0:T(8,128)(2,1)}, bf16[2,256,1024]{2,1,0:T(8,128)(2,1)S(1)}, u32[]{:S(2)}, u32[]{:S(2)}) %collective-permute-start.40) | collective-permute-done | bytes 1048608 | tf_op jit(solution)/shard_map/ppermute | solution.py:739
  532.5 5.9 collective-permute-done.43
  541.1 25.4 %collective-permute-done.48 = f32[2,2048]{1,0:T(2,128)S(1)} collective-permute-done((f32[2,2048]{1,0:T(2,128)S(1)}, f32[2,2048]{1,0:T(2,128)S(1)}, u32[]{:S(2)}, u32[]{:S(2)}) %collective-permute-start.48) | collective-permute-done | bytes 16416 | tf_op jit(solution)/shard_map/ppermute | solution.py:739
  567.6 3.7 collective-permute-done.49
  575.2 8.1 %collective-permute-done.56 = bf16[256,1024]{1,0:T(8,128)(2,1)S(1)} collective-permute-done((bf16[256,1024]{1,0:T(8,128)(2,1)}, bf16[256,1024]{1,0:T(8,128)(2,1)S(1)}, u32[]{:S(2)}, u32[]{:S(2)}) %collective-permute-start.56) | collective-permute-done | bytes 524320 | tf_op jit(solution)/shard_map/ppermute | solution.py:739
  593.4 18.3 %collective-permute-done.52 = bf16[2,256,512]{2,1,0:T(8,128)(2,1)S(1)} collective-permute-done((bf16[2,256,512]{2,1,0:T(8,128)(2,1)S(1)}, bf16[2,256,512]{2,1,0:T(8,128)(2,1)S(1)}, u32[]{:S(2)}, u32[]{:S(2)}) %collective-permute-start.52) | collective-permute-done | bytes 524320 | tf_op jit(solution)/shard_map/ppermute | solution.py:739
  612.5 13.0 %collective-permute-done.54 = bf16[1,256,512]{2,1,0:T(8,128)(2,1)S(1)} collective-permute-done((bf16[1,256,512]{2,1,0:T(8,128)(2,1)S(1)}, bf16[1,256,512]{2,1,0:T(8,128)(2,1)S(1)}, u32[]{:S(2)}, u32[]{:S(2)}) %collective-permute-start.54) | collective-permute-done | bytes 262176 | tf_op jit(solution)/shard_map/ppermute | solution.py:739
  (251 shorter events, 128.4 us)
Async XLA Ops:
  8.5 27.6 %collective-permute-start.3 = (bf16[512,512]{1,0:T(8,128)(2,1)}, bf16[512,512]{1,0:T(8,128)(2,1)S(1)}, u32[]{:S(2)}, u32[]{:S(2)}) collective-permute-start(bf16[512,512]{1,0:T(8,128)(2,1)} %get-tuple-element.117.refs_0_), channel_id=1, source_target_pairs={{0,16},{4,20},{8,24},{12,28},{16,0},{20,4},{24,8},{28,12},{1,17},{... | collective-permute-start | bytes 1572872 | tf_op jit(solution)/shard_map/ppermute | solution.py:739
  12.6 26.2 %collective-permute-start.1 = (bf16[512,512]{1,0:T(8,128)(2,1)}, bf16[512,512]{1,0:T(8,128)(2,1)S(1)}, u32[]{:S(2)}, u32[]{:S(2)}) collective-permute-start(bf16[512,512]{1,0:T(8,128)(2,1)} %get-tuple-element.117.refs_0_), channel_id=1, source_target_pairs={{0,8},{4,12},{8,0},{12,4},{16,24},{20,28},{24,16},{28,20},{1,9},{5... | collective-permute-start | bytes 1572872 | tf_op jit(solution)/shard_map/ppermute | solution.py:739
  36.1 14.9 %collective-permute-start.5 = (bf16[512,512]{1,0:T(8,128)(2,1)S(1)}, bf16[512,512]{1,0:T(8,128)(2,1)S(1)}, u32[]{:S(2)}, u32[]{:S(2)}) collective-permute-start(bf16[512,512]{1,0:T(8,128)(2,1)S(1)} %collective-permute-done.3.refs_4_), channel_id=1, source_target_pairs={{0,8},{4,12},{8,0},{12,4},{16,24},{20,28},{24,16},{28,20},{1,9},{5... | collective-permute-start | bytes 1572872 | tf_op jit(solution)/shard_map/ppermute | solution.py:739
  38.8 21.7 %collective-permute-start.8 = (bf16[128,2048]{1,0:T(8,128)(2,1)S(1)}, bf16[128,2048]{1,0:T(8,128)(2,1)}, u32[]{:S(2)}, u32[]{:S(2)}) collective-permute-start(bf16[128,2048]{1,0:T(8,128)(2,1)S(1)} %get-tuple-element.120), channel_id=1, source_target_pairs={{0,8},{4,12},{8,0},{12,4},{16,24},{20,28},{24,16},{28,20},{1,9},{5... | collective-permute-start | bytes 1572872 | tf_op jit(solution)/shard_map/ppermute | solution.py:739
  40.2 21.6 %collective-permute-start = (bf16[512,512]{1,0:T(8,128)(2,1)}, bf16[512,512]{1,0:T(8,128)(2,1)S(1)}, u32[]{:S(2)}, u32[]{:S(2)}) collective-permute-start(bf16[512,512]{1,0:T(8,128)(2,1)} %get-tuple-element.117.refs_0_), channel_id=1, source_target_pairs={{0,4},{4,0},{8,12},{12,8},{16,20},{20,16},{24,28},{28,24},{1,5},{5... | collective-permute-start | bytes 1572872 | tf_op jit(solution)/shard_map/ppermute | solution.py:739
  41.7 24.8 %collective-permute-start.2 = (bf16[512,512]{1,0:T(8,128)(2,1)S(1)}, bf16[512,512]{1,0:T(8,128)(2,1)S(1)}, u32[]{:S(2)}, u32[]{:S(2)}) collective-permute-start(bf16[512,512]{1,0:T(8,128)(2,1)S(1)} %collective-permute-done.1.refs_2_), channel_id=1, source_target_pairs={{0,4},{4,0},{8,12},{12,8},{16,20},{20,16},{24,28},{28,24},{1,5},{5... | collective-permute-start | bytes 1572872 | tf_op jit(solution)/shard_map/ppermute | solution.py:739
  42.2 35.5 %collective-permute-start.4 = (bf16[512,512]{1,0:T(8,128)(2,1)S(1)}, bf16[512,512]{1,0:T(8,128)(2,1)S(1)}, u32[]{:S(2)}, u32[]{:S(2)}) collective-permute-start(bf16[512,512]{1,0:T(8,128)(2,1)S(1)} %collective-permute-done.3.refs_4_), channel_id=1, source_target_pairs={{0,4},{4,0},{8,12},{12,8},{16,20},{20,16},{24,28},{28,24},{1,5},{5... | collective-permute-start | bytes 1572872 | tf_op jit(solution)/shard_map/ppermute | solution.py:739
  51.0 35.7 %collective-permute-start.6 = (bf16[512,512]{1,0:T(8,128)(2,1)S(1)}, bf16[512,512]{1,0:T(8,128)(2,1)}, u32[]{:S(2)}, u32[]{:S(2)}) collective-permute-start(bf16[512,512]{1,0:T(8,128)(2,1)S(1)} %collective-permute-done.5.refs_6_), channel_id=1, source_target_pairs={{0,4},{4,0},{8,12},{12,8},{16,20},{20,16},{24,28},{28,24},{1,5},{5... | collective-permute-start | bytes 1572872 | tf_op jit(solution)/shard_map/ppermute | solution.py:739
  60.5 56.1 %collective-permute-start.9 = (bf16[128,2048]{1,0:T(8,128)(2,1)}, bf16[128,2048]{1,0:T(8,128)(2,1)}, u32[]{:S(2)}, u32[]{:S(2)}) collective-permute-start(bf16[128,2048]{1,0:T(8,128)(2,1)} %collective-permute-done.8), channel_id=1, source_target_pairs={{0,2},{1,3},{2,0},{3,1},{4,6},{5,7},{6,4},{7,5},{8,10},{9,11},{10,... | collective-permute-start | bytes 1572872 | tf_op jit(solution)/shard_map/ppermute | solution.py:739
  124.9 14.0 %collective-permute-start.11 = (bf16[128,2048]{1,0:T(8,128)(2,1)S(1)}, bf16[128,2048]{1,0:T(8,128)(2,1)S(1)}, u32[]{:S(2)}, u32[]{:S(2)}) collective-permute-start(bf16[128,2048]{1,0:T(8,128)(2,1)S(1)} %slice.205), channel_id=1, source_target_pairs={{0,2},{1,3},{2,0},{3,1},{4,6},{5,7},{6,4},{7,5},{8,10},{9,11},{10,... | collective-permute-start | bytes 1572872 | tf_op jit(solution)/shard_map/ppermute | solution.py:739
  142.0 15.1 %collective-permute-start.12 = (bf16[128,2048]{1,0:T(8,128)(2,1)S(1)}, bf16[128,2048]{1,0:T(8,128)(2,1)S(1)}, u32[]{:S(2)}, u32[]{:S(2)}) collective-permute-start(bf16[128,2048]{1,0:T(8,128)(2,1)S(1)} %get-tuple-element.247), channel_id=1, source_target_pairs={{0,8},{4,12},{8,0},{12,4},{16,24},{20,28},{24,16},{28,20},{1,9},{5... | collective-permute-start | bytes 1572872 | tf_op jit(solution)/shard_map/ppermute | solution.py:739
  145.7 13.0 %collective-permute-start.13 = (bf16[128,2048]{1,0:T(8,128)(2,1)S(1)}, bf16[128,2048]{1,0:T(8,128)(2,1)S(1)}, u32[]{:S(2)}, u32[]{:S(2)}) collective-permute-start(bf16[128,2048]{1,0:T(8,128)(2,1)S(1)} %get-tuple-element.247), channel_id=1, source_target_pairs={{0,2},{1,3},{2,0},{3,1},{4,6},{5,7},{6,4},{7,5},{8,10},{9,11},{10,... | collective-permute-start | bytes 1572872 | tf_op jit(solution)/shard_map/ppermute | solution.py:739
  157.1 12.7 %collective-permute-start.14 = (bf16[128,2048]{1,0:T(8,128)(2,1)S(1)}, bf16[128,2048]{1,0:T(8,128)(2,1)S(1)}, u32[]{:S(2)}, u32[]{:S(2)}) collective-permute-start(bf16[128,2048]{1,0:T(8,128)(2,1)S(1)} %collective-permute-done.12), channel_id=1, source_target_pairs={{0,2},{1,3},{2,0},{3,1},{4,6},{5,7},{6,4},{7,5},{8,10},{9,11},{10,... | collective-permute-start | bytes 1572872 | tf_op jit(solution)/shard_map/ppermute | solution.py:739
  217.5 48.2 %collective-permute-start.18 = (bf16[4,256,1024]{2,1,0:T(8,128)(2,1)}, bf16[4,256,1024]{2,1,0:T(8,128)(2,1)}, u32[]{:S(2)}, u32[]{:S(2)}) collective-permute-start(bf16[4,256,1024]{2,1,0:T(8,128)(2,1)} %get-tuple-element.138), channel_id=1, source_target_pairs={{0,4},{4,0},{8,12},{12,8},{16,20},{20,16},{24,28},{28,24},{1,5},{5... | collective-permute-start | bytes 6291464 | tf_op jit(solution)/shard_map/ppermute | solution.py:739
  228.7 14.8 %collective-permute-start.17 = (bf16[128,2048]{1,0:T(8,128)(2,1)S(1)}, bf16[128,2048]{1,0:T(8,128)(2,1)S(1)}, u32[]{:S(2)}, u32[]{:S(2)}) collective-permute-start(bf16[128,2048]{1,0:T(8,128)(2,1)S(1)} %get-tuple-element.265), channel_id=1, source_target_pairs={{0,2},{1,3},{2,0},{3,1},{4,6},{5,7},{6,4},{7,5},{8,10},{9,11},{10,... | collective-permute-start | bytes 1572872 | tf_op jit(solution)/shard_map/ppermute | solution.py:739
  230.3 40.2 %collective-permute-start.19 = (bf16[128,2048]{1,0:T(8,128)(2,1)S(1)}, bf16[128,2048]{1,0:T(8,128)(2,1)S(1)}, u32[]{:S(2)}, u32[]{:S(2)}) collective-permute-start(bf16[128,2048]{1,0:T(8,128)(2,1)S(1)} %get-tuple-element.263), channel_id=1, source_target_pairs={{0,2},{1,3},{2,0},{3,1},{4,6},{5,7},{6,4},{7,5},{8,10},{9,11},{10,... | collective-permute-start | bytes 1572872 | tf_op jit(solution)/shard_map/ppermute | solution.py:739
  245.8 24.7 %collective-permute-start.20 = (bf16[128,2048]{1,0:T(8,128)(2,1)}, bf16[128,2048]{1,0:T(8,128)(2,1)S(1)}, u32[]{:S(2)}, u32[]{:S(2)}) collective-permute-start(bf16[128,2048]{1,0:T(8,128)(2,1)} %add_convert_fusion.33), channel_id=1, source_target_pairs={{0,8},{4,12},{8,0},{12,4},{16,24},{20,28},{24,16},{28,20},{1,9},{5... | collective-permute-start | bytes 1572872 | tf_op jit(solution)/shard_map/ppermute | solution.py:739
  270.2 62.8 %collective-permute-start.23 = (bf16[4,256,1024]{2,1,0:T(8,128)(2,1)}, bf16[4,256,1024]{2,1,0:T(8,128)(2,1)}, u32[]{:S(2)}, u32[]{:S(2)}) collective-permute-start(bf16[4,256,1024]{2,1,0:T(8,128)(2,1)} %get-tuple-element.156), channel_id=1, source_target_pairs={{0,4},{4,0},{8,12},{12,8},{16,20},{20,16},{24,28},{28,24},{1,5},{5... | collective-permute-start | bytes 6291464 | tf_op jit(solution)/shard_map/ppermute | solution.py:739
  273.2 13.4 %collective-permute-start.21 = (bf16[128,2048]{1,0:T(8,128)(2,1)S(1)}, bf16[128,2048]{1,0:T(8,128)(2,1)S(1)}, u32[]{:S(2)}, u32[]{:S(2)}) collective-permute-start(bf16[128,2048]{1,0:T(8,128)(2,1)S(1)} %get-tuple-element.244), channel_id=1, source_target_pairs={{0,2},{1,3},{2,0},{3,1},{4,6},{5,7},{6,4},{7,5},{8,10},{9,11},{10,... | collective-permute-start | bytes 1572872 | tf_op jit(solution)/shard_map/ppermute | solution.py:739
  286.8 50.6 %collective-permute-start.24 = (bf16[2,256,1024]{2,1,0:T(8,128)(2,1)}, bf16[2,256,1024]{2,1,0:T(8,128)(2,1)}, u32[]{:S(2)}, u32[]{:S(2)}) collective-permute-start(bf16[2,256,1024]{2,1,0:T(8,128)(2,1)} %get-tuple-element.261), channel_id=1, source_target_pairs={{0,16},{4,20},{8,24},{12,28},{16,0},{20,4},{24,8},{28,12},{1,17},{... | collective-permute-start | bytes 3145736 | tf_op jit(solution)/shard_map/ppermute | solution.py:739
  339.4 27.2 %collective-permute-start.57 = (bf16[256,1024]{1,0:T(8,128)(2,1)}, bf16[256,1024]{1,0:T(8,128)(2,1)}, u32[]{:S(2)}, u32[]{:S(2)}) collective-permute-start(bf16[256,1024]{1,0:T(8,128)(2,1)} %fusion.16), channel_id=1, source_target_pairs={{0,8},{4,12},{8,0},{12,4},{16,24},{20,28},{24,16},{28,20},{1,9},{5... | collective-permute-start | bytes 1572872 | tf_op jit(solution)/shard_map/ppermute | solution.py:739
  343.0 49.5 %collective-permute-start.25 = (bf16[2,256,1024]{2,1,0:T(8,128)(2,1)}, bf16[2,256,1024]{2,1,0:T(8,128)(2,1)}, u32[]{:S(2)}, u32[]{:S(2)}) collective-permute-start(bf16[2,256,1024]{2,1,0:T(8,128)(2,1)} %get-tuple-element.259), channel_id=1, source_target_pairs={{0,16},{4,20},{8,24},{12,28},{16,0},{20,4},{24,8},{28,12},{1,17},{... | collective-permute-start | bytes 3145736 | tf_op jit(solution)/shard_map/ppermute | solution.py:739
  346.5 48.7 %collective-permute-start.26 = (bf16[2048,256]{1,0:T(8,128)(2,1)}, bf16[2048,256]{1,0:T(8,128)(2,1)}, u32[]{:S(2)}, u32[]{:S(2)}) collective-permute-start(bf16[2048,256]{1,0:T(8,128)(2,1)} %get-tuple-element.166), channel_id=1, source_target_pairs={{0,4},{4,0},{8,12},{12,8},{16,20},{20,16},{24,28},{28,24},{1,5},{5... | collective-permute-start | bytes 3145736 | tf_op jit(solution)/shard_map/ppermute | solution.py:739
  346.5 50.4 %collective-permute-start.27 = (bf16[2048,256]{1,0:T(8,128)(2,1)}, bf16[2048,256]{1,0:T(8,128)(2,1)}, u32[]{:S(2)}, u32[]{:S(2)}) collective-permute-start(bf16[2048,256]{1,0:T(8,128)(2,1)} %get-tuple-element.170), channel_id=1, source_target_pairs={{0,4},{4,0},{8,12},{12,8},{16,20},{20,16},{24,28},{28,24},{1,5},{5... | collective-permute-start | bytes 3145736 | tf_op jit(solution)/shard_map/ppermute | solution.py:739
  398.7 48.0 %collective-permute-start.34 = (bf16[4,256,1024]{2,1,0:T(8,128)(2,1)S(1)}, bf16[4,256,1024]{2,1,0:T(8,128)(2,1)S(1)}, u32[]{:S(2)}, u32[]{:S(2)}) collective-permute-start(bf16[4,256,1024]{2,1,0:T(8,128)(2,1)S(1)} %copy-done.44), channel_id=1, source_target_pairs={{0,4},{4,0},{8,12},{12,8},{16,20},{20,16},{24,28},{28,24},{1,5},{5... | collective-permute-start | bytes 6291464 | tf_op jit(solution)/shard_map/ppermute | solution.py:739
  398.8 14.8 %collective-permute-start.29 = (bf16[1024,256]{1,0:T(8,128)(2,1)S(1)}, bf16[1024,256]{1,0:T(8,128)(2,1)S(1)}, u32[]{:S(2)}, u32[]{:S(2)}) collective-permute-start(bf16[1024,256]{1,0:T(8,128)(2,1)S(1)} %get-tuple-element.277), channel_id=1, source_target_pairs={{0,8},{4,12},{8,0},{12,4},{16,24},{20,28},{24,16},{28,20},{1,9},{5... | collective-permute-start | bytes 1572872 | tf_op jit(solution)/shard_map/ppermute | solution.py:739
  398.9 25.4 %collective-permute-start.30 = (bf16[1024,256]{1,0:T(8,128)(2,1)S(1)}, bf16[1024,256]{1,0:T(8,128)(2,1)S(1)}, u32[]{:S(2)}, u32[]{:S(2)}) collective-permute-start(bf16[1024,256]{1,0:T(8,128)(2,1)S(1)} %get-tuple-element.275), channel_id=1, source_target_pairs={{0,8},{4,12},{8,0},{12,4},{16,24},{20,28},{24,16},{28,20},{1,9},{5... | collective-permute-start | bytes 1572872 | tf_op jit(solution)/shard_map/ppermute | solution.py:739
  404.2 23.9 %collective-permute-start.31 = (bf16[128,2048]{1,0:T(8,128)(2,1)S(1)}, bf16[128,2048]{1,0:T(8,128)(2,1)S(1)}, u32[]{:S(2)}, u32[]{:S(2)}) collective-permute-start(bf16[128,2048]{1,0:T(8,128)(2,1)S(1)} %get-tuple-element.258), channel_id=1, source_target_pairs={{0,2},{1,3},{2,0},{3,1},{4,6},{5,7},{6,4},{7,5},{8,10},{9,11},{10,... | collective-permute-start | bytes 1572872 | tf_op jit(solution)/shard_map/ppermute | solution.py:739
  405.8 23.7 %collective-permute-start.32 = (bf16[128,2048]{1,0:T(8,128)(2,1)S(1)}, bf16[128,2048]{1,0:T(8,128)(2,1)S(1)}, u32[]{:S(2)}, u32[]{:S(2)}) collective-permute-start(bf16[128,2048]{1,0:T(8,128)(2,1)S(1)} %get-tuple-element.257), channel_id=1, source_target_pairs={{0,2},{1,3},{2,0},{3,1},{4,6},{5,7},{6,4},{7,5},{8,10},{9,11},{10,... | collective-permute-start | bytes 1572872 | tf_op jit(solution)/shard_map/ppermute | solution.py:739
  425.2 19.9 %collective-permute-start.33 = (bf16[512,256]{1,0:T(8,128)(2,1)S(1)}, bf16[512,256]{1,0:T(8,128)(2,1)S(1)}, u32[]{:S(2)}, u32[]{:S(2)}) collective-permute-start(bf16[512,256]{1,0:T(8,128)(2,1)S(1)} %get-tuple-element.287), channel_id=1, source_target_pairs={{0,16},{4,20},{8,24},{12,28},{16,0},{20,4},{24,8},{28,12},{1,17},{... | collective-permute-start | bytes 786440 | tf_op jit(solution)/shard_map/ppermute | solution.py:739
  426.3 24.3 %collective-permute-start.36 = (bf16[512,256]{1,0:T(8,128)(2,1)S(1)}, bf16[512,256]{1,0:T(8,128)(2,1)S(1)}, u32[]{:S(2)}, u32[]{:S(2)}) collective-permute-start(bf16[512,256]{1,0:T(8,128)(2,1)S(1)} %get-tuple-element.285), channel_id=1, source_target_pairs={{0,16},{4,20},{8,24},{12,28},{16,0},{20,4},{24,8},{28,12},{1,17},{... | collective-permute-start | bytes 786440 | tf_op jit(solution)/shard_map/ppermute | solution.py:739
  449.2 47.5 %collective-permute-start.39 = (bf16[4,256,1024]{2,1,0:T(8,128)(2,1)}, bf16[4,256,1024]{2,1,0:T(8,128)(2,1)}, u32[]{:S(2)}, u32[]{:S(2)}) collective-permute-start(bf16[4,256,1024]{2,1,0:T(8,128)(2,1)} %get-tuple-element.202), channel_id=1, source_target_pairs={{0,4},{4,0},{8,12},{12,8},{16,20},{20,16},{24,28},{28,24},{1,5},{5... | collective-permute-start | bytes 6291464 | tf_op jit(solution)/shard_map/ppermute | solution.py:739
  468.1 14.6 %collective-permute-start.38 = (bf16[128,2048]{1,0:T(8,128)(2,1)}, bf16[128,2048]{1,0:T(8,128)(2,1)}, u32[]{:S(2)}, u32[]{:S(2)}) collective-permute-start(bf16[128,2048]{1,0:T(8,128)(2,1)} %add_convert_fusion.17), channel_id=1, source_target_pairs={{0,2},{1,3},{2,0},{3,1},{4,6},{5,7},{6,4},{7,5},{8,10},{9,11},{10,... | collective-permute-start | bytes 1572872 | tf_op jit(solution)/shard_map/ppermute | solution.py:739
  469.7 54.5 %collective-permute-start.35 = (bf16[128,2048]{1,0:T(8,128)(2,1)}, bf16[128,2048]{1,0:T(8,128)(2,1)}, u32[]{:S(2)}, u32[]{:S(2)}) collective-permute-start(bf16[128,2048]{1,0:T(8,128)(2,1)} %add_convert_fusion.21), channel_id=1, source_target_pairs={{0,8},{4,12},{8,0},{12,4},{16,24},{20,28},{24,16},{28,20},{1,9},{5... | collective-permute-start | bytes 1572872 | tf_op jit(solution)/shard_map/ppermute | solution.py:739
  469.7 49.0 %collective-permute-start.40 = (bf16[2,256,1024]{2,1,0:T(8,128)(2,1)}, bf16[2,256,1024]{2,1,0:T(8,128)(2,1)S(1)}, u32[]{:S(2)}, u32[]{:S(2)}) collective-permute-start(bf16[2,256,1024]{2,1,0:T(8,128)(2,1)} %get-tuple-element.254), channel_id=1, source_target_pairs={{0,16},{4,20},{8,24},{12,28},{16,0},{20,4},{24,8},{28,12},{1,17},{... | collective-permute-start | bytes 3145736 | tf_op jit(solution)/shard_map/ppermute | solution.py:739
  524.2 14.3 %collective-permute-start.43 = (bf16[128,2048]{1,0:T(8,128)(2,1)}, bf16[128,2048]{1,0:T(8,128)(2,1)S(1)}, u32[]{:S(2)}, u32[]{:S(2)}) collective-permute-start(bf16[128,2048]{1,0:T(8,128)(2,1)} %get-tuple-element.241), channel_id=1, source_target_pairs={{0,2},{1,3},{2,0},{3,1},{4,6},{5,7},{6,4},{7,5},{8,10},{9,11},{10,... | collective-permute-start | bytes 1572872 | tf_op jit(solution)/shard_map/ppermute | solution.py:739
  525.8 14.2 %collective-permute-start.47 = (f32[2,2048]{1,0:T(2,128)S(1)}, f32[2,2048]{1,0:T(2,128)S(1)}, u32[]{:S(2)}, u32[]{:S(2)}) collective-permute-start(f32[2,2048]{1,0:T(2,128)S(1)} %add.355), channel_id=1, source_target_pairs={{0,4},{4,0},{8,12},{12,8},{16,20},{20,16},{24,28},{28,24},{1,5},{5... | collective-permute-start | bytes 49160 | tf_op jit(solution)/shard_map/ppermute | solution.py:739
  530.0 44.6 %collective-permute-start.55 = (bf16[256,1024]{1,0:T(8,128)(2,1)}, bf16[256,1024]{1,0:T(8,128)(2,1)}, u32[]{:S(2)}, u32[]{:S(2)}) collective-permute-start(bf16[256,1024]{1,0:T(8,128)(2,1)} %get-tuple-element.219), channel_id=1, source_target_pairs={{0,8},{4,12},{8,0},{12,4},{16,24},{20,28},{24,16},{28,20},{1,9},{5... | collective-permute-start | bytes 1572872 | tf_op jit(solution)/shard_map/ppermute | solution.py:739
  530.0 59.3 %collective-permute-start.51 = (bf16[4,256,512]{2,1,0:T(8,128)(2,1)}, bf16[4,256,512]{2,1,0:T(8,128)(2,1)}, u32[]{:S(2)}, u32[]{:S(2)}) collective-permute-start(bf16[4,256,512]{2,1,0:T(8,128)(2,1)} %get-tuple-element.214), channel_id=1, source_target_pairs={{0,4},{4,0},{8,12},{12,8},{16,20},{20,16},{24,28},{28,24},{1,5},{5... | collective-permute-start | bytes 3145736 | tf_op jit(solution)/shard_map/ppermute | solution.py:739
  530.5 57.2 %collective-permute-start.50 = (bf16[2,256,1024]{2,1,0:T(8,128)(2,1)}, bf16[2,256,1024]{2,1,0:T(8,128)(2,1)}, u32[]{:S(2)}, u32[]{:S(2)}) collective-permute-start(bf16[2,256,1024]{2,1,0:T(8,128)(2,1)} %get-tuple-element.252), channel_id=1, source_target_pairs={{0,8},{4,12},{8,0},{12,4},{16,24},{20,28},{24,16},{28,20},{1,9},{5... | collective-permute-start | bytes 3145736 | tf_op jit(solution)/shard_map/ppermute | solution.py:739
  538.4 33.8 %collective-permute-start.41 = (bf16[128,2048]{1,0:T(8,128)(2,1)}, bf16[128,2048]{1,0:T(8,128)(2,1)}, u32[]{:S(2)}, u32[]{:S(2)}) collective-permute-start(bf16[128,2048]{1,0:T(8,128)(2,1)} %get-tuple-element.207), channel_id=1, source_target_pairs={{0,2},{1,3},{2,0},{3,1},{4,6},{5,7},{6,4},{7,5},{8,10},{9,11},{10,... | collective-permute-start | bytes 1572872 | tf_op jit(solution)/shard_map/ppermute | solution.py:739
  540.0 26.6 %collective-permute-start.48 = (f32[2,2048]{1,0:T(2,128)S(1)}, f32[2,2048]{1,0:T(2,128)S(1)}, u32[]{:S(2)}, u32[]{:S(2)}) collective-permute-start(f32[2,2048]{1,0:T(2,128)S(1)} %add.356), channel_id=1, source_target_pairs={{0,8},{4,12},{8,0},{12,4},{16,24},{20,28},{24,16},{28,20},{1,9},{5... | collective-permute-start | bytes 49160 | tf_op jit(solution)/shard_map/ppermute | solution.py:739
  571.3 11.9 %collective-permute-start.56 = (bf16[256,1024]{1,0:T(8,128)(2,1)}, bf16[256,1024]{1,0:T(8,128)(2,1)S(1)}, u32[]{:S(2)}, u32[]{:S(2)}) collective-permute-start(bf16[256,1024]{1,0:T(8,128)(2,1)} %get-tuple-element.220), channel_id=1, source_target_pairs={{0,8},{4,12},{8,0},{12,4},{16,24},{20,28},{24,16},{28,20},{1,9},{5... | collective-permute-start | bytes 1572872 | tf_op jit(solution)/shard_map/ppermute | solution.py:739
  572.2 21.0 %collective-permute-start.44 = (bf16[256,2048]{1,0:T(8,128)(2,1)}, bf16[256,2048]{1,0:T(8,128)(2,1)S(1)}, u32[]{:S(2)}, u32[]{:S(2)}) collective-permute-start(bf16[256,2048]{1,0:T(8,128)(2,1)} %pad_maximum_fusion.5), channel_id=1, source_target_pairs={{0,1},{1,0},{2,3},{3,2},{4,5},{5,4},{6,7},{7,6},{8,9},{9,8},{10,11... | collective-permute-start | bytes 3145736 | tf_op jit(solution)/shard_map/ppermute | solution.py:739
  574.7 37.7 %collective-permute-start.42 = (bf16[256,2048]{1,0:T(8,128)(2,1)S(1)}, bf16[256,2048]{1,0:T(8,128)(2,1)S(1)}, u32[]{:S(2)}, u32[]{:S(2)}) collective-permute-start(bf16[256,2048]{1,0:T(8,128)(2,1)S(1)} %pad_maximum_fusion.4), channel_id=1, source_target_pairs={{0,1},{1,0},{2,3},{3,2},{4,5},{5,4},{6,7},{7,6},{8,9},{9,8},{10,11... | collective-permute-start | bytes 3145736 | tf_op jit(solution)/shard_map/ppermute | solution.py:739
  590.8 20.9 %collective-permute-start.52 = (bf16[2,256,512]{2,1,0:T(8,128)(2,1)S(1)}, bf16[2,256,512]{2,1,0:T(8,128)(2,1)S(1)}, u32[]{:S(2)}, u32[]{:S(2)}) collective-permute-start(bf16[2,256,512]{2,1,0:T(8,128)(2,1)S(1)} %get-tuple-element.273), channel_id=1, source_target_pairs={{0,8},{4,12},{8,0},{12,4},{16,24},{20,28},{24,16},{28,20},{1,9},{5... | collective-permute-start | bytes 1572872 | tf_op jit(solution)/shard_map/ppermute | solution.py:739
  591.4 34.2 %collective-permute-start.53 = (bf16[1,256,1024]{2,1,0:T(8,128)(2,1)S(1)}, bf16[1,256,1024]{2,1,0:T(8,128)(2,1)S(1)}, u32[]{:S(2)}, u32[]{:S(2)}) collective-permute-start(bf16[1,256,1024]{2,1,0:T(8,128)(2,1)S(1)} %get-tuple-element.270), channel_id=1, source_target_pairs={{0,16},{4,20},{8,24},{12,28},{16,0},{20,4},{24,8},{28,12},{1,17},{... | collective-permute-start | bytes 1572872 | tf_op jit(solution)/shard_map/ppermute | solution.py:739
  611.8 13.7 %collective-permute-start.54 = (bf16[1,256,512]{2,1,0:T(8,128)(2,1)S(1)}, bf16[1,256,512]{2,1,0:T(8,128)(2,1)S(1)}, u32[]{:S(2)}, u32[]{:S(2)}) collective-permute-start(bf16[1,256,512]{2,1,0:T(8,128)(2,1)S(1)} %add_convert_fusion.36), channel_id=1, source_target_pairs={{0,16},{4,20},{8,24},{12,28},{16,0},{20,4},{24,8},{28,12},{1,17},{... | collective-permute-start | bytes 786440 | tf_op jit(solution)/shard_map/ppermute | solution.py:739
  (55 other events, 793.8 us)

commit v7 on v6

--- a/solution.py
+++ b/solution.py
@@ -7,6 +7,7 @@
 from jax import lax
 from jax.experimental import pallas as pl
 from jax.experimental.pallas import tpu as pltpu
+from jax.sharding import Mesh
 from jax.sharding import PartitionSpec as P
 
 HEAD_SIZE = 128
@@ -506,7 +507,7 @@
     )(order, cont, where, gain.reshape(1, -1), x, wq, wk, wv, table)
 
 
-FILLERS = ("ffn_out", "up_shares", "branch_shares", "kv_shares", "grad_hidden")
+FILLERS = ("ffn_out", "gate_shares", "up_shares", "kv_shares", "grad_hidden", "grad_second_keep")
 
 
 def cost(name, flops, bytes_accessed):
@@ -517,9 +518,7 @@
 
 
 def put_share(value, index, x_bit, keep_ref, send_ref, swap_bits):
-    spot = lax.shift_right_logical(index, 1)
-    if swap_bits:
-        spot = (spot & 1) * (keep_ref.shape[0] // 2) + lax.shift_right_logical(spot, 1)
+    spot = share_spot(lax.shift_right_logical(index, 1), keep_ref.shape[0], swap_bits)
     stays = (index & 1) == x_bit
     value = value.astype(keep_ref.dtype)
 
@@ -604,11 +603,31 @@
     )(where, second, grad_hidden, w_gate, w_up)
 
 
-def grad_second_kernel(where_ref, gg_ref, gu_ref, wg_ref, wu_ref, keep_ref, send_ref):
+def grad_second_kernel(where_ref, gg_ref, gu_ref, wg_ref, wu_ref, out_ref):
     total = right_dot(gg_ref[...], wg_ref[...]) + right_dot(gu_ref[...], wu_ref[...])
-    half = keep_ref.shape[0]
-    keep_ref[...] = total[:half].astype(jnp.bfloat16)
-    send_ref[...] = total[half:].astype(jnp.bfloat16)
+    out_ref[...] = total.astype(jnp.bfloat16)
+
+
+def grad_second_half(half, name, grads, weights, where):
+    rows, units = grads[0].shape
+    rows //= 2
+    model = weights[0].shape[0]
+    block = 512
+    left_spec = pl.BlockSpec((rows, units), lambda n, w: (half, 0), pipeline_mode=pl.Buffered(1))
+    right_spec = pl.BlockSpec((block, units), lambda n, w: (n, pair_bit(w)))
+    return pl.pallas_call(
+        grad_second_kernel,
+        out_shape=jax.ShapeDtypeStruct((rows, model), jnp.bfloat16),
+        grid_spec=pltpu.PrefetchScalarGridSpec(
+            num_scalar_prefetch=1,
+            grid=(model // block,),
+            in_specs=[left_spec] * 2 + [right_spec] * 2,
+            out_specs=pl.BlockSpec((rows, block), lambda n, w: (0, n)),
+        ),
+        compiler_params=pltpu.CompilerParams(vmem_limit_bytes=VMEM_LIMIT),
+        cost_estimate=cost(name, 4 * rows * units * model, 4 * rows * model),
+        name=name,
+    )(where, *grads, *weights)
 
 
 def ffn_out_kernel(where_ref, hid_ref, wd_ref, keep_ref, send_ref):
@@ -644,6 +663,12 @@
     )(where, *lefts, *rights)
 
 
+def share_spot(spot, count, swap_bits):
+    if swap_bits:
+        return (spot & 1) * (count // 2) + lax.shift_right_logical(spot, 1)
+    return spot
+
+
 def shares_kernel(left_count, swap_bits, pairs, where_ref, *refs):
     lefts, refs = refs[:left_count], refs[left_count:]
     rights, (keep_ref, send_ref) = refs[:-2], refs[-2:]
@@ -651,6 +676,19 @@
     step = pl.program_id(0)
     pieces = [left_dot(lefts[l][...], rights[r][...]) for l, r in pairs]
     per_step = lefts[0].shape[1] // share
+    if per_step == 1:
+        value = jnp.concatenate(pieces, axis=1).astype(keep_ref.dtype)
+        sends = step < pl.num_programs(0) // 2
+
+        @pl.when(sends)
+        def _():
+            send_ref[0] = value
+
+        @pl.when(jnp.logical_not(sends))
+        def _():
+            keep_ref[0] = value
+
+        return
     for k in range(per_step):
         rows = slice(k * share, (k + 1) * share)
         value = jnp.concatenate([piece[rows] for piece in pieces], axis=1)
@@ -661,27 +699,86 @@
 def weight_shares(name, lefts, rights, pairs, ctx_count, swap_bits, where):
     rows, model = lefts[0].shape
     block = 256
-    share = model // ctx_count
+    share, half = model // ctx_count, ctx_count // 2
     width = sum(rights[r].shape[1] for _, r in pairs)
-    shares = jax.ShapeDtypeStruct((ctx_count // 2, share, width), jnp.bfloat16)
-    share_spec = pl.BlockSpec(shares.shape, lambda i, w: (0, 0, 0))
+    shares = jax.ShapeDtypeStruct((half, share, width), jnp.bfloat16)
+    if share == block:
+
+        def left_map(i, w):
+            mine = w[0] & 1
+            return 0, jnp.where(i < half, 2 * i + 1 - mine, 2 * (i - half) + mine)
+
+        left_spec = pl.BlockSpec((rows, block), left_map)
+        spot = lambda index: share_spot(index, half, swap_bits)
+        keep_spec = pl.BlockSpec(
+            (1, share, width), lambda i, w: (spot(jnp.maximum(i - half, 0)), 0, 0)
+        )
+        send_spec = pl.BlockSpec(
+            (1, share, width), lambda i, w: (spot(jnp.minimum(i, half - 1)), 0, 0)
+        )
+    else:
+        left_spec = pl.BlockSpec((rows, block), lambda i, w: (0, i))
+        keep_spec = send_spec = pl.BlockSpec(shares.shape, lambda i, w: (0, 0, 0))
     return pl.pallas_call(
         functools.partial(shares_kernel, len(lefts), swap_bits, pairs),
         out_shape=(shares, shares),
         grid_spec=pltpu.PrefetchScalarGridSpec(
             num_scalar_prefetch=1,
             grid=(model // block,),
-            in_specs=[pl.BlockSpec((rows, block), lambda i, w: (0, i))] * len(lefts)
+            in_specs=[left_spec] * len(lefts)
             + [
                 pl.BlockSpec(r.shape, lambda i, w: (0, 0), pipeline_mode=pl.Buffered(1))
                 for r in rights
             ],
-            out_specs=[share_spec, share_spec],
+            out_specs=[keep_spec, send_spec],
         ),
         compiler_params=pltpu.CompilerParams(vmem_limit_bytes=VMEM_LIMIT),
         cost_estimate=cost(name, 2 * rows * model * width, 4 * rows * model),
         name=name,
     )(where, *lefts, *rights)
+
+
+def unit_shares_kernel(where_ref, left_ref, right_ref, out_ref):
+    share = out_ref.shape[1]
+    total = left_dot(left_ref[...], right_ref[...]).astype(out_ref.dtype)
+    per_step = left_ref.shape[1] // share
+    if out_ref.shape[0] == 1:
+        out_ref[0] = total
+    else:
+        for k in range(per_step):
+            index = pl.program_id(0) * per_step + k
+            out_ref[pl.ds(unit_spot(index), 1)] = total[k * share : (k + 1) * share][None]
+
+
+def unit_spot(index):
+    return (index & ~3) + (index & 1) * 2 + (lax.shift_right_logical(index, 1) & 1)
+
+
+def unit_shares(name, left, right, ctx_count, where):
+    rows, model = left.shape
+    block, width = 256, right.shape[1]
+    share = model // ctx_count
+    shares = jax.ShapeDtypeStruct((ctx_count, share, width), jnp.bfloat16)
+    if share == block:
+        out_spec = pl.BlockSpec((1, share, width), lambda i, w: (unit_spot(i), 0, 0))
+    else:
+        out_spec = pl.BlockSpec(shares.shape, lambda i, w: (0, 0, 0))
+    return pl.pallas_call(
+        unit_shares_kernel,
+        out_shape=shares,
+        grid_spec=pltpu.PrefetchScalarGridSpec(
+            num_scalar_prefetch=1,
+            grid=(model // block,),
+            in_specs=[
+                pl.BlockSpec((rows, block), lambda i, w: (0, i)),
+                pl.BlockSpec(right.shape, lambda i, w: (0, 0), pipeline_mode=pl.Buffered(1)),
+            ],
+            out_specs=out_spec,
+        ),
+        compiler_params=pltpu.CompilerParams(vmem_limit_bytes=VMEM_LIMIT),
+        cost_estimate=cost(name, 2 * rows * model * width, 4 * rows * model),
+        name=name,
+    )(where, left, right)
 
 
 def tail_kernel(kv_heads, where_ref, *refs):
@@ -735,8 +832,16 @@
     )(where, *flat, cosine, sine, *grad_queries, wq, wk, wv)
 
 
-def flip(value, axis, mask):
+def flip(value, axis, mask=1):
     return lax.ppermute(value, axis, [(i, i ^ mask) for i in range(lax.axis_size(axis))])
+
+
+def ctx_flip(value, mask):
+    if mask == 1:
+        return flip(value, "x")
+    if mask == 2:
+        return flip(value, "l")
+    return flip(value, "hi", mask // 4)
 
 
 def add(left, right):
@@ -752,81 +857,70 @@
 
 
 def after(dep, *values):
-    held = lax.optimization_barrier((dep,) + values)[1:]
+    deps = dep if isinstance(dep, tuple) else (dep,)
+    held = lax.optimization_barrier(deps + values)[len(deps) :]
     return held[0] if len(held) == 1 else held
 
 
+class Stages:
+    def __init__(self, block_order):
+        self.live = block_order[0] >= 0
+
+    def __call__(self, function, *args):
+        shapes = jax.eval_shape(function, *args)
+        empty = lambda *_: jax.tree.map(lambda a: jnp.zeros(a.shape, a.dtype), shapes)
+        return lax.cond(self.live, function, empty, *args)
+
+
+def gather_pair(own):
+    partner = ctx_flip(own, 2)
+    near = jnp.concatenate([own, partner, flip(own, "y"), flip(partner, "y")])
+    return jnp.concatenate([near, flip(near, "core")])
+
+
 def gather_slots(own):
-    near = jnp.concatenate([own, flip(own, "tp", 2)])
-    return jnp.concatenate([near, flip(near, "tp", 1)])
-
-
-def gather_pair(own):
-    partner = flip(own, "ctx", 2)
-    near = jnp.concatenate([own, partner, flip(own, "tp", 2), flip(partner, "tp", 2)])
-    return jnp.concatenate([near, flip(near, "tp", 1)])
-
-
-def gather_rows(own, other, tensor):
+    near = jnp.concatenate([own, flip(own, "y")])
+    return near, flip(near, "core")
+
+
+def place_rows(own, near, core, far, tensor):
     rows = own.shape[0]
-    near = jnp.concatenate([own, other])
-    far = flip(near, "tp", 1)
-    pieces = (near[:rows], near[rows:], far[:rows], far[rows:])
     result = jnp.zeros((SLOTS * rows,) + own.shape[1:], own.dtype)
-    for u in range(SLOTS):
+    for u, piece in enumerate((own, near, core, far)):
         result = lax.dynamic_update_slice_in_dim(
-            result, pieces[u], (tensor ^ SLOT_XOR[u]) * rows, 0
+            result, piece, (tensor ^ SLOT_XOR[u]) * rows, 0
         )
     return result
 
 
 def scatter_slots(keep, send, fill=lambda value: value):
-    got = fill(flip(send, "tp", 1))
+    got = fill(flip(send, "core"))
     quarter = keep.shape[0] // 2
-    far = flip(add(keep[quarter:], got[quarter:]), "tp", 2)
+    far = flip(add(keep[quarter:], got[quarter:]), "y")
     return add(keep[:quarter], got[:quarter]), far
 
 
 def pair_scatter(keep, send, fill=lambda near: near):
-    got = fill(flip(send, "tp", 1))
+    got = fill(flip(send, "core"))
     n = keep.shape[0] // 4
     near = [add(keep[k * n : (k + 1) * n], got[k * n : (k + 1) * n]) for k in range(4)]
-    far = flip(near[3], "tp", 2)
-    got = flip(near[2], "tp", 2)
+    far = flip(near[3], "y")
+    got = flip(near[2], "y")
     return near, far, got
 
 
 def pair_finish(near, far, got):
     away = add(near[1], far)
-    return near[0], got, flip(away, "ctx", 2), away
+    return near[0], got, ctx_flip(away, 2), away
 
 
 def total(terms):
     return sum(term.astype(jnp.float32) for term in terms)
 
 
-def gather_keys(kv_local, ctx_count):
-    parts = {0: kv_local}
-    for bit in reversed(high_masks(ctx_count)):
-        for mask in list(parts):
-            parts[mask + bit] = flip(parts[mask], "ctx", bit)
-    for bit in (2, 1):
-        for mask in list(parts):
-            parts[mask + bit] = flip(parts[mask], "ctx", bit)
-    return [parts[mask] for mask in range(ctx_count)]
-
-
-def all_sum(value, ctx_count):
-    for axis, mask in [("tp", 1), ("tp", 2), ("ctx", 1), ("ctx", 2)] + [
-        ("ctx", mask) for mask in high_masks(ctx_count)
-    ]:
-        value = value + flip(value, axis, mask)
-    return value
-
-
 class Reduce:
     def __init__(self, keep, send):
-        self.keep, self.got = keep, flip(send, "ctx", 1)
+        self.keep, self.got = keep, ctx_flip(send, 1)
 
     def halve(self, mask, ctx, dep=None):
         keep, got = self.keep, self.got
@@ -835,7 +929,7 @@
         n = keep.shape[0] // 2
         bit = lax.div(ctx, mask) % 2
         pick = lambda value, index: lax.dynamic_slice_in_dim(value, index * n, n, 0)
-        away = flip(add(pick(keep, 1 - bit), pick(got, 1 - bit)), "ctx", mask)
+        away = ctx_flip(add(pick(keep, 1 - bit), pick(got, 1 - bit)), mask)
         self.keep, self.got = add(pick(keep, bit), pick(got, bit)), away
 
     def sum(self):
@@ -850,14 +944,15 @@
     return masks
 
 
-def split_halves(reduce, ctx, dep):
-    keep, got = after(dep, reduce.keep, reduce.got)
+def unit_sum_over(shares):
+    return lax.psum_scatter(shares, ("hi", "x"), scatter_dimension=0, tiled=True)
+
+
+def split_halves(summed, ctx, dep):
+    summed = after(dep, summed)
     pair = lax.div(ctx, 2) % 2
-    pick = lambda value, index: lax.dynamic_slice_in_dim(value, index, 1, 0)[0]
-    return (
-        add(pick(keep, pair), pick(got, pair)),
-        add(pick(keep, 1 - pair), pick(got, 1 - pair)),
-    )
+    pick = lambda index: lax.dynamic_index_in_dim(summed, index, 0, keepdims=False)
+    return pick(pair), pick(1 - pair)
 
 
 def join_halves(own, other, ctx):
@@ -867,14 +962,13 @@
 
 
 class KvReduce:
-    def __init__(self, keep, send):
-        self.keep, self.got = keep, flip(send, "ctx", 1)
-
-    def halve(self, mask, dep):
+    def __init__(self, keep, got):
+        self.keep, self.got = keep, got
+
+    def merge(self, dep):
         keep, got = after(dep, self.keep, self.got)
         n = keep.shape[0] // 2
-        away = flip(add(keep[n:], got[n:]), "ctx", mask)
-        self.keep, self.got = add(keep[:n], got[:n]), away
+        return add(keep[:n], got[:n]), add(keep[n:], got[n:])
 
 
 def norm_back(grad_out, normed, inv_scale, gain):
@@ -898,46 +992,55 @@
     block_order,
     cont_prompt,
 ):
-    ctx_count = lax.axis_size("ctx")
-    tp_count = lax.axis_size("tp")
-    ctx, tensor = lax.axis_index("ctx"), lax.axis_index("tp")
+    ctx_count = lax.axis_size("hi") * 4
+    ctx = (lax.axis_index("hi") * 2 + lax.axis_index("l")) * 2 + lax.axis_index("x")
+    tensor = lax.axis_index("y") * 2 + lax.axis_index("core")
     where = jnp.stack([ctx, tensor]).astype(jnp.int32)
     quarter = layer_input.shape[0] // SLOTS
     kv_heads = key_matrix.shape[1] // HEAD_SIZE
     highs = high_masks(ctx_count)
 
+    stage = Stages(block_order)
+    cot_own = lax.dynamic_slice_in_dim(cotangent, tensor * quarter, quarter)
+    cot_slots = slots_of(cotangent, tensor)
     first_input, queries, kv_local, cosine, sine = input_stage(
         layer_input, attn_gain, w_query, key_matrix, value_matrix, block_order, cont_prompt, where
     )
-    cot_own = lax.dynamic_slice_in_dim(cotangent, tensor * quarter, quarter)
-    cot_slots = slots_of(cotangent, tensor)
     parts = {0: kv_local}
+    parts[2], parts[1] = stage(lambda kv: (ctx_flip(kv, 2), ctx_flip(kv, 1)), kv_local)
+    high_parts = {0: after(parts[1], kv_local)}
     for bit in reversed(highs):
-        for mask in list(parts):
-            parts[mask + bit] = flip(parts[mask], "ctx", bit)
-    near_part = flip(kv_local, "ctx", 2)
-    parts[1] = flip(kv_local, "ctx", 1)
-    cot_part = flip(after(near_part, cot_own), "ctx", 2)
-    for mask in [m for m in parts if m >= 4]:
-        parts[mask + 2] = flip(parts[mask], "ctx", 2)
-        parts[mask + 1] = flip(parts[mask], "ctx", 1)
-    parts[2] = near_part
-    parts[3] = flip(near_part, "ctx", 1)
-    for mask in [m for m in list(parts) if m > 4 and m % 4 == 2]:
-        parts[mask + 1] = flip(parts[mask], "ctx", 1)
+        for mask in list(high_parts):
+            high_parts[mask + bit] = ctx_flip(high_parts[mask], bit)
+    del high_parts[0]
+    parts.update(high_parts)
+    parts[3], cot_part = stage(
+        lambda kv, cot: (ctx_flip(kv, 1), ctx_flip(cot, 2)), parts[2], cot_own
+    )
+    dep = parts[3]
+    for mask in high_parts:
+        parts[mask + 2], parts[mask + 1], more = stage(
+            lambda kv, cot: (ctx_flip(kv, 2), ctx_flip(kv, 1), flip(cot, "y")),
+            after(dep, parts[mask]),
+            cot_part,
+        )
+        dep = parts[mask + 1]
+    cot_part = jnp.concatenate([cot_part, more])
+    for mask in high_parts:
+        parts[mask + 3], cot_far = stage(
+            lambda kv, cot: (ctx_flip(kv, 1), flip(cot, "core")), parts[mask + 2], cot_part
+        )
     parts = [parts[mask] for mask in range(ctx_count)]
-    cot_part = jnp.concatenate([cot_part, flip(cot_part, "tp", 2)])
-    cot_far = flip(cot_part, "tp", 1)
     cot = jnp.concatenate(
         [cot_slots[0], cot_part[:quarter], cot_slots[1], cot_part[quarter:]]
         + [cot_slots[2], cot_far[:quarter], cot_slots[3], cot_far[quarter:]]
     )
     mixed, log_total, keep, send = attention_forward(
-        queries, w_out, parts, block_order, cont_prompt, where
-    )
-    first_half = flip(send, "tp", 1)
+        after(cot, queries), w_out, parts, block_order, cont_prompt, where
+    )
+    first_half = flip(send, "core")
     near = add(keep, first_half)
-    far = flip(near[quarter:], "tp", 2)
+    far = flip(near[quarter:], "y")
     grad_hidden = grad_hidden_stage(after(near, cot), w_down, where)
     own_input = lax.dynamic_slice_in_dim(layer_input, tensor * quarter, quarter)
     own_input = own_input.astype(jnp.float32)
@@ -947,40 +1050,37 @@
     second = gather_pair((normed_two * ffn_gain).astype(jnp.bfloat16))
     hidden, grad_gate, grad_up = ffn_stage(second, grad_hidden, w_gate, w_up, where)
 
-    down_shares = weight_shares(
-        "down_shares", (cot,), (hidden,), ((0, 0),), ctx_count, False, where
-    )
-    down = Reduce(*down_shares)
-    grad_gate, grad_up = after(down_shares[0], grad_gate, grad_up)
-    keep, send = unit_sum(
-        grad_second_kernel, "grad_second", (grad_gate, grad_up), (w_gate, w_up), True, where
-    )
-    ffn_halves = unit_sum(
-        ffn_out_kernel, "ffn_out", (after(keep, hidden),), (w_down,), False, where
-    )
-    near, far, got = pair_scatter(keep, send, lambda value: after(ffn_halves[0], value))
-
-    def unit_shares(name, grad, dep):
-        return weight_shares(
-            name, (second,), (after(dep, grad),), ((0, 0),), ctx_count, False, where
+    down_shares = unit_shares("down_shares", cot, hidden, ctx_count, where)
+    down = unit_sum_over(down_shares)
+    grads, weights = after(down_shares, grad_gate, grad_up), (w_gate, w_up)
+    send = grad_second_half(1, "grad_second_send", grads, weights, where)
+
+    def second_stage(send, grad_gate, grad_up, hidden):
+        keep = grad_second_half(0, "grad_second_keep", (grad_gate, grad_up), weights, where)
+        near, far, got = pair_scatter(keep, send)
+        shares = unit_shares("gate_shares", second, after(near[3], grad_gate), ctx_count, where)
+        *terms, away = pair_finish(near, after(shares, far), got)
+        halves = unit_sum(
+            ffn_out_kernel, "ffn_out", (after(away, hidden),), (w_down,), False, where
         )
-
-    gate_shares = unit_shares("gate_shares", grad_gate, near[3])
-    second_terms = pair_finish(near, after(gate_shares[0], far), got)
-    *second_terms, dep = second_terms
-    for mask in highs:
-        down.halve(mask, ctx, dep)
-        dep = down.keep
-    gate = Reduce(*after(dep, *gate_shares))
-    grad_norm_two, ffn_gain_part = norm_back(
-        total(after(dep, *second_terms)), normed_two, inv_two, ffn_gain
-    )
-    grad_middle = cot_own.astype(jnp.float32) + grad_norm_two
-    own_branch = grad_middle.astype(jnp.bfloat16)
-    up_shares = unit_shares("up_shares", grad_up, own_branch)
-    branch_near = jnp.concatenate([own_branch, after(up_shares[0], flip(own_branch, "tp", 2))])
-    grad_branch = jnp.concatenate([branch_near, flip(branch_near, "tp", 1)])
-    backward = []
+        return total(after(halves[0], *terms)), shares, halves
+
+    grad_second, gate_shares, ffn_halves = stage(second_stage, send, *grads, hidden)
+    gate = unit_sum_over(gate_shares)
+
+    def branch_stage(grad_second, grad_up, own):
+        grad_norm, gain_part = norm_back(grad_second, normed_two, inv_two, ffn_gain)
+        grad_middle = own.astype(jnp.float32) + grad_norm
+        branch = grad_middle.astype(jnp.bfloat16)
+        shares = unit_shares("up_shares", second, after(branch, grad_up), ctx_count, where)
+        near = jnp.concatenate([branch, after(shares, flip(branch, "y"))])
+        return grad_middle, gain_part, shares, jnp.concatenate([near, flip(near, "core")])
+
+    grad_middle, ffn_gain_part, up_shares, grad_branch = stage(
+        branch_stage, grad_second, grad_up, cot_own
+    )
+    up = unit_sum_over(up_shares)
+    backward, kv = [], []
     held = grad_branch
     for head in range(kv_heads):
         backward.append(
@@ -989,83 +1089,109 @@
                 block_order, cont_prompt, where,
             )
         )
-        held = after(backward[-1][0], grad_branch)
+        kv.append(KvReduce(backward[-1][1], ctx_flip(backward[-1][2], 1)))
+        dep = backward[-1][0]
+        if head == 0:
+            down_own, down_away = split_halves(down, ctx, dep)
+            down_other = ctx_flip(down_away, 2)
+            dep = down_own
+        held = after(dep, grad_branch)
     grad_queries = [item[0] for item in backward]
-    dep = grad_queries[-1]
-    for mask in highs:
-        gate.halve(mask, ctx, dep)
-        dep = gate.keep
-    kv = [KvReduce(*item[1:]) for item in backward]
-    down_own, down_away = split_halves(down, ctx, dep)
-    down_other = flip(down_away, "ctx", 2)
     branch_shares = weight_shares(
         "branch_shares",
         (first_input, grad_branch),
-        grad_queries + [after(down_own, mixed)],
+        grad_queries + [after(dep, mixed)],
         tuple((0, h) for h in range(kv_heads)) + ((1, kv_heads),),
         ctx_count,
         True,
         where,
     )
-    dep = branch_shares[0]
-    gate_own, gate_away = split_halves(gate, ctx, dep)
+    sum_down = join_halves(down_own, after(branch_shares[0], down_other), ctx).T
+    kv = [item.merge(sum_down) for item in kv]
+    dep = tuple(keep for keep, _ in kv)
+    branch = Reduce(*after(dep, *branch_shares))
+
+    got = [ctx_flip(value, 2) for _, value in kv]
+
+    def out_stage(keep, send):
+        got = flip(send, "core")
+        n = keep.shape[0] // 4
+        near = [add(keep[k * n : (k + 1) * n], got[k * n : (k + 1) * n]) for k in range(4)]
+        return near[0], near[2], add(near[1], flip(near[3], "y"))
+
+    out_near, out_own, out_away = stage(out_stage, *after(dep, *ffn_halves))
+    for mask in highs:
+        kv = [KvReduce(keep, value).merge(out_away) for (keep, _), value in zip(kv, got)]
+        got = [ctx_flip(value, mask) for _, value in kv]
+    out_far, out_got = stage(
+        lambda away, own: (ctx_flip(away, 2), flip(own, "y")),
+        *after(tuple(keep for keep, _ in kv), out_away, out_own),
+    )
+    got = [after(out_far, value) for value in got]
+    kv = [(keep, value) for (keep, _), value in zip(kv, got)]
+    gate_own, gate_away = split_halves(gate, ctx, tuple(got))
+    gate_other = ctx_flip(gate_away, 2)
     dep = gate_own
-    for item in kv:
-        item.halve(2, dep)
-        dep = item.keep
-    up = Reduce(*after(dep, *up_shares))
-    ffn_sums = pair_scatter(*after(dep, *ffn_halves))
-    dep = ffn_sums[0][3]
-    for mask in highs:
-        for item in kv:
-            item.halve(mask, dep)
-            dep = item.keep
-    ffn_terms = pair_finish(ffn_sums[0], *after(dep, *ffn_sums[1:]))
-    got = [after(ffn_terms[3], item.got) for item in kv]
-    for mask in highs:
-        up.halve(mask, ctx, got[-1])
-        dep = up.keep
-    branch = Reduce(*after(dep, *branch_shares))
-    output = (middle + total(after(dep, *ffn_terms[:3]))).astype(jnp.bfloat16)
+    output = (middle + total((out_near, out_got, after(dep, out_far)))).astype(jnp.bfloat16)
     keep, send, grad_kv = tail_stage(
-        [(item.keep, after(dep, value)) for item, value in zip(kv, got)], cosine, sine,
-        grad_queries, w_query, key_matrix, value_matrix, where,
-    )
-    kv_shares = weight_shares(
-        "kv_shares", (first_input,), (after(keep, grad_kv),), ((0, 0),), ctx_count, True, where
-    )
-    first_terms = scatter_slots(keep, send, lambda value: after(kv_shares[0], value))
-    inv_one = lax.rsqrt(jnp.mean(own_input * own_input, axis=-1, keepdims=True) + eps_norm)
-    grad_norm_one, attn_gain_part = norm_back(
-        total(first_terms), own_input * inv_one, inv_one, attn_gain
-    )
-    grad_input = (grad_middle + grad_norm_one).astype(jnp.bfloat16)
-    input_other = flip(grad_input, "tp", 2)
+        [(keep, after(dep, value)) for keep, value in kv], cosine, sine, grad_queries,
+        w_query, key_matrix, value_matrix, where,
+    )
+
+    def first_stage(keep, send, grad_kv, own_input, grad_middle):
+        shares = weight_shares(
+            "kv_shares", (first_input,), (grad_kv,), ((0, 0),), ctx_count, True, where
+        )
+        terms = scatter_slots(keep, send, lambda value: after(shares[0], value))
+        inv = lax.rsqrt(jnp.mean(own_input * own_input, axis=-1, keepdims=True) + eps_norm)
+        grad_norm, gain_part = norm_back(total(terms), own_input * inv, inv, attn_gain)
+        return shares, gain_part, (grad_middle + grad_norm).astype(jnp.bfloat16)
+
+    kv_shares, attn_gain_part, grad_input = stage(
+        first_stage, keep, send, grad_kv, own_input, grad_middle
+    )
+    near = jnp.concatenate([grad_input, after(grad_input, output)])
+    near_other = flip(near, "y")
     branch.halve(2, ctx, grad_input)
     last = Reduce(*after(branch.keep, *kv_shares))
-    up_own, up_away = split_halves(up, ctx, branch.keep)
-    dep = up_own
-    grad_input = gather_rows(grad_input, after(dep, input_other), tensor)
-    gate_other = flip(after(dep, gate_away), "ctx", 2)
-    gains = all_sum(after(dep, jnp.stack([attn_gain_part, ffn_gain_part])), ctx_count)
-    output = gather_rows(output, flip(after(dep, output), "tp", 2), tensor)
-    sum_down = join_halves(down_own, down_other, ctx).T
-    up_other = flip(after(gains, up_away), "ctx", 2)
+    sum_gate = join_halves(gate_own, after(branch.keep, gate_other), ctx)
+    dep = sum_gate
     for mask in highs:
-        branch.halve(mask, ctx, gains)
-    last.halve(2, ctx, branch.keep)
+        branch.halve(mask, ctx, dep)
+        dep = branch.keep
+    last.halve(2, ctx, dep)
+    near = jnp.concatenate([near, after(last.keep, near_other)])
+    far = flip(near, "core")
+    quarters = [near[n * quarter : (n + 1) * quarter] for n in range(4)]
+    quarters += [far[n * quarter : (n + 1) * quarter] for n in range(4)]
+    grad_input, output = [
+        place_rows(quarters[k], quarters[k + 2], quarters[k + 4], quarters[k + 6], tensor)
+        for k in range(2)
+    ]
+    dep = (grad_input, output)
     for mask in highs:
-        last.halve(mask, ctx)
-    sum_gate = join_halves(gate_own, gate_other, ctx)
-    sum_up = join_halves(up_own, up_other, ctx)
-    branch.keep, branch.got = after(last.keep, branch.keep, branch.got)
+        last.halve(mask, ctx, dep)
+        dep = last.keep
+
+    def gain_stage(gains):
+        gains = gains + flip(gains, "core")
+        gains = gains + flip(gains, "y")
+        for mask in [1, 2] + highs:
+            gains = gains + ctx_flip(gains, mask)
+        return gains
+
+    gains = stage(gain_stage, after(dep, jnp.stack([attn_gain_part, ffn_gain_part])))
+    up_own, up_away = split_halves(up, ctx, dep)
+    up_other = ctx_flip(up_away, 2)
+    sum_up = join_halves(up_own, after(gains, up_other), ctx)
+    branch.keep, branch.got = after(gains, branch.keep, branch.got)
     width_q, width_k = w_query.shape[1], key_matrix.shape[1]
     branch_sum, last_sum = branch.sum(), last.sum()
     sum_query, sum_out = branch_sum[:, :width_q], branch_sum[:, width_q:].T
     sum_key, sum_value = last_sum[:, :width_k], last_sum[:, width_k:]
 
-    gains = gains.reshape(2, ctx_count * tp_count, -1)
-    gains = lax.dynamic_index_in_dim(gains, ctx * tp_count + tensor, 1, keepdims=False)
+    gains = gains.reshape(2, ctx_count * SLOTS, -1)
+    gains = lax.dynamic_index_in_dim(gains, ctx * SLOTS + tensor, 1, keepdims=False)
     return (
         output,
         grad_input,
@@ -1082,37 +1208,39 @@
 
 
 def solution(mesh):
+    rows, heads = ("hi", "l", "x"), ("y", "core")
+    split = Mesh(mesh.devices.reshape(-1, 2, 2, 2, 2), rows + heads)
     placed = (
-        P("ctx", None),
+        P(rows, None),
         P(),
-        P(None, "tp"),
-        P(None, "tp"),
-        P(None, "tp"),
-        P("tp", None),
+        P(None, heads),
+        P(None, heads),
+        P(None, heads),
+        P(heads, None),
         P(),
-        P(None, "tp"),
-        P(None, "tp"),
-        P("tp", None),
-        P("ctx", None),
+        P(None, heads),
+        P(None, heads),
+        P(heads, None),
+        P(rows, None),
         P(),
         P(),
     )
     return jax.shard_map(
         body,
-        mesh=mesh,
+        mesh=split,
         in_specs=placed,
         out_specs=(
-            P("ctx", None),
-            P("ctx", None),
-            P(("ctx", "tp")),
-            P("ctx", "tp"),
-            P("ctx", "tp"),
-            P("ctx", "tp"),
-            P("tp", "ctx"),
-            P(("ctx", "tp")),
-            P("ctx", "tp"),
-            P("ctx", "tp"),
-            P("tp", "ctx"),
+            P(rows, None),
+            P(rows, None),
+            P(rows + heads),
+            P(rows, heads),
+            P(rows, heads),
+            P(rows, heads),
+            P(heads, rows),
+            P(rows + heads),
+            P(rows, heads),
+            P(rows, heads),
+            P(heads, rows),
         ),
         check_vma=False,
     )

time: 641 us -> 638 us (level)
  starting transfers between devices: 66.3 us -> 48.6 us
  local copies, waits for them, and re-layouts: 23.5 us -> 40.5 us
  between operations: 1.76 us -> 15.2 us
  other arithmetic: 66.6 us -> 55.7 us
    pallas_call x0 -> x5, Pallas kernels: none -> 49.6 us  [the longest x3 31.5 us: unit_shares(): pl.pallas_call(unit_shares_kernel, out_shape=shares, grid_spec=pltpu.Pref...]
    pallas_call x5 -> x2, Pallas kernels: 53 us -> 16.8 us  [weight_shares(): pl.pallas_call(functools.partial(shares_kernel, len(lefts), swap_bits, pa...]
    ppermute x58 -> x50, starting transfers between devices: 66.3 us -> 48.5 us  [flip(): lax.ppermute(value, axis, [(i, i ^ mask) for i in range(lax.axis_size(axi...]
    pallas_call x2 -> x1, Pallas kernels: 23 us -> 8.66 us  [unit_sum(): pl.pallas_call(kernel, out_shape=(half, half), grid_spec=pltpu.PrefetchSc...]
    convert_element_type x20 -> x12, other arithmetic: 38.7 us -> 25.9 us  [add(): (left.astype(jnp.float32) + right.astype(jnp.float32)).astype(jnp.bfloat16)]
    convert_element_type x1 -> x5, other arithmetic: 1.69 us -> 10.7 us  [the longest x2 3.96 us: total(): return sum((term.astype(jnp.float32) for term in terms))]
    ppermute x58 -> x50, waiting for transfers between devices: 288 us -> 289 us  [flip(): lax.ppermute(value, axis, [(i, i ^ mask) for i in range(lax.axis_size(axi...]
    unnamed x102 -> x78, local copies, waits for them, and re-layouts: 17 us -> 17.7 us
  transfers between devices with their start and end apart: 58 -> 53, of which waited for: 32 -> 35; matrix products, arithmetic and copies ran while one was open for 12% -> 12% of each run, Pallas kernels for 21% -> 19%
where the time goes in v7:
time: 638 us; the launch traced here: 632 us
  waiting for transfers between devices  289 us (45%)
  Pallas kernels  182 us (29%)
  other arithmetic  55.7 us (9%)
  starting transfers between devices  48.6 us (8%)
  local copies, waits for them, and re-layouts  40.5 us (6%)
  between operations  15.2 us (2%)
    ppermute x50, waiting for transfers between devices, flip(): lax.ppermute(value, axis, [(i, i ^ mask) for i in range(lax.axis_size(axi...  289 us
    ppermute x50, starting transfers between devices, flip(): lax.ppermute(value, axis, [(i, i ^ mask) for i in range(lax.axis_size(axi...  48.5 us
    pallas_call x2, Pallas kernels, attention_backward(): pl.pallas_call(functools.partial(backward_kernel, rep, 1, ctx_count, head...  39 us
    pallas_call x3, Pallas kernels, unit_shares(): pl.pallas_call(unit_shares_kernel, out_shape=shares, grid_spec=pltpu.Pref...  31.5 us
    pallas_call x1, Pallas kernels, attention_forward(): pl.pallas_call(functools.partial(forward_kernel, rep, kv_heads, ctx_count...  28.2 us
    convert_element_type x12, other arithmetic, add(): (left.astype(jnp.float32) + right.astype(jnp.float32)).astype(jnp.bfloat16)  25.9 us
    pallas_call x2, Pallas kernels, grad_second_half(): pl.pallas_call(grad_second_kernel, out_shape=jax.ShapeDtypeStruct((rows,...  18.1 us
    unnamed x78, local copies, waits for them, and re-layouts  17.7 us
  transfers between devices with their start and end apart: 53, of which 35 were waited for; matrix products, arithmetic and copies ran while one was open for 12% of the time, Pallas kernels for 19%

profile of v7, /device:TPU:0, one launch (start us, length us, event | category | flops | bytes accessed | tf_op | source)
XLA Modules:
  0.0 631.8 jit_solution(15480499066523228267)
XLA Ops:
  8.0 7.3 %input_stage.1 = (bf16[512,2048]{1,0:T(8,128)(2,1)}, bf16[512,512]{1,0:T(8,128)(2,1)}, bf16[512,512]{1,0:T(8,128)(2,1)S(1)}, f32[512,128]{1,0:T(8,128)}, f32[512,128]{1,0:T(8,128)}) custom-call(s32[32]{0:T(128)} %order_ref.7, s32[8]{0:T(128)} %cont_ref.7, s32[2]{0:T(128)S(1)} %pad_add_fusion.where_ref, f32[1,2048]{1,0:T(1,128)} %bitcast.32, ...), custom_call_target="tpu_custom_call" | custom-call | flops 42949672 | bytes 167772 | tf_op jit(solution)/shard_map/input_stage/pallas_call | solution.py:489
  15.3 16.6 %conditional.10 = (bf16[512,512]{1,0:T(8,128)(2,1)}, bf16[512,512]{1,0:T(8,128)(2,1)}) conditional(s32[]{:T(128)} %bitcast.2, () %tuple.142, bf16[512,512]{1,0:T(8,128)(2,1)S(1)} %get-tuple-element.246.refs_0_), branch_computations={%region_0.0_spmd, %region_1.0_spmd} | conditional | bytes 4194400 | solution.py:872
  19.9 10.5 %collective-permute-done = bf16[512,512]{1,0:T(8,128)(2,1)} collective-permute-done((bf16[512,512]{1,0:T(8,128)(2,1)S(1)}, bf16[512,512]{1,0:T(8,128)(2,1)}, u32[]{:S(2)}, u32[]{:S(2)}) %collective-permute-start) | collective-permute-done | bytes 524320 | tf_op jit(solution)/shard_map/cond/branch_1_fun/ppermute | solution.py:836
  35.6 24.7 %conditional.11 = (bf16[512,512]{1,0:T(8,128)(2,1)}, bf16[128,2048]{1,0:T(8,128)(2,1)}) conditional(s32[]{:T(128)} %bitcast.2, () %tuple.141, (bf16[512,512]{1,0:T(8,128)(2,1)}, bf16[128,2048]{1,0:T(8,128)(2,1)}) %tuple.143), branch_computations={%region_2.0_spmd, %region_3.0_spmd} | conditional | bytes 4194400 | solution.py:872
  37.5 10.6 %collective-permute-done.2 = bf16[512,512]{1,0:T(8,128)(2,1)} collective-permute-done((bf16[512,512]{1,0:T(8,128)(2,1)}, bf16[512,512]{1,0:T(8,128)(2,1)}, u32[]{:S(2)}, u32[]{:S(2)}) %collective-permute-start.2) | collective-permute-done | bytes 524320 | tf_op jit(solution)/shard_map/cond/branch_1_fun/ppermute | solution.py:836
  48.1 12.2 %collective-permute-done.3 = bf16[128,2048]{1,0:T(8,128)(2,1)} collective-permute-done((bf16[128,2048]{1,0:T(8,128)(2,1)}, bf16[128,2048]{1,0:T(8,128)(2,1)}, u32[]{:S(2)}, u32[]{:S(2)}) %collective-permute-start.3) | collective-permute-done | bytes 524320 | tf_op jit(solution)/shard_map/cond/branch_1_fun/ppermute | solution.py:836
  63.0 11.5 %conditional.12 = (bf16[512,512]{1,0:T(8,128)(2,1)}, bf16[512,512]{1,0:T(8,128)(2,1)}, bf16[128,2048]{1,0:T(8,128)(2,1)}) conditional(s32[]{:T(128)} %bitcast.2, () %tuple.144, (bf16[512,512]{1,0:T(8,128)(2,1)S(1)}, bf16[128,2048]{1,0:T(8,128)(2,1)}) %tuple.147), branch_computations={%region_4.0_spmd, %region_5.0_spmd} | conditional | bytes 6291600 | solution.py:872
  65.2 8.9 %collective-permute-done.4 = bf16[512,512]{1,0:T(8,128)(2,1)} collective-permute-done((bf16[512,512]{1,0:T(8,128)(2,1)S(1)}, bf16[512,512]{1,0:T(8,128)(2,1)}, u32[]{:S(2)}, u32[]{:S(2)}) %collective-permute-start.4) | collective-permute-done | bytes 524320 | tf_op jit(solution)/shard_map/cond/branch_1_fun/ppermute | solution.py:836
  77.7 15.1 %conditional.13 = (bf16[512,512]{1,0:T(8,128)(2,1)}, bf16[256,2048]{1,0:T(8,128)(2,1)}, bf16[128,2048]{1,0:T(8,128)(2,1)S(1)}, bf16[128,2048]{1,0:T(8,128)(2,1)S(1)}) conditional(s32[]{:T(128)} %bitcast.2, () %tuple.148, (bf16[512,512]{1,0:T(8,128)(2,1)}, bf16[256,2048]{1,0:T(8,128)(2,1)S(1)}) %tuple.149), branch_computations={%region_6.0_spmd, %region_7.0_spmd} | conditional | bytes 8388720 | solution.py:872
  81.7 10.6 %collective-permute-done.24 = bf16[512,512]{1,0:T(8,128)(2,1)} collective-permute-done((bf16[512,512]{1,0:T(8,128)(2,1)}, bf16[512,512]{1,0:T(8,128)(2,1)}, u32[]{:S(2)}, u32[]{:S(2)}) %collective-permute-start.24) | collective-permute-done | bytes 524320 | tf_op jit(solution)/shard_map/cond/branch_1_fun/ppermute | solution.py:836
  98.3 28.2 %attention_forward.1 = (bf16[512,512]{1,0:T(8,128)(2,1)}, f32[2,4,256]{2,1,0:T(4,128)}, bf16[256,2048]{1,0:T(8,128)(2,1)}, bf16[256,2048]{1,0:T(8,128)(2,1)}) custom-call(s32[32]{0:T(128)} %order_ref.7, s32[8]{0:T(128)} %cont_ref.7, s32[2]{0:T(128)S(1)} %pad_add_fusion.where_ref, bf16[512,512]{1,0:T(8,128)(2,1)} %get-tuple-element.252.q_ref, ...), custom_call_target="tpu_custom_call" | custom-call | flops 64424508 | bytes 167772 | tf_op jit(solution)/shard_map/attention_forward/pallas_call | solution.py:344
  133.6 9.7 %grad_hidden.1.gh_ref = f32[1024,1024]{1,0:T(8,128)} custom-call(s32[2]{0:T(128)S(1)} %pad_add_fusion.where_ref, bf16[1024,2048]{1,0:T(8,128)(2,1)} %constant_dynamic-update-slice_fusion.cot_ref.left_ref, bf16[2048,2048]{1,0:T(8,128)(2,1)} %wd_ref.1), custom_call_target="tpu_custom_call" | custom-call | flops 68719476736 | bytes 134217728 | tf_op jit(solution)/shard_map/grad_hidden/pallas_call | solution.py:547
  150.2 11.5 %collective-permute-done.29 = bf16[128,2048]{1,0:T(8,128)(2,1)S(1)} collective-permute-done((bf16[128,2048]{1,0:T(8,128)(2,1)S(1)}, bf16[128,2048]{1,0:T(8,128)(2,1)S(1)}, u32[]{:S(2)}, u32[]{:S(2)}) %collective-permute-start.29) | collective-permute-done | bytes 524320 | tf_op jit(solution)/shard_map/ppermute | solution.py:836
  163.2 10.6 %collective-permute-done.31 = bf16[128,2048]{1,0:T(8,128)(2,1)S(1)} collective-permute-done((bf16[128,2048]{1,0:T(8,128)(2,1)S(1)}, bf16[128,2048]{1,0:T(8,128)(2,1)S(1)}, u32[]{:S(2)}, u32[]{:S(2)}) %collective-permute-start.31) | collective-permute-done | bytes 524320 | tf_op jit(solution)/shard_map/ppermute | solution.py:836
  179.8 15.6 %ffn_stage.1 = (bf16[1024,1024]{1,0:T(8,128)(2,1)}, bf16[1024,1024]{1,0:T(8,128)(2,1)}, bf16[1024,1024]{1,0:T(8,128)(2,1)S(1)}) custom-call(s32[2]{0:T(128)S(1)} %pad_add_fusion.where_ref, bf16[1024,2048]{1,0:T(8,128)(2,1)} %constant_dynamic-update-slice_fusion.5.in_ref, f32[1024,1024]{1,0:T(8,128)} %grad_hidden.1.gh_ref, bf16[2048,2048]{1,0:T(8,128)(2,1)} %wg_ref.3, ...), custom_call_target="tpu_custom_call" | custom-call | flops 171798688 | bytes 251658 | tf_op jit(solution)/shard_map/ffn_stage/pallas_call | solution.py:586
  195.5 10.7 %down_shares.1 = bf16[8,256,1024]{2,1,0:T(8,128)(2,1)} custom-call(s32[2]{0:T(128)S(1)} %pad_add_fusion.where_ref, bf16[1024,2048]{1,0:T(8,128)(2,1)} %constant_dynamic-update-slice_fusion.cot_ref.left_ref, bf16[1024,1024]{1,0:T(8,128)(2,1)} %get-tuple-element.259.right_ref), custom_call_target="tpu_custom_call" | custom-call | flops 85899344 | bytes 167772 | tf_op jit(solution)/shard_map/down_shares/pallas_call | solution.py:766
  206.3 9.2 %grad_second_send.1 = bf16[512,2048]{1,0:T(8,128)(2,1)} custom-call(s32[2]{0:T(128)S(1)} %pad_add_fusion.where_ref, bf16[1024,1024]{1,0:T(8,128)(2,1)} %get-tuple-element.262.gg_ref, bf16[1024,1024]{1,0:T(8,128)(2,1)S(1)} %get-tuple-element.263.gu_ref, bf16[2048,2048]{1,0:T(8,128)(2,1)} %wg_ref.3, bf16[2048,2048]{1,0:T(8,128)(2,1)} %wu_ref.3), custom_call_target="tpu_custom_call" | custom-call | flops 85899344 | bytes 83886 | tf_op jit(solution)/shard_map/grad_second_send/pallas_call | solution.py:618
  215.5 58.8 %conditional.14 = (f32[128,2048]{1,0:T(8,128)}, bf16[8,256,1024]{2,1,0:T(8,128)(2,1)}, bf16[512,2048]{1,0:T(8,128)(2,1)}, bf16[512,2048]{1,0:T(8,128)(2,1)}) conditional(s32[]{:T(128)} %bitcast.2, () %tuple.153, (s32[2]{0:T(128)S(1)}, bf16[1024,1024]{1,0:T(8,128)(2,1)}, bf16[1024,1024]{1,0:T(8,128)(2,1)S(1)}, bf16[2048,2048]{1,0:T(8,128)(2,1)}, ...), branch_computations={%region_9.0_spmd, %region_10.0_spmd} | conditional | flops 206164983808 | bytes 359661760 | solution.py:872
  216.0 8.9 %grad_second_keep.1 = bf16[512,2048]{1,0:T(8,128)(2,1)} custom-call(s32[2]{0:T(128)S(1)} %get-tuple-element.87.where_ref, bf16[1024,1024]{1,0:T(8,128)(2,1)} %get-tuple-element.94.gg_ref.right_ref, bf16[1024,1024]{1,0:T(8,128)(2,1)S(1)} %get-tuple-element.89.gu_ref, bf16[2048,2048]{1,0:T(8,128)(2,1)} %get-tuple-element.90.wg_ref, ...), custom_call_target="tpu_custom_call" | custom-call | flops 68719476736 | bytes 67108864 | tf_op jit(solution)/shard_map/cond/branch_1_fun/grad_second_keep/pallas_call | solution.py:618
  230.2 10.8 %gate_shares.1 = bf16[8,256,1024]{2,1,0:T(8,128)(2,1)} custom-call(s32[2]{0:T(128)S(1)} %get-tuple-element.87.where_ref, bf16[1024,2048]{1,0:T(8,128)(2,1)} %get-tuple-element.93.left_ref, bf16[1024,1024]{1,0:T(8,128)(2,1)} %get-tuple-element.94.gg_ref.right_ref), custom_call_target="tpu_custom_call" | custom-call | flops 68719476736 | bytes 134217728 | tf_op jit(solution)/shard_map/cond/branch_1_fun/gate_shares/pallas_call | solution.py:766
  246.5 8.7 %ffn_out.1 = (bf16[512,2048]{1,0:T(8,128)(2,1)}, bf16[512,2048]{1,0:T(8,128)(2,1)}) custom-call(s32[2]{0:T(128)S(1)} %get-tuple-element.87.where_ref, bf16[1024,1024]{1,0:T(8,128)(2,1)} %get-tuple-element.97.hid_ref, bf16[2048,2048]{1,0:T(8,128)(2,1)} %get-tuple-element.98.wd_ref), custom_call_target="tpu_custom_call" | custom-call | flops 68719476736 | bytes 134217728 | tf_op jit(solution)/shard_map/cond/branch_1_fun/ffn_out/pallas_call | solution.py:651
  255.2 16.9 %collective-permute-done.17 = bf16[128,2048]{1,0:T(8,128)(2,1)} collective-permute-done((bf16[128,2048]{1,0:T(8,128)(2,1)}, bf16[128,2048]{1,0:T(8,128)(2,1)}, u32[]{:S(2)}, u32[]{:S(2)}) %collective-permute-start.17) | collective-permute-done | bytes 524320 | tf_op jit(solution)/shard_map/cond/branch_1_fun/ppermute | solution.py:836
  275.5 20.9 %conditional.15 = (f32[128,2048]{1,0:T(8,128)}, bf16[8,256,1024]{2,1,0:T(8,128)(2,1)}, bf16[512,2048]{1,0:T(8,128)(2,1)S(1)}, f32[1,2048]{1,0:T(1,128)S(1)}) conditional(s32[]{:T(128)} %bitcast.2, () %tuple.140, (bf16[128,2048]{1,0:T(8,128)(2,1)}, f32[128]{0:T(128)S(1)}, f32[2048]{0:T(1024)S(1)}, f32[128,2048]{1,0:T(8,128)}, ...), branch_computations={%region_11.0_spmd, %region_12.15_spmd} | conditional | flops 68731011072 | bytes 153119328 | solution.py:872
  279.6 9.9 %up_shares.1 = bf16[8,256,1024]{2,1,0:T(8,128)(2,1)} custom-call(s32[2]{0:T(128)S(1)} %get-tuple-element.109.where_ref, bf16[1024,2048]{1,0:T(8,128)(2,1)} %get-tuple-element.110.left_ref, bf16[1024,1024]{1,0:T(8,128)(2,1)S(1)} %get-tuple-element.112.right_ref), custom_call_target="tpu_custom_call" | custom-call | flops 68719476736 | bytes 134217728 | tf_op jit(solution)/shard_map/cond/branch_1_fun/up_shares/pallas_call | solution.py:766
  296.4 19.5 %attention_backward_0.1 = (bf16[512,256]{1,0:T(8,128)(2,1)}, bf16[2048,256]{1,0:T(8,128)(2,1)}, bf16[2048,256]{1,0:T(8,128)(2,1)}) custom-call(s32[32]{0:T(128)} %order_ref.7, s32[8]{0:T(128)} %cont_ref.7, s32[2]{0:T(128)S(1)} %pad_add_fusion.where_ref, bf16[512,512]{1,0:T(8,128)(2,1)} %get-tuple-element.252.q_ref, ...), custom_call_target="tpu_custom_call" | custom-call | flops 64424508 | bytes 125829 | tf_op jit(solution)/shard_map/attention_backward_0/pallas_call | solution.py:380
  318.3 19.6 %attention_backward_1.1 = (bf16[512,256]{1,0:T(8,128)(2,1)}, bf16[2048,256]{1,0:T(8,128)(2,1)}, bf16[2048,256]{1,0:T(8,128)(2,1)}) custom-call(s32[32]{0:T(128)} %order_ref.7, s32[8]{0:T(128)} %cont_ref.7, s32[2]{0:T(128)S(1)} %pad_add_fusion.where_ref, bf16[512,512]{1,0:T(8,128)(2,1)} %get-tuple-element.252.q_ref, ...), custom_call_target="tpu_custom_call" | custom-call | flops 64424508 | bytes 125829 | tf_op jit(solution)/shard_map/attention_backward_1/pallas_call | solution.py:380
  339.1 9.1 %branch_shares.1 = (bf16[4,256,1024]{2,1,0:T(8,128)(2,1)}, bf16[4,256,1024]{2,1,0:T(8,128)(2,1)}) custom-call(s32[2]{0:T(128)S(1)} %pad_add_fusion.where_ref, bf16[512,2048]{1,0:T(8,128)(2,1)} %get-tuple-element.239.refs_0_, bf16[512,2048]{1,0:T(8,128)(2,1)S(1)} %get-tuple-element.272.gb_ref.refs_1_, bf16[512,256]{1,0:T(8,128)(2,1)} %get-tuple-element.270.refs_2_.refs_6_, ...), custom_call_target="tpu_custom_call" | custom-call | flops 42949672 | bytes 83886 | tf_op jit(solution)/shard_map/branch_shares/pallas_call | solution.py:722
  349.5 5.8 collective-permute-done.34
  355.3 33.4 %collective-permute-done.35 = bf16[2048,256]{1,0:T(8,128)(2,1)} collective-permute-done((bf16[2048,256]{1,0:T(8,128)(2,1)}, bf16[2048,256]{1,0:T(8,128)(2,1)}, u32[]{:S(2)}, u32[]{:S(2)}) %collective-permute-start.35) | collective-permute-done | bytes 1048608 | tf_op jit(solution)/shard_map/ppermute | solution.py:836
  394.2 22.5 %conditional.16 = (bf16[128,2048]{1,0:T(8,128)(2,1)S(1)}, bf16[128,2048]{1,0:T(8,128)(2,1)S(1)}, f32[128,2048]{1,0:T(8,128)}) conditional(s32[]{:T(128)} %bitcast.2, () %tuple.139, (bf16[512,2048]{1,0:T(8,128)(2,1)}, bf16[512,2048]{1,0:T(8,128)(2,1)}) %tuple.164), branch_computations={%region_16.17_spmd, %region_17.0_spmd} | conditional | flops 5505024 | bytes 17825896 | solution.py:872
  394.2 4.4 collective-permute-done.18
  401.8 13.7 %collective-permute-done.19 = bf16[128,2048]{1,0:T(8,128)(2,1)S(1)} collective-permute-done((bf16[128,2048]{1,0:T(8,128)(2,1)S(1)}, bf16[128,2048]{1,0:T(8,128)(2,1)S(1)}, u32[]{:S(2)}, u32[]{:S(2)}) %collective-permute-start.19) | collective-permute-done | bytes 524320 | tf_op jit(solution)/shard_map/cond/branch_1_fun/ppermute | solution.py:836
  416.8 18.1 %collective-permute-done.36 = bf16[1024,256]{1,0:T(8,128)(2,1)} collective-permute-done((bf16[1024,256]{1,0:T(8,128)(2,1)}, bf16[1024,256]{1,0:T(8,128)(2,1)}, u32[]{:S(2)}, u32[]{:S(2)}) %collective-permute-start.36) | collective-permute-done | bytes 524320 | tf_op jit(solution)/shard_map/ppermute | solution.py:836
  441.6 27.6 %conditional.17 = (bf16[128,2048]{1,0:T(8,128)(2,1)}, f32[128,2048]{1,0:T(8,128)}) conditional(s32[]{:T(128)} %bitcast.2, () %tuple.166, (bf16[128,2048]{1,0:T(8,128)(2,1)}, bf16[128,2048]{1,0:T(8,128)(2,1)}) %tuple.255), branch_computations={%region_18.19_spmd, %region_19.20_spmd} | conditional | flops 262144 | bytes 5767264 | solution.py:872
  444.5 7.7 %collective-permute-done.8 = bf16[128,2048]{1,0:T(8,128)(2,1)S(1)} collective-permute-done((bf16[128,2048]{1,0:T(8,128)(2,1)}, bf16[128,2048]{1,0:T(8,128)(2,1)S(1)}, u32[]{:S(2)}, u32[]{:S(2)}) %collective-permute-start.8) | collective-permute-done | bytes 524320 | tf_op jit(solution)/shard_map/cond/branch_1_fun/ppermute | solution.py:836
  453.3 15.9 %collective-permute-done.7 = bf16[128,2048]{1,0:T(8,128)(2,1)} collective-permute-done((bf16[128,2048]{1,0:T(8,128)(2,1)}, bf16[128,2048]{1,0:T(8,128)(2,1)}, u32[]{:S(2)}, u32[]{:S(2)}) %collective-permute-start.7) | collective-permute-done | bytes 524320 | tf_op jit(solution)/shard_map/cond/branch_1_fun/ppermute | solution.py:836
  472.1 6.7 %tail_stage.1 = (bf16[256,2048]{1,0:T(8,128)(2,1)}, bf16[256,2048]{1,0:T(8,128)(2,1)}, bf16[512,512]{1,0:T(8,128)(2,1)}) custom-call(s32[2]{0:T(128)S(1)} %pad_add_fusion.where_ref, bf16[512,256]{1,0:T(8,128)(2,1)} %get-tuple-element.408.refs_0_, bf16[512,256]{1,0:T(8,128)(2,1)} %copy-done.28, bf16[512,256]{1,0:T(8,128)(2,1)} %get-tuple-element.406.refs_2_, ...), custom_call_target="tpu_custom_call" | custom-call | flops 42949672 | bytes 167772 | tf_op jit(solution)/shard_map/tail_stage/pallas_call | solution.py:818
  478.8 30.4 %conditional.18 = (bf16[4,256,512]{2,1,0:T(8,128)(2,1)}, bf16[4,256,512]{2,1,0:T(8,128)(2,1)}, bf16[128,2048]{1,0:T(8,128)(2,1)S(1)}, f32[1,2048]{1,0:T(1,128)S(1)}) conditional(s32[]{:T(128)} %bitcast.2, () %tuple.138, (s32[2]{0:T(128)S(1)}, bf16[512,2048]{1,0:T(8,128)(2,1)}, bf16[512,512]{1,0:T(8,128)(2,1)}, f32[128,2048]{1,0:T(8,128)S(1)}, ...), branch_computations={%region_21.22_spmd, %region_22.26_spmd} | conditional | flops 17188517888 | bytes 87061128 | solution.py:872
  478.9 7.7 %kv_shares.1 = (bf16[4,256,512]{2,1,0:T(8,128)(2,1)}, bf16[4,256,512]{2,1,0:T(8,128)(2,1)}) custom-call(s32[2]{0:T(128)S(1)} %get-tuple-element.118.where_ref, bf16[512,2048]{1,0:T(8,128)(2,1)} %get-tuple-element.119.refs_0_, bf16[512,512]{1,0:T(8,128)(2,1)} %get-tuple-element.120.refs_1_), custom_call_target="tpu_custom_call" | custom-call | flops 17179869184 | bytes 67108864 | tf_op jit(solution)/shard_map/cond/branch_1_fun/kv_shares/pallas_call | solution.py:722
  488.0 5.2 collective-permute-start.21
  493.4 12.5 %collective-permute-done.21 = bf16[128,2048]{1,0:T(8,128)(2,1)S(1)} collective-permute-done((bf16[128,2048]{1,0:T(8,128)(2,1)S(1)}, bf16[128,2048]{1,0:T(8,128)(2,1)S(1)}, u32[]{:S(2)}, u32[]{:S(2)}) %collective-permute-start.21) | collective-permute-done | bytes 524320 | tf_op jit(solution)/shard_map/cond/branch_1_fun/ppermute | solution.py:836
  509.3 4.7 add_convert_fusion.13
  524.4 15.0 %collective-permute-done.42 = bf16[2,256,1024]{2,1,0:T(8,128)(2,1)} collective-permute-done((bf16[2,256,1024]{2,1,0:T(8,128)(2,1)}, bf16[2,256,1024]{2,1,0:T(8,128)(2,1)}, u32[]{:S(2)}, u32[]{:S(2)}) %collective-permute-start.42) | collective-permute-done | bytes 1048608 | tf_op jit(solution)/shard_map/ppermute | solution.py:836
  557.1 8.8 %collective-permute-done.46 = bf16[2,256,512]{2,1,0:T(8,128)(2,1)S(1)} collective-permute-done((bf16[2,256,512]{2,1,0:T(8,128)(2,1)S(1)}, bf16[2,256,512]{2,1,0:T(8,128)(2,1)S(1)}, u32[]{:S(2)}, u32[]{:S(2)}) %collective-permute-start.46) | collective-permute-done | bytes 524320 | tf_op jit(solution)/shard_map/ppermute | solution.py:836
  571.5 21.0 %collective-permute-done.48 = bf16[1,256,512]{2,1,0:T(8,128)(2,1)S(1)} collective-permute-done((bf16[1,256,512]{2,1,0:T(8,128)(2,1)S(1)}, bf16[1,256,512]{2,1,0:T(8,128)(2,1)S(1)}, u32[]{:S(2)}, u32[]{:S(2)}) %collective-permute-start.48) | collective-permute-done | bytes 262176 | tf_op jit(solution)/shard_map/ppermute | solution.py:836
  594.7 25.2 %conditional.19 = (f32[2,2048]{1,0:T(2,128)S(1)}) conditional(s32[]{:T(128)} %bitcast.2, () %tuple.185, f32[2,2048]{1,0:T(2,128)S(1)} %pad_maximum_fusion.6), branch_computations={%region_26.27_spmd, %region_27.28_spmd} | conditional | flops 20480 | bytes 573648 | solution.py:872
  605.6 9.6 %collective-permute-done.12 = f32[2,2048]{1,0:T(2,128)S(1)} collective-permute-done((f32[2,2048]{1,0:T(2,128)S(1)}, f32[2,2048]{1,0:T(2,128)S(1)}, u32[]{:S(2)}, u32[]{:S(2)}) %collective-permute-start.12) | collective-permute-done | bytes 16416 | tf_op jit(solution)/shard_map/cond/branch_1_fun/ppermute | solution.py:836
  615.3 4.6 collective-permute-done.13
  (233 shorter events, 161.9 us)
Async XLA Ops:
  7.2 308.8 %reduce-scatter.4.cloned.1.call-start = ((), (), s32[]{:S(2)}) async-start(), calls=%async_computation.3 | async-start | bytes 5242880 | tf_op jit(solution)/shard_map/reduce_scatter | solution.py:948
  15.3 15.1 %collective-permute-start = (bf16[512,512]{1,0:T(8,128)(2,1)S(1)}, bf16[512,512]{1,0:T(8,128)(2,1)}, u32[]{:S(2)}, u32[]{:S(2)}) collective-permute-start(bf16[512,512]{1,0:T(8,128)(2,1)S(1)} %param.1), channel_id=1, source_target_pairs={{0,8},{8,0},{1,9},{9,1},{2,10},{10,2},{3,11},{11,3},{4,12},{12,4},... | collective-permute-start | bytes 1572872 | tf_op jit(solution)/shard_map/cond/branch_1_fun/ppermute | solution.py:836
  18.4 13.5 %collective-permute-start.1 = (bf16[512,512]{1,0:T(8,128)(2,1)S(1)}, bf16[512,512]{1,0:T(8,128)(2,1)}, u32[]{:S(2)}, u32[]{:S(2)}) collective-permute-start(bf16[512,512]{1,0:T(8,128)(2,1)S(1)} %param.1), channel_id=1, source_target_pairs={{0,4},{4,0},{1,5},{5,1},{2,6},{6,2},{3,7},{7,3},{8,12},{12,8},{9,1... | collective-permute-start | bytes 1572872 | tf_op jit(solution)/shard_map/cond/branch_1_fun/ppermute | solution.py:836
  31.9 31.2 %collective-permute-start.26 = (bf16[512,512]{1,0:T(8,128)(2,1)S(1)}, bf16[512,512]{1,0:T(8,128)(2,1)S(1)}, u32[]{:S(2)}, u32[]{:S(2)}) collective-permute-start(bf16[512,512]{1,0:T(8,128)(2,1)S(1)} %get-tuple-element.246.refs_0_), channel_id=1, source_target_pairs={{0,16},{16,0},{1,17},{17,1},{2,18},{18,2},{3,19},{19,3},{4,20},{20... | collective-permute-start | bytes 1572872 | tf_op jit(solution)/shard_map/ppermute | solution.py:836
  35.6 12.5 %collective-permute-start.2 = (bf16[512,512]{1,0:T(8,128)(2,1)}, bf16[512,512]{1,0:T(8,128)(2,1)}, u32[]{:S(2)}, u32[]{:S(2)}) collective-permute-start(bf16[512,512]{1,0:T(8,128)(2,1)} %get-tuple-element.81), channel_id=1, source_target_pairs={{0,4},{4,0},{1,5},{5,1},{2,6},{6,2},{3,7},{7,3},{8,12},{12,8},{9,1... | collective-permute-start | bytes 1572872 | tf_op jit(solution)/shard_map/cond/branch_1_fun/ppermute | solution.py:836
  37.1 23.3 %collective-permute-start.3 = (bf16[128,2048]{1,0:T(8,128)(2,1)}, bf16[128,2048]{1,0:T(8,128)(2,1)}, u32[]{:S(2)}, u32[]{:S(2)}) collective-permute-start(bf16[128,2048]{1,0:T(8,128)(2,1)} %get-tuple-element.82), channel_id=1, source_target_pairs={{0,8},{8,0},{1,9},{9,1},{2,10},{10,2},{3,11},{11,3},{4,12},{12,4},... | collective-permute-start | bytes 1572872 | tf_op jit(solution)/shard_map/cond/branch_1_fun/ppermute | solution.py:836
  63.0 11.1 %collective-permute-start.4 = (bf16[512,512]{1,0:T(8,128)(2,1)S(1)}, bf16[512,512]{1,0:T(8,128)(2,1)}, u32[]{:S(2)}, u32[]{:S(2)}) collective-permute-start(bf16[512,512]{1,0:T(8,128)(2,1)S(1)} %get-tuple-element.83), channel_id=1, source_target_pairs={{0,8},{8,0},{1,9},{9,1},{2,10},{10,2},{3,11},{11,3},{4,12},{12,4},... | collective-permute-start | bytes 1572872 | tf_op jit(solution)/shard_map/cond/branch_1_fun/ppermute | solution.py:836
  63.1 11.2 %collective-permute-start.5 = (bf16[512,512]{1,0:T(8,128)(2,1)S(1)}, bf16[512,512]{1,0:T(8,128)(2,1)}, u32[]{:S(2)}, u32[]{:S(2)}) collective-permute-start(bf16[512,512]{1,0:T(8,128)(2,1)S(1)} %get-tuple-element.83), channel_id=1, source_target_pairs={{0,4},{4,0},{1,5},{5,1},{2,6},{6,2},{3,7},{7,3},{8,12},{12,8},{9,1... | collective-permute-start | bytes 1572872 | tf_op jit(solution)/shard_map/cond/branch_1_fun/ppermute | solution.py:836
  63.7 10.8 %collective-permute-start.6 = (bf16[128,2048]{1,0:T(8,128)(2,1)}, bf16[128,2048]{1,0:T(8,128)(2,1)}, u32[]{:S(2)}, u32[]{:S(2)}) collective-permute-start(bf16[128,2048]{1,0:T(8,128)(2,1)} %get-tuple-element.84), channel_id=1, source_target_pairs={{0,2},{2,0},{1,3},{3,1},{4,6},{6,4},{5,7},{7,5},{8,10},{10,8},{9,1... | collective-permute-start | bytes 1572872 | tf_op jit(solution)/shard_map/cond/branch_1_fun/ppermute | solution.py:836
  77.7 14.7 %collective-permute-start.24 = (bf16[512,512]{1,0:T(8,128)(2,1)}, bf16[512,512]{1,0:T(8,128)(2,1)}, u32[]{:S(2)}, u32[]{:S(2)}) collective-permute-start(bf16[512,512]{1,0:T(8,128)(2,1)} %get-tuple-element.85), channel_id=1, source_target_pairs={{0,4},{4,0},{1,5},{5,1},{2,6},{6,2},{3,7},{7,3},{8,12},{12,8},{9,1... | collective-permute-start | bytes 1572872 | tf_op jit(solution)/shard_map/cond/branch_1_fun/ppermute | solution.py:836
  132.0 14.2 %collective-permute-start.28 = (bf16[128,2048]{1,0:T(8,128)(2,1)}, bf16[128,2048]{1,0:T(8,128)(2,1)S(1)}, u32[]{:S(2)}, u32[]{:S(2)}) collective-permute-start(bf16[128,2048]{1,0:T(8,128)(2,1)} %slice.213), channel_id=1, source_target_pairs={{0,2},{2,0},{1,3},{3,1},{4,6},{6,4},{5,7},{7,5},{8,10},{10,8},{9,1... | collective-permute-start | bytes 1572872 | tf_op jit(solution)/shard_map/ppermute | solution.py:836
  148.5 13.1 %collective-permute-start.29 = (bf16[128,2048]{1,0:T(8,128)(2,1)S(1)}, bf16[128,2048]{1,0:T(8,128)(2,1)S(1)}, u32[]{:S(2)}, u32[]{:S(2)}) collective-permute-start(bf16[128,2048]{1,0:T(8,128)(2,1)S(1)} %get-tuple-element.370), channel_id=1, source_target_pairs={{0,8},{8,0},{1,9},{9,1},{2,10},{10,2},{3,11},{11,3},{4,12},{12,4},... | collective-permute-start | bytes 1572872 | tf_op jit(solution)/shard_map/ppermute | solution.py:836
  148.5 14.7 %collective-permute-start.30 = (bf16[128,2048]{1,0:T(8,128)(2,1)S(1)}, bf16[128,2048]{1,0:T(8,128)(2,1)S(1)}, u32[]{:S(2)}, u32[]{:S(2)}) collective-permute-start(bf16[128,2048]{1,0:T(8,128)(2,1)S(1)} %get-tuple-element.370), channel_id=1, source_target_pairs={{0,2},{2,0},{1,3},{3,1},{4,6},{6,4},{5,7},{7,5},{8,10},{10,8},{9,1... | collective-permute-start | bytes 1572872 | tf_op jit(solution)/shard_map/ppermute | solution.py:836
  161.7 12.2 %collective-permute-start.31 = (bf16[128,2048]{1,0:T(8,128)(2,1)S(1)}, bf16[128,2048]{1,0:T(8,128)(2,1)S(1)}, u32[]{:S(2)}, u32[]{:S(2)}) collective-permute-start(bf16[128,2048]{1,0:T(8,128)(2,1)S(1)} %collective-permute-done.29), channel_id=1, source_target_pairs={{0,2},{2,0},{1,3},{3,1},{4,6},{6,4},{5,7},{7,5},{8,10},{10,8},{9,1... | collective-permute-start | bytes 1572872 | tf_op jit(solution)/shard_map/ppermute | solution.py:836
  174.1 4.2 collective-permute-start.32
  206.2 263.0 %reduce-scatter.6.cloned.1.call-start = ((), (), s32[]{:S(2)}) async-start(), calls=%async_computation.4 | async-start | bytes 5242880 | tf_op jit(solution)/shard_map/reduce_scatter | solution.py:948
  215.6 9.3 %collective-permute-start.14 = (bf16[512,2048]{1,0:T(8,128)(2,1)}, bf16[512,2048]{1,0:T(8,128)(2,1)}, u32[]{:S(2)}, u32[]{:S(2)}) collective-permute-start(bf16[512,2048]{1,0:T(8,128)(2,1)} %get-tuple-element.92), channel_id=1, source_target_pairs={{0,1},{1,0},{2,3},{3,2},{4,5},{5,4},{6,7},{7,6},{8,9},{9,8},{10,11... | collective-permute-start | bytes 6291464 | tf_op jit(solution)/shard_map/cond/branch_1_fun/ppermute | solution.py:836
  228.2 15.1 %collective-permute-start.15 = (bf16[128,2048]{1,0:T(8,128)(2,1)}, bf16[128,2048]{1,0:T(8,128)(2,1)}, u32[]{:S(2)}, u32[]{:S(2)}) collective-permute-start(bf16[128,2048]{1,0:T(8,128)(2,1)} %get-tuple-element.378), channel_id=1, source_target_pairs={{0,2},{2,0},{1,3},{3,1},{4,6},{6,4},{5,7},{7,5},{8,10},{10,8},{9,1... | collective-permute-start | bytes 1572872 | tf_op jit(solution)/shard_map/cond/branch_1_fun/ppermute | solution.py:836
  229.9 25.3 %collective-permute-start.16 = (bf16[128,2048]{1,0:T(8,128)(2,1)S(1)}, bf16[128,2048]{1,0:T(8,128)(2,1)S(1)}, u32[]{:S(2)}, u32[]{:S(2)}) collective-permute-start(bf16[128,2048]{1,0:T(8,128)(2,1)S(1)} %get-tuple-element.376), channel_id=1, source_target_pairs={{0,2},{2,0},{1,3},{3,1},{4,6},{6,4},{5,7},{7,5},{8,10},{10,8},{9,1... | collective-permute-start | bytes 1572872 | tf_op jit(solution)/shard_map/cond/branch_1_fun/ppermute | solution.py:836
  245.7 26.3 %collective-permute-start.17 = (bf16[128,2048]{1,0:T(8,128)(2,1)}, bf16[128,2048]{1,0:T(8,128)(2,1)}, u32[]{:S(2)}, u32[]{:S(2)}) collective-permute-start(bf16[128,2048]{1,0:T(8,128)(2,1)} %add_convert_fusion.2), channel_id=1, source_target_pairs={{0,8},{8,0},{1,9},{9,1},{2,10},{10,2},{3,11},{11,3},{4,12},{12,4},... | collective-permute-start | bytes 1572872 | tf_op jit(solution)/shard_map/cond/branch_1_fun/ppermute | solution.py:836
  274.3 319.2 %reduce-scatter.8.cloned.1.call-start = ((), (), s32[]{:S(2)}) async-start(), calls=%async_computation.5 | async-start | bytes 5242880 | tf_op jit(solution)/shard_map/reduce_scatter | solution.py:948
  279.6 13.8 %collective-permute-start.22 = (bf16[128,2048]{1,0:T(8,128)(2,1)S(1)}, bf16[128,2048]{1,0:T(8,128)(2,1)S(1)}, u32[]{:S(2)}, u32[]{:S(2)}) collective-permute-start(bf16[128,2048]{1,0:T(8,128)(2,1)S(1)} %get-tuple-element.365), channel_id=1, source_target_pairs={{0,2},{2,0},{1,3},{3,1},{4,6},{6,4},{5,7},{7,5},{8,10},{10,8},{9,1... | collective-permute-start | bytes 1572872 | tf_op jit(solution)/shard_map/cond/branch_1_fun/ppermute | solution.py:836
  318.3 29.8 %collective-permute-start.33 = (bf16[256,1024]{1,0:T(8,128)(2,1)}, bf16[256,1024]{1,0:T(8,128)(2,1)}, u32[]{:S(2)}, u32[]{:S(2)}) collective-permute-start(bf16[256,1024]{1,0:T(8,128)(2,1)} %get-tuple-element.411), channel_id=1, source_target_pairs={{0,8},{8,0},{1,9},{9,1},{2,10},{10,2},{3,11},{11,3},{4,12},{12,4},... | collective-permute-start | bytes 1572872 | tf_op jit(solution)/shard_map/ppermute | solution.py:836
  318.3 37.0 %collective-permute-start.34 = (bf16[2048,256]{1,0:T(8,128)(2,1)}, bf16[2048,256]{1,0:T(8,128)(2,1)}, u32[]{:S(2)}, u32[]{:S(2)}) collective-permute-start(bf16[2048,256]{1,0:T(8,128)(2,1)} %get-tuple-element.278), channel_id=1, source_target_pairs={{0,4},{4,0},{1,5},{5,1},{2,6},{6,2},{3,7},{7,3},{8,12},{12,8},{9,1... | collective-permute-start | bytes 3145736 | tf_op jit(solution)/shard_map/ppermute | solution.py:836
  337.9 50.8 %collective-permute-start.35 = (bf16[2048,256]{1,0:T(8,128)(2,1)}, bf16[2048,256]{1,0:T(8,128)(2,1)}, u32[]{:S(2)}, u32[]{:S(2)}) collective-permute-start(bf16[2048,256]{1,0:T(8,128)(2,1)} %get-tuple-element.282), channel_id=1, source_target_pairs={{0,4},{4,0},{1,5},{5,1},{2,6},{6,2},{3,7},{7,3},{8,12},{12,8},{9,1... | collective-permute-start | bytes 3145736 | tf_op jit(solution)/shard_map/ppermute | solution.py:836
  391.8 117.5 %collective-permute-start.40 = (bf16[4,256,1024]{2,1,0:T(8,128)(2,1)}, bf16[4,256,1024]{2,1,0:T(8,128)(2,1)}, u32[]{:S(2)}, u32[]{:S(2)}) collective-permute-start(bf16[4,256,1024]{2,1,0:T(8,128)(2,1)} %get-tuple-element.315), channel_id=1, source_target_pairs={{0,4},{4,0},{1,5},{5,1},{2,6},{6,2},{3,7},{7,3},{8,12},{12,8},{9,1... | collective-permute-start | bytes 6291464 | tf_op jit(solution)/shard_map/ppermute | solution.py:836
  392.1 24.6 %collective-permute-start.37 = (bf16[1024,256]{1,0:T(8,128)(2,1)}, bf16[1024,256]{1,0:T(8,128)(2,1)}, u32[]{:S(2)}, u32[]{:S(2)}) collective-permute-start(bf16[1024,256]{1,0:T(8,128)(2,1)} %get-tuple-element.391), channel_id=1, source_target_pairs={{0,8},{8,0},{1,9},{9,1},{2,10},{10,2},{3,11},{11,3},{4,12},{12,4},... | collective-permute-start | bytes 1572872 | tf_op jit(solution)/shard_map/ppermute | solution.py:836
  392.2 42.7 %collective-permute-start.36 = (bf16[1024,256]{1,0:T(8,128)(2,1)}, bf16[1024,256]{1,0:T(8,128)(2,1)}, u32[]{:S(2)}, u32[]{:S(2)}) collective-permute-start(bf16[1024,256]{1,0:T(8,128)(2,1)} %get-tuple-element.418), channel_id=1, source_target_pairs={{0,8},{8,0},{1,9},{9,1},{2,10},{10,2},{3,11},{11,3},{4,12},{12,4},... | collective-permute-start | bytes 1572872 | tf_op jit(solution)/shard_map/ppermute | solution.py:836
  394.2 4.4 collective-permute-start.18
  401.5 14.0 %collective-permute-start.19 = (bf16[128,2048]{1,0:T(8,128)(2,1)S(1)}, bf16[128,2048]{1,0:T(8,128)(2,1)S(1)}, u32[]{:S(2)}, u32[]{:S(2)}) collective-permute-start(bf16[128,2048]{1,0:T(8,128)(2,1)S(1)} %get-tuple-element.380), channel_id=1, source_target_pairs={{0,2},{2,0},{1,3},{3,1},{4,6},{6,4},{5,7},{7,5},{8,10},{10,8},{9,1... | collective-permute-start | bytes 1572872 | tf_op jit(solution)/shard_map/cond/branch_1_fun/ppermute | solution.py:836
  436.8 32.3 %collective-permute-start.39 = (bf16[512,256]{1,0:T(8,128)(2,1)}, bf16[512,256]{1,0:T(8,128)(2,1)S(1)}, u32[]{:S(2)}, u32[]{:S(2)}) collective-permute-start(bf16[512,256]{1,0:T(8,128)(2,1)} %get-tuple-element.405), channel_id=1, source_target_pairs={{0,16},{16,0},{1,17},{17,1},{2,18},{18,2},{3,19},{19,3},{4,20},{20... | collective-permute-start | bytes 786440 | tf_op jit(solution)/shard_map/ppermute | solution.py:836
  438.7 30.5 %collective-permute-start.38 = (bf16[512,256]{1,0:T(8,128)(2,1)S(1)}, bf16[512,256]{1,0:T(8,128)(2,1)S(1)}, u32[]{:S(2)}, u32[]{:S(2)}) collective-permute-start(bf16[512,256]{1,0:T(8,128)(2,1)S(1)} %get-tuple-element.407), channel_id=1, source_target_pairs={{0,16},{16,0},{1,17},{17,1},{2,18},{18,2},{3,19},{19,3},{4,20},{20... | collective-permute-start | bytes 786440 | tf_op jit(solution)/shard_map/ppermute | solution.py:836
  441.8 10.3 %collective-permute-start.8 = (bf16[128,2048]{1,0:T(8,128)(2,1)}, bf16[128,2048]{1,0:T(8,128)(2,1)S(1)}, u32[]{:S(2)}, u32[]{:S(2)}) collective-permute-start(bf16[128,2048]{1,0:T(8,128)(2,1)} %get-tuple-element.117), channel_id=1, source_target_pairs={{0,2},{2,0},{1,3},{3,1},{4,6},{6,4},{5,7},{7,5},{8,10},{10,8},{9,1... | collective-permute-start | bytes 1572872 | tf_op jit(solution)/shard_map/cond/branch_1_fun/ppermute | solution.py:836
  441.9 27.3 %collective-permute-start.7 = (bf16[128,2048]{1,0:T(8,128)(2,1)}, bf16[128,2048]{1,0:T(8,128)(2,1)}, u32[]{:S(2)}, u32[]{:S(2)}) collective-permute-start(bf16[128,2048]{1,0:T(8,128)(2,1)} %get-tuple-element.116), channel_id=1, source_target_pairs={{0,8},{8,0},{1,9},{9,1},{2,10},{10,2},{3,11},{11,3},{4,12},{12,4},... | collective-permute-start | bytes 1572872 | tf_op jit(solution)/shard_map/cond/branch_1_fun/ppermute | solution.py:836
  472.0 49.8 %collective-permute-start.41 = (bf16[256,1024]{1,0:T(8,128)(2,1)}, bf16[256,1024]{1,0:T(8,128)(2,1)}, u32[]{:S(2)}, u32[]{:S(2)}) collective-permute-start(bf16[256,1024]{1,0:T(8,128)(2,1)} %get-tuple-element.403), channel_id=1, source_target_pairs={{0,8},{8,0},{1,9},{9,1},{2,10},{10,2},{3,11},{11,3},{4,12},{12,4},... | collective-permute-start | bytes 1572872 | tf_op jit(solution)/shard_map/ppermute | solution.py:836
  478.8 7.8 %collective-permute-start.20 = (bf16[256,2048]{1,0:T(8,128)(2,1)}, bf16[256,2048]{1,0:T(8,128)(2,1)}, u32[]{:S(2)}, u32[]{:S(2)}) collective-permute-start(bf16[256,2048]{1,0:T(8,128)(2,1)} %get-tuple-element.126), channel_id=1, source_target_pairs={{0,1},{1,0},{2,3},{3,2},{4,5},{5,4},{6,7},{7,6},{8,9},{9,8},{10,11... | collective-permute-start | bytes 3145736 | tf_op jit(solution)/shard_map/cond/branch_1_fun/ppermute | solution.py:836
  488.0 17.8 %collective-permute-start.21 = (bf16[128,2048]{1,0:T(8,128)(2,1)S(1)}, bf16[128,2048]{1,0:T(8,128)(2,1)S(1)}, u32[]{:S(2)}, u32[]{:S(2)}) collective-permute-start(bf16[128,2048]{1,0:T(8,128)(2,1)S(1)} %add_convert_fusion.11), channel_id=1, source_target_pairs={{0,2},{2,0},{1,3},{3,1},{4,6},{6,4},{5,7},{7,5},{8,10},{10,8},{9,1... | collective-permute-start | bytes 1572872 | tf_op jit(solution)/shard_map/cond/branch_1_fun/ppermute | solution.py:836
  513.9 25.5 %collective-permute-start.42 = (bf16[2,256,1024]{2,1,0:T(8,128)(2,1)}, bf16[2,256,1024]{2,1,0:T(8,128)(2,1)}, u32[]{:S(2)}, u32[]{:S(2)}) collective-permute-start(bf16[2,256,1024]{2,1,0:T(8,128)(2,1)} %get-tuple-element.382), channel_id=1, source_target_pairs={{0,8},{8,0},{1,9},{9,1},{2,10},{10,2},{3,11},{11,3},{4,12},{12,4},... | collective-permute-start | bytes 3145736 | tf_op jit(solution)/shard_map/ppermute | solution.py:836
  518.2 25.1 %collective-permute-start.43 = (bf16[4,256,512]{2,1,0:T(8,128)(2,1)}, bf16[4,256,512]{2,1,0:T(8,128)(2,1)}, u32[]{:S(2)}, u32[]{:S(2)}) collective-permute-start(bf16[4,256,512]{2,1,0:T(8,128)(2,1)} %get-tuple-element.324), channel_id=1, source_target_pairs={{0,4},{4,0},{1,5},{5,1},{2,6},{6,2},{3,7},{7,3},{8,12},{12,8},{9,1... | collective-permute-start | bytes 3145736 | tf_op jit(solution)/shard_map/ppermute | solution.py:836
  520.0 25.1 %collective-permute-start.44 = (bf16[256,2048]{1,0:T(8,128)(2,1)}, bf16[256,2048]{1,0:T(8,128)(2,1)}, u32[]{:S(2)}, u32[]{:S(2)}) collective-permute-start(bf16[256,2048]{1,0:T(8,128)(2,1)} %pad_maximum_fusion.5), channel_id=1, source_target_pairs={{0,2},{2,0},{1,3},{3,1},{4,6},{6,4},{5,7},{7,5},{8,10},{10,8},{9,1... | collective-permute-start | bytes 3145736 | tf_op jit(solution)/shard_map/ppermute | solution.py:836
  546.7 7.7 %collective-permute-start.45 = (bf16[512,2048]{1,0:T(8,128)(2,1)S(1)}, bf16[512,2048]{1,0:T(8,128)(2,1)S(1)}, u32[]{:S(2)}, u32[]{:S(2)}) collective-permute-start(bf16[512,2048]{1,0:T(8,128)(2,1)S(1)} %pad_maximum_fusion.3), channel_id=1, source_target_pairs={{0,1},{1,0},{2,3},{3,2},{4,5},{5,4},{6,7},{7,6},{8,9},{9,8},{10,11... | collective-permute-start | bytes 6291464 | tf_op jit(solution)/shard_map/ppermute | solution.py:836
  551.6 14.3 %collective-permute-start.46 = (bf16[2,256,512]{2,1,0:T(8,128)(2,1)S(1)}, bf16[2,256,512]{2,1,0:T(8,128)(2,1)S(1)}, u32[]{:S(2)}, u32[]{:S(2)}) collective-permute-start(bf16[2,256,512]{2,1,0:T(8,128)(2,1)S(1)} %get-tuple-element.386), channel_id=1, source_target_pairs={{0,8},{8,0},{1,9},{9,1},{2,10},{10,2},{3,11},{11,3},{4,12},{12,4},... | collective-permute-start | bytes 1572872 | tf_op jit(solution)/shard_map/ppermute | solution.py:836
  566.7 25.8 %collective-permute-start.48 = (bf16[1,256,512]{2,1,0:T(8,128)(2,1)S(1)}, bf16[1,256,512]{2,1,0:T(8,128)(2,1)S(1)}, u32[]{:S(2)}, u32[]{:S(2)}) collective-permute-start(bf16[1,256,512]{2,1,0:T(8,128)(2,1)S(1)} %add_convert_fusion.25), channel_id=1, source_target_pairs={{0,16},{16,0},{1,17},{17,1},{2,18},{18,2},{3,19},{19,3},{4,20},{20... | collective-permute-start | bytes 786440 | tf_op jit(solution)/shard_map/ppermute | solution.py:836
  568.5 51.5 %collective-permute-start.47 = (bf16[1,256,1024]{2,1,0:T(8,128)(2,1)}, bf16[1,256,1024]{2,1,0:T(8,128)(2,1)S(1)}, u32[]{:S(2)}, u32[]{:S(2)}) collective-permute-start(bf16[1,256,1024]{2,1,0:T(8,128)(2,1)} %get-tuple-element.384), channel_id=1, source_target_pairs={{0,16},{16,0},{1,17},{17,1},{2,18},{18,2},{3,19},{19,3},{4,20},{20... | collective-permute-start | bytes 1572872 | tf_op jit(solution)/shard_map/ppermute | solution.py:836
  594.6 28.8 %collective-permute-start.49 = (bf16[256,1024]{1,0:T(8,128)(2,1)S(1)}, bf16[256,1024]{1,0:T(8,128)(2,1)S(1)}, u32[]{:S(2)}, u32[]{:S(2)}) collective-permute-start(bf16[256,1024]{1,0:T(8,128)(2,1)S(1)} %dynamic-slice_bitcast_fusion), channel_id=1, source_target_pairs={{0,8},{8,0},{1,9},{9,1},{2,10},{10,2},{3,11},{11,3},{4,12},{12,4},... | collective-permute-start | bytes 1572872 | tf_op jit(solution)/shard_map/ppermute | solution.py:836
  596.0 3.8 collective-permute-start.10
  603.6 11.6 %collective-permute-start.12 = (f32[2,2048]{1,0:T(2,128)S(1)}, f32[2,2048]{1,0:T(2,128)S(1)}, u32[]{:S(2)}, u32[]{:S(2)}) collective-permute-start(f32[2,2048]{1,0:T(2,128)S(1)} %add.210), channel_id=1, source_target_pairs={{0,8},{8,0},{1,9},{9,1},{2,10},{10,2},{3,11},{11,3},{4,12},{12,4},... | collective-permute-start | bytes 49160 | tf_op jit(solution)/shard_map/cond/branch_1_fun/ppermute | solution.py:836
  615.2 4.7 collective-permute-start.13
  (39 other events, 534.2 us)
Sparse Core Ops, SparseCore 0:
  206.4 86.0 reduce-scatter.3
  295.7 86.0 reduce-scatter.5
  392.3 104.6 reduce-scatter.7

commit v8 on v7

--- a/solution.py
+++ b/solution.py
@@ -747,11 +747,11 @@
     else:
         for k in range(per_step):
             index = pl.program_id(0) * per_step + k
-            out_ref[pl.ds(unit_spot(index), 1)] = total[k * share : (k + 1) * share][None]
-
-
-def unit_spot(index):
-    return (index & ~3) + (index & 1) * 2 + (lax.shift_right_logical(index, 1) & 1)
+            out_ref[pl.ds(unit_spot(index, out_ref.shape[0]), 1)] = total[k * share : (k + 1) * share][None]
+
+
+def unit_spot(index, ctx_count):
+    return (index & 1) * (ctx_count // 2) + lax.shift_right_logical(index, 1)
 
 
 def unit_shares(name, left, right, ctx_count, where):
@@ -760,7 +760,7 @@
     share = model // ctx_count
     shares = jax.ShapeDtypeStruct((ctx_count, share, width), jnp.bfloat16)
     if share == block:
-        out_spec = pl.BlockSpec((1, share, width), lambda i, w: (unit_spot(i), 0, 0))
+        out_spec = pl.BlockSpec((1, share, width), lambda i, w: (unit_spot(i, ctx_count), 0, 0))
     else:
         out_spec = pl.BlockSpec(shares.shape, lambda i, w: (0, 0, 0))
     return pl.pallas_call(
@@ -945,7 +945,7 @@
 
 
 def unit_sum_over(shares):
-    return lax.psum_scatter(shares, ("hi", "x"), scatter_dimension=0, tiled=True)
+    return lax.psum_scatter(shares, ("x", "hi"), scatter_dimension=0, tiled=True)
 
 
 def split_halves(summed, ctx, dep):
@@ -1003,20 +1003,21 @@
     stage = Stages(block_order)
     cot_own = lax.dynamic_slice_in_dim(cotangent, tensor * quarter, quarter)
     cot_slots = slots_of(cotangent, tensor)
+    cot_part = ctx_flip(cot_own, 2)
     first_input, queries, kv_local, cosine, sine = input_stage(
         layer_input, attn_gain, w_query, key_matrix, value_matrix, block_order, cont_prompt, where
     )
     parts = {0: kv_local}
-    parts[2], parts[1] = stage(lambda kv: (ctx_flip(kv, 2), ctx_flip(kv, 1)), kv_local)
+    parts[2], parts[1] = stage(
+        lambda kv: (ctx_flip(kv, 2), ctx_flip(kv, 1)), after(cot_part, kv_local)
+    )
     high_parts = {0: after(parts[1], kv_local)}
     for bit in reversed(highs):
         for mask in list(high_parts):
             high_parts[mask + bit] = ctx_flip(high_parts[mask], bit)
     del high_parts[0]
     parts.update(high_parts)
-    parts[3], cot_part = stage(
-        lambda kv, cot: (ctx_flip(kv, 1), ctx_flip(cot, 2)), parts[2], cot_own
-    )
+    parts[3] = stage(lambda kv: ctx_flip(kv, 1), parts[2])
     dep = parts[3]
     for mask in high_parts:
         parts[mask + 2], parts[mask + 1], more = stage(
@@ -1138,29 +1139,34 @@
         w_query, key_matrix, value_matrix, where,
     )
 
-    def first_stage(keep, send, grad_kv, own_input, grad_middle):
-        shares = weight_shares(
-            "kv_shares", (first_input,), (grad_kv,), ((0, 0),), ctx_count, True, where
-        )
-        terms = scatter_slots(keep, send, lambda value: after(shares[0], value))
+    kv_shares = weight_shares(
+        "kv_shares", (first_input,), (after(keep, grad_kv),), ((0, 0),), ctx_count, True, where
+    )
+    branch.halve(2, ctx, kv_shares[0])
+    last = Reduce(*after(branch.keep, *kv_shares))
+
+    def first_stage(keep, send, own_input, grad_middle):
+        terms = scatter_slots(keep, send)
         inv = lax.rsqrt(jnp.mean(own_input * own_input, axis=-1, keepdims=True) + eps_norm)
         grad_norm, gain_part = norm_back(total(terms), own_input * inv, inv, attn_gain)
-        return shares, gain_part, (grad_middle + grad_norm).astype(jnp.bfloat16)
-
-    kv_shares, attn_gain_part, grad_input = stage(
-        first_stage, keep, send, grad_kv, own_input, grad_middle
+        return gain_part, (grad_middle + grad_norm).astype(jnp.bfloat16)
+
+    attn_gain_part, grad_input = stage(
+        first_stage, after(branch.keep, keep), send, own_input, grad_middle
     )
     near = jnp.concatenate([grad_input, after(grad_input, output)])
     near_other = flip(near, "y")
-    branch.halve(2, ctx, grad_input)
-    last = Reduce(*after(branch.keep, *kv_shares))
-    sum_gate = join_halves(gate_own, after(branch.keep, gate_other), ctx)
-    dep = sum_gate
+    dep = grad_input
     for mask in highs:
         branch.halve(mask, ctx, dep)
         dep = branch.keep
     last.halve(2, ctx, dep)
-    near = jnp.concatenate([near, after(last.keep, near_other)])
+    sum_gate = join_halves(gate_own, after(last.keep, gate_other), ctx)
+    dep = sum_gate
+    for mask in highs:
+        last.halve(mask, ctx, dep)
+        dep = last.keep
+    near = jnp.concatenate([near, after(dep, near_other)])
     far = flip(near, "core")
     quarters = [near[n * quarter : (n + 1) * quarter] for n in range(4)]
     quarters += [far[n * quarter : (n + 1) * quarter] for n in range(4)]
@@ -1168,10 +1174,6 @@
         place_rows(quarters[k], quarters[k + 2], quarters[k + 4], quarters[k + 6], tensor)
         for k in range(2)
     ]
-    dep = (grad_input, output)
-    for mask in highs:
-        last.halve(mask, ctx, dep)
-        dep = last.keep
 
     def gain_stage(gains):
         gains = gains + flip(gains, "core")
@@ -1180,11 +1182,11 @@
             gains = gains + ctx_flip(gains, mask)
         return gains
 
-    gains = stage(gain_stage, after(dep, jnp.stack([attn_gain_part, ffn_gain_part])))
     up_own, up_away = split_halves(up, ctx, dep)
     up_other = ctx_flip(up_away, 2)
+    gains = stage(gain_stage, after(near, jnp.stack([attn_gain_part, ffn_gain_part])))
     sum_up = join_halves(up_own, after(gains, up_other), ctx)
-    branch.keep, branch.got = after(gains, branch.keep, branch.got)
+    branch.keep, branch.got = after(sum_up, branch.keep, branch.got)
     width_q, width_k = w_query.shape[1], key_matrix.shape[1]
     branch_sum, last_sum = branch.sum(), last.sum()
     sum_query, sum_out = branch_sum[:, :width_q], branch_sum[:, width_q:].T

time: 638 us -> 626 us (0.981); the launches traced: 632 us -> 627 us
  starting transfers between devices: 48.6 us -> 61.6 us
  waiting for transfers between devices: 289 us -> 279 us
  Pallas kernels: 182 us -> 174 us
  local copies, waits for them, and re-layouts: 40.5 us -> 47.5 us
    ppermute x50, starting transfers between devices: 48.5 us -> 61.5 us  [flip(): lax.ppermute(value, axis, [(i, i ^ mask) for i in range(lax.axis_size(axi...]
    ppermute x50, waiting for transfers between devices: 289 us -> 279 us  [flip(): lax.ppermute(value, axis, [(i, i ^ mask) for i in range(lax.axis_size(axi...]
    unnamed x78 -> x83, local copies, waits for them, and re-layouts: 17.7 us -> 23.8 us
  transfers between devices with their start and end apart: 53 -> 53, of which waited for: 35 -> 39; matrix products, arithmetic and copies ran while one was open for 12% -> 11% of each run, Pallas kernels for 19% -> 20%
where the time goes in v8:
time: 626 us; the launch traced here: 627 us
  waiting for transfers between devices  279 us (45%)
  Pallas kernels  174 us (28%)
  starting transfers between devices  61.6 us (10%)
  other arithmetic  49.6 us (8%)
  local copies, waits for them, and re-layouts  47.5 us (8%)
  between operations  14.9 us (2%)
    ppermute x50, waiting for transfers between devices, flip(): lax.ppermute(value, axis, [(i, i ^ mask) for i in range(lax.axis_size(axi...  279 us
    ppermute x50, starting transfers between devices, flip(): lax.ppermute(value, axis, [(i, i ^ mask) for i in range(lax.axis_size(axi...  61.5 us
    pallas_call x2, Pallas kernels, attention_backward(): pl.pallas_call(functools.partial(backward_kernel, rep, 1, ctx_count, head...  35.5 us
    pallas_call x3, Pallas kernels, unit_shares(): pl.pallas_call(unit_shares_kernel, out_shape=shares, grid_spec=pltpu.Pref...  31.6 us
    pallas_call x1, Pallas kernels, attention_forward(): pl.pallas_call(functools.partial(forward_kernel, rep, kv_heads, ctx_count...  25.4 us
    unnamed x83, local copies, waits for them, and re-layouts  23.8 us
    convert_element_type x12, other arithmetic, add(): (left.astype(jnp.float32) + right.astype(jnp.float32)).astype(jnp.bfloat16)  23.3 us
    pallas_call x2, Pallas kernels, grad_second_half(): pl.pallas_call(grad_second_kernel, out_shape=jax.ShapeDtypeStruct((rows,...  17.9 us
  transfers between devices with their start and end apart: 53, of which 39 were waited for; matrix products, arithmetic and copies ran while one was open for 11% of the time, Pallas kernels for 20%

profile of v8, /device:TPU:0, one launch (start us, length us, event | category | flops | bytes accessed | tf_op | source)
XLA Modules:
  0.0 627.3 jit_solution(17727594678996505669)
XLA Ops:
  13.0 7.2 %input_stage.1 = (bf16[512,2048]{1,0:T(8,128)(2,1)}, bf16[512,512]{1,0:T(8,128)(2,1)}, bf16[512,512]{1,0:T(8,128)(2,1)S(1)}, f32[512,128]{1,0:T(8,128)}, f32[512,128]{1,0:T(8,128)}) custom-call(s32[32]{0:T(128)} %order_ref.7, s32[8]{0:T(128)} %cont_ref.7, s32[2]{0:T(128)S(1)} %pad_add_fusion.where_ref, f32[1,2048]{1,0:T(1,128)} %bitcast.32, ...), custom_call_target="tpu_custom_call" | custom-call | flops 42949672 | bytes 167772 | tf_op jit(solution)/shard_map/input_stage/pallas_call | solution.py:489
  24.1 14.4 %conditional.10 = (bf16[512,512]{1,0:T(8,128)(2,1)}, bf16[512,512]{1,0:T(8,128)(2,1)}, bf16[512,512]{1,0:T(8,128)(2,1)S(1)}) conditional(s32[]{:T(128)} %bitcast.2, () %tuple.147, bf16[512,512]{1,0:T(8,128)(2,1)S(1)} %get-tuple-element.234.refs_0_), branch_computations={%region_0.0_spmd, %region_1.0_spmd} | conditional | bytes 5242984 | solution.py:872
  27.4 10.0 %collective-permute-done = bf16[512,512]{1,0:T(8,128)(2,1)} collective-permute-done((bf16[512,512]{1,0:T(8,128)(2,1)S(1)}, bf16[512,512]{1,0:T(8,128)(2,1)}, u32[]{:S(2)}, u32[]{:S(2)}) %collective-permute-start) | collective-permute-done | bytes 524320 | tf_op jit(solution)/shard_map/cond/branch_1_fun/ppermute | solution.py:836
  41.1 11.4 %conditional.11 = (bf16[512,512]{1,0:T(8,128)(2,1)}) conditional(s32[]{:T(128)} %bitcast.2, () %tuple.146, bf16[512,512]{1,0:T(8,128)(2,1)S(1)} %get-tuple-element.232), branch_computations={%region_2.0_spmd, %region_3.0_spmd} | conditional | bytes 2097200 | solution.py:872
  42.6 10.0 %collective-permute-done.2 = bf16[512,512]{1,0:T(8,128)(2,1)} collective-permute-done((bf16[512,512]{1,0:T(8,128)(2,1)S(1)}, bf16[512,512]{1,0:T(8,128)(2,1)}, u32[]{:S(2)}, u32[]{:S(2)}) %collective-permute-start.2) | collective-permute-done | bytes 524320 | tf_op jit(solution)/shard_map/cond/branch_1_fun/ppermute | solution.py:836
  55.3 7.5 %collective-permute-done.26.refs_4_ = bf16[512,512]{1,0:T(8,128)(2,1)S(1)} collective-permute-done((bf16[512,512]{1,0:T(8,128)(2,1)S(1)}, bf16[512,512]{1,0:T(8,128)(2,1)S(1)}, u32[]{:S(2)}, u32[]{:S(2)}) %collective-permute-start.26) | collective-permute-done | bytes 524320 | tf_op jit(solution)/shard_map/ppermute | solution.py:836
  62.7 15.1 %conditional.12 = (bf16[512,512]{1,0:T(8,128)(2,1)}, bf16[512,512]{1,0:T(8,128)(2,1)}, bf16[128,2048]{1,0:T(8,128)(2,1)}) conditional(s32[]{:T(128)} %bitcast.2, () %tuple.145, (bf16[512,512]{1,0:T(8,128)(2,1)S(1)}, bf16[128,2048]{1,0:T(8,128)(2,1)S(1)}) %tuple.151), branch_computations={%region_4.0_spmd, %region_5.0_spmd} | conditional | bytes 6291600 | solution.py:872
  65.9 10.1 %collective-permute-done.3 = bf16[512,512]{1,0:T(8,128)(2,1)} collective-permute-done((bf16[512,512]{1,0:T(8,128)(2,1)S(1)}, bf16[512,512]{1,0:T(8,128)(2,1)}, u32[]{:S(2)}, u32[]{:S(2)}) %collective-permute-start.3) | collective-permute-done | bytes 524320 | tf_op jit(solution)/shard_map/cond/branch_1_fun/ppermute | solution.py:836
  80.8 14.8 %conditional.13 = (bf16[512,512]{1,0:T(8,128)(2,1)}, bf16[256,2048]{1,0:T(8,128)(2,1)}, bf16[128,2048]{1,0:T(8,128)(2,1)S(1)}, bf16[128,2048]{1,0:T(8,128)(2,1)S(1)}) conditional(s32[]{:T(128)} %bitcast.2, () %tuple.152, (bf16[512,512]{1,0:T(8,128)(2,1)}, bf16[256,2048]{1,0:T(8,128)(2,1)S(1)}) %tuple.153), branch_computations={%region_6.0_spmd, %region_7.0_spmd} | conditional | bytes 8388720 | solution.py:872
  85.0 10.6 %collective-permute-done.23 = bf16[512,512]{1,0:T(8,128)(2,1)} collective-permute-done((bf16[512,512]{1,0:T(8,128)(2,1)}, bf16[512,512]{1,0:T(8,128)(2,1)}, u32[]{:S(2)}, u32[]{:S(2)}) %collective-permute-start.23) | collective-permute-done | bytes 524320 | tf_op jit(solution)/shard_map/cond/branch_1_fun/ppermute | solution.py:836
  101.2 25.4 %attention_forward.1 = (bf16[512,512]{1,0:T(8,128)(2,1)}, f32[2,4,256]{2,1,0:T(4,128)}, bf16[256,2048]{1,0:T(8,128)(2,1)}, bf16[256,2048]{1,0:T(8,128)(2,1)}) custom-call(s32[32]{0:T(128)} %order_ref.7, s32[8]{0:T(128)} %cont_ref.7, s32[2]{0:T(128)S(1)} %pad_add_fusion.where_ref, bf16[512,512]{1,0:T(8,128)(2,1)} %get-tuple-element.240.q_ref, ...), custom_call_target="tpu_custom_call" | custom-call | flops 64424508 | bytes 167772 | tf_op jit(solution)/shard_map/attention_forward/pallas_call | solution.py:344
  133.6 9.7 %grad_hidden.1.gh_ref = f32[1024,1024]{1,0:T(8,128)} custom-call(s32[2]{0:T(128)S(1)} %pad_add_fusion.where_ref, bf16[1024,2048]{1,0:T(8,128)(2,1)} %constant_dynamic-update-slice_fusion.cot_ref.left_ref, bf16[2048,2048]{1,0:T(8,128)(2,1)} %wd_ref.1), custom_call_target="tpu_custom_call" | custom-call | flops 68719476736 | bytes 134217728 | tf_op jit(solution)/shard_map/grad_hidden/pallas_call | solution.py:547
  150.1 11.5 %collective-permute-done.29 = bf16[128,2048]{1,0:T(8,128)(2,1)S(1)} collective-permute-done((bf16[128,2048]{1,0:T(8,128)(2,1)S(1)}, bf16[128,2048]{1,0:T(8,128)(2,1)S(1)}, u32[]{:S(2)}, u32[]{:S(2)}) %collective-permute-start.29) | collective-permute-done | bytes 524320 | tf_op jit(solution)/shard_map/ppermute | solution.py:836
  163.1 10.7 %collective-permute-done.31 = bf16[128,2048]{1,0:T(8,128)(2,1)S(1)} collective-permute-done((bf16[128,2048]{1,0:T(8,128)(2,1)S(1)}, bf16[128,2048]{1,0:T(8,128)(2,1)S(1)}, u32[]{:S(2)}, u32[]{:S(2)}) %collective-permute-start.31) | collective-permute-done | bytes 524320 | tf_op jit(solution)/shard_map/ppermute | solution.py:836
  179.8 15.6 %ffn_stage.1 = (bf16[1024,1024]{1,0:T(8,128)(2,1)}, bf16[1024,1024]{1,0:T(8,128)(2,1)}, bf16[1024,1024]{1,0:T(8,128)(2,1)S(1)}) custom-call(s32[2]{0:T(128)S(1)} %pad_add_fusion.where_ref, bf16[1024,2048]{1,0:T(8,128)(2,1)} %constant_dynamic-update-slice_fusion.5.in_ref, f32[1024,1024]{1,0:T(8,128)} %grad_hidden.1.gh_ref, bf16[2048,2048]{1,0:T(8,128)(2,1)} %wg_ref.3, ...), custom_call_target="tpu_custom_call" | custom-call | flops 171798688 | bytes 251658 | tf_op jit(solution)/shard_map/ffn_stage/pallas_call | solution.py:586
  195.4 10.9 %down_shares.1 = bf16[8,256,1024]{2,1,0:T(8,128)(2,1)} custom-call(s32[2]{0:T(128)S(1)} %pad_add_fusion.where_ref, bf16[1024,2048]{1,0:T(8,128)(2,1)} %constant_dynamic-update-slice_fusion.cot_ref.left_ref, bf16[1024,1024]{1,0:T(8,128)(2,1)} %get-tuple-element.248.right_ref), custom_call_target="tpu_custom_call" | custom-call | flops 85899344 | bytes 167772 | tf_op jit(solution)/shard_map/down_shares/pallas_call | solution.py:766
  206.4 9.0 %grad_second_send.1 = bf16[512,2048]{1,0:T(8,128)(2,1)} custom-call(s32[2]{0:T(128)S(1)} %pad_add_fusion.where_ref, bf16[1024,1024]{1,0:T(8,128)(2,1)} %get-tuple-element.251.gg_ref, bf16[1024,1024]{1,0:T(8,128)(2,1)S(1)} %get-tuple-element.252.gu_ref, bf16[2048,2048]{1,0:T(8,128)(2,1)} %wg_ref.3, bf16[2048,2048]{1,0:T(8,128)(2,1)} %wu_ref.3), custom_call_target="tpu_custom_call" | custom-call | flops 85899344 | bytes 83886 | tf_op jit(solution)/shard_map/grad_second_send/pallas_call | solution.py:618
  215.4 59.6 %conditional.14 = (f32[128,2048]{1,0:T(8,128)}, bf16[8,256,1024]{2,1,0:T(8,128)(2,1)}, bf16[512,2048]{1,0:T(8,128)(2,1)}, bf16[512,2048]{1,0:T(8,128)(2,1)}) conditional(s32[]{:T(128)} %bitcast.2, () %tuple.157, (s32[2]{0:T(128)S(1)}, bf16[1024,1024]{1,0:T(8,128)(2,1)}, bf16[1024,1024]{1,0:T(8,128)(2,1)S(1)}, bf16[2048,2048]{1,0:T(8,128)(2,1)}, ...), branch_computations={%region_9.0_spmd, %region_10.0_spmd} | conditional | flops 206164983808 | bytes 376439040 | solution.py:872
  215.5 9.0 %grad_second_keep.1 = bf16[512,2048]{1,0:T(8,128)(2,1)} custom-call(s32[2]{0:T(128)S(1)} %get-tuple-element.80.where_ref, bf16[1024,1024]{1,0:T(8,128)(2,1)} %get-tuple-element.87.gg_ref.right_ref, bf16[1024,1024]{1,0:T(8,128)(2,1)S(1)} %get-tuple-element.82.gu_ref, bf16[2048,2048]{1,0:T(8,128)(2,1)} %get-tuple-element.83.wg_ref, ...), custom_call_target="tpu_custom_call" | custom-call | flops 68719476736 | bytes 67108864 | tf_op jit(solution)/shard_map/cond/branch_1_fun/grad_second_keep/pallas_call | solution.py:618
  229.9 10.0 %gate_shares.1 = bf16[8,256,1024]{2,1,0:T(8,128)(2,1)} custom-call(s32[2]{0:T(128)S(1)} %get-tuple-element.80.where_ref, bf16[1024,2048]{1,0:T(8,128)(2,1)} %get-tuple-element.86.left_ref, bf16[1024,1024]{1,0:T(8,128)(2,1)S(1)} %copy-done.15), custom_call_target="tpu_custom_call" | custom-call | flops 68719476736 | bytes 134217728 | tf_op jit(solution)/shard_map/cond/branch_1_fun/gate_shares/pallas_call | solution.py:766
  246.6 8.0 %ffn_out.1 = (bf16[512,2048]{1,0:T(8,128)(2,1)}, bf16[512,2048]{1,0:T(8,128)(2,1)}) custom-call(s32[2]{0:T(128)S(1)} %get-tuple-element.80.where_ref, bf16[1024,1024]{1,0:T(8,128)(2,1)S(1)} %copy-done.22, bf16[2048,2048]{1,0:T(8,128)(2,1)} %get-tuple-element.91.wd_ref), custom_call_target="tpu_custom_call" | custom-call | flops 68719476736 | bytes 134217728 | tf_op jit(solution)/shard_map/cond/branch_1_fun/ffn_out/pallas_call | solution.py:651
  254.6 18.1 %collective-permute-done.16 = bf16[128,2048]{1,0:T(8,128)(2,1)} collective-permute-done((bf16[128,2048]{1,0:T(8,128)(2,1)}, bf16[128,2048]{1,0:T(8,128)(2,1)}, u32[]{:S(2)}, u32[]{:S(2)}) %collective-permute-start.16) | collective-permute-done | bytes 524320 | tf_op jit(solution)/shard_map/cond/branch_1_fun/ppermute | solution.py:836
  276.1 21.0 %conditional.15 = (f32[128,2048]{1,0:T(8,128)S(1)}, bf16[8,256,1024]{2,1,0:T(8,128)(2,1)}, bf16[512,2048]{1,0:T(8,128)(2,1)S(1)}, f32[1,2048]{1,0:T(1,128)S(1)}) conditional(s32[]{:T(128)} %bitcast.2, () %tuple.144, (bf16[128,2048]{1,0:T(8,128)(2,1)}, f32[128]{0:T(128)S(1)}, f32[2048]{0:T(1024)S(1)}, f32[128,2048]{1,0:T(8,128)}, ...), branch_computations={%region_11.0_spmd, %region_12.15_spmd} | conditional | flops 68731011072 | bytes 157313696 | solution.py:872
  280.9 10.7 %up_shares.1 = bf16[8,256,1024]{2,1,0:T(8,128)(2,1)} custom-call(s32[2]{0:T(128)S(1)} %get-tuple-element.102.where_ref, bf16[1024,2048]{1,0:T(8,128)(2,1)} %get-tuple-element.103.left_ref, bf16[1024,1024]{1,0:T(8,128)(2,1)} %get-tuple-element.105.right_ref), custom_call_target="tpu_custom_call" | custom-call | flops 68719476736 | bytes 134217728 | tf_op jit(solution)/shard_map/cond/branch_1_fun/up_shares/pallas_call | solution.py:766
  299.3 17.7 %attention_backward_0.1 = (bf16[512,256]{1,0:T(8,128)(2,1)}, bf16[2048,256]{1,0:T(8,128)(2,1)}, bf16[2048,256]{1,0:T(8,128)(2,1)}) custom-call(s32[32]{0:T(128)} %order_ref.7, s32[8]{0:T(128)} %cont_ref.7, s32[2]{0:T(128)S(1)} %pad_add_fusion.where_ref, bf16[512,512]{1,0:T(8,128)(2,1)} %get-tuple-element.240.q_ref, ...), custom_call_target="tpu_custom_call" | custom-call | flops 64424508 | bytes 125829 | tf_op jit(solution)/shard_map/attention_backward_0/pallas_call | solution.py:380
  319.3 7.0 %collective-permute-start.34 = (bf16[2048,256]{1,0:T(8,128)(2,1)}, bf16[2048,256]{1,0:T(8,128)(2,1)}, u32[]{:S(2)}, u32[]{:S(2)}) collective-permute-start(bf16[2048,256]{1,0:T(8,128)(2,1)} %get-tuple-element.267), channel_id=1, source_target_pairs={{0,4},{4,0},{1,5},{5,1},{2,6},{6,2},{3,7},{7,3},{8,12},{12,8},{9,1... | collective-permute-start | bytes 3145736 | tf_op jit(solution)/shard_map/ppermute | solution.py:836
  326.4 17.7 %attention_backward_1.1 = (bf16[512,256]{1,0:T(8,128)(2,1)}, bf16[2048,256]{1,0:T(8,128)(2,1)}, bf16[2048,256]{1,0:T(8,128)(2,1)}) custom-call(s32[32]{0:T(128)} %order_ref.7, s32[8]{0:T(128)} %cont_ref.7, s32[2]{0:T(128)S(1)} %pad_add_fusion.where_ref, bf16[512,512]{1,0:T(8,128)(2,1)} %get-tuple-element.240.q_ref, ...), custom_call_target="tpu_custom_call" | custom-call | flops 64424508 | bytes 125829 | tf_op jit(solution)/shard_map/attention_backward_1/pallas_call | solution.py:380
  344.1 4.1 collective-permute-start.35
  348.2 9.1 %branch_shares.1 = (bf16[4,256,1024]{2,1,0:T(8,128)(2,1)}, bf16[4,256,1024]{2,1,0:T(8,128)(2,1)}) custom-call(s32[2]{0:T(128)S(1)} %pad_add_fusion.where_ref, bf16[512,2048]{1,0:T(8,128)(2,1)} %get-tuple-element.228.refs_0_, bf16[512,2048]{1,0:T(8,128)(2,1)S(1)} %get-tuple-element.261.gb_ref.refs_1_, bf16[512,256]{1,0:T(8,128)(2,1)} %get-tuple-element.259.refs_2_.refs_6_, ...), custom_call_target="tpu_custom_call" | custom-call | flops 42949672 | bytes 83886 | tf_op jit(solution)/shard_map/branch_shares/pallas_call | solution.py:722
  361.9 33.1 %collective-permute-done.35 = bf16[2048,256]{1,0:T(8,128)(2,1)S(1)} collective-permute-done((bf16[2048,256]{1,0:T(8,128)(2,1)}, bf16[2048,256]{1,0:T(8,128)(2,1)S(1)}, u32[]{:S(2)}, u32[]{:S(2)}) %collective-permute-start.35) | collective-permute-done | bytes 1048608 | tf_op jit(solution)/shard_map/ppermute | solution.py:836
  401.6 22.8 %conditional.16 = (bf16[128,2048]{1,0:T(8,128)(2,1)S(1)}, bf16[128,2048]{1,0:T(8,128)(2,1)S(1)}, f32[128,2048]{1,0:T(8,128)}) conditional(s32[]{:T(128)} %bitcast.2, () %tuple.143, (bf16[512,2048]{1,0:T(8,128)(2,1)}, bf16[512,2048]{1,0:T(8,128)(2,1)}) %tuple.168), branch_computations={%region_16.17_spmd, %region_17.0_spmd} | conditional | flops 5505024 | bytes 17825896 | solution.py:872
  401.7 4.4 collective-permute-done.17
  410.8 12.1 %collective-permute-done.18 = bf16[128,2048]{1,0:T(8,128)(2,1)S(1)} collective-permute-done((bf16[128,2048]{1,0:T(8,128)(2,1)S(1)}, bf16[128,2048]{1,0:T(8,128)(2,1)S(1)}, u32[]{:S(2)}, u32[]{:S(2)}) %collective-permute-start.18) | collective-permute-done | bytes 524320 | tf_op jit(solution)/shard_map/cond/branch_1_fun/ppermute | solution.py:836
  425.4 18.8 %collective-permute-done.36 = bf16[1024,256]{1,0:T(8,128)(2,1)} collective-permute-done((bf16[1024,256]{1,0:T(8,128)(2,1)}, bf16[1024,256]{1,0:T(8,128)(2,1)}, u32[]{:S(2)}, u32[]{:S(2)}) %collective-permute-start.36) | collective-permute-done | bytes 524320 | tf_op jit(solution)/shard_map/ppermute | solution.py:836
  450.9 28.9 %conditional.17 = (bf16[128,2048]{1,0:T(8,128)(2,1)}, f32[128,2048]{1,0:T(8,128)}) conditional(s32[]{:T(128)} %bitcast.2, () %tuple.170, (bf16[128,2048]{1,0:T(8,128)(2,1)}, bf16[128,2048]{1,0:T(8,128)(2,1)}) %tuple.267), branch_computations={%region_18.19_spmd, %region_19.20_spmd} | conditional | flops 262144 | bytes 5767264 | solution.py:872
  453.5 10.4 %collective-permute-done.7 = bf16[128,2048]{1,0:T(8,128)(2,1)S(1)} collective-permute-done((bf16[128,2048]{1,0:T(8,128)(2,1)}, bf16[128,2048]{1,0:T(8,128)(2,1)S(1)}, u32[]{:S(2)}, u32[]{:S(2)}) %collective-permute-start.7) | collective-permute-done | bytes 524320 | tf_op jit(solution)/shard_map/cond/branch_1_fun/ppermute | solution.py:836
  465.0 14.9 %collective-permute-done.6 = bf16[128,2048]{1,0:T(8,128)(2,1)} collective-permute-done((bf16[128,2048]{1,0:T(8,128)(2,1)}, bf16[128,2048]{1,0:T(8,128)(2,1)}, u32[]{:S(2)}, u32[]{:S(2)}) %collective-permute-start.6) | collective-permute-done | bytes 524320 | tf_op jit(solution)/shard_map/cond/branch_1_fun/ppermute | solution.py:836
  483.5 10.5 %collective-permute-done.38.refs_1_ = bf16[512,256]{1,0:T(8,128)(2,1)S(1)} collective-permute-done((bf16[512,256]{1,0:T(8,128)(2,1)S(1)}, bf16[512,256]{1,0:T(8,128)(2,1)S(1)}, u32[]{:S(2)}, u32[]{:S(2)}) %collective-permute-start.38) | collective-permute-done | bytes 262176 | tf_op jit(solution)/shard_map/ppermute | solution.py:836
  496.4 6.6 %tail_stage.1 = (bf16[256,2048]{1,0:T(8,128)(2,1)}, bf16[256,2048]{1,0:T(8,128)(2,1)}, bf16[512,512]{1,0:T(8,128)(2,1)}) custom-call(s32[2]{0:T(128)S(1)} %pad_add_fusion.where_ref, bf16[512,256]{1,0:T(8,128)(2,1)} %get-tuple-element.399.refs_0_, bf16[512,256]{1,0:T(8,128)(2,1)} %copy-done.32, bf16[512,256]{1,0:T(8,128)(2,1)} %get-tuple-element.397.refs_2_, ...), custom_call_target="tpu_custom_call" | custom-call | flops 42949672 | bytes 167772 | tf_op jit(solution)/shard_map/tail_stage/pallas_call | solution.py:818
  503.0 7.7 %kv_shares.1 = (bf16[4,256,512]{2,1,0:T(8,128)(2,1)}, bf16[4,256,512]{2,1,0:T(8,128)(2,1)}) custom-call(s32[2]{0:T(128)S(1)} %pad_add_fusion.where_ref, bf16[512,2048]{1,0:T(8,128)(2,1)} %get-tuple-element.228.refs_0_, bf16[512,512]{1,0:T(8,128)(2,1)} %get-tuple-element.295.refs_1_), custom_call_target="tpu_custom_call" | custom-call | flops 17179869184 | bytes 67108864 | tf_op jit(solution)/shard_map/kv_shares/pallas_call | solution.py:722
  510.7 4.5 add_convert_fusion.13
  524.3 17.8 %conditional.18 = (bf16[128,2048]{1,0:T(8,128)(2,1)S(1)}, f32[1,2048]{1,0:T(1,128)S(1)}) conditional(s32[]{:T(128)} %bitcast.2, () %tuple.142, (f32[128,2048]{1,0:T(8,128)S(1)}, bf16[256,2048]{1,0:T(8,128)(2,1)S(1)}, bf16[256,2048]{1,0:T(8,128)(2,1)S(1)}, f32[2048]{0:T(1024)S(1)}, f32[128,2048]{1,0:T(8,128)S(1)}) %tuple.271), branch_computations={%region_21.22_spmd, %region_22.26_spmd} | conditional | flops 8648832 | bytes 15757920 | solution.py:872
  528.5 12.6 %collective-permute-done.20 = bf16[128,2048]{1,0:T(8,128)(2,1)S(1)} collective-permute-done((bf16[128,2048]{1,0:T(8,128)(2,1)S(1)}, bf16[128,2048]{1,0:T(8,128)(2,1)S(1)}, u32[]{:S(2)}, u32[]{:S(2)}) %collective-permute-start.20) | collective-permute-done | bytes 524320 | tf_op jit(solution)/shard_map/cond/branch_1_fun/ppermute | solution.py:836
  553.0 8.1 %collective-permute-done.44 = bf16[2,256,512]{2,1,0:T(8,128)(2,1)S(1)} collective-permute-done((bf16[2,256,512]{2,1,0:T(8,128)(2,1)S(1)}, bf16[2,256,512]{2,1,0:T(8,128)(2,1)S(1)}, u32[]{:S(2)}, u32[]{:S(2)}) %collective-permute-start.44) | collective-permute-done | bytes 524320 | tf_op jit(solution)/shard_map/ppermute | solution.py:836
  566.3 6.1 collective-permute-done.49
  578.2 28.3 %conditional.19 = (f32[2,2048]{1,0:T(2,128)S(1)}) conditional(s32[]{:T(128)} %bitcast.2, () %tuple.192, f32[2,2048]{1,0:T(2,128)S(1)} %pad_maximum_fusion.5), branch_computations={%region_26.27_spmd, %region_27.28_spmd} | conditional | flops 20480 | bytes 573648 | solution.py:872
  589.1 12.7 %collective-permute-done.11 = f32[2,2048]{1,0:T(2,128)S(1)} collective-permute-done((f32[2,2048]{1,0:T(2,128)S(1)}, f32[2,2048]{1,0:T(2,128)S(1)}, u32[]{:S(2)}, u32[]{:S(2)}) %collective-permute-start.11) | collective-permute-done | bytes 16416 | tf_op jit(solution)/shard_map/cond/branch_1_fun/ppermute | solution.py:836
  601.9 4.6 collective-permute-done.12
  (244 shorter events, 185.5 us)
Async XLA Ops:
  7.2 309.9 %reduce-scatter.4.cloned.1.call-start = ((), (), s32[]{:S(2)}) async-start(), calls=%async_computation.3 | async-start | bytes 5242880 | tf_op jit(solution)/shard_map/reduce_scatter | solution.py:948
  9.2 14.9 %collective-permute-start.25 = (bf16[128,2048]{1,0:T(8,128)(2,1)S(1)}, bf16[128,2048]{1,0:T(8,128)(2,1)S(1)}, u32[]{:S(2)}, u32[]{:S(2)}) collective-permute-start(bf16[128,2048]{1,0:T(8,128)(2,1)S(1)} %get-tuple-element.364), channel_id=1, source_target_pairs={{0,8},{8,0},{1,9},{9,1},{2,10},{10,2},{3,11},{11,3},{4,12},{12,4},... | collective-permute-start | bytes 1572872 | tf_op jit(solution)/shard_map/ppermute | solution.py:836
  24.1 13.2 %collective-permute-start = (bf16[512,512]{1,0:T(8,128)(2,1)S(1)}, bf16[512,512]{1,0:T(8,128)(2,1)}, u32[]{:S(2)}, u32[]{:S(2)}) collective-permute-start(bf16[512,512]{1,0:T(8,128)(2,1)S(1)} %param.1), channel_id=1, source_target_pairs={{0,8},{8,0},{1,9},{9,1},{2,10},{10,2},{3,11},{11,3},{4,12},{12,4},... | collective-permute-start | bytes 1572872 | tf_op jit(solution)/shard_map/cond/branch_1_fun/ppermute | solution.py:836
  25.9 12.6 %collective-permute-start.1 = (bf16[512,512]{1,0:T(8,128)(2,1)S(1)}, bf16[512,512]{1,0:T(8,128)(2,1)}, u32[]{:S(2)}, u32[]{:S(2)}) collective-permute-start(bf16[512,512]{1,0:T(8,128)(2,1)S(1)} %param.1), channel_id=1, source_target_pairs={{0,4},{4,0},{1,5},{5,1},{2,6},{6,2},{3,7},{7,3},{8,12},{12,8},{9,1... | collective-permute-start | bytes 1572872 | tf_op jit(solution)/shard_map/cond/branch_1_fun/ppermute | solution.py:836
  38.5 24.2 %collective-permute-start.26 = (bf16[512,512]{1,0:T(8,128)(2,1)S(1)}, bf16[512,512]{1,0:T(8,128)(2,1)S(1)}, u32[]{:S(2)}, u32[]{:S(2)}) collective-permute-start(bf16[512,512]{1,0:T(8,128)(2,1)S(1)} %get-tuple-element.234.refs_0_), channel_id=1, source_target_pairs={{0,16},{16,0},{1,17},{17,1},{2,18},{18,2},{3,19},{19,3},{4,20},{20... | collective-permute-start | bytes 1572872 | tf_op jit(solution)/shard_map/ppermute | solution.py:836
  41.1 11.4 %collective-permute-start.2 = (bf16[512,512]{1,0:T(8,128)(2,1)S(1)}, bf16[512,512]{1,0:T(8,128)(2,1)}, u32[]{:S(2)}, u32[]{:S(2)}) collective-permute-start(bf16[512,512]{1,0:T(8,128)(2,1)S(1)} %param.3), channel_id=1, source_target_pairs={{0,4},{4,0},{1,5},{5,1},{2,6},{6,2},{3,7},{7,3},{8,12},{12,8},{9,1... | collective-permute-start | bytes 1572872 | tf_op jit(solution)/shard_map/cond/branch_1_fun/ppermute | solution.py:836
  62.7 13.3 %collective-permute-start.3 = (bf16[512,512]{1,0:T(8,128)(2,1)S(1)}, bf16[512,512]{1,0:T(8,128)(2,1)}, u32[]{:S(2)}, u32[]{:S(2)}) collective-permute-start(bf16[512,512]{1,0:T(8,128)(2,1)S(1)} %get-tuple-element.76), channel_id=1, source_target_pairs={{0,8},{8,0},{1,9},{9,1},{2,10},{10,2},{3,11},{11,3},{4,12},{12,4},... | collective-permute-start | bytes 1572872 | tf_op jit(solution)/shard_map/cond/branch_1_fun/ppermute | solution.py:836
  62.9 13.7 %collective-permute-start.4 = (bf16[512,512]{1,0:T(8,128)(2,1)S(1)}, bf16[512,512]{1,0:T(8,128)(2,1)}, u32[]{:S(2)}, u32[]{:S(2)}) collective-permute-start(bf16[512,512]{1,0:T(8,128)(2,1)S(1)} %get-tuple-element.76), channel_id=1, source_target_pairs={{0,4},{4,0},{1,5},{5,1},{2,6},{6,2},{3,7},{7,3},{8,12},{12,8},{9,1... | collective-permute-start | bytes 1572872 | tf_op jit(solution)/shard_map/cond/branch_1_fun/ppermute | solution.py:836
  64.4 13.4 %collective-permute-start.5 = (bf16[128,2048]{1,0:T(8,128)(2,1)S(1)}, bf16[128,2048]{1,0:T(8,128)(2,1)}, u32[]{:S(2)}, u32[]{:S(2)}) collective-permute-start(bf16[128,2048]{1,0:T(8,128)(2,1)S(1)} %get-tuple-element.77), channel_id=1, source_target_pairs={{0,2},{2,0},{1,3},{3,1},{4,6},{6,4},{5,7},{7,5},{8,10},{10,8},{9,1... | collective-permute-start | bytes 1572872 | tf_op jit(solution)/shard_map/cond/branch_1_fun/ppermute | solution.py:836
  80.9 14.7 %collective-permute-start.23 = (bf16[512,512]{1,0:T(8,128)(2,1)}, bf16[512,512]{1,0:T(8,128)(2,1)}, u32[]{:S(2)}, u32[]{:S(2)}) collective-permute-start(bf16[512,512]{1,0:T(8,128)(2,1)} %get-tuple-element.78), channel_id=1, source_target_pairs={{0,4},{4,0},{1,5},{5,1},{2,6},{6,2},{3,7},{7,3},{8,12},{12,8},{9,1... | collective-permute-start | bytes 1572872 | tf_op jit(solution)/shard_map/cond/branch_1_fun/ppermute | solution.py:836
  132.0 14.2 %collective-permute-start.28 = (bf16[128,2048]{1,0:T(8,128)(2,1)}, bf16[128,2048]{1,0:T(8,128)(2,1)S(1)}, u32[]{:S(2)}, u32[]{:S(2)}) collective-permute-start(bf16[128,2048]{1,0:T(8,128)(2,1)} %slice.215), channel_id=1, source_target_pairs={{0,2},{2,0},{1,3},{3,1},{4,6},{6,4},{5,7},{7,5},{8,10},{10,8},{9,1... | collective-permute-start | bytes 1572872 | tf_op jit(solution)/shard_map/ppermute | solution.py:836
  148.5 13.1 %collective-permute-start.29 = (bf16[128,2048]{1,0:T(8,128)(2,1)S(1)}, bf16[128,2048]{1,0:T(8,128)(2,1)S(1)}, u32[]{:S(2)}, u32[]{:S(2)}) collective-permute-start(bf16[128,2048]{1,0:T(8,128)(2,1)S(1)} %get-tuple-element.361), channel_id=1, source_target_pairs={{0,8},{8,0},{1,9},{9,1},{2,10},{10,2},{3,11},{11,3},{4,12},{12,4},... | collective-permute-start | bytes 1572872 | tf_op jit(solution)/shard_map/ppermute | solution.py:836
  148.5 14.7 %collective-permute-start.30 = (bf16[128,2048]{1,0:T(8,128)(2,1)S(1)}, bf16[128,2048]{1,0:T(8,128)(2,1)S(1)}, u32[]{:S(2)}, u32[]{:S(2)}) collective-permute-start(bf16[128,2048]{1,0:T(8,128)(2,1)S(1)} %get-tuple-element.361), channel_id=1, source_target_pairs={{0,2},{2,0},{1,3},{3,1},{4,6},{6,4},{5,7},{7,5},{8,10},{10,8},{9,1... | collective-permute-start | bytes 1572872 | tf_op jit(solution)/shard_map/ppermute | solution.py:836
  161.6 12.2 %collective-permute-start.31 = (bf16[128,2048]{1,0:T(8,128)(2,1)S(1)}, bf16[128,2048]{1,0:T(8,128)(2,1)S(1)}, u32[]{:S(2)}, u32[]{:S(2)}) collective-permute-start(bf16[128,2048]{1,0:T(8,128)(2,1)S(1)} %collective-permute-done.29), channel_id=1, source_target_pairs={{0,2},{2,0},{1,3},{3,1},{4,6},{6,4},{5,7},{7,5},{8,10},{10,8},{9,1... | collective-permute-start | bytes 1572872 | tf_op jit(solution)/shard_map/ppermute | solution.py:836
  174.1 4.2 collective-permute-start.32
  206.3 287.7 %reduce-scatter.6.cloned.1.call-start = ((), (), s32[]{:S(2)}) async-start(), calls=%async_computation.4 | async-start | bytes 5242880 | tf_op jit(solution)/shard_map/reduce_scatter | solution.py:948
  215.4 9.1 %collective-permute-start.13 = (bf16[512,2048]{1,0:T(8,128)(2,1)}, bf16[512,2048]{1,0:T(8,128)(2,1)}, u32[]{:S(2)}, u32[]{:S(2)}) collective-permute-start(bf16[512,2048]{1,0:T(8,128)(2,1)} %get-tuple-element.85), channel_id=1, source_target_pairs={{0,1},{1,0},{2,3},{3,2},{4,5},{5,4},{6,7},{7,6},{8,9},{9,8},{10,11... | collective-permute-start | bytes 6291464 | tf_op jit(solution)/shard_map/cond/branch_1_fun/ppermute | solution.py:836
  227.9 15.1 %collective-permute-start.14 = (bf16[128,2048]{1,0:T(8,128)(2,1)}, bf16[128,2048]{1,0:T(8,128)(2,1)}, u32[]{:S(2)}, u32[]{:S(2)}) collective-permute-start(bf16[128,2048]{1,0:T(8,128)(2,1)} %get-tuple-element.369), channel_id=1, source_target_pairs={{0,2},{2,0},{1,3},{3,1},{4,6},{6,4},{5,7},{7,5},{8,10},{10,8},{9,1... | collective-permute-start | bytes 1572872 | tf_op jit(solution)/shard_map/cond/branch_1_fun/ppermute | solution.py:836
  229.4 25.2 %collective-permute-start.15 = (bf16[128,2048]{1,0:T(8,128)(2,1)S(1)}, bf16[128,2048]{1,0:T(8,128)(2,1)S(1)}, u32[]{:S(2)}, u32[]{:S(2)}) collective-permute-start(bf16[128,2048]{1,0:T(8,128)(2,1)S(1)} %get-tuple-element.367), channel_id=1, source_target_pairs={{0,2},{2,0},{1,3},{3,1},{4,6},{6,4},{5,7},{7,5},{8,10},{10,8},{9,1... | collective-permute-start | bytes 1572872 | tf_op jit(solution)/shard_map/cond/branch_1_fun/ppermute | solution.py:836
  245.3 27.3 %collective-permute-start.16 = (bf16[128,2048]{1,0:T(8,128)(2,1)}, bf16[128,2048]{1,0:T(8,128)(2,1)}, u32[]{:S(2)}, u32[]{:S(2)}) collective-permute-start(bf16[128,2048]{1,0:T(8,128)(2,1)} %add_convert_fusion.2), channel_id=1, source_target_pairs={{0,8},{8,0},{1,9},{9,1},{2,10},{10,2},{3,11},{11,3},{4,12},{12,4},... | collective-permute-start | bytes 1572872 | tf_op jit(solution)/shard_map/cond/branch_1_fun/ppermute | solution.py:836
  274.9 298.7 %reduce-scatter.8.cloned.1.call-start = ((), (), s32[]{:S(2)}) async-start(), calls=%async_computation.5 | async-start | bytes 5242880 | tf_op jit(solution)/shard_map/reduce_scatter | solution.py:948
  279.2 13.9 %collective-permute-start.21 = (bf16[128,2048]{1,0:T(8,128)(2,1)S(1)}, bf16[128,2048]{1,0:T(8,128)(2,1)S(1)}, u32[]{:S(2)}, u32[]{:S(2)}) collective-permute-start(bf16[128,2048]{1,0:T(8,128)(2,1)S(1)} %get-tuple-element.356), channel_id=1, source_target_pairs={{0,2},{2,0},{1,3},{3,1},{4,6},{6,4},{5,7},{7,5},{8,10},{10,8},{9,1... | collective-permute-start | bytes 1572872 | tf_op jit(solution)/shard_map/cond/branch_1_fun/ppermute | solution.py:836
  319.3 38.0 %collective-permute-start.33 = (bf16[256,1024]{1,0:T(8,128)(2,1)}, bf16[256,1024]{1,0:T(8,128)(2,1)}, u32[]{:S(2)}, u32[]{:S(2)}) collective-permute-start(bf16[256,1024]{1,0:T(8,128)(2,1)} %get-tuple-element.402), channel_id=1, source_target_pairs={{0,8},{8,0},{1,9},{9,1},{2,10},{10,2},{3,11},{11,3},{4,12},{12,4},... | collective-permute-start | bytes 1572872 | tf_op jit(solution)/shard_map/ppermute | solution.py:836
  319.3 42.5 %collective-permute-start.34 = (bf16[2048,256]{1,0:T(8,128)(2,1)}, bf16[2048,256]{1,0:T(8,128)(2,1)}, u32[]{:S(2)}, u32[]{:S(2)}) collective-permute-start(bf16[2048,256]{1,0:T(8,128)(2,1)} %get-tuple-element.267), channel_id=1, source_target_pairs={{0,4},{4,0},{1,5},{5,1},{2,6},{6,2},{3,7},{7,3},{8,12},{12,8},{9,1... | collective-permute-start | bytes 3145736 | tf_op jit(solution)/shard_map/ppermute | solution.py:836
  344.1 50.9 %collective-permute-start.35 = (bf16[2048,256]{1,0:T(8,128)(2,1)}, bf16[2048,256]{1,0:T(8,128)(2,1)S(1)}, u32[]{:S(2)}, u32[]{:S(2)}) collective-permute-start(bf16[2048,256]{1,0:T(8,128)(2,1)} %get-tuple-element.271), channel_id=1, source_target_pairs={{0,4},{4,0},{1,5},{5,1},{2,6},{6,2},{3,7},{7,3},{8,12},{12,8},{9,1... | collective-permute-start | bytes 3145736 | tf_op jit(solution)/shard_map/ppermute | solution.py:836
  399.0 26.4 %collective-permute-start.37 = (bf16[1024,256]{1,0:T(8,128)(2,1)}, bf16[1024,256]{1,0:T(8,128)(2,1)}, u32[]{:S(2)}, u32[]{:S(2)}) collective-permute-start(bf16[1024,256]{1,0:T(8,128)(2,1)} %get-tuple-element.381), channel_id=1, source_target_pairs={{0,8},{8,0},{1,9},{9,1},{2,10},{10,2},{3,11},{11,3},{4,12},{12,4},... | collective-permute-start | bytes 1572872 | tf_op jit(solution)/shard_map/ppermute | solution.py:836
  399.0 45.3 %collective-permute-start.36 = (bf16[1024,256]{1,0:T(8,128)(2,1)}, bf16[1024,256]{1,0:T(8,128)(2,1)}, u32[]{:S(2)}, u32[]{:S(2)}) collective-permute-start(bf16[1024,256]{1,0:T(8,128)(2,1)} %get-tuple-element.413), channel_id=1, source_target_pairs={{0,8},{8,0},{1,9},{9,1},{2,10},{10,2},{3,11},{11,3},{4,12},{12,4},... | collective-permute-start | bytes 1572872 | tf_op jit(solution)/shard_map/ppermute | solution.py:836
  401.0 109.7 %collective-permute-start.40 = (bf16[4,256,1024]{2,1,0:T(8,128)(2,1)}, bf16[4,256,1024]{2,1,0:T(8,128)(2,1)}, u32[]{:S(2)}, u32[]{:S(2)}) collective-permute-start(bf16[4,256,1024]{2,1,0:T(8,128)(2,1)} %get-tuple-element.299), channel_id=1, source_target_pairs={{0,4},{4,0},{1,5},{5,1},{2,6},{6,2},{3,7},{7,3},{8,12},{12,8},{9,1... | collective-permute-start | bytes 6291464 | tf_op jit(solution)/shard_map/ppermute | solution.py:836
  401.6 4.4 collective-permute-start.17
  408.9 14.0 %collective-permute-start.18 = (bf16[128,2048]{1,0:T(8,128)(2,1)S(1)}, bf16[128,2048]{1,0:T(8,128)(2,1)S(1)}, u32[]{:S(2)}, u32[]{:S(2)}) collective-permute-start(bf16[128,2048]{1,0:T(8,128)(2,1)S(1)} %get-tuple-element.371), channel_id=1, source_target_pairs={{0,2},{2,0},{1,3},{3,1},{4,6},{6,4},{5,7},{7,5},{8,10},{10,8},{9,1... | collective-permute-start | bytes 1572872 | tf_op jit(solution)/shard_map/cond/branch_1_fun/ppermute | solution.py:836
  446.1 37.4 %collective-permute-start.39 = (bf16[512,256]{1,0:T(8,128)(2,1)S(1)}, bf16[512,256]{1,0:T(8,128)(2,1)S(1)}, u32[]{:S(2)}, u32[]{:S(2)}) collective-permute-start(bf16[512,256]{1,0:T(8,128)(2,1)S(1)} %get-tuple-element.396), channel_id=1, source_target_pairs={{0,16},{16,0},{1,17},{17,1},{2,18},{18,2},{3,19},{19,3},{4,20},{20... | collective-permute-start | bytes 786440 | tf_op jit(solution)/shard_map/ppermute | solution.py:836
  448.0 46.0 %collective-permute-start.38 = (bf16[512,256]{1,0:T(8,128)(2,1)S(1)}, bf16[512,256]{1,0:T(8,128)(2,1)S(1)}, u32[]{:S(2)}, u32[]{:S(2)}) collective-permute-start(bf16[512,256]{1,0:T(8,128)(2,1)S(1)} %get-tuple-element.398), channel_id=1, source_target_pairs={{0,16},{16,0},{1,17},{17,1},{2,18},{18,2},{3,19},{19,3},{4,20},{20... | collective-permute-start | bytes 786440 | tf_op jit(solution)/shard_map/ppermute | solution.py:836
  450.9 13.0 %collective-permute-start.7 = (bf16[128,2048]{1,0:T(8,128)(2,1)}, bf16[128,2048]{1,0:T(8,128)(2,1)S(1)}, u32[]{:S(2)}, u32[]{:S(2)}) collective-permute-start(bf16[128,2048]{1,0:T(8,128)(2,1)} %get-tuple-element.110), channel_id=1, source_target_pairs={{0,2},{2,0},{1,3},{3,1},{4,6},{6,4},{5,7},{7,5},{8,10},{10,8},{9,1... | collective-permute-start | bytes 1572872 | tf_op jit(solution)/shard_map/cond/branch_1_fun/ppermute | solution.py:836
  452.4 27.5 %collective-permute-start.6 = (bf16[128,2048]{1,0:T(8,128)(2,1)}, bf16[128,2048]{1,0:T(8,128)(2,1)}, u32[]{:S(2)}, u32[]{:S(2)}) collective-permute-start(bf16[128,2048]{1,0:T(8,128)(2,1)} %get-tuple-element.109), channel_id=1, source_target_pairs={{0,8},{8,0},{1,9},{9,1},{2,10},{10,2},{3,11},{11,3},{4,12},{12,4},... | collective-permute-start | bytes 1572872 | tf_op jit(solution)/shard_map/cond/branch_1_fun/ppermute | solution.py:836
  515.2 28.3 %collective-permute-start.41 = (bf16[2,256,1024]{2,1,0:T(8,128)(2,1)}, bf16[2,256,1024]{2,1,0:T(8,128)(2,1)}, u32[]{:S(2)}, u32[]{:S(2)}) collective-permute-start(bf16[2,256,1024]{2,1,0:T(8,128)(2,1)} %get-tuple-element.373), channel_id=1, source_target_pairs={{0,8},{8,0},{1,9},{9,1},{2,10},{10,2},{3,11},{11,3},{4,12},{12,4},... | collective-permute-start | bytes 3145736 | tf_op jit(solution)/shard_map/ppermute | solution.py:836
  515.2 29.9 %collective-permute-start.42 = (bf16[4,256,512]{2,1,0:T(8,128)(2,1)}, bf16[4,256,512]{2,1,0:T(8,128)(2,1)}, u32[]{:S(2)}, u32[]{:S(2)}) collective-permute-start(bf16[4,256,512]{2,1,0:T(8,128)(2,1)} %get-tuple-element.314), channel_id=1, source_target_pairs={{0,4},{4,0},{1,5},{5,1},{2,6},{6,2},{3,7},{7,3},{8,12},{12,8},{9,1... | collective-permute-start | bytes 3145736 | tf_op jit(solution)/shard_map/ppermute | solution.py:836
  519.0 31.0 %collective-permute-start.43 = (bf16[256,1024]{1,0:T(8,128)(2,1)}, bf16[256,1024]{1,0:T(8,128)(2,1)}, u32[]{:S(2)}, u32[]{:S(2)}) collective-permute-start(bf16[256,1024]{1,0:T(8,128)(2,1)} %get-tuple-element.394), channel_id=1, source_target_pairs={{0,8},{8,0},{1,9},{9,1},{2,10},{10,2},{3,11},{11,3},{4,12},{12,4},... | collective-permute-start | bytes 1572872 | tf_op jit(solution)/shard_map/ppermute | solution.py:836
  527.1 14.0 %collective-permute-start.20 = (bf16[128,2048]{1,0:T(8,128)(2,1)S(1)}, bf16[128,2048]{1,0:T(8,128)(2,1)S(1)}, u32[]{:S(2)}, u32[]{:S(2)}) collective-permute-start(bf16[128,2048]{1,0:T(8,128)(2,1)S(1)} %add_convert_fusion.11), channel_id=1, source_target_pairs={{0,2},{2,0},{1,3},{3,1},{4,6},{6,4},{5,7},{7,5},{8,10},{10,8},{9,1... | collective-permute-start | bytes 1572872 | tf_op jit(solution)/shard_map/cond/branch_1_fun/ppermute | solution.py:836
  542.2 30.3 %collective-permute-start.45 = (bf16[256,2048]{1,0:T(8,128)(2,1)S(1)}, bf16[256,2048]{1,0:T(8,128)(2,1)S(1)}, u32[]{:S(2)}, u32[]{:S(2)}) collective-permute-start(bf16[256,2048]{1,0:T(8,128)(2,1)S(1)} %pad_maximum_fusion.4), channel_id=1, source_target_pairs={{0,2},{2,0},{1,3},{3,1},{4,6},{6,4},{5,7},{7,5},{8,10},{10,8},{9,1... | collective-permute-start | bytes 3145736 | tf_op jit(solution)/shard_map/ppermute | solution.py:836
  550.0 11.1 %collective-permute-start.44 = (bf16[2,256,512]{2,1,0:T(8,128)(2,1)S(1)}, bf16[2,256,512]{2,1,0:T(8,128)(2,1)S(1)}, u32[]{:S(2)}, u32[]{:S(2)}) collective-permute-start(bf16[2,256,512]{2,1,0:T(8,128)(2,1)S(1)} %get-tuple-element.379), channel_id=1, source_target_pairs={{0,8},{8,0},{1,9},{9,1},{2,10},{10,2},{3,11},{11,3},{4,12},{12,4},... | collective-permute-start | bytes 1572872 | tf_op jit(solution)/shard_map/ppermute | solution.py:836
  561.2 11.2 %collective-permute-start.49 = (bf16[1,256,512]{2,1,0:T(8,128)(2,1)S(1)}, bf16[1,256,512]{2,1,0:T(8,128)(2,1)S(1)}, u32[]{:S(2)}, u32[]{:S(2)}) collective-permute-start(bf16[1,256,512]{2,1,0:T(8,128)(2,1)S(1)} %add_convert_fusion.25), channel_id=1, source_target_pairs={{0,16},{16,0},{1,17},{17,1},{2,18},{18,2},{3,19},{19,3},{4,20},{20... | collective-permute-start | bytes 786440 | tf_op jit(solution)/shard_map/ppermute | solution.py:836
  573.5 41.2 %collective-permute-start.46 = (bf16[512,2048]{1,0:T(8,128)(2,1)}, bf16[512,2048]{1,0:T(8,128)(2,1)}, u32[]{:S(2)}, u32[]{:S(2)}) collective-permute-start(bf16[512,2048]{1,0:T(8,128)(2,1)} %constant_dynamic-update-slice_fusion.10), channel_id=1, source_target_pairs={{0,1},{1,0},{2,3},{3,2},{4,5},{5,4},{6,7},{7,6},{8,9},{9,8},{10,11... | collective-permute-start | bytes 6291464 | tf_op jit(solution)/shard_map/ppermute | solution.py:836
  573.6 38.1 %collective-permute-start.48 = (bf16[1,256,1024]{2,1,0:T(8,128)(2,1)S(1)}, bf16[1,256,1024]{2,1,0:T(8,128)(2,1)}, u32[]{:S(2)}, u32[]{:S(2)}) collective-permute-start(bf16[1,256,1024]{2,1,0:T(8,128)(2,1)S(1)} %get-tuple-element.375), channel_id=1, source_target_pairs={{0,16},{16,0},{1,17},{17,1},{2,18},{18,2},{3,19},{19,3},{4,20},{20... | collective-permute-start | bytes 1572872 | tf_op jit(solution)/shard_map/ppermute | solution.py:836
  574.8 34.2 %collective-permute-start.47 = (bf16[256,1024]{1,0:T(8,128)(2,1)S(1)}, bf16[256,1024]{1,0:T(8,128)(2,1)}, u32[]{:S(2)}, u32[]{:S(2)}) collective-permute-start(bf16[256,1024]{1,0:T(8,128)(2,1)S(1)} %dynamic-slice_bitcast_fusion), channel_id=1, source_target_pairs={{0,8},{8,0},{1,9},{9,1},{2,10},{10,2},{3,11},{11,3},{4,12},{12,4},... | collective-permute-start | bytes 1572872 | tf_op jit(solution)/shard_map/ppermute | solution.py:836
  579.4 5.6 collective-permute-start.9
  585.1 3.8 collective-permute-start.10
  588.9 12.9 %collective-permute-start.11 = (f32[2,2048]{1,0:T(2,128)S(1)}, f32[2,2048]{1,0:T(2,128)S(1)}, u32[]{:S(2)}, u32[]{:S(2)}) collective-permute-start(f32[2,2048]{1,0:T(2,128)S(1)} %add.210), channel_id=1, source_target_pairs={{0,8},{8,0},{1,9},{9,1},{2,10},{10,2},{3,11},{11,3},{4,12},{12,4},... | collective-permute-start | bytes 49160 | tf_op jit(solution)/shard_map/cond/branch_1_fun/ppermute | solution.py:836
  601.8 4.7 collective-permute-start.12
  (44 other events, 417.4 us)
Sparse Core Ops, SparseCore 0:
  206.5 93.1 reduce-scatter.3
  302.8 86.0 reduce-scatter.5
  392.0 103.5 reduce-scatter.7

commit v9 on v8

--- a/solution.py
+++ b/solution.py
@@ -21,6 +21,7 @@
 NEG = -1e30
 SLOTS = 4
 VMEM_LIMIT = 60 << 20
+PAIR_STEPS = (4, 1)
 
 eps_norm = 1e-05
 rope_base = 1000000.0
@@ -101,8 +102,12 @@
 
 
 def tile_pair(ref, rows_a, rows_b, column):
+    return tile(ref, (rows_a, rows_b), column)
+
+
+def tile(ref, rows, column):
     cols = pl.ds(column, HEAD_SIZE)
-    return jnp.concatenate([ref[rows_a, cols], ref[rows_b, cols]], axis=0)
+    return jnp.concatenate([ref[span, cols] for span in rows], axis=0)
 
 
 def own_mask(has_prev, rep):
@@ -171,24 +176,34 @@
             acc_ref[h] = dot(values.T, weights.astype(jnp.bfloat16))
             state += [best, total]
 
-        def one_pair(t, state):
-            rows_a = key_rows(inverse_ref, base + 2 * t)
-            rows_b = key_rows(inverse_ref, base + 2 * t + 1)
+        def fold(first, count, state):
+            rows = [key_rows(inverse_ref, first + n) for n in range(count)]
             after = []
             for h in range(hps):
                 best, total = state[2 * h], state[2 * h + 1]
-                keys = tile_pair(kv_ref, rows_a, rows_b, 2 * h * HEAD_SIZE)
+                keys = tile(kv_ref, rows, 2 * h * HEAD_SIZE)
                 scores = dot(keys, qt_ref[h]) * factor
                 newest = jnp.maximum(best, jnp.max(scores, axis=0, keepdims=True))
                 weights = jnp.exp2(scores - newest)
                 shrink = jnp.exp2(best - newest)
                 total = total * shrink + jnp.sum(weights, axis=0, keepdims=True)
-                values = tile_pair(kv_ref, rows_a, rows_b, (2 * h + 1) * HEAD_SIZE)
+                values = tile(kv_ref, rows, (2 * h + 1) * HEAD_SIZE)
                 acc_ref[h] = acc_ref[h] * shrink + dot(values.T, weights.astype(jnp.bfloat16))
                 after += [newest, total]
             return tuple(after)
 
-        state = lax.fori_loop(0, pairs, one_pair, tuple(state))
+        state, done = tuple(state), 0
+        for wide in PAIR_STEPS:
+            upto = lax.div(pairs, wide) * wide
+            state = lax.fori_loop(
+                0,
+                lax.div(upto - done, wide),
+                lambda t, state, done=done, wide=wide: fold(
+                    base + 2 * (done + wide * t), 2 * wide, state
+                ),
+                state,
+            )
+            done = upto
         for h in range(hps):
             best, total = state[2 * h], state[2 * h + 1]
             mixed = acc_ref[h] * (1.0 / total)
@@ -233,10 +248,10 @@
 
     lax.fori_loop(0, order_ref.shape[0], clear, 0)
 
-    def tile_terms(h, rows_a, rows_b, lse, delta, q_rows, gm_rows, mask):
+    def tile_terms(h, spans, lse, delta, q_rows, gm_rows, mask):
         kcol, vcol = 2 * h * HEAD_SIZE, (2 * h + 1) * HEAD_SIZE
-        keys = tile_pair(kv_ref, rows_a, rows_b, kcol)
-        values = tile_pair(kv_ref, rows_a, rows_b, vcol)
+        keys = tile(kv_ref, spans, kcol)
+        values = tile(kv_ref, spans, vcol)
         weights = jnp.exp2(dot(keys, qt_ref[h]) * factor - lse)
         if mask is not None:
             weights = jnp.where(mask, weights, 0.0)
@@ -244,10 +259,10 @@
         grad_scores = (weights * (grad_weights - delta)).astype(jnp.bfloat16)
         gv = dot(weights.astype(jnp.bfloat16), gm_rows)
         gk = dot(grad_scores, q_rows)
-        acc_ref[rows_a, pl.ds(kcol, HEAD_SIZE)] += gk[:BLOCK]
-        acc_ref[rows_b, pl.ds(kcol, HEAD_SIZE)] += gk[BLOCK:]
-        acc_ref[rows_a, pl.ds(vcol, HEAD_SIZE)] += gv[:BLOCK]
-        acc_ref[rows_b, pl.ds(vcol, HEAD_SIZE)] += gv[BLOCK:]
+        for n, span in enumerate(spans):
+            piece = slice(n * BLOCK, (n + 1) * BLOCK)
+            acc_ref[span, pl.ds(kcol, HEAD_SIZE)] += gk[piece]
+            acc_ref[span, pl.ds(vcol, HEAD_SIZE)] += gv[piece]
         return dot(keys.T, grad_scores)
 
     def one_query_block(qb, carry):
@@ -271,21 +286,29 @@
             q_rows = stack_rows(q_ref, rows, h * width, rep)
             gm_rows = stack_rows(gm_ref, rows, h * width, rep)
             gqt_ref[h] = tile_terms(
-                h, rows_a, rows_b, lses[h], deltas[h], q_rows, gm_rows, mask
+                h, (rows_a, rows_b), lses[h], deltas[h], q_rows, gm_rows, mask
             )
 
-        def one_pair(t, carry):
-            rows_a = key_rows(inverse_ref, base + 2 * t)
-            rows_b = key_rows(inverse_ref, base + 2 * t + 1)
+        def fold(first, count):
+            spans = [key_rows(inverse_ref, first + n) for n in range(count)]
             for h in range(hps):
                 q_rows = stack_rows(q_ref, rows, h * width, rep)
                 gm_rows = stack_rows(gm_ref, rows, h * width, rep)
                 gqt_ref[h] += tile_terms(
-                    h, rows_a, rows_b, lses[h], deltas[h], q_rows, gm_rows, None
+                    h, spans, lses[h], deltas[h], q_rows, gm_rows, None
                 )
-            return carry
-
-        lax.fori_loop(0, pairs, one_pair, 0)
+            return 0
+
+        done = 0
+        for wide in PAIR_STEPS:
+            upto = lax.div(pairs, wide) * wide
+            lax.fori_loop(
+                0,
+                lax.div(upto - done, wide),
+                lambda t, _, done=done, wide=wide: fold(base + 2 * (done + wide * t), 2 * wide),
+                0,
+            )
+            done = upto
         for h in range(hps):
             total = gqt_ref[h] * scale
             for r in range(rep):
@@ -507,7 +530,7 @@
     )(order, cont, where, gain.reshape(1, -1), x, wq, wk, wv, table)
 
 
-FILLERS = ("ffn_out", "gate_shares", "up_shares", "kv_shares", "grad_hidden", "grad_second_keep")
+FILLERS = ("ffn_out", "gate_shares", "kv_shares", "grad_hidden")
 
 
 def cost(name, flops, bytes_accessed):
@@ -1107,73 +1130,21 @@
         True,
         where,
     )
-    sum_down = join_halves(down_own, after(branch_shares[0], down_other), ctx).T
-    kv = [item.merge(sum_down) for item in kv]
-    dep = tuple(keep for keep, _ in kv)
-    branch = Reduce(*after(dep, *branch_shares))
-
-    got = [ctx_flip(value, 2) for _, value in kv]
-
     def out_stage(keep, send):
         got = flip(send, "core")
         n = keep.shape[0] // 4
         near = [add(keep[k * n : (k + 1) * n], got[k * n : (k + 1) * n]) for k in range(4)]
         return near[0], near[2], add(near[1], flip(near[3], "y"))
 
-    out_near, out_own, out_away = stage(out_stage, *after(dep, *ffn_halves))
-    for mask in highs:
-        kv = [KvReduce(keep, value).merge(out_away) for (keep, _), value in zip(kv, got)]
-        got = [ctx_flip(value, mask) for _, value in kv]
-    out_far, out_got = stage(
-        lambda away, own: (ctx_flip(away, 2), flip(own, "y")),
-        *after(tuple(keep for keep, _ in kv), out_away, out_own),
-    )
-    got = [after(out_far, value) for value in got]
-    kv = [(keep, value) for (keep, _), value in zip(kv, got)]
-    gate_own, gate_away = split_halves(gate, ctx, tuple(got))
-    gate_other = ctx_flip(gate_away, 2)
-    dep = gate_own
-    output = (middle + total((out_near, out_got, after(dep, out_far)))).astype(jnp.bfloat16)
-    keep, send, grad_kv = tail_stage(
-        [(keep, after(dep, value)) for keep, value in kv], cosine, sine, grad_queries,
-        w_query, key_matrix, value_matrix, where,
-    )
-
-    kv_shares = weight_shares(
-        "kv_shares", (first_input,), (after(keep, grad_kv),), ((0, 0),), ctx_count, True, where
-    )
-    branch.halve(2, ctx, kv_shares[0])
-    last = Reduce(*after(branch.keep, *kv_shares))
-
     def first_stage(keep, send, own_input, grad_middle):
         terms = scatter_slots(keep, send)
         inv = lax.rsqrt(jnp.mean(own_input * own_input, axis=-1, keepdims=True) + eps_norm)
         grad_norm, gain_part = norm_back(total(terms), own_input * inv, inv, attn_gain)
         return gain_part, (grad_middle + grad_norm).astype(jnp.bfloat16)
 
-    attn_gain_part, grad_input = stage(
-        first_stage, after(branch.keep, keep), send, own_input, grad_middle
-    )
-    near = jnp.concatenate([grad_input, after(grad_input, output)])
-    near_other = flip(near, "y")
-    dep = grad_input
-    for mask in highs:
-        branch.halve(mask, ctx, dep)
-        dep = branch.keep
-    last.halve(2, ctx, dep)
-    sum_gate = join_halves(gate_own, after(last.keep, gate_other), ctx)
-    dep = sum_gate
-    for mask in highs:
-        last.halve(mask, ctx, dep)
-        dep = last.keep
-    near = jnp.concatenate([near, after(dep, near_other)])
-    far = flip(near, "core")
-    quarters = [near[n * quarter : (n + 1) * quarter] for n in range(4)]
-    quarters += [far[n * quarter : (n + 1) * quarter] for n in range(4)]
-    grad_input, output = [
-        place_rows(quarters[k], quarters[k + 2], quarters[k + 4], quarters[k + 6], tensor)
-        for k in range(2)
-    ]
+    def row_stage(near, other):
+        near = jnp.concatenate([near, other])
+        return near, flip(near, "core")
 
     def gain_stage(gains):
         gains = gains + flip(gains, "core")
@@ -1182,13 +1153,82 @@
             gains = gains + ctx_flip(gains, mask)
         return gains
 
+    dep = branch_shares[0]
+    kv = [item.merge(dep) for item in kv]
+    dep = tuple(keep for keep, _ in kv)
+    sum_down = join_halves(down_own, after(dep, down_other), ctx).T
+    dep = sum_down
+    got = [ctx_flip(after(dep, value), 2) for _, value in kv]
+    branch = Reduce(*after(dep, *branch_shares))
+    out_near, out_own, out_away = stage(out_stage, *after(dep, *ffn_halves))
+    dep = out_away
+    for mask in highs:
+        kv = [
+            KvReduce(keep, value).merge(dep) for (keep, _), value in zip(kv, got)
+        ]
+        got = [ctx_flip(value, mask) for _, value in kv]
+    dep = tuple(keep for keep, _ in kv)
+    gate_own, gate_away = split_halves(gate, ctx, dep)
+    dep = gate_own
+    gate_other = ctx_flip(after(dep, gate_away), 2)
+    out_far, out_got = stage(
+        lambda away, own: (ctx_flip(away, 2), flip(own, "y")), *after(dep, out_away, out_own)
+    )
+    dep = out_far
+    branch.halve(2, ctx, dep)
+    dep = branch.keep
+    output = (middle + total(after(dep, out_near, out_got, out_far))).astype(jnp.bfloat16)
+    dep = output
+    keep, send, grad_kv = tail_stage(
+        [after(dep, keep, value) for (keep, _), value in zip(kv, got)], cosine, sine,
+        grad_queries, w_query, key_matrix, value_matrix, where,
+    )
+    dep = keep
+    kv_shares = weight_shares(
+        "kv_shares", (first_input,), (after(dep, grad_kv),), ((0, 0),), ctx_count, True, where
+    )
+    dep = kv_shares[0]
+    last = Reduce(*after(dep, *kv_shares))
+    attn_gain_part, grad_input = stage(
+        first_stage, after(dep, keep), send, own_input, grad_middle
+    )
+    dep = grad_input
+    near = jnp.concatenate([grad_input, output])
+    near_other = flip(after(dep, near), "y")
+    for mask in highs:
+        branch.halve(mask, ctx, dep)
+        dep = branch.keep
+    last.halve(2, ctx, dep)
+    dep = last.keep
+    sum_gate = join_halves(gate_own, after(dep, gate_other), ctx)
+    dep = sum_gate
+    for mask in highs:
+        last.halve(mask, ctx, dep)
+        dep = last.keep
+    near, far = stage(row_stage, near, after(dep, near_other))
+    dep = far
+    last.keep, last.got = after(dep, last.keep, last.got)
+    last_sum = last.sum()
+    dep = last_sum
+    quarters = [near[n * quarter : (n + 1) * quarter] for n in range(4)]
+    quarters += [after(dep, far)[n * quarter : (n + 1) * quarter] for n in range(4)]
+    grad_rows, output_rows = [
+        place_rows(quarters[k], quarters[k + 2], quarters[k + 4], quarters[k + 6], tensor)
+        for k in range(2)
+    ]
+    dep = (grad_rows, output_rows)
     up_own, up_away = split_halves(up, ctx, dep)
-    up_other = ctx_flip(up_away, 2)
-    gains = stage(gain_stage, after(near, jnp.stack([attn_gain_part, ffn_gain_part])))
-    sum_up = join_halves(up_own, after(gains, up_other), ctx)
-    branch.keep, branch.got = after(sum_up, branch.keep, branch.got)
+    dep = up_own
+    up_other = ctx_flip(after(dep, up_away), 2)
+    gains = stage(gain_stage, after(dep, jnp.stack([attn_gain_part, ffn_gain_part])))
+    dep = gains
+    sum_up = join_halves(up_own, after(dep, up_other), ctx)
+    dep = sum_up
+    branch.keep, branch.got = after(dep, branch.keep, branch.got)
+    branch_sum = branch.sum()
+    dep = branch_sum
+    grad_input, output = grad_rows, output_rows
     width_q, width_k = w_query.shape[1], key_matrix.shape[1]
-    branch_sum, last_sum = branch.sum(), last.sum()
     sum_query, sum_out = branch_sum[:, :width_q], branch_sum[:, width_q:].T
     sum_key, sum_value = last_sum[:, :width_k], last_sum[:, width_k:]
 

time: 626 us -> 612 us (0.978); the launches traced: 627 us -> 606 us
  waiting for transfers between devices: 279 us -> 268 us
  Pallas kernels: 174 us -> 165 us
  starting transfers between devices: 61.6 us -> 53.2 us
    ppermute x50, waiting for transfers between devices: 279 us -> 268 us  [flip(): lax.ppermute(value, axis, [(i, i ^ mask) for i in range(lax.axis_size(axi...]
    ppermute x50, starting transfers between devices: 61.5 us -> 53.1 us  [flip(): lax.ppermute(value, axis, [(i, i ^ mask) for i in range(lax.axis_size(axi...]
    convert_element_type x12 -> x13, other arithmetic: 23.3 us -> 29.7 us  [add(): (left.astype(jnp.float32) + right.astype(jnp.float32)).astype(jnp.bfloat16)]
    unnamed x83 -> x62, local copies, waits for them, and re-layouts: 23.8 us -> 20.9 us
  transfers between devices with their start and end apart: 53 -> 53, of which waited for: 39 -> 37; matrix products, arithmetic and copies ran while one was open for 11% -> 13% of each run, Pallas kernels for 20% -> 19%
where the time goes in v9:
time: 612 us; the launch traced here: 606 us
  waiting for transfers between devices  268 us (44%)
  Pallas kernels  165 us (27%)
  other arithmetic  55.2 us (9%)
  starting transfers between devices  53.2 us (9%)
  local copies, waits for them, and re-layouts  48.1 us (8%)
  between operations  15.3 us (2%)
    ppermute x50, waiting for transfers between devices, flip(): lax.ppermute(value, axis, [(i, i ^ mask) for i in range(lax.axis_size(axi...  268 us
    ppermute x50, starting transfers between devices, flip(): lax.ppermute(value, axis, [(i, i ^ mask) for i in range(lax.axis_size(axi...  53.1 us
    pallas_call x3, Pallas kernels, unit_shares(): pl.pallas_call(unit_shares_kernel, out_shape=shares, grid_spec=pltpu.Pref...  31.5 us
    pallas_call x2, Pallas kernels, attention_backward(): pl.pallas_call(functools.partial(backward_kernel, rep, 1, ctx_count, head...  29.7 us
    convert_element_type x13, other arithmetic, add(): (left.astype(jnp.float32) + right.astype(jnp.float32)).astype(jnp.bfloat16)  29.7 us
    unnamed x62, local copies, waits for them, and re-layouts  20.9 us
    pallas_call x1, Pallas kernels, attention_forward(): pl.pallas_call(functools.partial(forward_kernel, rep, kv_heads, ctx_count...  20.4 us
    pallas_call x2, Pallas kernels, grad_second_half(): pl.pallas_call(grad_second_kernel, out_shape=jax.ShapeDtypeStruct((rows,...  17.9 us
  transfers between devices with their start and end apart: 53, of which 37 were waited for; matrix products, arithmetic and copies ran while one was open for 13% of the time, Pallas kernels for 19%

profile of v9, /device:TPU:0, one launch (start us, length us, event | category | flops | bytes accessed | tf_op | source)
XLA Modules:
  0.0 605.5 jit_solution(15446451331659983476)
XLA Ops:
  13.0 7.2 %input_stage.1 = (bf16[512,2048]{1,0:T(8,128)(2,1)}, bf16[512,512]{1,0:T(8,128)(2,1)}, bf16[512,512]{1,0:T(8,128)(2,1)S(1)}, f32[512,128]{1,0:T(8,128)}, f32[512,128]{1,0:T(8,128)}) custom-call(s32[32]{0:T(128)} %order_ref.7, s32[8]{0:T(128)} %cont_ref.7, s32[2]{0:T(128)S(1)} %pad_add_fusion.where_ref, f32[1,2048]{1,0:T(1,128)} %bitcast.31, ...), custom_call_target="tpu_custom_call" | custom-call | flops 42949672 | bytes 167772 | tf_op jit(solution)/shard_map/input_stage/pallas_call | solution.py:512
  20.2 4.0 collective-permute-done.26
  24.2 14.4 %conditional.11 = (bf16[512,512]{1,0:T(8,128)(2,1)}, bf16[512,512]{1,0:T(8,128)(2,1)}, bf16[512,512]{1,0:T(8,128)(2,1)S(1)}) conditional(s32[]{:T(128)} %bitcast.2, () %tuple.154, bf16[512,512]{1,0:T(8,128)(2,1)S(1)} %get-tuple-element.248.refs_0_), branch_computations={%region_0.0_spmd, %region_1.0_spmd} | conditional | bytes 5242984 | solution.py:895
  27.4 10.0 %collective-permute-done = bf16[512,512]{1,0:T(8,128)(2,1)} collective-permute-done((bf16[512,512]{1,0:T(8,128)(2,1)S(1)}, bf16[512,512]{1,0:T(8,128)(2,1)}, u32[]{:S(2)}, u32[]{:S(2)}) %collective-permute-start) | collective-permute-done | bytes 524320 | tf_op jit(solution)/shard_map/cond/branch_1_fun/ppermute | solution.py:859
  41.1 11.4 %conditional.12 = (bf16[512,512]{1,0:T(8,128)(2,1)}) conditional(s32[]{:T(128)} %bitcast.2, () %tuple.153, bf16[512,512]{1,0:T(8,128)(2,1)S(1)} %get-tuple-element.246), branch_computations={%region_2.0_spmd, %region_3.0_spmd} | conditional | bytes 2097200 | solution.py:895
  42.6 10.0 %collective-permute-done.2 = bf16[512,512]{1,0:T(8,128)(2,1)} collective-permute-done((bf16[512,512]{1,0:T(8,128)(2,1)S(1)}, bf16[512,512]{1,0:T(8,128)(2,1)}, u32[]{:S(2)}, u32[]{:S(2)}) %collective-permute-start.2) | collective-permute-done | bytes 524320 | tf_op jit(solution)/shard_map/cond/branch_1_fun/ppermute | solution.py:859
  55.3 7.5 %collective-permute-done.27.refs_4_ = bf16[512,512]{1,0:T(8,128)(2,1)S(1)} collective-permute-done((bf16[512,512]{1,0:T(8,128)(2,1)S(1)}, bf16[512,512]{1,0:T(8,128)(2,1)S(1)}, u32[]{:S(2)}, u32[]{:S(2)}) %collective-permute-start.27) | collective-permute-done | bytes 524320 | tf_op jit(solution)/shard_map/ppermute | solution.py:859
  62.7 15.1 %conditional.13 = (bf16[512,512]{1,0:T(8,128)(2,1)}, bf16[512,512]{1,0:T(8,128)(2,1)}, bf16[128,2048]{1,0:T(8,128)(2,1)}) conditional(s32[]{:T(128)} %bitcast.2, () %tuple.152, (bf16[512,512]{1,0:T(8,128)(2,1)S(1)}, bf16[128,2048]{1,0:T(8,128)(2,1)S(1)}) %tuple.158), branch_computations={%region_4.0_spmd, %region_5.0_spmd} | conditional | bytes 6291600 | solution.py:895
  66.0 10.1 %collective-permute-done.3 = bf16[512,512]{1,0:T(8,128)(2,1)} collective-permute-done((bf16[512,512]{1,0:T(8,128)(2,1)S(1)}, bf16[512,512]{1,0:T(8,128)(2,1)}, u32[]{:S(2)}, u32[]{:S(2)}) %collective-permute-start.3) | collective-permute-done | bytes 524320 | tf_op jit(solution)/shard_map/cond/branch_1_fun/ppermute | solution.py:859
  80.8 14.9 %conditional.14 = (bf16[512,512]{1,0:T(8,128)(2,1)}, bf16[256,2048]{1,0:T(8,128)(2,1)}, bf16[128,2048]{1,0:T(8,128)(2,1)S(1)}, bf16[128,2048]{1,0:T(8,128)(2,1)S(1)}) conditional(s32[]{:T(128)} %bitcast.2, () %tuple.159, (bf16[512,512]{1,0:T(8,128)(2,1)}, bf16[256,2048]{1,0:T(8,128)(2,1)S(1)}) %tuple.160), branch_computations={%region_6.0_spmd, %region_7.0_spmd} | conditional | bytes 8388720 | solution.py:895
  85.0 10.6 %collective-permute-done.24 = bf16[512,512]{1,0:T(8,128)(2,1)} collective-permute-done((bf16[512,512]{1,0:T(8,128)(2,1)}, bf16[512,512]{1,0:T(8,128)(2,1)}, u32[]{:S(2)}, u32[]{:S(2)}) %collective-permute-start.24) | collective-permute-done | bytes 524320 | tf_op jit(solution)/shard_map/cond/branch_1_fun/ppermute | solution.py:859
  101.3 20.4 %attention_forward.1 = (bf16[512,512]{1,0:T(8,128)(2,1)}, f32[2,4,256]{2,1,0:T(4,128)}, bf16[256,2048]{1,0:T(8,128)(2,1)}, bf16[256,2048]{1,0:T(8,128)(2,1)}) custom-call(s32[32]{0:T(128)} %order_ref.7, s32[8]{0:T(128)} %cont_ref.7, s32[2]{0:T(128)S(1)} %pad_add_fusion.where_ref, bf16[512,512]{1,0:T(8,128)(2,1)} %get-tuple-element.255.q_ref, ...), custom_call_target="tpu_custom_call" | custom-call | flops 64424508 | bytes 167772 | tf_op jit(solution)/shard_map/attention_forward/pallas_call | solution.py:367
  128.8 9.7 %grad_hidden.1.gh_ref = f32[1024,1024]{1,0:T(8,128)} custom-call(s32[2]{0:T(128)S(1)} %pad_add_fusion.where_ref, bf16[1024,2048]{1,0:T(8,128)(2,1)} %constant_dynamic-update-slice_fusion.2.cot_ref.left_ref, bf16[2048,2048]{1,0:T(8,128)(2,1)} %wd_ref.1), custom_call_target="tpu_custom_call" | custom-call | flops 68719476736 | bytes 134217728 | tf_op jit(solution)/shard_map/grad_hidden/pallas_call | solution.py:570
  145.2 11.5 %collective-permute-done.30 = bf16[128,2048]{1,0:T(8,128)(2,1)S(1)} collective-permute-done((bf16[128,2048]{1,0:T(8,128)(2,1)S(1)}, bf16[128,2048]{1,0:T(8,128)(2,1)S(1)}, u32[]{:S(2)}, u32[]{:S(2)}) %collective-permute-start.30) | collective-permute-done | bytes 524320 | tf_op jit(solution)/shard_map/ppermute | solution.py:859
  158.3 10.7 %collective-permute-done.32 = bf16[128,2048]{1,0:T(8,128)(2,1)S(1)} collective-permute-done((bf16[128,2048]{1,0:T(8,128)(2,1)S(1)}, bf16[128,2048]{1,0:T(8,128)(2,1)S(1)}, u32[]{:S(2)}, u32[]{:S(2)}) %collective-permute-start.32) | collective-permute-done | bytes 524320 | tf_op jit(solution)/shard_map/ppermute | solution.py:859
  175.0 15.6 %ffn_stage.1 = (bf16[1024,1024]{1,0:T(8,128)(2,1)}, bf16[1024,1024]{1,0:T(8,128)(2,1)}, bf16[1024,1024]{1,0:T(8,128)(2,1)S(1)}) custom-call(s32[2]{0:T(128)S(1)} %pad_add_fusion.where_ref, bf16[1024,2048]{1,0:T(8,128)(2,1)} %constant_dynamic-update-slice_fusion.7.in_ref, f32[1024,1024]{1,0:T(8,128)} %grad_hidden.1.gh_ref, bf16[2048,2048]{1,0:T(8,128)(2,1)} %wg_ref.3, ...), custom_call_target="tpu_custom_call" | custom-call | flops 171798688 | bytes 251658 | tf_op jit(solution)/shard_map/ffn_stage/pallas_call | solution.py:609
  190.6 10.8 %down_shares.1 = bf16[8,256,1024]{2,1,0:T(8,128)(2,1)} custom-call(s32[2]{0:T(128)S(1)} %pad_add_fusion.where_ref, bf16[1024,2048]{1,0:T(8,128)(2,1)} %constant_dynamic-update-slice_fusion.2.cot_ref.left_ref, bf16[1024,1024]{1,0:T(8,128)(2,1)} %get-tuple-element.263.right_ref), custom_call_target="tpu_custom_call" | custom-call | flops 85899344 | bytes 167772 | tf_op jit(solution)/shard_map/down_shares/pallas_call | solution.py:789
  201.5 9.0 %grad_second_send.1 = bf16[512,2048]{1,0:T(8,128)(2,1)} custom-call(s32[2]{0:T(128)S(1)} %pad_add_fusion.where_ref, bf16[1024,1024]{1,0:T(8,128)(2,1)} %get-tuple-element.266.gg_ref, bf16[1024,1024]{1,0:T(8,128)(2,1)S(1)} %get-tuple-element.267.gu_ref, bf16[2048,2048]{1,0:T(8,128)(2,1)} %wg_ref.3, bf16[2048,2048]{1,0:T(8,128)(2,1)} %wu_ref.3), custom_call_target="tpu_custom_call" | custom-call | flops 85899344 | bytes 83886 | tf_op jit(solution)/shard_map/grad_second_send/pallas_call | solution.py:641
  210.4 59.0 %conditional.15 = (f32[128,2048]{1,0:T(8,128)}, bf16[8,256,1024]{2,1,0:T(8,128)(2,1)}, bf16[512,2048]{1,0:T(8,128)(2,1)}, bf16[512,2048]{1,0:T(8,128)(2,1)}) conditional(s32[]{:T(128)} %bitcast.2, () %tuple.167, (s32[2]{0:T(128)S(1)}, bf16[1024,1024]{1,0:T(8,128)(2,1)}, bf16[1024,1024]{1,0:T(8,128)(2,1)S(1)}, bf16[2048,2048]{1,0:T(8,128)(2,1)}, ...), branch_computations={%region_9.0_spmd, %region_10.0_spmd} | conditional | flops 137531408384 | bytes 292636768 | solution.py:895
  210.8 8.9 %grad_second_keep.1 = bf16[512,2048]{1,0:T(8,128)(2,1)} custom-call(s32[2]{0:T(128)S(1)} %get-tuple-element.82.where_ref, bf16[1024,1024]{1,0:T(8,128)(2,1)} %get-tuple-element.89.gg_ref.right_ref, bf16[1024,1024]{1,0:T(8,128)(2,1)S(1)} %get-tuple-element.84.gu_ref, bf16[2048,2048]{1,0:T(8,128)(2,1)} %get-tuple-element.85.wg_ref, ...), custom_call_target="tpu_custom_call" | custom-call | flops 85899344 | bytes 83886 | tf_op jit(solution)/shard_map/cond/branch_1_fun/grad_second_keep/pallas_call | solution.py:641
  225.1 10.8 %gate_shares.1 = bf16[8,256,1024]{2,1,0:T(8,128)(2,1)} custom-call(s32[2]{0:T(128)S(1)} %get-tuple-element.82.where_ref, bf16[1024,2048]{1,0:T(8,128)(2,1)} %get-tuple-element.88.left_ref, bf16[1024,1024]{1,0:T(8,128)(2,1)} %get-tuple-element.89.gg_ref.right_ref), custom_call_target="tpu_custom_call" | custom-call | flops 68719476736 | bytes 134217728 | tf_op jit(solution)/shard_map/cond/branch_1_fun/gate_shares/pallas_call | solution.py:789
  241.5 8.7 %ffn_out.1 = (bf16[512,2048]{1,0:T(8,128)(2,1)}, bf16[512,2048]{1,0:T(8,128)(2,1)}) custom-call(s32[2]{0:T(128)S(1)} %get-tuple-element.82.where_ref, bf16[1024,1024]{1,0:T(8,128)(2,1)} %get-tuple-element.92.hid_ref, bf16[2048,2048]{1,0:T(8,128)(2,1)} %get-tuple-element.93.wd_ref), custom_call_target="tpu_custom_call" | custom-call | flops 68719476736 | bytes 134217728 | tf_op jit(solution)/shard_map/cond/branch_1_fun/ffn_out/pallas_call | solution.py:674
  250.2 16.9 %collective-permute-done.16 = bf16[128,2048]{1,0:T(8,128)(2,1)} collective-permute-done((bf16[128,2048]{1,0:T(8,128)(2,1)}, bf16[128,2048]{1,0:T(8,128)(2,1)}, u32[]{:S(2)}, u32[]{:S(2)}) %collective-permute-start.16) | collective-permute-done | bytes 524320 | tf_op jit(solution)/shard_map/cond/branch_1_fun/ppermute | solution.py:859
  270.6 18.6 %conditional.16 = (f32[128,2048]{1,0:T(8,128)}, bf16[8,256,1024]{2,1,0:T(8,128)(2,1)}, bf16[512,2048]{1,0:T(8,128)(2,1)S(1)}, f32[1,2048]{1,0:T(1,128)S(1)}) conditional(s32[]{:T(128)} %bitcast.2, () %tuple.166, (bf16[128,2048]{1,0:T(8,128)(2,1)}, f32[128]{0:T(128)S(1)}, f32[2048]{0:T(1024)S(1)}, f32[128,2048]{1,0:T(8,128)}, ...), branch_computations={%region_11.0_spmd, %region_12.15_spmd} | conditional | flops 97431632 | bytes 21166568 | solution.py:895
  274.7 10.0 %up_shares.1 = bf16[8,256,1024]{2,1,0:T(8,128)(2,1)} custom-call(s32[2]{0:T(128)S(1)} %get-tuple-element.104.where_ref, bf16[1024,2048]{1,0:T(8,128)(2,1)} %get-tuple-element.105.left_ref, bf16[1024,1024]{1,0:T(8,128)(2,1)S(1)} %get-tuple-element.107.right_ref), custom_call_target="tpu_custom_call" | custom-call | flops 85899344 | bytes 167772 | tf_op jit(solution)/shard_map/cond/branch_1_fun/up_shares/pallas_call | solution.py:789
  289.3 14.9 %attention_backward_0.1 = (bf16[512,256]{1,0:T(8,128)(2,1)}, bf16[2048,256]{1,0:T(8,128)(2,1)}, bf16[2048,256]{1,0:T(8,128)(2,1)}) custom-call(s32[32]{0:T(128)} %order_ref.7, s32[8]{0:T(128)} %cont_ref.7, s32[2]{0:T(128)S(1)} %pad_add_fusion.where_ref, bf16[512,512]{1,0:T(8,128)(2,1)} %get-tuple-element.255.q_ref, ...), custom_call_target="tpu_custom_call" | custom-call | flops 64424508 | bytes 125829 | tf_op jit(solution)/shard_map/attention_backward_0/pallas_call | solution.py:403
  306.7 14.8 %attention_backward_1.1 = (bf16[512,256]{1,0:T(8,128)(2,1)}, bf16[2048,256]{1,0:T(8,128)(2,1)}, bf16[2048,256]{1,0:T(8,128)(2,1)}) custom-call(s32[32]{0:T(128)} %order_ref.7, s32[8]{0:T(128)} %cont_ref.7, s32[2]{0:T(128)S(1)} %pad_add_fusion.where_ref, bf16[512,512]{1,0:T(8,128)(2,1)} %get-tuple-element.255.q_ref, ...), custom_call_target="tpu_custom_call" | custom-call | flops 64424508 | bytes 125829 | tf_op jit(solution)/shard_map/attention_backward_1/pallas_call | solution.py:403
  322.7 9.0 %branch_shares.1 = (bf16[4,256,1024]{2,1,0:T(8,128)(2,1)}, bf16[4,256,1024]{2,1,0:T(8,128)(2,1)}) custom-call(s32[2]{0:T(128)S(1)} %pad_add_fusion.where_ref, bf16[512,2048]{1,0:T(8,128)(2,1)} %get-tuple-element.243.refs_0_, bf16[512,2048]{1,0:T(8,128)(2,1)S(1)} %get-tuple-element.276.gb_ref.refs_1_, bf16[512,256]{1,0:T(8,128)(2,1)} %get-tuple-element.274.refs_2_.refs_6_, ...), custom_call_target="tpu_custom_call" | custom-call | flops 42949672 | bytes 83886 | tf_op jit(solution)/shard_map/branch_shares/pallas_call | solution.py:745
  331.8 13.6 %collective-permute-done.34 = bf16[2048,256]{1,0:T(8,128)(2,1)} collective-permute-done((bf16[2048,256]{1,0:T(8,128)(2,1)}, bf16[2048,256]{1,0:T(8,128)(2,1)}, u32[]{:S(2)}, u32[]{:S(2)}) %collective-permute-start.34) | collective-permute-done | bytes 1048608 | tf_op jit(solution)/shard_map/ppermute | solution.py:859
  345.3 33.3 %collective-permute-done.35 = bf16[2048,256]{1,0:T(8,128)(2,1)S(1)} collective-permute-done((bf16[2048,256]{1,0:T(8,128)(2,1)}, bf16[2048,256]{1,0:T(8,128)(2,1)S(1)}, u32[]{:S(2)}, u32[]{:S(2)}) %collective-permute-start.35) | collective-permute-done | bytes 1048608 | tf_op jit(solution)/shard_map/ppermute | solution.py:859
  387.2 22.8 %conditional.17 = (bf16[128,2048]{1,0:T(8,128)(2,1)}, bf16[128,2048]{1,0:T(8,128)(2,1)}, bf16[128,2048]{1,0:T(8,128)(2,1)}) conditional(s32[]{:T(128)} %bitcast.2, () %tuple.165, (bf16[512,2048]{1,0:T(8,128)(2,1)}, bf16[512,2048]{1,0:T(8,128)(2,1)}) %tuple.178), branch_computations={%region_16.17_spmd, %region_17.0_spmd} | conditional | flops 5242880 | bytes 17301608 | solution.py:895
  387.6 4.4 collective-permute-done.17
  394.9 12.3 %collective-permute-done.18 = bf16[128,2048]{1,0:T(8,128)(2,1)S(1)} collective-permute-done((bf16[128,2048]{1,0:T(8,128)(2,1)S(1)}, bf16[128,2048]{1,0:T(8,128)(2,1)S(1)}, u32[]{:S(2)}, u32[]{:S(2)}) %collective-permute-start.18) | collective-permute-done | bytes 524320 | tf_op jit(solution)/shard_map/cond/branch_1_fun/ppermute | solution.py:859
  410.0 15.1 %collective-permute-done.37 = bf16[1024,256]{1,0:T(8,128)(2,1)} collective-permute-done((bf16[1024,256]{1,0:T(8,128)(2,1)}, bf16[1024,256]{1,0:T(8,128)(2,1)}, u32[]{:S(2)}, u32[]{:S(2)}) %collective-permute-start.37) | collective-permute-done | bytes 524320 | tf_op jit(solution)/shard_map/ppermute | solution.py:859
  434.2 20.2 %conditional.18 = (bf16[128,2048]{1,0:T(8,128)(2,1)}, bf16[128,2048]{1,0:T(8,128)(2,1)}) conditional(s32[]{:T(128)} %bitcast.2, () %tuple.164, (bf16[128,2048]{1,0:T(8,128)(2,1)}, bf16[128,2048]{1,0:T(8,128)(2,1)}) %tuple.185), branch_computations={%region_19.20_spmd, %region_20.21_spmd} | conditional | bytes 4194400 | solution.py:895
  438.0 16.4 %collective-permute-done.6 = bf16[128,2048]{1,0:T(8,128)(2,1)} collective-permute-done((bf16[128,2048]{1,0:T(8,128)(2,1)}, bf16[128,2048]{1,0:T(8,128)(2,1)}, u32[]{:S(2)}, u32[]{:S(2)}) %collective-permute-start.6) | collective-permute-done | bytes 524320 | tf_op jit(solution)/shard_map/cond/branch_1_fun/ppermute | solution.py:859
  455.0 4.6 add_convert_fusion.13
  466.2 7.0 %tail_stage.1 = (bf16[256,2048]{1,0:T(8,128)(2,1)}, bf16[256,2048]{1,0:T(8,128)(2,1)}, bf16[512,512]{1,0:T(8,128)(2,1)}) custom-call(s32[2]{0:T(128)S(1)} %pad_add_fusion.where_ref, bf16[512,256]{1,0:T(8,128)(2,1)} %get-tuple-element.316.refs_0_, bf16[512,256]{1,0:T(8,128)(2,1)} %copy-done.21, bf16[512,256]{1,0:T(8,128)(2,1)} %get-tuple-element.318.refs_2_, ...), custom_call_target="tpu_custom_call" | custom-call | flops 42949672 | bytes 167772 | tf_op jit(solution)/shard_map/tail_stage/pallas_call | solution.py:841
  473.3 7.7 %kv_shares.1 = (bf16[4,256,512]{2,1,0:T(8,128)(2,1)}, bf16[4,256,512]{2,1,0:T(8,128)(2,1)}) custom-call(s32[2]{0:T(128)S(1)} %pad_add_fusion.where_ref, bf16[512,2048]{1,0:T(8,128)(2,1)} %get-tuple-element.243.refs_0_, bf16[512,512]{1,0:T(8,128)(2,1)} %get-tuple-element.322.refs_1_), custom_call_target="tpu_custom_call" | custom-call | flops 17179869184 | bytes 67108864 | tf_op jit(solution)/shard_map/kv_shares/pallas_call | solution.py:745
  484.1 20.3 %conditional.19 = (bf16[128,2048]{1,0:T(8,128)(2,1)S(1)}, f32[1,2048]{1,0:T(1,128)S(1)}) conditional(s32[]{:T(128)} %bitcast.2, () %tuple.151, (f32[128,2048]{1,0:T(8,128)S(1)}, bf16[256,2048]{1,0:T(8,128)(2,1)}, bf16[256,2048]{1,0:T(8,128)(2,1)}, f32[2048]{0:T(1024)S(1)}, f32[128,2048]{1,0:T(8,128)}) %tuple.278), branch_computations={%region_21.22_spmd, %region_22.26_spmd} | conditional | flops 8648832 | bytes 19952252 | solution.py:895
  490.0 12.3 %collective-permute-done.20 = bf16[128,2048]{1,0:T(8,128)(2,1)S(1)} collective-permute-done((bf16[128,2048]{1,0:T(8,128)(2,1)S(1)}, bf16[128,2048]{1,0:T(8,128)(2,1)S(1)}, u32[]{:S(2)}, u32[]{:S(2)}) %collective-permute-start.20) | collective-permute-done | bytes 524320 | tf_op jit(solution)/shard_map/cond/branch_1_fun/ppermute | solution.py:859
  514.4 5.5 collective-permute-done.44
  522.6 10.5 %collective-permute-done.45 = bf16[2,256,512]{2,1,0:T(8,128)(2,1)S(1)} collective-permute-done((bf16[2,256,512]{2,1,0:T(8,128)(2,1)S(1)}, bf16[2,256,512]{2,1,0:T(8,128)(2,1)S(1)}, u32[]{:S(2)}, u32[]{:S(2)}) %collective-permute-start.45) | collective-permute-done | bytes 524320 | tf_op jit(solution)/shard_map/ppermute | solution.py:859
  533.3 7.3 %collective-permute-start.47 = (bf16[1,256,512]{2,1,0:T(8,128)(2,1)S(1)}, bf16[1,256,512]{2,1,0:T(8,128)(2,1)S(1)}, u32[]{:S(2)}, u32[]{:S(2)}) collective-permute-start(bf16[1,256,512]{2,1,0:T(8,128)(2,1)S(1)} %get-tuple-element.418), channel_id=1, source_target_pairs={{0,16},{16,0},{1,17},{17,1},{2,18},{18,2},{3,19},{19,3},{4,20},{20... | collective-permute-start | bytes 786440 | tf_op jit(solution)/shard_map/ppermute | solution.py:859
  540.5 9.1 %conditional.20 = (bf16[512,2048]{1,0:T(8,128)(2,1)}, bf16[512,2048]{1,0:T(8,128)(2,1)}) conditional(s32[]{:T(128)} %bitcast.2, () %tuple.150, (bf16[256,2048]{1,0:T(8,128)(2,1)}, bf16[256,2048]{1,0:T(8,128)(2,1)}) %tuple.202), branch_computations={%region_26.27_spmd, %region_27.28_spmd} | conditional | bytes 12582968 | solution.py:895
  545.1 4.5 collective-permute-done.21
  563.3 28.0 %conditional.21 = (f32[2,2048]{1,0:T(2,128)S(1)}) conditional(s32[]{:T(128)} %bitcast.2, () %tuple.205, f32[2,2048]{1,0:T(2,128)S(1)} %pad_maximum_fusion.5), branch_computations={%region_29.30_spmd, %region_30.31_spmd} | conditional | flops 20480 | bytes 573648 | solution.py:895
  572.5 14.0 %collective-permute-done.11 = f32[2,2048]{1,0:T(2,128)S(1)} collective-permute-done((f32[2,2048]{1,0:T(2,128)S(1)}, f32[2,2048]{1,0:T(2,128)S(1)}, u32[]{:S(2)}, u32[]{:S(2)}) %collective-permute-start.11) | collective-permute-done | bytes 16416 | tf_op jit(solution)/shard_map/cond/branch_1_fun/ppermute | solution.py:859
  (221 shorter events, 179.9 us)
Async XLA Ops:
  7.2 297.1 %reduce-scatter.4.cloned.1.call-start = ((), (), s32[]{:S(2)}) async-start(), calls=%async_computation.3 | async-start | bytes 5242880 | tf_op jit(solution)/shard_map/reduce_scatter | solution.py:971
  9.2 14.9 %collective-permute-start.26 = (bf16[128,2048]{1,0:T(8,128)(2,1)S(1)}, bf16[128,2048]{1,0:T(8,128)(2,1)S(1)}, u32[]{:S(2)}, u32[]{:S(2)}) collective-permute-start(bf16[128,2048]{1,0:T(8,128)(2,1)S(1)} %get-tuple-element.388), channel_id=1, source_target_pairs={{0,8},{8,0},{1,9},{9,1},{2,10},{10,2},{3,11},{11,3},{4,12},{12,4},... | collective-permute-start | bytes 1572872 | tf_op jit(solution)/shard_map/ppermute | solution.py:859
  24.2 13.2 %collective-permute-start = (bf16[512,512]{1,0:T(8,128)(2,1)S(1)}, bf16[512,512]{1,0:T(8,128)(2,1)}, u32[]{:S(2)}, u32[]{:S(2)}) collective-permute-start(bf16[512,512]{1,0:T(8,128)(2,1)S(1)} %param.1), channel_id=1, source_target_pairs={{0,8},{8,0},{1,9},{9,1},{2,10},{10,2},{3,11},{11,3},{4,12},{12,4},... | collective-permute-start | bytes 1572872 | tf_op jit(solution)/shard_map/cond/branch_1_fun/ppermute | solution.py:859
  25.9 12.6 %collective-permute-start.1 = (bf16[512,512]{1,0:T(8,128)(2,1)S(1)}, bf16[512,512]{1,0:T(8,128)(2,1)}, u32[]{:S(2)}, u32[]{:S(2)}) collective-permute-start(bf16[512,512]{1,0:T(8,128)(2,1)S(1)} %param.1), channel_id=1, source_target_pairs={{0,4},{4,0},{1,5},{5,1},{2,6},{6,2},{3,7},{7,3},{8,12},{12,8},{9,1... | collective-permute-start | bytes 1572872 | tf_op jit(solution)/shard_map/cond/branch_1_fun/ppermute | solution.py:859
  38.5 24.2 %collective-permute-start.27 = (bf16[512,512]{1,0:T(8,128)(2,1)S(1)}, bf16[512,512]{1,0:T(8,128)(2,1)S(1)}, u32[]{:S(2)}, u32[]{:S(2)}) collective-permute-start(bf16[512,512]{1,0:T(8,128)(2,1)S(1)} %get-tuple-element.248.refs_0_), channel_id=1, source_target_pairs={{0,16},{16,0},{1,17},{17,1},{2,18},{18,2},{3,19},{19,3},{4,20},{20... | collective-permute-start | bytes 1572872 | tf_op jit(solution)/shard_map/ppermute | solution.py:859
  41.1 11.4 %collective-permute-start.2 = (bf16[512,512]{1,0:T(8,128)(2,1)S(1)}, bf16[512,512]{1,0:T(8,128)(2,1)}, u32[]{:S(2)}, u32[]{:S(2)}) collective-permute-start(bf16[512,512]{1,0:T(8,128)(2,1)S(1)} %param.3), channel_id=1, source_target_pairs={{0,4},{4,0},{1,5},{5,1},{2,6},{6,2},{3,7},{7,3},{8,12},{12,8},{9,1... | collective-permute-start | bytes 1572872 | tf_op jit(solution)/shard_map/cond/branch_1_fun/ppermute | solution.py:859
  62.7 13.3 %collective-permute-start.3 = (bf16[512,512]{1,0:T(8,128)(2,1)S(1)}, bf16[512,512]{1,0:T(8,128)(2,1)}, u32[]{:S(2)}, u32[]{:S(2)}) collective-permute-start(bf16[512,512]{1,0:T(8,128)(2,1)S(1)} %get-tuple-element.78), channel_id=1, source_target_pairs={{0,8},{8,0},{1,9},{9,1},{2,10},{10,2},{3,11},{11,3},{4,12},{12,4},... | collective-permute-start | bytes 1572872 | tf_op jit(solution)/shard_map/cond/branch_1_fun/ppermute | solution.py:859
  63.0 13.7 %collective-permute-start.4 = (bf16[512,512]{1,0:T(8,128)(2,1)S(1)}, bf16[512,512]{1,0:T(8,128)(2,1)}, u32[]{:S(2)}, u32[]{:S(2)}) collective-permute-start(bf16[512,512]{1,0:T(8,128)(2,1)S(1)} %get-tuple-element.78), channel_id=1, source_target_pairs={{0,4},{4,0},{1,5},{5,1},{2,6},{6,2},{3,7},{7,3},{8,12},{12,8},{9,1... | collective-permute-start | bytes 1572872 | tf_op jit(solution)/shard_map/cond/branch_1_fun/ppermute | solution.py:859
  64.4 13.4 %collective-permute-start.5 = (bf16[128,2048]{1,0:T(8,128)(2,1)S(1)}, bf16[128,2048]{1,0:T(8,128)(2,1)}, u32[]{:S(2)}, u32[]{:S(2)}) collective-permute-start(bf16[128,2048]{1,0:T(8,128)(2,1)S(1)} %get-tuple-element.79), channel_id=1, source_target_pairs={{0,2},{2,0},{1,3},{3,1},{4,6},{6,4},{5,7},{7,5},{8,10},{10,8},{9,1... | collective-permute-start | bytes 1572872 | tf_op jit(solution)/shard_map/cond/branch_1_fun/ppermute | solution.py:859
  80.9 14.7 %collective-permute-start.24 = (bf16[512,512]{1,0:T(8,128)(2,1)}, bf16[512,512]{1,0:T(8,128)(2,1)}, u32[]{:S(2)}, u32[]{:S(2)}) collective-permute-start(bf16[512,512]{1,0:T(8,128)(2,1)} %get-tuple-element.80), channel_id=1, source_target_pairs={{0,4},{4,0},{1,5},{5,1},{2,6},{6,2},{3,7},{7,3},{8,12},{12,8},{9,1... | collective-permute-start | bytes 1572872 | tf_op jit(solution)/shard_map/cond/branch_1_fun/ppermute | solution.py:859
  127.3 14.2 %collective-permute-start.29 = (bf16[128,2048]{1,0:T(8,128)(2,1)}, bf16[128,2048]{1,0:T(8,128)(2,1)S(1)}, u32[]{:S(2)}, u32[]{:S(2)}) collective-permute-start(bf16[128,2048]{1,0:T(8,128)(2,1)} %slice.223), channel_id=1, source_target_pairs={{0,2},{2,0},{1,3},{3,1},{4,6},{6,4},{5,7},{7,5},{8,10},{10,8},{9,1... | collective-permute-start | bytes 1572872 | tf_op jit(solution)/shard_map/ppermute | solution.py:859
  143.7 13.1 %collective-permute-start.30 = (bf16[128,2048]{1,0:T(8,128)(2,1)S(1)}, bf16[128,2048]{1,0:T(8,128)(2,1)S(1)}, u32[]{:S(2)}, u32[]{:S(2)}) collective-permute-start(bf16[128,2048]{1,0:T(8,128)(2,1)S(1)} %get-tuple-element.385), channel_id=1, source_target_pairs={{0,8},{8,0},{1,9},{9,1},{2,10},{10,2},{3,11},{11,3},{4,12},{12,4},... | collective-permute-start | bytes 1572872 | tf_op jit(solution)/shard_map/ppermute | solution.py:859
  143.7 14.7 %collective-permute-start.31 = (bf16[128,2048]{1,0:T(8,128)(2,1)S(1)}, bf16[128,2048]{1,0:T(8,128)(2,1)S(1)}, u32[]{:S(2)}, u32[]{:S(2)}) collective-permute-start(bf16[128,2048]{1,0:T(8,128)(2,1)S(1)} %get-tuple-element.385), channel_id=1, source_target_pairs={{0,2},{2,0},{1,3},{3,1},{4,6},{6,4},{5,7},{7,5},{8,10},{10,8},{9,1... | collective-permute-start | bytes 1572872 | tf_op jit(solution)/shard_map/ppermute | solution.py:859
  156.8 12.2 %collective-permute-start.32 = (bf16[128,2048]{1,0:T(8,128)(2,1)S(1)}, bf16[128,2048]{1,0:T(8,128)(2,1)S(1)}, u32[]{:S(2)}, u32[]{:S(2)}) collective-permute-start(bf16[128,2048]{1,0:T(8,128)(2,1)S(1)} %collective-permute-done.30), channel_id=1, source_target_pairs={{0,2},{2,0},{1,3},{3,1},{4,6},{6,4},{5,7},{7,5},{8,10},{10,8},{9,1... | collective-permute-start | bytes 1572872 | tf_op jit(solution)/shard_map/ppermute | solution.py:859
  169.3 4.2 collective-permute-start.33
  201.4 227.8 %reduce-scatter.6.cloned.1.call-start = ((), (), s32[]{:S(2)}) async-start(), calls=%async_computation.4 | async-start | bytes 5242880 | tf_op jit(solution)/shard_map/reduce_scatter | solution.py:971
  210.6 9.1 %collective-permute-start.13 = (bf16[512,2048]{1,0:T(8,128)(2,1)}, bf16[512,2048]{1,0:T(8,128)(2,1)}, u32[]{:S(2)}, u32[]{:S(2)}) collective-permute-start(bf16[512,2048]{1,0:T(8,128)(2,1)} %get-tuple-element.87), channel_id=1, source_target_pairs={{0,1},{1,0},{2,3},{3,2},{4,5},{5,4},{6,7},{7,6},{8,9},{9,8},{10,11... | collective-permute-start | bytes 6291464 | tf_op jit(solution)/shard_map/cond/branch_1_fun/ppermute | solution.py:859
  223.0 15.1 %collective-permute-start.14 = (bf16[128,2048]{1,0:T(8,128)(2,1)}, bf16[128,2048]{1,0:T(8,128)(2,1)}, u32[]{:S(2)}, u32[]{:S(2)}) collective-permute-start(bf16[128,2048]{1,0:T(8,128)(2,1)} %get-tuple-element.393), channel_id=1, source_target_pairs={{0,2},{2,0},{1,3},{3,1},{4,6},{6,4},{5,7},{7,5},{8,10},{10,8},{9,1... | collective-permute-start | bytes 1572872 | tf_op jit(solution)/shard_map/cond/branch_1_fun/ppermute | solution.py:859
  224.6 25.7 %collective-permute-start.15 = (bf16[128,2048]{1,0:T(8,128)(2,1)S(1)}, bf16[128,2048]{1,0:T(8,128)(2,1)S(1)}, u32[]{:S(2)}, u32[]{:S(2)}) collective-permute-start(bf16[128,2048]{1,0:T(8,128)(2,1)S(1)} %get-tuple-element.391), channel_id=1, source_target_pairs={{0,2},{2,0},{1,3},{3,1},{4,6},{6,4},{5,7},{7,5},{8,10},{10,8},{9,1... | collective-permute-start | bytes 1572872 | tf_op jit(solution)/shard_map/cond/branch_1_fun/ppermute | solution.py:859
  240.6 26.5 %collective-permute-start.16 = (bf16[128,2048]{1,0:T(8,128)(2,1)}, bf16[128,2048]{1,0:T(8,128)(2,1)}, u32[]{:S(2)}, u32[]{:S(2)}) collective-permute-start(bf16[128,2048]{1,0:T(8,128)(2,1)} %add_convert_fusion.2), channel_id=1, source_target_pairs={{0,8},{8,0},{1,9},{9,1},{2,10},{10,2},{3,11},{11,3},{4,12},{12,4},... | collective-permute-start | bytes 1572872 | tf_op jit(solution)/shard_map/cond/branch_1_fun/ppermute | solution.py:859
  269.4 289.1 %reduce-scatter.8.cloned.1.call-start = ((), (), s32[]{:S(2)}) async-start(), calls=%async_computation.5 | async-start | bytes 5242880 | tf_op jit(solution)/shard_map/reduce_scatter | solution.py:971
  274.7 11.6 %collective-permute-start.22 = (bf16[128,2048]{1,0:T(8,128)(2,1)S(1)}, bf16[128,2048]{1,0:T(8,128)(2,1)S(1)}, u32[]{:S(2)}, u32[]{:S(2)}) collective-permute-start(bf16[128,2048]{1,0:T(8,128)(2,1)S(1)} %get-tuple-element.382), channel_id=1, source_target_pairs={{0,2},{2,0},{1,3},{3,1},{4,6},{6,4},{5,7},{7,5},{8,10},{10,8},{9,1... | collective-permute-start | bytes 1572872 | tf_op jit(solution)/shard_map/cond/branch_1_fun/ppermute | solution.py:859
  304.2 41.1 %collective-permute-start.34 = (bf16[2048,256]{1,0:T(8,128)(2,1)}, bf16[2048,256]{1,0:T(8,128)(2,1)}, u32[]{:S(2)}, u32[]{:S(2)}) collective-permute-start(bf16[2048,256]{1,0:T(8,128)(2,1)} %get-tuple-element.281), channel_id=1, source_target_pairs={{0,4},{4,0},{1,5},{5,1},{2,6},{6,2},{3,7},{7,3},{8,12},{12,8},{9,1... | collective-permute-start | bytes 3145736 | tf_op jit(solution)/shard_map/ppermute | solution.py:859
  321.5 57.2 %collective-permute-start.35 = (bf16[2048,256]{1,0:T(8,128)(2,1)}, bf16[2048,256]{1,0:T(8,128)(2,1)S(1)}, u32[]{:S(2)}, u32[]{:S(2)}) collective-permute-start(bf16[2048,256]{1,0:T(8,128)(2,1)} %get-tuple-element.285), channel_id=1, source_target_pairs={{0,4},{4,0},{1,5},{5,1},{2,6},{6,2},{3,7},{7,3},{8,12},{12,8},{9,1... | collective-permute-start | bytes 3145736 | tf_op jit(solution)/shard_map/ppermute | solution.py:859
  322.7 60.7 %collective-permute-start.36 = (bf16[256,1024]{1,0:T(8,128)(2,1)}, bf16[256,1024]{1,0:T(8,128)(2,1)}, u32[]{:S(2)}, u32[]{:S(2)}) collective-permute-start(bf16[256,1024]{1,0:T(8,128)(2,1)} %get-tuple-element.430), channel_id=1, source_target_pairs={{0,8},{8,0},{1,9},{9,1},{2,10},{10,2},{3,11},{11,3},{4,12},{12,4},... | collective-permute-start | bytes 1572872 | tf_op jit(solution)/shard_map/ppermute | solution.py:859
  384.8 70.2 %collective-permute-start.39 = (bf16[4,256,1024]{2,1,0:T(8,128)(2,1)}, bf16[4,256,1024]{2,1,0:T(8,128)(2,1)}, u32[]{:S(2)}, u32[]{:S(2)}) collective-permute-start(bf16[4,256,1024]{2,1,0:T(8,128)(2,1)} %get-tuple-element.308), channel_id=1, source_target_pairs={{0,4},{4,0},{1,5},{5,1},{2,6},{6,2},{3,7},{7,3},{8,12},{12,8},{9,1... | collective-permute-start | bytes 6291464 | tf_op jit(solution)/shard_map/ppermute | solution.py:859
  385.1 24.9 %collective-permute-start.38 = (bf16[1024,256]{1,0:T(8,128)(2,1)}, bf16[1024,256]{1,0:T(8,128)(2,1)}, u32[]{:S(2)}, u32[]{:S(2)}) collective-permute-start(bf16[1024,256]{1,0:T(8,128)(2,1)} %get-tuple-element.297), channel_id=1, source_target_pairs={{0,8},{8,0},{1,9},{9,1},{2,10},{10,2},{3,11},{11,3},{4,12},{12,4},... | collective-permute-start | bytes 1572872 | tf_op jit(solution)/shard_map/ppermute | solution.py:859
  386.9 38.2 %collective-permute-start.37 = (bf16[1024,256]{1,0:T(8,128)(2,1)}, bf16[1024,256]{1,0:T(8,128)(2,1)}, u32[]{:S(2)}, u32[]{:S(2)}) collective-permute-start(bf16[1024,256]{1,0:T(8,128)(2,1)} %get-tuple-element.294), channel_id=1, source_target_pairs={{0,8},{8,0},{1,9},{9,1},{2,10},{10,2},{3,11},{11,3},{4,12},{12,4},... | collective-permute-start | bytes 1572872 | tf_op jit(solution)/shard_map/ppermute | solution.py:859
  387.5 4.4 collective-permute-start.17
  393.1 14.0 %collective-permute-start.18 = (bf16[128,2048]{1,0:T(8,128)(2,1)S(1)}, bf16[128,2048]{1,0:T(8,128)(2,1)S(1)}, u32[]{:S(2)}, u32[]{:S(2)}) collective-permute-start(bf16[128,2048]{1,0:T(8,128)(2,1)S(1)} %add_convert_fusion.6), channel_id=1, source_target_pairs={{0,2},{2,0},{1,3},{3,1},{4,6},{6,4},{5,7},{7,5},{8,10},{10,8},{9,1... | collective-permute-start | bytes 1572872 | tf_op jit(solution)/shard_map/cond/branch_1_fun/ppermute | solution.py:859
  431.3 31.2 %collective-permute-start.41 = (bf16[512,256]{1,0:T(8,128)(2,1)}, bf16[512,256]{1,0:T(8,128)(2,1)S(1)}, u32[]{:S(2)}, u32[]{:S(2)}) collective-permute-start(bf16[512,256]{1,0:T(8,128)(2,1)} %get-tuple-element.424), channel_id=1, source_target_pairs={{0,16},{16,0},{1,17},{17,1},{2,18},{18,2},{3,19},{19,3},{4,20},{20... | collective-permute-start | bytes 786440 | tf_op jit(solution)/shard_map/ppermute | solution.py:859
  433.4 32.0 %collective-permute-start.40 = (bf16[512,256]{1,0:T(8,128)(2,1)}, bf16[512,256]{1,0:T(8,128)(2,1)S(1)}, u32[]{:S(2)}, u32[]{:S(2)}) collective-permute-start(bf16[512,256]{1,0:T(8,128)(2,1)} %get-tuple-element.426), channel_id=1, source_target_pairs={{0,16},{16,0},{1,17},{17,1},{2,18},{18,2},{3,19},{19,3},{4,20},{20... | collective-permute-start | bytes 786440 | tf_op jit(solution)/shard_map/ppermute | solution.py:859
  434.2 20.2 %collective-permute-start.6 = (bf16[128,2048]{1,0:T(8,128)(2,1)}, bf16[128,2048]{1,0:T(8,128)(2,1)}, u32[]{:S(2)}, u32[]{:S(2)}) collective-permute-start(bf16[128,2048]{1,0:T(8,128)(2,1)} %get-tuple-element.111), channel_id=1, source_target_pairs={{0,8},{8,0},{1,9},{9,1},{2,10},{10,2},{3,11},{11,3},{4,12},{12,4},... | collective-permute-start | bytes 1572872 | tf_op jit(solution)/shard_map/cond/branch_1_fun/ppermute | solution.py:859
  436.7 17.6 %collective-permute-start.7 = (bf16[128,2048]{1,0:T(8,128)(2,1)}, bf16[128,2048]{1,0:T(8,128)(2,1)}, u32[]{:S(2)}, u32[]{:S(2)}) collective-permute-start(bf16[128,2048]{1,0:T(8,128)(2,1)} %get-tuple-element.112), channel_id=1, source_target_pairs={{0,2},{2,0},{1,3},{3,1},{4,6},{6,4},{5,7},{7,5},{8,10},{10,8},{9,1... | collective-permute-start | bytes 1572872 | tf_op jit(solution)/shard_map/cond/branch_1_fun/ppermute | solution.py:859
  473.2 36.7 %collective-permute-start.42 = (bf16[2,256,1024]{2,1,0:T(8,128)(2,1)}, bf16[2,256,1024]{2,1,0:T(8,128)(2,1)}, u32[]{:S(2)}, u32[]{:S(2)}) collective-permute-start(bf16[2,256,1024]{2,1,0:T(8,128)(2,1)} %get-tuple-element.397), channel_id=1, source_target_pairs={{0,8},{8,0},{1,9},{9,1},{2,10},{10,2},{3,11},{11,3},{4,12},{12,4},... | collective-permute-start | bytes 3145736 | tf_op jit(solution)/shard_map/ppermute | solution.py:859
  481.0 31.8 %collective-permute-start.43 = (bf16[4,256,512]{2,1,0:T(8,128)(2,1)}, bf16[4,256,512]{2,1,0:T(8,128)(2,1)}, u32[]{:S(2)}, u32[]{:S(2)}) collective-permute-start(bf16[4,256,512]{2,1,0:T(8,128)(2,1)} %get-tuple-element.332), channel_id=1, source_target_pairs={{0,4},{4,0},{1,5},{5,1},{2,6},{6,2},{3,7},{7,3},{8,12},{12,8},{9,1... | collective-permute-start | bytes 3145736 | tf_op jit(solution)/shard_map/ppermute | solution.py:859
  482.1 37.8 %collective-permute-start.44 = (bf16[256,1024]{1,0:T(8,128)(2,1)}, bf16[256,1024]{1,0:T(8,128)(2,1)}, u32[]{:S(2)}, u32[]{:S(2)}) collective-permute-start(bf16[256,1024]{1,0:T(8,128)(2,1)} %get-tuple-element.335), channel_id=1, source_target_pairs={{0,8},{8,0},{1,9},{9,1},{2,10},{10,2},{3,11},{11,3},{4,12},{12,4},... | collective-permute-start | bytes 1572872 | tf_op jit(solution)/shard_map/ppermute | solution.py:859
  488.3 14.0 %collective-permute-start.20 = (bf16[128,2048]{1,0:T(8,128)(2,1)S(1)}, bf16[128,2048]{1,0:T(8,128)(2,1)S(1)}, u32[]{:S(2)}, u32[]{:S(2)}) collective-permute-start(bf16[128,2048]{1,0:T(8,128)(2,1)S(1)} %add_convert_fusion.11), channel_id=1, source_target_pairs={{0,2},{2,0},{1,3},{3,1},{4,6},{6,4},{5,7},{7,5},{8,10},{10,8},{9,1... | collective-permute-start | bytes 1572872 | tf_op jit(solution)/shard_map/cond/branch_1_fun/ppermute | solution.py:859
  506.6 26.6 %collective-permute-start.46 = (bf16[256,2048]{1,0:T(8,128)(2,1)}, bf16[256,2048]{1,0:T(8,128)(2,1)}, u32[]{:S(2)}, u32[]{:S(2)}) collective-permute-start(bf16[256,2048]{1,0:T(8,128)(2,1)} %pad_maximum_fusion.4), channel_id=1, source_target_pairs={{0,2},{2,0},{1,3},{3,1},{4,6},{6,4},{5,7},{7,5},{8,10},{10,8},{9,1... | collective-permute-start | bytes 3145736 | tf_op jit(solution)/shard_map/ppermute | solution.py:859
  519.9 13.2 %collective-permute-start.45 = (bf16[2,256,512]{2,1,0:T(8,128)(2,1)S(1)}, bf16[2,256,512]{2,1,0:T(8,128)(2,1)S(1)}, u32[]{:S(2)}, u32[]{:S(2)}) collective-permute-start(bf16[2,256,512]{2,1,0:T(8,128)(2,1)S(1)} %get-tuple-element.405), channel_id=1, source_target_pairs={{0,8},{8,0},{1,9},{9,1},{2,10},{10,2},{3,11},{11,3},{4,12},{12,4},... | collective-permute-start | bytes 1572872 | tf_op jit(solution)/shard_map/ppermute | solution.py:859
  533.3 20.4 %collective-permute-start.47 = (bf16[1,256,512]{2,1,0:T(8,128)(2,1)S(1)}, bf16[1,256,512]{2,1,0:T(8,128)(2,1)S(1)}, u32[]{:S(2)}, u32[]{:S(2)}) collective-permute-start(bf16[1,256,512]{2,1,0:T(8,128)(2,1)S(1)} %get-tuple-element.418), channel_id=1, source_target_pairs={{0,16},{16,0},{1,17},{17,1},{2,18},{18,2},{3,19},{19,3},{4,20},{20... | collective-permute-start | bytes 786440 | tf_op jit(solution)/shard_map/ppermute | solution.py:859
  545.1 4.5 collective-permute-start.21
  561.4 31.4 %collective-permute-start.48 = (bf16[256,1024]{1,0:T(8,128)(2,1)}, bf16[256,1024]{1,0:T(8,128)(2,1)}, u32[]{:S(2)}, u32[]{:S(2)}) collective-permute-start(bf16[256,1024]{1,0:T(8,128)(2,1)} %get-tuple-element.351), channel_id=1, source_target_pairs={{0,8},{8,0},{1,9},{9,1},{2,10},{10,2},{3,11},{11,3},{4,12},{12,4},... | collective-permute-start | bytes 1572872 | tf_op jit(solution)/shard_map/ppermute | solution.py:859
  563.2 32.3 %collective-permute-start.49 = (bf16[1,256,1024]{2,1,0:T(8,128)(2,1)}, bf16[1,256,1024]{2,1,0:T(8,128)(2,1)}, u32[]{:S(2)}, u32[]{:S(2)}) collective-permute-start(bf16[1,256,1024]{2,1,0:T(8,128)(2,1)} %get-tuple-element.399), channel_id=1, source_target_pairs={{0,16},{16,0},{1,17},{17,1},{2,18},{18,2},{3,19},{19,3},{4,20},{20... | collective-permute-start | bytes 1572872 | tf_op jit(solution)/shard_map/ppermute | solution.py:859
  564.6 3.8 collective-permute-start.9
  568.4 3.8 collective-permute-start.10
  572.2 14.3 %collective-permute-start.11 = (f32[2,2048]{1,0:T(2,128)S(1)}, f32[2,2048]{1,0:T(2,128)S(1)}, u32[]{:S(2)}, u32[]{:S(2)}) collective-permute-start(f32[2,2048]{1,0:T(2,128)S(1)} %add.210), channel_id=1, source_target_pairs={{0,8},{8,0},{1,9},{9,1},{2,10},{10,2},{3,11},{11,3},{4,12},{12,4},... | collective-permute-start | bytes 49160 | tf_op jit(solution)/shard_map/cond/branch_1_fun/ppermute | solution.py:859
  586.5 4.8 collective-permute-start.12
  (32 other events, 300.8 us)
Sparse Core Ops, SparseCore 0:
  201.5 87.6 reduce-scatter.3
  292.5 86.1 reduce-scatter.5
  387.3 108.1 reduce-scatter.7

commit v10 on v9

--- a/solution.py
+++ b/solution.py
@@ -530,7 +530,7 @@
     )(order, cont, where, gain.reshape(1, -1), x, wq, wk, wv, table)
 
 
-FILLERS = ("ffn_out", "gate_shares", "kv_shares", "grad_hidden")
+FILLERS = ("kv_shares", "grad_hidden")
 
 
 def cost(name, flops, bytes_accessed):
@@ -1030,37 +1030,40 @@
     first_input, queries, kv_local, cosine, sine = input_stage(
         layer_input, attn_gain, w_query, key_matrix, value_matrix, block_order, cont_prompt, where
     )
-    parts = {0: kv_local}
-    parts[2], parts[1] = stage(
-        lambda kv: (ctx_flip(kv, 2), ctx_flip(kv, 1)), after(cot_part, kv_local)
-    )
-    high_parts = {0: after(parts[1], kv_local)}
-    for bit in reversed(highs):
-        for mask in list(high_parts):
-            high_parts[mask + bit] = ctx_flip(high_parts[mask], bit)
-    del high_parts[0]
-    parts.update(high_parts)
-    parts[3] = stage(lambda kv: ctx_flip(kv, 1), parts[2])
-    dep = parts[3]
-    for mask in high_parts:
-        parts[mask + 2], parts[mask + 1], more = stage(
-            lambda kv, cot: (ctx_flip(kv, 2), ctx_flip(kv, 1), flip(cot, "y")),
-            after(dep, parts[mask]),
-            cot_part,
+    def first_keys(kv):
+        high = {0: kv}
+        for bit in reversed(highs):
+            for mask in list(high):
+                high[mask + bit] = ctx_flip(high[mask], bit)
+        del high[0]
+        return high, ctx_flip(kv, 2), ctx_flip(kv, 1)
+
+    def second_keys(high, low, cot):
+        return (
+            ctx_flip(low, 1),
+            flip(cot, "y"),
+            {mask: ctx_flip(value, 2) for mask, value in high.items()},
+            {mask: ctx_flip(value, 1) for mask, value in high.items()},
         )
-        dep = parts[mask + 1]
+
+    def third_keys(both, cot):
+        return {mask: ctx_flip(value, 1) for mask, value in both.items()}, flip(cot, "core")
+
+    high, part_l, part_x = stage(first_keys, after(cot_part, kv_local))
+    part_lx, more, high_l, high_x = stage(second_keys, high, part_l, cot_part)
     cot_part = jnp.concatenate([cot_part, more])
-    for mask in high_parts:
-        parts[mask + 3], cot_far = stage(
-            lambda kv, cot: (ctx_flip(kv, 1), flip(cot, "core")), parts[mask + 2], cot_part
-        )
+    high_lx, cot_far = stage(third_keys, high_l, cot_part)
+    parts = {0: kv_local, 1: part_x, 2: part_l, 3: part_lx}
+    for mask in high:
+        parts[mask], parts[mask + 1] = high[mask], high_x[mask]
+        parts[mask + 2], parts[mask + 3] = high_l[mask], high_lx[mask]
     parts = [parts[mask] for mask in range(ctx_count)]
     cot = jnp.concatenate(
         [cot_slots[0], cot_part[:quarter], cot_slots[1], cot_part[quarter:]]
         + [cot_slots[2], cot_far[:quarter], cot_slots[3], cot_far[quarter:]]
     )
     mixed, log_total, keep, send = attention_forward(
-        after(cot, queries), w_out, parts, block_order, cont_prompt, where
+        queries, w_out, parts, block_order, cont_prompt, where
     )
     first_half = flip(send, "core")
     near = add(keep, first_half)
@@ -1198,10 +1201,13 @@
     for mask in highs:
         branch.halve(mask, ctx, dep)
         dep = branch.keep
+    sum_gate = join_halves(gate_own, after(dep, gate_other), ctx)
+    dep = sum_gate
     last.halve(2, ctx, dep)
     dep = last.keep
-    sum_gate = join_halves(gate_own, after(dep, gate_other), ctx)
-    dep = sum_gate
+    up_own, up_away = split_halves(up, ctx, dep)
+    dep = up_own
+    up_other = ctx_flip(after(dep, up_away), 2)
     for mask in highs:
         last.halve(mask, ctx, dep)
         dep = last.keep
@@ -1217,9 +1223,6 @@
         for k in range(2)
     ]
     dep = (grad_rows, output_rows)
-    up_own, up_away = split_halves(up, ctx, dep)
-    dep = up_own
-    up_other = ctx_flip(after(dep, up_away), 2)
     gains = stage(gain_stage, after(dep, jnp.stack([attn_gain_part, ffn_gain_part])))
     dep = gains
     sum_up = join_halves(up_own, after(dep, up_other), ctx)

time: 612 us -> 622 us (1.016)
  waiting for transfers between devices: 268 us -> 279 us
  local copies, waits for them, and re-layouts: 48.1 us -> 38.7 us
  other arithmetic: 55.2 us -> 63.7 us
    ppermute x50, waiting for transfers between devices: 268 us -> 279 us  [flip(): lax.ppermute(value, axis, [(i, i ^ mask) for i in range(lax.axis_size(axi...]
    unnamed x62 -> x54, local copies, waits for them, and re-layouts: 20.9 us -> 14.5 us
  transfers between devices with their start and end apart: 53 -> 53, of which waited for: 37 -> 34; matrix products, arithmetic and copies ran while one was open for 13% -> 15% of each run, Pallas kernels for 19% -> 19%
where the time goes in v10:
time: 622 us; the launch traced here: 615 us
  waiting for transfers between devices  279 us (45%)
  Pallas kernels  159 us (26%)
  other arithmetic  63.7 us (10%)
  starting transfers between devices  57.8 us (9%)
  local copies, waits for them, and re-layouts  38.7 us (6%)
  between operations  15.3 us (2%)
    ppermute x50, waiting for transfers between devices, flip(): lax.ppermute(value, axis, [(i, i ^ mask) for i in range(lax.axis_size(axi...  279 us
    ppermute x50, starting transfers between devices, flip(): lax.ppermute(value, axis, [(i, i ^ mask) for i in range(lax.axis_size(axi...  57.7 us
    pallas_call x3, Pallas kernels, unit_shares(): pl.pallas_call(unit_shares_kernel, out_shape=shares, grid_spec=pltpu.Pref...  31.5 us
    convert_element_type x13, other arithmetic, add(): (left.astype(jnp.float32) + right.astype(jnp.float32)).astype(jnp.bfloat16)  31.3 us
    pallas_call x2, Pallas kernels, attention_backward(): pl.pallas_call(functools.partial(backward_kernel, rep, 1, ctx_count, head...  26.6 us
    pallas_call x2, Pallas kernels, grad_second_half(): pl.pallas_call(grad_second_kernel, out_shape=jax.ShapeDtypeStruct((rows,...  18.4 us
    pallas_call x1, Pallas kernels, attention_forward(): pl.pallas_call(functools.partial(forward_kernel, rep, kv_heads, ctx_count...  17.7 us
    pallas_call x2, Pallas kernels, weight_shares(): pl.pallas_call(functools.partial(shares_kernel, len(lefts), swap_bits, pa...  16.9 us
  transfers between devices with their start and end apart: 53, of which 34 were waited for; matrix products, arithmetic and copies ran while one was open for 15% of the time, Pallas kernels for 19%

profile of v10, /device:TPU:0, one launch (start us, length us, event | category | flops | bytes accessed | tf_op | source)
XLA Modules:
  0.0 614.7 jit_solution(16474210335125335449)
XLA Ops:
  13.0 7.2 %input_stage.1 = (bf16[512,2048]{1,0:T(8,128)(2,1)}, bf16[512,512]{1,0:T(8,128)(2,1)}, bf16[512,512]{1,0:T(8,128)(2,1)S(1)}, f32[512,128]{1,0:T(8,128)}, f32[512,128]{1,0:T(8,128)}) custom-call(s32[32]{0:T(128)} %order_ref.7, s32[8]{0:T(128)} %cont_ref.7, s32[2]{0:T(128)S(1)} %pad_add_fusion.where_ref, f32[1,2048]{1,0:T(1,128)} %bitcast.31, ...), custom_call_target="tpu_custom_call" | custom-call | flops 42949672 | bytes 167772 | tf_op jit(solution)/shard_map/input_stage/pallas_call | solution.py:512
  20.1 4.0 collective-permute-done.27
  24.1 25.6 %conditional.10 = (bf16[512,512]{1,0:T(8,128)(2,1)}, bf16[512,512]{1,0:T(8,128)(2,1)}, bf16[512,512]{1,0:T(8,128)(2,1)}) conditional(s32[]{:T(128)} %bitcast.2, () %tuple.139, bf16[512,512]{1,0:T(8,128)(2,1)S(1)} %get-tuple-element.242.refs_0_), branch_computations={%region_0.0_spmd, %region_1.0_spmd} | conditional | bytes 6291600 | solution.py:895
  30.0 19.6 %collective-permute-done = bf16[512,512]{1,0:T(8,128)(2,1)} collective-permute-done((bf16[512,512]{1,0:T(8,128)(2,1)S(1)}, bf16[512,512]{1,0:T(8,128)(2,1)}, u32[]{:S(2)}, u32[]{:S(2)}) %collective-permute-start) | collective-permute-done | bytes 524320 | tf_op jit(solution)/shard_map/cond/branch_1_fun/ppermute | solution.py:859
  49.8 25.2 %conditional.11 = (bf16[512,512]{1,0:T(8,128)(2,1)}, bf16[128,2048]{1,0:T(8,128)(2,1)}, bf16[512,512]{1,0:T(8,128)(2,1)}, bf16[512,512]{1,0:T(8,128)(2,1)}) conditional(s32[]{:T(128)} %bitcast.2, () %tuple.141, (bf16[512,512]{1,0:T(8,128)(2,1)}, bf16[128,2048]{1,0:T(8,128)(2,1)S(1)}, bf16[512,512]{1,0:T(8,128)(2,1)}) %tuple.142), branch_computations={%region_2.0_spmd, %region_3.0_spmd} | conditional | bytes 8388800 | solution.py:895
  54.6 8.2 %collective-permute-done.5 = bf16[512,512]{1,0:T(8,128)(2,1)} collective-permute-done((bf16[512,512]{1,0:T(8,128)(2,1)}, bf16[512,512]{1,0:T(8,128)(2,1)}, u32[]{:S(2)}, u32[]{:S(2)}) %collective-permute-start.5) | collective-permute-done | bytes 524320 | tf_op jit(solution)/shard_map/cond/branch_1_fun/ppermute | solution.py:859
  66.3 8.8 %collective-permute-done.3 = bf16[512,512]{1,0:T(8,128)(2,1)} collective-permute-done((bf16[512,512]{1,0:T(8,128)(2,1)}, bf16[512,512]{1,0:T(8,128)(2,1)}, u32[]{:S(2)}, u32[]{:S(2)}) %collective-permute-start.3) | collective-permute-done | bytes 524320 | tf_op jit(solution)/shard_map/cond/branch_1_fun/ppermute | solution.py:859
  76.2 14.9 %conditional.12 = (bf16[512,512]{1,0:T(8,128)(2,1)}, bf16[256,2048]{1,0:T(8,128)(2,1)}, bf16[128,2048]{1,0:T(8,128)(2,1)S(1)}, bf16[128,2048]{1,0:T(8,128)(2,1)S(1)}) conditional(s32[]{:T(128)} %bitcast.2, () %tuple.143, (bf16[512,512]{1,0:T(8,128)(2,1)}, bf16[256,2048]{1,0:T(8,128)(2,1)S(1)}) %tuple.144), branch_computations={%region_4.0_spmd, %region_5.0_spmd} | conditional | bytes 8388720 | solution.py:895
  80.3 10.6 %collective-permute-done.25 = bf16[512,512]{1,0:T(8,128)(2,1)} collective-permute-done((bf16[512,512]{1,0:T(8,128)(2,1)}, bf16[512,512]{1,0:T(8,128)(2,1)}, u32[]{:S(2)}, u32[]{:S(2)}) %collective-permute-start.25) | collective-permute-done | bytes 524320 | tf_op jit(solution)/shard_map/cond/branch_1_fun/ppermute | solution.py:859
  91.1 17.7 %attention_forward.1 = (bf16[512,512]{1,0:T(8,128)(2,1)}, f32[2,4,256]{2,1,0:T(4,128)}, bf16[256,2048]{1,0:T(8,128)(2,1)}, bf16[256,2048]{1,0:T(8,128)(2,1)}) custom-call(s32[32]{0:T(128)} %order_ref.7, s32[8]{0:T(128)} %cont_ref.7, s32[2]{0:T(128)S(1)} %pad_add_fusion.where_ref, bf16[512,512]{1,0:T(8,128)(2,1)} %get-tuple-element.240.q_ref, ...), custom_call_target="tpu_custom_call" | custom-call | flops 64424508 | bytes 167772 | tf_op jit(solution)/shard_map/attention_forward/pallas_call | solution.py:367
  119.0 9.7 %grad_hidden.1.gh_ref = f32[1024,1024]{1,0:T(8,128)} custom-call(s32[2]{0:T(128)S(1)} %pad_add_fusion.where_ref, bf16[1024,2048]{1,0:T(8,128)(2,1)} %constant_dynamic-update-slice_fusion.2.cot_ref.left_ref, bf16[2048,2048]{1,0:T(8,128)(2,1)} %wd_ref.1), custom_call_target="tpu_custom_call" | custom-call | flops 68719476736 | bytes 134217728 | tf_op jit(solution)/shard_map/grad_hidden/pallas_call | solution.py:570
  137.9 11.6 %collective-permute-done.30 = bf16[128,2048]{1,0:T(8,128)(2,1)S(1)} collective-permute-done((bf16[128,2048]{1,0:T(8,128)(2,1)S(1)}, bf16[128,2048]{1,0:T(8,128)(2,1)S(1)}, u32[]{:S(2)}, u32[]{:S(2)}) %collective-permute-start.30) | collective-permute-done | bytes 524320 | tf_op jit(solution)/shard_map/ppermute | solution.py:859
  151.0 11.1 %collective-permute-done.32 = bf16[128,2048]{1,0:T(8,128)(2,1)S(1)} collective-permute-done((bf16[128,2048]{1,0:T(8,128)(2,1)S(1)}, bf16[128,2048]{1,0:T(8,128)(2,1)S(1)}, u32[]{:S(2)}, u32[]{:S(2)}) %collective-permute-start.32) | collective-permute-done | bytes 524320 | tf_op jit(solution)/shard_map/ppermute | solution.py:859
  168.1 15.6 %ffn_stage.1 = (bf16[1024,1024]{1,0:T(8,128)(2,1)}, bf16[1024,1024]{1,0:T(8,128)(2,1)}, bf16[1024,1024]{1,0:T(8,128)(2,1)S(1)}) custom-call(s32[2]{0:T(128)S(1)} %pad_add_fusion.where_ref, bf16[1024,2048]{1,0:T(8,128)(2,1)} %constant_dynamic-update-slice_fusion.7.in_ref, f32[1024,1024]{1,0:T(8,128)} %grad_hidden.1.gh_ref, bf16[2048,2048]{1,0:T(8,128)(2,1)} %wg_ref.3, ...), custom_call_target="tpu_custom_call" | custom-call | flops 171798688 | bytes 251658 | tf_op jit(solution)/shard_map/ffn_stage/pallas_call | solution.py:609
  183.8 10.7 %down_shares.1 = bf16[8,256,1024]{2,1,0:T(8,128)(2,1)} custom-call(s32[2]{0:T(128)S(1)} %pad_add_fusion.where_ref, bf16[1024,2048]{1,0:T(8,128)(2,1)} %constant_dynamic-update-slice_fusion.2.cot_ref.left_ref, bf16[1024,1024]{1,0:T(8,128)(2,1)} %get-tuple-element.257.right_ref), custom_call_target="tpu_custom_call" | custom-call | flops 85899344 | bytes 167772 | tf_op jit(solution)/shard_map/down_shares/pallas_call | solution.py:789
  194.6 9.0 %grad_second_send.1 = bf16[512,2048]{1,0:T(8,128)(2,1)} custom-call(s32[2]{0:T(128)S(1)} %pad_add_fusion.where_ref, bf16[1024,1024]{1,0:T(8,128)(2,1)} %get-tuple-element.260.gg_ref, bf16[1024,1024]{1,0:T(8,128)(2,1)S(1)} %get-tuple-element.261.gu_ref, bf16[2048,2048]{1,0:T(8,128)(2,1)} %wg_ref.3, bf16[2048,2048]{1,0:T(8,128)(2,1)} %wu_ref.3), custom_call_target="tpu_custom_call" | custom-call | flops 85899344 | bytes 83886 | tf_op jit(solution)/shard_map/grad_second_send/pallas_call | solution.py:641
  203.5 58.8 %conditional.13 = (f32[128,2048]{1,0:T(8,128)}, bf16[8,256,1024]{2,1,0:T(8,128)(2,1)}, bf16[512,2048]{1,0:T(8,128)(2,1)}, bf16[512,2048]{1,0:T(8,128)(2,1)}) conditional(s32[]{:T(128)} %bitcast.2, () %tuple.150, (s32[2]{0:T(128)S(1)}, bf16[1024,1024]{1,0:T(8,128)(2,1)}, bf16[1024,1024]{1,0:T(8,128)(2,1)S(1)}, bf16[2048,2048]{1,0:T(8,128)(2,1)}, ...), branch_computations={%region_7.0_spmd, %region_8.0_spmd} | conditional | flops 264251632 | bytes 24536870 | solution.py:895
  203.9 9.4 %grad_second_keep.1 = bf16[512,2048]{1,0:T(8,128)(2,1)} custom-call(s32[2]{0:T(128)S(1)} %get-tuple-element.80.where_ref, bf16[1024,1024]{1,0:T(8,128)(2,1)} %get-tuple-element.87.gg_ref.right_ref, bf16[1024,1024]{1,0:T(8,128)(2,1)S(1)} %get-tuple-element.82.gu_ref, bf16[2048,2048]{1,0:T(8,128)(2,1)} %get-tuple-element.83.wg_ref, ...), custom_call_target="tpu_custom_call" | custom-call | flops 85899344 | bytes 83886 | tf_op jit(solution)/shard_map/cond/branch_1_fun/grad_second_keep/pallas_call | solution.py:641
  218.8 10.8 %gate_shares.1 = bf16[8,256,1024]{2,1,0:T(8,128)(2,1)} custom-call(s32[2]{0:T(128)S(1)} %get-tuple-element.80.where_ref, bf16[1024,2048]{1,0:T(8,128)(2,1)} %get-tuple-element.86.left_ref, bf16[1024,1024]{1,0:T(8,128)(2,1)} %get-tuple-element.87.gg_ref.right_ref), custom_call_target="tpu_custom_call" | custom-call | flops 85899344 | bytes 167772 | tf_op jit(solution)/shard_map/cond/branch_1_fun/gate_shares/pallas_call | solution.py:789
  234.9 8.6 %ffn_out.1 = (bf16[512,2048]{1,0:T(8,128)(2,1)}, bf16[512,2048]{1,0:T(8,128)(2,1)}) custom-call(s32[2]{0:T(128)S(1)} %get-tuple-element.80.where_ref, bf16[1024,1024]{1,0:T(8,128)(2,1)} %get-tuple-element.90.hid_ref, bf16[2048,2048]{1,0:T(8,128)(2,1)} %get-tuple-element.91.wd_ref), custom_call_target="tpu_custom_call" | custom-call | flops 85899344 | bytes 167772 | tf_op jit(solution)/shard_map/cond/branch_1_fun/ffn_out/pallas_call | solution.py:674
  243.5 16.4 %collective-permute-done.17 = bf16[128,2048]{1,0:T(8,128)(2,1)} collective-permute-done((bf16[128,2048]{1,0:T(8,128)(2,1)}, bf16[128,2048]{1,0:T(8,128)(2,1)}, u32[]{:S(2)}, u32[]{:S(2)}) %collective-permute-start.17) | collective-permute-done | bytes 524320 | tf_op jit(solution)/shard_map/cond/branch_1_fun/ppermute | solution.py:859
  262.4 21.5 %conditional.14 = (f32[128,2048]{1,0:T(8,128)}, bf16[8,256,1024]{2,1,0:T(8,128)(2,1)}, bf16[512,2048]{1,0:T(8,128)(2,1)S(1)}, f32[1,2048]{1,0:T(1,128)S(1)}) conditional(s32[]{:T(128)} %bitcast.2, () %tuple.149, (bf16[128,2048]{1,0:T(8,128)(2,1)}, f32[128]{0:T(128)S(1)}, f32[2048]{0:T(1024)S(1)}, f32[128,2048]{1,0:T(8,128)}, f32[128,2048]{1,0:T(8,128)}, ...), branch_computations={%region_9.0_spmd, %region_10.13_spmd} | conditional | flops 97431632 | bytes 25360900 | solution.py:895
  267.5 10.0 %up_shares.1 = bf16[8,256,1024]{2,1,0:T(8,128)(2,1)} custom-call(s32[2]{0:T(128)S(1)} %get-tuple-element.102.where_ref, bf16[1024,2048]{1,0:T(8,128)(2,1)} %get-tuple-element.103.left_ref, bf16[1024,1024]{1,0:T(8,128)(2,1)S(1)} %get-tuple-element.105.right_ref), custom_call_target="tpu_custom_call" | custom-call | flops 85899344 | bytes 167772 | tf_op jit(solution)/shard_map/cond/branch_1_fun/up_shares/pallas_call | solution.py:789
  284.0 13.4 %attention_backward_0.1 = (bf16[512,256]{1,0:T(8,128)(2,1)}, bf16[2048,256]{1,0:T(8,128)(2,1)}, bf16[2048,256]{1,0:T(8,128)(2,1)}) custom-call(s32[32]{0:T(128)} %order_ref.7, s32[8]{0:T(128)} %cont_ref.7, s32[2]{0:T(128)S(1)} %pad_add_fusion.where_ref, bf16[512,512]{1,0:T(8,128)(2,1)} %get-tuple-element.240.q_ref, ...), custom_call_target="tpu_custom_call" | custom-call | flops 64424508 | bytes 125829 | tf_op jit(solution)/shard_map/attention_backward_0/pallas_call | solution.py:403
  297.4 5.5 collective-permute-start.34
  305.3 13.3 %attention_backward_1.1 = (bf16[512,256]{1,0:T(8,128)(2,1)}, bf16[2048,256]{1,0:T(8,128)(2,1)}, bf16[2048,256]{1,0:T(8,128)(2,1)}) custom-call(s32[32]{0:T(128)} %order_ref.7, s32[8]{0:T(128)} %cont_ref.7, s32[2]{0:T(128)S(1)} %pad_add_fusion.where_ref, bf16[512,512]{1,0:T(8,128)(2,1)} %get-tuple-element.240.q_ref, ...), custom_call_target="tpu_custom_call" | custom-call | flops 64424508 | bytes 125829 | tf_op jit(solution)/shard_map/attention_backward_1/pallas_call | solution.py:403
  320.6 9.2 %branch_shares.1 = (bf16[4,256,1024]{2,1,0:T(8,128)(2,1)}, bf16[4,256,1024]{2,1,0:T(8,128)(2,1)}) custom-call(s32[2]{0:T(128)S(1)} %pad_add_fusion.where_ref, bf16[512,2048]{1,0:T(8,128)(2,1)} %get-tuple-element.239.refs_0_, bf16[512,2048]{1,0:T(8,128)(2,1)S(1)} %get-tuple-element.270.gb_ref.refs_1_, bf16[512,256]{1,0:T(8,128)(2,1)} %get-tuple-element.268.refs_2_.refs_6_, ...), custom_call_target="tpu_custom_call" | custom-call | flops 42949672 | bytes 83886 | tf_op jit(solution)/shard_map/branch_shares/pallas_call | solution.py:745
  329.8 12.0 %collective-permute-done.34 = bf16[2048,256]{1,0:T(8,128)(2,1)} collective-permute-done((bf16[2048,256]{1,0:T(8,128)(2,1)}, bf16[2048,256]{1,0:T(8,128)(2,1)}, u32[]{:S(2)}, u32[]{:S(2)}) %collective-permute-start.34) | collective-permute-done | bytes 1048608 | tf_op jit(solution)/shard_map/ppermute | solution.py:859
  341.7 33.5 %collective-permute-done.35 = bf16[2048,256]{1,0:T(8,128)(2,1)} collective-permute-done((bf16[2048,256]{1,0:T(8,128)(2,1)}, bf16[2048,256]{1,0:T(8,128)(2,1)}, u32[]{:S(2)}, u32[]{:S(2)}) %collective-permute-start.35) | collective-permute-done | bytes 1048608 | tf_op jit(solution)/shard_map/ppermute | solution.py:859
  375.2 3.9 add_convert_fusion.21
  383.0 22.8 %conditional.15 = (bf16[128,2048]{1,0:T(8,128)(2,1)}, bf16[128,2048]{1,0:T(8,128)(2,1)}, bf16[128,2048]{1,0:T(8,128)(2,1)}) conditional(s32[]{:T(128)} %bitcast.2, () %tuple.148, (bf16[512,2048]{1,0:T(8,128)(2,1)}, bf16[512,2048]{1,0:T(8,128)(2,1)}) %tuple.161), branch_computations={%region_14.15_spmd, %region_15.0_spmd} | conditional | flops 5242880 | bytes 17301608 | solution.py:895
  383.3 4.4 collective-permute-done.18
  390.6 12.3 %collective-permute-done.19 = bf16[128,2048]{1,0:T(8,128)(2,1)S(1)} collective-permute-done((bf16[128,2048]{1,0:T(8,128)(2,1)S(1)}, bf16[128,2048]{1,0:T(8,128)(2,1)S(1)}, u32[]{:S(2)}, u32[]{:S(2)}) %collective-permute-start.19) | collective-permute-done | bytes 524320 | tf_op jit(solution)/shard_map/cond/branch_1_fun/ppermute | solution.py:859
  406.3 21.2 %collective-permute-done.37 = bf16[1024,256]{1,0:T(8,128)(2,1)} collective-permute-done((bf16[1024,256]{1,0:T(8,128)(2,1)}, bf16[1024,256]{1,0:T(8,128)(2,1)}, u32[]{:S(2)}, u32[]{:S(2)}) %collective-permute-start.37) | collective-permute-done | bytes 524320 | tf_op jit(solution)/shard_map/ppermute | solution.py:859
  436.9 31.4 %conditional.16 = (bf16[128,2048]{1,0:T(8,128)(2,1)}, bf16[128,2048]{1,0:T(8,128)(2,1)}) conditional(s32[]{:T(128)} %bitcast.2, () %tuple.147, (bf16[128,2048]{1,0:T(8,128)(2,1)}, bf16[128,2048]{1,0:T(8,128)(2,1)}) %tuple.168), branch_computations={%region_17.18_spmd, %region_18.19_spmd} | conditional | bytes 4194400 | solution.py:895
  440.8 27.5 %collective-permute-done.7 = bf16[128,2048]{1,0:T(8,128)(2,1)} collective-permute-done((bf16[128,2048]{1,0:T(8,128)(2,1)}, bf16[128,2048]{1,0:T(8,128)(2,1)}, u32[]{:S(2)}, u32[]{:S(2)}) %collective-permute-start.7) | collective-permute-done | bytes 524320 | tf_op jit(solution)/shard_map/cond/branch_1_fun/ppermute | solution.py:859
  470.8 4.7 add_convert_fusion.13
  479.1 6.7 %tail_stage.1 = (bf16[256,2048]{1,0:T(8,128)(2,1)}, bf16[256,2048]{1,0:T(8,128)(2,1)}, bf16[512,512]{1,0:T(8,128)(2,1)}) custom-call(s32[2]{0:T(128)S(1)} %pad_add_fusion.where_ref, bf16[512,256]{1,0:T(8,128)(2,1)} %get-tuple-element.310.refs_0_, bf16[512,256]{1,0:T(8,128)(2,1)} %collective-permute-done.40.refs_1_, ...), custom_call_target="tpu_custom_call" | custom-call | flops 42949672 | bytes 167772 | tf_op jit(solution)/shard_map/tail_stage/pallas_call | solution.py:841
  485.9 7.8 %kv_shares.1 = (bf16[4,256,512]{2,1,0:T(8,128)(2,1)}, bf16[4,256,512]{2,1,0:T(8,128)(2,1)}) custom-call(s32[2]{0:T(128)S(1)} %pad_add_fusion.where_ref, bf16[512,2048]{1,0:T(8,128)(2,1)} %get-tuple-element.239.refs_0_, bf16[512,512]{1,0:T(8,128)(2,1)} %get-tuple-element.316.refs_1_), custom_call_target="tpu_custom_call" | custom-call | flops 17179869184 | bytes 67108864 | tf_op jit(solution)/shard_map/kv_shares/pallas_call | solution.py:745
  495.3 20.3 %conditional.17 = (bf16[128,2048]{1,0:T(8,128)(2,1)S(1)}, f32[1,2048]{1,0:T(1,128)S(1)}) conditional(s32[]{:T(128)} %bitcast.2, () %tuple.138, (f32[128,2048]{1,0:T(8,128)S(1)}, bf16[256,2048]{1,0:T(8,128)(2,1)}, bf16[256,2048]{1,0:T(8,128)(2,1)}, f32[2048]{0:T(1024)S(1)}, f32[128,2048]{1,0:T(8,128)}) %tuple.257), branch_computations={%region_19.20_spmd, %region_20.24_spmd} | conditional | flops 8648832 | bytes 19952252 | solution.py:895
  501.0 12.3 %collective-permute-done.21 = bf16[128,2048]{1,0:T(8,128)(2,1)S(1)} collective-permute-done((bf16[128,2048]{1,0:T(8,128)(2,1)S(1)}, bf16[128,2048]{1,0:T(8,128)(2,1)S(1)}, u32[]{:S(2)}, u32[]{:S(2)}) %collective-permute-start.21) | collective-permute-done | bytes 524320 | tf_op jit(solution)/shard_map/cond/branch_1_fun/ppermute | solution.py:859
  535.9 16.7 %collective-permute-done.45 = bf16[2,256,512]{2,1,0:T(8,128)(2,1)} collective-permute-done((bf16[2,256,512]{2,1,0:T(8,128)(2,1)}, bf16[2,256,512]{2,1,0:T(8,128)(2,1)}, u32[]{:S(2)}, u32[]{:S(2)}) %collective-permute-start.45) | collective-permute-done | bytes 524320 | tf_op jit(solution)/shard_map/ppermute | solution.py:859
  555.5 7.9 %conditional.18 = (bf16[512,2048]{1,0:T(8,128)(2,1)}, bf16[512,2048]{1,0:T(8,128)(2,1)}) conditional(s32[]{:T(128)} %bitcast.2, () %tuple.137, (bf16[256,2048]{1,0:T(8,128)(2,1)S(1)}, bf16[256,2048]{1,0:T(8,128)(2,1)}) %tuple.186), branch_computations={%region_25.26_spmd, %region_26.27_spmd} | conditional | bytes 12582968 | solution.py:895
  558.9 4.5 collective-permute-done.22
  567.4 8.5 %collective-permute-done.47 = bf16[1,256,512]{2,1,0:T(8,128)(2,1)} collective-permute-done((bf16[1,256,512]{2,1,0:T(8,128)(2,1)}, bf16[1,256,512]{2,1,0:T(8,128)(2,1)}, u32[]{:S(2)}, u32[]{:S(2)}) %collective-permute-start.47) | collective-permute-done | bytes 262176 | tf_op jit(solution)/shard_map/ppermute | solution.py:859
  580.9 17.5 %conditional.19 = (f32[2,2048]{1,0:T(2,128)S(1)}) conditional(s32[]{:T(128)} %bitcast.2, () %tuple.189, f32[2,2048]{1,0:T(2,128)S(1)} %pad_maximum_fusion.5), branch_computations={%region_27.28_spmd, %region_28.29_spmd} | conditional | flops 20480 | bytes 573648 | solution.py:895
  589.9 3.7 collective-permute-done.12
  593.7 4.6 collective-permute-done.13
  (213 shorter events, 174.0 us)
Async XLA Ops:
  7.2 295.8 %reduce-scatter.4.cloned.1.call-start = ((), (), s32[]{:S(2)}) async-start(), calls=%async_computation.3 | async-start | bytes 5242880 | tf_op jit(solution)/shard_map/reduce_scatter | solution.py:971
  9.2 14.9 %collective-permute-start.27 = (bf16[128,2048]{1,0:T(8,128)(2,1)S(1)}, bf16[128,2048]{1,0:T(8,128)(2,1)S(1)}, u32[]{:S(2)}, u32[]{:S(2)}) collective-permute-start(bf16[128,2048]{1,0:T(8,128)(2,1)S(1)} %get-tuple-element.382), channel_id=1, source_target_pairs={{0,8},{8,0},{1,9},{9,1},{2,10},{10,2},{3,11},{11,3},{4,12},{12,4},... | collective-permute-start | bytes 1572872 | tf_op jit(solution)/shard_map/ppermute | solution.py:859
  24.2 25.5 %collective-permute-start = (bf16[512,512]{1,0:T(8,128)(2,1)S(1)}, bf16[512,512]{1,0:T(8,128)(2,1)}, u32[]{:S(2)}, u32[]{:S(2)}) collective-permute-start(bf16[512,512]{1,0:T(8,128)(2,1)S(1)} %param.1), channel_id=1, source_target_pairs={{0,16},{16,0},{1,17},{17,1},{2,18},{18,2},{3,19},{19,3},{4,20},{20... | collective-permute-start | bytes 1572872 | tf_op jit(solution)/shard_map/cond/branch_1_fun/ppermute | solution.py:859
  26.9 22.9 %collective-permute-start.1 = (bf16[512,512]{1,0:T(8,128)(2,1)S(1)}, bf16[512,512]{1,0:T(8,128)(2,1)}, u32[]{:S(2)}, u32[]{:S(2)}) collective-permute-start(bf16[512,512]{1,0:T(8,128)(2,1)S(1)} %param.1), channel_id=1, source_target_pairs={{0,8},{8,0},{1,9},{9,1},{2,10},{10,2},{3,11},{11,3},{4,12},{12,4},... | collective-permute-start | bytes 1572872 | tf_op jit(solution)/shard_map/cond/branch_1_fun/ppermute | solution.py:859
  28.5 21.3 %collective-permute-start.2 = (bf16[512,512]{1,0:T(8,128)(2,1)S(1)}, bf16[512,512]{1,0:T(8,128)(2,1)}, u32[]{:S(2)}, u32[]{:S(2)}) collective-permute-start(bf16[512,512]{1,0:T(8,128)(2,1)S(1)} %param.1), channel_id=1, source_target_pairs={{0,4},{4,0},{1,5},{5,1},{2,6},{6,2},{3,7},{7,3},{8,12},{12,8},{9,1... | collective-permute-start | bytes 1572872 | tf_op jit(solution)/shard_map/cond/branch_1_fun/ppermute | solution.py:859
  49.8 13.0 %collective-permute-start.5 = (bf16[512,512]{1,0:T(8,128)(2,1)}, bf16[512,512]{1,0:T(8,128)(2,1)}, u32[]{:S(2)}, u32[]{:S(2)}) collective-permute-start(bf16[512,512]{1,0:T(8,128)(2,1)} %get-tuple-element.77), channel_id=1, source_target_pairs={{0,8},{8,0},{1,9},{9,1},{2,10},{10,2},{3,11},{11,3},{4,12},{12,4},... | collective-permute-start | bytes 1572872 | tf_op jit(solution)/shard_map/cond/branch_1_fun/ppermute | solution.py:859
  51.1 15.2 %collective-permute-start.6 = (bf16[512,512]{1,0:T(8,128)(2,1)}, bf16[512,512]{1,0:T(8,128)(2,1)}, u32[]{:S(2)}, u32[]{:S(2)}) collective-permute-start(bf16[512,512]{1,0:T(8,128)(2,1)} %get-tuple-element.77), channel_id=1, source_target_pairs={{0,4},{4,0},{1,5},{5,1},{2,6},{6,2},{3,7},{7,3},{8,12},{12,8},{9,1... | collective-permute-start | bytes 1572872 | tf_op jit(solution)/shard_map/cond/branch_1_fun/ppermute | solution.py:859
  52.6 22.5 %collective-permute-start.3 = (bf16[512,512]{1,0:T(8,128)(2,1)}, bf16[512,512]{1,0:T(8,128)(2,1)}, u32[]{:S(2)}, u32[]{:S(2)}) collective-permute-start(bf16[512,512]{1,0:T(8,128)(2,1)} %get-tuple-element.75), channel_id=1, source_target_pairs={{0,4},{4,0},{1,5},{5,1},{2,6},{6,2},{3,7},{7,3},{8,12},{12,8},{9,1... | collective-permute-start | bytes 1572872 | tf_op jit(solution)/shard_map/cond/branch_1_fun/ppermute | solution.py:859
  53.1 21.9 %collective-permute-start.4 = (bf16[128,2048]{1,0:T(8,128)(2,1)S(1)}, bf16[128,2048]{1,0:T(8,128)(2,1)}, u32[]{:S(2)}, u32[]{:S(2)}) collective-permute-start(bf16[128,2048]{1,0:T(8,128)(2,1)S(1)} %get-tuple-element.76), channel_id=1, source_target_pairs={{0,2},{2,0},{1,3},{3,1},{4,6},{6,4},{5,7},{7,5},{8,10},{10,8},{9,1... | collective-permute-start | bytes 1572872 | tf_op jit(solution)/shard_map/cond/branch_1_fun/ppermute | solution.py:859
  76.3 14.7 %collective-permute-start.25 = (bf16[512,512]{1,0:T(8,128)(2,1)}, bf16[512,512]{1,0:T(8,128)(2,1)}, u32[]{:S(2)}, u32[]{:S(2)}) collective-permute-start(bf16[512,512]{1,0:T(8,128)(2,1)} %get-tuple-element.78), channel_id=1, source_target_pairs={{0,4},{4,0},{1,5},{5,1},{2,6},{6,2},{3,7},{7,3},{8,12},{12,8},{9,1... | collective-permute-start | bytes 1572872 | tf_op jit(solution)/shard_map/cond/branch_1_fun/ppermute | solution.py:859
  108.9 8.1 %collective-permute-start.28 = (bf16[256,2048]{1,0:T(8,128)(2,1)}, bf16[256,2048]{1,0:T(8,128)(2,1)S(1)}, u32[]{:S(2)}, u32[]{:S(2)}) collective-permute-start(bf16[256,2048]{1,0:T(8,128)(2,1)} %get-tuple-element.252), channel_id=1, source_target_pairs={{0,1},{1,0},{2,3},{3,2},{4,5},{5,4},{6,7},{7,6},{8,9},{9,8},{10,11... | collective-permute-start | bytes 3145736 | tf_op jit(solution)/shard_map/ppermute | solution.py:859
  117.4 14.4 %collective-permute-start.29 = (bf16[128,2048]{1,0:T(8,128)(2,1)S(1)}, bf16[128,2048]{1,0:T(8,128)(2,1)S(1)}, u32[]{:S(2)}, u32[]{:S(2)}) collective-permute-start(bf16[128,2048]{1,0:T(8,128)(2,1)S(1)} %slice.223), channel_id=1, source_target_pairs={{0,2},{2,0},{1,3},{3,1},{4,6},{6,4},{5,7},{7,5},{8,10},{10,8},{9,1... | collective-permute-start | bytes 1572872 | tf_op jit(solution)/shard_map/ppermute | solution.py:859
  136.0 13.5 %collective-permute-start.30 = (bf16[128,2048]{1,0:T(8,128)(2,1)S(1)}, bf16[128,2048]{1,0:T(8,128)(2,1)S(1)}, u32[]{:S(2)}, u32[]{:S(2)}) collective-permute-start(bf16[128,2048]{1,0:T(8,128)(2,1)S(1)} %get-tuple-element.379), channel_id=1, source_target_pairs={{0,8},{8,0},{1,9},{9,1},{2,10},{10,2},{3,11},{11,3},{4,12},{12,4},... | collective-permute-start | bytes 1572872 | tf_op jit(solution)/shard_map/ppermute | solution.py:859
  136.7 14.3 %collective-permute-start.31 = (bf16[128,2048]{1,0:T(8,128)(2,1)S(1)}, bf16[128,2048]{1,0:T(8,128)(2,1)S(1)}, u32[]{:S(2)}, u32[]{:S(2)}) collective-permute-start(bf16[128,2048]{1,0:T(8,128)(2,1)S(1)} %get-tuple-element.379), channel_id=1, source_target_pairs={{0,2},{2,0},{1,3},{3,1},{4,6},{6,4},{5,7},{7,5},{8,10},{10,8},{9,1... | collective-permute-start | bytes 1572872 | tf_op jit(solution)/shard_map/ppermute | solution.py:859
  149.5 12.7 %collective-permute-start.32 = (bf16[128,2048]{1,0:T(8,128)(2,1)S(1)}, bf16[128,2048]{1,0:T(8,128)(2,1)S(1)}, u32[]{:S(2)}, u32[]{:S(2)}) collective-permute-start(bf16[128,2048]{1,0:T(8,128)(2,1)S(1)} %collective-permute-done.30), channel_id=1, source_target_pairs={{0,2},{2,0},{1,3},{3,1},{4,6},{6,4},{5,7},{7,5},{8,10},{10,8},{9,1... | collective-permute-start | bytes 1572872 | tf_op jit(solution)/shard_map/ppermute | solution.py:859
  162.4 4.2 collective-permute-start.33
  194.5 237.2 %reduce-scatter.6.cloned.1.call-start = ((), (), s32[]{:S(2)}) async-start(), calls=%async_computation.4 | async-start | bytes 5242880 | tf_op jit(solution)/shard_map/reduce_scatter | solution.py:971
  203.7 9.6 %collective-permute-start.14 = (bf16[512,2048]{1,0:T(8,128)(2,1)}, bf16[512,2048]{1,0:T(8,128)(2,1)}, u32[]{:S(2)}, u32[]{:S(2)}) collective-permute-start(bf16[512,2048]{1,0:T(8,128)(2,1)} %get-tuple-element.85), channel_id=1, source_target_pairs={{0,1},{1,0},{2,3},{3,2},{4,5},{5,4},{6,7},{7,6},{8,9},{9,8},{10,11... | collective-permute-start | bytes 6291464 | tf_op jit(solution)/shard_map/cond/branch_1_fun/ppermute | solution.py:859
  216.8 15.1 %collective-permute-start.15 = (bf16[128,2048]{1,0:T(8,128)(2,1)}, bf16[128,2048]{1,0:T(8,128)(2,1)}, u32[]{:S(2)}, u32[]{:S(2)}) collective-permute-start(bf16[128,2048]{1,0:T(8,128)(2,1)} %get-tuple-element.387), channel_id=1, source_target_pairs={{0,2},{2,0},{1,3},{3,1},{4,6},{6,4},{5,7},{7,5},{8,10},{10,8},{9,1... | collective-permute-start | bytes 1572872 | tf_op jit(solution)/shard_map/cond/branch_1_fun/ppermute | solution.py:859
  218.5 25.0 %collective-permute-start.16 = (bf16[128,2048]{1,0:T(8,128)(2,1)}, bf16[128,2048]{1,0:T(8,128)(2,1)}, u32[]{:S(2)}, u32[]{:S(2)}) collective-permute-start(bf16[128,2048]{1,0:T(8,128)(2,1)} %get-tuple-element.385), channel_id=1, source_target_pairs={{0,2},{2,0},{1,3},{3,1},{4,6},{6,4},{5,7},{7,5},{8,10},{10,8},{9,1... | collective-permute-start | bytes 1572872 | tf_op jit(solution)/shard_map/cond/branch_1_fun/ppermute | solution.py:859
  234.4 25.5 %collective-permute-start.17 = (bf16[128,2048]{1,0:T(8,128)(2,1)}, bf16[128,2048]{1,0:T(8,128)(2,1)}, u32[]{:S(2)}, u32[]{:S(2)}) collective-permute-start(bf16[128,2048]{1,0:T(8,128)(2,1)} %add_convert_fusion.2), channel_id=1, source_target_pairs={{0,8},{8,0},{1,9},{9,1},{2,10},{10,2},{3,11},{11,3},{4,12},{12,4},... | collective-permute-start | bytes 1572872 | tf_op jit(solution)/shard_map/cond/branch_1_fun/ppermute | solution.py:859
  262.4 267.6 %reduce-scatter.8.cloned.1.call-start = ((), (), s32[]{:S(2)}) async-start(), calls=%async_computation.5 | async-start | bytes 5242880 | tf_op jit(solution)/shard_map/reduce_scatter | solution.py:971
  267.0 12.0 %collective-permute-start.23 = (bf16[128,2048]{1,0:T(8,128)(2,1)S(1)}, bf16[128,2048]{1,0:T(8,128)(2,1)}, u32[]{:S(2)}, u32[]{:S(2)}) collective-permute-start(bf16[128,2048]{1,0:T(8,128)(2,1)S(1)} %get-tuple-element.376), channel_id=1, source_target_pairs={{0,2},{2,0},{1,3},{3,1},{4,6},{6,4},{5,7},{7,5},{8,10},{10,8},{9,1... | collective-permute-start | bytes 1572872 | tf_op jit(solution)/shard_map/cond/branch_1_fun/ppermute | solution.py:859
  297.4 44.3 %collective-permute-start.34 = (bf16[2048,256]{1,0:T(8,128)(2,1)}, bf16[2048,256]{1,0:T(8,128)(2,1)}, u32[]{:S(2)}, u32[]{:S(2)}) collective-permute-start(bf16[2048,256]{1,0:T(8,128)(2,1)} %get-tuple-element.275), channel_id=1, source_target_pairs={{0,4},{4,0},{1,5},{5,1},{2,6},{6,2},{3,7},{7,3},{8,12},{12,8},{9,1... | collective-permute-start | bytes 3145736 | tf_op jit(solution)/shard_map/ppermute | solution.py:859
  318.6 56.7 %collective-permute-start.35 = (bf16[2048,256]{1,0:T(8,128)(2,1)}, bf16[2048,256]{1,0:T(8,128)(2,1)}, u32[]{:S(2)}, u32[]{:S(2)}) collective-permute-start(bf16[2048,256]{1,0:T(8,128)(2,1)} %get-tuple-element.279), channel_id=1, source_target_pairs={{0,4},{4,0},{1,5},{5,1},{2,6},{6,2},{3,7},{7,3},{8,12},{12,8},{9,1... | collective-permute-start | bytes 3145736 | tf_op jit(solution)/shard_map/ppermute | solution.py:859
  320.6 58.5 %collective-permute-start.36 = (bf16[256,1024]{1,0:T(8,128)(2,1)}, bf16[256,1024]{1,0:T(8,128)(2,1)}, u32[]{:S(2)}, u32[]{:S(2)}) collective-permute-start(bf16[256,1024]{1,0:T(8,128)(2,1)} %get-tuple-element.424), channel_id=1, source_target_pairs={{0,8},{8,0},{1,9},{9,1},{2,10},{10,2},{3,11},{11,3},{4,12},{12,4},... | collective-permute-start | bytes 1572872 | tf_op jit(solution)/shard_map/ppermute | solution.py:859
  380.5 90.3 %collective-permute-start.39 = (bf16[4,256,1024]{2,1,0:T(8,128)(2,1)}, bf16[4,256,1024]{2,1,0:T(8,128)(2,1)}, u32[]{:S(2)}, u32[]{:S(2)}) collective-permute-start(bf16[4,256,1024]{2,1,0:T(8,128)(2,1)} %get-tuple-element.302), channel_id=1, source_target_pairs={{0,4},{4,0},{1,5},{5,1},{2,6},{6,2},{3,7},{7,3},{8,12},{12,8},{9,1... | collective-permute-start | bytes 6291464 | tf_op jit(solution)/shard_map/ppermute | solution.py:859
  381.0 25.4 %collective-permute-start.38 = (bf16[1024,256]{1,0:T(8,128)(2,1)}, bf16[1024,256]{1,0:T(8,128)(2,1)}, u32[]{:S(2)}, u32[]{:S(2)}) collective-permute-start(bf16[1024,256]{1,0:T(8,128)(2,1)} %get-tuple-element.291), channel_id=1, source_target_pairs={{0,8},{8,0},{1,9},{9,1},{2,10},{10,2},{3,11},{11,3},{4,12},{12,4},... | collective-permute-start | bytes 1572872 | tf_op jit(solution)/shard_map/ppermute | solution.py:859
  382.6 44.9 %collective-permute-start.37 = (bf16[1024,256]{1,0:T(8,128)(2,1)}, bf16[1024,256]{1,0:T(8,128)(2,1)}, u32[]{:S(2)}, u32[]{:S(2)}) collective-permute-start(bf16[1024,256]{1,0:T(8,128)(2,1)} %get-tuple-element.288), channel_id=1, source_target_pairs={{0,8},{8,0},{1,9},{9,1},{2,10},{10,2},{3,11},{11,3},{4,12},{12,4},... | collective-permute-start | bytes 1572872 | tf_op jit(solution)/shard_map/ppermute | solution.py:859
  383.2 4.4 collective-permute-start.18
  388.8 14.0 %collective-permute-start.19 = (bf16[128,2048]{1,0:T(8,128)(2,1)S(1)}, bf16[128,2048]{1,0:T(8,128)(2,1)S(1)}, u32[]{:S(2)}, u32[]{:S(2)}) collective-permute-start(bf16[128,2048]{1,0:T(8,128)(2,1)S(1)} %add_convert_fusion.6), channel_id=1, source_target_pairs={{0,2},{2,0},{1,3},{3,1},{4,6},{6,4},{5,7},{7,5},{8,10},{10,8},{9,1... | collective-permute-start | bytes 1572872 | tf_op jit(solution)/shard_map/cond/branch_1_fun/ppermute | solution.py:859
  434.0 44.4 %collective-permute-start.41 = (bf16[512,256]{1,0:T(8,128)(2,1)}, bf16[512,256]{1,0:T(8,128)(2,1)S(1)}, u32[]{:S(2)}, u32[]{:S(2)}) collective-permute-start(bf16[512,256]{1,0:T(8,128)(2,1)} %get-tuple-element.418), channel_id=1, source_target_pairs={{0,16},{16,0},{1,17},{17,1},{2,18},{18,2},{3,19},{19,3},{4,20},{20... | collective-permute-start | bytes 786440 | tf_op jit(solution)/shard_map/ppermute | solution.py:859
  436.5 42.7 %collective-permute-start.40 = (bf16[512,256]{1,0:T(8,128)(2,1)}, bf16[512,256]{1,0:T(8,128)(2,1)}, u32[]{:S(2)}, u32[]{:S(2)}) collective-permute-start(bf16[512,256]{1,0:T(8,128)(2,1)} %get-tuple-element.420), channel_id=1, source_target_pairs={{0,16},{16,0},{1,17},{17,1},{2,18},{18,2},{3,19},{19,3},{4,20},{20... | collective-permute-start | bytes 786440 | tf_op jit(solution)/shard_map/ppermute | solution.py:859
  436.9 31.4 %collective-permute-start.7 = (bf16[128,2048]{1,0:T(8,128)(2,1)}, bf16[128,2048]{1,0:T(8,128)(2,1)}, u32[]{:S(2)}, u32[]{:S(2)}) collective-permute-start(bf16[128,2048]{1,0:T(8,128)(2,1)} %get-tuple-element.109), channel_id=1, source_target_pairs={{0,8},{8,0},{1,9},{9,1},{2,10},{10,2},{3,11},{11,3},{4,12},{12,4},... | collective-permute-start | bytes 1572872 | tf_op jit(solution)/shard_map/cond/branch_1_fun/ppermute | solution.py:859
  439.4 28.9 %collective-permute-start.8 = (bf16[128,2048]{1,0:T(8,128)(2,1)}, bf16[128,2048]{1,0:T(8,128)(2,1)}, u32[]{:S(2)}, u32[]{:S(2)}) collective-permute-start(bf16[128,2048]{1,0:T(8,128)(2,1)} %get-tuple-element.110), channel_id=1, source_target_pairs={{0,2},{2,0},{1,3},{3,1},{4,6},{6,4},{5,7},{7,5},{8,10},{10,8},{9,1... | collective-permute-start | bytes 1572872 | tf_op jit(solution)/shard_map/cond/branch_1_fun/ppermute | solution.py:859
  468.3 52.6 %collective-permute-start.43 = (bf16[256,1024]{1,0:T(8,128)(2,1)}, bf16[256,1024]{1,0:T(8,128)(2,1)}, u32[]{:S(2)}, u32[]{:S(2)}) collective-permute-start(bf16[256,1024]{1,0:T(8,128)(2,1)} %get-tuple-element.324), channel_id=1, source_target_pairs={{0,8},{8,0},{1,9},{9,1},{2,10},{10,2},{3,11},{11,3},{4,12},{12,4},... | collective-permute-start | bytes 1572872 | tf_op jit(solution)/shard_map/ppermute | solution.py:859
  485.9 32.5 %collective-permute-start.42 = (bf16[2,256,1024]{2,1,0:T(8,128)(2,1)}, bf16[2,256,1024]{2,1,0:T(8,128)(2,1)}, u32[]{:S(2)}, u32[]{:S(2)}) collective-permute-start(bf16[2,256,1024]{2,1,0:T(8,128)(2,1)} %get-tuple-element.391), channel_id=1, source_target_pairs={{0,8},{8,0},{1,9},{9,1},{2,10},{10,2},{3,11},{11,3},{4,12},{12,4},... | collective-permute-start | bytes 3145736 | tf_op jit(solution)/shard_map/ppermute | solution.py:859
  493.6 30.0 %collective-permute-start.44 = (bf16[4,256,512]{2,1,0:T(8,128)(2,1)}, bf16[4,256,512]{2,1,0:T(8,128)(2,1)}, u32[]{:S(2)}, u32[]{:S(2)}) collective-permute-start(bf16[4,256,512]{2,1,0:T(8,128)(2,1)} %get-tuple-element.328), channel_id=1, source_target_pairs={{0,4},{4,0},{1,5},{5,1},{2,6},{6,2},{3,7},{7,3},{8,12},{12,8},{9,1... | collective-permute-start | bytes 3145736 | tf_op jit(solution)/shard_map/ppermute | solution.py:859
  499.3 14.0 %collective-permute-start.21 = (bf16[128,2048]{1,0:T(8,128)(2,1)S(1)}, bf16[128,2048]{1,0:T(8,128)(2,1)S(1)}, u32[]{:S(2)}, u32[]{:S(2)}) collective-permute-start(bf16[128,2048]{1,0:T(8,128)(2,1)S(1)} %add_convert_fusion.11), channel_id=1, source_target_pairs={{0,2},{2,0},{1,3},{3,1},{4,6},{6,4},{5,7},{7,5},{8,10},{10,8},{9,1... | collective-permute-start | bytes 1572872 | tf_op jit(solution)/shard_map/cond/branch_1_fun/ppermute | solution.py:859
  516.8 37.6 %collective-permute-start.46 = (bf16[256,2048]{1,0:T(8,128)(2,1)S(1)}, bf16[256,2048]{1,0:T(8,128)(2,1)}, u32[]{:S(2)}, u32[]{:S(2)}) collective-permute-start(bf16[256,2048]{1,0:T(8,128)(2,1)S(1)} %pad_maximum_fusion.4), channel_id=1, source_target_pairs={{0,2},{2,0},{1,3},{3,1},{4,6},{6,4},{5,7},{7,5},{8,10},{10,8},{9,1... | collective-permute-start | bytes 3145736 | tf_op jit(solution)/shard_map/ppermute | solution.py:859
  526.1 26.4 %collective-permute-start.45 = (bf16[2,256,512]{2,1,0:T(8,128)(2,1)}, bf16[2,256,512]{2,1,0:T(8,128)(2,1)}, u32[]{:S(2)}, u32[]{:S(2)}) collective-permute-start(bf16[2,256,512]{2,1,0:T(8,128)(2,1)} %get-tuple-element.399), channel_id=1, source_target_pairs={{0,8},{8,0},{1,9},{9,1},{2,10},{10,2},{3,11},{11,3},{4,12},{12,4},... | collective-permute-start | bytes 1572872 | tf_op jit(solution)/shard_map/ppermute | solution.py:859
  532.3 66.0 %collective-permute-start.48 = (bf16[256,1024]{1,0:T(8,128)(2,1)}, bf16[256,1024]{1,0:T(8,128)(2,1)}, u32[]{:S(2)}, u32[]{:S(2)}) collective-permute-start(bf16[256,1024]{1,0:T(8,128)(2,1)} %get-tuple-element.345), channel_id=1, source_target_pairs={{0,8},{8,0},{1,9},{9,1},{2,10},{10,2},{3,11},{11,3},{4,12},{12,4},... | collective-permute-start | bytes 1572872 | tf_op jit(solution)/shard_map/ppermute | solution.py:859
  532.3 71.8 %collective-permute-start.49 = (bf16[1,256,1024]{2,1,0:T(8,128)(2,1)}, bf16[1,256,1024]{2,1,0:T(8,128)(2,1)}, u32[]{:S(2)}, u32[]{:S(2)}) collective-permute-start(bf16[1,256,1024]{2,1,0:T(8,128)(2,1)} %get-tuple-element.393), channel_id=1, source_target_pairs={{0,16},{16,0},{1,17},{17,1},{2,18},{18,2},{3,19},{19,3},{4,20},{20... | collective-permute-start | bytes 1572872 | tf_op jit(solution)/shard_map/ppermute | solution.py:859
  554.4 21.4 %collective-permute-start.47 = (bf16[1,256,512]{2,1,0:T(8,128)(2,1)}, bf16[1,256,512]{2,1,0:T(8,128)(2,1)}, u32[]{:S(2)}, u32[]{:S(2)}) collective-permute-start(bf16[1,256,512]{2,1,0:T(8,128)(2,1)} %get-tuple-element.412), channel_id=1, source_target_pairs={{0,16},{16,0},{1,17},{17,1},{2,18},{18,2},{3,19},{19,3},{4,20},{20... | collective-permute-start | bytes 786440 | tf_op jit(solution)/shard_map/ppermute | solution.py:859
  558.9 4.5 collective-permute-start.22
  582.2 3.8 collective-permute-start.10
  586.0 3.8 collective-permute-start.11
  593.6 4.7 collective-permute-start.13
  (29 other events, 268.3 us)
Sparse Core Ops, SparseCore 0:
  194.6 90.9 reduce-scatter.3
  288.9 86.1 reduce-scatter.5
  378.1 102.3 reduce-scatter.7

commit v11 on v10

--- a/solution.py
+++ b/solution.py
@@ -530,7 +530,7 @@
     )(order, cont, where, gain.reshape(1, -1), x, wq, wk, wv, table)
 
 
-FILLERS = ("kv_shares", "grad_hidden")
+FILLERS = ("ffn_out", "gate_shares", "kv_shares", "grad_hidden")
 
 
 def cost(name, flops, bytes_accessed):
@@ -1201,10 +1201,10 @@
     for mask in highs:
         branch.halve(mask, ctx, dep)
         dep = branch.keep
+    last.halve(2, ctx, dep)
+    dep = last.keep
     sum_gate = join_halves(gate_own, after(dep, gate_other), ctx)
     dep = sum_gate
-    last.halve(2, ctx, dep)
-    dep = last.keep
     up_own, up_away = split_halves(up, ctx, dep)
     dep = up_own
     up_other = ctx_flip(after(dep, up_away), 2)

time: 622 us -> 613 us (0.986)
  other arithmetic: 63.7 us -> 53.3 us
  waiting for transfers between devices: 279 us -> 288 us
  starting transfers between devices: 57.8 us -> 49.3 us
    ppermute x50, starting transfers between devices: 57.7 us -> 49.2 us  [flip(): lax.ppermute(value, axis, [(i, i ^ mask) for i in range(lax.axis_size(axi...]
    ppermute x50, waiting for transfers between devices: 279 us -> 288 us  [flip(): lax.ppermute(value, axis, [(i, i ^ mask) for i in range(lax.axis_size(axi...]
    unnamed x54 -> x76, local copies, waits for them, and re-layouts: 14.5 us -> 17.3 us
  transfers between devices with their start and end apart: 53 -> 53, of which waited for: 34 -> 34; matrix products, arithmetic and copies ran while one was open for 15% -> 13% of each run, Pallas kernels for 19% -> 19%
where the time goes in v11:
time: 613 us; the launch traced here: 610 us
  waiting for transfers between devices  288 us (47%)
  Pallas kernels  162 us (26%)
  other arithmetic  53.3 us (9%)
  starting transfers between devices  49.3 us (8%)
  local copies, waits for them, and re-layouts  41.8 us (7%)
  between operations  15.4 us (3%)
    ppermute x50, waiting for transfers between devices, flip(): lax.ppermute(value, axis, [(i, i ^ mask) for i in range(lax.axis_size(axi...  288 us
    ppermute x50, starting transfers between devices, flip(): lax.ppermute(value, axis, [(i, i ^ mask) for i in range(lax.axis_size(axi...  49.2 us
    pallas_call x3, Pallas kernels, unit_shares(): pl.pallas_call(unit_shares_kernel, out_shape=shares, grid_spec=pltpu.Pref...  31.4 us
    pallas_call x2, Pallas kernels, attention_backward(): pl.pallas_call(functools.partial(backward_kernel, rep, 1, ctx_count, head...  28.1 us
    convert_element_type x13, other arithmetic, add(): (left.astype(jnp.float32) + right.astype(jnp.float32)).astype(jnp.bfloat16)  27.7 us
    pallas_call x1, Pallas kernels, attention_forward(): pl.pallas_call(functools.partial(forward_kernel, rep, kv_heads, ctx_count...  19.2 us
    pallas_call x2, Pallas kernels, grad_second_half(): pl.pallas_call(grad_second_kernel, out_shape=jax.ShapeDtypeStruct((rows,...  18.5 us
    unnamed x76, local copies, waits for them, and re-layouts  17.3 us
  transfers between devices with their start and end apart: 53, of which 34 were waited for; matrix products, arithmetic and copies ran while one was open for 13% of the time, Pallas kernels for 19%

profile of v11, /device:TPU:0, one launch (start us, length us, event | category | flops | bytes accessed | tf_op | source)
XLA Modules:
  0.0 610.2 jit_solution(17287414020601604048)
XLA Ops:
  13.0 7.2 %input_stage.1 = (bf16[512,2048]{1,0:T(8,128)(2,1)}, bf16[512,512]{1,0:T(8,128)(2,1)}, bf16[512,512]{1,0:T(8,128)(2,1)S(1)}, f32[512,128]{1,0:T(8,128)}, f32[512,128]{1,0:T(8,128)}) custom-call(s32[32]{0:T(128)} %order_ref.7, s32[8]{0:T(128)} %cont_ref.7, s32[2]{0:T(128)S(1)} %pad_add_fusion.where_ref, f32[1,2048]{1,0:T(1,128)} %bitcast.31, ...), custom_call_target="tpu_custom_call" | custom-call | flops 42949672 | bytes 167772 | tf_op jit(solution)/shard_map/input_stage/pallas_call | solution.py:512
  20.2 4.0 collective-permute-done.27
  24.2 25.6 %conditional.10 = (bf16[512,512]{1,0:T(8,128)(2,1)}, bf16[512,512]{1,0:T(8,128)(2,1)}, bf16[512,512]{1,0:T(8,128)(2,1)}) conditional(s32[]{:T(128)} %bitcast.2, () %tuple.139, bf16[512,512]{1,0:T(8,128)(2,1)S(1)} %get-tuple-element.242.refs_0_), branch_computations={%region_0.0_spmd, %region_1.0_spmd} | conditional | bytes 6291600 | solution.py:895
  30.0 19.6 %collective-permute-done = bf16[512,512]{1,0:T(8,128)(2,1)} collective-permute-done((bf16[512,512]{1,0:T(8,128)(2,1)S(1)}, bf16[512,512]{1,0:T(8,128)(2,1)}, u32[]{:S(2)}, u32[]{:S(2)}) %collective-permute-start) | collective-permute-done | bytes 524320 | tf_op jit(solution)/shard_map/cond/branch_1_fun/ppermute | solution.py:859
  49.8 25.2 %conditional.11 = (bf16[512,512]{1,0:T(8,128)(2,1)}, bf16[128,2048]{1,0:T(8,128)(2,1)}, bf16[512,512]{1,0:T(8,128)(2,1)}, bf16[512,512]{1,0:T(8,128)(2,1)}) conditional(s32[]{:T(128)} %bitcast.2, () %tuple.141, (bf16[512,512]{1,0:T(8,128)(2,1)}, bf16[128,2048]{1,0:T(8,128)(2,1)S(1)}, bf16[512,512]{1,0:T(8,128)(2,1)}) %tuple.142), branch_computations={%region_2.0_spmd, %region_3.0_spmd} | conditional | bytes 8388800 | solution.py:895
  54.6 8.2 %collective-permute-done.5 = bf16[512,512]{1,0:T(8,128)(2,1)} collective-permute-done((bf16[512,512]{1,0:T(8,128)(2,1)}, bf16[512,512]{1,0:T(8,128)(2,1)}, u32[]{:S(2)}, u32[]{:S(2)}) %collective-permute-start.5) | collective-permute-done | bytes 524320 | tf_op jit(solution)/shard_map/cond/branch_1_fun/ppermute | solution.py:859
  66.3 8.8 %collective-permute-done.3 = bf16[512,512]{1,0:T(8,128)(2,1)} collective-permute-done((bf16[512,512]{1,0:T(8,128)(2,1)}, bf16[512,512]{1,0:T(8,128)(2,1)}, u32[]{:S(2)}, u32[]{:S(2)}) %collective-permute-start.3) | collective-permute-done | bytes 524320 | tf_op jit(solution)/shard_map/cond/branch_1_fun/ppermute | solution.py:859
  76.2 14.9 %conditional.12 = (bf16[512,512]{1,0:T(8,128)(2,1)}, bf16[256,2048]{1,0:T(8,128)(2,1)}, bf16[128,2048]{1,0:T(8,128)(2,1)S(1)}, bf16[128,2048]{1,0:T(8,128)(2,1)S(1)}) conditional(s32[]{:T(128)} %bitcast.2, () %tuple.143, (bf16[512,512]{1,0:T(8,128)(2,1)}, bf16[256,2048]{1,0:T(8,128)(2,1)S(1)}) %tuple.144), branch_computations={%region_4.0_spmd, %region_5.0_spmd} | conditional | bytes 8388720 | solution.py:895
  80.3 10.6 %collective-permute-done.25 = bf16[512,512]{1,0:T(8,128)(2,1)} collective-permute-done((bf16[512,512]{1,0:T(8,128)(2,1)}, bf16[512,512]{1,0:T(8,128)(2,1)}, u32[]{:S(2)}, u32[]{:S(2)}) %collective-permute-start.25) | collective-permute-done | bytes 524320 | tf_op jit(solution)/shard_map/cond/branch_1_fun/ppermute | solution.py:859
  91.1 19.2 %attention_forward.1 = (bf16[512,512]{1,0:T(8,128)(2,1)}, f32[2,4,256]{2,1,0:T(4,128)}, bf16[256,2048]{1,0:T(8,128)(2,1)}, bf16[256,2048]{1,0:T(8,128)(2,1)}) custom-call(s32[32]{0:T(128)} %order_ref.7, s32[8]{0:T(128)} %cont_ref.7, s32[2]{0:T(128)S(1)} %pad_add_fusion.where_ref, bf16[512,512]{1,0:T(8,128)(2,1)} %get-tuple-element.240.q_ref, ...), custom_call_target="tpu_custom_call" | custom-call | flops 64424508 | bytes 167772 | tf_op jit(solution)/shard_map/attention_forward/pallas_call | solution.py:367
  121.1 9.7 %grad_hidden.1.gh_ref = f32[1024,1024]{1,0:T(8,128)} custom-call(s32[2]{0:T(128)S(1)} %pad_add_fusion.where_ref, bf16[1024,2048]{1,0:T(8,128)(2,1)} %constant_dynamic-update-slice_fusion.2.cot_ref.left_ref, bf16[2048,2048]{1,0:T(8,128)(2,1)} %wd_ref.1), custom_call_target="tpu_custom_call" | custom-call | flops 68719476736 | bytes 134217728 | tf_op jit(solution)/shard_map/grad_hidden/pallas_call | solution.py:570
  137.9 12.0 %collective-permute-done.30 = bf16[128,2048]{1,0:T(8,128)(2,1)S(1)} collective-permute-done((bf16[128,2048]{1,0:T(8,128)(2,1)S(1)}, bf16[128,2048]{1,0:T(8,128)(2,1)S(1)}, u32[]{:S(2)}, u32[]{:S(2)}) %collective-permute-start.30) | collective-permute-done | bytes 524320 | tf_op jit(solution)/shard_map/ppermute | solution.py:859
  151.4 11.1 %collective-permute-done.32 = bf16[128,2048]{1,0:T(8,128)(2,1)S(1)} collective-permute-done((bf16[128,2048]{1,0:T(8,128)(2,1)S(1)}, bf16[128,2048]{1,0:T(8,128)(2,1)S(1)}, u32[]{:S(2)}, u32[]{:S(2)}) %collective-permute-start.32) | collective-permute-done | bytes 524320 | tf_op jit(solution)/shard_map/ppermute | solution.py:859
  168.5 15.6 %ffn_stage.1 = (bf16[1024,1024]{1,0:T(8,128)(2,1)}, bf16[1024,1024]{1,0:T(8,128)(2,1)}, bf16[1024,1024]{1,0:T(8,128)(2,1)S(1)}) custom-call(s32[2]{0:T(128)S(1)} %pad_add_fusion.where_ref, bf16[1024,2048]{1,0:T(8,128)(2,1)} %constant_dynamic-update-slice_fusion.7.in_ref, f32[1024,1024]{1,0:T(8,128)} %grad_hidden.1.gh_ref, bf16[2048,2048]{1,0:T(8,128)(2,1)} %wg_ref.3, ...), custom_call_target="tpu_custom_call" | custom-call | flops 171798688 | bytes 251658 | tf_op jit(solution)/shard_map/ffn_stage/pallas_call | solution.py:609
  184.1 10.7 %down_shares.1 = bf16[8,256,1024]{2,1,0:T(8,128)(2,1)} custom-call(s32[2]{0:T(128)S(1)} %pad_add_fusion.where_ref, bf16[1024,2048]{1,0:T(8,128)(2,1)} %constant_dynamic-update-slice_fusion.2.cot_ref.left_ref, bf16[1024,1024]{1,0:T(8,128)(2,1)} %get-tuple-element.257.right_ref), custom_call_target="tpu_custom_call" | custom-call | flops 85899344 | bytes 167772 | tf_op jit(solution)/shard_map/down_shares/pallas_call | solution.py:789
  194.9 9.0 %grad_second_send.1 = bf16[512,2048]{1,0:T(8,128)(2,1)} custom-call(s32[2]{0:T(128)S(1)} %pad_add_fusion.where_ref, bf16[1024,1024]{1,0:T(8,128)(2,1)} %get-tuple-element.260.gg_ref, bf16[1024,1024]{1,0:T(8,128)(2,1)S(1)} %get-tuple-element.261.gu_ref, bf16[2048,2048]{1,0:T(8,128)(2,1)} %wg_ref.3, bf16[2048,2048]{1,0:T(8,128)(2,1)} %wu_ref.3), custom_call_target="tpu_custom_call" | custom-call | flops 85899344 | bytes 83886 | tf_op jit(solution)/shard_map/grad_second_send/pallas_call | solution.py:641
  203.9 58.8 %conditional.13 = (f32[128,2048]{1,0:T(8,128)}, bf16[8,256,1024]{2,1,0:T(8,128)(2,1)}, bf16[512,2048]{1,0:T(8,128)(2,1)}, bf16[512,2048]{1,0:T(8,128)(2,1)}) conditional(s32[]{:T(128)} %bitcast.2, () %tuple.150, (s32[2]{0:T(128)S(1)}, bf16[1024,1024]{1,0:T(8,128)(2,1)}, bf16[1024,1024]{1,0:T(8,128)(2,1)S(1)}, bf16[2048,2048]{1,0:T(8,128)(2,1)}, ...), branch_computations={%region_7.0_spmd, %region_8.0_spmd} | conditional | flops 137531408384 | bytes 292636768 | solution.py:895
  204.3 9.6 %grad_second_keep.1 = bf16[512,2048]{1,0:T(8,128)(2,1)} custom-call(s32[2]{0:T(128)S(1)} %get-tuple-element.80.where_ref, bf16[1024,1024]{1,0:T(8,128)(2,1)} %get-tuple-element.87.gg_ref.right_ref, bf16[1024,1024]{1,0:T(8,128)(2,1)S(1)} %get-tuple-element.82.gu_ref, bf16[2048,2048]{1,0:T(8,128)(2,1)} %get-tuple-element.83.wg_ref, ...), custom_call_target="tpu_custom_call" | custom-call | flops 85899344 | bytes 83886 | tf_op jit(solution)/shard_map/cond/branch_1_fun/grad_second_keep/pallas_call | solution.py:641
  219.2 10.7 %gate_shares.1 = bf16[8,256,1024]{2,1,0:T(8,128)(2,1)} custom-call(s32[2]{0:T(128)S(1)} %get-tuple-element.80.where_ref, bf16[1024,2048]{1,0:T(8,128)(2,1)} %get-tuple-element.86.left_ref, bf16[1024,1024]{1,0:T(8,128)(2,1)} %get-tuple-element.87.gg_ref.right_ref), custom_call_target="tpu_custom_call" | custom-call | flops 68719476736 | bytes 134217728 | tf_op jit(solution)/shard_map/cond/branch_1_fun/gate_shares/pallas_call | solution.py:789
  234.8 8.8 %ffn_out.1 = (bf16[512,2048]{1,0:T(8,128)(2,1)}, bf16[512,2048]{1,0:T(8,128)(2,1)}) custom-call(s32[2]{0:T(128)S(1)} %get-tuple-element.80.where_ref, bf16[1024,1024]{1,0:T(8,128)(2,1)} %get-tuple-element.90.hid_ref, bf16[2048,2048]{1,0:T(8,128)(2,1)} %get-tuple-element.91.wd_ref), custom_call_target="tpu_custom_call" | custom-call | flops 68719476736 | bytes 134217728 | tf_op jit(solution)/shard_map/cond/branch_1_fun/ffn_out/pallas_call | solution.py:674
  243.6 16.7 %collective-permute-done.17 = bf16[128,2048]{1,0:T(8,128)(2,1)} collective-permute-done((bf16[128,2048]{1,0:T(8,128)(2,1)}, bf16[128,2048]{1,0:T(8,128)(2,1)}, u32[]{:S(2)}, u32[]{:S(2)}) %collective-permute-start.17) | collective-permute-done | bytes 524320 | tf_op jit(solution)/shard_map/cond/branch_1_fun/ppermute | solution.py:859
  263.9 19.6 %conditional.14 = (f32[128,2048]{1,0:T(8,128)}, bf16[8,256,1024]{2,1,0:T(8,128)(2,1)}, bf16[512,2048]{1,0:T(8,128)(2,1)S(1)}, f32[1,2048]{1,0:T(1,128)S(1)}) conditional(s32[]{:T(128)} %bitcast.2, () %tuple.149, (bf16[128,2048]{1,0:T(8,128)(2,1)}, f32[128]{0:T(128)S(1)}, f32[2048]{0:T(1024)S(1)}, f32[128,2048]{1,0:T(8,128)}, ...), branch_computations={%region_9.0_spmd, %region_10.13_spmd} | conditional | flops 97431632 | bytes 21166568 | solution.py:895
  269.0 9.9 %up_shares.1 = bf16[8,256,1024]{2,1,0:T(8,128)(2,1)} custom-call(s32[2]{0:T(128)S(1)} %get-tuple-element.102.where_ref, bf16[1024,2048]{1,0:T(8,128)(2,1)} %get-tuple-element.103.left_ref, bf16[1024,1024]{1,0:T(8,128)(2,1)S(1)} %get-tuple-element.105.right_ref), custom_call_target="tpu_custom_call" | custom-call | flops 85899344 | bytes 167772 | tf_op jit(solution)/shard_map/cond/branch_1_fun/up_shares/pallas_call | solution.py:789
  284.6 14.0 %attention_backward_0.1 = (bf16[512,256]{1,0:T(8,128)(2,1)}, bf16[2048,256]{1,0:T(8,128)(2,1)}, bf16[2048,256]{1,0:T(8,128)(2,1)}) custom-call(s32[32]{0:T(128)} %order_ref.7, s32[8]{0:T(128)} %cont_ref.7, s32[2]{0:T(128)S(1)} %pad_add_fusion.where_ref, bf16[512,512]{1,0:T(8,128)(2,1)} %get-tuple-element.240.q_ref, ...), custom_call_target="tpu_custom_call" | custom-call | flops 64424508 | bytes 125829 | tf_op jit(solution)/shard_map/attention_backward_0/pallas_call | solution.py:403
  301.8 14.1 %attention_backward_1.1 = (bf16[512,256]{1,0:T(8,128)(2,1)}, bf16[2048,256]{1,0:T(8,128)(2,1)}, bf16[2048,256]{1,0:T(8,128)(2,1)}) custom-call(s32[32]{0:T(128)} %order_ref.7, s32[8]{0:T(128)} %cont_ref.7, s32[2]{0:T(128)S(1)} %pad_add_fusion.where_ref, bf16[512,512]{1,0:T(8,128)(2,1)} %get-tuple-element.240.q_ref, ...), custom_call_target="tpu_custom_call" | custom-call | flops 64424508 | bytes 125829 | tf_op jit(solution)/shard_map/attention_backward_1/pallas_call | solution.py:403
  317.3 9.1 %branch_shares.1 = (bf16[4,256,1024]{2,1,0:T(8,128)(2,1)}, bf16[4,256,1024]{2,1,0:T(8,128)(2,1)}) custom-call(s32[2]{0:T(128)S(1)} %pad_add_fusion.where_ref, bf16[512,2048]{1,0:T(8,128)(2,1)} %get-tuple-element.239.refs_0_, bf16[512,2048]{1,0:T(8,128)(2,1)S(1)} %get-tuple-element.270.gb_ref.refs_1_, bf16[512,256]{1,0:T(8,128)(2,1)} %get-tuple-element.268.refs_2_.refs_6_, ...), custom_call_target="tpu_custom_call" | custom-call | flops 42949672 | bytes 83886 | tf_op jit(solution)/shard_map/branch_shares/pallas_call | solution.py:745
  326.4 16.5 %collective-permute-done.34 = bf16[2048,256]{1,0:T(8,128)(2,1)} collective-permute-done((bf16[2048,256]{1,0:T(8,128)(2,1)}, bf16[2048,256]{1,0:T(8,128)(2,1)}, u32[]{:S(2)}, u32[]{:S(2)}) %collective-permute-start.34) | collective-permute-done | bytes 1048608 | tf_op jit(solution)/shard_map/ppermute | solution.py:859
  342.9 33.4 %collective-permute-done.35 = bf16[2048,256]{1,0:T(8,128)(2,1)} collective-permute-done((bf16[2048,256]{1,0:T(8,128)(2,1)}, bf16[2048,256]{1,0:T(8,128)(2,1)}, u32[]{:S(2)}, u32[]{:S(2)}) %collective-permute-start.35) | collective-permute-done | bytes 1048608 | tf_op jit(solution)/shard_map/ppermute | solution.py:859
  382.8 21.9 %conditional.15 = (bf16[128,2048]{1,0:T(8,128)(2,1)S(1)}, bf16[128,2048]{1,0:T(8,128)(2,1)S(1)}, bf16[128,2048]{1,0:T(8,128)(2,1)S(1)}) conditional(s32[]{:T(128)} %bitcast.2, () %tuple.148, (bf16[512,2048]{1,0:T(8,128)(2,1)}, bf16[512,2048]{1,0:T(8,128)(2,1)}) %tuple.161), branch_computations={%region_14.15_spmd, %region_15.0_spmd} | conditional | flops 5242880 | bytes 17301608 | solution.py:895
  383.1 4.4 collective-permute-done.18
  390.4 12.3 %collective-permute-done.19 = bf16[128,2048]{1,0:T(8,128)(2,1)S(1)} collective-permute-done((bf16[128,2048]{1,0:T(8,128)(2,1)S(1)}, bf16[128,2048]{1,0:T(8,128)(2,1)S(1)}, u32[]{:S(2)}, u32[]{:S(2)}) %collective-permute-start.19) | collective-permute-done | bytes 524320 | tf_op jit(solution)/shard_map/cond/branch_1_fun/ppermute | solution.py:859
  405.2 21.0 %collective-permute-done.37 = bf16[1024,256]{1,0:T(8,128)(2,1)} collective-permute-done((bf16[1024,256]{1,0:T(8,128)(2,1)}, bf16[1024,256]{1,0:T(8,128)(2,1)}, u32[]{:S(2)}, u32[]{:S(2)}) %collective-permute-start.37) | collective-permute-done | bytes 524320 | tf_op jit(solution)/shard_map/ppermute | solution.py:859
  435.5 29.0 %conditional.16 = (bf16[128,2048]{1,0:T(8,128)(2,1)}, bf16[128,2048]{1,0:T(8,128)(2,1)}) conditional(s32[]{:T(128)} %bitcast.2, () %tuple.147, (bf16[128,2048]{1,0:T(8,128)(2,1)S(1)}, bf16[128,2048]{1,0:T(8,128)(2,1)S(1)}) %tuple.260), branch_computations={%region_17.18_spmd, %region_18.19_spmd} | conditional | bytes 4194400 | solution.py:895
  439.1 25.3 %collective-permute-done.7 = bf16[128,2048]{1,0:T(8,128)(2,1)} collective-permute-done((bf16[128,2048]{1,0:T(8,128)(2,1)S(1)}, bf16[128,2048]{1,0:T(8,128)(2,1)}, u32[]{:S(2)}, u32[]{:S(2)}) %collective-permute-start.7) | collective-permute-done | bytes 524320 | tf_op jit(solution)/shard_map/cond/branch_1_fun/ppermute | solution.py:859
  464.5 4.7 add_convert_fusion.13
  471.9 5.1 collective-permute-done.40.refs_1_
  477.0 6.7 %tail_stage.1 = (bf16[256,2048]{1,0:T(8,128)(2,1)}, bf16[256,2048]{1,0:T(8,128)(2,1)}, bf16[512,512]{1,0:T(8,128)(2,1)}) custom-call(s32[2]{0:T(128)S(1)} %pad_add_fusion.where_ref, bf16[512,256]{1,0:T(8,128)(2,1)} %get-tuple-element.310.refs_0_, bf16[512,256]{1,0:T(8,128)(2,1)} %collective-permute-done.40.refs_1_, ...), custom_call_target="tpu_custom_call" | custom-call | flops 42949672 | bytes 167772 | tf_op jit(solution)/shard_map/tail_stage/pallas_call | solution.py:841
  483.7 7.7 %kv_shares.1 = (bf16[4,256,512]{2,1,0:T(8,128)(2,1)}, bf16[4,256,512]{2,1,0:T(8,128)(2,1)}) custom-call(s32[2]{0:T(128)S(1)} %pad_add_fusion.where_ref, bf16[512,2048]{1,0:T(8,128)(2,1)} %get-tuple-element.239.refs_0_, bf16[512,512]{1,0:T(8,128)(2,1)} %get-tuple-element.316.refs_1_), custom_call_target="tpu_custom_call" | custom-call | flops 17179869184 | bytes 67108864 | tf_op jit(solution)/shard_map/kv_shares/pallas_call | solution.py:745
  497.1 20.3 %conditional.17 = (bf16[128,2048]{1,0:T(8,128)(2,1)S(1)}, f32[1,2048]{1,0:T(1,128)S(1)}) conditional(s32[]{:T(128)} %bitcast.2, () %tuple.138, (f32[128,2048]{1,0:T(8,128)S(1)}, bf16[256,2048]{1,0:T(8,128)(2,1)}, bf16[256,2048]{1,0:T(8,128)(2,1)}, f32[2048]{0:T(1024)S(1)}, f32[128,2048]{1,0:T(8,128)}) %tuple.261), branch_computations={%region_19.20_spmd, %region_20.24_spmd} | conditional | flops 8648832 | bytes 19952252 | solution.py:895
  502.9 12.3 %collective-permute-done.21 = bf16[128,2048]{1,0:T(8,128)(2,1)S(1)} collective-permute-done((bf16[128,2048]{1,0:T(8,128)(2,1)S(1)}, bf16[128,2048]{1,0:T(8,128)(2,1)S(1)}, u32[]{:S(2)}, u32[]{:S(2)}) %collective-permute-start.21) | collective-permute-done | bytes 524320 | tf_op jit(solution)/shard_map/cond/branch_1_fun/ppermute | solution.py:859
  531.2 18.2 %collective-permute-done.45 = bf16[2,256,512]{2,1,0:T(8,128)(2,1)S(1)} collective-permute-done((bf16[2,256,512]{2,1,0:T(8,128)(2,1)S(1)}, bf16[2,256,512]{2,1,0:T(8,128)(2,1)S(1)}, u32[]{:S(2)}, u32[]{:S(2)}) %collective-permute-start.45) | collective-permute-done | bytes 524320 | tf_op jit(solution)/shard_map/ppermute | solution.py:859
  550.8 7.8 %conditional.18 = (bf16[512,2048]{1,0:T(8,128)(2,1)}, bf16[512,2048]{1,0:T(8,128)(2,1)}) conditional(s32[]{:T(128)} %bitcast.2, () %tuple.137, (bf16[256,2048]{1,0:T(8,128)(2,1)S(1)}, bf16[256,2048]{1,0:T(8,128)(2,1)}) %tuple.186), branch_computations={%region_25.26_spmd, %region_26.27_spmd} | conditional | bytes 12582968 | solution.py:895
  554.2 4.5 collective-permute-done.22
  562.7 8.1 %collective-permute-done.47 = bf16[1,256,512]{2,1,0:T(8,128)(2,1)S(1)} collective-permute-done((bf16[1,256,512]{2,1,0:T(8,128)(2,1)}, bf16[1,256,512]{2,1,0:T(8,128)(2,1)S(1)}, u32[]{:S(2)}, u32[]{:S(2)}) %collective-permute-start.47) | collective-permute-done | bytes 262176 | tf_op jit(solution)/shard_map/ppermute | solution.py:859
  576.4 17.5 %conditional.19 = (f32[2,2048]{1,0:T(2,128)S(1)}) conditional(s32[]{:T(128)} %bitcast.2, () %tuple.189, f32[2,2048]{1,0:T(2,128)S(1)} %pad_maximum_fusion.5), branch_computations={%region_27.28_spmd, %region_28.29_spmd} | conditional | flops 20480 | bytes 573648 | solution.py:895
  581.6 3.7 collective-permute-done.11
  585.4 3.7 collective-permute-done.12
  589.2 4.6 collective-permute-done.13
  (233 shorter events, 163.1 us)
Async XLA Ops:
  7.2 292.5 %reduce-scatter.4.cloned.1.call-start = ((), (), s32[]{:S(2)}) async-start(), calls=%async_computation.3 | async-start | bytes 5242880 | tf_op jit(solution)/shard_map/reduce_scatter | solution.py:971
  9.2 14.9 %collective-permute-start.27 = (bf16[128,2048]{1,0:T(8,128)(2,1)S(1)}, bf16[128,2048]{1,0:T(8,128)(2,1)S(1)}, u32[]{:S(2)}, u32[]{:S(2)}) collective-permute-start(bf16[128,2048]{1,0:T(8,128)(2,1)S(1)} %get-tuple-element.382), channel_id=1, source_target_pairs={{0,8},{8,0},{1,9},{9,1},{2,10},{10,2},{3,11},{11,3},{4,12},{12,4},... | collective-permute-start | bytes 1572872 | tf_op jit(solution)/shard_map/ppermute | solution.py:859
  24.2 25.5 %collective-permute-start = (bf16[512,512]{1,0:T(8,128)(2,1)S(1)}, bf16[512,512]{1,0:T(8,128)(2,1)}, u32[]{:S(2)}, u32[]{:S(2)}) collective-permute-start(bf16[512,512]{1,0:T(8,128)(2,1)S(1)} %param.1), channel_id=1, source_target_pairs={{0,16},{16,0},{1,17},{17,1},{2,18},{18,2},{3,19},{19,3},{4,20},{20... | collective-permute-start | bytes 1572872 | tf_op jit(solution)/shard_map/cond/branch_1_fun/ppermute | solution.py:859
  26.9 22.9 %collective-permute-start.1 = (bf16[512,512]{1,0:T(8,128)(2,1)S(1)}, bf16[512,512]{1,0:T(8,128)(2,1)}, u32[]{:S(2)}, u32[]{:S(2)}) collective-permute-start(bf16[512,512]{1,0:T(8,128)(2,1)S(1)} %param.1), channel_id=1, source_target_pairs={{0,8},{8,0},{1,9},{9,1},{2,10},{10,2},{3,11},{11,3},{4,12},{12,4},... | collective-permute-start | bytes 1572872 | tf_op jit(solution)/shard_map/cond/branch_1_fun/ppermute | solution.py:859
  28.5 21.3 %collective-permute-start.2 = (bf16[512,512]{1,0:T(8,128)(2,1)S(1)}, bf16[512,512]{1,0:T(8,128)(2,1)}, u32[]{:S(2)}, u32[]{:S(2)}) collective-permute-start(bf16[512,512]{1,0:T(8,128)(2,1)S(1)} %param.1), channel_id=1, source_target_pairs={{0,4},{4,0},{1,5},{5,1},{2,6},{6,2},{3,7},{7,3},{8,12},{12,8},{9,1... | collective-permute-start | bytes 1572872 | tf_op jit(solution)/shard_map/cond/branch_1_fun/ppermute | solution.py:859
  49.8 13.0 %collective-permute-start.5 = (bf16[512,512]{1,0:T(8,128)(2,1)}, bf16[512,512]{1,0:T(8,128)(2,1)}, u32[]{:S(2)}, u32[]{:S(2)}) collective-permute-start(bf16[512,512]{1,0:T(8,128)(2,1)} %get-tuple-element.77), channel_id=1, source_target_pairs={{0,8},{8,0},{1,9},{9,1},{2,10},{10,2},{3,11},{11,3},{4,12},{12,4},... | collective-permute-start | bytes 1572872 | tf_op jit(solution)/shard_map/cond/branch_1_fun/ppermute | solution.py:859
  51.1 15.2 %collective-permute-start.6 = (bf16[512,512]{1,0:T(8,128)(2,1)}, bf16[512,512]{1,0:T(8,128)(2,1)}, u32[]{:S(2)}, u32[]{:S(2)}) collective-permute-start(bf16[512,512]{1,0:T(8,128)(2,1)} %get-tuple-element.77), channel_id=1, source_target_pairs={{0,4},{4,0},{1,5},{5,1},{2,6},{6,2},{3,7},{7,3},{8,12},{12,8},{9,1... | collective-permute-start | bytes 1572872 | tf_op jit(solution)/shard_map/cond/branch_1_fun/ppermute | solution.py:859
  52.6 22.5 %collective-permute-start.3 = (bf16[512,512]{1,0:T(8,128)(2,1)}, bf16[512,512]{1,0:T(8,128)(2,1)}, u32[]{:S(2)}, u32[]{:S(2)}) collective-permute-start(bf16[512,512]{1,0:T(8,128)(2,1)} %get-tuple-element.75), channel_id=1, source_target_pairs={{0,4},{4,0},{1,5},{5,1},{2,6},{6,2},{3,7},{7,3},{8,12},{12,8},{9,1... | collective-permute-start | bytes 1572872 | tf_op jit(solution)/shard_map/cond/branch_1_fun/ppermute | solution.py:859
  53.1 21.9 %collective-permute-start.4 = (bf16[128,2048]{1,0:T(8,128)(2,1)S(1)}, bf16[128,2048]{1,0:T(8,128)(2,1)}, u32[]{:S(2)}, u32[]{:S(2)}) collective-permute-start(bf16[128,2048]{1,0:T(8,128)(2,1)S(1)} %get-tuple-element.76), channel_id=1, source_target_pairs={{0,2},{2,0},{1,3},{3,1},{4,6},{6,4},{5,7},{7,5},{8,10},{10,8},{9,1... | collective-permute-start | bytes 1572872 | tf_op jit(solution)/shard_map/cond/branch_1_fun/ppermute | solution.py:859
  76.3 14.7 %collective-permute-start.25 = (bf16[512,512]{1,0:T(8,128)(2,1)}, bf16[512,512]{1,0:T(8,128)(2,1)}, u32[]{:S(2)}, u32[]{:S(2)}) collective-permute-start(bf16[512,512]{1,0:T(8,128)(2,1)} %get-tuple-element.78), channel_id=1, source_target_pairs={{0,4},{4,0},{1,5},{5,1},{2,6},{6,2},{3,7},{7,3},{8,12},{12,8},{9,1... | collective-permute-start | bytes 1572872 | tf_op jit(solution)/shard_map/cond/branch_1_fun/ppermute | solution.py:859
  110.3 8.0 %collective-permute-start.28 = (bf16[256,2048]{1,0:T(8,128)(2,1)}, bf16[256,2048]{1,0:T(8,128)(2,1)S(1)}, u32[]{:S(2)}, u32[]{:S(2)}) collective-permute-start(bf16[256,2048]{1,0:T(8,128)(2,1)} %get-tuple-element.252), channel_id=1, source_target_pairs={{0,1},{1,0},{2,3},{3,2},{4,5},{5,4},{6,7},{7,6},{8,9},{9,8},{10,11... | collective-permute-start | bytes 3145736 | tf_op jit(solution)/shard_map/ppermute | solution.py:859
  119.6 14.5 %collective-permute-start.29 = (bf16[128,2048]{1,0:T(8,128)(2,1)}, bf16[128,2048]{1,0:T(8,128)(2,1)S(1)}, u32[]{:S(2)}, u32[]{:S(2)}) collective-permute-start(bf16[128,2048]{1,0:T(8,128)(2,1)} %slice.223), channel_id=1, source_target_pairs={{0,2},{2,0},{1,3},{3,1},{4,6},{6,4},{5,7},{7,5},{8,10},{10,8},{9,1... | collective-permute-start | bytes 1572872 | tf_op jit(solution)/shard_map/ppermute | solution.py:859
  136.3 13.5 %collective-permute-start.30 = (bf16[128,2048]{1,0:T(8,128)(2,1)S(1)}, bf16[128,2048]{1,0:T(8,128)(2,1)S(1)}, u32[]{:S(2)}, u32[]{:S(2)}) collective-permute-start(bf16[128,2048]{1,0:T(8,128)(2,1)S(1)} %get-tuple-element.379), channel_id=1, source_target_pairs={{0,8},{8,0},{1,9},{9,1},{2,10},{10,2},{3,11},{11,3},{4,12},{12,4},... | collective-permute-start | bytes 1572872 | tf_op jit(solution)/shard_map/ppermute | solution.py:859
  136.3 15.1 %collective-permute-start.31 = (bf16[128,2048]{1,0:T(8,128)(2,1)S(1)}, bf16[128,2048]{1,0:T(8,128)(2,1)S(1)}, u32[]{:S(2)}, u32[]{:S(2)}) collective-permute-start(bf16[128,2048]{1,0:T(8,128)(2,1)S(1)} %get-tuple-element.379), channel_id=1, source_target_pairs={{0,2},{2,0},{1,3},{3,1},{4,6},{6,4},{5,7},{7,5},{8,10},{10,8},{9,1... | collective-permute-start | bytes 1572872 | tf_op jit(solution)/shard_map/ppermute | solution.py:859
  149.9 12.7 %collective-permute-start.32 = (bf16[128,2048]{1,0:T(8,128)(2,1)S(1)}, bf16[128,2048]{1,0:T(8,128)(2,1)S(1)}, u32[]{:S(2)}, u32[]{:S(2)}) collective-permute-start(bf16[128,2048]{1,0:T(8,128)(2,1)S(1)} %collective-permute-done.30), channel_id=1, source_target_pairs={{0,2},{2,0},{1,3},{3,1},{4,6},{6,4},{5,7},{7,5},{8,10},{10,8},{9,1... | collective-permute-start | bytes 1572872 | tf_op jit(solution)/shard_map/ppermute | solution.py:859
  162.8 4.2 collective-permute-start.33
  194.9 235.3 %reduce-scatter.6.cloned.1.call-start = ((), (), s32[]{:S(2)}) async-start(), calls=%async_computation.4 | async-start | bytes 5242880 | tf_op jit(solution)/shard_map/reduce_scatter | solution.py:971
  204.1 9.8 %collective-permute-start.14 = (bf16[512,2048]{1,0:T(8,128)(2,1)}, bf16[512,2048]{1,0:T(8,128)(2,1)}, u32[]{:S(2)}, u32[]{:S(2)}) collective-permute-start(bf16[512,2048]{1,0:T(8,128)(2,1)} %get-tuple-element.85), channel_id=1, source_target_pairs={{0,1},{1,0},{2,3},{3,2},{4,5},{5,4},{6,7},{7,6},{8,9},{9,8},{10,11... | collective-permute-start | bytes 6291464 | tf_op jit(solution)/shard_map/cond/branch_1_fun/ppermute | solution.py:859
  217.1 15.0 %collective-permute-start.15 = (bf16[128,2048]{1,0:T(8,128)(2,1)}, bf16[128,2048]{1,0:T(8,128)(2,1)}, u32[]{:S(2)}, u32[]{:S(2)}) collective-permute-start(bf16[128,2048]{1,0:T(8,128)(2,1)} %get-tuple-element.387), channel_id=1, source_target_pairs={{0,2},{2,0},{1,3},{3,1},{4,6},{6,4},{5,7},{7,5},{8,10},{10,8},{9,1... | collective-permute-start | bytes 1572872 | tf_op jit(solution)/shard_map/cond/branch_1_fun/ppermute | solution.py:859
  218.3 25.3 %collective-permute-start.16 = (bf16[128,2048]{1,0:T(8,128)(2,1)S(1)}, bf16[128,2048]{1,0:T(8,128)(2,1)S(1)}, u32[]{:S(2)}, u32[]{:S(2)}) collective-permute-start(bf16[128,2048]{1,0:T(8,128)(2,1)S(1)} %get-tuple-element.385), channel_id=1, source_target_pairs={{0,2},{2,0},{1,3},{3,1},{4,6},{6,4},{5,7},{7,5},{8,10},{10,8},{9,1... | collective-permute-start | bytes 1572872 | tf_op jit(solution)/shard_map/cond/branch_1_fun/ppermute | solution.py:859
  234.7 25.7 %collective-permute-start.17 = (bf16[128,2048]{1,0:T(8,128)(2,1)}, bf16[128,2048]{1,0:T(8,128)(2,1)}, u32[]{:S(2)}, u32[]{:S(2)}) collective-permute-start(bf16[128,2048]{1,0:T(8,128)(2,1)} %add_convert_fusion.2), channel_id=1, source_target_pairs={{0,8},{8,0},{1,9},{9,1},{2,10},{10,2},{3,11},{11,3},{4,12},{12,4},... | collective-permute-start | bytes 1572872 | tf_op jit(solution)/shard_map/cond/branch_1_fun/ppermute | solution.py:859
  262.7 263.4 %reduce-scatter.8.cloned.1.call-start = ((), (), s32[]{:S(2)}) async-start(), calls=%async_computation.5 | async-start | bytes 5242880 | tf_op jit(solution)/shard_map/reduce_scatter | solution.py:971
  268.0 12.6 %collective-permute-start.23 = (bf16[128,2048]{1,0:T(8,128)(2,1)S(1)}, bf16[128,2048]{1,0:T(8,128)(2,1)S(1)}, u32[]{:S(2)}, u32[]{:S(2)}) collective-permute-start(bf16[128,2048]{1,0:T(8,128)(2,1)S(1)} %get-tuple-element.376), channel_id=1, source_target_pairs={{0,2},{2,0},{1,3},{3,1},{4,6},{6,4},{5,7},{7,5},{8,10},{10,8},{9,1... | collective-permute-start | bytes 1572872 | tf_op jit(solution)/shard_map/cond/branch_1_fun/ppermute | solution.py:859
  298.6 44.2 %collective-permute-start.34 = (bf16[2048,256]{1,0:T(8,128)(2,1)}, bf16[2048,256]{1,0:T(8,128)(2,1)}, u32[]{:S(2)}, u32[]{:S(2)}) collective-permute-start(bf16[2048,256]{1,0:T(8,128)(2,1)} %get-tuple-element.275), channel_id=1, source_target_pairs={{0,4},{4,0},{1,5},{5,1},{2,6},{6,2},{3,7},{7,3},{8,12},{12,8},{9,1... | collective-permute-start | bytes 3145736 | tf_op jit(solution)/shard_map/ppermute | solution.py:859
  315.9 60.4 %collective-permute-start.35 = (bf16[2048,256]{1,0:T(8,128)(2,1)}, bf16[2048,256]{1,0:T(8,128)(2,1)}, u32[]{:S(2)}, u32[]{:S(2)}) collective-permute-start(bf16[2048,256]{1,0:T(8,128)(2,1)} %get-tuple-element.279), channel_id=1, source_target_pairs={{0,4},{4,0},{1,5},{5,1},{2,6},{6,2},{3,7},{7,3},{8,12},{12,8},{9,1... | collective-permute-start | bytes 3145736 | tf_op jit(solution)/shard_map/ppermute | solution.py:859
  317.3 62.6 %collective-permute-start.36 = (bf16[256,1024]{1,0:T(8,128)(2,1)}, bf16[256,1024]{1,0:T(8,128)(2,1)S(1)}, u32[]{:S(2)}, u32[]{:S(2)}) collective-permute-start(bf16[256,1024]{1,0:T(8,128)(2,1)} %get-tuple-element.424), channel_id=1, source_target_pairs={{0,8},{8,0},{1,9},{9,1},{2,10},{10,2},{3,11},{11,3},{4,12},{12,4},... | collective-permute-start | bytes 1572872 | tf_op jit(solution)/shard_map/ppermute | solution.py:859
  380.3 84.2 %collective-permute-start.39 = (bf16[4,256,1024]{2,1,0:T(8,128)(2,1)}, bf16[4,256,1024]{2,1,0:T(8,128)(2,1)}, u32[]{:S(2)}, u32[]{:S(2)}) collective-permute-start(bf16[4,256,1024]{2,1,0:T(8,128)(2,1)} %get-tuple-element.302), channel_id=1, source_target_pairs={{0,4},{4,0},{1,5},{5,1},{2,6},{6,2},{3,7},{7,3},{8,12},{12,8},{9,1... | collective-permute-start | bytes 6291464 | tf_op jit(solution)/shard_map/ppermute | solution.py:859
  380.7 24.5 %collective-permute-start.38 = (bf16[1024,256]{1,0:T(8,128)(2,1)}, bf16[1024,256]{1,0:T(8,128)(2,1)}, u32[]{:S(2)}, u32[]{:S(2)}) collective-permute-start(bf16[1024,256]{1,0:T(8,128)(2,1)} %get-tuple-element.291), channel_id=1, source_target_pairs={{0,8},{8,0},{1,9},{9,1},{2,10},{10,2},{3,11},{11,3},{4,12},{12,4},... | collective-permute-start | bytes 1572872 | tf_op jit(solution)/shard_map/ppermute | solution.py:859
  382.4 43.9 %collective-permute-start.37 = (bf16[1024,256]{1,0:T(8,128)(2,1)}, bf16[1024,256]{1,0:T(8,128)(2,1)}, u32[]{:S(2)}, u32[]{:S(2)}) collective-permute-start(bf16[1024,256]{1,0:T(8,128)(2,1)} %get-tuple-element.288), channel_id=1, source_target_pairs={{0,8},{8,0},{1,9},{9,1},{2,10},{10,2},{3,11},{11,3},{4,12},{12,4},... | collective-permute-start | bytes 1572872 | tf_op jit(solution)/shard_map/ppermute | solution.py:859
  383.0 4.4 collective-permute-start.18
  388.6 14.0 %collective-permute-start.19 = (bf16[128,2048]{1,0:T(8,128)(2,1)S(1)}, bf16[128,2048]{1,0:T(8,128)(2,1)S(1)}, u32[]{:S(2)}, u32[]{:S(2)}) collective-permute-start(bf16[128,2048]{1,0:T(8,128)(2,1)S(1)} %add_convert_fusion.6), channel_id=1, source_target_pairs={{0,2},{2,0},{1,3},{3,1},{4,6},{6,4},{5,7},{7,5},{8,10},{10,8},{9,1... | collective-permute-start | bytes 1572872 | tf_op jit(solution)/shard_map/cond/branch_1_fun/ppermute | solution.py:859
  432.5 39.4 %collective-permute-start.41 = (bf16[512,256]{1,0:T(8,128)(2,1)}, bf16[512,256]{1,0:T(8,128)(2,1)S(1)}, u32[]{:S(2)}, u32[]{:S(2)}) collective-permute-start(bf16[512,256]{1,0:T(8,128)(2,1)} %get-tuple-element.418), channel_id=1, source_target_pairs={{0,16},{16,0},{1,17},{17,1},{2,18},{18,2},{3,19},{19,3},{4,20},{20... | collective-permute-start | bytes 786440 | tf_op jit(solution)/shard_map/ppermute | solution.py:859
  434.6 42.4 %collective-permute-start.40 = (bf16[512,256]{1,0:T(8,128)(2,1)}, bf16[512,256]{1,0:T(8,128)(2,1)}, u32[]{:S(2)}, u32[]{:S(2)}) collective-permute-start(bf16[512,256]{1,0:T(8,128)(2,1)} %get-tuple-element.420), channel_id=1, source_target_pairs={{0,16},{16,0},{1,17},{17,1},{2,18},{18,2},{3,19},{19,3},{4,20},{20... | collective-permute-start | bytes 786440 | tf_op jit(solution)/shard_map/ppermute | solution.py:859
  435.5 29.0 %collective-permute-start.7 = (bf16[128,2048]{1,0:T(8,128)(2,1)S(1)}, bf16[128,2048]{1,0:T(8,128)(2,1)}, u32[]{:S(2)}, u32[]{:S(2)}) collective-permute-start(bf16[128,2048]{1,0:T(8,128)(2,1)S(1)} %get-tuple-element.109), channel_id=1, source_target_pairs={{0,8},{8,0},{1,9},{9,1},{2,10},{10,2},{3,11},{11,3},{4,12},{12,4},... | collective-permute-start | bytes 1572872 | tf_op jit(solution)/shard_map/cond/branch_1_fun/ppermute | solution.py:859
  438.0 26.5 %collective-permute-start.8 = (bf16[128,2048]{1,0:T(8,128)(2,1)S(1)}, bf16[128,2048]{1,0:T(8,128)(2,1)}, u32[]{:S(2)}, u32[]{:S(2)}) collective-permute-start(bf16[128,2048]{1,0:T(8,128)(2,1)S(1)} %get-tuple-element.110), channel_id=1, source_target_pairs={{0,2},{2,0},{1,3},{3,1},{4,6},{6,4},{5,7},{7,5},{8,10},{10,8},{9,1... | collective-permute-start | bytes 1572872 | tf_op jit(solution)/shard_map/cond/branch_1_fun/ppermute | solution.py:859
  483.7 35.4 %collective-permute-start.42 = (bf16[2,256,1024]{2,1,0:T(8,128)(2,1)}, bf16[2,256,1024]{2,1,0:T(8,128)(2,1)}, u32[]{:S(2)}, u32[]{:S(2)}) collective-permute-start(bf16[2,256,1024]{2,1,0:T(8,128)(2,1)} %get-tuple-element.391), channel_id=1, source_target_pairs={{0,8},{8,0},{1,9},{9,1},{2,10},{10,2},{3,11},{11,3},{4,12},{12,4},... | collective-permute-start | bytes 3145736 | tf_op jit(solution)/shard_map/ppermute | solution.py:859
  491.4 30.3 %collective-permute-start.43 = (bf16[4,256,512]{2,1,0:T(8,128)(2,1)}, bf16[4,256,512]{2,1,0:T(8,128)(2,1)}, u32[]{:S(2)}, u32[]{:S(2)}) collective-permute-start(bf16[4,256,512]{2,1,0:T(8,128)(2,1)} %get-tuple-element.326), channel_id=1, source_target_pairs={{0,4},{4,0},{1,5},{5,1},{2,6},{6,2},{3,7},{7,3},{8,12},{12,8},{9,1... | collective-permute-start | bytes 3145736 | tf_op jit(solution)/shard_map/ppermute | solution.py:859
  495.0 28.2 %collective-permute-start.44 = (bf16[256,1024]{1,0:T(8,128)(2,1)}, bf16[256,1024]{1,0:T(8,128)(2,1)}, u32[]{:S(2)}, u32[]{:S(2)}) collective-permute-start(bf16[256,1024]{1,0:T(8,128)(2,1)} %get-tuple-element.329), channel_id=1, source_target_pairs={{0,8},{8,0},{1,9},{9,1},{2,10},{10,2},{3,11},{11,3},{4,12},{12,4},... | collective-permute-start | bytes 1572872 | tf_op jit(solution)/shard_map/ppermute | solution.py:859
  501.2 14.0 %collective-permute-start.21 = (bf16[128,2048]{1,0:T(8,128)(2,1)S(1)}, bf16[128,2048]{1,0:T(8,128)(2,1)S(1)}, u32[]{:S(2)}, u32[]{:S(2)}) collective-permute-start(bf16[128,2048]{1,0:T(8,128)(2,1)S(1)} %add_convert_fusion.11), channel_id=1, source_target_pairs={{0,2},{2,0},{1,3},{3,1},{4,6},{6,4},{5,7},{7,5},{8,10},{10,8},{9,1... | collective-permute-start | bytes 1572872 | tf_op jit(solution)/shard_map/cond/branch_1_fun/ppermute | solution.py:859
  517.5 32.7 %collective-permute-start.46 = (bf16[256,2048]{1,0:T(8,128)(2,1)S(1)}, bf16[256,2048]{1,0:T(8,128)(2,1)}, u32[]{:S(2)}, u32[]{:S(2)}) collective-permute-start(bf16[256,2048]{1,0:T(8,128)(2,1)S(1)} %pad_maximum_fusion.4), channel_id=1, source_target_pairs={{0,2},{2,0},{1,3},{3,1},{4,6},{6,4},{5,7},{7,5},{8,10},{10,8},{9,1... | collective-permute-start | bytes 3145736 | tf_op jit(solution)/shard_map/ppermute | solution.py:859
  523.3 26.2 %collective-permute-start.45 = (bf16[2,256,512]{2,1,0:T(8,128)(2,1)S(1)}, bf16[2,256,512]{2,1,0:T(8,128)(2,1)S(1)}, u32[]{:S(2)}, u32[]{:S(2)}) collective-permute-start(bf16[2,256,512]{2,1,0:T(8,128)(2,1)S(1)} %get-tuple-element.399), channel_id=1, source_target_pairs={{0,8},{8,0},{1,9},{9,1},{2,10},{10,2},{3,11},{11,3},{4,12},{12,4},... | collective-permute-start | bytes 1572872 | tf_op jit(solution)/shard_map/ppermute | solution.py:859
  528.2 65.7 %collective-permute-start.48 = (bf16[256,1024]{1,0:T(8,128)(2,1)}, bf16[256,1024]{1,0:T(8,128)(2,1)}, u32[]{:S(2)}, u32[]{:S(2)}) collective-permute-start(bf16[256,1024]{1,0:T(8,128)(2,1)} %get-tuple-element.345), channel_id=1, source_target_pairs={{0,8},{8,0},{1,9},{9,1},{2,10},{10,2},{3,11},{11,3},{4,12},{12,4},... | collective-permute-start | bytes 1572872 | tf_op jit(solution)/shard_map/ppermute | solution.py:859
  530.1 69.5 %collective-permute-start.49 = (bf16[1,256,1024]{2,1,0:T(8,128)(2,1)}, bf16[1,256,1024]{2,1,0:T(8,128)(2,1)}, u32[]{:S(2)}, u32[]{:S(2)}) collective-permute-start(bf16[1,256,1024]{2,1,0:T(8,128)(2,1)} %get-tuple-element.393), channel_id=1, source_target_pairs={{0,16},{16,0},{1,17},{17,1},{2,18},{18,2},{3,19},{19,3},{4,20},{20... | collective-permute-start | bytes 1572872 | tf_op jit(solution)/shard_map/ppermute | solution.py:859
  550.3 20.5 %collective-permute-start.47 = (bf16[1,256,512]{2,1,0:T(8,128)(2,1)}, bf16[1,256,512]{2,1,0:T(8,128)(2,1)S(1)}, u32[]{:S(2)}, u32[]{:S(2)}) collective-permute-start(bf16[1,256,512]{2,1,0:T(8,128)(2,1)} %get-tuple-element.412), channel_id=1, source_target_pairs={{0,16},{16,0},{1,17},{17,1},{2,18},{18,2},{3,19},{19,3},{4,20},{20... | collective-permute-start | bytes 786440 | tf_op jit(solution)/shard_map/ppermute | solution.py:859
  554.2 4.5 collective-permute-start.22
  577.7 3.8 collective-permute-start.10
  581.5 3.8 collective-permute-start.11
  589.1 4.7 collective-permute-start.13
  (39 other events, 342.3 us)
Sparse Core Ops, SparseCore 0:
  195.0 91.6 reduce-scatter.3
  290.0 86.1 reduce-scatter.5
  379.1 100.0 reduce-scatter.7

commit v12 on v10

--- a/solution.py
+++ b/solution.py
@@ -1106,7 +1106,6 @@
     grad_middle, ffn_gain_part, up_shares, grad_branch = stage(
         branch_stage, grad_second, grad_up, cot_own
     )
-    up = unit_sum_over(up_shares)
     backward, kv = [], []
     held = grad_branch
     for head in range(kv_heads):
@@ -1159,6 +1158,7 @@
     dep = branch_shares[0]
     kv = [item.merge(dep) for item in kv]
     dep = tuple(keep for keep, _ in kv)
+    up = unit_sum_over(after(dep, up_shares))
     sum_down = join_halves(down_own, after(dep, down_other), ctx).T
     dep = sum_down
     got = [ctx_flip(after(dep, value), 2) for _, value in kv]
@@ -1198,21 +1198,23 @@
     dep = grad_input
     near = jnp.concatenate([grad_input, output])
     near_other = flip(after(dep, near), "y")
+    sum_gate = join_halves(gate_own, after(dep, gate_other), ctx)
+    dep = sum_gate
     for mask in highs:
         branch.halve(mask, ctx, dep)
         dep = branch.keep
-    sum_gate = join_halves(gate_own, after(dep, gate_other), ctx)
-    dep = sum_gate
     last.halve(2, ctx, dep)
     dep = last.keep
-    up_own, up_away = split_halves(up, ctx, dep)
-    dep = up_own
-    up_other = ctx_flip(after(dep, up_away), 2)
+    gains = stage(gain_stage, after(dep, jnp.stack([attn_gain_part, ffn_gain_part])))
+    dep = gains
     for mask in highs:
         last.halve(mask, ctx, dep)
         dep = last.keep
     near, far = stage(row_stage, near, after(dep, near_other))
     dep = far
+    up_own, up_away = split_halves(up, ctx, dep)
+    dep = up_own
+    up_other = ctx_flip(after(dep, up_away), 2)
     last.keep, last.got = after(dep, last.keep, last.got)
     last_sum = last.sum()
     dep = last_sum
@@ -1223,13 +1225,11 @@
         for k in range(2)
     ]
     dep = (grad_rows, output_rows)
-    gains = stage(gain_stage, after(dep, jnp.stack([attn_gain_part, ffn_gain_part])))
-    dep = gains
-    sum_up = join_halves(up_own, after(dep, up_other), ctx)
-    dep = sum_up
     branch.keep, branch.got = after(dep, branch.keep, branch.got)
     branch_sum = branch.sum()
     dep = branch_sum
+    sum_up = join_halves(up_own, after(dep, up_other), ctx)
+    dep = sum_up
     grad_input, output = grad_rows, output_rows
     width_q, width_k = w_query.shape[1], key_matrix.shape[1]
     sum_query, sum_out = branch_sum[:, :width_q], branch_sum[:, width_q:].T

time: 622 us -> 610 us (0.981)
  waiting for transfers between devices: 279 us -> 257 us
  starting transfers between devices: 57.8 us -> 65.9 us
  local copies, waits for them, and re-layouts: 38.7 us -> 45.2 us
    ppermute x50, waiting for transfers between devices: 279 us -> 257 us  [flip(): lax.ppermute(value, axis, [(i, i ^ mask) for i in range(lax.axis_size(axi...]
    ppermute x50, starting transfers between devices: 57.7 us -> 65.8 us  [flip(): lax.ppermute(value, axis, [(i, i ^ mask) for i in range(lax.axis_size(axi...]
    unnamed x54 -> x52, local copies, waits for them, and re-layouts: 14.5 us -> 18.7 us
  transfers between devices with their start and end apart: 53 -> 53, of which waited for: 34 -> 33; matrix products, arithmetic and copies ran while one was open for 15% -> 15% of each run, Pallas kernels for 19% -> 19%
where the time goes in v12:
time: 610 us; the launch traced here: 604 us
  waiting for transfers between devices  257 us (42%)
  Pallas kernels  157 us (26%)
  starting transfers between devices  65.9 us (11%)
  other arithmetic  62.8 us (10%)
  local copies, waits for them, and re-layouts  45.2 us (7%)
  between operations  15.3 us (3%)
    ppermute x50, waiting for transfers between devices, flip(): lax.ppermute(value, axis, [(i, i ^ mask) for i in range(lax.axis_size(axi...  257 us
    ppermute x50, starting transfers between devices, flip(): lax.ppermute(value, axis, [(i, i ^ mask) for i in range(lax.axis_size(axi...  65.8 us
    pallas_call x3, Pallas kernels, unit_shares(): pl.pallas_call(unit_shares_kernel, out_shape=shares, grid_spec=pltpu.Pref...  31.5 us
    convert_element_type x13, other arithmetic, add(): (left.astype(jnp.float32) + right.astype(jnp.float32)).astype(jnp.bfloat16)  31.4 us
    pallas_call x2, Pallas kernels, attention_backward(): pl.pallas_call(functools.partial(backward_kernel, rep, 1, ctx_count, head...  26 us
    unnamed x52, local copies, waits for them, and re-layouts  18.7 us
    pallas_call x2, Pallas kernels, grad_second_half(): pl.pallas_call(grad_second_kernel, out_shape=jax.ShapeDtypeStruct((rows,...  18 us
    pallas_call x1, Pallas kernels, attention_forward(): pl.pallas_call(functools.partial(forward_kernel, rep, kv_heads, ctx_count...  17 us
  transfers between devices with their start and end apart: 53, of which 33 were waited for; matrix products, arithmetic and copies ran while one was open for 15% of the time, Pallas kernels for 19%

profile of v12, /device:TPU:0, one launch (start us, length us, event | category | flops | bytes accessed | tf_op | source)
XLA Modules:
  0.0 603.9 jit_solution(14709652449166719961)
XLA Ops:
  13.0 7.2 %input_stage.1 = (bf16[512,2048]{1,0:T(8,128)(2,1)}, bf16[512,512]{1,0:T(8,128)(2,1)}, bf16[512,512]{1,0:T(8,128)(2,1)S(1)}, f32[512,128]{1,0:T(8,128)}, f32[512,128]{1,0:T(8,128)}) custom-call(s32[32]{0:T(128)} %order_ref.7, s32[8]{0:T(128)} %cont_ref.7, s32[2]{0:T(128)S(1)} %pad_add_fusion.where_ref, f32[1,2048]{1,0:T(1,128)} %bitcast.31, ...), custom_call_target="tpu_custom_call" | custom-call | flops 42949672 | bytes 167772 | tf_op jit(solution)/shard_map/input_stage/pallas_call | solution.py:512
  20.2 4.0 collective-permute-done.27
  24.2 25.6 %conditional.10 = (bf16[512,512]{1,0:T(8,128)(2,1)}, bf16[512,512]{1,0:T(8,128)(2,1)}, bf16[512,512]{1,0:T(8,128)(2,1)}) conditional(s32[]{:T(128)} %bitcast.2, () %tuple.140, bf16[512,512]{1,0:T(8,128)(2,1)S(1)} %get-tuple-element.243.refs_0_), branch_computations={%region_0.0_spmd, %region_1.0_spmd} | conditional | bytes 6291600 | solution.py:895
  30.0 19.6 %collective-permute-done = bf16[512,512]{1,0:T(8,128)(2,1)} collective-permute-done((bf16[512,512]{1,0:T(8,128)(2,1)S(1)}, bf16[512,512]{1,0:T(8,128)(2,1)}, u32[]{:S(2)}, u32[]{:S(2)}) %collective-permute-start) | collective-permute-done | bytes 524320 | tf_op jit(solution)/shard_map/cond/branch_1_fun/ppermute | solution.py:859
  49.8 25.2 %conditional.11 = (bf16[512,512]{1,0:T(8,128)(2,1)}, bf16[128,2048]{1,0:T(8,128)(2,1)}, bf16[512,512]{1,0:T(8,128)(2,1)}, bf16[512,512]{1,0:T(8,128)(2,1)}) conditional(s32[]{:T(128)} %bitcast.2, () %tuple.142, (bf16[512,512]{1,0:T(8,128)(2,1)}, bf16[128,2048]{1,0:T(8,128)(2,1)S(1)}, bf16[512,512]{1,0:T(8,128)(2,1)}) %tuple.143), branch_computations={%region_2.0_spmd, %region_3.0_spmd} | conditional | bytes 8388800 | solution.py:895
  54.6 8.2 %collective-permute-done.5 = bf16[512,512]{1,0:T(8,128)(2,1)} collective-permute-done((bf16[512,512]{1,0:T(8,128)(2,1)}, bf16[512,512]{1,0:T(8,128)(2,1)}, u32[]{:S(2)}, u32[]{:S(2)}) %collective-permute-start.5) | collective-permute-done | bytes 524320 | tf_op jit(solution)/shard_map/cond/branch_1_fun/ppermute | solution.py:859
  62.8 3.4 collective-permute-done.6
  66.3 8.8 %collective-permute-done.3 = bf16[512,512]{1,0:T(8,128)(2,1)} collective-permute-done((bf16[512,512]{1,0:T(8,128)(2,1)}, bf16[512,512]{1,0:T(8,128)(2,1)}, u32[]{:S(2)}, u32[]{:S(2)}) %collective-permute-start.3) | collective-permute-done | bytes 524320 | tf_op jit(solution)/shard_map/cond/branch_1_fun/ppermute | solution.py:859
  76.2 14.9 %conditional.12 = (bf16[512,512]{1,0:T(8,128)(2,1)}, bf16[256,2048]{1,0:T(8,128)(2,1)}, bf16[128,2048]{1,0:T(8,128)(2,1)S(1)}, bf16[128,2048]{1,0:T(8,128)(2,1)S(1)}) conditional(s32[]{:T(128)} %bitcast.2, () %tuple.144, (bf16[512,512]{1,0:T(8,128)(2,1)}, bf16[256,2048]{1,0:T(8,128)(2,1)S(1)}) %tuple.145), branch_computations={%region_4.0_spmd, %region_5.0_spmd} | conditional | bytes 8388720 | solution.py:895
  80.3 10.6 %collective-permute-done.25 = bf16[512,512]{1,0:T(8,128)(2,1)} collective-permute-done((bf16[512,512]{1,0:T(8,128)(2,1)}, bf16[512,512]{1,0:T(8,128)(2,1)}, u32[]{:S(2)}, u32[]{:S(2)}) %collective-permute-start.25) | collective-permute-done | bytes 524320 | tf_op jit(solution)/shard_map/cond/branch_1_fun/ppermute | solution.py:859
  91.1 17.0 %attention_forward.1 = (bf16[512,512]{1,0:T(8,128)(2,1)}, f32[2,4,256]{2,1,0:T(4,128)}, bf16[256,2048]{1,0:T(8,128)(2,1)}, bf16[256,2048]{1,0:T(8,128)(2,1)}) custom-call(s32[32]{0:T(128)} %order_ref.7, s32[8]{0:T(128)} %cont_ref.7, s32[2]{0:T(128)S(1)} %pad_add_fusion.where_ref, bf16[512,512]{1,0:T(8,128)(2,1)} %get-tuple-element.241.q_ref, ...), custom_call_target="tpu_custom_call" | custom-call | flops 64424508 | bytes 167772 | tf_op jit(solution)/shard_map/attention_forward/pallas_call | solution.py:367
  118.3 9.7 %grad_hidden.1.gh_ref = f32[1024,1024]{1,0:T(8,128)} custom-call(s32[2]{0:T(128)S(1)} %pad_add_fusion.where_ref, bf16[1024,2048]{1,0:T(8,128)(2,1)} %constant_dynamic-update-slice_fusion.2.cot_ref.left_ref, bf16[2048,2048]{1,0:T(8,128)(2,1)} %wd_ref.1), custom_call_target="tpu_custom_call" | custom-call | flops 68719476736 | bytes 134217728 | tf_op jit(solution)/shard_map/grad_hidden/pallas_call | solution.py:570
  135.3 3.6 collective-permute-start.30
  140.2 10.6 %collective-permute-done.30 = bf16[128,2048]{1,0:T(8,128)(2,1)S(1)} collective-permute-done((bf16[128,2048]{1,0:T(8,128)(2,1)S(1)}, bf16[128,2048]{1,0:T(8,128)(2,1)S(1)}, u32[]{:S(2)}, u32[]{:S(2)}) %collective-permute-start.30) | collective-permute-done | bytes 524320 | tf_op jit(solution)/shard_map/ppermute | solution.py:859
  152.2 11.5 %collective-permute-done.32 = bf16[128,2048]{1,0:T(8,128)(2,1)S(1)} collective-permute-done((bf16[128,2048]{1,0:T(8,128)(2,1)S(1)}, bf16[128,2048]{1,0:T(8,128)(2,1)S(1)}, u32[]{:S(2)}, u32[]{:S(2)}) %collective-permute-start.32) | collective-permute-done | bytes 524320 | tf_op jit(solution)/shard_map/ppermute | solution.py:859
  169.7 15.6 %ffn_stage.1 = (bf16[1024,1024]{1,0:T(8,128)(2,1)}, bf16[1024,1024]{1,0:T(8,128)(2,1)}, bf16[1024,1024]{1,0:T(8,128)(2,1)S(1)}) custom-call(s32[2]{0:T(128)S(1)} %pad_add_fusion.where_ref, bf16[1024,2048]{1,0:T(8,128)(2,1)} %constant_dynamic-update-slice_fusion.7.in_ref, f32[1024,1024]{1,0:T(8,128)} %grad_hidden.1.gh_ref, bf16[2048,2048]{1,0:T(8,128)(2,1)} %wg_ref.3, ...), custom_call_target="tpu_custom_call" | custom-call | flops 171798688 | bytes 251658 | tf_op jit(solution)/shard_map/ffn_stage/pallas_call | solution.py:609
  185.4 10.7 %down_shares.1 = bf16[8,256,1024]{2,1,0:T(8,128)(2,1)} custom-call(s32[2]{0:T(128)S(1)} %pad_add_fusion.where_ref, bf16[1024,2048]{1,0:T(8,128)(2,1)} %constant_dynamic-update-slice_fusion.2.cot_ref.left_ref, bf16[1024,1024]{1,0:T(8,128)(2,1)} %get-tuple-element.258.right_ref), custom_call_target="tpu_custom_call" | custom-call | flops 85899344 | bytes 167772 | tf_op jit(solution)/shard_map/down_shares/pallas_call | solution.py:789
  196.2 9.0 %grad_second_send.1 = bf16[512,2048]{1,0:T(8,128)(2,1)} custom-call(s32[2]{0:T(128)S(1)} %pad_add_fusion.where_ref, bf16[1024,1024]{1,0:T(8,128)(2,1)} %get-tuple-element.261.gg_ref, bf16[1024,1024]{1,0:T(8,128)(2,1)S(1)} %get-tuple-element.262.gu_ref, bf16[2048,2048]{1,0:T(8,128)(2,1)} %wg_ref.3, bf16[2048,2048]{1,0:T(8,128)(2,1)} %wu_ref.3), custom_call_target="tpu_custom_call" | custom-call | flops 85899344 | bytes 83886 | tf_op jit(solution)/shard_map/grad_second_send/pallas_call | solution.py:641
  205.1 58.7 %conditional.13 = (f32[128,2048]{1,0:T(8,128)}, bf16[8,256,1024]{2,1,0:T(8,128)(2,1)}, bf16[512,2048]{1,0:T(8,128)(2,1)}, bf16[512,2048]{1,0:T(8,128)(2,1)}) conditional(s32[]{:T(128)} %bitcast.2, () %tuple.151, (s32[2]{0:T(128)S(1)}, bf16[1024,1024]{1,0:T(8,128)(2,1)}, bf16[1024,1024]{1,0:T(8,128)(2,1)S(1)}, bf16[2048,2048]{1,0:T(8,128)(2,1)}, ...), branch_computations={%region_7.0_spmd, %region_8.0_spmd} | conditional | flops 264251632 | bytes 24536870 | solution.py:895
  205.5 9.0 %grad_second_keep.1 = bf16[512,2048]{1,0:T(8,128)(2,1)} custom-call(s32[2]{0:T(128)S(1)} %get-tuple-element.80.where_ref, bf16[1024,1024]{1,0:T(8,128)(2,1)} %get-tuple-element.87.gg_ref.right_ref, bf16[1024,1024]{1,0:T(8,128)(2,1)S(1)} %get-tuple-element.82.gu_ref, bf16[2048,2048]{1,0:T(8,128)(2,1)} %get-tuple-element.83.wg_ref, ...), custom_call_target="tpu_custom_call" | custom-call | flops 85899344 | bytes 83886 | tf_op jit(solution)/shard_map/cond/branch_1_fun/grad_second_keep/pallas_call | solution.py:641
  214.6 3.5 add_convert_fusion
  220.1 10.8 %gate_shares.1 = bf16[8,256,1024]{2,1,0:T(8,128)(2,1)} custom-call(s32[2]{0:T(128)S(1)} %get-tuple-element.80.where_ref, bf16[1024,2048]{1,0:T(8,128)(2,1)} %get-tuple-element.86.left_ref, bf16[1024,1024]{1,0:T(8,128)(2,1)} %get-tuple-element.87.gg_ref.right_ref), custom_call_target="tpu_custom_call" | custom-call | flops 85899344 | bytes 167772 | tf_op jit(solution)/shard_map/cond/branch_1_fun/gate_shares/pallas_call | solution.py:789
  237.3 8.7 %ffn_out.1 = (bf16[512,2048]{1,0:T(8,128)(2,1)}, bf16[512,2048]{1,0:T(8,128)(2,1)}) custom-call(s32[2]{0:T(128)S(1)} %get-tuple-element.80.where_ref, bf16[1024,1024]{1,0:T(8,128)(2,1)} %get-tuple-element.90.hid_ref, bf16[2048,2048]{1,0:T(8,128)(2,1)} %get-tuple-element.91.wd_ref), custom_call_target="tpu_custom_call" | custom-call | flops 85899344 | bytes 167772 | tf_op jit(solution)/shard_map/cond/branch_1_fun/ffn_out/pallas_call | solution.py:674
  246.0 15.4 %collective-permute-done.17 = bf16[128,2048]{1,0:T(8,128)(2,1)} collective-permute-done((bf16[128,2048]{1,0:T(8,128)(2,1)}, bf16[128,2048]{1,0:T(8,128)(2,1)}, u32[]{:S(2)}, u32[]{:S(2)}) %collective-permute-start.17) | collective-permute-done | bytes 524320 | tf_op jit(solution)/shard_map/cond/branch_1_fun/ppermute | solution.py:859
  264.0 22.1 %conditional.14 = (f32[128,2048]{1,0:T(8,128)}, bf16[8,256,1024]{2,1,0:T(8,128)(2,1)}, bf16[512,2048]{1,0:T(8,128)(2,1)S(1)}, f32[1,2048]{1,0:T(1,128)S(1)}) conditional(s32[]{:T(128)} %bitcast.2, () %tuple.150, (bf16[128,2048]{1,0:T(8,128)(2,1)}, f32[128]{0:T(128)S(1)}, f32[2048]{0:T(1024)S(1)}, f32[128,2048]{1,0:T(8,128)}, f32[128,2048]{1,0:T(8,128)}, ...), branch_computations={%region_9.0_spmd, %region_10.13_spmd} | conditional | flops 97431632 | bytes 25360900 | solution.py:895
  268.7 10.0 %up_shares.1 = bf16[8,256,1024]{2,1,0:T(8,128)(2,1)} custom-call(s32[2]{0:T(128)S(1)} %get-tuple-element.102.where_ref, bf16[1024,2048]{1,0:T(8,128)(2,1)} %get-tuple-element.103.left_ref, bf16[1024,1024]{1,0:T(8,128)(2,1)S(1)} %get-tuple-element.105.right_ref), custom_call_target="tpu_custom_call" | custom-call | flops 85899344 | bytes 167772 | tf_op jit(solution)/shard_map/cond/branch_1_fun/up_shares/pallas_call | solution.py:789
  286.1 13.0 %attention_backward_0.1 = (bf16[512,256]{1,0:T(8,128)(2,1)}, bf16[2048,256]{1,0:T(8,128)(2,1)}, bf16[2048,256]{1,0:T(8,128)(2,1)}) custom-call(s32[32]{0:T(128)} %order_ref.7, s32[8]{0:T(128)} %cont_ref.7, s32[2]{0:T(128)S(1)} %pad_add_fusion.where_ref, bf16[512,512]{1,0:T(8,128)(2,1)} %get-tuple-element.241.q_ref, ...), custom_call_target="tpu_custom_call" | custom-call | flops 64424508 | bytes 125829 | tf_op jit(solution)/shard_map/attention_backward_0/pallas_call | solution.py:403
  302.7 13.0 %attention_backward_1.1 = (bf16[512,256]{1,0:T(8,128)(2,1)}, bf16[2048,256]{1,0:T(8,128)(2,1)}, bf16[2048,256]{1,0:T(8,128)(2,1)}) custom-call(s32[32]{0:T(128)} %order_ref.7, s32[8]{0:T(128)} %cont_ref.7, s32[2]{0:T(128)S(1)} %pad_add_fusion.where_ref, bf16[512,512]{1,0:T(8,128)(2,1)} %get-tuple-element.241.q_ref, ...), custom_call_target="tpu_custom_call" | custom-call | flops 64424508 | bytes 125829 | tf_op jit(solution)/shard_map/attention_backward_1/pallas_call | solution.py:403
  319.2 9.1 %branch_shares.1 = (bf16[4,256,1024]{2,1,0:T(8,128)(2,1)}, bf16[4,256,1024]{2,1,0:T(8,128)(2,1)}) custom-call(s32[2]{0:T(128)S(1)} %pad_add_fusion.where_ref, bf16[512,2048]{1,0:T(8,128)(2,1)} %get-tuple-element.240.refs_0_, bf16[512,2048]{1,0:T(8,128)(2,1)S(1)} %get-tuple-element.271.gb_ref.refs_1_, bf16[512,256]{1,0:T(8,128)(2,1)} %get-tuple-element.269.refs_2_.refs_6_, ...), custom_call_target="tpu_custom_call" | custom-call | flops 42949672 | bytes 83886 | tf_op jit(solution)/shard_map/branch_shares/pallas_call | solution.py:745
  328.3 14.6 %collective-permute-done.34 = bf16[2048,256]{1,0:T(8,128)(2,1)} collective-permute-done((bf16[2048,256]{1,0:T(8,128)(2,1)}, bf16[2048,256]{1,0:T(8,128)(2,1)}, u32[]{:S(2)}, u32[]{:S(2)}) %collective-permute-start.34) | collective-permute-done | bytes 1048608 | tf_op jit(solution)/shard_map/ppermute | solution.py:859
  342.9 33.4 %collective-permute-done.35 = bf16[2048,256]{1,0:T(8,128)(2,1)} collective-permute-done((bf16[2048,256]{1,0:T(8,128)(2,1)}, bf16[2048,256]{1,0:T(8,128)(2,1)}, u32[]{:S(2)}, u32[]{:S(2)}) %collective-permute-start.35) | collective-permute-done | bytes 1048608 | tf_op jit(solution)/shard_map/ppermute | solution.py:859
  376.3 3.8 add_convert_fusion.21
  385.0 22.8 %conditional.15 = (bf16[128,2048]{1,0:T(8,128)(2,1)}, bf16[128,2048]{1,0:T(8,128)(2,1)}, bf16[128,2048]{1,0:T(8,128)(2,1)}) conditional(s32[]{:T(128)} %bitcast.2, () %tuple.149, (bf16[512,2048]{1,0:T(8,128)(2,1)}, bf16[512,2048]{1,0:T(8,128)(2,1)}) %tuple.162), branch_computations={%region_14.15_spmd, %region_15.16_spmd} | conditional | flops 5242880 | bytes 17301608 | solution.py:895
  385.4 4.4 collective-permute-done.18
  392.6 12.3 %collective-permute-done.19 = bf16[128,2048]{1,0:T(8,128)(2,1)S(1)} collective-permute-done((bf16[128,2048]{1,0:T(8,128)(2,1)S(1)}, bf16[128,2048]{1,0:T(8,128)(2,1)S(1)}, u32[]{:S(2)}, u32[]{:S(2)}) %collective-permute-start.19) | collective-permute-done | bytes 524320 | tf_op jit(solution)/shard_map/cond/branch_1_fun/ppermute | solution.py:859
  407.9 21.0 %collective-permute-done.37 = bf16[1024,256]{1,0:T(8,128)(2,1)} collective-permute-done((bf16[1024,256]{1,0:T(8,128)(2,1)}, bf16[1024,256]{1,0:T(8,128)(2,1)}, u32[]{:S(2)}, u32[]{:S(2)}) %collective-permute-start.37) | collective-permute-done | bytes 524320 | tf_op jit(solution)/shard_map/ppermute | solution.py:859
  438.3 32.4 %conditional.16 = (bf16[128,2048]{1,0:T(8,128)(2,1)}, bf16[128,2048]{1,0:T(8,128)(2,1)}) conditional(s32[]{:T(128)} %bitcast.2, () %tuple.148, (bf16[128,2048]{1,0:T(8,128)(2,1)}, bf16[128,2048]{1,0:T(8,128)(2,1)}) %tuple.169), branch_computations={%region_17.18_spmd, %region_18.19_spmd} | conditional | bytes 4194400 | solution.py:895
  442.0 28.7 %collective-permute-done.7 = bf16[128,2048]{1,0:T(8,128)(2,1)} collective-permute-done((bf16[128,2048]{1,0:T(8,128)(2,1)}, bf16[128,2048]{1,0:T(8,128)(2,1)}, u32[]{:S(2)}, u32[]{:S(2)}) %collective-permute-start.7) | collective-permute-done | bytes 524320 | tf_op jit(solution)/shard_map/cond/branch_1_fun/ppermute | solution.py:859
  473.2 4.6 add_convert_fusion.13
  481.3 6.6 %tail_stage.1 = (bf16[256,2048]{1,0:T(8,128)(2,1)}, bf16[256,2048]{1,0:T(8,128)(2,1)}, bf16[512,512]{1,0:T(8,128)(2,1)}) custom-call(s32[2]{0:T(128)S(1)} %pad_add_fusion.where_ref, bf16[512,256]{1,0:T(8,128)(2,1)} %get-tuple-element.311.refs_0_, bf16[512,256]{1,0:T(8,128)(2,1)} %collective-permute-done.40.refs_1_, ...), custom_call_target="tpu_custom_call" | custom-call | flops 42949672 | bytes 167772 | tf_op jit(solution)/shard_map/tail_stage/pallas_call | solution.py:841
  488.0 7.7 %kv_shares.1 = (bf16[4,256,512]{2,1,0:T(8,128)(2,1)}, bf16[4,256,512]{2,1,0:T(8,128)(2,1)}) custom-call(s32[2]{0:T(128)S(1)} %pad_add_fusion.where_ref, bf16[512,2048]{1,0:T(8,128)(2,1)} %get-tuple-element.240.refs_0_, bf16[512,512]{1,0:T(8,128)(2,1)} %get-tuple-element.317.refs_1_), custom_call_target="tpu_custom_call" | custom-call | flops 17179869184 | bytes 67108864 | tf_op jit(solution)/shard_map/kv_shares/pallas_call | solution.py:745
  496.8 20.3 %conditional.17 = (bf16[128,2048]{1,0:T(8,128)(2,1)S(1)}, f32[1,2048]{1,0:T(1,128)S(1)}) conditional(s32[]{:T(128)} %bitcast.2, () %tuple.139, (f32[128,2048]{1,0:T(8,128)S(1)}, bf16[256,2048]{1,0:T(8,128)(2,1)}, bf16[256,2048]{1,0:T(8,128)(2,1)}, f32[2048]{0:T(1024)S(1)}, f32[128,2048]{1,0:T(8,128)}) %tuple.259), branch_computations={%region_19.20_spmd, %region_20.24_spmd} | conditional | flops 8648832 | bytes 19952252 | solution.py:895
  502.6 12.3 %collective-permute-done.21 = bf16[128,2048]{1,0:T(8,128)(2,1)S(1)} collective-permute-done((bf16[128,2048]{1,0:T(8,128)(2,1)S(1)}, bf16[128,2048]{1,0:T(8,128)(2,1)S(1)}, u32[]{:S(2)}, u32[]{:S(2)}) %collective-permute-start.21) | collective-permute-done | bytes 524320 | tf_op jit(solution)/shard_map/cond/branch_1_fun/ppermute | solution.py:859
  534.0 24.9 %conditional.18 = (f32[2,2048]{1,0:T(2,128)S(1)}) conditional(s32[]{:T(128)} %bitcast.2, () %tuple.178, f32[2,2048]{1,0:T(2,128)S(1)} %pad_maximum_fusion.5), branch_computations={%region_24.25_spmd, %region_25.26_spmd} | conditional | flops 20480 | bytes 573648 | solution.py:895
  535.9 7.4 %collective-permute-done.10 = f32[2,2048]{1,0:T(2,128)S(1)} collective-permute-done((f32[2,2048]{1,0:T(2,128)S(1)}, f32[2,2048]{1,0:T(2,128)S(1)}, u32[]{:S(2)}, u32[]{:S(2)}) %collective-permute-start.10) | collective-permute-done | bytes 16416 | tf_op jit(solution)/shard_map/cond/branch_1_fun/ppermute | solution.py:859
  552.1 5.0 collective-permute-start.13
  564.5 7.9 %conditional.19 = (bf16[512,2048]{1,0:T(8,128)(2,1)}, bf16[512,2048]{1,0:T(8,128)(2,1)}) conditional(s32[]{:T(128)} %bitcast.2, () %tuple.138, (bf16[256,2048]{1,0:T(8,128)(2,1)S(1)}, bf16[256,2048]{1,0:T(8,128)(2,1)}) %tuple.188), branch_computations={%region_26.27_spmd, %region_27.28_spmd} | conditional | bytes 12582968 | solution.py:895
  567.9 4.5 collective-permute-done.22
  (211 shorter events, 179.4 us)
Async XLA Ops:
  7.2 293.2 %reduce-scatter.4.cloned.1.call-start = ((), (), s32[]{:S(2)}) async-start(), calls=%async_computation.3 | async-start | bytes 5242880 | tf_op jit(solution)/shard_map/reduce_scatter | solution.py:971
  9.2 14.9 %collective-permute-start.27 = (bf16[128,2048]{1,0:T(8,128)(2,1)S(1)}, bf16[128,2048]{1,0:T(8,128)(2,1)S(1)}, u32[]{:S(2)}, u32[]{:S(2)}) collective-permute-start(bf16[128,2048]{1,0:T(8,128)(2,1)S(1)} %get-tuple-element.384), channel_id=1, source_target_pairs={{0,8},{8,0},{1,9},{9,1},{2,10},{10,2},{3,11},{11,3},{4,12},{12,4},... | collective-permute-start | bytes 1572872 | tf_op jit(solution)/shard_map/ppermute | solution.py:859
  24.2 25.5 %collective-permute-start = (bf16[512,512]{1,0:T(8,128)(2,1)S(1)}, bf16[512,512]{1,0:T(8,128)(2,1)}, u32[]{:S(2)}, u32[]{:S(2)}) collective-permute-start(bf16[512,512]{1,0:T(8,128)(2,1)S(1)} %param.1), channel_id=1, source_target_pairs={{0,16},{16,0},{1,17},{17,1},{2,18},{18,2},{3,19},{19,3},{4,20},{20... | collective-permute-start | bytes 1572872 | tf_op jit(solution)/shard_map/cond/branch_1_fun/ppermute | solution.py:859
  26.9 22.9 %collective-permute-start.1 = (bf16[512,512]{1,0:T(8,128)(2,1)S(1)}, bf16[512,512]{1,0:T(8,128)(2,1)}, u32[]{:S(2)}, u32[]{:S(2)}) collective-permute-start(bf16[512,512]{1,0:T(8,128)(2,1)S(1)} %param.1), channel_id=1, source_target_pairs={{0,8},{8,0},{1,9},{9,1},{2,10},{10,2},{3,11},{11,3},{4,12},{12,4},... | collective-permute-start | bytes 1572872 | tf_op jit(solution)/shard_map/cond/branch_1_fun/ppermute | solution.py:859
  28.5 21.3 %collective-permute-start.2 = (bf16[512,512]{1,0:T(8,128)(2,1)S(1)}, bf16[512,512]{1,0:T(8,128)(2,1)}, u32[]{:S(2)}, u32[]{:S(2)}) collective-permute-start(bf16[512,512]{1,0:T(8,128)(2,1)S(1)} %param.1), channel_id=1, source_target_pairs={{0,4},{4,0},{1,5},{5,1},{2,6},{6,2},{3,7},{7,3},{8,12},{12,8},{9,1... | collective-permute-start | bytes 1572872 | tf_op jit(solution)/shard_map/cond/branch_1_fun/ppermute | solution.py:859
  49.8 13.0 %collective-permute-start.5 = (bf16[512,512]{1,0:T(8,128)(2,1)}, bf16[512,512]{1,0:T(8,128)(2,1)}, u32[]{:S(2)}, u32[]{:S(2)}) collective-permute-start(bf16[512,512]{1,0:T(8,128)(2,1)} %get-tuple-element.77), channel_id=1, source_target_pairs={{0,8},{8,0},{1,9},{9,1},{2,10},{10,2},{3,11},{11,3},{4,12},{12,4},... | collective-permute-start | bytes 1572872 | tf_op jit(solution)/shard_map/cond/branch_1_fun/ppermute | solution.py:859
  51.1 15.2 %collective-permute-start.6 = (bf16[512,512]{1,0:T(8,128)(2,1)}, bf16[512,512]{1,0:T(8,128)(2,1)}, u32[]{:S(2)}, u32[]{:S(2)}) collective-permute-start(bf16[512,512]{1,0:T(8,128)(2,1)} %get-tuple-element.77), channel_id=1, source_target_pairs={{0,4},{4,0},{1,5},{5,1},{2,6},{6,2},{3,7},{7,3},{8,12},{12,8},{9,1... | collective-permute-start | bytes 1572872 | tf_op jit(solution)/shard_map/cond/branch_1_fun/ppermute | solution.py:859
  52.6 22.5 %collective-permute-start.3 = (bf16[512,512]{1,0:T(8,128)(2,1)}, bf16[512,512]{1,0:T(8,128)(2,1)}, u32[]{:S(2)}, u32[]{:S(2)}) collective-permute-start(bf16[512,512]{1,0:T(8,128)(2,1)} %get-tuple-element.75), channel_id=1, source_target_pairs={{0,4},{4,0},{1,5},{5,1},{2,6},{6,2},{3,7},{7,3},{8,12},{12,8},{9,1... | collective-permute-start | bytes 1572872 | tf_op jit(solution)/shard_map/cond/branch_1_fun/ppermute | solution.py:859
  53.1 21.9 %collective-permute-start.4 = (bf16[128,2048]{1,0:T(8,128)(2,1)S(1)}, bf16[128,2048]{1,0:T(8,128)(2,1)}, u32[]{:S(2)}, u32[]{:S(2)}) collective-permute-start(bf16[128,2048]{1,0:T(8,128)(2,1)S(1)} %get-tuple-element.76), channel_id=1, source_target_pairs={{0,2},{2,0},{1,3},{3,1},{4,6},{6,4},{5,7},{7,5},{8,10},{10,8},{9,1... | collective-permute-start | bytes 1572872 | tf_op jit(solution)/shard_map/cond/branch_1_fun/ppermute | solution.py:859
  76.3 14.7 %collective-permute-start.25 = (bf16[512,512]{1,0:T(8,128)(2,1)}, bf16[512,512]{1,0:T(8,128)(2,1)}, u32[]{:S(2)}, u32[]{:S(2)}) collective-permute-start(bf16[512,512]{1,0:T(8,128)(2,1)} %get-tuple-element.78), channel_id=1, source_target_pairs={{0,4},{4,0},{1,5},{5,1},{2,6},{6,2},{3,7},{7,3},{8,12},{12,8},{9,1... | collective-permute-start | bytes 1572872 | tf_op jit(solution)/shard_map/cond/branch_1_fun/ppermute | solution.py:859
  108.1 8.1 %collective-permute-start.28 = (bf16[256,2048]{1,0:T(8,128)(2,1)}, bf16[256,2048]{1,0:T(8,128)(2,1)S(1)}, u32[]{:S(2)}, u32[]{:S(2)}) collective-permute-start(bf16[256,2048]{1,0:T(8,128)(2,1)} %get-tuple-element.253), channel_id=1, source_target_pairs={{0,1},{1,0},{2,3},{3,2},{4,5},{5,4},{6,7},{7,6},{8,9},{9,8},{10,11... | collective-permute-start | bytes 3145736 | tf_op jit(solution)/shard_map/ppermute | solution.py:859
  116.7 14.4 %collective-permute-start.29 = (bf16[128,2048]{1,0:T(8,128)(2,1)S(1)}, bf16[128,2048]{1,0:T(8,128)(2,1)S(1)}, u32[]{:S(2)}, u32[]{:S(2)}) collective-permute-start(bf16[128,2048]{1,0:T(8,128)(2,1)S(1)} %slice.223), channel_id=1, source_target_pairs={{0,2},{2,0},{1,3},{3,1},{4,6},{6,4},{5,7},{7,5},{8,10},{10,8},{9,1... | collective-permute-start | bytes 1572872 | tf_op jit(solution)/shard_map/ppermute | solution.py:859
  135.3 15.4 %collective-permute-start.30 = (bf16[128,2048]{1,0:T(8,128)(2,1)S(1)}, bf16[128,2048]{1,0:T(8,128)(2,1)S(1)}, u32[]{:S(2)}, u32[]{:S(2)}) collective-permute-start(bf16[128,2048]{1,0:T(8,128)(2,1)S(1)} %get-tuple-element.381), channel_id=1, source_target_pairs={{0,8},{8,0},{1,9},{9,1},{2,10},{10,2},{3,11},{11,3},{4,12},{12,4},... | collective-permute-start | bytes 1572872 | tf_op jit(solution)/shard_map/ppermute | solution.py:859
  139.0 13.3 %collective-permute-start.31 = (bf16[128,2048]{1,0:T(8,128)(2,1)S(1)}, bf16[128,2048]{1,0:T(8,128)(2,1)S(1)}, u32[]{:S(2)}, u32[]{:S(2)}) collective-permute-start(bf16[128,2048]{1,0:T(8,128)(2,1)S(1)} %get-tuple-element.381), channel_id=1, source_target_pairs={{0,2},{2,0},{1,3},{3,1},{4,6},{6,4},{5,7},{7,5},{8,10},{10,8},{9,1... | collective-permute-start | bytes 1572872 | tf_op jit(solution)/shard_map/ppermute | solution.py:859
  150.8 13.0 %collective-permute-start.32 = (bf16[128,2048]{1,0:T(8,128)(2,1)S(1)}, bf16[128,2048]{1,0:T(8,128)(2,1)S(1)}, u32[]{:S(2)}, u32[]{:S(2)}) collective-permute-start(bf16[128,2048]{1,0:T(8,128)(2,1)S(1)} %collective-permute-done.30), channel_id=1, source_target_pairs={{0,2},{2,0},{1,3},{3,1},{4,6},{6,4},{5,7},{7,5},{8,10},{10,8},{9,1... | collective-permute-start | bytes 1572872 | tf_op jit(solution)/shard_map/ppermute | solution.py:859
  164.0 4.2 collective-permute-start.33
  196.1 237.1 %reduce-scatter.6.cloned.1.call-start = ((), (), s32[]{:S(2)}) async-start(), calls=%async_computation.4 | async-start | bytes 5242880 | tf_op jit(solution)/shard_map/reduce_scatter | solution.py:971
  205.3 9.2 %collective-permute-start.14 = (bf16[512,2048]{1,0:T(8,128)(2,1)}, bf16[512,2048]{1,0:T(8,128)(2,1)}, u32[]{:S(2)}, u32[]{:S(2)}) collective-permute-start(bf16[512,2048]{1,0:T(8,128)(2,1)} %get-tuple-element.85), channel_id=1, source_target_pairs={{0,1},{1,0},{2,3},{3,2},{4,5},{5,4},{6,7},{7,6},{8,9},{9,8},{10,11... | collective-permute-start | bytes 6291464 | tf_op jit(solution)/shard_map/cond/branch_1_fun/ppermute | solution.py:859
  218.0 15.1 %collective-permute-start.15 = (bf16[128,2048]{1,0:T(8,128)(2,1)}, bf16[128,2048]{1,0:T(8,128)(2,1)}, u32[]{:S(2)}, u32[]{:S(2)}) collective-permute-start(bf16[128,2048]{1,0:T(8,128)(2,1)} %get-tuple-element.389), channel_id=1, source_target_pairs={{0,2},{2,0},{1,3},{3,1},{4,6},{6,4},{5,7},{7,5},{8,10},{10,8},{9,1... | collective-permute-start | bytes 1572872 | tf_op jit(solution)/shard_map/cond/branch_1_fun/ppermute | solution.py:859
  219.7 26.3 %collective-permute-start.16 = (bf16[128,2048]{1,0:T(8,128)(2,1)}, bf16[128,2048]{1,0:T(8,128)(2,1)}, u32[]{:S(2)}, u32[]{:S(2)}) collective-permute-start(bf16[128,2048]{1,0:T(8,128)(2,1)} %get-tuple-element.387), channel_id=1, source_target_pairs={{0,2},{2,0},{1,3},{3,1},{4,6},{6,4},{5,7},{7,5},{8,10},{10,8},{9,1... | collective-permute-start | bytes 1572872 | tf_op jit(solution)/shard_map/cond/branch_1_fun/ppermute | solution.py:859
  235.6 25.8 %collective-permute-start.17 = (bf16[128,2048]{1,0:T(8,128)(2,1)}, bf16[128,2048]{1,0:T(8,128)(2,1)}, u32[]{:S(2)}, u32[]{:S(2)}) collective-permute-start(bf16[128,2048]{1,0:T(8,128)(2,1)} %add_convert_fusion.2), channel_id=1, source_target_pairs={{0,8},{8,0},{1,9},{9,1},{2,10},{10,2},{3,11},{11,3},{4,12},{12,4},... | collective-permute-start | bytes 1572872 | tf_op jit(solution)/shard_map/cond/branch_1_fun/ppermute | solution.py:859
  263.9 313.8 %reduce-scatter.8.cloned.1.call-start = ((), (), s32[]{:S(2)}) async-start(), calls=%async_computation.5 | async-start | bytes 5242880 | tf_op jit(solution)/shard_map/reduce_scatter | solution.py:971
  268.5 12.5 %collective-permute-start.23 = (bf16[128,2048]{1,0:T(8,128)(2,1)S(1)}, bf16[128,2048]{1,0:T(8,128)(2,1)}, u32[]{:S(2)}, u32[]{:S(2)}) collective-permute-start(bf16[128,2048]{1,0:T(8,128)(2,1)S(1)} %get-tuple-element.378), channel_id=1, source_target_pairs={{0,2},{2,0},{1,3},{3,1},{4,6},{6,4},{5,7},{7,5},{8,10},{10,8},{9,1... | collective-permute-start | bytes 1572872 | tf_op jit(solution)/shard_map/cond/branch_1_fun/ppermute | solution.py:859
  299.1 43.8 %collective-permute-start.34 = (bf16[2048,256]{1,0:T(8,128)(2,1)}, bf16[2048,256]{1,0:T(8,128)(2,1)}, u32[]{:S(2)}, u32[]{:S(2)}) collective-permute-start(bf16[2048,256]{1,0:T(8,128)(2,1)} %get-tuple-element.276), channel_id=1, source_target_pairs={{0,4},{4,0},{1,5},{5,1},{2,6},{6,2},{3,7},{7,3},{8,12},{12,8},{9,1... | collective-permute-start | bytes 3145736 | tf_op jit(solution)/shard_map/ppermute | solution.py:859
  315.7 60.7 %collective-permute-start.35 = (bf16[2048,256]{1,0:T(8,128)(2,1)}, bf16[2048,256]{1,0:T(8,128)(2,1)}, u32[]{:S(2)}, u32[]{:S(2)}) collective-permute-start(bf16[2048,256]{1,0:T(8,128)(2,1)} %get-tuple-element.280), channel_id=1, source_target_pairs={{0,4},{4,0},{1,5},{5,1},{2,6},{6,2},{3,7},{7,3},{8,12},{12,8},{9,1... | collective-permute-start | bytes 3145736 | tf_op jit(solution)/shard_map/ppermute | solution.py:859
  318.1 62.1 %collective-permute-start.36 = (bf16[256,1024]{1,0:T(8,128)(2,1)}, bf16[256,1024]{1,0:T(8,128)(2,1)}, u32[]{:S(2)}, u32[]{:S(2)}) collective-permute-start(bf16[256,1024]{1,0:T(8,128)(2,1)} %get-tuple-element.426), channel_id=1, source_target_pairs={{0,8},{8,0},{1,9},{9,1},{2,10},{10,2},{3,11},{11,3},{4,12},{12,4},... | collective-permute-start | bytes 1572872 | tf_op jit(solution)/shard_map/ppermute | solution.py:859
  382.5 90.7 %collective-permute-start.39 = (bf16[4,256,1024]{2,1,0:T(8,128)(2,1)}, bf16[4,256,1024]{2,1,0:T(8,128)(2,1)}, u32[]{:S(2)}, u32[]{:S(2)}) collective-permute-start(bf16[4,256,1024]{2,1,0:T(8,128)(2,1)} %get-tuple-element.303), channel_id=1, source_target_pairs={{0,4},{4,0},{1,5},{5,1},{2,6},{6,2},{3,7},{7,3},{8,12},{12,8},{9,1... | collective-permute-start | bytes 6291464 | tf_op jit(solution)/shard_map/ppermute | solution.py:859
  383.0 24.9 %collective-permute-start.38 = (bf16[1024,256]{1,0:T(8,128)(2,1)}, bf16[1024,256]{1,0:T(8,128)(2,1)}, u32[]{:S(2)}, u32[]{:S(2)}) collective-permute-start(bf16[1024,256]{1,0:T(8,128)(2,1)} %get-tuple-element.292), channel_id=1, source_target_pairs={{0,8},{8,0},{1,9},{9,1},{2,10},{10,2},{3,11},{11,3},{4,12},{12,4},... | collective-permute-start | bytes 1572872 | tf_op jit(solution)/shard_map/ppermute | solution.py:859
  384.6 44.3 %collective-permute-start.37 = (bf16[1024,256]{1,0:T(8,128)(2,1)}, bf16[1024,256]{1,0:T(8,128)(2,1)}, u32[]{:S(2)}, u32[]{:S(2)}) collective-permute-start(bf16[1024,256]{1,0:T(8,128)(2,1)} %get-tuple-element.289), channel_id=1, source_target_pairs={{0,8},{8,0},{1,9},{9,1},{2,10},{10,2},{3,11},{11,3},{4,12},{12,4},... | collective-permute-start | bytes 1572872 | tf_op jit(solution)/shard_map/ppermute | solution.py:859
  385.3 4.4 collective-permute-start.18
  390.9 14.0 %collective-permute-start.19 = (bf16[128,2048]{1,0:T(8,128)(2,1)S(1)}, bf16[128,2048]{1,0:T(8,128)(2,1)S(1)}, u32[]{:S(2)}, u32[]{:S(2)}) collective-permute-start(bf16[128,2048]{1,0:T(8,128)(2,1)S(1)} %add_convert_fusion.6), channel_id=1, source_target_pairs={{0,2},{2,0},{1,3},{3,1},{4,6},{6,4},{5,7},{7,5},{8,10},{10,8},{9,1... | collective-permute-start | bytes 1572872 | tf_op jit(solution)/shard_map/cond/branch_1_fun/ppermute | solution.py:859
  435.4 45.2 %collective-permute-start.41 = (bf16[512,256]{1,0:T(8,128)(2,1)}, bf16[512,256]{1,0:T(8,128)(2,1)S(1)}, u32[]{:S(2)}, u32[]{:S(2)}) collective-permute-start(bf16[512,256]{1,0:T(8,128)(2,1)} %get-tuple-element.420), channel_id=1, source_target_pairs={{0,16},{16,0},{1,17},{17,1},{2,18},{18,2},{3,19},{19,3},{4,20},{20... | collective-permute-start | bytes 786440 | tf_op jit(solution)/shard_map/ppermute | solution.py:859
  437.4 43.2 %collective-permute-start.40 = (bf16[512,256]{1,0:T(8,128)(2,1)}, bf16[512,256]{1,0:T(8,128)(2,1)}, u32[]{:S(2)}, u32[]{:S(2)}) collective-permute-start(bf16[512,256]{1,0:T(8,128)(2,1)} %get-tuple-element.422), channel_id=1, source_target_pairs={{0,16},{16,0},{1,17},{17,1},{2,18},{18,2},{3,19},{19,3},{4,20},{20... | collective-permute-start | bytes 786440 | tf_op jit(solution)/shard_map/ppermute | solution.py:859
  438.3 32.4 %collective-permute-start.7 = (bf16[128,2048]{1,0:T(8,128)(2,1)}, bf16[128,2048]{1,0:T(8,128)(2,1)}, u32[]{:S(2)}, u32[]{:S(2)}) collective-permute-start(bf16[128,2048]{1,0:T(8,128)(2,1)} %get-tuple-element.109), channel_id=1, source_target_pairs={{0,8},{8,0},{1,9},{9,1},{2,10},{10,2},{3,11},{11,3},{4,12},{12,4},... | collective-permute-start | bytes 1572872 | tf_op jit(solution)/shard_map/cond/branch_1_fun/ppermute | solution.py:859
  440.8 29.9 %collective-permute-start.8 = (bf16[128,2048]{1,0:T(8,128)(2,1)}, bf16[128,2048]{1,0:T(8,128)(2,1)}, u32[]{:S(2)}, u32[]{:S(2)}) collective-permute-start(bf16[128,2048]{1,0:T(8,128)(2,1)} %get-tuple-element.110), channel_id=1, source_target_pairs={{0,2},{2,0},{1,3},{3,1},{4,6},{6,4},{5,7},{7,5},{8,10},{10,8},{9,1... | collective-permute-start | bytes 1572872 | tf_op jit(solution)/shard_map/cond/branch_1_fun/ppermute | solution.py:859
  470.7 49.2 %collective-permute-start.42 = (bf16[256,1024]{1,0:T(8,128)(2,1)}, bf16[256,1024]{1,0:T(8,128)(2,1)}, u32[]{:S(2)}, u32[]{:S(2)}) collective-permute-start(bf16[256,1024]{1,0:T(8,128)(2,1)} %get-tuple-element.323), channel_id=1, source_target_pairs={{0,8},{8,0},{1,9},{9,1},{2,10},{10,2},{3,11},{11,3},{4,12},{12,4},... | collective-permute-start | bytes 1572872 | tf_op jit(solution)/shard_map/ppermute | solution.py:859
  488.0 34.7 %collective-permute-start.43 = (bf16[2,256,1024]{2,1,0:T(8,128)(2,1)}, bf16[2,256,1024]{2,1,0:T(8,128)(2,1)}, u32[]{:S(2)}, u32[]{:S(2)}) collective-permute-start(bf16[2,256,1024]{2,1,0:T(8,128)(2,1)} %get-tuple-element.393), channel_id=1, source_target_pairs={{0,8},{8,0},{1,9},{9,1},{2,10},{10,2},{3,11},{11,3},{4,12},{12,4},... | collective-permute-start | bytes 3145736 | tf_op jit(solution)/shard_map/ppermute | solution.py:859
  495.7 29.6 %collective-permute-start.44 = (bf16[4,256,512]{2,1,0:T(8,128)(2,1)}, bf16[4,256,512]{2,1,0:T(8,128)(2,1)}, u32[]{:S(2)}, u32[]{:S(2)}) collective-permute-start(bf16[4,256,512]{2,1,0:T(8,128)(2,1)} %get-tuple-element.329), channel_id=1, source_target_pairs={{0,4},{4,0},{1,5},{5,1},{2,6},{6,2},{3,7},{7,3},{8,12},{12,8},{9,1... | collective-permute-start | bytes 3145736 | tf_op jit(solution)/shard_map/ppermute | solution.py:859
  500.9 14.0 %collective-permute-start.21 = (bf16[128,2048]{1,0:T(8,128)(2,1)S(1)}, bf16[128,2048]{1,0:T(8,128)(2,1)S(1)}, u32[]{:S(2)}, u32[]{:S(2)}) collective-permute-start(bf16[128,2048]{1,0:T(8,128)(2,1)S(1)} %add_convert_fusion.11), channel_id=1, source_target_pairs={{0,2},{2,0},{1,3},{3,1},{4,6},{6,4},{5,7},{7,5},{8,10},{10,8},{9,1... | collective-permute-start | bytes 1572872 | tf_op jit(solution)/shard_map/cond/branch_1_fun/ppermute | solution.py:859
  518.3 43.2 %collective-permute-start.46 = (bf16[256,2048]{1,0:T(8,128)(2,1)S(1)}, bf16[256,2048]{1,0:T(8,128)(2,1)}, u32[]{:S(2)}, u32[]{:S(2)}) collective-permute-start(bf16[256,2048]{1,0:T(8,128)(2,1)S(1)} %pad_maximum_fusion.4), channel_id=1, source_target_pairs={{0,2},{2,0},{1,3},{3,1},{4,6},{6,4},{5,7},{7,5},{8,10},{10,8},{9,1... | collective-permute-start | bytes 3145736 | tf_op jit(solution)/shard_map/ppermute | solution.py:859
  527.8 31.8 %collective-permute-start.45 = (bf16[2,256,512]{2,1,0:T(8,128)(2,1)}, bf16[2,256,512]{2,1,0:T(8,128)(2,1)}, u32[]{:S(2)}, u32[]{:S(2)}) collective-permute-start(bf16[2,256,512]{2,1,0:T(8,128)(2,1)} %get-tuple-element.401), channel_id=1, source_target_pairs={{0,8},{8,0},{1,9},{9,1},{2,10},{10,2},{3,11},{11,3},{4,12},{12,4},... | collective-permute-start | bytes 1572872 | tf_op jit(solution)/shard_map/ppermute | solution.py:859
  531.6 55.3 %collective-permute-start.48 = (bf16[1,256,1024]{2,1,0:T(8,128)(2,1)}, bf16[1,256,1024]{2,1,0:T(8,128)(2,1)}, u32[]{:S(2)}, u32[]{:S(2)}) collective-permute-start(bf16[1,256,1024]{2,1,0:T(8,128)(2,1)} %get-tuple-element.395), channel_id=1, source_target_pairs={{0,16},{16,0},{1,17},{17,1},{2,18},{18,2},{3,19},{19,3},{4,20},{20... | collective-permute-start | bytes 1572872 | tf_op jit(solution)/shard_map/ppermute | solution.py:859
  535.2 8.0 %collective-permute-start.10 = (f32[2,2048]{1,0:T(2,128)S(1)}, f32[2,2048]{1,0:T(2,128)S(1)}, u32[]{:S(2)}, u32[]{:S(2)}) collective-permute-start(f32[2,2048]{1,0:T(2,128)S(1)} %add.208), channel_id=1, source_target_pairs={{0,2},{2,0},{1,3},{3,1},{4,6},{6,4},{5,7},{7,5},{8,10},{10,8},{9,1... | collective-permute-start | bytes 49160 | tf_op jit(solution)/shard_map/cond/branch_1_fun/ppermute | solution.py:859
  547.1 5.1 collective-permute-start.12
  552.1 6.8 %collective-permute-start.13 = (f32[2,2048]{1,0:T(2,128)S(1)}, f32[2,2048]{1,0:T(2,128)S(1)}, u32[]{:S(2)}, u32[]{:S(2)}) collective-permute-start(f32[2,2048]{1,0:T(2,128)S(1)} %add.211), channel_id=1, source_target_pairs={{0,16},{16,0},{1,17},{17,1},{2,18},{18,2},{3,19},{19,3},{4,20},{20... | collective-permute-start | bytes 49160 | tf_op jit(solution)/shard_map/cond/branch_1_fun/ppermute | solution.py:859
  561.6 18.4 %collective-permute-start.47 = (bf16[1,256,512]{2,1,0:T(8,128)(2,1)}, bf16[1,256,512]{2,1,0:T(8,128)(2,1)}, u32[]{:S(2)}, u32[]{:S(2)}) collective-permute-start(bf16[1,256,512]{2,1,0:T(8,128)(2,1)} %get-tuple-element.414), channel_id=1, source_target_pairs={{0,16},{16,0},{1,17},{17,1},{2,18},{18,2},{3,19},{19,3},{4,20},{20... | collective-permute-start | bytes 786440 | tf_op jit(solution)/shard_map/ppermute | solution.py:859
  567.9 4.5 collective-permute-start.22
  580.0 14.3 %collective-permute-start.49 = (bf16[256,1024]{1,0:T(8,128)(2,1)}, bf16[256,1024]{1,0:T(8,128)(2,1)}, u32[]{:S(2)}, u32[]{:S(2)}) collective-permute-start(bf16[256,1024]{1,0:T(8,128)(2,1)} %get-tuple-element.349), channel_id=1, source_target_pairs={{0,8},{8,0},{1,9},{9,1},{2,10},{10,2},{3,11},{11,3},{4,12},{12,4},... | collective-permute-start | bytes 1572872 | tf_op jit(solution)/shard_map/ppermute | solution.py:859
  (28 other events, 204.7 us)
Sparse Core Ops, SparseCore 0:
  196.2 90.4 reduce-scatter.3
  290.0 86.1 reduce-scatter.5
  380.3 101.0 reduce-scatter.7

commit v13 on v12

--- a/solution.py
+++ b/solution.py
@@ -21,6 +21,7 @@
 NEG = -1e30
 SLOTS = 4
 VMEM_LIMIT = 60 << 20
+VMEM_SMALL = 28 << 20
 PAIR_STEPS = (4, 1)
 
 eps_norm = 1e-05
@@ -755,7 +756,7 @@
             ],
             out_specs=[keep_spec, send_spec],
         ),
-        compiler_params=pltpu.CompilerParams(vmem_limit_bytes=VMEM_LIMIT),
+        compiler_params=pltpu.CompilerParams(vmem_limit_bytes=VMEM_SMALL),
         cost_estimate=cost(name, 2 * rows * model * width, 4 * rows * model),
         name=name,
     )(where, *lefts, *rights)
@@ -848,7 +849,7 @@
         in_specs=[pl.BlockSpec(memory_space=pltpu.SMEM)]
         + [vmem] * (len(flat) + 2 + kv_heads + 3),
         out_specs=[vmem] * 3,
-        compiler_params=pltpu.CompilerParams(vmem_limit_bytes=VMEM_LIMIT),
+        compiler_params=pltpu.CompilerParams(vmem_limit_bytes=VMEM_SMALL),
         cost_estimate=cost("tail_stage", 2 * rows * model * (wq.shape[1] + 2 * wk.shape[1]), 4 * rows * model + 4 * wq.size
         ),
         name="tail_stage",

time: 610 us -> 605 us (level)
  waiting for transfers between devices: 257 us -> 264 us
  starting transfers between devices: 65.9 us -> 59.3 us
    ppermute x50, waiting for transfers between devices: 257 us -> 263 us  [flip(): lax.ppermute(value, axis, [(i, i ^ mask) for i in range(lax.axis_size(axi...]
    ppermute x50, starting transfers between devices: 65.8 us -> 59.2 us  [flip(): lax.ppermute(value, axis, [(i, i ^ mask) for i in range(lax.axis_size(axi...]
    unnamed x52 -> x90, local copies, waits for them, and re-layouts: 18.7 us -> 18.9 us
where the time goes in v13:
time: 605 us; the launch traced here: 599 us
  waiting for transfers between devices  264 us (44%)
  Pallas kernels  156 us (26%)
  starting transfers between devices  59.3 us (10%)
  other arithmetic  58.6 us (10%)
  local copies, waits for them, and re-layouts  45.4 us (8%)
  between operations  15.4 us (3%)
    ppermute x50, waiting for transfers between devices, flip(): lax.ppermute(value, axis, [(i, i ^ mask) for i in range(lax.axis_size(axi...  263 us
    ppermute x50, starting transfers between devices, flip(): lax.ppermute(value, axis, [(i, i ^ mask) for i in range(lax.axis_size(axi...  59.2 us
    pallas_call x3, Pallas kernels, unit_shares(): pl.pallas_call(unit_shares_kernel, out_shape=shares, grid_spec=pltpu.Pref...  31.5 us
    pallas_call x2, Pallas kernels, attention_backward(): pl.pallas_call(functools.partial(backward_kernel, rep, 1, ctx_count, head...  28.4 us
    convert_element_type x13, other arithmetic, add(): (left.astype(jnp.float32) + right.astype(jnp.float32)).astype(jnp.bfloat16)  28.1 us
    unnamed x90, local copies, waits for them, and re-layouts  18.9 us
    pallas_call x2, Pallas kernels, grad_second_half(): pl.pallas_call(grad_second_kernel, out_shape=jax.ShapeDtypeStruct((rows,...  18.5 us
    pallas_call x1, Pallas kernels, attention_forward(): pl.pallas_call(functools.partial(forward_kernel, rep, kv_heads, ctx_count...  18.5 us
  transfers between devices with their start and end apart: 53, of which 33 were waited for; matrix products, arithmetic and copies ran while one was open for 15% of the time, Pallas kernels for 19%

profile of v13, /device:TPU:0, one launch (start us, length us, event | category | flops | bytes accessed | tf_op | source)
XLA Modules:
  0.0 598.8 jit_solution(6099821931278230347)
XLA Ops:
  9.2 3.0 collective-permute-start.27
  13.0 7.2 %input_stage.1 = (bf16[512,2048]{1,0:T(8,128)(2,1)}, bf16[512,512]{1,0:T(8,128)(2,1)}, bf16[512,512]{1,0:T(8,128)(2,1)S(1)}, f32[512,128]{1,0:T(8,128)}, f32[512,128]{1,0:T(8,128)}) custom-call(s32[32]{0:T(128)} %order_ref.7, s32[8]{0:T(128)} %cont_ref.7, s32[2]{0:T(128)S(1)} %pad_add_fusion.where_ref, f32[1,2048]{1,0:T(1,128)} %bitcast.31, ...), custom_call_target="tpu_custom_call" | custom-call | flops 42949672 | bytes 167772 | tf_op jit(solution)/shard_map/input_stage/pallas_call | solution.py:513
  20.1 4.0 collective-permute-done.27
  24.1 25.6 %conditional.10 = (bf16[512,512]{1,0:T(8,128)(2,1)}, bf16[512,512]{1,0:T(8,128)(2,1)}, bf16[512,512]{1,0:T(8,128)(2,1)}) conditional(s32[]{:T(128)} %bitcast.2, () %tuple.140, bf16[512,512]{1,0:T(8,128)(2,1)S(1)} %get-tuple-element.243.refs_0_), branch_computations={%region_0.0_spmd, %region_1.0_spmd} | conditional | bytes 6291600 | solution.py:896
  30.0 19.6 %collective-permute-done = bf16[512,512]{1,0:T(8,128)(2,1)} collective-permute-done((bf16[512,512]{1,0:T(8,128)(2,1)S(1)}, bf16[512,512]{1,0:T(8,128)(2,1)}, u32[]{:S(2)}, u32[]{:S(2)}) %collective-permute-start) | collective-permute-done | bytes 524320 | tf_op jit(solution)/shard_map/cond/branch_1_fun/ppermute | solution.py:860
  49.8 25.2 %conditional.11 = (bf16[512,512]{1,0:T(8,128)(2,1)}, bf16[128,2048]{1,0:T(8,128)(2,1)}, bf16[512,512]{1,0:T(8,128)(2,1)}, bf16[512,512]{1,0:T(8,128)(2,1)}) conditional(s32[]{:T(128)} %bitcast.2, () %tuple.142, (bf16[512,512]{1,0:T(8,128)(2,1)}, bf16[128,2048]{1,0:T(8,128)(2,1)S(1)}, bf16[512,512]{1,0:T(8,128)(2,1)}) %tuple.143), branch_computations={%region_2.0_spmd, %region_3.0_spmd} | conditional | bytes 8388800 | solution.py:896
  54.6 8.2 %collective-permute-done.5 = bf16[512,512]{1,0:T(8,128)(2,1)} collective-permute-done((bf16[512,512]{1,0:T(8,128)(2,1)}, bf16[512,512]{1,0:T(8,128)(2,1)}, u32[]{:S(2)}, u32[]{:S(2)}) %collective-permute-start.5) | collective-permute-done | bytes 524320 | tf_op jit(solution)/shard_map/cond/branch_1_fun/ppermute | solution.py:860
  62.8 3.4 collective-permute-done.6
  66.3 8.8 %collective-permute-done.3 = bf16[512,512]{1,0:T(8,128)(2,1)} collective-permute-done((bf16[512,512]{1,0:T(8,128)(2,1)}, bf16[512,512]{1,0:T(8,128)(2,1)}, u32[]{:S(2)}, u32[]{:S(2)}) %collective-permute-start.3) | collective-permute-done | bytes 524320 | tf_op jit(solution)/shard_map/cond/branch_1_fun/ppermute | solution.py:860
  76.2 14.9 %conditional.12 = (bf16[512,512]{1,0:T(8,128)(2,1)}, bf16[256,2048]{1,0:T(8,128)(2,1)}, bf16[128,2048]{1,0:T(8,128)(2,1)S(1)}, bf16[128,2048]{1,0:T(8,128)(2,1)S(1)}) conditional(s32[]{:T(128)} %bitcast.2, () %tuple.144, (bf16[512,512]{1,0:T(8,128)(2,1)}, bf16[256,2048]{1,0:T(8,128)(2,1)S(1)}) %tuple.145), branch_computations={%region_4.0_spmd, %region_5.0_spmd} | conditional | bytes 8388720 | solution.py:896
  80.3 10.6 %collective-permute-done.25 = bf16[512,512]{1,0:T(8,128)(2,1)} collective-permute-done((bf16[512,512]{1,0:T(8,128)(2,1)}, bf16[512,512]{1,0:T(8,128)(2,1)}, u32[]{:S(2)}, u32[]{:S(2)}) %collective-permute-start.25) | collective-permute-done | bytes 524320 | tf_op jit(solution)/shard_map/cond/branch_1_fun/ppermute | solution.py:860
  91.1 18.5 %attention_forward.1 = (bf16[512,512]{1,0:T(8,128)(2,1)}, f32[2,4,256]{2,1,0:T(4,128)}, bf16[256,2048]{1,0:T(8,128)(2,1)}, bf16[256,2048]{1,0:T(8,128)(2,1)}) custom-call(s32[32]{0:T(128)} %order_ref.7, s32[8]{0:T(128)} %cont_ref.7, s32[2]{0:T(128)S(1)} %pad_add_fusion.where_ref, bf16[512,512]{1,0:T(8,128)(2,1)} %get-tuple-element.241.q_ref, ...), custom_call_target="tpu_custom_call" | custom-call | flops 64424508 | bytes 167772 | tf_op jit(solution)/shard_map/attention_forward/pallas_call | solution.py:368
  119.7 9.7 %grad_hidden.1.gh_ref = f32[1024,1024]{1,0:T(8,128)} custom-call(s32[2]{0:T(128)S(1)} %pad_add_fusion.where_ref, bf16[1024,2048]{1,0:T(8,128)(2,1)} %constant_dynamic-update-slice_fusion.2.cot_ref.left_ref, bf16[2048,2048]{1,0:T(8,128)(2,1)} %wd_ref.1), custom_call_target="tpu_custom_call" | custom-call | flops 68719476736 | bytes 134217728 | tf_op jit(solution)/shard_map/grad_hidden/pallas_call | solution.py:571
  129.4 3.1 collective-permute-done.29
  139.4 10.8 %collective-permute-done.30 = bf16[128,2048]{1,0:T(8,128)(2,1)S(1)} collective-permute-done((bf16[128,2048]{1,0:T(8,128)(2,1)S(1)}, bf16[128,2048]{1,0:T(8,128)(2,1)S(1)}, u32[]{:S(2)}, u32[]{:S(2)}) %collective-permute-start.30) | collective-permute-done | bytes 524320 | tf_op jit(solution)/shard_map/ppermute | solution.py:860
  151.8 11.1 %collective-permute-done.32 = bf16[128,2048]{1,0:T(8,128)(2,1)S(1)} collective-permute-done((bf16[128,2048]{1,0:T(8,128)(2,1)S(1)}, bf16[128,2048]{1,0:T(8,128)(2,1)S(1)}, u32[]{:S(2)}, u32[]{:S(2)}) %collective-permute-start.32) | collective-permute-done | bytes 524320 | tf_op jit(solution)/shard_map/ppermute | solution.py:860
  168.9 15.6 %ffn_stage.1 = (bf16[1024,1024]{1,0:T(8,128)(2,1)}, bf16[1024,1024]{1,0:T(8,128)(2,1)}, bf16[1024,1024]{1,0:T(8,128)(2,1)S(1)}) custom-call(s32[2]{0:T(128)S(1)} %pad_add_fusion.where_ref, bf16[1024,2048]{1,0:T(8,128)(2,1)} %constant_dynamic-update-slice_fusion.7.in_ref, f32[1024,1024]{1,0:T(8,128)} %grad_hidden.1.gh_ref, bf16[2048,2048]{1,0:T(8,128)(2,1)} %wg_ref.3, ...), custom_call_target="tpu_custom_call" | custom-call | flops 171798688 | bytes 251658 | tf_op jit(solution)/shard_map/ffn_stage/pallas_call | solution.py:610
  184.5 10.7 %down_shares.1 = bf16[8,256,1024]{2,1,0:T(8,128)(2,1)} custom-call(s32[2]{0:T(128)S(1)} %pad_add_fusion.where_ref, bf16[1024,2048]{1,0:T(8,128)(2,1)} %constant_dynamic-update-slice_fusion.2.cot_ref.left_ref, bf16[1024,1024]{1,0:T(8,128)(2,1)} %get-tuple-element.258.right_ref), custom_call_target="tpu_custom_call" | custom-call | flops 85899344 | bytes 167772 | tf_op jit(solution)/shard_map/down_shares/pallas_call | solution.py:790
  195.3 9.0 %grad_second_send.1 = bf16[512,2048]{1,0:T(8,128)(2,1)} custom-call(s32[2]{0:T(128)S(1)} %pad_add_fusion.where_ref, bf16[1024,1024]{1,0:T(8,128)(2,1)} %get-tuple-element.261.gg_ref, bf16[1024,1024]{1,0:T(8,128)(2,1)S(1)} %get-tuple-element.262.gu_ref, bf16[2048,2048]{1,0:T(8,128)(2,1)} %wg_ref.3, bf16[2048,2048]{1,0:T(8,128)(2,1)} %wu_ref.3), custom_call_target="tpu_custom_call" | custom-call | flops 85899344 | bytes 83886 | tf_op jit(solution)/shard_map/grad_second_send/pallas_call | solution.py:642
  204.3 59.5 %conditional.13 = (f32[128,2048]{1,0:T(8,128)}, bf16[8,256,1024]{2,1,0:T(8,128)(2,1)}, bf16[512,2048]{1,0:T(8,128)(2,1)}, bf16[512,2048]{1,0:T(8,128)(2,1)}) conditional(s32[]{:T(128)} %bitcast.2, () %tuple.151, (s32[2]{0:T(128)S(1)}, bf16[1024,1024]{1,0:T(8,128)(2,1)}, bf16[1024,1024]{1,0:T(8,128)(2,1)S(1)}, bf16[2048,2048]{1,0:T(8,128)(2,1)}, ...), branch_computations={%region_7.0_spmd, %region_8.0_spmd} | conditional | flops 264251632 | bytes 24536870 | solution.py:896
  204.7 9.6 %grad_second_keep.1 = bf16[512,2048]{1,0:T(8,128)(2,1)} custom-call(s32[2]{0:T(128)S(1)} %get-tuple-element.80.where_ref, bf16[1024,1024]{1,0:T(8,128)(2,1)} %get-tuple-element.87.gg_ref.right_ref, bf16[1024,1024]{1,0:T(8,128)(2,1)S(1)} %get-tuple-element.82.gu_ref, bf16[2048,2048]{1,0:T(8,128)(2,1)} %get-tuple-element.83.wg_ref, ...), custom_call_target="tpu_custom_call" | custom-call | flops 85899344 | bytes 83886 | tf_op jit(solution)/shard_map/cond/branch_1_fun/grad_second_keep/pallas_call | solution.py:642
  214.2 3.5 add_convert_fusion
  219.8 10.8 %gate_shares.1 = bf16[8,256,1024]{2,1,0:T(8,128)(2,1)} custom-call(s32[2]{0:T(128)S(1)} %get-tuple-element.80.where_ref, bf16[1024,2048]{1,0:T(8,128)(2,1)} %get-tuple-element.86.left_ref, bf16[1024,1024]{1,0:T(8,128)(2,1)} %get-tuple-element.87.gg_ref.right_ref), custom_call_target="tpu_custom_call" | custom-call | flops 85899344 | bytes 167772 | tf_op jit(solution)/shard_map/cond/branch_1_fun/gate_shares/pallas_call | solution.py:790
  236.8 8.6 %ffn_out.1 = (bf16[512,2048]{1,0:T(8,128)(2,1)}, bf16[512,2048]{1,0:T(8,128)(2,1)}) custom-call(s32[2]{0:T(128)S(1)} %get-tuple-element.80.where_ref, bf16[1024,1024]{1,0:T(8,128)(2,1)} %get-tuple-element.90.hid_ref, bf16[2048,2048]{1,0:T(8,128)(2,1)} %get-tuple-element.91.wd_ref), custom_call_target="tpu_custom_call" | custom-call | flops 85899344 | bytes 167772 | tf_op jit(solution)/shard_map/cond/branch_1_fun/ffn_out/pallas_call | solution.py:675
  245.5 15.8 %collective-permute-done.17 = bf16[128,2048]{1,0:T(8,128)(2,1)} collective-permute-done((bf16[128,2048]{1,0:T(8,128)(2,1)}, bf16[128,2048]{1,0:T(8,128)(2,1)}, u32[]{:S(2)}, u32[]{:S(2)}) %collective-permute-start.17) | collective-permute-done | bytes 524320 | tf_op jit(solution)/shard_map/cond/branch_1_fun/ppermute | solution.py:860
  263.9 19.5 %conditional.14 = (f32[128,2048]{1,0:T(8,128)}, bf16[8,256,1024]{2,1,0:T(8,128)(2,1)}, bf16[512,2048]{1,0:T(8,128)(2,1)S(1)}, f32[1,2048]{1,0:T(1,128)S(1)}) conditional(s32[]{:T(128)} %bitcast.2, () %tuple.150, (bf16[128,2048]{1,0:T(8,128)(2,1)}, f32[128]{0:T(128)S(1)}, f32[2048]{0:T(1024)S(1)}, f32[128,2048]{1,0:T(8,128)}, ...), branch_computations={%region_9.0_spmd, %region_10.13_spmd} | conditional | flops 97431632 | bytes 21166568 | solution.py:896
  268.1 10.0 %up_shares.1 = bf16[8,256,1024]{2,1,0:T(8,128)(2,1)} custom-call(s32[2]{0:T(128)S(1)} %get-tuple-element.102.where_ref, bf16[1024,2048]{1,0:T(8,128)(2,1)} %get-tuple-element.103.left_ref, bf16[1024,1024]{1,0:T(8,128)(2,1)S(1)} %get-tuple-element.105.right_ref), custom_call_target="tpu_custom_call" | custom-call | flops 85899344 | bytes 167772 | tf_op jit(solution)/shard_map/cond/branch_1_fun/up_shares/pallas_call | solution.py:790
  283.5 13.9 %attention_backward_0.1 = (bf16[512,256]{1,0:T(8,128)(2,1)}, bf16[2048,256]{1,0:T(8,128)(2,1)}, bf16[2048,256]{1,0:T(8,128)(2,1)}) custom-call(s32[32]{0:T(128)} %order_ref.7, s32[8]{0:T(128)} %cont_ref.7, s32[2]{0:T(128)S(1)} %pad_add_fusion.where_ref, bf16[512,512]{1,0:T(8,128)(2,1)} %get-tuple-element.241.q_ref, ...), custom_call_target="tpu_custom_call" | custom-call | flops 64424508 | bytes 125829 | tf_op jit(solution)/shard_map/attention_backward_0/pallas_call | solution.py:404
  299.8 14.5 %attention_backward_1.1 = (bf16[512,256]{1,0:T(8,128)(2,1)}, bf16[2048,256]{1,0:T(8,128)(2,1)}, bf16[2048,256]{1,0:T(8,128)(2,1)}) custom-call(s32[32]{0:T(128)} %order_ref.7, s32[8]{0:T(128)} %cont_ref.7, s32[2]{0:T(128)S(1)} %pad_add_fusion.where_ref, bf16[512,512]{1,0:T(8,128)(2,1)} %get-tuple-element.241.q_ref, bf16[512,2048]{1,0:T(8,128)(2,1)} %copy-done.11, ...), custom_call_target="tpu_custom_call" | custom-call | flops 64424508 | bytes 125829 | tf_op jit(solution)/shard_map/attention_backward_1/pallas_call | solution.py:404
  317.7 8.5 %branch_shares.1 = (bf16[4,256,1024]{2,1,0:T(8,128)(2,1)S(1)}, bf16[4,256,1024]{2,1,0:T(8,128)(2,1)}) custom-call(s32[2]{0:T(128)S(1)} %pad_add_fusion.where_ref, bf16[512,2048]{1,0:T(8,128)(2,1)S(1)} %copy-done.6, bf16[512,2048]{1,0:T(8,128)(2,1)} %copy-done.11, bf16[512,256]{1,0:T(8,128)(2,1)S(1)} %copy-done.8, bf16[512,256]{1,0:T(8,128)(2,1)S(1)} %copy-done.9, ...), custom_call_target="tpu_custom_call" | custom-call | flops 42949672 | bytes 83886 | tf_op jit(solution)/shard_map/branch_shares/pallas_call | solution.py:746
  326.2 16.6 %collective-permute-done.34 = bf16[2048,256]{1,0:T(8,128)(2,1)} collective-permute-done((bf16[2048,256]{1,0:T(8,128)(2,1)}, bf16[2048,256]{1,0:T(8,128)(2,1)}, u32[]{:S(2)}, u32[]{:S(2)}) %collective-permute-start.34) | collective-permute-done | bytes 1048608 | tf_op jit(solution)/shard_map/ppermute | solution.py:860
  342.8 33.3 %collective-permute-done.35 = bf16[2048,256]{1,0:T(8,128)(2,1)S(1)} collective-permute-done((bf16[2048,256]{1,0:T(8,128)(2,1)}, bf16[2048,256]{1,0:T(8,128)(2,1)S(1)}, u32[]{:S(2)}, u32[]{:S(2)}) %collective-permute-start.35) | collective-permute-done | bytes 1048608 | tf_op jit(solution)/shard_map/ppermute | solution.py:860
  384.8 21.8 %conditional.15 = (bf16[128,2048]{1,0:T(8,128)(2,1)S(1)}, bf16[128,2048]{1,0:T(8,128)(2,1)S(1)}, bf16[128,2048]{1,0:T(8,128)(2,1)S(1)}) conditional(s32[]{:T(128)} %bitcast.2, () %tuple.149, (bf16[512,2048]{1,0:T(8,128)(2,1)}, bf16[512,2048]{1,0:T(8,128)(2,1)}) %tuple.162), branch_computations={%region_14.15_spmd, %region_15.16_spmd} | conditional | flops 5242880 | bytes 17301608 | solution.py:896
  385.2 4.4 collective-permute-done.18
  392.5 12.2 %collective-permute-done.19 = bf16[128,2048]{1,0:T(8,128)(2,1)S(1)} collective-permute-done((bf16[128,2048]{1,0:T(8,128)(2,1)S(1)}, bf16[128,2048]{1,0:T(8,128)(2,1)S(1)}, u32[]{:S(2)}, u32[]{:S(2)}) %collective-permute-start.19) | collective-permute-done | bytes 524320 | tf_op jit(solution)/shard_map/cond/branch_1_fun/ppermute | solution.py:860
  408.3 21.1 %collective-permute-done.37 = bf16[1024,256]{1,0:T(8,128)(2,1)} collective-permute-done((bf16[1024,256]{1,0:T(8,128)(2,1)}, bf16[1024,256]{1,0:T(8,128)(2,1)}, u32[]{:S(2)}, u32[]{:S(2)}) %collective-permute-start.37) | collective-permute-done | bytes 524320 | tf_op jit(solution)/shard_map/ppermute | solution.py:860
  438.6 31.3 %conditional.16 = (bf16[128,2048]{1,0:T(8,128)(2,1)}, bf16[128,2048]{1,0:T(8,128)(2,1)}) conditional(s32[]{:T(128)} %bitcast.2, () %tuple.148, (bf16[128,2048]{1,0:T(8,128)(2,1)S(1)}, bf16[128,2048]{1,0:T(8,128)(2,1)S(1)}) %tuple.260), branch_computations={%region_17.18_spmd, %region_18.19_spmd} | conditional | bytes 4194400 | solution.py:896
  442.5 27.3 %collective-permute-done.7 = bf16[128,2048]{1,0:T(8,128)(2,1)} collective-permute-done((bf16[128,2048]{1,0:T(8,128)(2,1)S(1)}, bf16[128,2048]{1,0:T(8,128)(2,1)}, u32[]{:S(2)}, u32[]{:S(2)}) %collective-permute-start.7) | collective-permute-done | bytes 524320 | tf_op jit(solution)/shard_map/cond/branch_1_fun/ppermute | solution.py:860
  472.4 4.8 add_convert_fusion.13
  481.6 4.2 tail_stage.1
  485.9 5.1 kv_shares.1
  492.2 20.3 %conditional.17 = (bf16[128,2048]{1,0:T(8,128)(2,1)S(1)}, f32[1,2048]{1,0:T(1,128)S(1)}) conditional(s32[]{:T(128)} %bitcast.2, () %tuple.139, (f32[128,2048]{1,0:T(8,128)}, bf16[256,2048]{1,0:T(8,128)(2,1)}, bf16[256,2048]{1,0:T(8,128)(2,1)}, f32[2048]{0:T(1024)S(1)}, f32[128,2048]{1,0:T(8,128)}) %tuple.261), branch_computations={%region_19.20_spmd, %region_20.24_spmd} | conditional | flops 8648832 | bytes 24146584 | solution.py:896
  497.9 12.3 %collective-permute-done.21 = bf16[128,2048]{1,0:T(8,128)(2,1)S(1)} collective-permute-done((bf16[128,2048]{1,0:T(8,128)(2,1)S(1)}, bf16[128,2048]{1,0:T(8,128)(2,1)S(1)}, u32[]{:S(2)}, u32[]{:S(2)}) %collective-permute-start.21) | collective-permute-done | bytes 524320 | tf_op jit(solution)/shard_map/cond/branch_1_fun/ppermute | solution.py:860
  529.3 24.7 %conditional.18 = (f32[2,2048]{1,0:T(2,128)S(1)}) conditional(s32[]{:T(128)} %bitcast.2, () %tuple.178, f32[2,2048]{1,0:T(2,128)S(1)} %pad_maximum_fusion.5), branch_computations={%region_24.25_spmd, %region_25.26_spmd} | conditional | flops 20480 | bytes 573648 | solution.py:896
  531.1 8.6 %collective-permute-done.10 = f32[2,2048]{1,0:T(2,128)S(1)} collective-permute-done((f32[2,2048]{1,0:T(2,128)S(1)}, f32[2,2048]{1,0:T(2,128)S(1)}, u32[]{:S(2)}, u32[]{:S(2)}) %collective-permute-start.10) | collective-permute-done | bytes 16416 | tf_op jit(solution)/shard_map/cond/branch_1_fun/ppermute | solution.py:860
  547.8 4.4 collective-permute-start.13
  558.4 9.1 %conditional.19 = (bf16[512,2048]{1,0:T(8,128)(2,1)}, bf16[512,2048]{1,0:T(8,128)(2,1)}) conditional(s32[]{:T(128)} %bitcast.2, () %tuple.138, (bf16[256,2048]{1,0:T(8,128)(2,1)}, bf16[256,2048]{1,0:T(8,128)(2,1)}) %tuple.188), branch_computations={%region_26.27_spmd, %region_27.28_spmd} | conditional | bytes 12582968 | solution.py:896
  563.0 4.5 collective-permute-done.22
  (249 shorter events, 175.2 us)
Async XLA Ops:
  7.2 290.3 %reduce-scatter.4.cloned.1.call-start = ((), (), s32[]{:S(2)}) async-start(), calls=%async_computation.3 | async-start | bytes 5242880 | tf_op jit(solution)/shard_map/reduce_scatter | solution.py:972
  9.2 14.9 %collective-permute-start.27 = (bf16[128,2048]{1,0:T(8,128)(2,1)S(1)}, bf16[128,2048]{1,0:T(8,128)(2,1)S(1)}, u32[]{:S(2)}, u32[]{:S(2)}) collective-permute-start(bf16[128,2048]{1,0:T(8,128)(2,1)S(1)} %get-tuple-element.384), channel_id=1, source_target_pairs={{0,8},{8,0},{1,9},{9,1},{2,10},{10,2},{3,11},{11,3},{4,12},{12,4},... | collective-permute-start | bytes 1572872 | tf_op jit(solution)/shard_map/ppermute | solution.py:860
  24.1 25.5 %collective-permute-start = (bf16[512,512]{1,0:T(8,128)(2,1)S(1)}, bf16[512,512]{1,0:T(8,128)(2,1)}, u32[]{:S(2)}, u32[]{:S(2)}) collective-permute-start(bf16[512,512]{1,0:T(8,128)(2,1)S(1)} %param.1), channel_id=1, source_target_pairs={{0,16},{16,0},{1,17},{17,1},{2,18},{18,2},{3,19},{19,3},{4,20},{20... | collective-permute-start | bytes 1572872 | tf_op jit(solution)/shard_map/cond/branch_1_fun/ppermute | solution.py:860
  26.9 22.9 %collective-permute-start.1 = (bf16[512,512]{1,0:T(8,128)(2,1)S(1)}, bf16[512,512]{1,0:T(8,128)(2,1)}, u32[]{:S(2)}, u32[]{:S(2)}) collective-permute-start(bf16[512,512]{1,0:T(8,128)(2,1)S(1)} %param.1), channel_id=1, source_target_pairs={{0,8},{8,0},{1,9},{9,1},{2,10},{10,2},{3,11},{11,3},{4,12},{12,4},... | collective-permute-start | bytes 1572872 | tf_op jit(solution)/shard_map/cond/branch_1_fun/ppermute | solution.py:860
  28.5 21.3 %collective-permute-start.2 = (bf16[512,512]{1,0:T(8,128)(2,1)S(1)}, bf16[512,512]{1,0:T(8,128)(2,1)}, u32[]{:S(2)}, u32[]{:S(2)}) collective-permute-start(bf16[512,512]{1,0:T(8,128)(2,1)S(1)} %param.1), channel_id=1, source_target_pairs={{0,4},{4,0},{1,5},{5,1},{2,6},{6,2},{3,7},{7,3},{8,12},{12,8},{9,1... | collective-permute-start | bytes 1572872 | tf_op jit(solution)/shard_map/cond/branch_1_fun/ppermute | solution.py:860
  49.8 13.0 %collective-permute-start.5 = (bf16[512,512]{1,0:T(8,128)(2,1)}, bf16[512,512]{1,0:T(8,128)(2,1)}, u32[]{:S(2)}, u32[]{:S(2)}) collective-permute-start(bf16[512,512]{1,0:T(8,128)(2,1)} %get-tuple-element.77), channel_id=1, source_target_pairs={{0,8},{8,0},{1,9},{9,1},{2,10},{10,2},{3,11},{11,3},{4,12},{12,4},... | collective-permute-start | bytes 1572872 | tf_op jit(solution)/shard_map/cond/branch_1_fun/ppermute | solution.py:860
  51.1 15.2 %collective-permute-start.6 = (bf16[512,512]{1,0:T(8,128)(2,1)}, bf16[512,512]{1,0:T(8,128)(2,1)}, u32[]{:S(2)}, u32[]{:S(2)}) collective-permute-start(bf16[512,512]{1,0:T(8,128)(2,1)} %get-tuple-element.77), channel_id=1, source_target_pairs={{0,4},{4,0},{1,5},{5,1},{2,6},{6,2},{3,7},{7,3},{8,12},{12,8},{9,1... | collective-permute-start | bytes 1572872 | tf_op jit(solution)/shard_map/cond/branch_1_fun/ppermute | solution.py:860
  52.6 22.5 %collective-permute-start.3 = (bf16[512,512]{1,0:T(8,128)(2,1)}, bf16[512,512]{1,0:T(8,128)(2,1)}, u32[]{:S(2)}, u32[]{:S(2)}) collective-permute-start(bf16[512,512]{1,0:T(8,128)(2,1)} %get-tuple-element.75), channel_id=1, source_target_pairs={{0,4},{4,0},{1,5},{5,1},{2,6},{6,2},{3,7},{7,3},{8,12},{12,8},{9,1... | collective-permute-start | bytes 1572872 | tf_op jit(solution)/shard_map/cond/branch_1_fun/ppermute | solution.py:860
  53.1 21.9 %collective-permute-start.4 = (bf16[128,2048]{1,0:T(8,128)(2,1)S(1)}, bf16[128,2048]{1,0:T(8,128)(2,1)}, u32[]{:S(2)}, u32[]{:S(2)}) collective-permute-start(bf16[128,2048]{1,0:T(8,128)(2,1)S(1)} %get-tuple-element.76), channel_id=1, source_target_pairs={{0,2},{2,0},{1,3},{3,1},{4,6},{6,4},{5,7},{7,5},{8,10},{10,8},{9,1... | collective-permute-start | bytes 1572872 | tf_op jit(solution)/shard_map/cond/branch_1_fun/ppermute | solution.py:860
  76.3 14.7 %collective-permute-start.25 = (bf16[512,512]{1,0:T(8,128)(2,1)}, bf16[512,512]{1,0:T(8,128)(2,1)}, u32[]{:S(2)}, u32[]{:S(2)}) collective-permute-start(bf16[512,512]{1,0:T(8,128)(2,1)} %get-tuple-element.78), channel_id=1, source_target_pairs={{0,4},{4,0},{1,5},{5,1},{2,6},{6,2},{3,7},{7,3},{8,12},{12,8},{9,1... | collective-permute-start | bytes 1572872 | tf_op jit(solution)/shard_map/cond/branch_1_fun/ppermute | solution.py:860
  109.6 8.1 %collective-permute-start.28 = (bf16[256,2048]{1,0:T(8,128)(2,1)}, bf16[256,2048]{1,0:T(8,128)(2,1)S(1)}, u32[]{:S(2)}, u32[]{:S(2)}) collective-permute-start(bf16[256,2048]{1,0:T(8,128)(2,1)} %get-tuple-element.253), channel_id=1, source_target_pairs={{0,1},{1,0},{2,3},{3,2},{4,5},{5,4},{6,7},{7,6},{8,9},{9,8},{10,11... | collective-permute-start | bytes 3145736 | tf_op jit(solution)/shard_map/ppermute | solution.py:860
  118.1 14.4 %collective-permute-start.29 = (bf16[128,2048]{1,0:T(8,128)(2,1)S(1)}, bf16[128,2048]{1,0:T(8,128)(2,1)S(1)}, u32[]{:S(2)}, u32[]{:S(2)}) collective-permute-start(bf16[128,2048]{1,0:T(8,128)(2,1)S(1)} %slice.223), channel_id=1, source_target_pairs={{0,2},{2,0},{1,3},{3,1},{4,6},{6,4},{5,7},{7,5},{8,10},{10,8},{9,1... | collective-permute-start | bytes 1572872 | tf_op jit(solution)/shard_map/ppermute | solution.py:860
  136.7 13.5 %collective-permute-start.30 = (bf16[128,2048]{1,0:T(8,128)(2,1)S(1)}, bf16[128,2048]{1,0:T(8,128)(2,1)S(1)}, u32[]{:S(2)}, u32[]{:S(2)}) collective-permute-start(bf16[128,2048]{1,0:T(8,128)(2,1)S(1)} %get-tuple-element.381), channel_id=1, source_target_pairs={{0,8},{8,0},{1,9},{9,1},{2,10},{10,2},{3,11},{11,3},{4,12},{12,4},... | collective-permute-start | bytes 1572872 | tf_op jit(solution)/shard_map/ppermute | solution.py:860
  138.2 13.6 %collective-permute-start.31 = (bf16[128,2048]{1,0:T(8,128)(2,1)S(1)}, bf16[128,2048]{1,0:T(8,128)(2,1)S(1)}, u32[]{:S(2)}, u32[]{:S(2)}) collective-permute-start(bf16[128,2048]{1,0:T(8,128)(2,1)S(1)} %get-tuple-element.381), channel_id=1, source_target_pairs={{0,2},{2,0},{1,3},{3,1},{4,6},{6,4},{5,7},{7,5},{8,10},{10,8},{9,1... | collective-permute-start | bytes 1572872 | tf_op jit(solution)/shard_map/ppermute | solution.py:860
  150.3 12.7 %collective-permute-start.32 = (bf16[128,2048]{1,0:T(8,128)(2,1)S(1)}, bf16[128,2048]{1,0:T(8,128)(2,1)S(1)}, u32[]{:S(2)}, u32[]{:S(2)}) collective-permute-start(bf16[128,2048]{1,0:T(8,128)(2,1)S(1)} %collective-permute-done.30), channel_id=1, source_target_pairs={{0,2},{2,0},{1,3},{3,1},{4,6},{6,4},{5,7},{7,5},{8,10},{10,8},{9,1... | collective-permute-start | bytes 1572872 | tf_op jit(solution)/shard_map/ppermute | solution.py:860
  163.2 4.2 collective-permute-start.33
  195.3 238.0 %reduce-scatter.6.cloned.1.call-start = ((), (), s32[]{:S(2)}) async-start(), calls=%async_computation.4 | async-start | bytes 5242880 | tf_op jit(solution)/shard_map/reduce_scatter | solution.py:972
  204.5 9.8 %collective-permute-start.14 = (bf16[512,2048]{1,0:T(8,128)(2,1)}, bf16[512,2048]{1,0:T(8,128)(2,1)}, u32[]{:S(2)}, u32[]{:S(2)}) collective-permute-start(bf16[512,2048]{1,0:T(8,128)(2,1)} %get-tuple-element.85), channel_id=1, source_target_pairs={{0,1},{1,0},{2,3},{3,2},{4,5},{5,4},{6,7},{7,6},{8,9},{9,8},{10,11... | collective-permute-start | bytes 6291464 | tf_op jit(solution)/shard_map/cond/branch_1_fun/ppermute | solution.py:860
  217.8 15.1 %collective-permute-start.15 = (bf16[128,2048]{1,0:T(8,128)(2,1)}, bf16[128,2048]{1,0:T(8,128)(2,1)}, u32[]{:S(2)}, u32[]{:S(2)}) collective-permute-start(bf16[128,2048]{1,0:T(8,128)(2,1)} %get-tuple-element.389), channel_id=1, source_target_pairs={{0,2},{2,0},{1,3},{3,1},{4,6},{6,4},{5,7},{7,5},{8,10},{10,8},{9,1... | collective-permute-start | bytes 1572872 | tf_op jit(solution)/shard_map/cond/branch_1_fun/ppermute | solution.py:860
  219.4 26.1 %collective-permute-start.16 = (bf16[128,2048]{1,0:T(8,128)(2,1)}, bf16[128,2048]{1,0:T(8,128)(2,1)}, u32[]{:S(2)}, u32[]{:S(2)}) collective-permute-start(bf16[128,2048]{1,0:T(8,128)(2,1)} %get-tuple-element.387), channel_id=1, source_target_pairs={{0,2},{2,0},{1,3},{3,1},{4,6},{6,4},{5,7},{7,5},{8,10},{10,8},{9,1... | collective-permute-start | bytes 1572872 | tf_op jit(solution)/shard_map/cond/branch_1_fun/ppermute | solution.py:860
  235.4 25.9 %collective-permute-start.17 = (bf16[128,2048]{1,0:T(8,128)(2,1)}, bf16[128,2048]{1,0:T(8,128)(2,1)}, u32[]{:S(2)}, u32[]{:S(2)}) collective-permute-start(bf16[128,2048]{1,0:T(8,128)(2,1)} %add_convert_fusion.2), channel_id=1, source_target_pairs={{0,8},{8,0},{1,9},{9,1},{2,10},{10,2},{3,11},{11,3},{4,12},{12,4},... | collective-permute-start | bytes 1572872 | tf_op jit(solution)/shard_map/cond/branch_1_fun/ppermute | solution.py:860
  263.8 309.0 %reduce-scatter.8.cloned.1.call-start = ((), (), s32[]{:S(2)}) async-start(), calls=%async_computation.5 | async-start | bytes 5242880 | tf_op jit(solution)/shard_map/reduce_scatter | solution.py:972
  268.0 12.5 %collective-permute-start.23 = (bf16[128,2048]{1,0:T(8,128)(2,1)S(1)}, bf16[128,2048]{1,0:T(8,128)(2,1)S(1)}, u32[]{:S(2)}, u32[]{:S(2)}) collective-permute-start(bf16[128,2048]{1,0:T(8,128)(2,1)S(1)} %get-tuple-element.378), channel_id=1, source_target_pairs={{0,2},{2,0},{1,3},{3,1},{4,6},{6,4},{5,7},{7,5},{8,10},{10,8},{9,1... | collective-permute-start | bytes 1572872 | tf_op jit(solution)/shard_map/cond/branch_1_fun/ppermute | solution.py:860
  297.4 45.3 %collective-permute-start.34 = (bf16[2048,256]{1,0:T(8,128)(2,1)}, bf16[2048,256]{1,0:T(8,128)(2,1)}, u32[]{:S(2)}, u32[]{:S(2)}) collective-permute-start(bf16[2048,256]{1,0:T(8,128)(2,1)} %get-tuple-element.276), channel_id=1, source_target_pairs={{0,4},{4,0},{1,5},{5,1},{2,6},{6,2},{3,7},{7,3},{8,12},{12,8},{9,1... | collective-permute-start | bytes 3145736 | tf_op jit(solution)/shard_map/ppermute | solution.py:860
  314.3 61.8 %collective-permute-start.35 = (bf16[2048,256]{1,0:T(8,128)(2,1)}, bf16[2048,256]{1,0:T(8,128)(2,1)S(1)}, u32[]{:S(2)}, u32[]{:S(2)}) collective-permute-start(bf16[2048,256]{1,0:T(8,128)(2,1)} %get-tuple-element.280), channel_id=1, source_target_pairs={{0,4},{4,0},{1,5},{5,1},{2,6},{6,2},{3,7},{7,3},{8,12},{12,8},{9,1... | collective-permute-start | bytes 3145736 | tf_op jit(solution)/shard_map/ppermute | solution.py:860
  315.2 63.6 %collective-permute-start.36 = (bf16[256,1024]{1,0:T(8,128)(2,1)}, bf16[256,1024]{1,0:T(8,128)(2,1)}, u32[]{:S(2)}, u32[]{:S(2)}) collective-permute-start(bf16[256,1024]{1,0:T(8,128)(2,1)} %get-tuple-element.426), channel_id=1, source_target_pairs={{0,8},{8,0},{1,9},{9,1},{2,10},{10,2},{3,11},{11,3},{4,12},{12,4},... | collective-permute-start | bytes 1572872 | tf_op jit(solution)/shard_map/ppermute | solution.py:860
  382.5 90.0 %collective-permute-start.39 = (bf16[4,256,1024]{2,1,0:T(8,128)(2,1)}, bf16[4,256,1024]{2,1,0:T(8,128)(2,1)}, u32[]{:S(2)}, u32[]{:S(2)}) collective-permute-start(bf16[4,256,1024]{2,1,0:T(8,128)(2,1)} %get-tuple-element.303), channel_id=1, source_target_pairs={{0,4},{4,0},{1,5},{5,1},{2,6},{6,2},{3,7},{7,3},{8,12},{12,8},{9,1... | collective-permute-start | bytes 6291464 | tf_op jit(solution)/shard_map/ppermute | solution.py:860
  382.8 25.5 %collective-permute-start.38 = (bf16[1024,256]{1,0:T(8,128)(2,1)}, bf16[1024,256]{1,0:T(8,128)(2,1)}, u32[]{:S(2)}, u32[]{:S(2)}) collective-permute-start(bf16[1024,256]{1,0:T(8,128)(2,1)} %get-tuple-element.292), channel_id=1, source_target_pairs={{0,8},{8,0},{1,9},{9,1},{2,10},{10,2},{3,11},{11,3},{4,12},{12,4},... | collective-permute-start | bytes 1572872 | tf_op jit(solution)/shard_map/ppermute | solution.py:860
  384.5 44.9 %collective-permute-start.37 = (bf16[1024,256]{1,0:T(8,128)(2,1)}, bf16[1024,256]{1,0:T(8,128)(2,1)}, u32[]{:S(2)}, u32[]{:S(2)}) collective-permute-start(bf16[1024,256]{1,0:T(8,128)(2,1)} %get-tuple-element.289), channel_id=1, source_target_pairs={{0,8},{8,0},{1,9},{9,1},{2,10},{10,2},{3,11},{11,3},{4,12},{12,4},... | collective-permute-start | bytes 1572872 | tf_op jit(solution)/shard_map/ppermute | solution.py:860
  385.1 4.4 collective-permute-start.18
  390.7 14.0 %collective-permute-start.19 = (bf16[128,2048]{1,0:T(8,128)(2,1)S(1)}, bf16[128,2048]{1,0:T(8,128)(2,1)S(1)}, u32[]{:S(2)}, u32[]{:S(2)}) collective-permute-start(bf16[128,2048]{1,0:T(8,128)(2,1)S(1)} %add_convert_fusion.6), channel_id=1, source_target_pairs={{0,2},{2,0},{1,3},{3,1},{4,6},{6,4},{5,7},{7,5},{8,10},{10,8},{9,1... | collective-permute-start | bytes 1572872 | tf_op jit(solution)/shard_map/cond/branch_1_fun/ppermute | solution.py:860
  435.6 44.5 %collective-permute-start.41 = (bf16[512,256]{1,0:T(8,128)(2,1)}, bf16[512,256]{1,0:T(8,128)(2,1)S(1)}, u32[]{:S(2)}, u32[]{:S(2)}) collective-permute-start(bf16[512,256]{1,0:T(8,128)(2,1)} %get-tuple-element.420), channel_id=1, source_target_pairs={{0,16},{16,0},{1,17},{17,1},{2,18},{18,2},{3,19},{19,3},{4,20},{20... | collective-permute-start | bytes 786440 | tf_op jit(solution)/shard_map/ppermute | solution.py:860
  438.4 43.2 %collective-permute-start.40 = (bf16[512,256]{1,0:T(8,128)(2,1)}, bf16[512,256]{1,0:T(8,128)(2,1)S(1)}, u32[]{:S(2)}, u32[]{:S(2)}) collective-permute-start(bf16[512,256]{1,0:T(8,128)(2,1)} %get-tuple-element.422), channel_id=1, source_target_pairs={{0,16},{16,0},{1,17},{17,1},{2,18},{18,2},{3,19},{19,3},{4,20},{20... | collective-permute-start | bytes 786440 | tf_op jit(solution)/shard_map/ppermute | solution.py:860
  438.6 31.3 %collective-permute-start.7 = (bf16[128,2048]{1,0:T(8,128)(2,1)S(1)}, bf16[128,2048]{1,0:T(8,128)(2,1)}, u32[]{:S(2)}, u32[]{:S(2)}) collective-permute-start(bf16[128,2048]{1,0:T(8,128)(2,1)S(1)} %get-tuple-element.109), channel_id=1, source_target_pairs={{0,8},{8,0},{1,9},{9,1},{2,10},{10,2},{3,11},{11,3},{4,12},{12,4},... | collective-permute-start | bytes 1572872 | tf_op jit(solution)/shard_map/cond/branch_1_fun/ppermute | solution.py:860
  441.0 28.8 %collective-permute-start.8 = (bf16[128,2048]{1,0:T(8,128)(2,1)S(1)}, bf16[128,2048]{1,0:T(8,128)(2,1)}, u32[]{:S(2)}, u32[]{:S(2)}) collective-permute-start(bf16[128,2048]{1,0:T(8,128)(2,1)S(1)} %get-tuple-element.110), channel_id=1, source_target_pairs={{0,2},{2,0},{1,3},{3,1},{4,6},{6,4},{5,7},{7,5},{8,10},{10,8},{9,1... | collective-permute-start | bytes 1572872 | tf_op jit(solution)/shard_map/cond/branch_1_fun/ppermute | solution.py:860
  469.8 46.3 %collective-permute-start.42 = (bf16[256,1024]{1,0:T(8,128)(2,1)}, bf16[256,1024]{1,0:T(8,128)(2,1)}, u32[]{:S(2)}, u32[]{:S(2)}) collective-permute-start(bf16[256,1024]{1,0:T(8,128)(2,1)} %get-tuple-element.323), channel_id=1, source_target_pairs={{0,8},{8,0},{1,9},{9,1},{2,10},{10,2},{3,11},{11,3},{4,12},{12,4},... | collective-permute-start | bytes 1572872 | tf_op jit(solution)/shard_map/ppermute | solution.py:860
  485.8 33.0 %collective-permute-start.43 = (bf16[2,256,1024]{2,1,0:T(8,128)(2,1)}, bf16[2,256,1024]{2,1,0:T(8,128)(2,1)}, u32[]{:S(2)}, u32[]{:S(2)}) collective-permute-start(bf16[2,256,1024]{2,1,0:T(8,128)(2,1)} %get-tuple-element.393), channel_id=1, source_target_pairs={{0,8},{8,0},{1,9},{9,1},{2,10},{10,2},{3,11},{11,3},{4,12},{12,4},... | collective-permute-start | bytes 3145736 | tf_op jit(solution)/shard_map/ppermute | solution.py:860
  490.9 30.5 %collective-permute-start.44 = (bf16[4,256,512]{2,1,0:T(8,128)(2,1)}, bf16[4,256,512]{2,1,0:T(8,128)(2,1)}, u32[]{:S(2)}, u32[]{:S(2)}) collective-permute-start(bf16[4,256,512]{2,1,0:T(8,128)(2,1)} %get-tuple-element.329), channel_id=1, source_target_pairs={{0,4},{4,0},{1,5},{5,1},{2,6},{6,2},{3,7},{7,3},{8,12},{12,8},{9,1... | collective-permute-start | bytes 3145736 | tf_op jit(solution)/shard_map/ppermute | solution.py:860
  496.2 14.0 %collective-permute-start.21 = (bf16[128,2048]{1,0:T(8,128)(2,1)S(1)}, bf16[128,2048]{1,0:T(8,128)(2,1)S(1)}, u32[]{:S(2)}, u32[]{:S(2)}) collective-permute-start(bf16[128,2048]{1,0:T(8,128)(2,1)S(1)} %add_convert_fusion.11), channel_id=1, source_target_pairs={{0,2},{2,0},{1,3},{3,1},{4,6},{6,4},{5,7},{7,5},{8,10},{10,8},{9,1... | collective-permute-start | bytes 1572872 | tf_op jit(solution)/shard_map/cond/branch_1_fun/ppermute | solution.py:860
  514.6 40.8 %collective-permute-start.46 = (bf16[256,2048]{1,0:T(8,128)(2,1)}, bf16[256,2048]{1,0:T(8,128)(2,1)}, u32[]{:S(2)}, u32[]{:S(2)}) collective-permute-start(bf16[256,2048]{1,0:T(8,128)(2,1)} %pad_maximum_fusion.4), channel_id=1, source_target_pairs={{0,2},{2,0},{1,3},{3,1},{4,6},{6,4},{5,7},{7,5},{8,10},{10,8},{9,1... | collective-permute-start | bytes 3145736 | tf_op jit(solution)/shard_map/ppermute | solution.py:860
  524.0 30.6 %collective-permute-start.45 = (bf16[2,256,512]{2,1,0:T(8,128)(2,1)}, bf16[2,256,512]{2,1,0:T(8,128)(2,1)S(1)}, u32[]{:S(2)}, u32[]{:S(2)}) collective-permute-start(bf16[2,256,512]{2,1,0:T(8,128)(2,1)} %get-tuple-element.401), channel_id=1, source_target_pairs={{0,8},{8,0},{1,9},{9,1},{2,10},{10,2},{3,11},{11,3},{4,12},{12,4},... | collective-permute-start | bytes 1572872 | tf_op jit(solution)/shard_map/ppermute | solution.py:860
  527.3 53.8 %collective-permute-start.48 = (bf16[1,256,1024]{2,1,0:T(8,128)(2,1)}, bf16[1,256,1024]{2,1,0:T(8,128)(2,1)}, u32[]{:S(2)}, u32[]{:S(2)}) collective-permute-start(bf16[1,256,1024]{2,1,0:T(8,128)(2,1)} %get-tuple-element.395), channel_id=1, source_target_pairs={{0,16},{16,0},{1,17},{17,1},{2,18},{18,2},{3,19},{19,3},{4,20},{20... | collective-permute-start | bytes 1572872 | tf_op jit(solution)/shard_map/ppermute | solution.py:860
  530.5 9.2 %collective-permute-start.10 = (f32[2,2048]{1,0:T(2,128)S(1)}, f32[2,2048]{1,0:T(2,128)S(1)}, u32[]{:S(2)}, u32[]{:S(2)}) collective-permute-start(f32[2,2048]{1,0:T(2,128)S(1)} %add.208), channel_id=1, source_target_pairs={{0,2},{2,0},{1,3},{3,1},{4,6},{6,4},{5,7},{7,5},{8,10},{10,8},{9,1... | collective-permute-start | bytes 49160 | tf_op jit(solution)/shard_map/cond/branch_1_fun/ppermute | solution.py:860
  543.5 4.3 collective-permute-start.12
  547.8 6.2 %collective-permute-start.13 = (f32[2,2048]{1,0:T(2,128)S(1)}, f32[2,2048]{1,0:T(2,128)S(1)}, u32[]{:S(2)}, u32[]{:S(2)}) collective-permute-start(f32[2,2048]{1,0:T(2,128)S(1)} %add.211), channel_id=1, source_target_pairs={{0,16},{16,0},{1,17},{17,1},{2,18},{18,2},{3,19},{19,3},{4,20},{20... | collective-permute-start | bytes 49160 | tf_op jit(solution)/shard_map/cond/branch_1_fun/ppermute | solution.py:860
  555.4 19.4 %collective-permute-start.47 = (bf16[1,256,512]{2,1,0:T(8,128)(2,1)}, bf16[1,256,512]{2,1,0:T(8,128)(2,1)}, u32[]{:S(2)}, u32[]{:S(2)}) collective-permute-start(bf16[1,256,512]{2,1,0:T(8,128)(2,1)} %get-tuple-element.414), channel_id=1, source_target_pairs={{0,16},{16,0},{1,17},{17,1},{2,18},{18,2},{3,19},{19,3},{4,20},{20... | collective-permute-start | bytes 786440 | tf_op jit(solution)/shard_map/ppermute | solution.py:860
  563.0 4.5 collective-permute-start.22
  574.9 14.3 %collective-permute-start.49 = (bf16[256,1024]{1,0:T(8,128)(2,1)}, bf16[256,1024]{1,0:T(8,128)(2,1)}, u32[]{:S(2)}, u32[]{:S(2)}) collective-permute-start(bf16[256,1024]{1,0:T(8,128)(2,1)} %get-tuple-element.349), channel_id=1, source_target_pairs={{0,8},{8,0},{1,9},{9,1},{2,10},{10,2},{3,11},{11,3},{4,12},{12,4},... | collective-permute-start | bytes 1572872 | tf_op jit(solution)/shard_map/ppermute | solution.py:860
  (47 other events, 567.3 us)
Sparse Core Ops, SparseCore 0:
  195.4 91.1 reduce-scatter.3
  289.9 86.1 reduce-scatter.5
  379.0 103.9 reduce-scatter.7

commit v14 on v13

--- a/solution.py
+++ b/solution.py
@@ -382,7 +382,7 @@
             pltpu.VMEM((kv_heads, HEAD_SIZE, rep * BLOCK), jnp.float32),
             pltpu.SemaphoreType.DMA((ctx_count,)),
         ],
-        compiler_params=pltpu.CompilerParams(vmem_limit_bytes=VMEM_LIMIT),
+        compiler_params=pltpu.CompilerParams(vmem_limit_bytes=VMEM_SMALL),
         cost_estimate=cost("attention_forward", flops, 2 * tokens * parts[0].shape[1] + 4 * rows * model),
         name="attention_forward",
     )(order, cont, where, q, w_out, *parts)
@@ -648,7 +648,7 @@
             in_specs=[left_spec] * 2 + [right_spec] * 2,
             out_specs=pl.BlockSpec((rows, block), lambda n, w: (0, n)),
         ),
-        compiler_params=pltpu.CompilerParams(vmem_limit_bytes=VMEM_LIMIT),
+        compiler_params=pltpu.CompilerParams(vmem_limit_bytes=VMEM_SMALL),
         cost_estimate=cost(name, 4 * rows * units * model, 4 * rows * model),
         name=name,
     )(where, *grads, *weights)
@@ -799,7 +799,7 @@
             ],
             out_specs=out_spec,
         ),
-        compiler_params=pltpu.CompilerParams(vmem_limit_bytes=VMEM_LIMIT),
+        compiler_params=pltpu.CompilerParams(vmem_limit_bytes=VMEM_SMALL),
         cost_estimate=cost(name, 2 * rows * model * width, 4 * rows * model),
         name=name,
     )(where, left, right)

time: 605 us -> 599 us (0.990)
    unnamed x90 -> x122, local copies, waits for them, and re-layouts: 18.9 us -> 19 us
  transfers between devices with their start and end apart: 53 -> 53, of which waited for: 33 -> 35; matrix products, arithmetic and copies ran while one was open for 15% -> 13% of each run, Pallas kernels for 19% -> 19%
where the time goes in v14:
time: 599 us; the launch traced here: 593 us
  waiting for transfers between devices  267 us (45%)
  Pallas kernels  154 us (26%)
  starting transfers between devices  56 us (9%)
  other arithmetic  55.1 us (9%)
  local copies, waits for them, and re-layouts  44.7 us (7%)
  between operations  15.7 us (3%)
    ppermute x50, waiting for transfers between devices, flip(): lax.ppermute(value, axis, [(i, i ^ mask) for i in range(lax.axis_size(axi...  267 us
    ppermute x50, starting transfers between devices, flip(): lax.ppermute(value, axis, [(i, i ^ mask) for i in range(lax.axis_size(axi...  55.9 us
    pallas_call x2, Pallas kernels, attention_backward(): pl.pallas_call(functools.partial(backward_kernel, rep, 1, ctx_count, head...  31.6 us
    pallas_call x3, Pallas kernels, unit_shares(): pl.pallas_call(unit_shares_kernel, out_shape=shares, grid_spec=pltpu.Pref...  28.5 us
    convert_element_type x13, other arithmetic, add(): (left.astype(jnp.float32) + right.astype(jnp.float32)).astype(jnp.bfloat16)  24.6 us
    pallas_call x1, Pallas kernels, attention_forward(): pl.pallas_call(functools.partial(forward_kernel, rep, kv_heads, ctx_count...  19.1 us
    unnamed x122, local copies, waits for them, and re-layouts  19 us
    pallas_call x2, Pallas kernels, grad_second_half(): pl.pallas_call(grad_second_kernel, out_shape=jax.ShapeDtypeStruct((rows,...  16 us
  transfers between devices with their start and end apart: 53, of which 35 were waited for; matrix products, arithmetic and copies ran while one was open for 13% of the time, Pallas kernels for 19%

profile of v14, /device:TPU:0, one launch (start us, length us, event | category | flops | bytes accessed | tf_op | source)
XLA Modules:
  0.0 593.3 jit_solution(11567889667465426750)
XLA Ops:
  9.2 3.0 collective-permute-start.27
  13.0 7.2 %input_stage.1 = (bf16[512,2048]{1,0:T(8,128)(2,1)}, bf16[512,512]{1,0:T(8,128)(2,1)}, bf16[512,512]{1,0:T(8,128)(2,1)S(1)}, f32[512,128]{1,0:T(8,128)}, f32[512,128]{1,0:T(8,128)}) custom-call(s32[32]{0:T(128)} %order_ref.7, s32[8]{0:T(128)} %cont_ref.7, s32[2]{0:T(128)S(1)} %pad_add_fusion.where_ref, f32[1,2048]{1,0:T(1,128)} %bitcast.32, ...), custom_call_target="tpu_custom_call" | custom-call | flops 42949672 | bytes 167772 | tf_op jit(solution)/shard_map/input_stage/pallas_call | solution.py:513
  20.2 4.0 collective-permute-done.27
  24.2 25.6 %conditional.10 = (bf16[512,512]{1,0:T(8,128)(2,1)}, bf16[512,512]{1,0:T(8,128)(2,1)}, bf16[512,512]{1,0:T(8,128)(2,1)}) conditional(s32[]{:T(128)} %bitcast.2, () %tuple.140, bf16[512,512]{1,0:T(8,128)(2,1)S(1)} %get-tuple-element.243.refs_0_), branch_computations={%region_0.0_spmd, %region_1.0_spmd} | conditional | bytes 6291600 | solution.py:896
  30.0 19.6 %collective-permute-done = bf16[512,512]{1,0:T(8,128)(2,1)} collective-permute-done((bf16[512,512]{1,0:T(8,128)(2,1)S(1)}, bf16[512,512]{1,0:T(8,128)(2,1)}, u32[]{:S(2)}, u32[]{:S(2)}) %collective-permute-start) | collective-permute-done | bytes 524320 | tf_op jit(solution)/shard_map/cond/branch_1_fun/ppermute | solution.py:860
  49.8 25.2 %conditional.11 = (bf16[512,512]{1,0:T(8,128)(2,1)}, bf16[128,2048]{1,0:T(8,128)(2,1)}, bf16[512,512]{1,0:T(8,128)(2,1)}, bf16[512,512]{1,0:T(8,128)(2,1)}) conditional(s32[]{:T(128)} %bitcast.2, () %tuple.142, (bf16[512,512]{1,0:T(8,128)(2,1)}, bf16[128,2048]{1,0:T(8,128)(2,1)S(1)}, bf16[512,512]{1,0:T(8,128)(2,1)}) %tuple.143), branch_computations={%region_2.0_spmd, %region_3.0_spmd} | conditional | bytes 8388800 | solution.py:896
  54.6 8.2 %collective-permute-done.5 = bf16[512,512]{1,0:T(8,128)(2,1)} collective-permute-done((bf16[512,512]{1,0:T(8,128)(2,1)}, bf16[512,512]{1,0:T(8,128)(2,1)}, u32[]{:S(2)}, u32[]{:S(2)}) %collective-permute-start.5) | collective-permute-done | bytes 524320 | tf_op jit(solution)/shard_map/cond/branch_1_fun/ppermute | solution.py:860
  62.9 3.4 collective-permute-done.6
  66.3 8.8 %collective-permute-done.3 = bf16[512,512]{1,0:T(8,128)(2,1)} collective-permute-done((bf16[512,512]{1,0:T(8,128)(2,1)}, bf16[512,512]{1,0:T(8,128)(2,1)}, u32[]{:S(2)}, u32[]{:S(2)}) %collective-permute-start.3) | collective-permute-done | bytes 524320 | tf_op jit(solution)/shard_map/cond/branch_1_fun/ppermute | solution.py:860
  76.3 14.9 %conditional.12 = (bf16[512,512]{1,0:T(8,128)(2,1)}, bf16[256,2048]{1,0:T(8,128)(2,1)}, bf16[128,2048]{1,0:T(8,128)(2,1)S(1)}, bf16[128,2048]{1,0:T(8,128)(2,1)S(1)}) conditional(s32[]{:T(128)} %bitcast.2, () %tuple.144, (bf16[512,512]{1,0:T(8,128)(2,1)}, bf16[256,2048]{1,0:T(8,128)(2,1)S(1)}) %tuple.145), branch_computations={%region_4.0_spmd, %region_5.0_spmd} | conditional | bytes 8388720 | solution.py:896
  80.4 10.6 %collective-permute-done.25 = bf16[512,512]{1,0:T(8,128)(2,1)} collective-permute-done((bf16[512,512]{1,0:T(8,128)(2,1)}, bf16[512,512]{1,0:T(8,128)(2,1)}, u32[]{:S(2)}, u32[]{:S(2)}) %collective-permute-start.25) | collective-permute-done | bytes 524320 | tf_op jit(solution)/shard_map/cond/branch_1_fun/ppermute | solution.py:860
  92.2 19.1 %attention_forward.1 = (bf16[512,512]{1,0:T(8,128)(2,1)S(1)}, f32[2,4,256]{2,1,0:T(4,128)S(1)}, bf16[256,2048]{1,0:T(8,128)(2,1)S(1)}, bf16[256,2048]{1,0:T(8,128)(2,1)S(1)}) custom-call(s32[32]{0:T(128)S(1)} %copy-done.19, s32[8]{0:T(128)S(1)} %copy-done.20, s32[2]{0:T(128)S(1)} %pad_add_fusion.where_ref, bf16[512,512]{1,0:T(8,128)(2,1)S(1)} %copy-done.6, ...), custom_call_target="tpu_custom_call" | custom-call | flops 64424508 | bytes 167772 | tf_op jit(solution)/shard_map/attention_forward/pallas_call | solution.py:368
  116.5 9.7 %grad_hidden.1.gh_ref = f32[1024,1024]{1,0:T(8,128)} custom-call(s32[2]{0:T(128)S(1)} %pad_add_fusion.where_ref, bf16[1024,2048]{1,0:T(8,128)(2,1)} %copy-done.4, bf16[2048,2048]{1,0:T(8,128)(2,1)} %wd_ref.1), custom_call_target="tpu_custom_call" | custom-call | flops 68719476736 | bytes 134217728 | tf_op jit(solution)/shard_map/grad_hidden/pallas_call | solution.py:571
  126.2 3.0 collective-permute-done.29
  135.0 11.9 %collective-permute-done.30 = bf16[128,2048]{1,0:T(8,128)(2,1)S(1)} collective-permute-done((bf16[128,2048]{1,0:T(8,128)(2,1)S(1)}, bf16[128,2048]{1,0:T(8,128)(2,1)S(1)}, u32[]{:S(2)}, u32[]{:S(2)}) %collective-permute-start.30) | collective-permute-done | bytes 524320 | tf_op jit(solution)/shard_map/ppermute | solution.py:860
  148.5 11.0 %collective-permute-done.32 = bf16[128,2048]{1,0:T(8,128)(2,1)S(1)} collective-permute-done((bf16[128,2048]{1,0:T(8,128)(2,1)S(1)}, bf16[128,2048]{1,0:T(8,128)(2,1)S(1)}, u32[]{:S(2)}, u32[]{:S(2)}) %collective-permute-start.32) | collective-permute-done | bytes 524320 | tf_op jit(solution)/shard_map/ppermute | solution.py:860
  165.4 15.6 %ffn_stage.1 = (bf16[1024,1024]{1,0:T(8,128)(2,1)}, bf16[1024,1024]{1,0:T(8,128)(2,1)}, bf16[1024,1024]{1,0:T(8,128)(2,1)S(1)}) custom-call(s32[2]{0:T(128)S(1)} %pad_add_fusion.where_ref, bf16[1024,2048]{1,0:T(8,128)(2,1)} %constant_dynamic-update-slice_fusion.7.in_ref, f32[1024,1024]{1,0:T(8,128)} %grad_hidden.1.gh_ref, bf16[2048,2048]{1,0:T(8,128)(2,1)} %wg_ref.3, ...), custom_call_target="tpu_custom_call" | custom-call | flops 171798688 | bytes 251658 | tf_op jit(solution)/shard_map/ffn_stage/pallas_call | solution.py:610
  183.3 8.7 %down_shares.1 = bf16[8,256,1024]{2,1,0:T(8,128)(2,1)S(1)} custom-call(s32[2]{0:T(128)S(1)} %pad_add_fusion.where_ref, bf16[1024,2048]{1,0:T(8,128)(2,1)S(1)} %copy-done.5, bf16[1024,1024]{1,0:T(8,128)(2,1)} %get-tuple-element.258.right_ref), custom_call_target="tpu_custom_call" | custom-call | flops 85899344 | bytes 167772 | tf_op jit(solution)/shard_map/down_shares/pallas_call | solution.py:790
  194.1 8.3 %grad_second_send.1 = bf16[512,2048]{1,0:T(8,128)(2,1)S(1)} custom-call(s32[2]{0:T(128)S(1)} %pad_add_fusion.where_ref, bf16[1024,1024]{1,0:T(8,128)(2,1)} %get-tuple-element.261.gg_ref, bf16[1024,1024]{1,0:T(8,128)(2,1)S(1)} %get-tuple-element.262.gu_ref, bf16[2048,2048]{1,0:T(8,128)(2,1)} %wg_ref.3, bf16[2048,2048]{1,0:T(8,128)(2,1)} %wu_ref.3), custom_call_target="tpu_custom_call" | custom-call | flops 85899344 | bytes 83886 | tf_op jit(solution)/shard_map/grad_second_send/pallas_call | solution.py:642
  202.4 54.2 %conditional.13 = (f32[128,2048]{1,0:T(8,128)}, bf16[8,256,1024]{2,1,0:T(8,128)(2,1)}, bf16[512,2048]{1,0:T(8,128)(2,1)}, bf16[512,2048]{1,0:T(8,128)(2,1)}) conditional(s32[]{:T(128)} %bitcast.2, () %tuple.151, (s32[2]{0:T(128)S(1)}, bf16[1024,1024]{1,0:T(8,128)(2,1)S(1)}, bf16[1024,1024]{1,0:T(8,128)(2,1)S(1)}, bf16[2048,2048]{1,0:T(8,128)(2,1)}, ...), branch_computations={%region_7.0_spmd, %region_8.0_spmd} | conditional | flops 264251632 | bytes 24536870 | solution.py:896
  202.7 7.7 %grad_second_keep.1 = bf16[512,2048]{1,0:T(8,128)(2,1)S(1)} custom-call(s32[2]{0:T(128)S(1)} %get-tuple-element.80.where_ref, bf16[1024,1024]{1,0:T(8,128)(2,1)S(1)} %get-tuple-element.87.gg_ref.right_ref, bf16[1024,1024]{1,0:T(8,128)(2,1)S(1)} %get-tuple-element.82.gu_ref, bf16[2048,2048]{1,0:T(8,128)(2,1)} %get-tuple-element.83.wg_ref, ...), custom_call_target="tpu_custom_call" | custom-call | flops 85899344 | bytes 83886 | tf_op jit(solution)/shard_map/cond/branch_1_fun/grad_second_keep/pallas_call | solution.py:642
  213.9 10.0 %gate_shares.1 = bf16[8,256,1024]{2,1,0:T(8,128)(2,1)} custom-call(s32[2]{0:T(128)S(1)} %get-tuple-element.80.where_ref, bf16[1024,2048]{1,0:T(8,128)(2,1)} %get-tuple-element.86.left_ref, bf16[1024,1024]{1,0:T(8,128)(2,1)S(1)} %get-tuple-element.87.gg_ref.right_ref), custom_call_target="tpu_custom_call" | custom-call | flops 85899344 | bytes 167772 | tf_op jit(solution)/shard_map/cond/branch_1_fun/gate_shares/pallas_call | solution.py:790
  228.1 8.6 %ffn_out.1 = (bf16[512,2048]{1,0:T(8,128)(2,1)}, bf16[512,2048]{1,0:T(8,128)(2,1)}) custom-call(s32[2]{0:T(128)S(1)} %get-tuple-element.80.where_ref, bf16[1024,1024]{1,0:T(8,128)(2,1)} %get-tuple-element.90.hid_ref, bf16[2048,2048]{1,0:T(8,128)(2,1)} %get-tuple-element.91.wd_ref), custom_call_target="tpu_custom_call" | custom-call | flops 85899344 | bytes 167772 | tf_op jit(solution)/shard_map/cond/branch_1_fun/ffn_out/pallas_call | solution.py:675
  237.5 16.6 %collective-permute-done.17 = bf16[128,2048]{1,0:T(8,128)(2,1)} collective-permute-done((bf16[128,2048]{1,0:T(8,128)(2,1)}, bf16[128,2048]{1,0:T(8,128)(2,1)}, u32[]{:S(2)}, u32[]{:S(2)}) %collective-permute-start.17) | collective-permute-done | bytes 524320 | tf_op jit(solution)/shard_map/cond/branch_1_fun/ppermute | solution.py:860
  256.7 20.8 %conditional.14 = (f32[128,2048]{1,0:T(8,128)}, bf16[8,256,1024]{2,1,0:T(8,128)(2,1)}, bf16[512,2048]{1,0:T(8,128)(2,1)S(1)}, f32[1,2048]{1,0:T(1,128)S(1)}) conditional(s32[]{:T(128)} %bitcast.2, () %tuple.150, (bf16[128,2048]{1,0:T(8,128)(2,1)}, f32[128]{0:T(128)S(1)}, f32[2048]{0:T(1024)S(1)}, f32[128,2048]{1,0:T(8,128)}, ...), branch_computations={%region_9.0_spmd, %region_10.13_spmd} | conditional | flops 97431632 | bytes 21166568 | solution.py:896
  262.5 9.9 %up_shares.1 = bf16[8,256,1024]{2,1,0:T(8,128)(2,1)} custom-call(s32[2]{0:T(128)S(1)} %get-tuple-element.102.where_ref, bf16[1024,2048]{1,0:T(8,128)(2,1)} %get-tuple-element.103.left_ref, bf16[1024,1024]{1,0:T(8,128)(2,1)S(1)} %get-tuple-element.105.right_ref), custom_call_target="tpu_custom_call" | custom-call | flops 85899344 | bytes 167772 | tf_op jit(solution)/shard_map/cond/branch_1_fun/up_shares/pallas_call | solution.py:790
  277.6 15.5 %attention_backward_0.1 = (bf16[512,256]{1,0:T(8,128)(2,1)}, bf16[2048,256]{1,0:T(8,128)(2,1)}, bf16[2048,256]{1,0:T(8,128)(2,1)}) custom-call(s32[32]{0:T(128)} %order_ref.7, s32[8]{0:T(128)} %cont_ref.7, s32[2]{0:T(128)S(1)} %pad_add_fusion.where_ref, bf16[512,512]{1,0:T(8,128)(2,1)} %get-tuple-element.241.q_ref, ...), custom_call_target="tpu_custom_call" | custom-call | flops 64424508 | bytes 125829 | tf_op jit(solution)/shard_map/attention_backward_0/pallas_call | solution.py:404
  295.5 16.1 %attention_backward_1.1 = (bf16[512,256]{1,0:T(8,128)(2,1)}, bf16[2048,256]{1,0:T(8,128)(2,1)}, bf16[2048,256]{1,0:T(8,128)(2,1)}) custom-call(s32[32]{0:T(128)} %order_ref.7, s32[8]{0:T(128)} %cont_ref.7, s32[2]{0:T(128)S(1)} %pad_add_fusion.where_ref, bf16[512,512]{1,0:T(8,128)(2,1)} %get-tuple-element.241.q_ref, bf16[512,2048]{1,0:T(8,128)(2,1)} %copy-done.21, ...), custom_call_target="tpu_custom_call" | custom-call | flops 64424508 | bytes 125829 | tf_op jit(solution)/shard_map/attention_backward_1/pallas_call | solution.py:404
  312.8 8.5 %branch_shares.1 = (bf16[4,256,1024]{2,1,0:T(8,128)(2,1)S(1)}, bf16[4,256,1024]{2,1,0:T(8,128)(2,1)}) custom-call(s32[2]{0:T(128)S(1)} %pad_add_fusion.where_ref, bf16[512,2048]{1,0:T(8,128)(2,1)S(1)} %copy-done.13, bf16[512,2048]{1,0:T(8,128)(2,1)} %copy-done.21, bf16[512,256]{1,0:T(8,128)(2,1)S(1)} %copy-done.15, bf16[512,256]{1,0:T(8,128)(2,1)S(1)} %copy-done.16, ...), custom_call_target="tpu_custom_call" | custom-call | flops 42949672 | bytes 83886 | tf_op jit(solution)/shard_map/branch_shares/pallas_call | solution.py:746
  321.3 16.0 %collective-permute-done.34 = bf16[2048,256]{1,0:T(8,128)(2,1)} collective-permute-done((bf16[2048,256]{1,0:T(8,128)(2,1)}, bf16[2048,256]{1,0:T(8,128)(2,1)}, u32[]{:S(2)}, u32[]{:S(2)}) %collective-permute-start.34) | collective-permute-done | bytes 1048608 | tf_op jit(solution)/shard_map/ppermute | solution.py:860
  337.3 33.3 %collective-permute-done.35 = bf16[2048,256]{1,0:T(8,128)(2,1)S(1)} collective-permute-done((bf16[2048,256]{1,0:T(8,128)(2,1)}, bf16[2048,256]{1,0:T(8,128)(2,1)S(1)}, u32[]{:S(2)}, u32[]{:S(2)}) %collective-permute-start.35) | collective-permute-done | bytes 1048608 | tf_op jit(solution)/shard_map/ppermute | solution.py:860
  379.4 21.8 %conditional.15 = (bf16[128,2048]{1,0:T(8,128)(2,1)S(1)}, bf16[128,2048]{1,0:T(8,128)(2,1)S(1)}, bf16[128,2048]{1,0:T(8,128)(2,1)S(1)}) conditional(s32[]{:T(128)} %bitcast.2, () %tuple.149, (bf16[512,2048]{1,0:T(8,128)(2,1)}, bf16[512,2048]{1,0:T(8,128)(2,1)}) %tuple.162), branch_computations={%region_14.15_spmd, %region_15.16_spmd} | conditional | flops 5242880 | bytes 17301608 | solution.py:896
  379.7 4.4 collective-permute-done.18
  387.1 12.2 %collective-permute-done.19 = bf16[128,2048]{1,0:T(8,128)(2,1)S(1)} collective-permute-done((bf16[128,2048]{1,0:T(8,128)(2,1)S(1)}, bf16[128,2048]{1,0:T(8,128)(2,1)S(1)}, u32[]{:S(2)}, u32[]{:S(2)}) %collective-permute-start.19) | collective-permute-done | bytes 524320 | tf_op jit(solution)/shard_map/cond/branch_1_fun/ppermute | solution.py:860
  402.9 21.1 %collective-permute-done.37 = bf16[1024,256]{1,0:T(8,128)(2,1)} collective-permute-done((bf16[1024,256]{1,0:T(8,128)(2,1)}, bf16[1024,256]{1,0:T(8,128)(2,1)}, u32[]{:S(2)}, u32[]{:S(2)}) %collective-permute-start.37) | collective-permute-done | bytes 524320 | tf_op jit(solution)/shard_map/ppermute | solution.py:860
  433.2 31.2 %conditional.16 = (bf16[128,2048]{1,0:T(8,128)(2,1)}, bf16[128,2048]{1,0:T(8,128)(2,1)}) conditional(s32[]{:T(128)} %bitcast.2, () %tuple.148, (bf16[128,2048]{1,0:T(8,128)(2,1)S(1)}, bf16[128,2048]{1,0:T(8,128)(2,1)S(1)}) %tuple.261), branch_computations={%region_17.18_spmd, %region_18.19_spmd} | conditional | bytes 4194400 | solution.py:896
  437.2 27.2 %collective-permute-done.7 = bf16[128,2048]{1,0:T(8,128)(2,1)} collective-permute-done((bf16[128,2048]{1,0:T(8,128)(2,1)S(1)}, bf16[128,2048]{1,0:T(8,128)(2,1)}, u32[]{:S(2)}, u32[]{:S(2)}) %collective-permute-start.7) | collective-permute-done | bytes 524320 | tf_op jit(solution)/shard_map/cond/branch_1_fun/ppermute | solution.py:860
  467.0 4.8 add_convert_fusion.13
  476.4 4.2 tail_stage.1
  480.6 5.1 kv_shares.1
  486.8 20.3 %conditional.17 = (bf16[128,2048]{1,0:T(8,128)(2,1)S(1)}, f32[1,2048]{1,0:T(1,128)S(1)}) conditional(s32[]{:T(128)} %bitcast.2, () %tuple.139, (f32[128,2048]{1,0:T(8,128)}, bf16[256,2048]{1,0:T(8,128)(2,1)}, bf16[256,2048]{1,0:T(8,128)(2,1)}, f32[2048]{0:T(1024)S(1)}, f32[128,2048]{1,0:T(8,128)}) %tuple.262), branch_computations={%region_19.20_spmd, %region_20.24_spmd} | conditional | flops 8648832 | bytes 24146584 | solution.py:896
  492.4 12.5 %collective-permute-done.21 = bf16[128,2048]{1,0:T(8,128)(2,1)S(1)} collective-permute-done((bf16[128,2048]{1,0:T(8,128)(2,1)S(1)}, bf16[128,2048]{1,0:T(8,128)(2,1)S(1)}, u32[]{:S(2)}, u32[]{:S(2)}) %collective-permute-start.21) | collective-permute-done | bytes 524320 | tf_op jit(solution)/shard_map/cond/branch_1_fun/ppermute | solution.py:860
  523.7 24.7 %conditional.18 = (f32[2,2048]{1,0:T(2,128)S(1)}) conditional(s32[]{:T(128)} %bitcast.2, () %tuple.178, f32[2,2048]{1,0:T(2,128)S(1)} %pad_maximum_fusion.5), branch_computations={%region_24.25_spmd, %region_25.26_spmd} | conditional | flops 20480 | bytes 573648 | solution.py:896
  525.7 8.5 %collective-permute-done.10 = f32[2,2048]{1,0:T(2,128)S(1)} collective-permute-done((f32[2,2048]{1,0:T(2,128)S(1)}, f32[2,2048]{1,0:T(2,128)S(1)}, u32[]{:S(2)}, u32[]{:S(2)}) %collective-permute-start.10) | collective-permute-done | bytes 16416 | tf_op jit(solution)/shard_map/cond/branch_1_fun/ppermute | solution.py:860
  542.9 3.8 collective-permute-start.13
  549.9 2.9 collective-permute-start.47
  552.8 9.1 %conditional.19 = (bf16[512,2048]{1,0:T(8,128)(2,1)}, bf16[512,2048]{1,0:T(8,128)(2,1)}) conditional(s32[]{:T(128)} %bitcast.2, () %tuple.138, (bf16[256,2048]{1,0:T(8,128)(2,1)}, bf16[256,2048]{1,0:T(8,128)(2,1)}) %tuple.188), branch_computations={%region_26.27_spmd, %region_27.28_spmd} | conditional | bytes 12582968 | solution.py:896
  557.4 4.5 collective-permute-done.22
  (281 shorter events, 170.8 us)
Async XLA Ops:
  7.2 286.1 %reduce-scatter.4.cloned.1.call-start = ((), (), s32[]{:S(2)}) async-start(), calls=%async_computation.3 | async-start | bytes 5242880 | tf_op jit(solution)/shard_map/reduce_scatter | solution.py:972
  9.2 14.9 %collective-permute-start.27 = (bf16[128,2048]{1,0:T(8,128)(2,1)S(1)}, bf16[128,2048]{1,0:T(8,128)(2,1)S(1)}, u32[]{:S(2)}, u32[]{:S(2)}) collective-permute-start(bf16[128,2048]{1,0:T(8,128)(2,1)S(1)} %get-tuple-element.384), channel_id=1, source_target_pairs={{0,8},{8,0},{1,9},{9,1},{2,10},{10,2},{3,11},{11,3},{4,12},{12,4},... | collective-permute-start | bytes 1572872 | tf_op jit(solution)/shard_map/ppermute | solution.py:860
  24.2 25.5 %collective-permute-start = (bf16[512,512]{1,0:T(8,128)(2,1)S(1)}, bf16[512,512]{1,0:T(8,128)(2,1)}, u32[]{:S(2)}, u32[]{:S(2)}) collective-permute-start(bf16[512,512]{1,0:T(8,128)(2,1)S(1)} %param.1), channel_id=1, source_target_pairs={{0,16},{16,0},{1,17},{17,1},{2,18},{18,2},{3,19},{19,3},{4,20},{20... | collective-permute-start | bytes 1572872 | tf_op jit(solution)/shard_map/cond/branch_1_fun/ppermute | solution.py:860
  26.9 22.9 %collective-permute-start.1 = (bf16[512,512]{1,0:T(8,128)(2,1)S(1)}, bf16[512,512]{1,0:T(8,128)(2,1)}, u32[]{:S(2)}, u32[]{:S(2)}) collective-permute-start(bf16[512,512]{1,0:T(8,128)(2,1)S(1)} %param.1), channel_id=1, source_target_pairs={{0,8},{8,0},{1,9},{9,1},{2,10},{10,2},{3,11},{11,3},{4,12},{12,4},... | collective-permute-start | bytes 1572872 | tf_op jit(solution)/shard_map/cond/branch_1_fun/ppermute | solution.py:860
  28.5 21.3 %collective-permute-start.2 = (bf16[512,512]{1,0:T(8,128)(2,1)S(1)}, bf16[512,512]{1,0:T(8,128)(2,1)}, u32[]{:S(2)}, u32[]{:S(2)}) collective-permute-start(bf16[512,512]{1,0:T(8,128)(2,1)S(1)} %param.1), channel_id=1, source_target_pairs={{0,4},{4,0},{1,5},{5,1},{2,6},{6,2},{3,7},{7,3},{8,12},{12,8},{9,1... | collective-permute-start | bytes 1572872 | tf_op jit(solution)/shard_map/cond/branch_1_fun/ppermute | solution.py:860
  49.8 13.0 %collective-permute-start.5 = (bf16[512,512]{1,0:T(8,128)(2,1)}, bf16[512,512]{1,0:T(8,128)(2,1)}, u32[]{:S(2)}, u32[]{:S(2)}) collective-permute-start(bf16[512,512]{1,0:T(8,128)(2,1)} %get-tuple-element.77), channel_id=1, source_target_pairs={{0,8},{8,0},{1,9},{9,1},{2,10},{10,2},{3,11},{11,3},{4,12},{12,4},... | collective-permute-start | bytes 1572872 | tf_op jit(solution)/shard_map/cond/branch_1_fun/ppermute | solution.py:860
  51.1 15.2 %collective-permute-start.6 = (bf16[512,512]{1,0:T(8,128)(2,1)}, bf16[512,512]{1,0:T(8,128)(2,1)}, u32[]{:S(2)}, u32[]{:S(2)}) collective-permute-start(bf16[512,512]{1,0:T(8,128)(2,1)} %get-tuple-element.77), channel_id=1, source_target_pairs={{0,4},{4,0},{1,5},{5,1},{2,6},{6,2},{3,7},{7,3},{8,12},{12,8},{9,1... | collective-permute-start | bytes 1572872 | tf_op jit(solution)/shard_map/cond/branch_1_fun/ppermute | solution.py:860
  52.6 22.5 %collective-permute-start.3 = (bf16[512,512]{1,0:T(8,128)(2,1)}, bf16[512,512]{1,0:T(8,128)(2,1)}, u32[]{:S(2)}, u32[]{:S(2)}) collective-permute-start(bf16[512,512]{1,0:T(8,128)(2,1)} %get-tuple-element.75), channel_id=1, source_target_pairs={{0,4},{4,0},{1,5},{5,1},{2,6},{6,2},{3,7},{7,3},{8,12},{12,8},{9,1... | collective-permute-start | bytes 1572872 | tf_op jit(solution)/shard_map/cond/branch_1_fun/ppermute | solution.py:860
  53.1 21.9 %collective-permute-start.4 = (bf16[128,2048]{1,0:T(8,128)(2,1)S(1)}, bf16[128,2048]{1,0:T(8,128)(2,1)}, u32[]{:S(2)}, u32[]{:S(2)}) collective-permute-start(bf16[128,2048]{1,0:T(8,128)(2,1)S(1)} %get-tuple-element.76), channel_id=1, source_target_pairs={{0,2},{2,0},{1,3},{3,1},{4,6},{6,4},{5,7},{7,5},{8,10},{10,8},{9,1... | collective-permute-start | bytes 1572872 | tf_op jit(solution)/shard_map/cond/branch_1_fun/ppermute | solution.py:860
  76.4 14.7 %collective-permute-start.25 = (bf16[512,512]{1,0:T(8,128)(2,1)}, bf16[512,512]{1,0:T(8,128)(2,1)}, u32[]{:S(2)}, u32[]{:S(2)}) collective-permute-start(bf16[512,512]{1,0:T(8,128)(2,1)} %get-tuple-element.78), channel_id=1, source_target_pairs={{0,4},{4,0},{1,5},{5,1},{2,6},{6,2},{3,7},{7,3},{8,12},{12,8},{9,1... | collective-permute-start | bytes 1572872 | tf_op jit(solution)/shard_map/cond/branch_1_fun/ppermute | solution.py:860
  115.0 14.3 %collective-permute-start.29 = (bf16[128,2048]{1,0:T(8,128)(2,1)S(1)}, bf16[128,2048]{1,0:T(8,128)(2,1)S(1)}, u32[]{:S(2)}, u32[]{:S(2)}) collective-permute-start(bf16[128,2048]{1,0:T(8,128)(2,1)S(1)} %slice.223), channel_id=1, source_target_pairs={{0,2},{2,0},{1,3},{3,1},{4,6},{6,4},{5,7},{7,5},{8,10},{10,8},{9,1... | collective-permute-start | bytes 1572872 | tf_op jit(solution)/shard_map/ppermute | solution.py:860
  133.5 13.5 %collective-permute-start.30 = (bf16[128,2048]{1,0:T(8,128)(2,1)S(1)}, bf16[128,2048]{1,0:T(8,128)(2,1)S(1)}, u32[]{:S(2)}, u32[]{:S(2)}) collective-permute-start(bf16[128,2048]{1,0:T(8,128)(2,1)S(1)} %get-tuple-element.381), channel_id=1, source_target_pairs={{0,8},{8,0},{1,9},{9,1},{2,10},{10,2},{3,11},{11,3},{4,12},{12,4},... | collective-permute-start | bytes 1572872 | tf_op jit(solution)/shard_map/ppermute | solution.py:860
  133.5 15.0 %collective-permute-start.31 = (bf16[128,2048]{1,0:T(8,128)(2,1)S(1)}, bf16[128,2048]{1,0:T(8,128)(2,1)S(1)}, u32[]{:S(2)}, u32[]{:S(2)}) collective-permute-start(bf16[128,2048]{1,0:T(8,128)(2,1)S(1)} %get-tuple-element.381), channel_id=1, source_target_pairs={{0,2},{2,0},{1,3},{3,1},{4,6},{6,4},{5,7},{7,5},{8,10},{10,8},{9,1... | collective-permute-start | bytes 1572872 | tf_op jit(solution)/shard_map/ppermute | solution.py:860
  147.0 12.6 %collective-permute-start.32 = (bf16[128,2048]{1,0:T(8,128)(2,1)S(1)}, bf16[128,2048]{1,0:T(8,128)(2,1)S(1)}, u32[]{:S(2)}, u32[]{:S(2)}) collective-permute-start(bf16[128,2048]{1,0:T(8,128)(2,1)S(1)} %collective-permute-done.30), channel_id=1, source_target_pairs={{0,2},{2,0},{1,3},{3,1},{4,6},{6,4},{5,7},{7,5},{8,10},{10,8},{9,1... | collective-permute-start | bytes 1572872 | tf_op jit(solution)/shard_map/ppermute | solution.py:860
  159.8 4.2 collective-permute-start.33
  194.0 233.9 %reduce-scatter.6.cloned.1.call-start = ((), (), s32[]{:S(2)}) async-start(), calls=%async_computation.4 | async-start | bytes 5242880 | tf_op jit(solution)/shard_map/reduce_scatter | solution.py:972
  202.6 7.8 %collective-permute-start.14 = (bf16[512,2048]{1,0:T(8,128)(2,1)S(1)}, bf16[512,2048]{1,0:T(8,128)(2,1)S(1)}, u32[]{:S(2)}, u32[]{:S(2)}) collective-permute-start(bf16[512,2048]{1,0:T(8,128)(2,1)S(1)} %get-tuple-element.85), channel_id=1, source_target_pairs={{0,1},{1,0},{2,3},{3,2},{4,5},{5,4},{6,7},{7,6},{8,9},{9,8},{10,11... | collective-permute-start | bytes 6291464 | tf_op jit(solution)/shard_map/cond/branch_1_fun/ppermute | solution.py:860
  211.9 14.7 %collective-permute-start.15 = (bf16[128,2048]{1,0:T(8,128)(2,1)S(1)}, bf16[128,2048]{1,0:T(8,128)(2,1)S(1)}, u32[]{:S(2)}, u32[]{:S(2)}) collective-permute-start(bf16[128,2048]{1,0:T(8,128)(2,1)S(1)} %get-tuple-element.389), channel_id=1, source_target_pairs={{0,2},{2,0},{1,3},{3,1},{4,6},{6,4},{5,7},{7,5},{8,10},{10,8},{9,1... | collective-permute-start | bytes 1572872 | tf_op jit(solution)/shard_map/cond/branch_1_fun/ppermute | solution.py:860
  213.3 24.3 %collective-permute-start.16 = (bf16[128,2048]{1,0:T(8,128)(2,1)}, bf16[128,2048]{1,0:T(8,128)(2,1)}, u32[]{:S(2)}, u32[]{:S(2)}) collective-permute-start(bf16[128,2048]{1,0:T(8,128)(2,1)} %get-tuple-element.387), channel_id=1, source_target_pairs={{0,2},{2,0},{1,3},{3,1},{4,6},{6,4},{5,7},{7,5},{8,10},{10,8},{9,1... | collective-permute-start | bytes 1572872 | tf_op jit(solution)/shard_map/cond/branch_1_fun/ppermute | solution.py:860
  227.6 26.5 %collective-permute-start.17 = (bf16[128,2048]{1,0:T(8,128)(2,1)}, bf16[128,2048]{1,0:T(8,128)(2,1)}, u32[]{:S(2)}, u32[]{:S(2)}) collective-permute-start(bf16[128,2048]{1,0:T(8,128)(2,1)} %add_convert_fusion.2), channel_id=1, source_target_pairs={{0,8},{8,0},{1,9},{9,1},{2,10},{10,2},{3,11},{11,3},{4,12},{12,4},... | collective-permute-start | bytes 1572872 | tf_op jit(solution)/shard_map/cond/branch_1_fun/ppermute | solution.py:860
  256.7 310.6 %reduce-scatter.8.cloned.1.call-start = ((), (), s32[]{:S(2)}) async-start(), calls=%async_computation.5 | async-start | bytes 5242880 | tf_op jit(solution)/shard_map/reduce_scatter | solution.py:972
  260.8 13.8 %collective-permute-start.23 = (bf16[128,2048]{1,0:T(8,128)(2,1)S(1)}, bf16[128,2048]{1,0:T(8,128)(2,1)S(1)}, u32[]{:S(2)}, u32[]{:S(2)}) collective-permute-start(bf16[128,2048]{1,0:T(8,128)(2,1)S(1)} %get-tuple-element.378), channel_id=1, source_target_pairs={{0,2},{2,0},{1,3},{3,1},{4,6},{6,4},{5,7},{7,5},{8,10},{10,8},{9,1... | collective-permute-start | bytes 1572872 | tf_op jit(solution)/shard_map/cond/branch_1_fun/ppermute | solution.py:860
  293.1 44.2 %collective-permute-start.34 = (bf16[2048,256]{1,0:T(8,128)(2,1)}, bf16[2048,256]{1,0:T(8,128)(2,1)}, u32[]{:S(2)}, u32[]{:S(2)}) collective-permute-start(bf16[2048,256]{1,0:T(8,128)(2,1)} %get-tuple-element.276), channel_id=1, source_target_pairs={{0,4},{4,0},{1,5},{5,1},{2,6},{6,2},{3,7},{7,3},{8,12},{12,8},{9,1... | collective-permute-start | bytes 3145736 | tf_op jit(solution)/shard_map/ppermute | solution.py:860
  311.6 59.0 %collective-permute-start.35 = (bf16[2048,256]{1,0:T(8,128)(2,1)}, bf16[2048,256]{1,0:T(8,128)(2,1)S(1)}, u32[]{:S(2)}, u32[]{:S(2)}) collective-permute-start(bf16[2048,256]{1,0:T(8,128)(2,1)} %get-tuple-element.280), channel_id=1, source_target_pairs={{0,4},{4,0},{1,5},{5,1},{2,6},{6,2},{3,7},{7,3},{8,12},{12,8},{9,1... | collective-permute-start | bytes 3145736 | tf_op jit(solution)/shard_map/ppermute | solution.py:860
  311.7 61.7 %collective-permute-start.36 = (bf16[256,1024]{1,0:T(8,128)(2,1)}, bf16[256,1024]{1,0:T(8,128)(2,1)}, u32[]{:S(2)}, u32[]{:S(2)}) collective-permute-start(bf16[256,1024]{1,0:T(8,128)(2,1)} %get-tuple-element.426), channel_id=1, source_target_pairs={{0,8},{8,0},{1,9},{9,1},{2,10},{10,2},{3,11},{11,3},{4,12},{12,4},... | collective-permute-start | bytes 1572872 | tf_op jit(solution)/shard_map/ppermute | solution.py:860
  377.0 89.9 %collective-permute-start.39 = (bf16[4,256,1024]{2,1,0:T(8,128)(2,1)}, bf16[4,256,1024]{2,1,0:T(8,128)(2,1)}, u32[]{:S(2)}, u32[]{:S(2)}) collective-permute-start(bf16[4,256,1024]{2,1,0:T(8,128)(2,1)} %get-tuple-element.303), channel_id=1, source_target_pairs={{0,4},{4,0},{1,5},{5,1},{2,6},{6,2},{3,7},{7,3},{8,12},{12,8},{9,1... | collective-permute-start | bytes 6291464 | tf_op jit(solution)/shard_map/ppermute | solution.py:860
  377.4 25.5 %collective-permute-start.38 = (bf16[1024,256]{1,0:T(8,128)(2,1)}, bf16[1024,256]{1,0:T(8,128)(2,1)}, u32[]{:S(2)}, u32[]{:S(2)}) collective-permute-start(bf16[1024,256]{1,0:T(8,128)(2,1)} %get-tuple-element.292), channel_id=1, source_target_pairs={{0,8},{8,0},{1,9},{9,1},{2,10},{10,2},{3,11},{11,3},{4,12},{12,4},... | collective-permute-start | bytes 1572872 | tf_op jit(solution)/shard_map/ppermute | solution.py:860
  379.1 44.9 %collective-permute-start.37 = (bf16[1024,256]{1,0:T(8,128)(2,1)}, bf16[1024,256]{1,0:T(8,128)(2,1)}, u32[]{:S(2)}, u32[]{:S(2)}) collective-permute-start(bf16[1024,256]{1,0:T(8,128)(2,1)} %get-tuple-element.289), channel_id=1, source_target_pairs={{0,8},{8,0},{1,9},{9,1},{2,10},{10,2},{3,11},{11,3},{4,12},{12,4},... | collective-permute-start | bytes 1572872 | tf_op jit(solution)/shard_map/ppermute | solution.py:860
  379.7 4.4 collective-permute-start.18
  385.3 14.0 %collective-permute-start.19 = (bf16[128,2048]{1,0:T(8,128)(2,1)S(1)}, bf16[128,2048]{1,0:T(8,128)(2,1)S(1)}, u32[]{:S(2)}, u32[]{:S(2)}) collective-permute-start(bf16[128,2048]{1,0:T(8,128)(2,1)S(1)} %add_convert_fusion.6), channel_id=1, source_target_pairs={{0,2},{2,0},{1,3},{3,1},{4,6},{6,4},{5,7},{7,5},{8,10},{10,8},{9,1... | collective-permute-start | bytes 1572872 | tf_op jit(solution)/shard_map/cond/branch_1_fun/ppermute | solution.py:860
  430.3 44.4 %collective-permute-start.41 = (bf16[512,256]{1,0:T(8,128)(2,1)}, bf16[512,256]{1,0:T(8,128)(2,1)S(1)}, u32[]{:S(2)}, u32[]{:S(2)}) collective-permute-start(bf16[512,256]{1,0:T(8,128)(2,1)} %get-tuple-element.420), channel_id=1, source_target_pairs={{0,16},{16,0},{1,17},{17,1},{2,18},{18,2},{3,19},{19,3},{4,20},{20... | collective-permute-start | bytes 786440 | tf_op jit(solution)/shard_map/ppermute | solution.py:860
  433.0 43.4 %collective-permute-start.40 = (bf16[512,256]{1,0:T(8,128)(2,1)}, bf16[512,256]{1,0:T(8,128)(2,1)S(1)}, u32[]{:S(2)}, u32[]{:S(2)}) collective-permute-start(bf16[512,256]{1,0:T(8,128)(2,1)} %get-tuple-element.422), channel_id=1, source_target_pairs={{0,16},{16,0},{1,17},{17,1},{2,18},{18,2},{3,19},{19,3},{4,20},{20... | collective-permute-start | bytes 786440 | tf_op jit(solution)/shard_map/ppermute | solution.py:860
  433.2 31.2 %collective-permute-start.7 = (bf16[128,2048]{1,0:T(8,128)(2,1)S(1)}, bf16[128,2048]{1,0:T(8,128)(2,1)}, u32[]{:S(2)}, u32[]{:S(2)}) collective-permute-start(bf16[128,2048]{1,0:T(8,128)(2,1)S(1)} %get-tuple-element.109), channel_id=1, source_target_pairs={{0,8},{8,0},{1,9},{9,1},{2,10},{10,2},{3,11},{11,3},{4,12},{12,4},... | collective-permute-start | bytes 1572872 | tf_op jit(solution)/shard_map/cond/branch_1_fun/ppermute | solution.py:860
  435.7 28.7 %collective-permute-start.8 = (bf16[128,2048]{1,0:T(8,128)(2,1)S(1)}, bf16[128,2048]{1,0:T(8,128)(2,1)}, u32[]{:S(2)}, u32[]{:S(2)}) collective-permute-start(bf16[128,2048]{1,0:T(8,128)(2,1)S(1)} %get-tuple-element.110), channel_id=1, source_target_pairs={{0,2},{2,0},{1,3},{3,1},{4,6},{6,4},{5,7},{7,5},{8,10},{10,8},{9,1... | collective-permute-start | bytes 1572872 | tf_op jit(solution)/shard_map/cond/branch_1_fun/ppermute | solution.py:860
  464.4 46.2 %collective-permute-start.42 = (bf16[256,1024]{1,0:T(8,128)(2,1)}, bf16[256,1024]{1,0:T(8,128)(2,1)}, u32[]{:S(2)}, u32[]{:S(2)}) collective-permute-start(bf16[256,1024]{1,0:T(8,128)(2,1)} %get-tuple-element.323), channel_id=1, source_target_pairs={{0,8},{8,0},{1,9},{9,1},{2,10},{10,2},{3,11},{11,3},{4,12},{12,4},... | collective-permute-start | bytes 1572872 | tf_op jit(solution)/shard_map/ppermute | solution.py:860
  480.6 32.7 %collective-permute-start.43 = (bf16[2,256,1024]{2,1,0:T(8,128)(2,1)}, bf16[2,256,1024]{2,1,0:T(8,128)(2,1)}, u32[]{:S(2)}, u32[]{:S(2)}) collective-permute-start(bf16[2,256,1024]{2,1,0:T(8,128)(2,1)} %get-tuple-element.393), channel_id=1, source_target_pairs={{0,8},{8,0},{1,9},{9,1},{2,10},{10,2},{3,11},{11,3},{4,12},{12,4},... | collective-permute-start | bytes 3145736 | tf_op jit(solution)/shard_map/ppermute | solution.py:860
  485.7 30.2 %collective-permute-start.44 = (bf16[4,256,512]{2,1,0:T(8,128)(2,1)}, bf16[4,256,512]{2,1,0:T(8,128)(2,1)}, u32[]{:S(2)}, u32[]{:S(2)}) collective-permute-start(bf16[4,256,512]{2,1,0:T(8,128)(2,1)} %get-tuple-element.329), channel_id=1, source_target_pairs={{0,4},{4,0},{1,5},{5,1},{2,6},{6,2},{3,7},{7,3},{8,12},{12,8},{9,1... | collective-permute-start | bytes 3145736 | tf_op jit(solution)/shard_map/ppermute | solution.py:860
  490.8 14.0 %collective-permute-start.21 = (bf16[128,2048]{1,0:T(8,128)(2,1)S(1)}, bf16[128,2048]{1,0:T(8,128)(2,1)S(1)}, u32[]{:S(2)}, u32[]{:S(2)}) collective-permute-start(bf16[128,2048]{1,0:T(8,128)(2,1)S(1)} %add_convert_fusion.11), channel_id=1, source_target_pairs={{0,2},{2,0},{1,3},{3,1},{4,6},{6,4},{5,7},{7,5},{8,10},{10,8},{9,1... | collective-permute-start | bytes 1572872 | tf_op jit(solution)/shard_map/cond/branch_1_fun/ppermute | solution.py:860
  509.2 40.7 %collective-permute-start.46 = (bf16[256,2048]{1,0:T(8,128)(2,1)}, bf16[256,2048]{1,0:T(8,128)(2,1)}, u32[]{:S(2)}, u32[]{:S(2)}) collective-permute-start(bf16[256,2048]{1,0:T(8,128)(2,1)} %pad_maximum_fusion.4), channel_id=1, source_target_pairs={{0,2},{2,0},{1,3},{3,1},{4,6},{6,4},{5,7},{7,5},{8,10},{10,8},{9,1... | collective-permute-start | bytes 3145736 | tf_op jit(solution)/shard_map/ppermute | solution.py:860
  518.5 30.5 %collective-permute-start.45 = (bf16[2,256,512]{2,1,0:T(8,128)(2,1)}, bf16[2,256,512]{2,1,0:T(8,128)(2,1)S(1)}, u32[]{:S(2)}, u32[]{:S(2)}) collective-permute-start(bf16[2,256,512]{2,1,0:T(8,128)(2,1)} %get-tuple-element.401), channel_id=1, source_target_pairs={{0,8},{8,0},{1,9},{9,1},{2,10},{10,2},{3,11},{11,3},{4,12},{12,4},... | collective-permute-start | bytes 1572872 | tf_op jit(solution)/shard_map/ppermute | solution.py:860
  522.4 53.2 %collective-permute-start.48 = (bf16[1,256,1024]{2,1,0:T(8,128)(2,1)}, bf16[1,256,1024]{2,1,0:T(8,128)(2,1)}, u32[]{:S(2)}, u32[]{:S(2)}) collective-permute-start(bf16[1,256,1024]{2,1,0:T(8,128)(2,1)} %get-tuple-element.395), channel_id=1, source_target_pairs={{0,16},{16,0},{1,17},{17,1},{2,18},{18,2},{3,19},{19,3},{4,20},{20... | collective-permute-start | bytes 1572872 | tf_op jit(solution)/shard_map/ppermute | solution.py:860
  524.9 9.4 %collective-permute-start.10 = (f32[2,2048]{1,0:T(2,128)S(1)}, f32[2,2048]{1,0:T(2,128)S(1)}, u32[]{:S(2)}, u32[]{:S(2)}) collective-permute-start(f32[2,2048]{1,0:T(2,128)S(1)} %add.208), channel_id=1, source_target_pairs={{0,2},{2,0},{1,3},{3,1},{4,6},{6,4},{5,7},{7,5},{8,10},{10,8},{9,1... | collective-permute-start | bytes 49160 | tf_op jit(solution)/shard_map/cond/branch_1_fun/ppermute | solution.py:860
  534.3 3.8 collective-permute-start.11
  538.1 4.7 collective-permute-start.12
  542.9 5.6 collective-permute-start.13
  549.9 19.5 %collective-permute-start.47 = (bf16[1,256,512]{2,1,0:T(8,128)(2,1)}, bf16[1,256,512]{2,1,0:T(8,128)(2,1)}, u32[]{:S(2)}, u32[]{:S(2)}) collective-permute-start(bf16[1,256,512]{2,1,0:T(8,128)(2,1)} %get-tuple-element.414), channel_id=1, source_target_pairs={{0,16},{16,0},{1,17},{17,1},{2,18},{18,2},{3,19},{19,3},{4,20},{20... | collective-permute-start | bytes 786440 | tf_op jit(solution)/shard_map/ppermute | solution.py:860
  557.4 4.5 collective-permute-start.22
  569.3 14.3 %collective-permute-start.49 = (bf16[256,1024]{1,0:T(8,128)(2,1)}, bf16[256,1024]{1,0:T(8,128)(2,1)}, u32[]{:S(2)}, u32[]{:S(2)}) collective-permute-start(bf16[256,1024]{1,0:T(8,128)(2,1)} %get-tuple-element.349), channel_id=1, source_target_pairs={{0,8},{8,0},{1,9},{9,1},{2,10},{10,2},{3,11},{11,3},{4,12},{12,4},... | collective-permute-start | bytes 1572872 | tf_op jit(solution)/shard_map/ppermute | solution.py:860
  (63 other events, 754.0 us)
Sparse Core Ops, SparseCore 0:
  194.1 86.9 reduce-scatter.3
  284.4 86.1 reduce-scatter.5
  373.6 104.2 reduce-scatter.7

commit v15 on v14

--- a/solution.py
+++ b/solution.py
@@ -580,7 +580,7 @@
             ],
             out_specs=pl.BlockSpec((rows, block), lambda i, w: (0, i)),
         ),
-        compiler_params=pltpu.CompilerParams(vmem_limit_bytes=VMEM_LIMIT),
+        compiler_params=pltpu.CompilerParams(vmem_limit_bytes=VMEM_SMALL),
         cost_estimate=cost("grad_hidden", 2 * rows * model * units, 4 * rows * model),
         name="grad_hidden",
     )(where, cot, w_down)
@@ -621,7 +621,7 @@
             ],
             out_specs=[unit_spec] * 3,
         ),
-        compiler_params=pltpu.CompilerParams(vmem_limit_bytes=VMEM_LIMIT),
+        compiler_params=pltpu.CompilerParams(vmem_limit_bytes=VMEM_SMALL),
         cost_estimate=cost("ffn_stage", 4 * rows * model * units, 6 * rows * model),
         name="ffn_stage",
     )(where, second, grad_hidden, w_gate, w_up)
@@ -681,7 +681,7 @@
             in_specs=[left_spec] * len(lefts) + [right_spec] * len(rights),
             out_specs=[half_spec, half_spec],
         ),
-        compiler_params=pltpu.CompilerParams(vmem_limit_bytes=VMEM_LIMIT),
+        compiler_params=pltpu.CompilerParams(vmem_limit_bytes=VMEM_SMALL),
         cost_estimate=cost(name, 2 * len(lefts) * rows * units * model, 4 * rows * model),
         name=name,
     )(where, *lefts, *rights)

time: 599 us -> 590 us (0.985)
  Pallas kernels: 154 us -> 136 us
  waiting for transfers between devices: 267 us -> 280 us
  starting transfers between devices: 56 us -> 63.6 us
    ppermute x50, waiting for transfers between devices: 267 us -> 280 us  [flip(): lax.ppermute(value, axis, [(i, i ^ mask) for i in range(lax.axis_size(axi...]
    ppermute x50, starting transfers between devices: 55.9 us -> 63.5 us  [flip(): lax.ppermute(value, axis, [(i, i ^ mask) for i in range(lax.axis_size(axi...]
    unnamed x122 -> x136, local copies, waits for them, and re-layouts: 19 us -> 15.2 us
  transfers between devices with their start and end apart: 53 -> 53, of which waited for: 35 -> 36; matrix products, arithmetic and copies ran while one was open for 13% -> 13% of each run, Pallas kernels for 19% -> 17%
where the time goes in v15:
time: 590 us; the launch traced here: 585 us
  waiting for transfers between devices  280 us (47%)
  Pallas kernels  136 us (23%)
  starting transfers between devices  63.6 us (11%)
  other arithmetic  49.8 us (8%)
  local copies, waits for them, and re-layouts  39.6 us (7%)
  between operations  15.8 us (3%)
    ppermute x50, waiting for transfers between devices, flip(): lax.ppermute(value, axis, [(i, i ^ mask) for i in range(lax.axis_size(axi...  280 us
    ppermute x50, starting transfers between devices, flip(): lax.ppermute(value, axis, [(i, i ^ mask) for i in range(lax.axis_size(axi...  63.5 us
    pallas_call x2, Pallas kernels, attention_backward(): pl.pallas_call(functools.partial(backward_kernel, rep, 1, ctx_count, head...  27.7 us
    pallas_call x3, Pallas kernels, unit_shares(): pl.pallas_call(unit_shares_kernel, out_shape=shares, grid_spec=pltpu.Pref...  23 us
    convert_element_type x13, other arithmetic, add(): (left.astype(jnp.float32) + right.astype(jnp.float32)).astype(jnp.bfloat16)  22.9 us
    pallas_call x2, Pallas kernels, grad_second_half(): pl.pallas_call(grad_second_kernel, out_shape=jax.ShapeDtypeStruct((rows,...  16 us
    pallas_call x1, Pallas kernels, attention_forward(): pl.pallas_call(functools.partial(forward_kernel, rep, kv_heads, ctx_count...  15.5 us
    unnamed x136, local copies, waits for them, and re-layouts  15.2 us
  transfers between devices with their start and end apart: 53, of which 36 were waited for; matrix products, arithmetic and copies ran while one was open for 13% of the time, Pallas kernels for 17%

profile of v15, /device:TPU:0, one launch (start us, length us, event | category | flops | bytes accessed | tf_op | source)
XLA Modules:
  0.0 585.3 jit_solution(34931684469583891)
XLA Ops:
  13.0 7.2 %input_stage.1 = (bf16[512,2048]{1,0:T(8,128)(2,1)}, bf16[512,512]{1,0:T(8,128)(2,1)}, bf16[512,512]{1,0:T(8,128)(2,1)S(1)}, f32[512,128]{1,0:T(8,128)}, f32[512,128]{1,0:T(8,128)}) custom-call(s32[32]{0:T(128)} %order_ref.7, s32[8]{0:T(128)} %cont_ref.7, s32[2]{0:T(128)S(1)} %pad_add_fusion.where_ref, f32[1,2048]{1,0:T(1,128)} %bitcast.38, ...), custom_call_target="tpu_custom_call" | custom-call | flops 42949672 | bytes 167772 | tf_op jit(solution)/shard_map/input_stage/pallas_call | solution.py:513
  20.2 4.0 collective-permute-done.27
  24.2 25.6 %conditional.10 = (bf16[512,512]{1,0:T(8,128)(2,1)}, bf16[512,512]{1,0:T(8,128)(2,1)}, bf16[512,512]{1,0:T(8,128)(2,1)}) conditional(s32[]{:T(128)} %bitcast.2, () %tuple.140, bf16[512,512]{1,0:T(8,128)(2,1)S(1)} %get-tuple-element.243.refs_0_), branch_computations={%region_0.0_spmd, %region_1.0_spmd} | conditional | bytes 6291600 | solution.py:896
  30.0 19.6 %collective-permute-done = bf16[512,512]{1,0:T(8,128)(2,1)} collective-permute-done((bf16[512,512]{1,0:T(8,128)(2,1)S(1)}, bf16[512,512]{1,0:T(8,128)(2,1)}, u32[]{:S(2)}, u32[]{:S(2)}) %collective-permute-start) | collective-permute-done | bytes 524320 | tf_op jit(solution)/shard_map/cond/branch_1_fun/ppermute | solution.py:860
  49.8 25.2 %conditional.11 = (bf16[512,512]{1,0:T(8,128)(2,1)}, bf16[128,2048]{1,0:T(8,128)(2,1)}, bf16[512,512]{1,0:T(8,128)(2,1)}, bf16[512,512]{1,0:T(8,128)(2,1)}) conditional(s32[]{:T(128)} %bitcast.2, () %tuple.142, (bf16[512,512]{1,0:T(8,128)(2,1)}, bf16[128,2048]{1,0:T(8,128)(2,1)S(1)}, bf16[512,512]{1,0:T(8,128)(2,1)}) %tuple.143), branch_computations={%region_2.0_spmd, %region_3.0_spmd} | conditional | bytes 8388800 | solution.py:896
  54.6 8.2 %collective-permute-done.5 = bf16[512,512]{1,0:T(8,128)(2,1)} collective-permute-done((bf16[512,512]{1,0:T(8,128)(2,1)}, bf16[512,512]{1,0:T(8,128)(2,1)}, u32[]{:S(2)}, u32[]{:S(2)}) %collective-permute-start.5) | collective-permute-done | bytes 524320 | tf_op jit(solution)/shard_map/cond/branch_1_fun/ppermute | solution.py:860
  66.3 8.8 %collective-permute-done.3 = bf16[512,512]{1,0:T(8,128)(2,1)} collective-permute-done((bf16[512,512]{1,0:T(8,128)(2,1)}, bf16[512,512]{1,0:T(8,128)(2,1)}, u32[]{:S(2)}, u32[]{:S(2)}) %collective-permute-start.3) | collective-permute-done | bytes 524320 | tf_op jit(solution)/shard_map/cond/branch_1_fun/ppermute | solution.py:860
  76.2 14.9 %conditional.12 = (bf16[512,512]{1,0:T(8,128)(2,1)}, bf16[256,2048]{1,0:T(8,128)(2,1)}, bf16[128,2048]{1,0:T(8,128)(2,1)S(1)}, bf16[128,2048]{1,0:T(8,128)(2,1)S(1)}) conditional(s32[]{:T(128)} %bitcast.2, () %tuple.144, (bf16[512,512]{1,0:T(8,128)(2,1)}, bf16[256,2048]{1,0:T(8,128)(2,1)S(1)}) %tuple.145), branch_computations={%region_4.0_spmd, %region_5.0_spmd} | conditional | bytes 8388720 | solution.py:896
  80.4 10.6 %collective-permute-done.25 = bf16[512,512]{1,0:T(8,128)(2,1)} collective-permute-done((bf16[512,512]{1,0:T(8,128)(2,1)}, bf16[512,512]{1,0:T(8,128)(2,1)}, u32[]{:S(2)}, u32[]{:S(2)}) %collective-permute-start.25) | collective-permute-done | bytes 524320 | tf_op jit(solution)/shard_map/cond/branch_1_fun/ppermute | solution.py:860
  92.2 15.5 %attention_forward.1 = (bf16[512,512]{1,0:T(8,128)(2,1)S(1)}, f32[2,4,256]{2,1,0:T(4,128)S(1)}, bf16[256,2048]{1,0:T(8,128)(2,1)S(1)}, bf16[256,2048]{1,0:T(8,128)(2,1)S(1)}) custom-call(s32[32]{0:T(128)S(1)} %copy-done.17, s32[8]{0:T(128)S(1)} %copy-done.18, s32[2]{0:T(128)S(1)} %pad_add_fusion.where_ref, bf16[512,512]{1,0:T(8,128)(2,1)S(1)} %copy-done.4, ...), custom_call_target="tpu_custom_call" | custom-call | flops 64424508 | bytes 167772 | tf_op jit(solution)/shard_map/attention_forward/pallas_call | solution.py:368
  112.6 8.0 %grad_hidden.1.gh_ref = f32[1024,1024]{1,0:T(8,128)S(1)} custom-call(s32[2]{0:T(128)S(1)} %pad_add_fusion.where_ref, bf16[1024,2048]{1,0:T(8,128)(2,1)S(1)} %constant_dynamic-update-slice_fusion.2.cot_ref.left_ref, bf16[2048,2048]{1,0:T(8,128)(2,1)} %wd_ref.1), custom_call_target="tpu_custom_call" | custom-call | flops 68719476736 | bytes 134217728 | tf_op jit(solution)/shard_map/grad_hidden/pallas_call | solution.py:571
  120.6 4.4 collective-permute-done.29
  131.0 10.2 %collective-permute-done.30 = bf16[128,2048]{1,0:T(8,128)(2,1)S(1)} collective-permute-done((bf16[128,2048]{1,0:T(8,128)(2,1)S(1)}, bf16[128,2048]{1,0:T(8,128)(2,1)S(1)}, u32[]{:S(2)}, u32[]{:S(2)}) %collective-permute-start.30) | collective-permute-done | bytes 524320 | tf_op jit(solution)/shard_map/ppermute | solution.py:860
  142.7 11.1 %collective-permute-done.32 = bf16[128,2048]{1,0:T(8,128)(2,1)S(1)} collective-permute-done((bf16[128,2048]{1,0:T(8,128)(2,1)S(1)}, bf16[128,2048]{1,0:T(8,128)(2,1)S(1)}, u32[]{:S(2)}, u32[]{:S(2)}) %collective-permute-start.32) | collective-permute-done | bytes 524320 | tf_op jit(solution)/shard_map/ppermute | solution.py:860
  154.3 4.0 collective-permute-done.33
  158.6 13.7 %ffn_stage.1 = (bf16[1024,1024]{1,0:T(8,128)(2,1)S(1)}, bf16[1024,1024]{1,0:T(8,128)(2,1)}, bf16[1024,1024]{1,0:T(8,128)(2,1)S(1)}) custom-call(s32[2]{0:T(128)S(1)} %pad_add_fusion.where_ref, bf16[1024,2048]{1,0:T(8,128)(2,1)S(1)} %constant_dynamic-update-slice_fusion.7.in_ref, f32[1024,1024]{1,0:T(8,128)S(1)} %grad_hidden.1.gh_ref, ...), custom_call_target="tpu_custom_call" | custom-call | flops 171798688 | bytes 251658 | tf_op jit(solution)/shard_map/ffn_stage/pallas_call | solution.py:610
  173.7 7.1 %down_shares.1 = bf16[8,256,1024]{2,1,0:T(8,128)(2,1)S(1)} custom-call(s32[2]{0:T(128)S(1)} %pad_add_fusion.where_ref, bf16[1024,2048]{1,0:T(8,128)(2,1)S(1)} %constant_dynamic-update-slice_fusion.2.cot_ref.left_ref, bf16[1024,1024]{1,0:T(8,128)(2,1)S(1)} %get-tuple-element.258.right_ref), custom_call_target="tpu_custom_call" | custom-call | flops 85899344 | bytes 167772 | tf_op jit(solution)/shard_map/down_shares/pallas_call | solution.py:790
  182.9 8.3 %grad_second_send.1 = bf16[512,2048]{1,0:T(8,128)(2,1)S(1)} custom-call(s32[2]{0:T(128)S(1)} %pad_add_fusion.where_ref, bf16[1024,1024]{1,0:T(8,128)(2,1)} %get-tuple-element.261.gg_ref, bf16[1024,1024]{1,0:T(8,128)(2,1)S(1)} %get-tuple-element.262.gu_ref, bf16[2048,2048]{1,0:T(8,128)(2,1)} %wg_ref.3, bf16[2048,2048]{1,0:T(8,128)(2,1)} %wu_ref.3), custom_call_target="tpu_custom_call" | custom-call | flops 85899344 | bytes 83886 | tf_op jit(solution)/shard_map/grad_second_send/pallas_call | solution.py:642
  191.2 54.7 %conditional.13 = (f32[128,2048]{1,0:T(8,128)}, bf16[8,256,1024]{2,1,0:T(8,128)(2,1)}, bf16[512,2048]{1,0:T(8,128)(2,1)}, bf16[512,2048]{1,0:T(8,128)(2,1)}) conditional(s32[]{:T(128)} %bitcast.2, () %tuple.151, (s32[2]{0:T(128)S(1)}, bf16[1024,1024]{1,0:T(8,128)(2,1)S(1)}, bf16[1024,1024]{1,0:T(8,128)(2,1)S(1)}, bf16[2048,2048]{1,0:T(8,128)(2,1)}, ...), branch_computations={%region_7.0_spmd, %region_8.0_spmd} | conditional | flops 264251632 | bytes 49702740 | solution.py:896
  191.7 7.7 %grad_second_keep.1 = bf16[512,2048]{1,0:T(8,128)(2,1)S(1)} custom-call(s32[2]{0:T(128)S(1)} %get-tuple-element.80.where_ref, bf16[1024,1024]{1,0:T(8,128)(2,1)S(1)} %get-tuple-element.87.gg_ref.right_ref, bf16[1024,1024]{1,0:T(8,128)(2,1)S(1)} %get-tuple-element.82.gu_ref, bf16[2048,2048]{1,0:T(8,128)(2,1)} %get-tuple-element.83.wg_ref, ...), custom_call_target="tpu_custom_call" | custom-call | flops 85899344 | bytes 83886 | tf_op jit(solution)/shard_map/cond/branch_1_fun/grad_second_keep/pallas_call | solution.py:642
  202.1 7.9 %gate_shares.1 = bf16[8,256,1024]{2,1,0:T(8,128)(2,1)} custom-call(s32[2]{0:T(128)S(1)} %get-tuple-element.80.where_ref, bf16[1024,2048]{1,0:T(8,128)(2,1)S(1)} %get-tuple-element.86.left_ref, bf16[1024,1024]{1,0:T(8,128)(2,1)S(1)} %get-tuple-element.87.gg_ref.right_ref), custom_call_target="tpu_custom_call" | custom-call | flops 85899344 | bytes 167772 | tf_op jit(solution)/shard_map/cond/branch_1_fun/gate_shares/pallas_call | solution.py:790
  210.0 4.8 collective-permute-done.15
  216.5 6.8 %ffn_out.1 = (bf16[512,2048]{1,0:T(8,128)(2,1)}, bf16[512,2048]{1,0:T(8,128)(2,1)}) custom-call(s32[2]{0:T(128)S(1)} %get-tuple-element.80.where_ref, bf16[1024,1024]{1,0:T(8,128)(2,1)S(1)} %get-tuple-element.90.hid_ref, bf16[2048,2048]{1,0:T(8,128)(2,1)S(1)} %bitcast.37), custom_call_target="tpu_custom_call" | custom-call | flops 85899344 | bytes 167772 | tf_op jit(solution)/shard_map/cond/branch_1_fun/ffn_out/pallas_call | solution.py:675
  225.5 19.3 %collective-permute-done.17 = bf16[128,2048]{1,0:T(8,128)(2,1)S(1)} collective-permute-done((bf16[128,2048]{1,0:T(8,128)(2,1)S(1)}, bf16[128,2048]{1,0:T(8,128)(2,1)S(1)}, u32[]{:S(2)}, u32[]{:S(2)}) %collective-permute-start.17) | collective-permute-done | bytes 524320 | tf_op jit(solution)/shard_map/cond/branch_1_fun/ppermute | solution.py:860
  246.0 20.7 %conditional.14 = (f32[128,2048]{1,0:T(8,128)}, bf16[8,256,1024]{2,1,0:T(8,128)(2,1)}, bf16[512,2048]{1,0:T(8,128)(2,1)S(1)}, f32[1,2048]{1,0:T(1,128)S(1)}) conditional(s32[]{:T(128)} %bitcast.2, () %tuple.150, (bf16[128,2048]{1,0:T(8,128)(2,1)}, f32[128]{0:T(128)S(1)}, f32[2048]{0:T(1024)S(1)}, f32[128,2048]{1,0:T(8,128)}, ...), branch_computations={%region_9.0_spmd, %region_10.13_spmd} | conditional | flops 97431632 | bytes 37943812 | solution.py:896
  251.5 8.0 %up_shares.1 = bf16[8,256,1024]{2,1,0:T(8,128)(2,1)} custom-call(s32[2]{0:T(128)S(1)} %get-tuple-element.102.where_ref, bf16[1024,2048]{1,0:T(8,128)(2,1)S(1)} %copy-done.21, bf16[1024,1024]{1,0:T(8,128)(2,1)S(1)} %get-tuple-element.105.right_ref), custom_call_target="tpu_custom_call" | custom-call | flops 85899344 | bytes 167772 | tf_op jit(solution)/shard_map/cond/branch_1_fun/up_shares/pallas_call | solution.py:790
  259.4 4.3 collective-permute-done.23
  266.8 13.5 %attention_backward_0.1 = (bf16[512,256]{1,0:T(8,128)(2,1)}, bf16[2048,256]{1,0:T(8,128)(2,1)}, bf16[2048,256]{1,0:T(8,128)(2,1)}) custom-call(s32[32]{0:T(128)} %order_ref.7, s32[8]{0:T(128)} %cont_ref.7, s32[2]{0:T(128)S(1)} %pad_add_fusion.where_ref, bf16[512,512]{1,0:T(8,128)(2,1)} %get-tuple-element.241.q_ref, ...), custom_call_target="tpu_custom_call" | custom-call | flops 64424508 | bytes 125829 | tf_op jit(solution)/shard_map/attention_backward_0/pallas_call | solution.py:404
  285.7 14.2 %attention_backward_1.1 = (bf16[512,256]{1,0:T(8,128)(2,1)}, bf16[2048,256]{1,0:T(8,128)(2,1)}, bf16[2048,256]{1,0:T(8,128)(2,1)}) custom-call(s32[32]{0:T(128)} %order_ref.7, s32[8]{0:T(128)} %cont_ref.7, s32[2]{0:T(128)S(1)} %pad_add_fusion.where_ref, bf16[512,512]{1,0:T(8,128)(2,1)} %get-tuple-element.241.q_ref, bf16[512,2048]{1,0:T(8,128)(2,1)} %copy-done.22, ...), custom_call_target="tpu_custom_call" | custom-call | flops 64424508 | bytes 125829 | tf_op jit(solution)/shard_map/attention_backward_1/pallas_call | solution.py:404
  302.0 8.5 %branch_shares.1 = (bf16[4,256,1024]{2,1,0:T(8,128)(2,1)S(1)}, bf16[4,256,1024]{2,1,0:T(8,128)(2,1)}) custom-call(s32[2]{0:T(128)S(1)} %pad_add_fusion.where_ref, bf16[512,2048]{1,0:T(8,128)(2,1)S(1)} %copy-done.11, bf16[512,2048]{1,0:T(8,128)(2,1)} %copy-done.22, bf16[512,256]{1,0:T(8,128)(2,1)S(1)} %copy-done.13, bf16[512,256]{1,0:T(8,128)(2,1)S(1)} %copy-done.14, ...), custom_call_target="tpu_custom_call" | custom-call | flops 42949672 | bytes 83886 | tf_op jit(solution)/shard_map/branch_shares/pallas_call | solution.py:746
  310.5 17.9 %collective-permute-done.34 = bf16[2048,256]{1,0:T(8,128)(2,1)} collective-permute-done((bf16[2048,256]{1,0:T(8,128)(2,1)}, bf16[2048,256]{1,0:T(8,128)(2,1)}, u32[]{:S(2)}, u32[]{:S(2)}) %collective-permute-start.34) | collective-permute-done | bytes 1048608 | tf_op jit(solution)/shard_map/ppermute | solution.py:860
  328.4 33.4 %collective-permute-done.35 = bf16[2048,256]{1,0:T(8,128)(2,1)S(1)} collective-permute-done((bf16[2048,256]{1,0:T(8,128)(2,1)}, bf16[2048,256]{1,0:T(8,128)(2,1)S(1)}, u32[]{:S(2)}, u32[]{:S(2)}) %collective-permute-start.35) | collective-permute-done | bytes 1048608 | tf_op jit(solution)/shard_map/ppermute | solution.py:860
  370.6 21.8 %conditional.15 = (bf16[128,2048]{1,0:T(8,128)(2,1)S(1)}, bf16[128,2048]{1,0:T(8,128)(2,1)S(1)}, bf16[128,2048]{1,0:T(8,128)(2,1)S(1)}) conditional(s32[]{:T(128)} %bitcast.2, () %tuple.149, (bf16[512,2048]{1,0:T(8,128)(2,1)}, bf16[512,2048]{1,0:T(8,128)(2,1)}) %tuple.162), branch_computations={%region_14.15_spmd, %region_15.16_spmd} | conditional | flops 5242880 | bytes 17301608 | solution.py:896
  370.9 4.4 collective-permute-done.18
  378.2 12.2 %collective-permute-done.19 = bf16[128,2048]{1,0:T(8,128)(2,1)S(1)} collective-permute-done((bf16[128,2048]{1,0:T(8,128)(2,1)S(1)}, bf16[128,2048]{1,0:T(8,128)(2,1)S(1)}, u32[]{:S(2)}, u32[]{:S(2)}) %collective-permute-start.19) | collective-permute-done | bytes 524320 | tf_op jit(solution)/shard_map/cond/branch_1_fun/ppermute | solution.py:860
  394.0 21.1 %collective-permute-done.37 = bf16[1024,256]{1,0:T(8,128)(2,1)} collective-permute-done((bf16[1024,256]{1,0:T(8,128)(2,1)}, bf16[1024,256]{1,0:T(8,128)(2,1)}, u32[]{:S(2)}, u32[]{:S(2)}) %collective-permute-start.37) | collective-permute-done | bytes 524320 | tf_op jit(solution)/shard_map/ppermute | solution.py:860
  424.4 31.2 %conditional.16 = (bf16[128,2048]{1,0:T(8,128)(2,1)}, bf16[128,2048]{1,0:T(8,128)(2,1)}) conditional(s32[]{:T(128)} %bitcast.2, () %tuple.148, (bf16[128,2048]{1,0:T(8,128)(2,1)S(1)}, bf16[128,2048]{1,0:T(8,128)(2,1)S(1)}) %tuple.264), branch_computations={%region_17.18_spmd, %region_18.19_spmd} | conditional | bytes 4194400 | solution.py:896
  428.3 27.3 %collective-permute-done.7 = bf16[128,2048]{1,0:T(8,128)(2,1)} collective-permute-done((bf16[128,2048]{1,0:T(8,128)(2,1)S(1)}, bf16[128,2048]{1,0:T(8,128)(2,1)}, u32[]{:S(2)}, u32[]{:S(2)}) %collective-permute-start.7) | collective-permute-done | bytes 524320 | tf_op jit(solution)/shard_map/cond/branch_1_fun/ppermute | solution.py:860
  458.2 4.7 add_convert_fusion.13
  467.3 4.2 tail_stage.1
  471.7 5.1 kv_shares.1
  478.6 20.3 %conditional.17 = (bf16[128,2048]{1,0:T(8,128)(2,1)S(1)}, f32[1,2048]{1,0:T(1,128)S(1)}) conditional(s32[]{:T(128)} %bitcast.2, () %tuple.139, (f32[128,2048]{1,0:T(8,128)}, bf16[256,2048]{1,0:T(8,128)(2,1)}, bf16[256,2048]{1,0:T(8,128)(2,1)}, f32[2048]{0:T(1024)S(1)}, f32[128,2048]{1,0:T(8,128)}) %tuple.265), branch_computations={%region_19.20_spmd, %region_20.24_spmd} | conditional | flops 8648832 | bytes 24146584 | solution.py:896
  484.3 12.3 %collective-permute-done.21 = bf16[128,2048]{1,0:T(8,128)(2,1)S(1)} collective-permute-done((bf16[128,2048]{1,0:T(8,128)(2,1)S(1)}, bf16[128,2048]{1,0:T(8,128)(2,1)S(1)}, u32[]{:S(2)}, u32[]{:S(2)}) %collective-permute-start.21) | collective-permute-done | bytes 524320 | tf_op jit(solution)/shard_map/cond/branch_1_fun/ppermute | solution.py:860
  515.7 24.8 %conditional.18 = (f32[2,2048]{1,0:T(2,128)S(1)}) conditional(s32[]{:T(128)} %bitcast.2, () %tuple.178, f32[2,2048]{1,0:T(2,128)S(1)} %pad_maximum_fusion.5), branch_computations={%region_24.25_spmd, %region_25.26_spmd} | conditional | flops 20480 | bytes 573648 | solution.py:896
  517.5 8.5 %collective-permute-done.10 = f32[2,2048]{1,0:T(2,128)S(1)} collective-permute-done((f32[2,2048]{1,0:T(2,128)S(1)}, f32[2,2048]{1,0:T(2,128)S(1)}, u32[]{:S(2)}, u32[]{:S(2)}) %collective-permute-start.10) | collective-permute-done | bytes 16416 | tf_op jit(solution)/shard_map/cond/branch_1_fun/ppermute | solution.py:860
  534.3 4.5 collective-permute-start.13
  544.9 9.1 %conditional.19 = (bf16[512,2048]{1,0:T(8,128)(2,1)}, bf16[512,2048]{1,0:T(8,128)(2,1)}) conditional(s32[]{:T(128)} %bitcast.2, () %tuple.138, (bf16[256,2048]{1,0:T(8,128)(2,1)}, bf16[256,2048]{1,0:T(8,128)(2,1)}) %tuple.188), branch_computations={%region_26.27_spmd, %region_27.28_spmd} | conditional | bytes 12582968 | solution.py:896
  549.5 4.5 collective-permute-done.22
  (304 shorter events, 172.7 us)
Async XLA Ops:
  7.2 276.2 %reduce-scatter.4.cloned.1.call-start = ((), (), s32[]{:S(2)}) async-start(), calls=%async_computation.3 | async-start | bytes 5242880 | tf_op jit(solution)/shard_map/reduce_scatter | solution.py:972
  9.2 14.9 %collective-permute-start.27 = (bf16[128,2048]{1,0:T(8,128)(2,1)S(1)}, bf16[128,2048]{1,0:T(8,128)(2,1)S(1)}, u32[]{:S(2)}, u32[]{:S(2)}) collective-permute-start(bf16[128,2048]{1,0:T(8,128)(2,1)S(1)} %get-tuple-element.384), channel_id=1, source_target_pairs={{0,8},{8,0},{1,9},{9,1},{2,10},{10,2},{3,11},{11,3},{4,12},{12,4},... | collective-permute-start | bytes 1572872 | tf_op jit(solution)/shard_map/ppermute | solution.py:860
  24.2 25.5 %collective-permute-start = (bf16[512,512]{1,0:T(8,128)(2,1)S(1)}, bf16[512,512]{1,0:T(8,128)(2,1)}, u32[]{:S(2)}, u32[]{:S(2)}) collective-permute-start(bf16[512,512]{1,0:T(8,128)(2,1)S(1)} %param.1), channel_id=1, source_target_pairs={{0,16},{16,0},{1,17},{17,1},{2,18},{18,2},{3,19},{19,3},{4,20},{20... | collective-permute-start | bytes 1572872 | tf_op jit(solution)/shard_map/cond/branch_1_fun/ppermute | solution.py:860
  26.9 22.9 %collective-permute-start.1 = (bf16[512,512]{1,0:T(8,128)(2,1)S(1)}, bf16[512,512]{1,0:T(8,128)(2,1)}, u32[]{:S(2)}, u32[]{:S(2)}) collective-permute-start(bf16[512,512]{1,0:T(8,128)(2,1)S(1)} %param.1), channel_id=1, source_target_pairs={{0,8},{8,0},{1,9},{9,1},{2,10},{10,2},{3,11},{11,3},{4,12},{12,4},... | collective-permute-start | bytes 1572872 | tf_op jit(solution)/shard_map/cond/branch_1_fun/ppermute | solution.py:860
  28.5 21.3 %collective-permute-start.2 = (bf16[512,512]{1,0:T(8,128)(2,1)S(1)}, bf16[512,512]{1,0:T(8,128)(2,1)}, u32[]{:S(2)}, u32[]{:S(2)}) collective-permute-start(bf16[512,512]{1,0:T(8,128)(2,1)S(1)} %param.1), channel_id=1, source_target_pairs={{0,4},{4,0},{1,5},{5,1},{2,6},{6,2},{3,7},{7,3},{8,12},{12,8},{9,1... | collective-permute-start | bytes 1572872 | tf_op jit(solution)/shard_map/cond/branch_1_fun/ppermute | solution.py:860
  49.8 13.0 %collective-permute-start.5 = (bf16[512,512]{1,0:T(8,128)(2,1)}, bf16[512,512]{1,0:T(8,128)(2,1)}, u32[]{:S(2)}, u32[]{:S(2)}) collective-permute-start(bf16[512,512]{1,0:T(8,128)(2,1)} %get-tuple-element.77), channel_id=1, source_target_pairs={{0,8},{8,0},{1,9},{9,1},{2,10},{10,2},{3,11},{11,3},{4,12},{12,4},... | collective-permute-start | bytes 1572872 | tf_op jit(solution)/shard_map/cond/branch_1_fun/ppermute | solution.py:860
  51.1 15.2 %collective-permute-start.6 = (bf16[512,512]{1,0:T(8,128)(2,1)}, bf16[512,512]{1,0:T(8,128)(2,1)}, u32[]{:S(2)}, u32[]{:S(2)}) collective-permute-start(bf16[512,512]{1,0:T(8,128)(2,1)} %get-tuple-element.77), channel_id=1, source_target_pairs={{0,4},{4,0},{1,5},{5,1},{2,6},{6,2},{3,7},{7,3},{8,12},{12,8},{9,1... | collective-permute-start | bytes 1572872 | tf_op jit(solution)/shard_map/cond/branch_1_fun/ppermute | solution.py:860
  52.6 22.5 %collective-permute-start.3 = (bf16[512,512]{1,0:T(8,128)(2,1)}, bf16[512,512]{1,0:T(8,128)(2,1)}, u32[]{:S(2)}, u32[]{:S(2)}) collective-permute-start(bf16[512,512]{1,0:T(8,128)(2,1)} %get-tuple-element.75), channel_id=1, source_target_pairs={{0,4},{4,0},{1,5},{5,1},{2,6},{6,2},{3,7},{7,3},{8,12},{12,8},{9,1... | collective-permute-start | bytes 1572872 | tf_op jit(solution)/shard_map/cond/branch_1_fun/ppermute | solution.py:860
  53.1 21.9 %collective-permute-start.4 = (bf16[128,2048]{1,0:T(8,128)(2,1)S(1)}, bf16[128,2048]{1,0:T(8,128)(2,1)}, u32[]{:S(2)}, u32[]{:S(2)}) collective-permute-start(bf16[128,2048]{1,0:T(8,128)(2,1)S(1)} %get-tuple-element.76), channel_id=1, source_target_pairs={{0,2},{2,0},{1,3},{3,1},{4,6},{6,4},{5,7},{7,5},{8,10},{10,8},{9,1... | collective-permute-start | bytes 1572872 | tf_op jit(solution)/shard_map/cond/branch_1_fun/ppermute | solution.py:860
  76.3 14.7 %collective-permute-start.25 = (bf16[512,512]{1,0:T(8,128)(2,1)}, bf16[512,512]{1,0:T(8,128)(2,1)}, u32[]{:S(2)}, u32[]{:S(2)}) collective-permute-start(bf16[512,512]{1,0:T(8,128)(2,1)} %get-tuple-element.78), channel_id=1, source_target_pairs={{0,4},{4,0},{1,5},{5,1},{2,6},{6,2},{3,7},{7,3},{8,12},{12,8},{9,1... | collective-permute-start | bytes 1572872 | tf_op jit(solution)/shard_map/cond/branch_1_fun/ppermute | solution.py:860
  111.0 14.0 %collective-permute-start.29 = (bf16[128,2048]{1,0:T(8,128)(2,1)S(1)}, bf16[128,2048]{1,0:T(8,128)(2,1)S(1)}, u32[]{:S(2)}, u32[]{:S(2)}) collective-permute-start(bf16[128,2048]{1,0:T(8,128)(2,1)S(1)} %slice.223), channel_id=1, source_target_pairs={{0,2},{2,0},{1,3},{3,1},{4,6},{6,4},{5,7},{7,5},{8,10},{10,8},{9,1... | collective-permute-start | bytes 1572872 | tf_op jit(solution)/shard_map/ppermute | solution.py:860
  126.8 14.3 %collective-permute-start.30 = (bf16[128,2048]{1,0:T(8,128)(2,1)S(1)}, bf16[128,2048]{1,0:T(8,128)(2,1)S(1)}, u32[]{:S(2)}, u32[]{:S(2)}) collective-permute-start(bf16[128,2048]{1,0:T(8,128)(2,1)S(1)} %get-tuple-element.381), channel_id=1, source_target_pairs={{0,8},{8,0},{1,9},{9,1},{2,10},{10,2},{3,11},{11,3},{4,12},{12,4},... | collective-permute-start | bytes 1572872 | tf_op jit(solution)/shard_map/ppermute | solution.py:860
  129.8 13.0 %collective-permute-start.31 = (bf16[128,2048]{1,0:T(8,128)(2,1)S(1)}, bf16[128,2048]{1,0:T(8,128)(2,1)S(1)}, u32[]{:S(2)}, u32[]{:S(2)}) collective-permute-start(bf16[128,2048]{1,0:T(8,128)(2,1)S(1)} %get-tuple-element.381), channel_id=1, source_target_pairs={{0,2},{2,0},{1,3},{3,1},{4,6},{6,4},{5,7},{7,5},{8,10},{10,8},{9,1... | collective-permute-start | bytes 1572872 | tf_op jit(solution)/shard_map/ppermute | solution.py:860
  141.2 12.7 %collective-permute-start.32 = (bf16[128,2048]{1,0:T(8,128)(2,1)S(1)}, bf16[128,2048]{1,0:T(8,128)(2,1)S(1)}, u32[]{:S(2)}, u32[]{:S(2)}) collective-permute-start(bf16[128,2048]{1,0:T(8,128)(2,1)S(1)} %collective-permute-done.30), channel_id=1, source_target_pairs={{0,2},{2,0},{1,3},{3,1},{4,6},{6,4},{5,7},{7,5},{8,10},{10,8},{9,1... | collective-permute-start | bytes 1572872 | tf_op jit(solution)/shard_map/ppermute | solution.py:860
  154.1 4.2 collective-permute-start.33
  182.8 236.2 %reduce-scatter.6.cloned.1.call-start = ((), (), s32[]{:S(2)}) async-start(), calls=%async_computation.4 | async-start | bytes 5242880 | tf_op jit(solution)/shard_map/reduce_scatter | solution.py:972
  191.4 7.9 %collective-permute-start.14 = (bf16[512,2048]{1,0:T(8,128)(2,1)S(1)}, bf16[512,2048]{1,0:T(8,128)(2,1)S(1)}, u32[]{:S(2)}, u32[]{:S(2)}) collective-permute-start(bf16[512,2048]{1,0:T(8,128)(2,1)S(1)} %get-tuple-element.85), channel_id=1, source_target_pairs={{0,1},{1,0},{2,3},{3,2},{4,5},{5,4},{6,7},{7,6},{8,9},{9,8},{10,11... | collective-permute-start | bytes 6291464 | tf_op jit(solution)/shard_map/cond/branch_1_fun/ppermute | solution.py:860
  200.0 14.8 %collective-permute-start.15 = (bf16[128,2048]{1,0:T(8,128)(2,1)S(1)}, bf16[128,2048]{1,0:T(8,128)(2,1)S(1)}, u32[]{:S(2)}, u32[]{:S(2)}) collective-permute-start(bf16[128,2048]{1,0:T(8,128)(2,1)S(1)} %get-tuple-element.389), channel_id=1, source_target_pairs={{0,2},{2,0},{1,3},{3,1},{4,6},{6,4},{5,7},{7,5},{8,10},{10,8},{9,1... | collective-permute-start | bytes 1572872 | tf_op jit(solution)/shard_map/cond/branch_1_fun/ppermute | solution.py:860
  201.4 24.1 %collective-permute-start.16 = (bf16[128,2048]{1,0:T(8,128)(2,1)S(1)}, bf16[128,2048]{1,0:T(8,128)(2,1)S(1)}, u32[]{:S(2)}, u32[]{:S(2)}) collective-permute-start(bf16[128,2048]{1,0:T(8,128)(2,1)S(1)} %get-tuple-element.387), channel_id=1, source_target_pairs={{0,2},{2,0},{1,3},{3,1},{4,6},{6,4},{5,7},{7,5},{8,10},{10,8},{9,1... | collective-permute-start | bytes 1572872 | tf_op jit(solution)/shard_map/cond/branch_1_fun/ppermute | solution.py:860
  215.1 29.7 %collective-permute-start.17 = (bf16[128,2048]{1,0:T(8,128)(2,1)S(1)}, bf16[128,2048]{1,0:T(8,128)(2,1)S(1)}, u32[]{:S(2)}, u32[]{:S(2)}) collective-permute-start(bf16[128,2048]{1,0:T(8,128)(2,1)S(1)} %add_convert_fusion.2), channel_id=1, source_target_pairs={{0,8},{8,0},{1,9},{9,1},{2,10},{10,2},{3,11},{11,3},{4,12},{12,4},... | collective-permute-start | bytes 1572872 | tf_op jit(solution)/shard_map/cond/branch_1_fun/ppermute | solution.py:860
  246.0 313.4 %reduce-scatter.8.cloned.1.call-start = ((), (), s32[]{:S(2)}) async-start(), calls=%async_computation.5 | async-start | bytes 5242880 | tf_op jit(solution)/shard_map/reduce_scatter | solution.py:972
  250.3 13.5 %collective-permute-start.23 = (bf16[128,2048]{1,0:T(8,128)(2,1)S(1)}, bf16[128,2048]{1,0:T(8,128)(2,1)S(1)}, u32[]{:S(2)}, u32[]{:S(2)}) collective-permute-start(bf16[128,2048]{1,0:T(8,128)(2,1)S(1)} %get-tuple-element.378), channel_id=1, source_target_pairs={{0,2},{2,0},{1,3},{3,1},{4,6},{6,4},{5,7},{7,5},{8,10},{10,8},{9,1... | collective-permute-start | bytes 1572872 | tf_op jit(solution)/shard_map/cond/branch_1_fun/ppermute | solution.py:860
  280.3 48.1 %collective-permute-start.34 = (bf16[2048,256]{1,0:T(8,128)(2,1)}, bf16[2048,256]{1,0:T(8,128)(2,1)}, u32[]{:S(2)}, u32[]{:S(2)}) collective-permute-start(bf16[2048,256]{1,0:T(8,128)(2,1)} %get-tuple-element.276), channel_id=1, source_target_pairs={{0,4},{4,0},{1,5},{5,1},{2,6},{6,2},{3,7},{7,3},{8,12},{12,8},{9,1... | collective-permute-start | bytes 3145736 | tf_op jit(solution)/shard_map/ppermute | solution.py:860
  299.8 62.0 %collective-permute-start.35 = (bf16[2048,256]{1,0:T(8,128)(2,1)}, bf16[2048,256]{1,0:T(8,128)(2,1)S(1)}, u32[]{:S(2)}, u32[]{:S(2)}) collective-permute-start(bf16[2048,256]{1,0:T(8,128)(2,1)} %get-tuple-element.280), channel_id=1, source_target_pairs={{0,4},{4,0},{1,5},{5,1},{2,6},{6,2},{3,7},{7,3},{8,12},{12,8},{9,1... | collective-permute-start | bytes 3145736 | tf_op jit(solution)/shard_map/ppermute | solution.py:860
  301.1 63.5 %collective-permute-start.36 = (bf16[256,1024]{1,0:T(8,128)(2,1)}, bf16[256,1024]{1,0:T(8,128)(2,1)}, u32[]{:S(2)}, u32[]{:S(2)}) collective-permute-start(bf16[256,1024]{1,0:T(8,128)(2,1)} %get-tuple-element.426), channel_id=1, source_target_pairs={{0,8},{8,0},{1,9},{9,1},{2,10},{10,2},{3,11},{11,3},{4,12},{12,4},... | collective-permute-start | bytes 1572872 | tf_op jit(solution)/shard_map/ppermute | solution.py:860
  368.2 90.0 %collective-permute-start.39 = (bf16[4,256,1024]{2,1,0:T(8,128)(2,1)}, bf16[4,256,1024]{2,1,0:T(8,128)(2,1)}, u32[]{:S(2)}, u32[]{:S(2)}) collective-permute-start(bf16[4,256,1024]{2,1,0:T(8,128)(2,1)} %get-tuple-element.303), channel_id=1, source_target_pairs={{0,4},{4,0},{1,5},{5,1},{2,6},{6,2},{3,7},{7,3},{8,12},{12,8},{9,1... | collective-permute-start | bytes 6291464 | tf_op jit(solution)/shard_map/ppermute | solution.py:860
  368.6 25.4 %collective-permute-start.38 = (bf16[1024,256]{1,0:T(8,128)(2,1)}, bf16[1024,256]{1,0:T(8,128)(2,1)}, u32[]{:S(2)}, u32[]{:S(2)}) collective-permute-start(bf16[1024,256]{1,0:T(8,128)(2,1)} %get-tuple-element.292), channel_id=1, source_target_pairs={{0,8},{8,0},{1,9},{9,1},{2,10},{10,2},{3,11},{11,3},{4,12},{12,4},... | collective-permute-start | bytes 1572872 | tf_op jit(solution)/shard_map/ppermute | solution.py:860
  370.3 44.9 %collective-permute-start.37 = (bf16[1024,256]{1,0:T(8,128)(2,1)}, bf16[1024,256]{1,0:T(8,128)(2,1)}, u32[]{:S(2)}, u32[]{:S(2)}) collective-permute-start(bf16[1024,256]{1,0:T(8,128)(2,1)} %get-tuple-element.289), channel_id=1, source_target_pairs={{0,8},{8,0},{1,9},{9,1},{2,10},{10,2},{3,11},{11,3},{4,12},{12,4},... | collective-permute-start | bytes 1572872 | tf_op jit(solution)/shard_map/ppermute | solution.py:860
  370.8 4.4 collective-permute-start.18
  376.5 14.0 %collective-permute-start.19 = (bf16[128,2048]{1,0:T(8,128)(2,1)S(1)}, bf16[128,2048]{1,0:T(8,128)(2,1)S(1)}, u32[]{:S(2)}, u32[]{:S(2)}) collective-permute-start(bf16[128,2048]{1,0:T(8,128)(2,1)S(1)} %add_convert_fusion.6), channel_id=1, source_target_pairs={{0,2},{2,0},{1,3},{3,1},{4,6},{6,4},{5,7},{7,5},{8,10},{10,8},{9,1... | collective-permute-start | bytes 1572872 | tf_op jit(solution)/shard_map/cond/branch_1_fun/ppermute | solution.py:860
  421.4 44.5 %collective-permute-start.41 = (bf16[512,256]{1,0:T(8,128)(2,1)}, bf16[512,256]{1,0:T(8,128)(2,1)S(1)}, u32[]{:S(2)}, u32[]{:S(2)}) collective-permute-start(bf16[512,256]{1,0:T(8,128)(2,1)} %get-tuple-element.420), channel_id=1, source_target_pairs={{0,16},{16,0},{1,17},{17,1},{2,18},{18,2},{3,19},{19,3},{4,20},{20... | collective-permute-start | bytes 786440 | tf_op jit(solution)/shard_map/ppermute | solution.py:860
  424.3 42.9 %collective-permute-start.40 = (bf16[512,256]{1,0:T(8,128)(2,1)}, bf16[512,256]{1,0:T(8,128)(2,1)S(1)}, u32[]{:S(2)}, u32[]{:S(2)}) collective-permute-start(bf16[512,256]{1,0:T(8,128)(2,1)} %get-tuple-element.422), channel_id=1, source_target_pairs={{0,16},{16,0},{1,17},{17,1},{2,18},{18,2},{3,19},{19,3},{4,20},{20... | collective-permute-start | bytes 786440 | tf_op jit(solution)/shard_map/ppermute | solution.py:860
  424.4 31.2 %collective-permute-start.7 = (bf16[128,2048]{1,0:T(8,128)(2,1)S(1)}, bf16[128,2048]{1,0:T(8,128)(2,1)}, u32[]{:S(2)}, u32[]{:S(2)}) collective-permute-start(bf16[128,2048]{1,0:T(8,128)(2,1)S(1)} %get-tuple-element.109), channel_id=1, source_target_pairs={{0,8},{8,0},{1,9},{9,1},{2,10},{10,2},{3,11},{11,3},{4,12},{12,4},... | collective-permute-start | bytes 1572872 | tf_op jit(solution)/shard_map/cond/branch_1_fun/ppermute | solution.py:860
  426.8 28.8 %collective-permute-start.8 = (bf16[128,2048]{1,0:T(8,128)(2,1)S(1)}, bf16[128,2048]{1,0:T(8,128)(2,1)}, u32[]{:S(2)}, u32[]{:S(2)}) collective-permute-start(bf16[128,2048]{1,0:T(8,128)(2,1)S(1)} %get-tuple-element.110), channel_id=1, source_target_pairs={{0,2},{2,0},{1,3},{3,1},{4,6},{6,4},{5,7},{7,5},{8,10},{10,8},{9,1... | collective-permute-start | bytes 1572872 | tf_op jit(solution)/shard_map/cond/branch_1_fun/ppermute | solution.py:860
  455.6 46.9 %collective-permute-start.42 = (bf16[256,1024]{1,0:T(8,128)(2,1)}, bf16[256,1024]{1,0:T(8,128)(2,1)}, u32[]{:S(2)}, u32[]{:S(2)}) collective-permute-start(bf16[256,1024]{1,0:T(8,128)(2,1)} %get-tuple-element.323), channel_id=1, source_target_pairs={{0,8},{8,0},{1,9},{9,1},{2,10},{10,2},{3,11},{11,3},{4,12},{12,4},... | collective-permute-start | bytes 1572872 | tf_op jit(solution)/shard_map/ppermute | solution.py:860
  471.5 33.7 %collective-permute-start.43 = (bf16[2,256,1024]{2,1,0:T(8,128)(2,1)}, bf16[2,256,1024]{2,1,0:T(8,128)(2,1)}, u32[]{:S(2)}, u32[]{:S(2)}) collective-permute-start(bf16[2,256,1024]{2,1,0:T(8,128)(2,1)} %get-tuple-element.393), channel_id=1, source_target_pairs={{0,8},{8,0},{1,9},{9,1},{2,10},{10,2},{3,11},{11,3},{4,12},{12,4},... | collective-permute-start | bytes 3145736 | tf_op jit(solution)/shard_map/ppermute | solution.py:860
  476.8 31.0 %collective-permute-start.44 = (bf16[4,256,512]{2,1,0:T(8,128)(2,1)}, bf16[4,256,512]{2,1,0:T(8,128)(2,1)}, u32[]{:S(2)}, u32[]{:S(2)}) collective-permute-start(bf16[4,256,512]{2,1,0:T(8,128)(2,1)} %get-tuple-element.329), channel_id=1, source_target_pairs={{0,4},{4,0},{1,5},{5,1},{2,6},{6,2},{3,7},{7,3},{8,12},{12,8},{9,1... | collective-permute-start | bytes 3145736 | tf_op jit(solution)/shard_map/ppermute | solution.py:860
  482.6 14.0 %collective-permute-start.21 = (bf16[128,2048]{1,0:T(8,128)(2,1)S(1)}, bf16[128,2048]{1,0:T(8,128)(2,1)S(1)}, u32[]{:S(2)}, u32[]{:S(2)}) collective-permute-start(bf16[128,2048]{1,0:T(8,128)(2,1)S(1)} %add_convert_fusion.11), channel_id=1, source_target_pairs={{0,2},{2,0},{1,3},{3,1},{4,6},{6,4},{5,7},{7,5},{8,10},{10,8},{9,1... | collective-permute-start | bytes 1572872 | tf_op jit(solution)/shard_map/cond/branch_1_fun/ppermute | solution.py:860
  501.0 40.9 %collective-permute-start.46 = (bf16[256,2048]{1,0:T(8,128)(2,1)}, bf16[256,2048]{1,0:T(8,128)(2,1)}, u32[]{:S(2)}, u32[]{:S(2)}) collective-permute-start(bf16[256,2048]{1,0:T(8,128)(2,1)} %pad_maximum_fusion.4), channel_id=1, source_target_pairs={{0,2},{2,0},{1,3},{3,1},{4,6},{6,4},{5,7},{7,5},{8,10},{10,8},{9,1... | collective-permute-start | bytes 3145736 | tf_op jit(solution)/shard_map/ppermute | solution.py:860
  510.4 30.7 %collective-permute-start.45 = (bf16[2,256,512]{2,1,0:T(8,128)(2,1)}, bf16[2,256,512]{2,1,0:T(8,128)(2,1)S(1)}, u32[]{:S(2)}, u32[]{:S(2)}) collective-permute-start(bf16[2,256,512]{2,1,0:T(8,128)(2,1)} %get-tuple-element.401), channel_id=1, source_target_pairs={{0,8},{8,0},{1,9},{9,1},{2,10},{10,2},{3,11},{11,3},{4,12},{12,4},... | collective-permute-start | bytes 1572872 | tf_op jit(solution)/shard_map/ppermute | solution.py:860
  513.5 54.1 %collective-permute-start.48 = (bf16[1,256,1024]{2,1,0:T(8,128)(2,1)}, bf16[1,256,1024]{2,1,0:T(8,128)(2,1)}, u32[]{:S(2)}, u32[]{:S(2)}) collective-permute-start(bf16[1,256,1024]{2,1,0:T(8,128)(2,1)} %get-tuple-element.395), channel_id=1, source_target_pairs={{0,16},{16,0},{1,17},{17,1},{2,18},{18,2},{3,19},{19,3},{4,20},{20... | collective-permute-start | bytes 1572872 | tf_op jit(solution)/shard_map/ppermute | solution.py:860
  516.9 9.2 %collective-permute-start.10 = (f32[2,2048]{1,0:T(2,128)S(1)}, f32[2,2048]{1,0:T(2,128)S(1)}, u32[]{:S(2)}, u32[]{:S(2)}) collective-permute-start(f32[2,2048]{1,0:T(2,128)S(1)} %add.208), channel_id=1, source_target_pairs={{0,2},{2,0},{1,3},{3,1},{4,6},{6,4},{5,7},{7,5},{8,10},{10,8},{9,1... | collective-permute-start | bytes 49160 | tf_op jit(solution)/shard_map/cond/branch_1_fun/ppermute | solution.py:860
  526.1 3.8 collective-permute-start.11
  529.9 4.3 collective-permute-start.12
  534.3 6.2 %collective-permute-start.13 = (f32[2,2048]{1,0:T(2,128)S(1)}, f32[2,2048]{1,0:T(2,128)S(1)}, u32[]{:S(2)}, u32[]{:S(2)}) collective-permute-start(f32[2,2048]{1,0:T(2,128)S(1)} %add.211), channel_id=1, source_target_pairs={{0,16},{16,0},{1,17},{17,1},{2,18},{18,2},{3,19},{19,3},{4,20},{20... | collective-permute-start | bytes 49160 | tf_op jit(solution)/shard_map/cond/branch_1_fun/ppermute | solution.py:860
  542.0 19.5 %collective-permute-start.47 = (bf16[1,256,512]{2,1,0:T(8,128)(2,1)}, bf16[1,256,512]{2,1,0:T(8,128)(2,1)}, u32[]{:S(2)}, u32[]{:S(2)}) collective-permute-start(bf16[1,256,512]{2,1,0:T(8,128)(2,1)} %get-tuple-element.414), channel_id=1, source_target_pairs={{0,16},{16,0},{1,17},{17,1},{2,18},{18,2},{3,19},{19,3},{4,20},{20... | collective-permute-start | bytes 786440 | tf_op jit(solution)/shard_map/ppermute | solution.py:860
  549.5 4.5 collective-permute-start.22
  561.4 14.3 %collective-permute-start.49 = (bf16[256,1024]{1,0:T(8,128)(2,1)}, bf16[256,1024]{1,0:T(8,128)(2,1)}, u32[]{:S(2)}, u32[]{:S(2)}) collective-permute-start(bf16[256,1024]{1,0:T(8,128)(2,1)} %get-tuple-element.349), channel_id=1, source_target_pairs={{0,8},{8,0},{1,9},{9,1},{2,10},{10,2},{3,11},{11,3},{4,12},{12,4},... | collective-permute-start | bytes 1572872 | tf_op jit(solution)/shard_map/ppermute | solution.py:860
  (73 other events, 978.6 us)
Sparse Core Ops, SparseCore 0:
  182.9 89.4 reduce-scatter.3
  275.6 86.0 reduce-scatter.5
  364.7 103.9 reduce-scatter.7
